TPU v7x, 128 devices: a whole 4x4x4 slice. The times are simulated.
128 devices in a mesh: tile: 64 (over z_hi, y, x, core), vec: 2 (over z_lo).
Axes of the slice: x: 4, y: 4, z: 4 (z_hi: 2, z_lo: 2; z = z_hi * 2 + z_lo), core: 2. Of those that a mesh axis runs over, the one named last changes fastest.
Arguments:
- trial: bfloat16 [1, 1024, 1024], P(None, ('tile', 'vec')), may hold values from -0.005859375 to 0.005859375
- psi_v: bfloat16 [1024, 8192], P(None, 'tile'), may hold values from -16 to 16
- psi_c: bfloat16 [1024, 2, 4096], P(None, 'vec', 'tile'), may hold values from -6 to 6
- screened: float32 [8192, 8192], P('tile', 'vec'), may hold values from -0.0007324219 to 0.0007324219
Outputs:
- result: float32 [1, 1024, 1024], P(None, ('tile', 'vec'))
All inputs are finite; a program needn't handle non-finite values.
Results may differ from a plain program's by a relative error of at most 0.0041.
Values may be sent and summed in bfloat16 or wider, within the bound.
No kernel may reach another device: no remote copies, remote signals or barrier semaphores. Data moves between devices by JAX's collectives and lax.ppermute only.
A program may use at most 64 MiB of HBM per device.

v0:
```python
import jax
import jax.numpy as jnp
from jax import lax
from jax.sharding import Mesh
from jax.sharding import PartitionSpec as P

TILE_VEC = ("tile_0", "tile_1", "tile_2", "tile_3", "vec")
TILE = ("tile_0", "tile_1", "tile_2", "tile_3")


def piece_ends(length, count):
    turn = length // count
    if turn >= 8:
        turn -= turn % 8
    return [turn * k for k in range(1, count)]


def all_blocks(value, axes, sequence):
    tiles = value
    for k in sequence:
        tiles = lax.all_gather(tiles, axes[k])
    done = sequence[::-1]
    back = [done.index(k) for k in range(len(axes))]
    tiles = tiles.transpose(*back, *range(len(axes), tiles.ndim))
    return tiles.reshape(-1, *value.shape)


def laid_out(tiles, dim):
    shape = list(tiles.shape[1:])
    shape[dim] *= tiles.shape[0]
    return jnp.moveaxis(tiles, 0, dim).reshape(shape)


def gather_at_once(value, axes, dim):
    cut = max(range(max(1, value.ndim - 1)), key=lambda d: value.shape[d])
    count, outs = (len(axes), [])
    for first, slab in enumerate(jnp.split(value, piece_ends(value.shape[cut], count), axis=cut)):
        if slab.size:
            sequence = [(first - k) % count for k in range(count)]
            outs.append(all_blocks(slab, axes, sequence))
    return laid_out(jnp.concatenate(outs, axis=cut + 1), dim)


def from_everyone(value, axis):
    copies = jnp.broadcast_to(value, (lax.axis_size(axis), *value.shape))
    return lax.all_to_all(copies, axis, split_axis=0, concat_axis=0, tiled=True)


def of_everyone(value, axis):
    everything = from_everyone(value, axis)
    return jnp.sum(everything, axis=0)


def back_product(weighted_flat, panel):
    return lax.dot_general(
        weighted_flat, panel, (((1,), (1,)), ((), ())), preferred_element_type=jnp.float32
    )


def shards(trial, psi_v, psi_c, screened):
    count = trial.shape[0]
    points = psi_v.shape[1]
    conduct = trial.shape[2]
    whole = gather_at_once(trial, TILE_VEC, 1)
    projected = jnp.einsum("vp,kvc->kpc", psi_v, whole, preferred_element_type=jnp.float32).astype(
        jnp.bfloat16
    )
    flat = projected.reshape(count * points, conduct)
    panel_local = psi_c[:, 0, :]
    panel = lax.all_gather(panel_local, TILE, axis=1, tiled=True)
    pair = jnp.dot(flat, panel, preferred_element_type=jnp.float32)
    weighted = (screened[None] * pair.reshape(count, points, -1)).astype(jnp.bfloat16)
    weighted_flat = weighted.reshape(count * points, -1)
    back = back_product(weighted_flat, panel)
    back = back.reshape(count, points, conduct)
    left = psi_v.astype(jnp.float32)
    summed = of_everyone(back, "vec")
    tiles = lax.axis_size(TILE)
    halves = lax.axis_size("vec")
    owned = left.shape[0] // (tiles * halves)
    grouped = left.reshape(tiles, halves, owned, points)
    mine = lax.dynamic_index_in_dim(grouped, lax.axis_index("vec"), 1, keepdims=False).reshape(
        tiles * owned, points
    )
    term = jnp.dot(mine, summed[0], precision=lax.Precision.HIGHEST)
    pieces = [lax.psum_scatter(term, TILE, scatter_dimension=0, tiled=True)]
    return jnp.stack(pieces, axis=0)


def solution(mesh):
    split = Mesh(
        mesh.devices.reshape(2, 4, 4, 2, mesh.shape["vec"]),
        ("tile_0", "tile_1", "tile_2", "tile_3", "vec"),
    )
    return jax.shard_map(
        shards,
        mesh=split,
        in_specs=(P(None, TILE_VEC, None), P(None, TILE), P(None, "vec", TILE), P(TILE, "vec")),
        out_specs=P(None, TILE_VEC, None),
        check_vma=False,
    )
```

profile of v0, /device:TPU:1, one launch (start us, length us, event | category | flops | bytes accessed | tf_op | source)
XLA Modules:
  0.0 567.2 jit_solution(8643632401018379686)
XLA Ops:
  14.6 9.9 %all-gather.22 = bf16[8,2,1,4,1024]{4,3,2,1,0:T(4,128)(2,1)S(1)} all-gather(bf16[2,2,1,4,1024]{4,3,2,1,0:T(4,128)(2,1)S(1)} %bitcast.108), channel_id=24, replica_groups=mesh['tile_0'=2,'tile_1'=4,'tile_2'=4,'tile_3'=2,'vec'=2] {'tile_2'}, dimensions={0}, use_global_device_ids=true | all-gather | bytes 163840 | tf_op jit(solution)/shard_map/all_gather | solution.py:21
  24.4 11.3 %all-gather.23 = bf16[16,2,2,1,4,1024]{5,4,3,2,1,0:T(4,128)(2,1)} all-gather(bf16[4,2,2,1,4,1024]{5,4,3,2,1,0:T(4,128)(2,1)S(1)} %bitcast.101), channel_id=25, replica_groups=mesh['tile_0'=2,'tile_1'=4,'tile_2'=4,'tile_3'=2,'vec'=2] {'tile_1'}, dimensions={0}, use_global_device_ids=true | all-gather | bytes 655360 | tf_op jit(solution)/shard_map/all_gather | solution.py:21
  37.4 7.7 %all-gather.15 = bf16[2,1,1024]{2,1,0:T(2,128)(2,1)S(1)} all-gather(bf16[1,1,1024]{2,1,0:T(2,128)(2,1)S(1)} %get-tuple-element.5), channel_id=17, replica_groups=mesh['tile_0'=2,'tile_1'=4,'tile_2'=4,'tile_3'=2,'vec'=2] {'tile_3'}, dimensions={0}, use_global_device_ids=true | all-gather | bytes 6144 | tf_op jit(solution)/shard_map/all_gather | solution.py:21
  45.1 9.0 %all-gather.16 = bf16[8,1,1024]{2,1,0:T(2,128)(2,1)S(1)} all-gather(bf16[2,1,1024]{2,1,0:T(2,128)(2,1)S(1)} %all-gather.15), channel_id=18, replica_groups=mesh['tile_0'=2,'tile_1'=4,'tile_2'=4,'tile_3'=2,'vec'=2] {'tile_2'}, dimensions={0}, use_global_device_ids=true | all-gather | bytes 20480 | tf_op jit(solution)/shard_map/all_gather | solution.py:21
  54.2 10.2 %all-gather.17 = bf16[16,2,1,1,1024]{4,1,3,2,0:T(2,128)(2,1)S(1)} all-gather(bf16[4,2,1,1,1024]{4,1,3,2,0:T(2,128)(2,1)S(1)} %bitcast.111), channel_id=19, replica_groups=mesh['tile_0'=2,'tile_1'=4,'tile_2'=4,'tile_3'=2,'vec'=2] {'tile_1'}, dimensions={0}, use_global_device_ids=true | all-gather | bytes 81920 | tf_op jit(solution)/shard_map/all_gather | solution.py:21
  64.4 5.6 all-gather.18
  70.0 4.8 all-gather.19
  75.5 9.1 %all-gather.10 = bf16[4,1,1024]{2,1,0:T(2,128)(2,1)S(1)} all-gather(bf16[1,1,1024]{2,1,0:T(2,128)(2,1)S(1)} %get-tuple-element.6), channel_id=12, replica_groups=mesh['tile_0'=2,'tile_1'=4,'tile_2'=4,'tile_3'=2,'vec'=2] {'tile_2'}, dimensions={0}, use_global_device_ids=true | all-gather | bytes 10240 | tf_op jit(solution)/shard_map/all_gather | solution.py:21
  84.6 9.6 %all-gather.11 = bf16[16,1,1024]{2,1,0:T(2,128)(2,1)S(1)} all-gather(bf16[4,1,1024]{2,1,0:T(2,128)(2,1)S(1)} %all-gather.10), channel_id=13, replica_groups=mesh['tile_0'=2,'tile_1'=4,'tile_2'=4,'tile_3'=2,'vec'=2] {'tile_1'}, dimensions={0}, use_global_device_ids=true | all-gather | bytes 40960 | tf_op jit(solution)/shard_map/all_gather | solution.py:21
  94.4 6.3 %all-gather.12 = bf16[8,4,1,1,1024]{4,1,3,2,0:T(4,128)(2,1)S(1)} all-gather(bf16[4,4,1,1,1024]{4,1,3,2,0:T(4,128)(2,1)S(1)} %bitcast.109), channel_id=14, replica_groups=mesh['tile_0'=2,'tile_1'=4,'tile_2'=4,'tile_3'=2,'vec'=2] {'tile_0'}, dimensions={0}, use_global_device_ids=true | all-gather | bytes 98304 | tf_op jit(solution)/shard_map/all_gather | solution.py:21
  100.7 5.3 all-gather.13
  106.0 13.4 %all-gather.14 = bf16[4,2,4,4,1,1,1024]{6,3,5,4,2,1,0:T(4,128)(2,1)S(1)} all-gather(bf16[2,2,4,4,1,1,1024]{6,3,5,4,2,1,0:T(4,128)(2,1)S(1)} %bitcast.103), channel_id=16, replica_groups=mesh['tile_0'=2,'tile_1'=4,'tile_2'=4,'tile_3'=2,'vec'=2] {'tile_3'}, dimensions={0}, use_global_device_ids=true | all-gather | bytes 393216 | tf_op jit(solution)/shard_map/all_gather | solution.py:21
  119.9 9.7 %all-gather.5 = bf16[4,1,1024]{2,1,0:T(2,128)(2,1)S(1)} all-gather(bf16[1,1,1024]{2,1,0:T(2,128)(2,1)S(1)} %get-tuple-element.7), channel_id=7, replica_groups=mesh['tile_0'=2,'tile_1'=4,'tile_2'=4,'tile_3'=2,'vec'=2] {'tile_1'}, dimensions={0}, use_global_device_ids=true | all-gather | bytes 10240 | tf_op jit(solution)/shard_map/all_gather | solution.py:21
  129.6 5.7 %all-gather.6 = bf16[8,1,1024]{2,1,0:T(2,128)(2,1)S(1)} all-gather(bf16[4,1,1024]{2,1,0:T(2,128)(2,1)S(1)} %all-gather.5), channel_id=8, replica_groups=mesh['tile_0'=2,'tile_1'=4,'tile_2'=4,'tile_3'=2,'vec'=2] {'tile_0'}, dimensions={0}, use_global_device_ids=true | all-gather | bytes 24576 | tf_op jit(solution)/shard_map/all_gather | solution.py:21
  139.4 5.0 all-gather.8
  144.5 10.5 %all-gather.9 = bf16[8,2,2,4,1,1,1024]{6,3,5,4,2,1,0:T(4,128)(2,1)S(1)} all-gather(bf16[2,2,2,4,1,1,1024]{6,3,5,4,2,1,0:T(4,128)(2,1)S(1)} %bitcast.106), channel_id=11, replica_groups=mesh['tile_0'=2,'tile_1'=4,'tile_2'=4,'tile_3'=2,'vec'=2] {'tile_2'}, dimensions={0}, use_global_device_ids=true | all-gather | bytes 327680 | tf_op jit(solution)/shard_map/all_gather | solution.py:21
  156.2 4.7 all-gather
  164.2 6.6 %all-gather.2 = bf16[4,2,1,1,1024]{4,1,3,2,0:T(2,128)(2,1)S(1)} all-gather(bf16[2,2,1,1,1024]{4,1,3,2,0:T(2,128)(2,1)S(1)} %bitcast.114), channel_id=4, replica_groups=mesh['tile_0'=2,'tile_1'=4,'tile_2'=4,'tile_3'=2,'vec'=2] {'tile_3'}, dimensions={0}, use_global_device_ids=true | all-gather | bytes 24576 | tf_op jit(solution)/shard_map/all_gather | solution.py:21
  170.7 9.0 %all-gather.3 = bf16[8,2,2,1,1,1024]{5,2,4,3,1,0:T(2,128)(2,1)S(1)} all-gather(bf16[2,2,2,1,1,1024]{5,2,4,3,1,0:T(2,128)(2,1)S(1)} %bitcast.113), channel_id=5, replica_groups=mesh['tile_0'=2,'tile_1'=4,'tile_2'=4,'tile_3'=2,'vec'=2] {'tile_2'}, dimensions={0}, use_global_device_ids=true | all-gather | bytes 81920 | tf_op jit(solution)/shard_map/all_gather | solution.py:21
  179.7 9.4 %all-gather.4 = bf16[16,2,2,2,1,1,1024]{6,3,5,4,2,1,0:T(2,128)(2,1)S(1)} all-gather(bf16[4,2,2,2,1,1,1024]{6,3,5,4,2,1,0:T(2,128)(2,1)S(1)} %bitcast.104), channel_id=6, replica_groups=mesh['tile_0'=2,'tile_1'=4,'tile_2'=4,'tile_3'=2,'vec'=2] {'tile_1'}, dimensions={0}, use_global_device_ids=true | all-gather | bytes 327680 | tf_op jit(solution)/shard_map/all_gather | solution.py:21
  190.2 9.1 %concatenate.3 = bf16[128,1,8,1024]{3,2,0,1:T(8,128)(2,1)S(1)} concatenate(bf16[128,1,1,1024]{3,2,0,1:T(2,128)(2,1)} %reshape.75, bf16[128,1,1,1024]{3,2,0,1:T(2,128)(2,1)} %reshape.76, bf16[128,1,1,1024]{3,2,0,1:T(2,128)(2,1)S(1)} %reshape.77, bf16[128,1,1,1024]{3,2,0,1:T(2,128)(2,1)S(1)} %reshape.78, bf16[128,1,4,1024]{3,2,0,1:T(4,128)(2,1)} %bitcast.93), dimensions={2} | concatenate | bytes 4194304 | tf_op jit(solution)/shard_map/concatenate | solution.py:41
  200.2 10.4 %fusion = f32[128,1024]{1,0:T(8,128)S(1)} fusion(bf16[1024,1,4096]{0,2,1:T(8,128)(2,1)} %all-gather.31.cloned.1.call-done, f32[128,4096]{1,0:T(8,128)} %param.7, bf16[128,1024]{0,1:T(8,128)(2,1)S(1)} %fusion.17), kind=kOutput, calls=%fused_computation | convolution fusion | flops 2148532224 | bytes 11272192 | tf_op jit(solution)/shard_map/dot_general | solution.py:55
  215.4 8.2 %all-to-all-done = f32[2,1,128,1024]{3,2,1,0:T(8,128)S(1)} async-done(((f32[2,1,128,1024]{3,2,1,0:T(8,128)}), f32[2,1,128,1024]{3,2,1,0:T(8,128)S(1)}, u32[]{:S(2)}, u32[]{:S(2)}) %all-to-all-start) | async-done | bytes 1048608 | tf_op jit(solution)/shard_map/all_to_all | solution.py:46
  226.0 334.6 %reduce-scatter.2.cloned.1.call-done = f32[8,1024]{1,0:T(8,128)} async-done(((f32[512,1024]{1,0:T(8,128)}), f32[8,1024]{1,0:T(8,128)}) %reduce-scatter.2.cloned.1.call-update) | async-done | bytes 32784 | tf_op jit(solution)/shard_map/reduce_scatter | solution.py:86
  (39 shorter events, 29.0 us)
Async XLA Ops:
  6.5 192.8 %copy-start = (bf16[1024,128]{1,0:T(8,128)(2,1)S(1)}, bf16[1024,128]{1,0:T(8,128)(2,1)}, u32[]{:S(2)}) copy-start(bf16[1024,128]{1,0:T(8,128)(2,1)} %param.5) | copy-start | bytes 786436
  6.5 183.7 %all-gather.29.cloned.1.call-start = ((), (), s32[]{:S(2)}) async-start(), calls=%async_computation.3 | async-start | bytes 1572864 | tf_op jit(solution)/shard_map/all_gather | solution.py:21
  35.8 164.4 %all-gather.31.cloned.1.call-start = ((), (), s32[]{:S(2)}) async-start(), calls=%async_computation.4 | async-start | bytes 8519680 | tf_op jit(solution)/shard_map/all_gather | solution.py:70
  211.7 11.8 %all-to-all-start = ((f32[2,1,128,1024]{3,2,1,0:T(8,128)}), f32[2,1,128,1024]{3,2,1,0:T(8,128)S(1)}, u32[]{:S(2)}, u32[]{:S(2)}) async-start(f32[2,1,128,1024]{3,2,1,0:T(8,128)} %broadcast_in_dim.4), calls=%async_computation | async-start | bytes 2097152 | tf_op jit(solution)/shard_map/all_to_all | solution.py:46
  215.3 345.4 %reduce-scatter.2.cloned.1.call-start = ((), (), s32[]{:S(2)}) async-start(), calls=%async_computation.2 | async-start | bytes 2129920 | tf_op jit(solution)/shard_map/reduce_scatter | solution.py:86
Sparse Core Ops, SparseCore 0:
  35.9 31.5 all-gather.28
  70.7 83.8 all-gather.30
  226.1 334.4 reduce-scatter.1
where the time goes:
time: 575 us; the launch traced here: 567 us
  waiting for transfers between devices  344 us (60%)
  blocking collectives  177 us (31%)
  local copies, waits for them, and re-layouts  15.6 us (3%)
  matrix products  13.6 us (2%)
  between operations  13.2 us (2%)
    reduce_scatter x1, waiting for transfers between devices, shards(): pieces = [lax.psum_scatter(term, TILE, scatter_dimension=0, tiled=True)]  335 us
    all_gather x24, blocking collectives, all_blocks(): tiles = lax.all_gather(tiles, axes[k])  177 us
  transfers between devices with their start and end apart: 4, of which 2 were waited for; matrix products, arithmetic and copies ran while one was open for 3% of the time, Pallas kernels for 0%

commit v1 on v0

v1 whole, which is shorter than its diff:
```python
import jax
import jax.numpy as jnp
from jax import lax
from jax.experimental import pallas as pl
from jax.experimental.pallas import tpu as pltpu
from jax.sharding import Mesh
from jax.sharding import PartitionSpec as P

TILE_VEC = ("zh", "y", "x", "core", "zl")
TILE = ("zh", "y", "x", "core")
VMEM_LIMIT = 48 * 1024 * 1024
F32 = jnp.float32
BF16 = jnp.bfloat16


def shift(value, axis, by):
    n = lax.axis_size(axis)
    return lax.ppermute(value, axis, [(k, (k + by) % n) for k in range(n)])


def around(value, axis):
    return [value, shift(value, axis, 1), shift(value, axis, -1), shift(value, axis, 2)]


STEPS = (0, -1, 1, -2)


def any_spec():
    return pl.BlockSpec(memory_space=pl.ANY)


def vmem_spec():
    return pl.BlockSpec(memory_space=pltpu.VMEM)


def params():
    return pltpu.CompilerParams(vmem_limit_bytes=VMEM_LIMIT)


def project(trial_half, left_own, left_other):
    points = left_own.shape[1]
    cols = trial_half.shape[1]

    def kernel(trial_ref, own_ref, other_ref, out_ref):
        core = lax.axis_index("core")
        for ref, at in ((own_ref, core), (other_ref, 1 - core)):
            part = lax.dot_general(
                ref[...], trial_ref[...], (((0,), (0,)), ((), ())), preferred_element_type=F32
            )
            out_ref[pl.ds(pl.multiple_of(at * points, points), points), :] = part.astype(BF16)

    return pl.pallas_call(
        kernel,
        out_shape=jax.ShapeDtypeStruct((2 * points, cols), BF16),
        in_specs=[vmem_spec()] * 3,
        out_specs=vmem_spec(),
        compiler_params=params(),
        name="project",
    )(trial_half, left_own, left_other)


def direct(proj_own, proj_other, sets_a, sets_b, screened, screened_other):
    rows, half = proj_own.shape
    points = screened.shape[0]
    states = 2 * half
    block = sets_a[0].shape[0] // 4
    count = 32 * block
    chunk = 512

    def kernel(*refs):
        own_ref, other_ref = refs[:2]
        a_refs, b_refs = refs[2:6], refs[6:10]
        scr_ref, scr_other_ref = refs[10:12]
        keep_ref, send_ref = refs[12:14]
        proj, panel, scr, back, sems = refs[14:]
        core, y, x = lax.axis_index("core"), lax.axis_index("y"), lax.axis_index("x")
        copies = [
            (own_ref, proj.at[:, pl.ds(pl.multiple_of(core * half, half), half)]),
            (other_ref, proj.at[:, pl.ds(pl.multiple_of((1 - core) * half, half), half)]),
            (
                scr_ref.at[:, pl.ds(pl.multiple_of(core * count, count), count)],
                scr.at[pl.ds(pl.multiple_of(core * points, points), points), :],
            ),
            (scr_other_ref, scr.at[pl.ds(pl.multiple_of((1 - core) * points, points), points), :]),
        ]
        for outer in range(4):
            for inner in range(4):
                for which, ref in ((0, a_refs[outer]), (1, b_refs[outer])):
                    dy, dx = (outer, inner) if which == 0 else (inner, outer)
                    at = lax.rem(y + STEPS[dy] + 4, 4) * 4 + lax.rem(x + STEPS[dx] + 4, 4)
                    start = pl.multiple_of(at * (2 * block) + which * block, block)
                    copies.append(
                        (ref.at[pl.ds(inner * block, block), :], panel.at[pl.ds(start, block), :])
                    )
        made = [
            pltpu.make_async_copy(source, target, sems.at[k])
            for k, (source, target) in enumerate(copies)
        ]
        for copy in made:
            copy.start()
        for copy in made:
            copy.wait()
        for k in range(count // chunk):
            here = pl.ds(k * chunk, chunk)
            pair = lax.dot_general(
                proj[...], panel[here, :], (((1,), (1,)), ((), ())), preferred_element_type=F32
            )
            weighted = (scr[:, here] * pair).astype(BF16)
            part = jnp.dot(weighted, panel[here, :], preferred_element_type=F32)
            if k == 0:
                back[...] = part
            else:
                back[...] += part
        keep_ref[...] = back[:, pl.ds(pl.multiple_of(core * half, half), half)]
        send_ref[...] = back[:, pl.ds(pl.multiple_of((1 - core) * half, half), half)]

    return pl.pallas_call(
        kernel,
        out_shape=[jax.ShapeDtypeStruct((rows, half), F32)] * 2,
        in_specs=[any_spec()] * 12,
        out_specs=[vmem_spec()] * 2,
        scratch_shapes=[
            pltpu.VMEM((rows, states), BF16),
            pltpu.VMEM((count, states), BF16),
            pltpu.VMEM((rows, count), F32),
            pltpu.VMEM((rows, states), F32),
            pltpu.SemaphoreType.DMA((36,)),
        ],
        compiler_params=params(),
        name="direct",
    )(proj_own, proj_other, *sets_a, *sets_b, screened, screened_other)


def finish(left_own, left_other, back_own, back_other):
    states, points = left_own.shape
    cols = back_own.shape[1]

    def kernel(own_ref, other_ref, a_ref, b_ref, out_ref, high, low):
        core = lax.axis_index("core")
        back = a_ref[...] + b_ref[...]
        top = back.astype(BF16)
        high[...] = top
        low[...] = (back - top.astype(F32)).astype(BF16)
        total = None
        for ref, at in ((own_ref, core), (other_ref, 1 - core)):
            here = pl.ds(pl.multiple_of(at * points, points), points)
            for piece in (high, low):
                part = jnp.dot(ref[...], piece[here, :], preferred_element_type=F32)
                total = part if total is None else total + part
        out_ref[...] = total.astype(BF16)

    return pl.pallas_call(
        kernel,
        out_shape=jax.ShapeDtypeStruct((states, cols), BF16),
        in_specs=[vmem_spec()] * 4,
        out_specs=vmem_spec(),
        scratch_shapes=[pltpu.VMEM((2 * points, cols), BF16)] * 2,
        compiler_params=params(),
        name="finish",
    )(left_own, left_other, back_own, back_other)


def shards(trial, psi_v, psi_c, screened):
    rows, states = trial.shape[1:]
    half = states // 2
    devices = lax.axis_size(TILE_VEC)
    core = lax.axis_index("core")
    zh = lax.axis_index("zh")
    halves = trial[0].reshape(rows, 2, half).transpose(1, 0, 2)
    outgoing = jnp.broadcast_to(
        halves[None, :, None], (devices // 4, 2, 2, rows, half)
    ).reshape(devices, rows, half)
    trial_half = lax.all_to_all(outgoing, TILE_VEC, split_axis=0, concat_axis=0, tiled=True)
    trial_half = trial_half.reshape(devices * rows, half)
    own = psi_c[:, 0, :].T
    first = lax.ppermute(own, ("zh", "core"), [(1, 0), (2, 1), (0, 2), (3, 3)])
    second = lax.ppermute(own, ("zh", "core"), [(0, 0), (3, 1), (1, 2), (2, 3)])
    same = core == zh
    block_a = jnp.where(same, second, first)
    block_b = jnp.where(same, first, second)
    left_other = shift(psi_v, "core", 1)
    width = screened.shape[1] // 2
    screened_other = shift(
        lax.dynamic_slice_in_dim(screened, (1 - core) * width, width, 1), "core", 1
    )
    line_a = jnp.concatenate(around(block_a, "x"), 0)
    line_b = jnp.concatenate(around(block_b, "y"), 0)
    sets_a = around(line_a, "y")
    sets_b = around(line_b, "x")
    proj_own = project(trial_half, psi_v, left_other)
    proj_other = shift(proj_own, "core", 1)
    keep, send = direct(proj_own, proj_other, sets_a, sets_b, screened, screened_other)
    got = shift(send, "core", 1)
    term = finish(psi_v, left_other, keep, got)
    pieces = lax.all_to_all(
        term.reshape(devices, rows, half), TILE_VEC, split_axis=0, concat_axis=0, tiled=True
    )
    pieces = pieces.reshape(devices // 4, 2, 2, rows, half).astype(F32)
    total = jnp.sum(pieces, axis=(0, 2))
    return total.transpose(1, 0, 2).reshape(1, rows, states)


def solution(mesh):
    split = Mesh(
        mesh.devices.reshape(2, 4, 4, 2, mesh.shape["vec"]),
        TILE_VEC,
    )
    return jax.shard_map(
        shards,
        mesh=split,
        in_specs=(P(None, TILE_VEC, None), P(None, TILE), P(None, "zl", TILE), P(TILE, "zl")),
        out_specs=P(None, TILE_VEC, None),
        check_vma=False,
    )
```

time: 575 us -> 126 us (0.22); the launches traced: 567 us -> 126 us
  waiting for transfers between devices: 344 us -> 44.7 us
  blocking collectives: 177 us -> 25.8 us
  starting transfers between devices: 3.66 us -> 40 us
  matrix products: 13.6 us -> 0 us
  between operations: 13.2 us -> 0.12 us
  local copies, waits for them, and re-layouts: 15.6 us -> 4.93 us
  Pallas kernels: 0 us -> 9.43 us
    reduce_scatter x1 -> x0, waiting for transfers between devices: 335 us -> none  [shards(): pieces = [lax.psum_scatter(term, TILE, scatter_dimension=0, tiled=True)]]
    all_gather x24 -> x0, blocking collectives: 177 us -> none  [all_blocks(): tiles = lax.all_gather(tiles, axes[k])]
    ppermute x0 -> x18, waiting for transfers between devices: none -> 44.7 us  [the longest x16 42.4 us: shift(): return lax.ppermute(value, axis, [(k, (k + by) % n) for k in range(n)])]
    ppermute x0 -> x18, starting transfers between devices: none -> 29.5 us  [the longest x16 20.7 us: shift(): return lax.ppermute(value, axis, [(k, (k + by) % n) for k in range(n)])]
    all_to_all x0 -> x1, blocking collectives: none -> 25.8 us  [shards(): lax.all_to_all(term.reshape(devices, rows, half), TILE_VEC, split_axis=0,...]
    dot_general x3 -> x0, matrix products: 13.6 us -> none  [the longest x1 10.4 us: back_product(): lax.dot_general(weighted_flat, panel, (((1,), (1,)), ((), ())), preferred...]
    pallas_call x0 -> x3, Pallas kernels: none -> 9.43 us  [the longest x1 7.61 us: direct(): pl.pallas_call(kernel, out_shape=[jax.ShapeDtypeStruct((rows, half), F32)...]
    concatenate x1 -> x0, local copies, waits for them, and re-layouts: 9.13 us -> none  [gather_at_once(): return laid_out(jnp.concatenate(outs, axis=cut + 1), dim)]
  transfers between devices with their start and end apart: 4 -> 19, of which waited for: 2 -> 9; matrix products, arithmetic and copies ran while one was open for 3% -> 3% of each run, Pallas kernels for 0% -> 0%
where the time goes in v1:
time: 126 us
  waiting for transfers between devices  44.7 us (35%)
  starting transfers between devices  40 us (32%)
  blocking collectives  25.8 us (20%)
  Pallas kernels  9.43 us (7%)
  local copies, waits for them, and re-layouts  4.93 us (4%)
    ppermute x16, waiting for transfers between devices, shift(): return lax.ppermute(value, axis, [(k, (k + by) % n) for k in range(n)])  42.4 us
    all_to_all x1, blocking collectives, shards(): lax.all_to_all(term.reshape(devices, rows, half), TILE_VEC, split_axis=0,...  25.8 us
    ppermute x16, starting transfers between devices, shift(): return lax.ppermute(value, axis, [(k, (k + by) % n) for k in range(n)])  20.7 us
    all_to_all x1, starting transfers between devices, shards(): lax.all_to_all(outgoing, TILE_VEC, split_axis=0, concat_axis=0, tiled=True)  10.5 us
    pallas_call x1, Pallas kernels, direct(): pl.pallas_call(kernel, out_shape=[jax.ShapeDtypeStruct((rows, half), F32)...  7.61 us
    ppermute x1, starting transfers between devices, shards(): second = lax.ppermute(own, ('zh', 'core'), [(0, 0), (3, 1), (1, 2), (2, 3)])  5.48 us
    ppermute x1, starting transfers between devices, shards(): first = lax.ppermute(own, ('zh', 'core'), [(1, 0), (2, 1), (0, 2), (3, 3)])  3.32 us
  transfers between devices with their start and end apart: 19, of which 9 were waited for; matrix products, arithmetic and copies ran while one was open for 3% of the time, Pallas kernels for 0%

profile of v1, /device:TPU:1, one launch (start us, length us, event | category | flops | bytes accessed | tf_op | source)
XLA Modules:
  0.0 125.8 jit_solution(16293887200274651466)
XLA Ops:
  0.0 3.3 %collective-permute-start.3 = (bf16[64,1024]{1,0:T(8,128)(2,1)}, bf16[64,1024]{1,0:T(8,128)(2,1)S(1)}, u32[]{:S(2)}, u32[]{:S(2)}) collective-permute-start(bf16[64,1024]{1,0:T(8,128)(2,1)} %bitcast.18), channel_id=1, source_target_pairs={{2,0},{64,2},{0,64},{66,66},{3,1},{65,3},{1,65},{67,67},{6,4},{68,... | collective-permute-start | bytes 393224 | tf_op jit(solution)/shard_map/ppermute | solution.py:176
  3.3 5.5 %collective-permute-start.2 = (bf16[64,1024]{1,0:T(8,128)(2,1)}, bf16[64,1024]{1,0:T(8,128)(2,1)S(1)}, u32[]{:S(2)}, u32[]{:S(2)}) collective-permute-start(bf16[64,1024]{1,0:T(8,128)(2,1)} %bitcast.19), channel_id=1, source_target_pairs={{0,0},{66,2},{2,64},{64,66},{1,1},{67,3},{3,65},{65,67},{4,4},{70,... | collective-permute-start | bytes 393224 | tf_op jit(solution)/shard_map/ppermute | solution.py:177
  8.8 1.3 %collective-permute-done.3 = bf16[64,1024]{1,0:T(8,128)(2,1)S(1)} collective-permute-done((bf16[64,1024]{1,0:T(8,128)(2,1)}, bf16[64,1024]{1,0:T(8,128)(2,1)S(1)}, u32[]{:S(2)}, u32[]{:S(2)}) %collective-permute-start.3) | collective-permute-done | bytes 131104 | tf_op jit(solution)/shard_map/ppermute | solution.py:176
  11.2 2.8 %collective-permute-start.6 = (bf16[64,1024]{1,0:T(8,128)(2,1)S(1)}, bf16[64,1024]{1,0:T(8,128)(2,1)S(1)}, u32[]{:S(2)}, u32[]{:S(2)}) collective-permute-start(bf16[64,1024]{1,0:T(8,128)(2,1)S(1)} %get-tuple-element.10), channel_id=1, source_target_pairs={{0,8},{4,12},{8,0},{12,4},{1,9},{5,13},{9,1},{13,5},{2,10},{6,14},... | collective-permute-start | bytes 393224 | tf_op jit(solution)/shard_map/ppermute | solution.py:18
  15.5 1.8 %broadcast_in_dim.2 = bf16[32,2,2,8,512]{4,3,2,1,0:T(8,128)(2,1)} broadcast(bf16[2,8,512]{2,1,0:T(8,128)(2,1)} %bitcast.17), dimensions={1,3,4} | broadcast | bytes 1064960 | tf_op jit(solution)/shard_map/broadcast_in_dim | solution.py:170
  17.3 10.5 %all-to-all-start = ((bf16[128,8,512]{2,1,0:T(8,128)(2,1)}), bf16[128,8,512]{2,1,0:T(8,128)(2,1)S(1)}, u32[]{:S(2)}, u32[]{:S(2)}) async-start(bf16[128,8,512]{2,1,0:T(8,128)(2,1)} %bitcast.2), calls=%async_computation | async-start | bytes 2097152 | tf_op jit(solution)/shard_map/all_to_all | solution.py:173
  27.8 3.0 %collective-permute-start.12 = (bf16[64,1024]{1,0:T(8,128)(2,1)S(1)}, bf16[64,1024]{1,0:T(8,128)(2,1)S(1)}, u32[]{:S(2)}, u32[]{:S(2)}) collective-permute-start(bf16[64,1024]{1,0:T(8,128)(2,1)S(1)} %get-tuple-element.9), channel_id=1, source_target_pairs={{0,32},{16,48},{32,0},{48,16},{1,33},{17,49},{33,1},{49,17},{2,34}... | collective-permute-start | bytes 393224 | tf_op jit(solution)/shard_map/ppermute | solution.py:18
  31.2 2.3 %collective-permute-start.8 = (bf16[256,1024]{1,0:T(8,128)(2,1)S(1)}, bf16[256,1024]{1,0:T(8,128)(2,1)S(1)}, u32[]{:S(2)}, u32[]{:S(2)}) collective-permute-start(bf16[256,1024]{1,0:T(8,128)(2,1)S(1)} %pad_maximum_fusion.refs_2_), channel_id=1, source_target_pairs={{0,48},{16,0},{32,16},{48,32},{1,49},{17,1},{33,17},{49,33},{2,50}... | collective-permute-start | bytes 1572872 | tf_op jit(solution)/shard_map/ppermute | solution.py:18
  33.6 2.3 %constant_dynamic-slice_fusion = f32[128,2048]{1,0:T(8,128)} fusion(f32[128,4096]{1,0:T(8,128)} %refs_10_.1, s32[]{:T(128)S(6)} %select_n.18), kind=kLoop, calls=%fused_computation.5 | loop fusion | bytes 2097156 | tf_op jit(solution)/shard_map/dynamic_slice | solution.py:184
  35.9 1.2 collective-permute-start.16
  37.1 7.7 %collective-permute-done.12 = bf16[64,1024]{1,0:T(8,128)(2,1)S(1)} collective-permute-done((bf16[64,1024]{1,0:T(8,128)(2,1)S(1)}, bf16[64,1024]{1,0:T(8,128)(2,1)S(1)}, u32[]{:S(2)}, u32[]{:S(2)}) %collective-permute-start.12) | collective-permute-done | bytes 131104 | tf_op jit(solution)/shard_map/ppermute | solution.py:18
  44.9 12.4 %collective-permute-done.11 = bf16[64,1024]{1,0:T(8,128)(2,1)S(1)} collective-permute-done((bf16[64,1024]{1,0:T(8,128)(2,1)S(1)}, bf16[64,1024]{1,0:T(8,128)(2,1)S(1)}, u32[]{:S(2)}, u32[]{:S(2)}) %collective-permute-start.11) | collective-permute-done | bytes 131104 | tf_op jit(solution)/shard_map/ppermute | solution.py:18
  59.2 1.5 %collective-permute-start.9 = (bf16[256,1024]{1,0:T(8,128)(2,1)S(1)}, bf16[256,1024]{1,0:T(8,128)(2,1)}, u32[]{:S(2)}, u32[]{:S(2)}) collective-permute-start(bf16[256,1024]{1,0:T(8,128)(2,1)S(1)} %pad_maximum_fusion.refs_2_), channel_id=1, source_target_pairs={{0,32},{16,48},{32,0},{48,16},{1,33},{17,49},{33,1},{49,17},{2,34}... | collective-permute-start | bytes 1572872 | tf_op jit(solution)/shard_map/ppermute | solution.py:18
  60.7 1.3 %collective-permute-start.13 = (bf16[256,1024]{1,0:T(8,128)(2,1)S(1)}, bf16[256,1024]{1,0:T(8,128)(2,1)}, u32[]{:S(2)}, u32[]{:S(2)}) collective-permute-start(bf16[256,1024]{1,0:T(8,128)(2,1)S(1)} %pad_maximum_fusion.1.refs_6_), channel_id=1, source_target_pairs={{0,4},{4,8},{8,12},{12,0},{1,5},{5,9},{9,13},{13,1},{2,6},{6,10},{... | collective-permute-start | bytes 1572872 | tf_op jit(solution)/shard_map/ppermute | solution.py:18
  62.0 1.5 %collective-permute-start.14 = (bf16[256,1024]{1,0:T(8,128)(2,1)S(1)}, bf16[256,1024]{1,0:T(8,128)(2,1)}, u32[]{:S(2)}, u32[]{:S(2)}) collective-permute-start(bf16[256,1024]{1,0:T(8,128)(2,1)S(1)} %pad_maximum_fusion.1.refs_6_), channel_id=1, source_target_pairs={{0,12},{4,0},{8,4},{12,8},{1,13},{5,1},{9,5},{13,9},{2,14},{6,2},{... | collective-permute-start | bytes 1572872 | tf_op jit(solution)/shard_map/ppermute | solution.py:18
  64.3 1.5 %collective-permute-start.15 = (bf16[256,1024]{1,0:T(8,128)(2,1)S(1)}, bf16[256,1024]{1,0:T(8,128)(2,1)}, u32[]{:S(2)}, u32[]{:S(2)}) collective-permute-start(bf16[256,1024]{1,0:T(8,128)(2,1)S(1)} %pad_maximum_fusion.1.refs_6_), channel_id=1, source_target_pairs={{0,8},{4,12},{8,0},{12,4},{1,9},{5,13},{9,1},{13,5},{2,10},{6,14},... | collective-permute-start | bytes 1572872 | tf_op jit(solution)/shard_map/ppermute | solution.py:18
  66.2 7.4 %collective-permute-done.9.refs_5_ = bf16[256,1024]{1,0:T(8,128)(2,1)} collective-permute-done((bf16[256,1024]{1,0:T(8,128)(2,1)S(1)}, bf16[256,1024]{1,0:T(8,128)(2,1)}, u32[]{:S(2)}, u32[]{:S(2)}) %collective-permute-start.9) | collective-permute-done | bytes 524320 | tf_op jit(solution)/shard_map/ppermute | solution.py:18
  73.7 1.4 %collective-permute-start.1 = (bf16[256,512]{1,0:T(8,128)(2,1)S(1)}, bf16[256,512]{1,0:T(8,128)(2,1)S(1)}, u32[]{:S(2)}, u32[]{:S(2)}) collective-permute-start(bf16[256,512]{1,0:T(8,128)(2,1)S(1)} %project.1.refs_0_), channel_id=1, source_target_pairs={{0,2},{2,0},{1,3},{3,1},{4,6},{6,4},{5,7},{7,5},{8,10},{10,8},{9,1... | collective-permute-start | bytes 786440 | tf_op jit(solution)/shard_map/ppermute | solution.py:18
  75.3 12.2 %collective-permute-done.15.refs_9_ = bf16[256,1024]{1,0:T(8,128)(2,1)} collective-permute-done((bf16[256,1024]{1,0:T(8,128)(2,1)S(1)}, bf16[256,1024]{1,0:T(8,128)(2,1)}, u32[]{:S(2)}, u32[]{:S(2)}) %collective-permute-start.15) | collective-permute-done | bytes 524320 | tf_op jit(solution)/shard_map/ppermute | solution.py:18
  87.5 7.6 %direct.1 = (f32[256,512]{1,0:T(8,128)S(1)}, f32[256,512]{1,0:T(8,128)S(1)}) custom-call(bf16[256,512]{1,0:T(8,128)(2,1)S(1)} %project.1.refs_0_, bf16[256,512]{1,0:T(8,128)(2,1)S(1)} %collective-permute-done.1.refs_1_, bf16[256,1024]{1,0:T(8,128)(2,1)S(1)} %pad_maximum_fusion.refs_2_, bf16[256,1024]{1,0:T(8,128)(2,1)S(1)} %collective-permute-done.7.refs_3_, ...), custom_call_target="tpu_custom_call" | custom-call | tf_op jit(solution)/shard_map/direct/pallas_call | solution.py:117
  95.1 1.3 collective-permute-start.17
  96.4 1.5 %collective-permute-done.17.b_ref = f32[256,512]{1,0:T(8,128)S(1)} collective-permute-done((f32[256,512]{1,0:T(8,128)S(1)}, f32[256,512]{1,0:T(8,128)S(1)}, u32[]{:S(2)}, u32[]{:S(2)}) %collective-permute-start.17) | collective-permute-done | bytes 524320 | tf_op jit(solution)/shard_map/ppermute | solution.py:18
  97.9 1.4 %finish.1 = bf16[1024,512]{1,0:T(8,128)(2,1)S(1)} custom-call(bf16[1024,128]{1,0:T(8,128)(2,1)S(1)} %copy-done, bf16[1024,128]{1,0:T(8,128)(2,1)S(1)} %collective-permute-done.other_ref, f32[256,512]{1,0:T(8,128)S(1)} %get-tuple-element.7.a_ref, f32[256,512]{1,0:T(8,128)S(1)} %collective-permute-done.17.b_ref), custom_call_target="tpu_custom_call" | custom-call | tf_op jit(solution)/shard_map/finish/pallas_call | solution.py:152
  99.3 25.8 %all_to_all.10 = bf16[128,8,512]{2,1,0:T(8,128)(2,1)S(1)} all-to-all(bf16[128,8,512]{2,1,0:T(8,128)(2,1)S(1)} %bitcast.15), channel_id=1, replica_groups=mesh['zh'=2,'y'=4,'x'=4,'core'=2,'zl'=2] {'zh','y','x','core','zl'}, dimensions={0} | all-to-all | bytes 2097152 | tf_op jit(solution)/shard_map/all_to_all | solution.py:195
  (30 shorter events, 7.2 us)
Async XLA Ops:
  0.0 10.1 %collective-permute-start.3 = (bf16[64,1024]{1,0:T(8,128)(2,1)}, bf16[64,1024]{1,0:T(8,128)(2,1)S(1)}, u32[]{:S(2)}, u32[]{:S(2)}) collective-permute-start(bf16[64,1024]{1,0:T(8,128)(2,1)} %bitcast.18), channel_id=1, source_target_pairs={{2,0},{64,2},{0,64},{66,66},{3,1},{65,3},{1,65},{67,67},{6,4},{68,... | collective-permute-start | bytes 393224 | tf_op jit(solution)/shard_map/ppermute | solution.py:176
  3.3 7.8 %collective-permute-start.2 = (bf16[64,1024]{1,0:T(8,128)(2,1)}, bf16[64,1024]{1,0:T(8,128)(2,1)S(1)}, u32[]{:S(2)}, u32[]{:S(2)}) collective-permute-start(bf16[64,1024]{1,0:T(8,128)(2,1)} %bitcast.19), channel_id=1, source_target_pairs={{0,0},{66,2},{2,64},{64,66},{1,1},{67,3},{3,65},{65,67},{4,4},{70,... | collective-permute-start | bytes 393224 | tf_op jit(solution)/shard_map/ppermute | solution.py:177
  11.2 19.6 %collective-permute-start.6 = (bf16[64,1024]{1,0:T(8,128)(2,1)S(1)}, bf16[64,1024]{1,0:T(8,128)(2,1)S(1)}, u32[]{:S(2)}, u32[]{:S(2)}) collective-permute-start(bf16[64,1024]{1,0:T(8,128)(2,1)S(1)} %get-tuple-element.10), channel_id=1, source_target_pairs={{0,8},{4,12},{8,0},{12,4},{1,9},{5,13},{9,1},{13,5},{2,10},{6,14},... | collective-permute-start | bytes 393224 | tf_op jit(solution)/shard_map/ppermute | solution.py:18
  14.0 16.8 %collective-permute-start.5 = (bf16[64,1024]{1,0:T(8,128)(2,1)S(1)}, bf16[64,1024]{1,0:T(8,128)(2,1)S(1)}, u32[]{:S(2)}, u32[]{:S(2)}) collective-permute-start(bf16[64,1024]{1,0:T(8,128)(2,1)S(1)} %get-tuple-element.10), channel_id=1, source_target_pairs={{0,12},{4,0},{8,4},{12,8},{1,13},{5,1},{9,5},{13,9},{2,14},{6,2},{... | collective-permute-start | bytes 393224 | tf_op jit(solution)/shard_map/ppermute | solution.py:18
  14.9 15.9 %collective-permute-start.4 = (bf16[64,1024]{1,0:T(8,128)(2,1)S(1)}, bf16[64,1024]{1,0:T(8,128)(2,1)S(1)}, u32[]{:S(2)}, u32[]{:S(2)}) collective-permute-start(bf16[64,1024]{1,0:T(8,128)(2,1)S(1)} %get-tuple-element.10), channel_id=1, source_target_pairs={{0,4},{4,8},{8,12},{12,0},{1,5},{5,9},{9,13},{13,1},{2,6},{6,10},{... | collective-permute-start | bytes 393224 | tf_op jit(solution)/shard_map/ppermute | solution.py:18
  17.3 48.5 %all-to-all-start = ((bf16[128,8,512]{2,1,0:T(8,128)(2,1)}), bf16[128,8,512]{2,1,0:T(8,128)(2,1)S(1)}, u32[]{:S(2)}, u32[]{:S(2)}) async-start(bf16[128,8,512]{2,1,0:T(8,128)(2,1)} %bitcast.2), calls=%async_computation | async-start | bytes 2097152 | tf_op jit(solution)/shard_map/all_to_all | solution.py:173
  27.8 29.5 %copy-start = (bf16[1024,128]{1,0:T(8,128)(2,1)S(1)}, bf16[1024,128]{1,0:T(8,128)(2,1)}, u32[]{:S(2)}) copy-start(bf16[1024,128]{1,0:T(8,128)(2,1)} %own_ref.3) | copy-start | bytes 786436
  27.8 17.0 %collective-permute-start.12 = (bf16[64,1024]{1,0:T(8,128)(2,1)S(1)}, bf16[64,1024]{1,0:T(8,128)(2,1)S(1)}, u32[]{:S(2)}, u32[]{:S(2)}) collective-permute-start(bf16[64,1024]{1,0:T(8,128)(2,1)S(1)} %get-tuple-element.9), channel_id=1, source_target_pairs={{0,32},{16,48},{32,0},{48,16},{1,33},{17,49},{33,1},{49,17},{2,34}... | collective-permute-start | bytes 393224 | tf_op jit(solution)/shard_map/ppermute | solution.py:18
  30.8 31.2 %collective-permute-start.7 = (bf16[256,1024]{1,0:T(8,128)(2,1)S(1)}, bf16[256,1024]{1,0:T(8,128)(2,1)S(1)}, u32[]{:S(2)}, u32[]{:S(2)}) collective-permute-start(bf16[256,1024]{1,0:T(8,128)(2,1)S(1)} %pad_maximum_fusion.refs_2_), channel_id=1, source_target_pairs={{0,16},{16,32},{32,48},{48,0},{1,17},{17,33},{33,49},{49,1},{2,18}... | collective-permute-start | bytes 1572872 | tf_op jit(solution)/shard_map/ppermute | solution.py:18
  31.2 32.3 %collective-permute-start.8 = (bf16[256,1024]{1,0:T(8,128)(2,1)S(1)}, bf16[256,1024]{1,0:T(8,128)(2,1)S(1)}, u32[]{:S(2)}, u32[]{:S(2)}) collective-permute-start(bf16[256,1024]{1,0:T(8,128)(2,1)S(1)} %pad_maximum_fusion.refs_2_), channel_id=1, source_target_pairs={{0,48},{16,0},{32,16},{48,32},{1,49},{17,1},{33,17},{49,33},{2,50}... | collective-permute-start | bytes 1572872 | tf_op jit(solution)/shard_map/ppermute | solution.py:18
  35.9 51.6 %collective-permute-start.16 = (f32[128,2048]{1,0:T(8,128)}, f32[128,2048]{1,0:T(8,128)}, u32[]{:S(2)}, u32[]{:S(2)}) collective-permute-start(f32[128,2048]{1,0:T(8,128)} %constant_dynamic-slice_fusion), channel_id=1, source_target_pairs={{0,2},{2,0},{1,3},{3,1},{4,6},{6,4},{5,7},{7,5},{8,10},{10,8},{9,1... | collective-permute-start | bytes 3145736 | tf_op jit(solution)/shard_map/ppermute | solution.py:18
  37.1 20.2 %collective-permute-start.11 = (bf16[64,1024]{1,0:T(8,128)(2,1)S(1)}, bf16[64,1024]{1,0:T(8,128)(2,1)S(1)}, u32[]{:S(2)}, u32[]{:S(2)}) collective-permute-start(bf16[64,1024]{1,0:T(8,128)(2,1)S(1)} %get-tuple-element.9), channel_id=1, source_target_pairs={{0,48},{16,0},{32,16},{48,32},{1,49},{17,1},{33,17},{49,33},{2,50}... | collective-permute-start | bytes 393224 | tf_op jit(solution)/shard_map/ppermute | solution.py:18
  44.8 14.3 %collective-permute-start.10 = (bf16[64,1024]{1,0:T(8,128)(2,1)S(1)}, bf16[64,1024]{1,0:T(8,128)(2,1)S(1)}, u32[]{:S(2)}, u32[]{:S(2)}) collective-permute-start(bf16[64,1024]{1,0:T(8,128)(2,1)S(1)} %get-tuple-element.9), channel_id=1, source_target_pairs={{0,16},{16,32},{32,48},{48,0},{1,17},{17,33},{33,49},{49,1},{2,18}... | collective-permute-start | bytes 393224 | tf_op jit(solution)/shard_map/ppermute | solution.py:18
  57.3 3.5 %collective-permute-start = (bf16[1024,128]{1,0:T(8,128)(2,1)S(1)}, bf16[1024,128]{1,0:T(8,128)(2,1)S(1)}, u32[]{:S(2)}, u32[]{:S(2)}) collective-permute-start(bf16[1024,128]{1,0:T(8,128)(2,1)S(1)} %copy-done), channel_id=1, source_target_pairs={{0,2},{2,0},{1,3},{3,1},{4,6},{6,4},{5,7},{7,5},{8,10},{10,8},{9,1... | collective-permute-start | bytes 786440 | tf_op jit(solution)/shard_map/ppermute | solution.py:18
  59.2 14.5 %collective-permute-start.9 = (bf16[256,1024]{1,0:T(8,128)(2,1)S(1)}, bf16[256,1024]{1,0:T(8,128)(2,1)}, u32[]{:S(2)}, u32[]{:S(2)}) collective-permute-start(bf16[256,1024]{1,0:T(8,128)(2,1)S(1)} %pad_maximum_fusion.refs_2_), channel_id=1, source_target_pairs={{0,32},{16,48},{32,0},{48,16},{1,33},{17,49},{33,1},{49,17},{2,34}... | collective-permute-start | bytes 1572872 | tf_op jit(solution)/shard_map/ppermute | solution.py:18
  60.7 14.5 %collective-permute-start.13 = (bf16[256,1024]{1,0:T(8,128)(2,1)S(1)}, bf16[256,1024]{1,0:T(8,128)(2,1)}, u32[]{:S(2)}, u32[]{:S(2)}) collective-permute-start(bf16[256,1024]{1,0:T(8,128)(2,1)S(1)} %pad_maximum_fusion.1.refs_6_), channel_id=1, source_target_pairs={{0,4},{4,8},{8,12},{12,0},{1,5},{5,9},{9,13},{13,1},{2,6},{6,10},{... | collective-permute-start | bytes 1572872 | tf_op jit(solution)/shard_map/ppermute | solution.py:18
  62.0 13.3 %collective-permute-start.14 = (bf16[256,1024]{1,0:T(8,128)(2,1)S(1)}, bf16[256,1024]{1,0:T(8,128)(2,1)}, u32[]{:S(2)}, u32[]{:S(2)}) collective-permute-start(bf16[256,1024]{1,0:T(8,128)(2,1)S(1)} %pad_maximum_fusion.1.refs_6_), channel_id=1, source_target_pairs={{0,12},{4,0},{8,4},{12,8},{1,13},{5,1},{9,5},{13,9},{2,14},{6,2},{... | collective-permute-start | bytes 1572872 | tf_op jit(solution)/shard_map/ppermute | solution.py:18
  63.5 0.8 copy-start.1
  64.3 23.2 %collective-permute-start.15 = (bf16[256,1024]{1,0:T(8,128)(2,1)S(1)}, bf16[256,1024]{1,0:T(8,128)(2,1)}, u32[]{:S(2)}, u32[]{:S(2)}) collective-permute-start(bf16[256,1024]{1,0:T(8,128)(2,1)S(1)} %pad_maximum_fusion.1.refs_6_), channel_id=1, source_target_pairs={{0,8},{4,12},{8,0},{12,4},{1,9},{5,13},{9,1},{13,5},{2,10},{6,14},... | collective-permute-start | bytes 1572872 | tf_op jit(solution)/shard_map/ppermute | solution.py:18
  65.8 21.7 %copy-start.2 = (bf16[256,1024]{1,0:T(8,128)(2,1)S(1)}, bf16[256,1024]{1,0:T(8,128)(2,1)}, u32[]{:S(2)}) copy-start(bf16[256,1024]{1,0:T(8,128)(2,1)} %copy-done.1) | copy-start | bytes 1572868
  73.7 13.8 %collective-permute-start.1 = (bf16[256,512]{1,0:T(8,128)(2,1)S(1)}, bf16[256,512]{1,0:T(8,128)(2,1)S(1)}, u32[]{:S(2)}, u32[]{:S(2)}) collective-permute-start(bf16[256,512]{1,0:T(8,128)(2,1)S(1)} %project.1.refs_0_), channel_id=1, source_target_pairs={{0,2},{2,0},{1,3},{3,1},{4,6},{6,4},{5,7},{7,5},{8,10},{10,8},{9,1... | collective-permute-start | bytes 786440 | tf_op jit(solution)/shard_map/ppermute | solution.py:18
  95.1 2.8 %collective-permute-start.17 = (f32[256,512]{1,0:T(8,128)S(1)}, f32[256,512]{1,0:T(8,128)S(1)}, u32[]{:S(2)}, u32[]{:S(2)}) collective-permute-start(f32[256,512]{1,0:T(8,128)S(1)} %get-tuple-element.8), channel_id=1, source_target_pairs={{0,2},{2,0},{1,3},{3,1},{4,6},{6,4},{5,7},{7,5},{8,10},{10,8},{9,1... | collective-permute-start | bytes 1572872 | tf_op jit(solution)/shard_map/ppermute | solution.py:18

commit v2 on v0

v2 whole, which is shorter than its diff:
```python
import jax
import jax.numpy as jnp
from jax import lax
from jax.experimental import pallas as pl
from jax.experimental.pallas import tpu as pltpu
from jax.sharding import Mesh
from jax.sharding import PartitionSpec as P

TILE_VEC = ("zh", "y", "x", "core", "zl")
TILE = ("zh", "y", "x", "core")
F32 = jnp.float32
BF16 = jnp.bfloat16
SIBLING = (1, 0, 3, 2)


def others(sibling, partner, diagonal):
    return [
        lax.ppermute(sibling, "core", [(0, 1), (1, 0)]),
        lax.ppermute(partner, "zh", [(0, 1), (1, 0)]),
        lax.ppermute(diagonal, ("zh", "core"), [(0, 3), (1, 2), (2, 1), (3, 0)]),
    ]


def vmem_spec():
    return pl.BlockSpec(memory_space=pltpu.VMEM)


def params(mebibytes):
    return pltpu.CompilerParams(vmem_limit_bytes=mebibytes * 1024 * 1024)


def pack(screened):
    points, count = screened.shape
    plane, steps = count // 2, 4
    width = plane // 2

    def kernel(in_ref, *out_refs):
        core, zh = lax.axis_index("core"), lax.axis_index("zh")
        rows = in_ref.shape[0]
        low = lax.broadcasted_iota(jnp.int32, (rows, 128), 1) < 64
        first = core == 0
        for far in range(2):
            base = plane * (zh if far == 0 else 1 - zh)
            for m in range(width // 128):
                a = in_ref[:, pl.ds(pl.multiple_of(base + m * 256, 256), 128)]
                b = in_ref[:, pl.ds(pl.multiple_of(base + m * 256 + 128, 128), 128)]
                zero = jnp.where(low, a, pltpu.roll(b, 64, 1))
                one = jnp.where(low, pltpu.roll(a, 64, 1), b)
                here = pl.ds(m * 128, 128)
                out_refs[2 * far][:, here] = jnp.where(first, zero, one)
                out_refs[2 * far + 1][:, here] = jnp.where(first, one, zero)

    return pl.pallas_call(
        kernel,
        grid=(steps,),
        out_shape=[jax.ShapeDtypeStruct((points, width), F32)] * 4,
        in_specs=[pl.BlockSpec((points // steps, count), lambda k: (k, 0))],
        out_specs=[pl.BlockSpec((points // steps, width), lambda k: (k, 0))] * 4,
        compiler_params=params(8),
        name="pack",
    )(screened)


def project(trial_half, lefts):
    points = lefts[0].shape[1]
    cols = trial_half.shape[1]

    def kernel(trial_ref, *refs):
        out_ref = refs[4]
        for k in range(4):
            part = lax.dot_general(
                refs[k][...], trial_ref[...], (((0,), (0,)), ((), ())), preferred_element_type=F32
            )
            out_ref[k * points : (k + 1) * points, :] = part.astype(BF16)

    return pl.pallas_call(
        kernel,
        out_shape=jax.ShapeDtypeStruct((4 * points, cols), BF16),
        in_specs=[vmem_spec()] * 5,
        out_specs=vmem_spec(),
        compiler_params=params(8),
        name="project",
    )(trial_half, *lefts)


def direct(proj_own, proj_other, panel, weights):
    rows, half = proj_own.shape
    points = rows // 4
    count = panel.shape[0]
    chunk = 512

    def kernel(own_ref, other_ref, panel_ref, *refs):
        scr_refs, (keep_ref, send_ref, proj) = refs[:4], refs[4:]
        core = lax.axis_index("core")
        mine = pl.ds(pl.multiple_of(core * half, half), half)
        sibs = pl.ds(pl.multiple_of((1 - core) * half, half), half)
        for k in range(4):
            proj[k * points : (k + 1) * points, :] = other_ref[
                SIBLING[k] * points : (SIBLING[k] + 1) * points, :
            ]
        nt = (((1,), (1,)), ((), ()))
        for k in range(count // chunk):
            here = pl.ds(k * chunk, chunk)
            pair = lax.dot_general(own_ref[...], panel_ref[here, mine], nt, preferred_element_type=F32)
            pair += lax.dot_general(proj[...], panel_ref[here, sibs], nt, preferred_element_type=F32)
            weighted = jnp.concatenate(
                [
                    (scr_refs[j][:, here] * pair[j * points : (j + 1) * points]).astype(BF16)
                    for j in range(4)
                ],
                0,
            )
            send = jnp.dot(weighted, panel_ref[here, sibs], preferred_element_type=F32)
            keep = jnp.dot(weighted, panel_ref[here, mine], preferred_element_type=F32)
            if k == 0:
                send_ref[...] = send
                keep_ref[...] = keep
            else:
                send_ref[...] += send
                keep_ref[...] += keep

    return pl.pallas_call(
        kernel,
        out_shape=[jax.ShapeDtypeStruct((rows, half), F32)] * 2,
        in_specs=[vmem_spec()] * 7,
        out_specs=[vmem_spec()] * 2,
        scratch_shapes=[pltpu.VMEM((rows, half), BF16)],
        compiler_params=params(24),
        name="direct",
    )(proj_own, proj_other, panel, *weights)


def finish(lefts, keep, got):
    states, points = lefts[0].shape
    cols = keep.shape[1]

    def kernel(*refs):
        left_refs, (keep_ref, got_ref, out_ref, left, high, low) = refs[:4], refs[4:]
        for k in range(4):
            here = slice(k * points, (k + 1) * points)
            there = slice(SIBLING[k] * points, (SIBLING[k] + 1) * points)
            back = keep_ref[here, :] + got_ref[there, :]
            top = back.astype(BF16)
            high[here, :] = top
            low[here, :] = (back - top.astype(F32)).astype(BF16)
            left[:, here] = left_refs[k][...]
        total = jnp.dot(left[...], high[...], preferred_element_type=F32)
        total += jnp.dot(left[...], low[...], preferred_element_type=F32)
        out_ref[...] = total.astype(BF16)

    return pl.pallas_call(
        kernel,
        out_shape=jax.ShapeDtypeStruct((states, cols), BF16),
        in_specs=[vmem_spec()] * 6,
        out_specs=vmem_spec(),
        scratch_shapes=[
            pltpu.VMEM((states, 4 * points), BF16),
            pltpu.VMEM((4 * points, cols), BF16),
            pltpu.VMEM((4 * points, cols), BF16),
        ],
        compiler_params=params(16),
        name="finish",
    )(*lefts, keep, got)


def shards(trial, psi_v, psi_c, screened):
    rows, states = trial.shape[1:]
    half = states // 2
    devices = lax.axis_size(TILE_VEC)
    own = psi_c[:, 0, :].T
    plane = lax.axis_size(("y", "x"))
    panel = lax.all_to_all(
        jnp.broadcast_to(own[None], (plane, *own.shape)), ("y", "x"), split_axis=0, concat_axis=0, tiled=True
    ).reshape(plane * own.shape[0], states)
    packed = pack(screened)
    weights = [packed[0], *others(*packed[1:])]
    halves = trial[0].reshape(rows, 2, half).transpose(1, 0, 2)
    outgoing = jnp.broadcast_to(
        halves[None, :, None], (devices // 4, 2, 2, rows, half)
    ).reshape(devices, rows, half)
    trial_half = lax.all_to_all(outgoing, TILE_VEC, split_axis=0, concat_axis=0, tiled=True)
    trial_half = trial_half.reshape(devices * rows, half)
    lefts = [psi_v, *others(psi_v, psi_v, psi_v)]
    proj_own = project(trial_half, lefts)
    proj_other = lax.ppermute(proj_own, "core", [(0, 1), (1, 0)])
    keep, send = direct(proj_own, proj_other, panel, weights)
    got = lax.ppermute(send, "core", [(0, 1), (1, 0)])
    term = finish(lefts, keep, got)
    pieces = lax.all_to_all(
        term.reshape(devices, rows, half), TILE_VEC, split_axis=0, concat_axis=0, tiled=True
    )
    pieces = pieces.reshape(devices // 4, 2, 2, rows, half).astype(F32)
    total = jnp.sum(pieces, axis=(0, 2))
    return total.transpose(1, 0, 2).reshape(1, rows, states)


def solution(mesh):
    split = Mesh(
        mesh.devices.reshape(2, 4, 4, 2, mesh.shape["vec"]),
        TILE_VEC,
    )
    return jax.shard_map(
        shards,
        mesh=split,
        in_specs=(P(None, TILE_VEC, None), P(None, TILE), P(None, "zl", TILE), P(TILE, "zl")),
        out_specs=P(None, TILE_VEC, None),
        check_vma=False,
    )
```

time: 575 us -> 117 us (0.20); the launches traced: 567 us -> 116 us
  waiting for transfers between devices: 344 us -> 27.1 us
  blocking collectives: 177 us -> 55.9 us
  matrix products: 13.6 us -> 0 us
  between operations: 13.2 us -> 0.13 us
  starting transfers between devices: 3.66 us -> 12.5 us
    reduce_scatter x1 -> x0, waiting for transfers between devices: 335 us -> none  [shards(): pieces = [lax.psum_scatter(term, TILE, scatter_dimension=0, tiled=True)]]
    all_gather x24 -> x0, blocking collectives: 177 us -> none  [all_blocks(): tiles = lax.all_gather(tiles, axes[k])]
    all_to_all x0 -> x2, blocking collectives: none -> 55.9 us  [the longest x1 29.8 us: shards(): lax.all_to_all(outgoing, TILE_VEC, split_axis=0, concat_axis=0, tiled=True)]
    ppermute x0 -> x8, waiting for transfers between devices: none -> 27.1 us  [the longest x2 12.7 us: others(): lax.ppermute(partner, 'zh', [(0, 1), (1, 0)])]
    dot_general x3 -> x0, matrix products: 13.6 us -> none  [the longest x1 10.4 us: back_product(): lax.dot_general(weighted_flat, panel, (((1,), (1,)), ((), ())), preferred...]
    unnamed x2 -> x42, local copies, waits for them, and re-layouts: 0.01 us -> 11.9 us
    concatenate x1 -> x0, local copies, waits for them, and re-layouts: 9.13 us -> none  [gather_at_once(): return laid_out(jnp.concatenate(outs, axis=cut + 1), dim)]
    ppermute x0 -> x8, starting transfers between devices: none -> 8.54 us  [the longest x2 4.1 us: others(): lax.ppermute(diagonal, ('zh', 'core'), [(0, 3), (1, 2), (2, 1), (3, 0)])]
  transfers between devices with their start and end apart: 4 -> 9, of which waited for: 2 -> 5; matrix products, arithmetic and copies ran while one was open for 3% -> 0% of each run, Pallas kernels for 0% -> 1%
where the time goes in v2:
time: 117 us; the launch traced here: 116 us
  blocking collectives  55.9 us (48%)
  waiting for transfers between devices  27.1 us (23%)
  local copies, waits for them, and re-layouts  14.4 us (12%)
  starting transfers between devices  12.5 us (11%)
  Pallas kernels  5.29 us (5%)
    all_to_all x1, blocking collectives, shards(): lax.all_to_all(outgoing, TILE_VEC, split_axis=0, concat_axis=0, tiled=True)  29.8 us
    all_to_all x1, blocking collectives, shards(): lax.all_to_all(term.reshape(devices, rows, half), TILE_VEC, split_axis=0,...  26.1 us
    ppermute x2, waiting for transfers between devices, others(): lax.ppermute(partner, 'zh', [(0, 1), (1, 0)])  12.7 us
    ppermute x2, waiting for transfers between devices, others(): lax.ppermute(diagonal, ('zh', 'core'), [(0, 3), (1, 2), (2, 1), (3, 0)])  12.2 us
    unnamed x42, local copies, waits for them, and re-layouts  11.9 us
    ppermute x2, starting transfers between devices, others(): lax.ppermute(diagonal, ('zh', 'core'), [(0, 3), (1, 2), (2, 1), (3, 0)])  4.1 us
    all_to_all x1, starting transfers between devices, shards(): lax.all_to_all(jnp.broadcast_to(own[None], (plane, *own.shape)), ('y', 'x...  4.01 us
    ppermute x2, starting transfers between devices, others(): lax.ppermute(partner, 'zh', [(0, 1), (1, 0)])  2.98 us
  transfers between devices with their start and end apart: 9, of which 5 were waited for; matrix products, arithmetic and copies ran while one was open for 0% of the time, Pallas kernels for 1%

profile of v2, /device:TPU:1, one launch (start us, length us, event | category | flops | bytes accessed | tf_op | source)
XLA Modules:
  0.0 116.2 jit_solution(17384073562938968387)
XLA Ops:
  0.0 0.9 broadcast_in_dim.4
  0.9 29.8 %all_to_all.15 = bf16[128,8,512]{2,1,0:T(8,128)(2,1)S(1)} all-to-all(bf16[128,8,512]{2,1,0:T(8,128)(2,1)S(1)} %bitcast.19), channel_id=1, replica_groups=mesh['zh'=2,'y'=4,'x'=4,'core'=2,'zl'=2] {'zh','y','x','core','zl'}, dimensions={0} | all-to-all | bytes 2097152 | tf_op jit(solution)/shard_map/all_to_all | solution.py:181
  30.7 1.6 %broadcast_in_dim.5 = bf16[16,64,1024]{2,1,0:T(8,128)(2,1)} broadcast(bf16[64,1024]{1,0:T(8,128)(2,1)S(1)} %bitcast.20), dimensions={1,2} | broadcast | bytes 2228224 | tf_op jit(solution)/shard_map/broadcast_in_dim | solution.py:173
  32.3 4.0 %all-to-all-start.1 = ((bf16[16,64,1024]{2,1,0:T(8,128)(2,1)}), bf16[16,64,1024]{2,1,0:T(8,128)(2,1)S(1)}, u32[]{:S(2)}, u32[]{:S(2)}) async-start(bf16[16,64,1024]{2,1,0:T(8,128)(2,1)} %broadcast_in_dim.5), calls=%async_computation.1 | async-start | bytes 4194304 | tf_op jit(solution)/shard_map/all_to_all | solution.py:172
  36.3 2.1 %collective-permute-start.2 = (bf16[1024,128]{1,0:T(8,128)(2,1)S(1)}, bf16[1024,128]{1,0:T(8,128)(2,1)S(1)}, u32[]{:S(2)}, u32[]{:S(2)}) collective-permute-start(bf16[1024,128]{1,0:T(8,128)(2,1)S(1)} %copy-done.3), channel_id=1, source_target_pairs={{0,66},{2,64},{64,2},{66,0},{1,67},{3,65},{65,3},{67,1},{4,70},{6,... | collective-permute-start | bytes 786440 | tf_op jit(solution)/shard_map/ppermute | solution.py:20
  38.4 1.9 %collective-permute-start.1 = (bf16[1024,128]{1,0:T(8,128)(2,1)S(1)}, bf16[1024,128]{1,0:T(8,128)(2,1)S(1)}, u32[]{:S(2)}, u32[]{:S(2)}) collective-permute-start(bf16[1024,128]{1,0:T(8,128)(2,1)S(1)} %copy-done.3), channel_id=1, source_target_pairs={{0,64},{64,0},{1,65},{65,1},{2,66},{66,2},{3,67},{67,3},{4,68},{68... | collective-permute-start | bytes 786440 | tf_op jit(solution)/shard_map/ppermute | solution.py:19
  40.3 1.6 %copy-done.2 = f32[128,4096]{1,0:T(8,128)S(1)} copy-done((f32[128,4096]{1,0:T(8,128)S(1)}, f32[128,4096]{1,0:T(8,128)}, u32[]{:S(2)}) %copy-start.2) | copy-done | bytes 2097176
  41.9 0.9 pack.1
  43.4 1.1 collective-permute-start.5
  44.5 2.0 %collective-permute-done.2.refs_3_ = bf16[1024,128]{1,0:T(8,128)(2,1)S(1)} collective-permute-done((bf16[1024,128]{1,0:T(8,128)(2,1)S(1)}, bf16[1024,128]{1,0:T(8,128)(2,1)S(1)}, u32[]{:S(2)}, u32[]{:S(2)}) %collective-permute-start.2) | collective-permute-done | bytes 262176 | tf_op jit(solution)/shard_map/ppermute | solution.py:20
  46.5 2.0 %collective-permute-start.6 = (f32[128,1024]{1,0:T(8,128)S(1)}, f32[128,1024]{1,0:T(8,128)S(1)}, u32[]{:S(2)}, u32[]{:S(2)}) collective-permute-start(f32[128,1024]{1,0:T(8,128)S(1)} %get-tuple-element.14), channel_id=1, source_target_pairs={{0,66},{2,64},{64,2},{66,0},{1,67},{3,65},{65,3},{67,1},{4,70},{6,... | collective-permute-start | bytes 1572872 | tf_op jit(solution)/shard_map/ppermute | solution.py:20
  48.5 4.2 %collective-permute-done.1.refs_2_ = bf16[1024,128]{1,0:T(8,128)(2,1)S(1)} collective-permute-done((bf16[1024,128]{1,0:T(8,128)(2,1)S(1)}, bf16[1024,128]{1,0:T(8,128)(2,1)S(1)}, u32[]{:S(2)}, u32[]{:S(2)}) %collective-permute-start.1) | collective-permute-done | bytes 262176 | tf_op jit(solution)/shard_map/ppermute | solution.py:19
  55.2 8.5 %collective-permute-done.5.refs_2_ = f32[128,1024]{1,0:T(8,128)S(1)} collective-permute-done((f32[128,1024]{1,0:T(8,128)S(1)}, f32[128,1024]{1,0:T(8,128)S(1)}, u32[]{:S(2)}, u32[]{:S(2)}) %collective-permute-start.5) | collective-permute-done | bytes 524320 | tf_op jit(solution)/shard_map/ppermute | solution.py:19
  64.5 10.1 %collective-permute-done.6.refs_3_ = f32[128,1024]{1,0:T(8,128)S(1)} collective-permute-done((f32[128,1024]{1,0:T(8,128)S(1)}, f32[128,1024]{1,0:T(8,128)S(1)}, u32[]{:S(2)}, u32[]{:S(2)}) %collective-permute-start.6) | collective-permute-done | bytes 524320 | tf_op jit(solution)/shard_map/ppermute | solution.py:20
  76.2 1.0 copy-done.1
  77.3 1.0 copy-done.11
  78.3 1.0 copy-done.13
  79.4 1.0 copy-done.15
  80.4 1.0 copy-done.17
  81.4 1.0 copy-done.19
  82.5 2.4 %direct.1 = (f32[512,512]{1,0:T(8,128)S(1)}, f32[512,512]{1,0:T(8,128)S(1)}) custom-call(bf16[512,512]{1,0:T(8,128)(2,1)S(1)} %copy-done.1, bf16[512,512]{1,0:T(8,128)(2,1)S(1)} %copy-done.19, bf16[1024,1024]{1,0:T(8,128)(2,1)S(1)} %bitcast.15, f32[128,1024]{1,0:T(8,128)S(1)} %copy-done.11, f32[128,1024]{1,0:T(8,128)S(1)} %copy-done.13, ...), custom_call_target="tpu_custom_call" | custom-call | tf_op jit(solution)/shard_map/direct/pallas_call | solution.py:122
  85.6 2.3 %collective-permute-done.7.refs_5_ = f32[512,512]{1,0:T(8,128)S(1)} collective-permute-done((f32[512,512]{1,0:T(8,128)S(1)}, f32[512,512]{1,0:T(8,128)S(1)}, u32[]{:S(2)}, u32[]{:S(2)}) %collective-permute-start.7) | collective-permute-done | bytes 1048608 | tf_op jit(solution)/shard_map/ppermute | solution.py:187
  87.9 1.3 %finish.1 = bf16[1024,512]{1,0:T(8,128)(2,1)S(1)} custom-call(bf16[1024,128]{1,0:T(8,128)(2,1)S(1)} %copy-done.3, bf16[1024,128]{1,0:T(8,128)(2,1)S(1)} %copy-done.9, bf16[1024,128]{1,0:T(8,128)(2,1)S(1)} %copy-done.7, bf16[1024,128]{1,0:T(8,128)(2,1)S(1)} %copy-done.5, f32[512,512]{1,0:T(8,128)S(1)} %get-tuple-element.15.refs_4_, ...), custom_call_target="tpu_custom_call" | custom-call | tf_op jit(solution)/shard_map/finish/pallas_call | solution.py:151
  89.3 26.1 %all_to_all.16 = bf16[128,8,512]{2,1,0:T(8,128)(2,1)S(1)} all-to-all(bf16[128,8,512]{2,1,0:T(8,128)(2,1)S(1)} %bitcast.17), channel_id=1, replica_groups=mesh['zh'=2,'y'=4,'x'=4,'core'=2,'zl'=2] {'zh','y','x','core','zl'}, dimensions={0} | all-to-all | bytes 2097152 | tf_op jit(solution)/shard_map/all_to_all | solution.py:189
  (45 shorter events, 7.1 us)
Async XLA Ops:
  0.0 30.7 %copy-start.20 = (bf16[1024,1,64]{0,2,1:T(8,128)(2,1)S(1)}, bf16[1024,1,64]{0,2,1:T(8,128)(2,1)}, u32[]{:S(2)}) copy-start(bf16[1024,1,64]{0,2,1:T(8,128)(2,1)} %param.6) | copy-start | bytes 393220
  32.3 4.0 %copy-start.3 = (bf16[1024,128]{1,0:T(8,128)(2,1)S(1)}, bf16[1024,128]{1,0:T(8,128)(2,1)}, u32[]{:S(2)}) copy-start(bf16[1024,128]{1,0:T(8,128)(2,1)} %refs_0_.3) | copy-start | bytes 786436
  32.3 43.9 %all-to-all-start.1 = ((bf16[16,64,1024]{2,1,0:T(8,128)(2,1)}), bf16[16,64,1024]{2,1,0:T(8,128)(2,1)S(1)}, u32[]{:S(2)}, u32[]{:S(2)}) async-start(bf16[16,64,1024]{2,1,0:T(8,128)(2,1)} %broadcast_in_dim.5), calls=%async_computation.1 | async-start | bytes 4194304 | tf_op jit(solution)/shard_map/all_to_all | solution.py:172
  36.3 10.2 %collective-permute-start.2 = (bf16[1024,128]{1,0:T(8,128)(2,1)S(1)}, bf16[1024,128]{1,0:T(8,128)(2,1)S(1)}, u32[]{:S(2)}, u32[]{:S(2)}) collective-permute-start(bf16[1024,128]{1,0:T(8,128)(2,1)S(1)} %copy-done.3), channel_id=1, source_target_pairs={{0,66},{2,64},{64,2},{66,0},{1,67},{3,65},{65,3},{67,1},{4,70},{6,... | collective-permute-start | bytes 786440 | tf_op jit(solution)/shard_map/ppermute | solution.py:20
  38.4 14.3 %collective-permute-start.1 = (bf16[1024,128]{1,0:T(8,128)(2,1)S(1)}, bf16[1024,128]{1,0:T(8,128)(2,1)S(1)}, u32[]{:S(2)}, u32[]{:S(2)}) collective-permute-start(bf16[1024,128]{1,0:T(8,128)(2,1)S(1)} %copy-done.3), channel_id=1, source_target_pairs={{0,64},{64,0},{1,65},{65,1},{2,66},{66,2},{3,67},{67,3},{4,68},{68... | collective-permute-start | bytes 786440 | tf_op jit(solution)/shard_map/ppermute | solution.py:19
  40.3 12.4 %collective-permute-start = (bf16[1024,128]{1,0:T(8,128)(2,1)S(1)}, bf16[1024,128]{1,0:T(8,128)(2,1)S(1)}, u32[]{:S(2)}, u32[]{:S(2)}) collective-permute-start(bf16[1024,128]{1,0:T(8,128)(2,1)S(1)} %copy-done.3), channel_id=1, source_target_pairs={{0,2},{2,0},{1,3},{3,1},{4,6},{6,4},{5,7},{7,5},{8,10},{10,8},{9,1... | collective-permute-start | bytes 786440 | tf_op jit(solution)/shard_map/ppermute | solution.py:18
  40.3 1.6 %copy-start.2 = (f32[128,4096]{1,0:T(8,128)S(1)}, f32[128,4096]{1,0:T(8,128)}, u32[]{:S(2)}) copy-start(f32[128,4096]{1,0:T(8,128)} %in_ref.1) | copy-start | bytes 6291460
  42.8 31.8 %copy-start.10 = (f32[128,1024]{1,0:T(8,128)}, f32[128,1024]{1,0:T(8,128)S(1)}, u32[]{:S(2)}) copy-start(f32[128,1024]{1,0:T(8,128)S(1)} %get-tuple-element.11.refs_0_) | copy-start | bytes 1572868
  42.8 11.6 %collective-permute-start.4 = (f32[128,1024]{1,0:T(8,128)S(1)}, f32[128,1024]{1,0:T(8,128)S(1)}, u32[]{:S(2)}, u32[]{:S(2)}) collective-permute-start(f32[128,1024]{1,0:T(8,128)S(1)} %get-tuple-element.12), channel_id=1, source_target_pairs={{0,2},{2,0},{1,3},{3,1},{4,6},{6,4},{5,7},{7,5},{8,10},{10,8},{9,1... | collective-permute-start | bytes 1572872 | tf_op jit(solution)/shard_map/ppermute | solution.py:18
  43.4 20.3 %collective-permute-start.5 = (f32[128,1024]{1,0:T(8,128)S(1)}, f32[128,1024]{1,0:T(8,128)S(1)}, u32[]{:S(2)}, u32[]{:S(2)}) collective-permute-start(f32[128,1024]{1,0:T(8,128)S(1)} %get-tuple-element.13), channel_id=1, source_target_pairs={{0,64},{64,0},{1,65},{65,1},{2,66},{66,2},{3,67},{67,3},{4,68},{68... | collective-permute-start | bytes 1572872 | tf_op jit(solution)/shard_map/ppermute | solution.py:19
  46.5 28.1 %copy-start.4 = (bf16[1024,128]{1,0:T(8,128)(2,1)}, bf16[1024,128]{1,0:T(8,128)(2,1)S(1)}, u32[]{:S(2)}) copy-start(bf16[1024,128]{1,0:T(8,128)(2,1)S(1)} %collective-permute-done.2.refs_3_) | copy-start | bytes 786436
  46.5 28.1 %collective-permute-start.6 = (f32[128,1024]{1,0:T(8,128)S(1)}, f32[128,1024]{1,0:T(8,128)S(1)}, u32[]{:S(2)}, u32[]{:S(2)}) collective-permute-start(f32[128,1024]{1,0:T(8,128)S(1)} %get-tuple-element.14), channel_id=1, source_target_pairs={{0,66},{2,64},{64,2},{66,0},{1,67},{3,65},{65,3},{67,1},{4,70},{6,... | collective-permute-start | bytes 1572872 | tf_op jit(solution)/shard_map/ppermute | solution.py:20
  52.7 21.9 %copy-start.6 = (bf16[1024,128]{1,0:T(8,128)(2,1)}, bf16[1024,128]{1,0:T(8,128)(2,1)S(1)}, u32[]{:S(2)}) copy-start(bf16[1024,128]{1,0:T(8,128)(2,1)S(1)} %collective-permute-done.1.refs_2_) | copy-start | bytes 786436
  52.7 21.9 %copy-start.8 = (bf16[1024,128]{1,0:T(8,128)(2,1)}, bf16[1024,128]{1,0:T(8,128)(2,1)S(1)}, u32[]{:S(2)}) copy-start(bf16[1024,128]{1,0:T(8,128)(2,1)S(1)} %collective-permute-done.refs_1_) | copy-start | bytes 786436
  53.5 22.0 %collective-permute-start.3 = (bf16[512,512]{1,0:T(8,128)(2,1)S(1)}, bf16[512,512]{1,0:T(8,128)(2,1)S(1)}, u32[]{:S(2)}, u32[]{:S(2)}) collective-permute-start(bf16[512,512]{1,0:T(8,128)(2,1)S(1)} %project.1.own_ref), channel_id=1, source_target_pairs={{0,2},{2,0},{1,3},{3,1},{4,6},{6,4},{5,7},{7,5},{8,10},{10,8},{9,1... | collective-permute-start | bytes 1572872 | tf_op jit(solution)/shard_map/ppermute | solution.py:185
  76.2 1.0 copy-start.1
  77.3 1.0 copy-start.11
  78.3 1.0 copy-start.13
  79.4 1.0 copy-start.15
  81.4 1.0 copy-start.19
  82.5 5.5 %copy-start.5 = (bf16[1024,128]{1,0:T(8,128)(2,1)S(1)}, bf16[1024,128]{1,0:T(8,128)(2,1)}, u32[]{:S(2)}) copy-start(bf16[1024,128]{1,0:T(8,128)(2,1)} %copy-done.4) | copy-start | bytes 786436
  82.5 5.5 %copy-start.7 = (bf16[1024,128]{1,0:T(8,128)(2,1)S(1)}, bf16[1024,128]{1,0:T(8,128)(2,1)}, u32[]{:S(2)}) copy-start(bf16[1024,128]{1,0:T(8,128)(2,1)} %copy-done.6) | copy-start | bytes 786436
  82.5 5.5 %copy-start.9 = (bf16[1024,128]{1,0:T(8,128)(2,1)S(1)}, bf16[1024,128]{1,0:T(8,128)(2,1)}, u32[]{:S(2)}) copy-start(bf16[1024,128]{1,0:T(8,128)(2,1)} %copy-done.8) | copy-start | bytes 786436
  84.9 3.1 %collective-permute-start.7 = (f32[512,512]{1,0:T(8,128)S(1)}, f32[512,512]{1,0:T(8,128)S(1)}, u32[]{:S(2)}, u32[]{:S(2)}) collective-permute-start(f32[512,512]{1,0:T(8,128)S(1)} %get-tuple-element.16), channel_id=1, source_target_pairs={{0,2},{2,0},{1,3},{3,1},{4,6},{6,4},{5,7},{7,5},{8,10},{10,8},{9,1... | collective-permute-start | bytes 3145736 | tf_op jit(solution)/shard_map/ppermute | solution.py:187
  (6 other events, 5.1 us)

commit v3 on v2

--- a/solution.py
+++ b/solution.py
@@ -13,9 +13,13 @@
 SIBLING = (1, 0, 3, 2)
 
 
+def swap(value):
+    return lax.ppermute(value, "core", [(0, 1), (1, 0)])
+
+
 def others(sibling, partner, diagonal):
     return [
-        lax.ppermute(sibling, "core", [(0, 1), (1, 0)]),
+        swap(sibling),
         lax.ppermute(partner, "zh", [(0, 1), (1, 0)]),
         lax.ppermute(diagonal, ("zh", "core"), [(0, 3), (1, 2), (2, 1), (3, 0)]),
     ]
@@ -47,13 +51,16 @@
                 zero = jnp.where(low, a, pltpu.roll(b, 64, 1))
                 one = jnp.where(low, pltpu.roll(a, 64, 1), b)
                 here = pl.ds(m * 128, 128)
-                out_refs[2 * far][:, here] = jnp.where(first, zero, one)
-                out_refs[2 * far + 1][:, here] = jnp.where(first, one, zero)
+                for ref, piece in (
+                    (out_refs[2 * far], jnp.where(first, zero, one)),
+                    (out_refs[2 * far + 1], jnp.where(first, one, zero)),
+                ):
+                    ref[:, here] = piece.astype(ref.dtype)
 
     return pl.pallas_call(
         kernel,
         grid=(steps,),
-        out_shape=[jax.ShapeDtypeStruct((points, width), F32)] * 4,
+        out_shape=[jax.ShapeDtypeStruct((points, width), kind) for kind in (F32, BF16, BF16, BF16)],
         in_specs=[pl.BlockSpec((points // steps, count), lambda k: (k, 0))],
         out_specs=[pl.BlockSpec((points // steps, width), lambda k: (k, 0))] * 4,
         compiler_params=params(8),
@@ -105,7 +112,7 @@
             pair += lax.dot_general(proj[...], panel_ref[here, sibs], nt, preferred_element_type=F32)
             weighted = jnp.concatenate(
                 [
-                    (scr_refs[j][:, here] * pair[j * points : (j + 1) * points]).astype(BF16)
+                    (scr_refs[j][:, here].astype(F32) * pair[j * points : (j + 1) * points]).astype(BF16)
                     for j in range(4)
                 ],
                 0,
@@ -168,10 +175,7 @@
     half = states // 2
     devices = lax.axis_size(TILE_VEC)
     own = psi_c[:, 0, :].T
-    plane = lax.axis_size(("y", "x"))
-    panel = lax.all_to_all(
-        jnp.broadcast_to(own[None], (plane, *own.shape)), ("y", "x"), split_axis=0, concat_axis=0, tiled=True
-    ).reshape(plane * own.shape[0], states)
+    panel = lax.all_gather(own, ("y", "x"), axis=0, tiled=True)
     packed = pack(screened)
     weights = [packed[0], *others(*packed[1:])]
     halves = trial[0].reshape(rows, 2, half).transpose(1, 0, 2)
@@ -180,11 +184,12 @@
     ).reshape(devices, rows, half)
     trial_half = lax.all_to_all(outgoing, TILE_VEC, split_axis=0, concat_axis=0, tiled=True)
     trial_half = trial_half.reshape(devices * rows, half)
-    lefts = [psi_v, *others(psi_v, psi_v, psi_v)]
+    partner = lax.ppermute(psi_v, "zh", [(0, 1), (1, 0)])
+    lefts = [psi_v, swap(psi_v), partner, swap(partner)]
     proj_own = project(trial_half, lefts)
-    proj_other = lax.ppermute(proj_own, "core", [(0, 1), (1, 0)])
+    proj_other = swap(proj_own)
     keep, send = direct(proj_own, proj_other, panel, weights)
-    got = lax.ppermute(send, "core", [(0, 1), (1, 0)])
+    got = swap(send)
     term = finish(lefts, keep, got)
     pieces = lax.all_to_all(
         term.reshape(devices, rows, half), TILE_VEC, split_axis=0, concat_axis=0, tiled=True

time: 117 us -> 105 us (0.90)
  blocking collectives: 55.9 us -> 25.7 us
  between operations: 0.13 us -> 13.4 us
  starting transfers between devices: 12.5 us -> 22.1 us
  local copies, waits for them, and re-layouts: 14.4 us -> 5 us
  waiting for transfers between devices: 27.1 us -> 32.1 us
    all_to_all x1 -> x0, blocking collectives: 29.8 us -> none  [shards(): lax.all_to_all(outgoing, TILE_VEC, split_axis=0, concat_axis=0, tiled=True)]
    ppermute x4 -> x6, waiting for transfers between devices: 2.29 us -> 19.7 us  [the longest x1 16.2 us: shards(): partner = lax.ppermute(psi_v, 'zh', [(0, 1), (1, 0)])]
    unnamed x42 -> x6, local copies, waits for them, and re-layouts: 11.9 us -> 3.19 us
    all_to_all x1, starting transfers between devices: 4.01 us -> 11.5 us  [shards(): lax.all_to_all(outgoing, TILE_VEC, split_axis=0, concat_axis=0, tiled=True)]
    ppermute x2 -> x1, waiting for transfers between devices: 12.7 us -> 5.51 us  [others(): lax.ppermute(partner, 'zh', [(0, 1), (1, 0)])]
    ppermute x2 -> x1, waiting for transfers between devices: 12.2 us -> 6.17 us  [others(): lax.ppermute(diagonal, ('zh', 'core'), [(0, 3), (1, 2), (2, 1), (3, 0)])]
    ppermute x4 -> x6, starting transfers between devices: 1.45 us -> 7.13 us  [the longest x5 3.77 us: swap(): return lax.ppermute(value, 'core', [(0, 1), (1, 0)])]
    ppermute x2 -> x1, starting transfers between devices: 2.98 us -> 1.15 us  [others(): lax.ppermute(partner, 'zh', [(0, 1), (1, 0)])]
  transfers between devices with their start and end apart: 9 -> 10, of which waited for: 5 -> 5; matrix products, arithmetic and copies ran while one was open for 0% -> 2% of each run, Pallas kernels for 1% -> 1%
where the time goes in v3:
time: 105 us; the launch traced here: 104 us
  waiting for transfers between devices  32.1 us (31%)
  blocking collectives  25.7 us (24%)
  starting transfers between devices  22.1 us (21%)
  between operations  13.4 us (13%)
  Pallas kernels  5.19 us (5%)
  local copies, waits for them, and re-layouts  5 us (5%)
    all_to_all x1, blocking collectives, shards(): lax.all_to_all(term.reshape(devices, rows, half), TILE_VEC, split_axis=0,...  25.7 us
    ppermute x1, waiting for transfers between devices, shards(): partner = lax.ppermute(psi_v, 'zh', [(0, 1), (1, 0)])  16.2 us
    all_to_all x1, starting transfers between devices, shards(): lax.all_to_all(outgoing, TILE_VEC, split_axis=0, concat_axis=0, tiled=True)  11.5 us
    ppermute x1, waiting for transfers between devices, others(): lax.ppermute(diagonal, ('zh', 'core'), [(0, 3), (1, 2), (2, 1), (3, 0)])  6.17 us
    ppermute x1, waiting for transfers between devices, others(): lax.ppermute(partner, 'zh', [(0, 1), (1, 0)])  5.51 us
    ppermute x5, starting transfers between devices, swap(): return lax.ppermute(value, 'core', [(0, 1), (1, 0)])  3.77 us
    ppermute x5, waiting for transfers between devices, swap(): return lax.ppermute(value, 'core', [(0, 1), (1, 0)])  3.45 us
    ppermute x1, starting transfers between devices, shards(): partner = lax.ppermute(psi_v, 'zh', [(0, 1), (1, 0)])  3.36 us
  transfers between devices with their start and end apart: 10, of which 5 were waited for; matrix products, arithmetic and copies ran while one was open for 2% of the time, Pallas kernels for 1%

profile of v3, /device:TPU:1, one launch (start us, length us, event | category | flops | bytes accessed | tf_op | source)
XLA Modules:
  0.0 104.3 jit_solution(4935890940635782203)
XLA Ops:
  6.5 0.7 all-gather.2.cloned.1.call-update
  7.3 1.8 %broadcast_in_dim.2 = bf16[32,2,2,8,512]{4,3,2,1,0:T(8,128)(2,1)} broadcast(bf16[2,8,512]{2,1,0:T(8,128)(2,1)} %bitcast.18), dimensions={1,3,4} | broadcast | bytes 1064960 | tf_op jit(solution)/shard_map/broadcast_in_dim | solution.py:182
  9.1 11.5 %all-to-all-start = ((bf16[128,8,512]{2,1,0:T(8,128)(2,1)}), bf16[128,8,512]{2,1,0:T(8,128)(2,1)S(1)}, u32[]{:S(2)}, u32[]{:S(2)}) async-start(bf16[128,8,512]{2,1,0:T(8,128)(2,1)} %bitcast.2), calls=%async_computation | async-start | bytes 2097152 | tf_op jit(solution)/shard_map/all_to_all | solution.py:185
  20.6 3.4 %collective-permute-start.1 = (bf16[1024,128]{1,0:T(8,128)(2,1)S(1)}, bf16[1024,128]{1,0:T(8,128)(2,1)S(1)}, u32[]{:S(2)}, u32[]{:S(2)}) collective-permute-start(bf16[1024,128]{1,0:T(8,128)(2,1)S(1)} %copy-done.2), channel_id=1, source_target_pairs={{0,64},{64,0},{1,65},{65,1},{2,66},{66,2},{3,67},{67,3},{4,68},{68... | collective-permute-start | bytes 786440 | tf_op jit(solution)/shard_map/ppermute | solution.py:187
  23.9 0.6 collective-permute-start
  24.6 16.2 %collective-permute-done.1.refs_2_ = bf16[1024,128]{1,0:T(8,128)(2,1)S(1)} collective-permute-done((bf16[1024,128]{1,0:T(8,128)(2,1)S(1)}, bf16[1024,128]{1,0:T(8,128)(2,1)S(1)}, u32[]{:S(2)}, u32[]{:S(2)}) %collective-permute-start.1) | collective-permute-done | bytes 262176 | tf_op jit(solution)/shard_map/ppermute | solution.py:187
  40.8 1.4 %collective-permute-start.2 = (bf16[1024,128]{1,0:T(8,128)(2,1)S(1)}, bf16[1024,128]{1,0:T(8,128)(2,1)S(1)}, u32[]{:S(2)}, u32[]{:S(2)}) collective-permute-start(bf16[1024,128]{1,0:T(8,128)(2,1)S(1)} %collective-permute-done.1.refs_2_), channel_id=1, source_target_pairs={{0,2},{2,0},{1,3},{3,1},{4,6},{6,4},{5,7},{7,5},{8,10},{10,8},{9,1... | collective-permute-start | bytes 786440 | tf_op jit(solution)/shard_map/ppermute | solution.py:17
  42.2 1.2 %collective-permute-done.2.refs_3_ = bf16[1024,128]{1,0:T(8,128)(2,1)S(1)} collective-permute-done((bf16[1024,128]{1,0:T(8,128)(2,1)S(1)}, bf16[1024,128]{1,0:T(8,128)(2,1)S(1)}, u32[]{:S(2)}, u32[]{:S(2)}) %collective-permute-start.2) | collective-permute-done | bytes 262176 | tf_op jit(solution)/shard_map/ppermute | solution.py:17
  43.4 0.7 project.1.own_ref
  44.1 0.5 collective-permute-start.3
  44.6 1.6 %copy-done = f32[128,4096]{1,0:T(8,128)S(1)} copy-done((f32[128,4096]{1,0:T(8,128)S(1)}, f32[128,4096]{1,0:T(8,128)}, u32[]{:S(2)}) %copy-start) | copy-done | bytes 2097176
  46.2 0.8 pack.1
  47.0 0.2 collective-permute-start.4
  47.2 1.2 %collective-permute-start.5 = (bf16[128,1024]{1,0:T(8,128)(2,1)S(1)}, bf16[128,1024]{1,0:T(8,128)(2,1)S(1)}, u32[]{:S(2)}, u32[]{:S(2)}) collective-permute-start(bf16[128,1024]{1,0:T(8,128)(2,1)S(1)} %get-tuple-element.13), channel_id=1, source_target_pairs={{0,64},{64,0},{1,65},{65,1},{2,66},{66,2},{3,67},{67,3},{4,68},{68... | collective-permute-start | bytes 786440 | tf_op jit(solution)/shard_map/ppermute | solution.py:23
  48.3 2.4 %collective-permute-start.6 = (bf16[128,1024]{1,0:T(8,128)(2,1)S(1)}, bf16[128,1024]{1,0:T(8,128)(2,1)S(1)}, u32[]{:S(2)}, u32[]{:S(2)}) collective-permute-start(bf16[128,1024]{1,0:T(8,128)(2,1)S(1)} %get-tuple-element.14), channel_id=1, source_target_pairs={{0,66},{2,64},{64,2},{66,0},{1,67},{3,65},{65,3},{67,1},{4,70},{6,... | collective-permute-start | bytes 786440 | tf_op jit(solution)/shard_map/ppermute | solution.py:24
  50.7 5.5 %collective-permute-done.5.refs_2_ = bf16[128,1024]{1,0:T(8,128)(2,1)S(1)} collective-permute-done((bf16[128,1024]{1,0:T(8,128)(2,1)S(1)}, bf16[128,1024]{1,0:T(8,128)(2,1)S(1)}, u32[]{:S(2)}, u32[]{:S(2)}) %collective-permute-start.5) | collective-permute-done | bytes 262176 | tf_op jit(solution)/shard_map/ppermute | solution.py:23
  56.2 6.2 %collective-permute-done.6.refs_3_ = bf16[128,1024]{1,0:T(8,128)(2,1)S(1)} collective-permute-done((bf16[128,1024]{1,0:T(8,128)(2,1)S(1)}, bf16[128,1024]{1,0:T(8,128)(2,1)S(1)}, u32[]{:S(2)}, u32[]{:S(2)}) %collective-permute-start.6) | collective-permute-done | bytes 262176 | tf_op jit(solution)/shard_map/ppermute | solution.py:24
  62.4 1.6 %copy-done.1 = bf16[1024,1024]{1,0:T(8,128)(2,1)S(1)} copy-done((bf16[1024,1024]{1,0:T(8,128)(2,1)S(1)}, bf16[1024,1024]{1,0:T(8,128)(2,1)}, u32[]{:S(2)}) %copy-start.1) | copy-done | bytes 2097176
  64.0 2.4 %direct.1 = (f32[512,512]{1,0:T(8,128)S(1)}, f32[512,512]{1,0:T(8,128)S(1)}) custom-call(bf16[512,512]{1,0:T(8,128)(2,1)S(1)} %project.1.own_ref, bf16[512,512]{1,0:T(8,128)(2,1)S(1)} %collective-permute-done.3.other_ref, bf16[1024,1024]{1,0:T(8,128)(2,1)S(1)} %copy-done.1, f32[128,1024]{1,0:T(8,128)S(1)} %get-tuple-element.11.refs_0_, ...), custom_call_target="tpu_custom_call" | custom-call | tf_op jit(solution)/shard_map/direct/pallas_call | solution.py:129
  66.4 1.0 collective-permute-start.7
  67.4 2.3 %collective-permute-done.7.refs_5_ = f32[512,512]{1,0:T(8,128)S(1)} collective-permute-done((f32[512,512]{1,0:T(8,128)S(1)}, f32[512,512]{1,0:T(8,128)S(1)}, u32[]{:S(2)}, u32[]{:S(2)}) %collective-permute-start.7) | collective-permute-done | bytes 1048608 | tf_op jit(solution)/shard_map/ppermute | solution.py:17
  69.7 1.3 %finish.1 = bf16[1024,512]{1,0:T(8,128)(2,1)S(1)} custom-call(bf16[1024,128]{1,0:T(8,128)(2,1)S(1)} %copy-done.2, bf16[1024,128]{1,0:T(8,128)(2,1)S(1)} %collective-permute-done.refs_1_, bf16[1024,128]{1,0:T(8,128)(2,1)S(1)} %collective-permute-done.1.refs_2_, bf16[1024,128]{1,0:T(8,128)(2,1)S(1)} %collective-permute-done.2.refs_3_, ...), custom_call_target="tpu_custom_call" | custom-call | tf_op jit(solution)/shard_map/finish/pallas_call | solution.py:158
  71.0 25.7 %all_to_all.10 = bf16[128,8,512]{2,1,0:T(8,128)(2,1)S(1)} all-to-all(bf16[128,8,512]{2,1,0:T(8,128)(2,1)S(1)} %bitcast.15), channel_id=1, replica_groups=mesh['zh'=2,'y'=4,'x'=4,'core'=2,'zl'=2] {'zh','y','x','core','zl'}, dimensions={0} | all-to-all | bytes 2097152 | tf_op jit(solution)/shard_map/all_to_all | solution.py:194
  96.7 0.8 convert_reduce_fusion
  (10 shorter events, 0.0 us)
Async XLA Ops:
  6.5 14.0 %copy-start.2 = (bf16[1024,128]{1,0:T(8,128)(2,1)S(1)}, bf16[1024,128]{1,0:T(8,128)(2,1)}, u32[]{:S(2)}) copy-start(bf16[1024,128]{1,0:T(8,128)(2,1)} %refs_0_.3) | copy-start | bytes 786436
  6.5 55.9 %all-gather.2.cloned.1.call-start = ((), (), s32[]{:S(2)}) async-start(), calls=%async_computation.2 | async-start | bytes 2228224 | tf_op jit(solution)/shard_map/all_gather | solution.py:178
  9.1 34.3 %all-to-all-start = ((bf16[128,8,512]{2,1,0:T(8,128)(2,1)}), bf16[128,8,512]{2,1,0:T(8,128)(2,1)S(1)}, u32[]{:S(2)}, u32[]{:S(2)}) async-start(bf16[128,8,512]{2,1,0:T(8,128)(2,1)} %bitcast.2), calls=%async_computation | async-start | bytes 2097152 | tf_op jit(solution)/shard_map/all_to_all | solution.py:185
  20.6 20.2 %collective-permute-start.1 = (bf16[1024,128]{1,0:T(8,128)(2,1)S(1)}, bf16[1024,128]{1,0:T(8,128)(2,1)S(1)}, u32[]{:S(2)}, u32[]{:S(2)}) collective-permute-start(bf16[1024,128]{1,0:T(8,128)(2,1)S(1)} %copy-done.2), channel_id=1, source_target_pairs={{0,64},{64,0},{1,65},{65,1},{2,66},{66,2},{3,67},{67,3},{4,68},{68... | collective-permute-start | bytes 786440 | tf_op jit(solution)/shard_map/ppermute | solution.py:187
  23.9 18.3 %collective-permute-start = (bf16[1024,128]{1,0:T(8,128)(2,1)S(1)}, bf16[1024,128]{1,0:T(8,128)(2,1)S(1)}, u32[]{:S(2)}, u32[]{:S(2)}) collective-permute-start(bf16[1024,128]{1,0:T(8,128)(2,1)S(1)} %copy-done.2), channel_id=1, source_target_pairs={{0,2},{2,0},{1,3},{3,1},{4,6},{6,4},{5,7},{7,5},{8,10},{10,8},{9,1... | collective-permute-start | bytes 786440 | tf_op jit(solution)/shard_map/ppermute | solution.py:17
  40.8 2.6 %collective-permute-start.2 = (bf16[1024,128]{1,0:T(8,128)(2,1)S(1)}, bf16[1024,128]{1,0:T(8,128)(2,1)S(1)}, u32[]{:S(2)}, u32[]{:S(2)}) collective-permute-start(bf16[1024,128]{1,0:T(8,128)(2,1)S(1)} %collective-permute-done.1.refs_2_), channel_id=1, source_target_pairs={{0,2},{2,0},{1,3},{3,1},{4,6},{6,4},{5,7},{7,5},{8,10},{10,8},{9,1... | collective-permute-start | bytes 786440 | tf_op jit(solution)/shard_map/ppermute | solution.py:17
  44.1 18.3 %collective-permute-start.3 = (bf16[512,512]{1,0:T(8,128)(2,1)S(1)}, bf16[512,512]{1,0:T(8,128)(2,1)S(1)}, u32[]{:S(2)}, u32[]{:S(2)}) collective-permute-start(bf16[512,512]{1,0:T(8,128)(2,1)S(1)} %project.1.own_ref), channel_id=1, source_target_pairs={{0,2},{2,0},{1,3},{3,1},{4,6},{6,4},{5,7},{7,5},{8,10},{10,8},{9,1... | collective-permute-start | bytes 1572872 | tf_op jit(solution)/shard_map/ppermute | solution.py:17
  44.6 1.6 %copy-start = (f32[128,4096]{1,0:T(8,128)S(1)}, f32[128,4096]{1,0:T(8,128)}, u32[]{:S(2)}) copy-start(f32[128,4096]{1,0:T(8,128)} %in_ref.1) | copy-start | bytes 6291460
  47.0 3.7 %collective-permute-start.4 = (bf16[128,1024]{1,0:T(8,128)(2,1)S(1)}, bf16[128,1024]{1,0:T(8,128)(2,1)S(1)}, u32[]{:S(2)}, u32[]{:S(2)}) collective-permute-start(bf16[128,1024]{1,0:T(8,128)(2,1)S(1)} %get-tuple-element.12), channel_id=1, source_target_pairs={{0,2},{2,0},{1,3},{3,1},{4,6},{6,4},{5,7},{7,5},{8,10},{10,8},{9,1... | collective-permute-start | bytes 786440 | tf_op jit(solution)/shard_map/ppermute | solution.py:17
  47.2 9.0 %collective-permute-start.5 = (bf16[128,1024]{1,0:T(8,128)(2,1)S(1)}, bf16[128,1024]{1,0:T(8,128)(2,1)S(1)}, u32[]{:S(2)}, u32[]{:S(2)}) collective-permute-start(bf16[128,1024]{1,0:T(8,128)(2,1)S(1)} %get-tuple-element.13), channel_id=1, source_target_pairs={{0,64},{64,0},{1,65},{65,1},{2,66},{66,2},{3,67},{67,3},{4,68},{68... | collective-permute-start | bytes 786440 | tf_op jit(solution)/shard_map/ppermute | solution.py:23
  48.3 14.0 %collective-permute-start.6 = (bf16[128,1024]{1,0:T(8,128)(2,1)S(1)}, bf16[128,1024]{1,0:T(8,128)(2,1)S(1)}, u32[]{:S(2)}, u32[]{:S(2)}) collective-permute-start(bf16[128,1024]{1,0:T(8,128)(2,1)S(1)} %get-tuple-element.14), channel_id=1, source_target_pairs={{0,66},{2,64},{64,2},{66,0},{1,67},{3,65},{65,3},{67,1},{4,70},{6,... | collective-permute-start | bytes 786440 | tf_op jit(solution)/shard_map/ppermute | solution.py:24
  62.4 1.6 %copy-start.1 = (bf16[1024,1024]{1,0:T(8,128)(2,1)S(1)}, bf16[1024,1024]{1,0:T(8,128)(2,1)}, u32[]{:S(2)}) copy-start(bf16[1024,1024]{1,0:T(8,128)(2,1)} %all-gather.2.cloned.1.call-done.panel_ref) | copy-start | bytes 6291460
  66.4 3.3 %collective-permute-start.7 = (f32[512,512]{1,0:T(8,128)S(1)}, f32[512,512]{1,0:T(8,128)S(1)}, u32[]{:S(2)}, u32[]{:S(2)}) collective-permute-start(f32[512,512]{1,0:T(8,128)S(1)} %get-tuple-element.16), channel_id=1, source_target_pairs={{0,2},{2,0},{1,3},{3,1},{4,6},{6,4},{5,7},{7,5},{8,10},{10,8},{9,1... | collective-permute-start | bytes 3145736 | tf_op jit(solution)/shard_map/ppermute | solution.py:17
Sparse Core Ops, SparseCore 0:
  9.5 52.3 all-gather.1

commit v4 on v3

--- a/solution.py
+++ b/solution.py
@@ -8,9 +8,16 @@
 
 TILE_VEC = ("zh", "y", "x", "core", "zl")
 TILE = ("zh", "y", "x", "core")
+PLANE = ("y", "x")
+ORDER = ("zh", "core", "zl", "y", "x")
+STEPS = (0, -1, 1, -2)
 F32 = jnp.float32
 BF16 = jnp.bfloat16
 SIBLING = (1, 0, 3, 2)
+
+
+def exchange(value, axes):
+    return lax.all_to_all(value, axes, split_axis=0, concat_axis=0, tiled=True)
 
 
 def swap(value):
@@ -27,6 +34,10 @@
 
 def vmem_spec():
     return pl.BlockSpec(memory_space=pltpu.VMEM)
+
+
+def hbm_spec():
+    return pl.BlockSpec(memory_space=pltpu.HBM)
 
 
 def params(mebibytes):
@@ -68,26 +79,38 @@
     )(screened)
 
 
-def project(trial_half, lefts):
-    points = lefts[0].shape[1]
-    cols = trial_half.shape[1]
-
-    def kernel(trial_ref, *refs):
-        out_ref = refs[4]
+def project(rounds, lefts):
+    states, points = lefts[0].shape
+    block = rounds[0].shape[0] // 2
+    cols = rounds[0].shape[1]
+
+    def kernel(*refs):
+        trial_refs, left_refs, (out_ref, trial) = refs[:4], refs[4:8], refs[8:]
+        core = lax.axis_index("core")
+        place = 2 * lax.axis_index("zh") + lax.axis_index("zl")
+        for k in range(4):
+            source = lax.rem(place + STEPS[k] + 4, 4)
+            for m in range(2):
+                owner = core if m == 0 else 1 - core
+                group = lax.div(source, 2) * 4 + owner * 2 + lax.rem(source, 2)
+                trial[pl.ds(pl.multiple_of(group * block, block), block), :] = trial_refs[k][
+                    m * block : (m + 1) * block, :
+                ]
         for k in range(4):
             part = lax.dot_general(
-                refs[k][...], trial_ref[...], (((0,), (0,)), ((), ())), preferred_element_type=F32
+                left_refs[k][...], trial[...], (((0,), (0,)), ((), ())), preferred_element_type=F32
             )
             out_ref[k * points : (k + 1) * points, :] = part.astype(BF16)
 
     return pl.pallas_call(
         kernel,
         out_shape=jax.ShapeDtypeStruct((4 * points, cols), BF16),
-        in_specs=[vmem_spec()] * 5,
+        in_specs=[vmem_spec()] * 8,
         out_specs=vmem_spec(),
+        scratch_shapes=[pltpu.VMEM((states, cols), BF16)],
         compiler_params=params(8),
         name="project",
-    )(trial_half, *lefts)
+    )(*rounds, *lefts)
 
 
 def direct(proj_own, proj_other, panel, weights):
@@ -96,20 +119,32 @@
     count = panel.shape[0]
     chunk = 512
 
-    def kernel(own_ref, other_ref, panel_ref, *refs):
-        scr_refs, (keep_ref, send_ref, proj) = refs[:4], refs[4:]
+    def kernel(own_hbm, other_hbm, panel_ref, *refs):
+        scr_hbm, (keep_ref, send_ref, own_ref, proj), refs = refs[:4], refs[4:8], refs[8:]
+        scr_refs, sems = refs[:4], refs[4]
         core = lax.axis_index("core")
         mine = pl.ds(pl.multiple_of(core * half, half), half)
         sibs = pl.ds(pl.multiple_of((1 - core) * half, half), half)
-        for k in range(4):
-            proj[k * points : (k + 1) * points, :] = other_ref[
-                SIBLING[k] * points : (SIBLING[k] + 1) * points, :
-            ]
+        first = [pltpu.make_async_copy(own_hbm, own_ref, sems.at[0])]
+        for k in range(4):
+            source = other_hbm.at[SIBLING[k] * points : (SIBLING[k] + 1) * points, :]
+            target = proj.at[k * points : (k + 1) * points, :]
+            first.append(pltpu.make_async_copy(source, target, sems.at[1 + k]))
+        later = [
+            pltpu.make_async_copy(scr_hbm[j], scr_refs[j], sems.at[5 + j]) for j in range(4)
+        ]
+        for copy in first + later:
+            copy.start()
+        for copy in first:
+            copy.wait()
         nt = (((1,), (1,)), ((), ()))
         for k in range(count // chunk):
             here = pl.ds(k * chunk, chunk)
             pair = lax.dot_general(own_ref[...], panel_ref[here, mine], nt, preferred_element_type=F32)
             pair += lax.dot_general(proj[...], panel_ref[here, sibs], nt, preferred_element_type=F32)
+            if k == 0:
+                for copy in later:
+                    copy.wait()
             weighted = jnp.concatenate(
                 [
                     (scr_refs[j][:, here].astype(F32) * pair[j * points : (j + 1) * points]).astype(BF16)
@@ -129,9 +164,14 @@
     return pl.pallas_call(
         kernel,
         out_shape=[jax.ShapeDtypeStruct((rows, half), F32)] * 2,
-        in_specs=[vmem_spec()] * 7,
+        in_specs=[hbm_spec(), hbm_spec(), vmem_spec()] + [hbm_spec()] * 4,
         out_specs=[vmem_spec()] * 2,
-        scratch_shapes=[pltpu.VMEM((rows, half), BF16)],
+        scratch_shapes=[
+            pltpu.VMEM((rows, half), BF16),
+            pltpu.VMEM((rows, half), BF16),
+            *(pltpu.VMEM(w.shape, w.dtype) for w in weights),
+            pltpu.SemaphoreType.DMA((9,)),
+        ],
         compiler_params=params(24),
         name="direct",
     )(proj_own, proj_other, panel, *weights)
@@ -170,32 +210,40 @@
     )(*lefts, keep, got)
 
 
+def ring(value, by):
+    return lax.ppermute(value, ("zh", "zl"), [(k, (k + by) % 4) for k in range(4)])
+
+
+def to_all(value):
+    copies = jnp.broadcast_to(value[None], (lax.axis_size(PLANE), *value.shape))
+    return copies
+
+
 def shards(trial, psi_v, psi_c, screened):
     rows, states = trial.shape[1:]
     half = states // 2
-    devices = lax.axis_size(TILE_VEC)
-    own = psi_c[:, 0, :].T
-    panel = lax.all_gather(own, ("y", "x"), axis=0, tiled=True)
+    devices = lax.axis_size(ORDER)
+    core = lax.axis_index("core")
+    left = psi_v.reshape(2, 4, 4, 2, 2, rows, -1).transpose(0, 3, 4, 1, 2, 5, 6).reshape(psi_v.shape)
+    level = exchange(to_all(trial[0]), PLANE).reshape(-1, states)
+    outgoing, level = lax.optimization_barrier((to_all(psi_c[:, 0, :].T), level))
+    panel = exchange(outgoing, PLANE).reshape(-1, states)
     packed = pack(screened)
     weights = [packed[0], *others(*packed[1:])]
-    halves = trial[0].reshape(rows, 2, half).transpose(1, 0, 2)
-    outgoing = jnp.broadcast_to(
-        halves[None, :, None], (devices // 4, 2, 2, rows, half)
-    ).reshape(devices, rows, half)
-    trial_half = lax.all_to_all(outgoing, TILE_VEC, split_axis=0, concat_axis=0, tiled=True)
-    trial_half = trial_half.reshape(devices * rows, half)
-    partner = lax.ppermute(psi_v, "zh", [(0, 1), (1, 0)])
-    lefts = [psi_v, swap(psi_v), partner, swap(partner)]
-    proj_own = project(trial_half, lefts)
+    partner = lax.ppermute(left, "zh", [(0, 1), (1, 0)])
+    lefts = [left, swap(left), partner, swap(partner)]
+    mine = lax.dynamic_slice_in_dim(level, core * half, half, 1)
+    sent = lax.dynamic_slice_in_dim(level, (1 - core) * half, half, 1)
+    pieces = jnp.concatenate([mine, swap(sent)], 0)
+    rounds = [pieces, ring(pieces, 1), ring(pieces, -1), ring(pieces, 2)]
+    proj_own = project(rounds, lefts)
     proj_other = swap(proj_own)
     keep, send = direct(proj_own, proj_other, panel, weights)
     got = swap(send)
     term = finish(lefts, keep, got)
-    pieces = lax.all_to_all(
-        term.reshape(devices, rows, half), TILE_VEC, split_axis=0, concat_axis=0, tiled=True
-    )
-    pieces = pieces.reshape(devices // 4, 2, 2, rows, half).astype(F32)
-    total = jnp.sum(pieces, axis=(0, 2))
+    parts = exchange(term.reshape(devices, rows, half), ORDER)
+    parts = parts.reshape(2, 2, 2, -1, rows, half).astype(F32)
+    total = jnp.sum(parts, axis=(0, 2, 3))
     return total.transpose(1, 0, 2).reshape(1, rows, states)
 
 

time: 105 us -> 110 us (1.048)
  blocking collectives: 25.7 us -> 42.4 us
  between operations: 13.4 us -> 0.12 us
  local copies, waits for them, and re-layouts: 5 us -> 12 us
  waiting for transfers between devices: 32.1 us -> 26.1 us
  Pallas kernels: 5.19 us -> 6.34 us
    all_to_all x1 -> x2, blocking collectives: 25.7 us -> 42.4 us  [exchange(): return lax.all_to_all(value, axes, split_axis=0, concat_axis=0, tiled=True)]
    all_to_all x1, starting transfers between devices: 11.5 us -> 3.85 us  [exchange(): return lax.all_to_all(value, axes, split_axis=0, concat_axis=0, tiled=True)]
    unnamed x6 -> x28, local copies, waits for them, and re-layouts: 3.19 us -> 8.66 us
    ppermute x1 -> x4, starting transfers between devices: 3.36 us -> 8.19 us  [the longest x3 4.51 us: ring(): lax.ppermute(value, ('zh', 'zl'), [(k, (k + by) % 4) for k in range(4)])]
    ppermute x1 -> x4, waiting for transfers between devices: 16.2 us -> 13.3 us  [the longest x3 11.4 us: ring(): lax.ppermute(value, ('zh', 'zl'), [(k, (k + by) % 4) for k in range(4)])]
    ppermute x5 -> x6, starting transfers between devices: 3.77 us -> 6.32 us  [swap(): return lax.ppermute(value, 'core', [(0, 1), (1, 0)])]
    broadcast_in_dim x1 -> x2, local copies, waits for them, and re-layouts: 1.82 us -> 3.24 us  [to_all(): copies = jnp.broadcast_to(value[None], (lax.axis_size(PLANE), *value.shape))]
    ppermute x5 -> x6, waiting for transfers between devices: 3.45 us -> 2.66 us  [swap(): return lax.ppermute(value, 'core', [(0, 1), (1, 0)])]
  transfers between devices with their start and end apart: 10 -> 13, of which waited for: 5 -> 6; matrix products, arithmetic and copies ran while one was open for 2% -> 0% of each run, Pallas kernels for 1% -> 1%
where the time goes in v4:
time: 110 us
  blocking collectives  42.4 us (39%)
  waiting for transfers between devices  26.1 us (24%)
  starting transfers between devices  21.9 us (20%)
  local copies, waits for them, and re-layouts  12 us (11%)
  Pallas kernels  6.34 us (6%)
    all_to_all x2, blocking collectives, exchange(): return lax.all_to_all(value, axes, split_axis=0, concat_axis=0, tiled=True)  42.4 us
    ppermute x3, waiting for transfers between devices, ring(): lax.ppermute(value, ('zh', 'zl'), [(k, (k + by) % 4) for k in range(4)])  11.4 us
    unnamed x28, local copies, waits for them, and re-layouts  8.66 us
    ppermute x6, starting transfers between devices, swap(): return lax.ppermute(value, 'core', [(0, 1), (1, 0)])  6.32 us
    ppermute x1, waiting for transfers between devices, others(): lax.ppermute(diagonal, ('zh', 'core'), [(0, 3), (1, 2), (2, 1), (3, 0)])  5.54 us
    ppermute x1, waiting for transfers between devices, others(): lax.ppermute(partner, 'zh', [(0, 1), (1, 0)])  4.6 us
    ppermute x3, starting transfers between devices, ring(): lax.ppermute(value, ('zh', 'zl'), [(k, (k + by) % 4) for k in range(4)])  4.51 us
    all_to_all x1, starting transfers between devices, exchange(): return lax.all_to_all(value, axes, split_axis=0, concat_axis=0, tiled=True)  3.85 us
  transfers between devices with their start and end apart: 13, of which 6 were waited for; matrix products, arithmetic and copies ran while one was open for 0% of the time, Pallas kernels for 1%

profile of v4, /device:TPU:1, one launch (start us, length us, event | category | flops | bytes accessed | tf_op | source)
XLA Modules:
  0.0 109.7 jit_solution(10376732699627014697)
XLA Ops:
  0.7 14.9 %all_to_all.15 = bf16[16,8,1024]{2,1,0:T(8,128)(2,1)S(1)} all-to-all(bf16[16,8,1024]{2,1,0:T(8,128)(2,1)S(1)} %broadcast_in_dim.15), channel_id=1, replica_groups=mesh['zh'=2,'y'=4,'x'=4,'core'=2,'zl'=2] {'y','x'}, dimensions={0} | all-to-all | bytes 524288 | tf_op jit(solution)/shard_map/all_to_all | solution.py:20
  15.7 2.5 %broadcast_in_dim.6 = bf16[16,64,1024]{2,1,0:T(8,128)(2,1)} broadcast(bf16[64,1024]{1,0:T(8,128)(2,1)} %bitcast.25), dimensions={1,2} | broadcast | bytes 2228224 | tf_op jit(solution)/shard_map/broadcast_in_dim | solution.py:218
  18.2 3.8 %all-to-all-start.1 = ((bf16[16,64,1024]{2,1,0:T(8,128)(2,1)}), bf16[16,64,1024]{2,1,0:T(8,128)(2,1)S(1)}, u32[]{:S(2)}, u32[]{:S(2)}) async-start(bf16[16,64,1024]{2,1,0:T(8,128)(2,1)} %broadcast_in_dim.6), calls=%async_computation.1 | async-start | bytes 4194304 | tf_op jit(solution)/shard_map/all_to_all | solution.py:20
  22.1 3.7 %collective-permute-start.1 = (bf16[1024,128]{1,0:T(8,128)(2,1)S(1)}, bf16[1024,128]{1,0:T(8,128)(2,1)S(1)}, u32[]{:S(2)}, u32[]{:S(2)}) collective-permute-start(bf16[1024,128]{1,0:T(8,128)(2,1)S(1)} %bitcast.18), channel_id=1, source_target_pairs={{0,64},{64,0},{1,65},{65,1},{2,66},{66,2},{3,67},{67,3},{4,68},{68... | collective-permute-start | bytes 786440 | tf_op jit(solution)/shard_map/ppermute | solution.py:233
  25.8 2.5 %collective-permute-start.3 = (bf16[128,512]{1,0:T(8,128)(2,1)S(1)}, bf16[128,512]{1,0:T(8,128)(2,1)S(1)}, u32[]{:S(2)}, u32[]{:S(2)}) collective-permute-start(bf16[128,512]{1,0:T(8,128)(2,1)S(1)} %get-tuple-element.22), channel_id=1, source_target_pairs={{0,2},{2,0},{1,3},{3,1},{4,6},{6,4},{5,7},{7,5},{8,10},{10,8},{9,1... | collective-permute-start | bytes 393224 | tf_op jit(solution)/shard_map/ppermute | solution.py:24
  28.4 1.9 %collective-permute-done.1.refs_6_.refs_2_ = bf16[1024,128]{1,0:T(8,128)(2,1)S(1)} collective-permute-done((bf16[1024,128]{1,0:T(8,128)(2,1)S(1)}, bf16[1024,128]{1,0:T(8,128)(2,1)S(1)}, u32[]{:S(2)}, u32[]{:S(2)}) %collective-permute-start.1) | collective-permute-done | bytes 262176 | tf_op jit(solution)/shard_map/ppermute | solution.py:233
  30.3 2.7 %collective-permute-start.2 = (bf16[1024,128]{1,0:T(8,128)(2,1)S(1)}, bf16[1024,128]{1,0:T(8,128)(2,1)S(1)}, u32[]{:S(2)}, u32[]{:S(2)}) collective-permute-start(bf16[1024,128]{1,0:T(8,128)(2,1)S(1)} %collective-permute-done.1.refs_6_.refs_2_), channel_id=1, source_target_pairs={{0,2},{2,0},{1,3},{3,1},{4,6},{6,4},{5,7},{7,5},{8,10},{10,8},{9,1... | collective-permute-start | bytes 786440 | tf_op jit(solution)/shard_map/ppermute | solution.py:24
  33.1 3.0 %collective-permute-start.6 = (bf16[256,512]{1,0:T(8,128)(2,1)S(1)}, bf16[256,512]{1,0:T(8,128)(2,1)S(1)}, u32[]{:S(2)}, u32[]{:S(2)}) collective-permute-start(bf16[256,512]{1,0:T(8,128)(2,1)S(1)} %pad_maximum_fusion.refs_0_), channel_id=1, source_target_pairs={{0,64},{1,65},{64,0},{65,1},{2,66},{3,67},{66,2},{67,3},{4,68},{5,... | collective-permute-start | bytes 786440 | tf_op jit(solution)/shard_map/ppermute | solution.py:214
  36.5 1.0 collective-permute-start.4
  37.6 5.0 %collective-permute-done.6.refs_3_ = bf16[256,512]{1,0:T(8,128)(2,1)S(1)} collective-permute-done((bf16[256,512]{1,0:T(8,128)(2,1)S(1)}, bf16[256,512]{1,0:T(8,128)(2,1)S(1)}, u32[]{:S(2)}, u32[]{:S(2)}) %collective-permute-start.6) | collective-permute-done | bytes 262176 | tf_op jit(solution)/shard_map/ppermute | solution.py:214
  42.6 6.4 %collective-permute-done.5.refs_2_ = bf16[256,512]{1,0:T(8,128)(2,1)S(1)} collective-permute-done((bf16[256,512]{1,0:T(8,128)(2,1)S(1)}, bf16[256,512]{1,0:T(8,128)(2,1)S(1)}, u32[]{:S(2)}, u32[]{:S(2)}) %collective-permute-start.5) | collective-permute-done | bytes 262176 | tf_op jit(solution)/shard_map/ppermute | solution.py:214
  52.3 2.2 %collective-permute-start.9 = (bf16[128,1024]{1,0:T(8,128)(2,1)S(1)}, bf16[128,1024]{1,0:T(8,128)(2,1)S(1)}, u32[]{:S(2)}, u32[]{:S(2)}) collective-permute-start(bf16[128,1024]{1,0:T(8,128)(2,1)S(1)} %get-tuple-element.17), channel_id=1, source_target_pairs={{0,64},{64,0},{1,65},{65,1},{2,66},{66,2},{3,67},{67,3},{4,68},{68... | collective-permute-start | bytes 786440 | tf_op jit(solution)/shard_map/ppermute | solution.py:30
  54.5 1.4 %collective-permute-start.10 = (bf16[128,1024]{1,0:T(8,128)(2,1)S(1)}, bf16[128,1024]{1,0:T(8,128)(2,1)S(1)}, u32[]{:S(2)}, u32[]{:S(2)}) collective-permute-start(bf16[128,1024]{1,0:T(8,128)(2,1)S(1)} %get-tuple-element.18), channel_id=1, source_target_pairs={{0,66},{2,64},{64,2},{66,0},{1,67},{3,65},{65,3},{67,1},{4,70},{6,... | collective-permute-start | bytes 786440 | tf_op jit(solution)/shard_map/ppermute | solution.py:31
  56.7 4.6 %collective-permute-done.9.refs_2_ = bf16[128,1024]{1,0:T(8,128)(2,1)S(1)} collective-permute-done((bf16[128,1024]{1,0:T(8,128)(2,1)S(1)}, bf16[128,1024]{1,0:T(8,128)(2,1)S(1)}, u32[]{:S(2)}, u32[]{:S(2)}) %collective-permute-start.9) | collective-permute-done | bytes 262176 | tf_op jit(solution)/shard_map/ppermute | solution.py:30
  62.0 5.5 %collective-permute-done.10.refs_3_ = bf16[128,1024]{1,0:T(8,128)(2,1)S(1)} collective-permute-done((bf16[128,1024]{1,0:T(8,128)(2,1)S(1)}, bf16[128,1024]{1,0:T(8,128)(2,1)S(1)}, u32[]{:S(2)}, u32[]{:S(2)}) %collective-permute-start.10) | collective-permute-done | bytes 262176 | tf_op jit(solution)/shard_map/ppermute | solution.py:31
  69.0 1.0 copy-done.4
  70.1 1.0 copy-done.6
  71.1 0.9 copy-done.8
  72.1 0.9 copy-done.10
  73.0 0.9 copy-done.12
  74.0 3.4 %direct.1 = (f32[512,512]{1,0:T(8,128)S(1)}, f32[512,512]{1,0:T(8,128)S(1)}) custom-call(bf16[512,512]{1,0:T(8,128)(2,1)S(1)} %project.1.own_hbm, bf16[512,512]{1,0:T(8,128)(2,1)S(1)} %copy-done.4, bf16[1024,1024]{1,0:T(8,128)(2,1)S(1)} %bitcast.16, f32[128,1024]{1,0:T(8,128)S(1)} %copy-done.6, bf16[128,1024]{1,0:T(8,128)(2,1)S(1)} %copy-done.8, ...), custom_call_target="tpu_custom_call" | custom-call | tf_op jit(solution)/shard_map/direct/pallas_call | solution.py:164
  77.5 2.6 %collective-permute-done.11.refs_5_ = f32[512,512]{1,0:T(8,128)S(1)} collective-permute-done((f32[512,512]{1,0:T(8,128)S(1)}, f32[512,512]{1,0:T(8,128)S(1)}, u32[]{:S(2)}, u32[]{:S(2)}) %collective-permute-start.11) | collective-permute-done | bytes 1048608 | tf_op jit(solution)/shard_map/ppermute | solution.py:24
  80.1 1.3 %finish.1 = bf16[1024,512]{1,0:T(8,128)(2,1)S(1)} custom-call(bf16[1024,128]{1,0:T(8,128)(2,1)S(1)} %bitcast.21, bf16[1024,128]{1,0:T(8,128)(2,1)S(1)} %collective-permute-done.refs_5_.refs_1_, bf16[1024,128]{1,0:T(8,128)(2,1)S(1)} %collective-permute-done.1.refs_6_.refs_2_, bf16[1024,128]{1,0:T(8,128)(2,1)S(1)} %copy-done.2, ...), custom_call_target="tpu_custom_call" | custom-call | tf_op jit(solution)/shard_map/finish/pallas_call | solution.py:198
  81.5 27.5 %all_to_all.16 = bf16[128,8,512]{2,1,0:T(8,128)(2,1)S(1)} all-to-all(bf16[128,8,512]{2,1,0:T(8,128)(2,1)S(1)} %bitcast.17), channel_id=1, replica_groups=mesh['zh'=2,'y'=4,'x'=4,'core'=2,'zl'=2] {'zh','core','zl','y','x'}, dimensions={0} | all-to-all | bytes 2097152 | tf_op jit(solution)/shard_map/all_to_all | solution.py:20
  (42 shorter events, 8.5 us)
Async XLA Ops:
  18.2 3.9 %copy-start.13 = (bf16[1024,128]{1,0:T(8,128)(2,1)S(1)}, bf16[1024,128]{1,0:T(8,128)(2,1)}, u32[]{:S(2)}) copy-start(bf16[1024,128]{1,0:T(8,128)(2,1)} %param.5) | copy-start | bytes 786436
  18.2 50.8 %all-to-all-start.1 = ((bf16[16,64,1024]{2,1,0:T(8,128)(2,1)}), bf16[16,64,1024]{2,1,0:T(8,128)(2,1)S(1)}, u32[]{:S(2)}, u32[]{:S(2)}) async-start(bf16[16,64,1024]{2,1,0:T(8,128)(2,1)} %broadcast_in_dim.6), calls=%async_computation.1 | async-start | bytes 4194304 | tf_op jit(solution)/shard_map/all_to_all | solution.py:20
  22.1 8.2 %collective-permute-start.1 = (bf16[1024,128]{1,0:T(8,128)(2,1)S(1)}, bf16[1024,128]{1,0:T(8,128)(2,1)S(1)}, u32[]{:S(2)}, u32[]{:S(2)}) collective-permute-start(bf16[1024,128]{1,0:T(8,128)(2,1)S(1)} %bitcast.18), channel_id=1, source_target_pairs={{0,64},{64,0},{1,65},{65,1},{2,66},{66,2},{3,67},{67,3},{4,68},{68... | collective-permute-start | bytes 786440 | tf_op jit(solution)/shard_map/ppermute | solution.py:233
  25.8 24.9 %copy-start = (f32[128,4096]{1,0:T(8,128)S(1)}, f32[128,4096]{1,0:T(8,128)}, u32[]{:S(2)}) copy-start(f32[128,4096]{1,0:T(8,128)} %in_ref.1) | copy-start | bytes 6291460
  25.8 7.2 %collective-permute-start.3 = (bf16[128,512]{1,0:T(8,128)(2,1)S(1)}, bf16[128,512]{1,0:T(8,128)(2,1)S(1)}, u32[]{:S(2)}, u32[]{:S(2)}) collective-permute-start(bf16[128,512]{1,0:T(8,128)(2,1)S(1)} %get-tuple-element.22), channel_id=1, source_target_pairs={{0,2},{2,0},{1,3},{3,1},{4,6},{6,4},{5,7},{7,5},{8,10},{10,8},{9,1... | collective-permute-start | bytes 393224 | tf_op jit(solution)/shard_map/ppermute | solution.py:24
  28.3 9.3 %collective-permute-start = (bf16[1024,128]{1,0:T(8,128)(2,1)S(1)}, bf16[1024,128]{1,0:T(8,128)(2,1)S(1)}, u32[]{:S(2)}, u32[]{:S(2)}) collective-permute-start(bf16[1024,128]{1,0:T(8,128)(2,1)S(1)} %bitcast.19), channel_id=1, source_target_pairs={{0,2},{2,0},{1,3},{3,1},{4,6},{6,4},{5,7},{7,5},{8,10},{10,8},{9,1... | collective-permute-start | bytes 786440 | tf_op jit(solution)/shard_map/ppermute | solution.py:24
  30.3 7.3 %collective-permute-start.2 = (bf16[1024,128]{1,0:T(8,128)(2,1)S(1)}, bf16[1024,128]{1,0:T(8,128)(2,1)S(1)}, u32[]{:S(2)}, u32[]{:S(2)}) collective-permute-start(bf16[1024,128]{1,0:T(8,128)(2,1)S(1)} %collective-permute-done.1.refs_6_.refs_2_), channel_id=1, source_target_pairs={{0,2},{2,0},{1,3},{3,1},{4,6},{6,4},{5,7},{7,5},{8,10},{10,8},{9,1... | collective-permute-start | bytes 786440 | tf_op jit(solution)/shard_map/ppermute | solution.py:24
  33.1 9.6 %collective-permute-start.6 = (bf16[256,512]{1,0:T(8,128)(2,1)S(1)}, bf16[256,512]{1,0:T(8,128)(2,1)S(1)}, u32[]{:S(2)}, u32[]{:S(2)}) collective-permute-start(bf16[256,512]{1,0:T(8,128)(2,1)S(1)} %pad_maximum_fusion.refs_0_), channel_id=1, source_target_pairs={{0,64},{1,65},{64,0},{65,1},{2,66},{3,67},{66,2},{67,3},{4,68},{5,... | collective-permute-start | bytes 786440 | tf_op jit(solution)/shard_map/ppermute | solution.py:214
  36.1 12.9 %collective-permute-start.5 = (bf16[256,512]{1,0:T(8,128)(2,1)S(1)}, bf16[256,512]{1,0:T(8,128)(2,1)S(1)}, u32[]{:S(2)}, u32[]{:S(2)}) collective-permute-start(bf16[256,512]{1,0:T(8,128)(2,1)S(1)} %pad_maximum_fusion.refs_0_), channel_id=1, source_target_pairs={{0,65},{1,0},{64,1},{65,64},{2,67},{3,2},{66,3},{67,66},{4,69},{5,... | collective-permute-start | bytes 786440 | tf_op jit(solution)/shard_map/ppermute | solution.py:214
  36.5 12.4 %collective-permute-start.4 = (bf16[256,512]{1,0:T(8,128)(2,1)S(1)}, bf16[256,512]{1,0:T(8,128)(2,1)S(1)}, u32[]{:S(2)}, u32[]{:S(2)}) collective-permute-start(bf16[256,512]{1,0:T(8,128)(2,1)S(1)} %pad_maximum_fusion.refs_0_), channel_id=1, source_target_pairs={{0,1},{1,64},{64,65},{65,0},{2,3},{3,66},{66,67},{67,2},{4,5},{5,6... | collective-permute-start | bytes 786440 | tf_op jit(solution)/shard_map/ppermute | solution.py:214
  37.6 13.9 %copy-start.1 = (bf16[1024,128]{1,0:T(8,128)(2,1)}, bf16[1024,128]{1,0:T(8,128)(2,1)S(1)}, u32[]{:S(2)}) copy-start(bf16[1024,128]{1,0:T(8,128)(2,1)S(1)} %collective-permute-done.2.refs_7_.refs_3_) | copy-start | bytes 786436
  49.8 18.4 %collective-permute-start.7 = (bf16[512,512]{1,0:T(8,128)(2,1)S(1)}, bf16[512,512]{1,0:T(8,128)(2,1)S(1)}, u32[]{:S(2)}, u32[]{:S(2)}) collective-permute-start(bf16[512,512]{1,0:T(8,128)(2,1)S(1)} %project.1.own_hbm), channel_id=1, source_target_pairs={{0,2},{2,0},{1,3},{3,1},{4,6},{6,4},{5,7},{7,5},{8,10},{10,8},{9,1... | collective-permute-start | bytes 1572872 | tf_op jit(solution)/shard_map/ppermute | solution.py:24
  51.5 0.8 copy-start.5
  52.3 3.6 %collective-permute-start.8 = (bf16[128,1024]{1,0:T(8,128)(2,1)S(1)}, bf16[128,1024]{1,0:T(8,128)(2,1)S(1)}, u32[]{:S(2)}, u32[]{:S(2)}) collective-permute-start(bf16[128,1024]{1,0:T(8,128)(2,1)S(1)} %get-tuple-element.16), channel_id=1, source_target_pairs={{0,2},{2,0},{1,3},{3,1},{4,6},{6,4},{5,7},{7,5},{8,10},{10,8},{9,1... | collective-permute-start | bytes 786440 | tf_op jit(solution)/shard_map/ppermute | solution.py:24
  52.3 8.9 %collective-permute-start.9 = (bf16[128,1024]{1,0:T(8,128)(2,1)S(1)}, bf16[128,1024]{1,0:T(8,128)(2,1)S(1)}, u32[]{:S(2)}, u32[]{:S(2)}) collective-permute-start(bf16[128,1024]{1,0:T(8,128)(2,1)S(1)} %get-tuple-element.17), channel_id=1, source_target_pairs={{0,64},{64,0},{1,65},{65,1},{2,66},{66,2},{3,67},{67,3},{4,68},{68... | collective-permute-start | bytes 786440 | tf_op jit(solution)/shard_map/ppermute | solution.py:30
  54.5 13.0 %collective-permute-start.10 = (bf16[128,1024]{1,0:T(8,128)(2,1)S(1)}, bf16[128,1024]{1,0:T(8,128)(2,1)S(1)}, u32[]{:S(2)}, u32[]{:S(2)}) collective-permute-start(bf16[128,1024]{1,0:T(8,128)(2,1)S(1)} %get-tuple-element.18), channel_id=1, source_target_pairs={{0,66},{2,64},{64,2},{66,0},{1,67},{3,65},{65,3},{67,1},{4,70},{6,... | collective-permute-start | bytes 786440 | tf_op jit(solution)/shard_map/ppermute | solution.py:31
  68.2 0.8 copy-start.3
  69.0 1.0 copy-start.4
  70.1 1.0 copy-start.6
  71.1 0.9 copy-start.8
  72.0 0.9 copy-start.10
  73.0 0.9 copy-start.12
  74.0 6.2 %copy-start.2 = (bf16[1024,128]{1,0:T(8,128)(2,1)S(1)}, bf16[1024,128]{1,0:T(8,128)(2,1)}, u32[]{:S(2)}) copy-start(bf16[1024,128]{1,0:T(8,128)(2,1)} %copy-done.1) | copy-start | bytes 786436
  77.4 2.7 %collective-permute-start.11 = (f32[512,512]{1,0:T(8,128)S(1)}, f32[512,512]{1,0:T(8,128)S(1)}, u32[]{:S(2)}, u32[]{:S(2)}) collective-permute-start(f32[512,512]{1,0:T(8,128)S(1)} %get-tuple-element.20), channel_id=1, source_target_pairs={{0,2},{2,0},{1,3},{3,1},{4,6},{6,4},{5,7},{7,5},{8,10},{10,8},{9,1... | collective-permute-start | bytes 3145736 | tf_op jit(solution)/shard_map/ppermute | solution.py:24
  (3 other events, 2.1 us)

commit v5 on v4

--- a/solution.py
+++ b/solution.py
@@ -116,12 +116,12 @@
 def direct(proj_own, proj_other, panel, weights):
     rows, half = proj_own.shape
     points = rows // 4
-    count = panel.shape[0]
-    chunk = 512
-
-    def kernel(own_hbm, other_hbm, panel_ref, *refs):
-        scr_hbm, (keep_ref, send_ref, own_ref, proj), refs = refs[:4], refs[4:8], refs[8:]
-        scr_refs, sems = refs[:4], refs[4]
+    count, states = panel.shape
+    chunk = 256
+
+    def kernel(own_hbm, other_hbm, panel_hbm, *refs):
+        scr_hbm, (keep_ref, send_ref, own_ref, proj, panel_ref), refs = refs[:4], refs[4:9], refs[9:]
+        scr_refs, (sems, chunk_sems) = refs[:4], refs[4:]
         core = lax.axis_index("core")
         mine = pl.ds(pl.multiple_of(core * half, half), half)
         sibs = pl.ds(pl.multiple_of((1 - core) * half, half), half)
@@ -130,21 +130,30 @@
             source = other_hbm.at[SIBLING[k] * points : (SIBLING[k] + 1) * points, :]
             target = proj.at[k * points : (k + 1) * points, :]
             first.append(pltpu.make_async_copy(source, target, sems.at[1 + k]))
-        later = [
-            pltpu.make_async_copy(scr_hbm[j], scr_refs[j], sems.at[5 + j]) for j in range(4)
-        ]
-        for copy in first + later:
-            copy.start()
+        chunks = []
+        for k in range(count // chunk):
+            here = pl.ds(k * chunk, chunk)
+            chunks.append(
+                [pltpu.make_async_copy(panel_hbm.at[here, :], panel_ref.at[here, :], chunk_sems.at[k, 0])]
+                + [
+                    pltpu.make_async_copy(
+                        scr_hbm[j].at[:, here], scr_refs[j].at[:, here], chunk_sems.at[k, 1 + j]
+                    )
+                    for j in range(4)
+                ]
+            )
+        for copies in (first, *chunks):
+            for copy in copies:
+                copy.start()
         for copy in first:
             copy.wait()
         nt = (((1,), (1,)), ((), ()))
         for k in range(count // chunk):
             here = pl.ds(k * chunk, chunk)
+            for copy in chunks[k]:
+                copy.wait()
             pair = lax.dot_general(own_ref[...], panel_ref[here, mine], nt, preferred_element_type=F32)
             pair += lax.dot_general(proj[...], panel_ref[here, sibs], nt, preferred_element_type=F32)
-            if k == 0:
-                for copy in later:
-                    copy.wait()
             weighted = jnp.concatenate(
                 [
                     (scr_refs[j][:, here].astype(F32) * pair[j * points : (j + 1) * points]).astype(BF16)
@@ -164,15 +173,17 @@
     return pl.pallas_call(
         kernel,
         out_shape=[jax.ShapeDtypeStruct((rows, half), F32)] * 2,
-        in_specs=[hbm_spec(), hbm_spec(), vmem_spec()] + [hbm_spec()] * 4,
+        in_specs=[hbm_spec()] * 7,
         out_specs=[vmem_spec()] * 2,
         scratch_shapes=[
             pltpu.VMEM((rows, half), BF16),
             pltpu.VMEM((rows, half), BF16),
+            pltpu.VMEM((count, states), BF16),
             *(pltpu.VMEM(w.shape, w.dtype) for w in weights),
-            pltpu.SemaphoreType.DMA((9,)),
+            pltpu.SemaphoreType.DMA((5,)),
+            pltpu.SemaphoreType.DMA((count // chunk, 5)),
         ],
-        compiler_params=params(24),
+        compiler_params=params(58),
         name="direct",
     )(proj_own, proj_other, panel, *weights)
 
@@ -225,12 +236,15 @@
     devices = lax.axis_size(ORDER)
     core = lax.axis_index("core")
     left = psi_v.reshape(2, 4, 4, 2, 2, rows, -1).transpose(0, 3, 4, 1, 2, 5, 6).reshape(psi_v.shape)
-    level = exchange(to_all(trial[0]), PLANE).reshape(-1, states)
-    outgoing, level = lax.optimization_barrier((to_all(psi_c[:, 0, :].T), level))
-    panel = exchange(outgoing, PLANE).reshape(-1, states)
     packed = pack(screened)
+    copies, packed = lax.optimization_barrier((to_all(trial[0]), packed))
+    level = exchange(copies, PLANE).reshape(-1, states)
     weights = [packed[0], *others(*packed[1:])]
     partner = lax.ppermute(left, "zh", [(0, 1), (1, 0)])
+    outgoing, level, weights, partner = lax.optimization_barrier(
+        (to_all(psi_c[:, 0, :].T), level, weights, partner)
+    )
+    panel = exchange(outgoing, PLANE).reshape(-1, states)
     lefts = [left, swap(left), partner, swap(partner)]
     mine = lax.dynamic_slice_in_dim(level, core * half, half, 1)
     sent = lax.dynamic_slice_in_dim(level, (1 - core) * half, half, 1)

time: 110 us -> 106 us (0.964)
  local copies, waits for them, and re-layouts: 12 us -> 6.28 us
  Pallas kernels: 6.34 us -> 11.3 us
  blocking collectives: 42.4 us -> 40.2 us
    all_to_all x1, waiting for transfers between devices: 0.01 us -> 8.81 us  [exchange(): return lax.all_to_all(value, axes, split_axis=0, concat_axis=0, tiled=True)]
    ppermute x1, waiting for transfers between devices: 5.54 us -> 0.01 us  [others(): lax.ppermute(diagonal, ('zh', 'core'), [(0, 3), (1, 2), (2, 1), (3, 0)])]
    unnamed x28 -> x20, local copies, waits for them, and re-layouts: 8.66 us -> 3.63 us
    pallas_call x1, Pallas kernels: 3.44 us -> 8.4 us  [direct(): pl.pallas_call(kernel, out_shape=[jax.ShapeDtypeStruct((rows, half), F32)...]
    ppermute x1, waiting for transfers between devices: 4.6 us -> 0.01 us  [others(): lax.ppermute(partner, 'zh', [(0, 1), (1, 0)])]
    ppermute x1, starting transfers between devices: 2.18 us -> 0.01 us  [others(): lax.ppermute(partner, 'zh', [(0, 1), (1, 0)])]
    all_to_all x2, blocking collectives: 42.4 us -> 40.2 us  [exchange(): return lax.all_to_all(value, axes, split_axis=0, concat_axis=0, tiled=True)]
    ppermute x1, waiting for transfers between devices: 1.93 us -> 0.01 us  [shards(): partner = lax.ppermute(left, 'zh', [(0, 1), (1, 0)])]
  transfers between devices with their start and end apart: 13 -> 13, of which waited for: 6 -> 7; matrix products, arithmetic and copies ran while one was open for 0% -> 0% of each run, Pallas kernels for 1% -> 1%
where the time goes in v5:
time: 106 us
  blocking collectives  40.2 us (38%)
  waiting for transfers between devices  25.6 us (24%)
  starting transfers between devices  21.3 us (20%)
  Pallas kernels  11.3 us (11%)
  local copies, waits for them, and re-layouts  6.28 us (6%)
    all_to_all x2, blocking collectives, exchange(): return lax.all_to_all(value, axes, split_axis=0, concat_axis=0, tiled=True)  40.2 us
    ppermute x3, waiting for transfers between devices, ring(): lax.ppermute(value, ('zh', 'zl'), [(k, (k + by) % 4) for k in range(4)])  12.3 us
    all_to_all x1, waiting for transfers between devices, exchange(): return lax.all_to_all(value, axes, split_axis=0, concat_axis=0, tiled=True)  8.81 us
    pallas_call x1, Pallas kernels, direct(): pl.pallas_call(kernel, out_shape=[jax.ShapeDtypeStruct((rows, half), F32)...  8.4 us
    ppermute x6, starting transfers between devices, swap(): return lax.ppermute(value, 'core', [(0, 1), (1, 0)])  5.91 us
    ppermute x6, waiting for transfers between devices, swap(): return lax.ppermute(value, 'core', [(0, 1), (1, 0)])  4.52 us
    ppermute x1, starting transfers between devices, shards(): partner = lax.ppermute(left, 'zh', [(0, 1), (1, 0)])  4.51 us
    all_to_all x1, starting transfers between devices, exchange(): return lax.all_to_all(value, axes, split_axis=0, concat_axis=0, tiled=True)  4.44 us
  transfers between devices with their start and end apart: 13, of which 7 were waited for; matrix products, arithmetic and copies ran while one was open for 0% of the time, Pallas kernels for 1%

profile of v5, /device:TPU:1, one launch (start us, length us, event | category | flops | bytes accessed | tf_op | source)
XLA Modules:
  0.0 105.7 jit_solution(12863319478296146694)
XLA Ops:
  0.0 1.0 copy.5
  1.0 4.5 %collective-permute-start.4 = (bf16[1024,128]{1,0:T(8,128)(2,1)S(1)}, bf16[1024,128]{1,0:T(8,128)(2,1)S(1)}, u32[]{:S(2)}, u32[]{:S(2)}) collective-permute-start(bf16[1024,128]{1,0:T(8,128)(2,1)S(1)} %bitcast.17), channel_id=1, source_target_pairs={{0,64},{64,0},{1,65},{65,1},{2,66},{66,2},{3,67},{67,3},{4,68},{68... | collective-permute-start | bytes 786440 | tf_op jit(solution)/shard_map/ppermute | solution.py:243
  5.5 1.6 %copy-done.1 = f32[128,4096]{1,0:T(8,128)S(1)} copy-done((f32[128,4096]{1,0:T(8,128)S(1)}, f32[128,4096]{1,0:T(8,128)}, u32[]{:S(2)}) %copy-start.1) | copy-done | bytes 2097176
  7.9 0.8 copy-done.3
  8.8 1.0 collective-permute-start.1
  9.8 3.2 %collective-permute-start.3 = (bf16[128,1024]{1,0:T(8,128)(2,1)S(1)}, bf16[128,1024]{1,0:T(8,128)(2,1)S(1)}, u32[]{:S(2)}, u32[]{:S(2)}) collective-permute-start(bf16[128,1024]{1,0:T(8,128)(2,1)S(1)} %get-tuple-element.31), channel_id=1, source_target_pairs={{0,66},{2,64},{64,2},{66,0},{1,67},{3,65},{65,3},{67,1},{4,70},{6,... | collective-permute-start | bytes 786440 | tf_op jit(solution)/shard_map/ppermute | solution.py:31
  13.0 14.9 %all_to_all.15 = bf16[16,8,1024]{2,1,0:T(8,128)(2,1)S(1)} all-to-all(bf16[16,8,1024]{2,1,0:T(8,128)(2,1)S(1)} %broadcast_in_dim.15), channel_id=1, replica_groups=mesh['zh'=2,'y'=4,'x'=4,'core'=2,'zl'=2] {'y','x'}, dimensions={0} | all-to-all | bytes 524288 | tf_op jit(solution)/shard_map/all_to_all | solution.py:20
  28.0 1.6 %broadcast_in_dim.6 = bf16[16,64,1024]{2,1,0:T(8,128)(2,1)} broadcast(bf16[64,1024]{1,0:T(8,128)(2,1)S(1)} %bitcast.24), dimensions={1,2} | broadcast | bytes 2228224 | tf_op jit(solution)/shard_map/broadcast_in_dim | solution.py:229
  29.6 4.4 %all-to-all-start.1 = ((bf16[16,64,1024]{2,1,0:T(8,128)(2,1)}), bf16[16,64,1024]{2,1,0:T(8,128)(2,1)}, u32[]{:S(2)}, u32[]{:S(2)}) async-start(bf16[16,64,1024]{2,1,0:T(8,128)(2,1)} %broadcast_in_dim.6), calls=%async_computation.1 | async-start | bytes 4194304 | tf_op jit(solution)/shard_map/all_to_all | solution.py:20
  34.0 1.4 %collective-permute-start.6 = (bf16[128,512]{1,0:T(8,128)(2,1)S(1)}, bf16[128,512]{1,0:T(8,128)(2,1)S(1)}, u32[]{:S(2)}, u32[]{:S(2)}) collective-permute-start(bf16[128,512]{1,0:T(8,128)(2,1)S(1)} %get-tuple-element.42), channel_id=1, source_target_pairs={{0,2},{2,0},{1,3},{3,1},{4,6},{6,4},{5,7},{7,5},{8,10},{10,8},{9,1... | collective-permute-start | bytes 393224 | tf_op jit(solution)/shard_map/ppermute | solution.py:24
  36.5 3.1 %collective-permute-start.8 = (bf16[256,512]{1,0:T(8,128)(2,1)S(1)}, bf16[256,512]{1,0:T(8,128)(2,1)S(1)}, u32[]{:S(2)}, u32[]{:S(2)}) collective-permute-start(bf16[256,512]{1,0:T(8,128)(2,1)S(1)} %pad_maximum_fusion.refs_0_), channel_id=1, source_target_pairs={{0,65},{1,0},{64,1},{65,64},{2,67},{3,2},{66,3},{67,66},{4,69},{5,... | collective-permute-start | bytes 786440 | tf_op jit(solution)/shard_map/ppermute | solution.py:225
  39.6 6.0 %collective-permute-done.9.refs_3_ = bf16[256,512]{1,0:T(8,128)(2,1)S(1)} collective-permute-done((bf16[256,512]{1,0:T(8,128)(2,1)S(1)}, bf16[256,512]{1,0:T(8,128)(2,1)S(1)}, u32[]{:S(2)}, u32[]{:S(2)}) %collective-permute-start.9) | collective-permute-done | bytes 262176 | tf_op jit(solution)/shard_map/ppermute | solution.py:225
  45.7 3.7 %collective-permute-done.8.refs_2_ = bf16[256,512]{1,0:T(8,128)(2,1)S(1)} collective-permute-done((bf16[256,512]{1,0:T(8,128)(2,1)S(1)}, bf16[256,512]{1,0:T(8,128)(2,1)S(1)}, u32[]{:S(2)}, u32[]{:S(2)}) %collective-permute-start.8) | collective-permute-done | bytes 262176 | tf_op jit(solution)/shard_map/ppermute | solution.py:225
  49.3 2.6 %collective-permute-done.7.refs_1_ = bf16[256,512]{1,0:T(8,128)(2,1)S(1)} collective-permute-done((bf16[256,512]{1,0:T(8,128)(2,1)S(1)}, bf16[256,512]{1,0:T(8,128)(2,1)S(1)}, u32[]{:S(2)}, u32[]{:S(2)}) %collective-permute-start.7) | collective-permute-done | bytes 262176 | tf_op jit(solution)/shard_map/ppermute | solution.py:225
  51.9 0.8 project.1.own_hbm
  53.2 1.5 %collective-permute-done.10.other_hbm = bf16[512,512]{1,0:T(8,128)(2,1)S(1)} collective-permute-done((bf16[512,512]{1,0:T(8,128)(2,1)S(1)}, bf16[512,512]{1,0:T(8,128)(2,1)S(1)}, u32[]{:S(2)}, u32[]{:S(2)}) %collective-permute-start.10) | collective-permute-done | bytes 524320 | tf_op jit(solution)/shard_map/ppermute | solution.py:24
  54.8 8.8 %all-to-all-done.1 = bf16[16,64,1024]{2,1,0:T(8,128)(2,1)} async-done(((bf16[16,64,1024]{2,1,0:T(8,128)(2,1)}), bf16[16,64,1024]{2,1,0:T(8,128)(2,1)}, u32[]{:S(2)}, u32[]{:S(2)}) %all-to-all-start.1) | async-done | bytes 2097184 | tf_op jit(solution)/shard_map/all_to_all | solution.py:20
  63.6 8.4 %direct.1 = (f32[512,512]{1,0:T(8,128)}, f32[512,512]{1,0:T(8,128)}) custom-call(bf16[512,512]{1,0:T(8,128)(2,1)} %copy-done, bf16[512,512]{1,0:T(8,128)(2,1)} %copy-done.4, bf16[1024,1024]{1,0:T(8,128)(2,1)} %bitcast.8.panel_hbm, f32[128,1024]{1,0:T(8,128)} %copy-done.3, bf16[128,1024]{1,0:T(8,128)(2,1)} %copy-done.5, bf16[128,1024]{1,0:T(8,128)(2,1)} %copy-done.6, ...), custom_call_target="tpu_custom_call" | custom-call | tf_op jit(solution)/shard_map/direct/pallas_call | solution.py:173
  72.0 2.5 %collective-permute-start.11 = (f32[512,512]{1,0:T(8,128)}, f32[512,512]{1,0:T(8,128)S(1)}, u32[]{:S(2)}, u32[]{:S(2)}) collective-permute-start(f32[512,512]{1,0:T(8,128)} %get-tuple-element.40), channel_id=1, source_target_pairs={{0,2},{2,0},{1,3},{3,1},{4,6},{6,4},{5,7},{7,5},{8,10},{10,8},{9,1... | collective-permute-start | bytes 3145736 | tf_op jit(solution)/shard_map/ppermute | solution.py:24
  74.5 2.5 %collective-permute-done.11.refs_5_ = f32[512,512]{1,0:T(8,128)S(1)} collective-permute-done((f32[512,512]{1,0:T(8,128)}, f32[512,512]{1,0:T(8,128)S(1)}, u32[]{:S(2)}, u32[]{:S(2)}) %collective-permute-start.11) | collective-permute-done | bytes 1048608 | tf_op jit(solution)/shard_map/ppermute | solution.py:24
  77.0 1.2 %copy-done.2 = f32[512,512]{1,0:T(8,128)S(1)} copy-done((f32[512,512]{1,0:T(8,128)S(1)}, f32[512,512]{1,0:T(8,128)}, u32[]{:S(2)}) %copy-start.2) | copy-done | bytes 1048600
  78.3 1.3 %finish.1 = bf16[1024,512]{1,0:T(8,128)(2,1)S(1)} custom-call(bf16[1024,128]{1,0:T(8,128)(2,1)S(1)} %bitcast.20, bf16[1024,128]{1,0:T(8,128)(2,1)S(1)} %collective-permute-done.refs_5_.refs_1_, bf16[1024,128]{1,0:T(8,128)(2,1)S(1)} %collective-permute-done.4.refs_6_.refs_2_, bf16[1024,128]{1,0:T(8,128)(2,1)S(1)} %collective-permute-done.5.refs_7_.refs_3_, ...), custom_call_target="tpu_custom_call" | custom-call | tf_op jit(solution)/shard_map/finish/pallas_call | solution.py:209
  79.6 25.3 %all_to_all.16 = bf16[128,8,512]{2,1,0:T(8,128)(2,1)S(1)} all-to-all(bf16[128,8,512]{2,1,0:T(8,128)(2,1)S(1)} %bitcast.16), channel_id=1, replica_groups=mesh['zh'=2,'y'=4,'x'=4,'core'=2,'zl'=2] {'zh','core','zl','y','x'}, dimensions={0} | all-to-all | bytes 2097152 | tf_op jit(solution)/shard_map/all_to_all | solution.py:20
  104.9 0.8 convert_reduce_fusion
  (34 shorter events, 2.4 us)
Async XLA Ops:
  0.0 8.7 %copy-start.9 = (bf16[1,8,1024]{2,1,0:T(8,128)(2,1)S(1)}, bf16[1,8,1024]{2,1,0:T(8,128)(2,1)}, u32[]{:S(2)}) copy-start(bf16[1,8,1024]{2,1,0:T(8,128)(2,1)} %param.4) | copy-start | bytes 49156
  0.0 28.0 %copy-start.8 = (bf16[1024,1,64]{0,2,1:T(8,128)(2,1)S(1)}, bf16[1024,1,64]{0,2,1:T(8,128)(2,1)}, u32[]{:S(2)}) copy-start(bf16[1024,1,64]{0,2,1:T(8,128)(2,1)} %param.6) | copy-start | bytes 393220
  1.0 26.9 %collective-permute-start.4 = (bf16[1024,128]{1,0:T(8,128)(2,1)S(1)}, bf16[1024,128]{1,0:T(8,128)(2,1)S(1)}, u32[]{:S(2)}, u32[]{:S(2)}) collective-permute-start(bf16[1024,128]{1,0:T(8,128)(2,1)S(1)} %bitcast.17), channel_id=1, source_target_pairs={{0,64},{64,0},{1,65},{65,1},{2,66},{66,2},{3,67},{67,3},{4,68},{68... | collective-permute-start | bytes 786440 | tf_op jit(solution)/shard_map/ppermute | solution.py:243
  5.5 1.6 %copy-start.1 = (f32[128,4096]{1,0:T(8,128)S(1)}, f32[128,4096]{1,0:T(8,128)}, u32[]{:S(2)}) copy-start(f32[128,4096]{1,0:T(8,128)} %in_ref.1) | copy-start | bytes 6291460
  7.9 0.8 copy-start.3
  8.8 19.2 %collective-permute-start.1 = (bf16[128,1024]{1,0:T(8,128)(2,1)S(1)}, bf16[128,1024]{1,0:T(8,128)(2,1)S(1)}, u32[]{:S(2)}, u32[]{:S(2)}) collective-permute-start(bf16[128,1024]{1,0:T(8,128)(2,1)S(1)} %get-tuple-element.29), channel_id=1, source_target_pairs={{0,2},{2,0},{1,3},{3,1},{4,6},{6,4},{5,7},{7,5},{8,10},{10,8},{9,1... | collective-permute-start | bytes 786440 | tf_op jit(solution)/shard_map/ppermute | solution.py:24
  9.8 18.1 %collective-permute-start.2 = (bf16[128,1024]{1,0:T(8,128)(2,1)S(1)}, bf16[128,1024]{1,0:T(8,128)(2,1)S(1)}, u32[]{:S(2)}, u32[]{:S(2)}) collective-permute-start(bf16[128,1024]{1,0:T(8,128)(2,1)S(1)} %get-tuple-element.30), channel_id=1, source_target_pairs={{0,64},{64,0},{1,65},{65,1},{2,66},{66,2},{3,67},{67,3},{4,68},{68... | collective-permute-start | bytes 786440 | tf_op jit(solution)/shard_map/ppermute | solution.py:30
  9.8 18.2 %collective-permute-start.3 = (bf16[128,1024]{1,0:T(8,128)(2,1)S(1)}, bf16[128,1024]{1,0:T(8,128)(2,1)S(1)}, u32[]{:S(2)}, u32[]{:S(2)}) collective-permute-start(bf16[128,1024]{1,0:T(8,128)(2,1)S(1)} %get-tuple-element.31), channel_id=1, source_target_pairs={{0,66},{2,64},{64,2},{66,0},{1,67},{3,65},{65,3},{67,1},{4,70},{6,... | collective-permute-start | bytes 786440 | tf_op jit(solution)/shard_map/ppermute | solution.py:31
  27.9 1.6 %copy-start.5 = (bf16[128,1024]{1,0:T(8,128)(2,1)}, bf16[128,1024]{1,0:T(8,128)(2,1)S(1)}, u32[]{:S(2)}) copy-start(bf16[128,1024]{1,0:T(8,128)(2,1)S(1)} %collective-permute-done.1.refs_1_) | copy-start | bytes 786436
  27.9 1.6 %copy-start.6 = (bf16[128,1024]{1,0:T(8,128)(2,1)}, bf16[128,1024]{1,0:T(8,128)(2,1)S(1)}, u32[]{:S(2)}) copy-start(bf16[128,1024]{1,0:T(8,128)(2,1)S(1)} %collective-permute-done.2.refs_2_) | copy-start | bytes 786436
  28.0 1.6 %copy-start.7 = (bf16[128,1024]{1,0:T(8,128)(2,1)}, bf16[128,1024]{1,0:T(8,128)(2,1)S(1)}, u32[]{:S(2)}) copy-start(bf16[128,1024]{1,0:T(8,128)(2,1)S(1)} %collective-permute-done.3.refs_3_) | copy-start | bytes 786436
  29.6 34.0 %all-to-all-start.1 = ((bf16[16,64,1024]{2,1,0:T(8,128)(2,1)}), bf16[16,64,1024]{2,1,0:T(8,128)(2,1)}, u32[]{:S(2)}, u32[]{:S(2)}) async-start(bf16[16,64,1024]{2,1,0:T(8,128)(2,1)} %broadcast_in_dim.6), calls=%async_computation.1 | async-start | bytes 4194304 | tf_op jit(solution)/shard_map/all_to_all | solution.py:20
  34.0 2.3 %collective-permute-start.6 = (bf16[128,512]{1,0:T(8,128)(2,1)S(1)}, bf16[128,512]{1,0:T(8,128)(2,1)S(1)}, u32[]{:S(2)}, u32[]{:S(2)}) collective-permute-start(bf16[128,512]{1,0:T(8,128)(2,1)S(1)} %get-tuple-element.42), channel_id=1, source_target_pairs={{0,2},{2,0},{1,3},{3,1},{4,6},{6,4},{5,7},{7,5},{8,10},{10,8},{9,1... | collective-permute-start | bytes 393224 | tf_op jit(solution)/shard_map/ppermute | solution.py:24
  35.4 4.2 %collective-permute-start = (bf16[1024,128]{1,0:T(8,128)(2,1)S(1)}, bf16[1024,128]{1,0:T(8,128)(2,1)S(1)}, u32[]{:S(2)}, u32[]{:S(2)}) collective-permute-start(bf16[1024,128]{1,0:T(8,128)(2,1)S(1)} %bitcast.18), channel_id=1, source_target_pairs={{0,2},{2,0},{1,3},{3,1},{4,6},{6,4},{5,7},{7,5},{8,10},{10,8},{9,1... | collective-permute-start | bytes 786440 | tf_op jit(solution)/shard_map/ppermute | solution.py:24
  35.5 4.1 %collective-permute-start.5 = (bf16[1024,128]{1,0:T(8,128)(2,1)S(1)}, bf16[1024,128]{1,0:T(8,128)(2,1)S(1)}, u32[]{:S(2)}, u32[]{:S(2)}) collective-permute-start(bf16[1024,128]{1,0:T(8,128)(2,1)S(1)} %collective-permute-done.4.refs_6_.refs_2_), channel_id=1, source_target_pairs={{0,2},{2,0},{1,3},{3,1},{4,6},{6,4},{5,7},{7,5},{8,10},{10,8},{9,1... | collective-permute-start | bytes 786440 | tf_op jit(solution)/shard_map/ppermute | solution.py:24
  36.4 9.3 %collective-permute-start.9 = (bf16[256,512]{1,0:T(8,128)(2,1)S(1)}, bf16[256,512]{1,0:T(8,128)(2,1)S(1)}, u32[]{:S(2)}, u32[]{:S(2)}) collective-permute-start(bf16[256,512]{1,0:T(8,128)(2,1)S(1)} %pad_maximum_fusion.refs_0_), channel_id=1, source_target_pairs={{0,64},{1,65},{64,0},{65,1},{2,66},{3,67},{66,2},{67,3},{4,68},{5,... | collective-permute-start | bytes 786440 | tf_op jit(solution)/shard_map/ppermute | solution.py:225
  36.5 12.8 %collective-permute-start.8 = (bf16[256,512]{1,0:T(8,128)(2,1)S(1)}, bf16[256,512]{1,0:T(8,128)(2,1)S(1)}, u32[]{:S(2)}, u32[]{:S(2)}) collective-permute-start(bf16[256,512]{1,0:T(8,128)(2,1)S(1)} %pad_maximum_fusion.refs_0_), channel_id=1, source_target_pairs={{0,65},{1,0},{64,1},{65,64},{2,67},{3,2},{66,3},{67,66},{4,69},{5,... | collective-permute-start | bytes 786440 | tf_op jit(solution)/shard_map/ppermute | solution.py:225
  39.6 12.3 %collective-permute-start.7 = (bf16[256,512]{1,0:T(8,128)(2,1)S(1)}, bf16[256,512]{1,0:T(8,128)(2,1)S(1)}, u32[]{:S(2)}, u32[]{:S(2)}) collective-permute-start(bf16[256,512]{1,0:T(8,128)(2,1)S(1)} %pad_maximum_fusion.refs_0_), channel_id=1, source_target_pairs={{0,1},{1,64},{64,65},{65,0},{2,3},{3,66},{66,67},{67,2},{4,5},{5,6... | collective-permute-start | bytes 786440 | tf_op jit(solution)/shard_map/ppermute | solution.py:225
  52.7 10.8 %copy-start = (bf16[512,512]{1,0:T(8,128)(2,1)}, bf16[512,512]{1,0:T(8,128)(2,1)S(1)}, u32[]{:S(2)}) copy-start(bf16[512,512]{1,0:T(8,128)(2,1)S(1)} %project.1.own_hbm) | copy-start | bytes 1572868
  52.8 2.0 %collective-permute-start.10 = (bf16[512,512]{1,0:T(8,128)(2,1)S(1)}, bf16[512,512]{1,0:T(8,128)(2,1)S(1)}, u32[]{:S(2)}, u32[]{:S(2)}) collective-permute-start(bf16[512,512]{1,0:T(8,128)(2,1)S(1)} %project.1.own_hbm), channel_id=1, source_target_pairs={{0,2},{2,0},{1,3},{3,1},{4,6},{6,4},{5,7},{7,5},{8,10},{10,8},{9,1... | collective-permute-start | bytes 1572872 | tf_op jit(solution)/shard_map/ppermute | solution.py:24
  54.8 8.8 %copy-start.4 = (bf16[512,512]{1,0:T(8,128)(2,1)}, bf16[512,512]{1,0:T(8,128)(2,1)S(1)}, u32[]{:S(2)}) copy-start(bf16[512,512]{1,0:T(8,128)(2,1)S(1)} %collective-permute-done.10.other_hbm) | copy-start | bytes 1572868
  72.0 5.0 %collective-permute-start.11 = (f32[512,512]{1,0:T(8,128)}, f32[512,512]{1,0:T(8,128)S(1)}, u32[]{:S(2)}, u32[]{:S(2)}) collective-permute-start(f32[512,512]{1,0:T(8,128)} %get-tuple-element.40), channel_id=1, source_target_pairs={{0,2},{2,0},{1,3},{3,1},{4,6},{6,4},{5,7},{7,5},{8,10},{10,8},{9,1... | collective-permute-start | bytes 3145736 | tf_op jit(solution)/shard_map/ppermute | solution.py:24
  77.0 1.2 %copy-start.2 = (f32[512,512]{1,0:T(8,128)S(1)}, f32[512,512]{1,0:T(8,128)}, u32[]{:S(2)}) copy-start(f32[512,512]{1,0:T(8,128)} %get-tuple-element.39.refs_4_) | copy-start | bytes 3145732

commit v6 on v4

v6 whole, which is shorter than its diff:
```python
import jax
import jax.numpy as jnp
from jax import lax
from jax.experimental import pallas as pl
from jax.experimental.pallas import tpu as pltpu
from jax.sharding import Mesh
from jax.sharding import PartitionSpec as P

TILE_VEC = ("zh", "y", "x", "core", "zl")
TILE = ("zh", "y", "x", "core")
PLANE = ("y", "x")
ORDER = ("zh", "core", "zl", "y", "x")
STEPS = (0, -1, 1, -2)
F32 = jnp.float32
BF16 = jnp.bfloat16
SIBLING = (1, 0, 3, 2)


def shift(value, axis, by):
    n = lax.axis_size(axis)
    return lax.ppermute(value, axis, [(k, (k + by) % n) for k in range(n)])


def exchange(value, axes):
    return lax.all_to_all(value, axes, split_axis=0, concat_axis=0, tiled=True)


def swap(value):
    return lax.ppermute(value, "core", [(0, 1), (1, 0)])


def vmem_spec():
    return pl.BlockSpec(memory_space=pltpu.VMEM)


def params(mebibytes):
    return pltpu.CompilerParams(vmem_limit_bytes=mebibytes * 1024 * 1024)


def pack(screened, left):
    points, count = screened.shape
    plane, steps = count // 2, 4
    width = plane // 2
    rows = points // steps

    def kernel(in_ref, left_ref, own_ref, near_ref, far_ref):
        core, zh = lax.axis_index("core"), lax.axis_index("zh")
        low = lax.broadcasted_iota(jnp.int32, (rows, 128), 1) < 64
        first = core == 0
        for far in range(2):
            base = plane * (zh if far == 0 else 1 - zh)
            for m in range(width // 128):
                a = in_ref[:, pl.ds(pl.multiple_of(base + m * 256, 256), 128)]
                b = in_ref[:, pl.ds(pl.multiple_of(base + m * 256 + 128, 128), 128)]
                zero = jnp.where(low, a, pltpu.roll(b, 64, 1))
                one = jnp.where(low, pltpu.roll(a, 64, 1), b)
                here = pl.ds(m * 128, 128)
                mine, others = jnp.where(first, zero, one), jnp.where(first, one, zero)
                if far == 0:
                    own_ref[:, here] = mine
                    near_ref[0, :, here] = others.astype(BF16)
                else:
                    far_ref[0, :, here] = mine.astype(BF16)
                    far_ref[1, :, here] = others.astype(BF16)
        for g in range(left_ref.shape[0] // points):
            start = pl.multiple_of(g * points + pl.program_id(0) * rows, rows)
            piece = left_ref[pl.ds(start, rows), :]
            near_ref[1, :, pl.ds(g * points, points)] = piece
            far_ref[2, :, pl.ds(g * points, points)] = piece

    return pl.pallas_call(
        kernel,
        grid=(steps,),
        out_shape=[
            jax.ShapeDtypeStruct((points, width), F32),
            jax.ShapeDtypeStruct((2, points, width), BF16),
            jax.ShapeDtypeStruct((3, points, width), BF16),
        ],
        in_specs=[
            pl.BlockSpec((rows, count), lambda k: (k, 0)),
            pl.BlockSpec(left.shape, lambda k: (0, 0)),
        ],
        out_specs=[
            pl.BlockSpec((rows, width), lambda k: (k, 0)),
            pl.BlockSpec((2, rows, width), lambda k: (0, k, 0)),
            pl.BlockSpec((3, rows, width), lambda k: (0, k, 0)),
        ],
        compiler_params=params(8),
        name="pack",
    )(screened, left)


def project(rounds, left, near, far, passed):
    states, points = left.shape
    block = rounds[0].shape[0] // 2
    cols = rounds[0].shape[1]

    def kernel(*refs):
        trial_refs, left_ref, boxes, (out_ref, psi_ref, trial) = refs[:4], refs[4], refs[5:8], refs[8:]
        core = lax.axis_index("core")
        place = 2 * lax.axis_index("zh") + lax.axis_index("zl")
        for k in range(4):
            source = lax.rem(place + STEPS[k] + 4, 4)
            for m in range(2):
                owner = core if m == 0 else 1 - core
                group = lax.div(source, 2) * 4 + owner * 2 + lax.rem(source, 2)
                trial[pl.ds(pl.multiple_of(group * block, block), block), :] = trial_refs[k][
                    m * block : (m + 1) * block, :
                ]
        psi_ref[:, :points] = left_ref[...]
        for k in range(1, 4):
            box = boxes[k - 1]
            for g in range(states // points):
                psi_ref[g * points : (g + 1) * points, k * points : (k + 1) * points] = box[
                    box.shape[0] - 1, :, g * points : (g + 1) * points
                ]
        out_ref[...] = lax.dot_general(
            psi_ref[...], trial[...], (((0,), (0,)), ((), ())), preferred_element_type=F32
        ).astype(BF16)

    return pl.pallas_call(
        kernel,
        out_shape=[
            jax.ShapeDtypeStruct((4 * points, cols), BF16),
            jax.ShapeDtypeStruct((states, 4 * points), BF16),
        ],
        in_specs=[vmem_spec()] * 8,
        out_specs=[vmem_spec()] * 2,
        scratch_shapes=[pltpu.VMEM((states, cols), BF16)],
        compiler_params=params(12),
        name="project",
    )(*rounds, left, near, far, passed)


def direct(proj_own, proj_other, lines, own, boxes):
    rows, half = proj_own.shape
    points = rows // 4
    block = lines[0].shape[0] // 2
    count, states = 16 * block, lines[0].shape[1]
    chunk = 512

    def kernel(own_ref, other_ref, *refs):
        line_refs, scr_refs, (keep_ref, send_ref, proj, panel_ref) = refs[:8], refs[8:12], refs[12:]
        y, x = lax.axis_index("y"), lax.axis_index("x")
        for k in range(16):
            at = lax.rem(y + STEPS[k // 4] + 4, 4) * 4 + lax.rem(x + STEPS[k % 4] + 4, 4)
            panel_ref[pl.ds(pl.multiple_of(at * block, block), block), :] = line_refs[k // 2][
                k % 2 * block : (k % 2 + 1) * block, :
            ]
        core = lax.axis_index("core")
        mine = pl.ds(pl.multiple_of(core * half, half), half)
        sibs = pl.ds(pl.multiple_of((1 - core) * half, half), half)
        for k in range(4):
            proj[k * points : (k + 1) * points, :] = other_ref[
                SIBLING[k] * points : (SIBLING[k] + 1) * points, :
            ]
        nt = (((1,), (1,)), ((), ()))
        for k in range(count // chunk):
            here = pl.ds(k * chunk, chunk)
            pair = lax.dot_general(own_ref[...], panel_ref[here, mine], nt, preferred_element_type=F32)
            pair += lax.dot_general(proj[...], panel_ref[here, sibs], nt, preferred_element_type=F32)
            weighted = jnp.concatenate(
                [
                    (
                        (scr_refs[0][:, here] if j == 0 else scr_refs[j][0, :, here].astype(F32))
                        * pair[j * points : (j + 1) * points]
                    ).astype(BF16)
                    for j in range(4)
                ],
                0,
            )
            send = jnp.dot(weighted, panel_ref[here, sibs], preferred_element_type=F32)
            keep = jnp.dot(weighted, panel_ref[here, mine], preferred_element_type=F32)
            if k == 0:
                send_ref[...] = send
                keep_ref[...] = keep
            else:
                send_ref[...] += send
                keep_ref[...] += keep

    return pl.pallas_call(
        kernel,
        out_shape=[jax.ShapeDtypeStruct((rows, half), F32)] * 2,
        in_specs=[vmem_spec()] * 14,
        out_specs=[vmem_spec()] * 2,
        scratch_shapes=[pltpu.VMEM((rows, half), BF16), pltpu.VMEM((count, states), BF16)],
        compiler_params=params(24),
        name="direct",
    )(proj_own, proj_other, *lines, own, *boxes)


def finish(psi, keep, got):
    states, count = psi.shape
    points = count // 4
    cols = keep.shape[1]

    def kernel(psi_ref, keep_ref, got_ref, out_ref, high, low):
        for k in range(4):
            here = slice(k * points, (k + 1) * points)
            there = slice(SIBLING[k] * points, (SIBLING[k] + 1) * points)
            back = keep_ref[here, :] + got_ref[there, :]
            top = back.astype(BF16)
            high[here, :] = top
            low[here, :] = (back - top.astype(F32)).astype(BF16)
        total = jnp.dot(psi_ref[...], high[...], preferred_element_type=F32)
        total += jnp.dot(psi_ref[...], low[...], preferred_element_type=F32)
        out_ref[...] = total.astype(BF16)

    return pl.pallas_call(
        kernel,
        out_shape=jax.ShapeDtypeStruct((states, cols), BF16),
        in_specs=[vmem_spec()] * 3,
        out_specs=vmem_spec(),
        scratch_shapes=[pltpu.VMEM((count, cols), BF16)] * 2,
        compiler_params=params(16),
        name="finish",
    )(psi, keep, got)


def ring(value, by):
    return lax.ppermute(value, ("zh", "zl"), [(k, (k + by) % 4) for k in range(4)])


def to_all(value):
    copies = jnp.broadcast_to(value[None], (lax.axis_size(PLANE), *value.shape))
    return copies


def shards(trial, psi_v, psi_c, screened):
    rows, states = trial.shape[1:]
    half = states // 2
    devices = lax.axis_size(ORDER)
    core = lax.axis_index("core")
    left = psi_v.reshape(2, 4, 4, 2, 2, rows, -1).transpose(0, 3, 4, 1, 2, 5, 6).reshape(psi_v.shape)
    own, near, far = pack(screened, left)
    block = psi_c[:, 0, :].T
    line = [
        jnp.concatenate([block, shift(block, "x", 1)], 0),
        jnp.concatenate([shift(block, "x", -1), shift(block, "x", 2)], 0),
    ]
    copies, near, far = lax.optimization_barrier((to_all(trial[0]), near, far))
    level = exchange(copies, PLANE).reshape(-1, states)
    near = swap(near)
    far = lax.ppermute(far, "zh", [(0, 1), (1, 0)])
    behind = [shift(part, "y", 1) for part in line]
    ahead = [shift(part, "y", -1) for part in line]
    mine = lax.dynamic_slice_in_dim(level, core * half, half, 1)
    sent = lax.dynamic_slice_in_dim(level, (1 - core) * half, half, 1)
    pieces = jnp.concatenate([mine, swap(sent)], 0)
    pieces, near, far, behind[0], ahead[1] = lax.optimization_barrier(
        (pieces, near, far, behind[0], ahead[1])
    )
    passed = swap(far[1:])
    rounds = [pieces, ring(pieces, 1), ring(pieces, -1), ring(pieces, 2)]
    beyond = [shift(behind[0], "y", 1), shift(ahead[1], "y", -1)]
    rounds, behind[1], ahead[0], beyond = lax.optimization_barrier(
        (rounds, behind[1], ahead[0], beyond)
    )
    proj_own, psi = project(rounds, left, near, far, passed)
    proj_other = swap(proj_own)
    panel = [*line, *behind, *ahead, *beyond]
    keep, send = direct(proj_own, proj_other, panel, own, [near, far, passed])
    got = swap(send)
    term = finish(psi, keep, got)
    parts = exchange(term.reshape(devices, rows, half), ORDER)
    parts = parts.reshape(2, 2, 2, -1, rows, half).astype(F32)
    total = jnp.sum(parts, axis=(0, 2, 3))
    return total.transpose(1, 0, 2).reshape(1, rows, states)


def solution(mesh):
    split = Mesh(
        mesh.devices.reshape(2, 4, 4, 2, mesh.shape["vec"]),
        TILE_VEC,
    )
    return jax.shard_map(
        shards,
        mesh=split,
        in_specs=(P(None, TILE_VEC, None), P(None, TILE), P(None, "zl", TILE), P(TILE, "zl")),
        out_specs=P(None, TILE_VEC, None),
        check_vma=False,
    )
```

time: 110 us -> 90.1 us (0.82)
  blocking collectives: 42.4 us -> 23.3 us
  starting transfers between devices: 21.9 us -> 32 us
  local copies, waits for them, and re-layouts: 12 us -> 3.38 us
  waiting for transfers between devices: 26.1 us -> 23.5 us
    all_to_all x2 -> x1, blocking collectives: 42.4 us -> 23.3 us  [exchange(): return lax.all_to_all(value, axes, split_axis=0, concat_axis=0, tiled=True)]
    ppermute x3 -> x10, starting transfers between devices: 7.27 us -> 14.9 us  [the longest x9 11.3 us: shift(): return lax.ppermute(value, axis, [(k, (k + by) % n) for k in range(n)])]
    unnamed x28 -> x7, local copies, waits for them, and re-layouts: 8.66 us -> 1.6 us
    ppermute x3, waiting for transfers between devices: 11.4 us -> 6.56 us  [ring(): lax.ppermute(value, ('zh', 'zl'), [(k, (k + by) % 4) for k in range(4)])]
    ppermute x6 -> x5, starting transfers between devices: 6.32 us -> 9.97 us  [swap(): return lax.ppermute(value, 'core', [(0, 1), (1, 0)])]
    ppermute x3, starting transfers between devices: 4.51 us -> 1.62 us  [ring(): lax.ppermute(value, ('zh', 'zl'), [(k, (k + by) % 4) for k in range(4)])]
    broadcast_in_dim x2 -> x1, local copies, waits for them, and re-layouts: 3.24 us -> 0.72 us  [to_all(): copies = jnp.broadcast_to(value[None], (lax.axis_size(PLANE), *value.shape))]
    all_to_all x1, waiting for transfers between devices: 0.01 us -> 2.39 us  [exchange(): return lax.all_to_all(value, axes, split_axis=0, concat_axis=0, tiled=True)]
  transfers between devices with their start and end apart: 13 -> 19, of which waited for: 6 -> 10; matrix products, arithmetic and copies ran while one was open for 0% -> 2% of each run, Pallas kernels for 1% -> 2%
where the time goes in v6:
time: 90.1 us; the launch traced here: 89.8 us
  starting transfers between devices  32 us (36%)
  waiting for transfers between devices  23.5 us (26%)
  blocking collectives  23.3 us (26%)
  Pallas kernels  6.73 us (7%)
  local copies, waits for them, and re-layouts  3.38 us (4%)
    all_to_all x1, blocking collectives, exchange(): return lax.all_to_all(value, axes, split_axis=0, concat_axis=0, tiled=True)  23.3 us
    ppermute x9, starting transfers between devices, shift(): return lax.ppermute(value, axis, [(k, (k + by) % n) for k in range(n)])  11.3 us
    ppermute x5, starting transfers between devices, swap(): return lax.ppermute(value, 'core', [(0, 1), (1, 0)])  9.97 us
    ppermute x9, waiting for transfers between devices, shift(): return lax.ppermute(value, axis, [(k, (k + by) % n) for k in range(n)])  9.76 us
    ppermute x3, waiting for transfers between devices, ring(): lax.ppermute(value, ('zh', 'zl'), [(k, (k + by) % 4) for k in range(4)])  6.56 us
    all_to_all x1, starting transfers between devices, exchange(): return lax.all_to_all(value, axes, split_axis=0, concat_axis=0, tiled=True)  5.45 us
    ppermute x5, waiting for transfers between devices, swap(): return lax.ppermute(value, 'core', [(0, 1), (1, 0)])  4.82 us
    ppermute x1, starting transfers between devices, shards(): far = lax.ppermute(far, 'zh', [(0, 1), (1, 0)])  3.6 us
  transfers between devices with their start and end apart: 19, of which 10 were waited for; matrix products, arithmetic and copies ran while one was open for 2% of the time, Pallas kernels for 2%

profile of v6, /device:TPU:1, one launch (start us, length us, event | category | flops | bytes accessed | tf_op | source)
XLA Modules:
  0.0 89.8 jit_solution(14559756842416551126)
XLA Ops:
  0.0 2.0 %collective-permute-start.3 = (bf16[64,1024]{1,0:T(8,128)(2,1)}, bf16[64,1024]{1,0:T(8,128)(2,1)S(1)}, u32[]{:S(2)}, u32[]{:S(2)}) collective-permute-start(bf16[64,1024]{1,0:T(8,128)(2,1)} %bitcast.21), channel_id=1, source_target_pairs={{0,4},{4,8},{8,12},{12,0},{1,5},{5,9},{9,13},{13,1},{2,6},{6,10},{... | collective-permute-start | bytes 393224 | tf_op jit(solution)/shard_map/ppermute | solution.py:21
  3.1 1.6 %copy-done = f32[128,4096]{1,0:T(8,128)S(1)} copy-done((f32[128,4096]{1,0:T(8,128)S(1)}, f32[128,4096]{1,0:T(8,128)}, u32[]{:S(2)}) %copy-start) | copy-done | bytes 2097176
  4.6 2.1 %pack.1 = (f32[128,1024]{1,0:T(8,128)S(1)}, bf16[2,128,1024]{2,1,0:T(8,128)(2,1)}, bf16[3,128,1024]{2,1,0:T(8,128)(2,1)}) custom-call(f32[128,4096]{1,0:T(8,128)S(1)} %copy-done, bf16[1024,128]{1,0:T(8,128)(2,1)S(1)} %bitcast.16), custom_call_target="tpu_custom_call" | custom-call | tf_op jit(solution)/shard_map/pack/pallas_call | solution.py:71
  7.4 3.6 %collective-permute-start.2 = (bf16[3,128,1024]{2,1,0:T(8,128)(2,1)}, bf16[3,128,1024]{2,1,0:T(8,128)(2,1)S(1)}, u32[]{:S(2)}, u32[]{:S(2)}) collective-permute-start(bf16[3,128,1024]{2,1,0:T(8,128)(2,1)} %get-tuple-element.32), channel_id=1, source_target_pairs={{0,64},{64,0},{1,65},{65,1},{2,66},{66,2},{3,67},{67,3},{4,68},{68... | collective-permute-start | bytes 2359304 | tf_op jit(solution)/shard_map/ppermute | solution.py:244
  11.0 1.5 %collective-permute-start.5 = (bf16[64,1024]{1,0:T(8,128)(2,1)S(1)}, bf16[64,1024]{1,0:T(8,128)(2,1)S(1)}, u32[]{:S(2)}, u32[]{:S(2)}) collective-permute-start(bf16[64,1024]{1,0:T(8,128)(2,1)S(1)} %bitcast.22), channel_id=1, source_target_pairs={{0,12},{4,0},{8,4},{12,8},{1,13},{5,1},{9,5},{13,9},{2,14},{6,2},{... | collective-permute-start | bytes 393224 | tf_op jit(solution)/shard_map/ppermute | solution.py:21
  12.5 1.5 %collective-permute-start.6 = (bf16[64,1024]{1,0:T(8,128)(2,1)S(1)}, bf16[64,1024]{1,0:T(8,128)(2,1)S(1)}, u32[]{:S(2)}, u32[]{:S(2)}) collective-permute-start(bf16[64,1024]{1,0:T(8,128)(2,1)S(1)} %bitcast.23), channel_id=1, source_target_pairs={{0,8},{4,12},{8,0},{12,4},{1,9},{5,13},{9,1},{13,5},{2,10},{6,14},... | collective-permute-start | bytes 393224 | tf_op jit(solution)/shard_map/ppermute | solution.py:21
  14.0 5.4 %all-to-all-start = ((bf16[16,8,1024]{2,1,0:T(8,128)(2,1)}), bf16[16,8,1024]{2,1,0:T(8,128)(2,1)S(1)}, u32[]{:S(2)}, u32[]{:S(2)}) async-start(bf16[16,8,1024]{2,1,0:T(8,128)(2,1)} %broadcast_in_dim.8), calls=%async_computation | async-start | bytes 524288 | tf_op jit(solution)/shard_map/all_to_all | solution.py:25
  19.5 2.2 %collective-permute-start.1 = (bf16[2,128,1024]{2,1,0:T(8,128)(2,1)}, bf16[2,128,1024]{2,1,0:T(8,128)(2,1)S(1)}, u32[]{:S(2)}, u32[]{:S(2)}) collective-permute-start(bf16[2,128,1024]{2,1,0:T(8,128)(2,1)} %get-tuple-element.31), channel_id=1, source_target_pairs={{0,2},{2,0},{1,3},{3,1},{4,6},{6,4},{5,7},{7,5},{8,10},{10,8},{9,1... | collective-permute-start | bytes 1572872 | tf_op jit(solution)/shard_map/ppermute | solution.py:29
  21.6 1.6 %collective-permute-start.4 = (bf16[128,1024]{1,0:T(8,128)(2,1)S(1)}, bf16[128,1024]{1,0:T(8,128)(2,1)S(1)}, u32[]{:S(2)}, u32[]{:S(2)}) collective-permute-start(bf16[128,1024]{1,0:T(8,128)(2,1)S(1)} %pad_maximum_fusion.1.refs_0_), channel_id=1, source_target_pairs={{0,16},{16,32},{32,48},{48,0},{1,17},{17,33},{33,49},{49,1},{2,18}... | collective-permute-start | bytes 786440 | tf_op jit(solution)/shard_map/ppermute | solution.py:21
  23.3 1.3 %collective-permute-start.7 = (bf16[128,1024]{1,0:T(8,128)(2,1)S(1)}, bf16[128,1024]{1,0:T(8,128)(2,1)S(1)}, u32[]{:S(2)}, u32[]{:S(2)}) collective-permute-start(bf16[128,1024]{1,0:T(8,128)(2,1)S(1)} %constant_dynamic-update-slice_fusion.refs_1_), channel_id=1, source_target_pairs={{0,48},{16,0},{32,16},{48,32},{1,49},{17,1},{33,17},{49,33},{2,50}... | collective-permute-start | bytes 786440 | tf_op jit(solution)/shard_map/ppermute | solution.py:21
  24.6 2.4 %all-to-all-done = bf16[16,8,1024]{2,1,0:T(8,128)(2,1)S(1)} async-done(((bf16[16,8,1024]{2,1,0:T(8,128)(2,1)}), bf16[16,8,1024]{2,1,0:T(8,128)(2,1)S(1)}, u32[]{:S(2)}, u32[]{:S(2)}) %all-to-all-start) | async-done | bytes 262176 | tf_op jit(solution)/shard_map/all_to_all | solution.py:25
  27.0 3.3 %collective-permute-start = (bf16[128,512]{1,0:T(8,128)(2,1)S(1)}, bf16[128,512]{1,0:T(8,128)(2,1)S(1)}, u32[]{:S(2)}, u32[]{:S(2)}) collective-permute-start(bf16[128,512]{1,0:T(8,128)(2,1)S(1)} %get-tuple-element.52), channel_id=1, source_target_pairs={{0,2},{2,0},{1,3},{3,1},{4,6},{6,4},{5,7},{7,5},{8,10},{10,8},{9,1... | collective-permute-start | bytes 393224 | tf_op jit(solution)/shard_map/ppermute | solution.py:29
  33.8 1.3 %collective-permute-start.15 = (bf16[2,128,1024]{2,1,0:T(8,128)(2,1)S(1)}, bf16[2,128,1024]{2,1,0:T(8,128)(2,1)S(1)}, u32[]{:S(2)}, u32[]{:S(2)}) collective-permute-start(bf16[2,128,1024]{2,1,0:T(8,128)(2,1)S(1)} %slice.3), channel_id=1, source_target_pairs={{0,2},{2,0},{1,3},{3,1},{4,6},{6,4},{5,7},{7,5},{8,10},{10,8},{9,1... | collective-permute-start | bytes 1572872 | tf_op jit(solution)/shard_map/ppermute | solution.py:29
  35.2 1.8 %collective-permute-start.14 = (bf16[128,1024]{1,0:T(8,128)(2,1)S(1)}, bf16[128,1024]{1,0:T(8,128)(2,1)S(1)}, u32[]{:S(2)}, u32[]{:S(2)}) collective-permute-start(bf16[128,1024]{1,0:T(8,128)(2,1)S(1)} %collective-permute-done.7.refs_5_), channel_id=1, source_target_pairs={{0,48},{16,0},{32,16},{48,32},{1,49},{17,1},{33,17},{49,33},{2,50}... | collective-permute-start | bytes 786440 | tf_op jit(solution)/shard_map/ppermute | solution.py:21
  37.0 1.9 %collective-permute-done.12.refs_4_ = bf16[128,1024]{1,0:T(8,128)(2,1)S(1)} collective-permute-done((bf16[128,1024]{1,0:T(8,128)(2,1)S(1)}, bf16[128,1024]{1,0:T(8,128)(2,1)S(1)}, u32[]{:S(2)}, u32[]{:S(2)}) %collective-permute-start.12) | collective-permute-done | bytes 262176 | tf_op jit(solution)/shard_map/ppermute | solution.py:21
  38.9 2.3 %collective-permute-done.11.refs_3_ = bf16[128,1024]{1,0:T(8,128)(2,1)S(1)} collective-permute-done((bf16[128,1024]{1,0:T(8,128)(2,1)S(1)}, bf16[128,1024]{1,0:T(8,128)(2,1)S(1)}, u32[]{:S(2)}, u32[]{:S(2)}) %collective-permute-start.11) | collective-permute-done | bytes 262176 | tf_op jit(solution)/shard_map/ppermute | solution.py:21
  42.0 4.7 %collective-permute-done.13.refs_6_ = bf16[128,1024]{1,0:T(8,128)(2,1)S(1)} collective-permute-done((bf16[128,1024]{1,0:T(8,128)(2,1)S(1)}, bf16[128,1024]{1,0:T(8,128)(2,1)S(1)}, u32[]{:S(2)}, u32[]{:S(2)}) %collective-permute-start.13) | collective-permute-done | bytes 262176 | tf_op jit(solution)/shard_map/ppermute | solution.py:21
  47.5 2.6 %collective-permute-done.9.refs_2_ = bf16[256,512]{1,0:T(8,128)(2,1)S(1)} collective-permute-done((bf16[256,512]{1,0:T(8,128)(2,1)S(1)}, bf16[256,512]{1,0:T(8,128)(2,1)S(1)}, u32[]{:S(2)}, u32[]{:S(2)}) %collective-permute-start.9) | collective-permute-done | bytes 262176 | tf_op jit(solution)/shard_map/ppermute | solution.py:221
  50.1 3.9 %collective-permute-done.8.refs_1_ = bf16[256,512]{1,0:T(8,128)(2,1)S(1)} collective-permute-done((bf16[256,512]{1,0:T(8,128)(2,1)S(1)}, bf16[256,512]{1,0:T(8,128)(2,1)S(1)}, u32[]{:S(2)}, u32[]{:S(2)}) %collective-permute-start.8) | collective-permute-done | bytes 262176 | tf_op jit(solution)/shard_map/ppermute | solution.py:221
  54.9 2.7 %collective-permute-start.16 = (bf16[512,512]{1,0:T(8,128)(2,1)S(1)}, bf16[512,512]{1,0:T(8,128)(2,1)S(1)}, u32[]{:S(2)}, u32[]{:S(2)}) collective-permute-start(bf16[512,512]{1,0:T(8,128)(2,1)S(1)} %get-tuple-element.43.own_ref), channel_id=1, source_target_pairs={{0,2},{2,0},{1,3},{3,1},{4,6},{6,4},{5,7},{7,5},{8,10},{10,8},{9,1... | collective-permute-start | bytes 1572872 | tf_op jit(solution)/shard_map/ppermute | solution.py:29
  57.6 1.5 %collective-permute-done.16.other_ref = bf16[512,512]{1,0:T(8,128)(2,1)S(1)} collective-permute-done((bf16[512,512]{1,0:T(8,128)(2,1)S(1)}, bf16[512,512]{1,0:T(8,128)(2,1)S(1)}, u32[]{:S(2)}, u32[]{:S(2)}) %collective-permute-start.16) | collective-permute-done | bytes 524320 | tf_op jit(solution)/shard_map/ppermute | solution.py:29
  59.2 2.5 %direct.1 = (f32[512,512]{1,0:T(8,128)S(1)}, f32[512,512]{1,0:T(8,128)S(1)}) custom-call(bf16[512,512]{1,0:T(8,128)(2,1)S(1)} %get-tuple-element.43.own_ref, bf16[512,512]{1,0:T(8,128)(2,1)S(1)} %collective-permute-done.16.other_ref, bf16[128,1024]{1,0:T(8,128)(2,1)S(1)} %pad_maximum_fusion.1.refs_0_, ...), custom_call_target="tpu_custom_call" | custom-call | tf_op jit(solution)/shard_map/direct/pallas_call | solution.py:181
  62.2 2.3 %collective-permute-done.17.got_ref = f32[512,512]{1,0:T(8,128)S(1)} collective-permute-done((f32[512,512]{1,0:T(8,128)S(1)}, f32[512,512]{1,0:T(8,128)S(1)}, u32[]{:S(2)}, u32[]{:S(2)}) %collective-permute-start.17) | collective-permute-done | bytes 1048608 | tf_op jit(solution)/shard_map/ppermute | solution.py:29
  65.7 23.3 %all_to_all.10 = bf16[128,8,512]{2,1,0:T(8,128)(2,1)S(1)} all-to-all(bf16[128,8,512]{2,1,0:T(8,128)(2,1)S(1)} %bitcast.15), channel_id=1, replica_groups=mesh['zh'=2,'y'=4,'x'=4,'core'=2,'zl'=2] {'zh','core','zl','y','x'}, dimensions={0} | all-to-all | bytes 2097152 | tf_op jit(solution)/shard_map/all_to_all | solution.py:25
  (34 shorter events, 10.3 us)
Async XLA Ops:
  0.0 11.0 %copy-start.1 = (bf16[1024,1,64]{0,2,1:T(8,128)(2,1)S(1)}, bf16[1024,1,64]{0,2,1:T(8,128)(2,1)}, u32[]{:S(2)}) copy-start(bf16[1024,1,64]{0,2,1:T(8,128)(2,1)} %param.6) | copy-start | bytes 393220
  0.0 6.7 %copy-start.2 = (bf16[1,8,1024]{2,1,0:T(8,128)(2,1)S(1)}, bf16[1,8,1024]{2,1,0:T(8,128)(2,1)}, u32[]{:S(2)}) copy-start(bf16[1,8,1024]{2,1,0:T(8,128)(2,1)} %param.4) | copy-start | bytes 49156
  0.0 21.6 %collective-permute-start.3 = (bf16[64,1024]{1,0:T(8,128)(2,1)}, bf16[64,1024]{1,0:T(8,128)(2,1)S(1)}, u32[]{:S(2)}, u32[]{:S(2)}) collective-permute-start(bf16[64,1024]{1,0:T(8,128)(2,1)} %bitcast.21), channel_id=1, source_target_pairs={{0,4},{4,8},{8,12},{12,0},{1,5},{5,9},{9,13},{13,1},{2,6},{6,10},{... | collective-permute-start | bytes 393224 | tf_op jit(solution)/shard_map/ppermute | solution.py:21
  3.0 1.6 %copy-start = (f32[128,4096]{1,0:T(8,128)S(1)}, f32[128,4096]{1,0:T(8,128)}, u32[]{:S(2)}) copy-start(f32[128,4096]{1,0:T(8,128)} %in_ref.1) | copy-start | bytes 6291460
  7.4 25.5 %collective-permute-start.2 = (bf16[3,128,1024]{2,1,0:T(8,128)(2,1)}, bf16[3,128,1024]{2,1,0:T(8,128)(2,1)S(1)}, u32[]{:S(2)}, u32[]{:S(2)}) collective-permute-start(bf16[3,128,1024]{2,1,0:T(8,128)(2,1)} %get-tuple-element.32), channel_id=1, source_target_pairs={{0,64},{64,0},{1,65},{65,1},{2,66},{66,2},{3,67},{67,3},{4,68},{68... | collective-permute-start | bytes 2359304 | tf_op jit(solution)/shard_map/ppermute | solution.py:244
  11.0 12.3 %collective-permute-start.5 = (bf16[64,1024]{1,0:T(8,128)(2,1)S(1)}, bf16[64,1024]{1,0:T(8,128)(2,1)S(1)}, u32[]{:S(2)}, u32[]{:S(2)}) collective-permute-start(bf16[64,1024]{1,0:T(8,128)(2,1)S(1)} %bitcast.22), channel_id=1, source_target_pairs={{0,12},{4,0},{8,4},{12,8},{1,13},{5,1},{9,5},{13,9},{2,14},{6,2},{... | collective-permute-start | bytes 393224 | tf_op jit(solution)/shard_map/ppermute | solution.py:21
  12.5 10.8 %collective-permute-start.6 = (bf16[64,1024]{1,0:T(8,128)(2,1)S(1)}, bf16[64,1024]{1,0:T(8,128)(2,1)S(1)}, u32[]{:S(2)}, u32[]{:S(2)}) collective-permute-start(bf16[64,1024]{1,0:T(8,128)(2,1)S(1)} %bitcast.23), channel_id=1, source_target_pairs={{0,8},{4,12},{8,0},{12,4},{1,9},{5,13},{9,1},{13,5},{2,10},{6,14},... | collective-permute-start | bytes 393224 | tf_op jit(solution)/shard_map/ppermute | solution.py:21
  14.0 13.0 %all-to-all-start = ((bf16[16,8,1024]{2,1,0:T(8,128)(2,1)}), bf16[16,8,1024]{2,1,0:T(8,128)(2,1)S(1)}, u32[]{:S(2)}, u32[]{:S(2)}) async-start(bf16[16,8,1024]{2,1,0:T(8,128)(2,1)} %broadcast_in_dim.8), calls=%async_computation | async-start | bytes 524288 | tf_op jit(solution)/shard_map/all_to_all | solution.py:25
  19.5 13.5 %collective-permute-start.1 = (bf16[2,128,1024]{2,1,0:T(8,128)(2,1)}, bf16[2,128,1024]{2,1,0:T(8,128)(2,1)S(1)}, u32[]{:S(2)}, u32[]{:S(2)}) collective-permute-start(bf16[2,128,1024]{2,1,0:T(8,128)(2,1)} %get-tuple-element.31), channel_id=1, source_target_pairs={{0,2},{2,0},{1,3},{3,1},{4,6},{6,4},{5,7},{7,5},{8,10},{10,8},{9,1... | collective-permute-start | bytes 1572872 | tf_op jit(solution)/shard_map/ppermute | solution.py:29
  21.6 11.3 %collective-permute-start.4 = (bf16[128,1024]{1,0:T(8,128)(2,1)S(1)}, bf16[128,1024]{1,0:T(8,128)(2,1)S(1)}, u32[]{:S(2)}, u32[]{:S(2)}) collective-permute-start(bf16[128,1024]{1,0:T(8,128)(2,1)S(1)} %pad_maximum_fusion.1.refs_0_), channel_id=1, source_target_pairs={{0,16},{16,32},{32,48},{48,0},{1,17},{17,33},{33,49},{49,1},{2,18}... | collective-permute-start | bytes 786440 | tf_op jit(solution)/shard_map/ppermute | solution.py:21
  23.3 9.6 %collective-permute-start.7 = (bf16[128,1024]{1,0:T(8,128)(2,1)S(1)}, bf16[128,1024]{1,0:T(8,128)(2,1)S(1)}, u32[]{:S(2)}, u32[]{:S(2)}) collective-permute-start(bf16[128,1024]{1,0:T(8,128)(2,1)S(1)} %constant_dynamic-update-slice_fusion.refs_1_), channel_id=1, source_target_pairs={{0,48},{16,0},{32,16},{48,32},{1,49},{17,1},{33,17},{49,33},{2,50}... | collective-permute-start | bytes 786440 | tf_op jit(solution)/shard_map/ppermute | solution.py:21
  27.0 4.3 %collective-permute-start = (bf16[128,512]{1,0:T(8,128)(2,1)S(1)}, bf16[128,512]{1,0:T(8,128)(2,1)S(1)}, u32[]{:S(2)}, u32[]{:S(2)}) collective-permute-start(bf16[128,512]{1,0:T(8,128)(2,1)S(1)} %get-tuple-element.52), channel_id=1, source_target_pairs={{0,2},{2,0},{1,3},{3,1},{4,6},{6,4},{5,7},{7,5},{8,10},{10,8},{9,1... | collective-permute-start | bytes 393224 | tf_op jit(solution)/shard_map/ppermute | solution.py:29
  31.3 7.5 %collective-permute-start.12 = (bf16[128,1024]{1,0:T(8,128)(2,1)S(1)}, bf16[128,1024]{1,0:T(8,128)(2,1)S(1)}, u32[]{:S(2)}, u32[]{:S(2)}) collective-permute-start(bf16[128,1024]{1,0:T(8,128)(2,1)S(1)} %pad_maximum_fusion.1.refs_0_), channel_id=1, source_target_pairs={{0,48},{16,0},{32,16},{48,32},{1,49},{17,1},{33,17},{49,33},{2,50}... | collective-permute-start | bytes 786440 | tf_op jit(solution)/shard_map/ppermute | solution.py:21
  32.9 8.2 %collective-permute-start.11 = (bf16[128,1024]{1,0:T(8,128)(2,1)S(1)}, bf16[128,1024]{1,0:T(8,128)(2,1)S(1)}, u32[]{:S(2)}, u32[]{:S(2)}) collective-permute-start(bf16[128,1024]{1,0:T(8,128)(2,1)S(1)} %constant_dynamic-update-slice_fusion.refs_1_), channel_id=1, source_target_pairs={{0,16},{16,32},{32,48},{48,0},{1,17},{17,33},{33,49},{49,1},{2,18}... | collective-permute-start | bytes 786440 | tf_op jit(solution)/shard_map/ppermute | solution.py:21
  32.9 13.8 %collective-permute-start.13 = (bf16[128,1024]{1,0:T(8,128)(2,1)S(1)}, bf16[128,1024]{1,0:T(8,128)(2,1)S(1)}, u32[]{:S(2)}, u32[]{:S(2)}) collective-permute-start(bf16[128,1024]{1,0:T(8,128)(2,1)S(1)} %collective-permute-done.4.refs_2_), channel_id=1, source_target_pairs={{0,16},{16,32},{32,48},{48,0},{1,17},{17,33},{33,49},{49,1},{2,18}... | collective-permute-start | bytes 786440 | tf_op jit(solution)/shard_map/ppermute | solution.py:21
  33.8 20.2 %collective-permute-start.15 = (bf16[2,128,1024]{2,1,0:T(8,128)(2,1)S(1)}, bf16[2,128,1024]{2,1,0:T(8,128)(2,1)S(1)}, u32[]{:S(2)}, u32[]{:S(2)}) collective-permute-start(bf16[2,128,1024]{2,1,0:T(8,128)(2,1)S(1)} %slice.3), channel_id=1, source_target_pairs={{0,2},{2,0},{1,3},{3,1},{4,6},{6,4},{5,7},{7,5},{8,10},{10,8},{9,1... | collective-permute-start | bytes 1572872 | tf_op jit(solution)/shard_map/ppermute | solution.py:29
  35.2 12.3 %collective-permute-start.14 = (bf16[128,1024]{1,0:T(8,128)(2,1)S(1)}, bf16[128,1024]{1,0:T(8,128)(2,1)S(1)}, u32[]{:S(2)}, u32[]{:S(2)}) collective-permute-start(bf16[128,1024]{1,0:T(8,128)(2,1)S(1)} %collective-permute-done.7.refs_5_), channel_id=1, source_target_pairs={{0,48},{16,0},{32,16},{48,32},{1,49},{17,1},{33,17},{49,33},{2,50}... | collective-permute-start | bytes 786440 | tf_op jit(solution)/shard_map/ppermute | solution.py:21
  38.9 8.6 %collective-permute-start.10 = (bf16[256,512]{1,0:T(8,128)(2,1)S(1)}, bf16[256,512]{1,0:T(8,128)(2,1)S(1)}, u32[]{:S(2)}, u32[]{:S(2)}) collective-permute-start(bf16[256,512]{1,0:T(8,128)(2,1)S(1)} %pad_maximum_fusion.refs_0_), channel_id=1, source_target_pairs={{0,64},{1,65},{64,0},{65,1},{2,66},{3,67},{66,2},{67,3},{4,68},{5,... | collective-permute-start | bytes 786440 | tf_op jit(solution)/shard_map/ppermute | solution.py:221
  41.1 9.0 %collective-permute-start.9 = (bf16[256,512]{1,0:T(8,128)(2,1)S(1)}, bf16[256,512]{1,0:T(8,128)(2,1)S(1)}, u32[]{:S(2)}, u32[]{:S(2)}) collective-permute-start(bf16[256,512]{1,0:T(8,128)(2,1)S(1)} %pad_maximum_fusion.refs_0_), channel_id=1, source_target_pairs={{0,65},{1,0},{64,1},{65,64},{2,67},{3,2},{66,3},{67,66},{4,69},{5,... | collective-permute-start | bytes 786440 | tf_op jit(solution)/shard_map/ppermute | solution.py:221
  46.8 7.3 %collective-permute-start.8 = (bf16[256,512]{1,0:T(8,128)(2,1)S(1)}, bf16[256,512]{1,0:T(8,128)(2,1)S(1)}, u32[]{:S(2)}, u32[]{:S(2)}) collective-permute-start(bf16[256,512]{1,0:T(8,128)(2,1)S(1)} %pad_maximum_fusion.refs_0_), channel_id=1, source_target_pairs={{0,1},{1,64},{64,65},{65,0},{2,3},{3,66},{66,67},{67,2},{4,5},{5,6... | collective-permute-start | bytes 786440 | tf_op jit(solution)/shard_map/ppermute | solution.py:221
  54.9 4.2 %collective-permute-start.16 = (bf16[512,512]{1,0:T(8,128)(2,1)S(1)}, bf16[512,512]{1,0:T(8,128)(2,1)S(1)}, u32[]{:S(2)}, u32[]{:S(2)}) collective-permute-start(bf16[512,512]{1,0:T(8,128)(2,1)S(1)} %get-tuple-element.43.own_ref), channel_id=1, source_target_pairs={{0,2},{2,0},{1,3},{3,1},{4,6},{6,4},{5,7},{7,5},{8,10},{10,8},{9,1... | collective-permute-start | bytes 1572872 | tf_op jit(solution)/shard_map/ppermute | solution.py:29
  61.7 2.7 %collective-permute-start.17 = (f32[512,512]{1,0:T(8,128)S(1)}, f32[512,512]{1,0:T(8,128)S(1)}, u32[]{:S(2)}, u32[]{:S(2)}) collective-permute-start(f32[512,512]{1,0:T(8,128)S(1)} %get-tuple-element.50), channel_id=1, source_target_pairs={{0,2},{2,0},{1,3},{3,1},{4,6},{6,4},{5,7},{7,5},{8,10},{10,8},{9,1... | collective-permute-start | bytes 3145736 | tf_op jit(solution)/shard_map/ppermute | solution.py:29

commit v7 on v6

--- a/solution.py
+++ b/solution.py
@@ -253,10 +253,10 @@
     passed = swap(far[1:])
     rounds = [pieces, ring(pieces, 1), ring(pieces, -1), ring(pieces, 2)]
     beyond = [shift(behind[0], "y", 1), shift(ahead[1], "y", -1)]
-    rounds, behind[1], ahead[0], beyond = lax.optimization_barrier(
-        (rounds, behind[1], ahead[0], beyond)
-    )
     proj_own, psi = project(rounds, left, near, far, passed)
+    proj_own, behind[1], ahead[0], beyond = lax.optimization_barrier(
+        (proj_own, behind[1], ahead[0], beyond)
+    )
     proj_other = swap(proj_own)
     panel = [*line, *behind, *ahead, *beyond]
     keep, send = direct(proj_own, proj_other, panel, own, [near, far, passed])

time: 90.1 us -> 93.1 us (1.033)
  blocking collectives: 23.3 us -> 26.3 us
  starting transfers between devices: 32 us -> 33.9 us
  waiting for transfers between devices: 23.5 us -> 21.7 us
    ppermute x9, waiting for transfers between devices: 9.76 us -> 6 us  [shift(): return lax.ppermute(value, axis, [(k, (k + by) % n) for k in range(n)])]
    all_to_all x1, blocking collectives: 23.3 us -> 26.3 us  [exchange(): return lax.all_to_all(value, axes, split_axis=0, concat_axis=0, tiled=True)]
    ppermute x3, waiting for transfers between devices: 6.56 us -> 8.52 us  [ring(): lax.ppermute(value, ('zh', 'zl'), [(k, (k + by) % 4) for k in range(4)])]
    ppermute x3, starting transfers between devices: 1.62 us -> 3.41 us  [ring(): lax.ppermute(value, ('zh', 'zl'), [(k, (k + by) % 4) for k in range(4)])]
  transfers between devices with their start and end apart: 19 -> 19, of which waited for: 10 -> 10; matrix products, arithmetic and copies ran while one was open for 2% -> 2% of each run, Pallas kernels for 2% -> 3%
where the time goes in v7:
time: 93.1 us; the launch traced here: 92.9 us
  starting transfers between devices  33.9 us (36%)
  blocking collectives  26.3 us (28%)
  waiting for transfers between devices  21.7 us (23%)
  Pallas kernels  6.73 us (7%)
  local copies, waits for them, and re-layouts  3.38 us (4%)
    all_to_all x1, blocking collectives, exchange(): return lax.all_to_all(value, axes, split_axis=0, concat_axis=0, tiled=True)  26.3 us
    ppermute x9, starting transfers between devices, shift(): return lax.ppermute(value, axis, [(k, (k + by) % n) for k in range(n)])  12.1 us
    ppermute x5, starting transfers between devices, swap(): return lax.ppermute(value, 'core', [(0, 1), (1, 0)])  9.31 us
    ppermute x3, waiting for transfers between devices, ring(): lax.ppermute(value, ('zh', 'zl'), [(k, (k + by) % 4) for k in range(4)])  8.52 us
    ppermute x9, waiting for transfers between devices, shift(): return lax.ppermute(value, axis, [(k, (k + by) % n) for k in range(n)])  6 us
    all_to_all x1, starting transfers between devices, exchange(): return lax.all_to_all(value, axes, split_axis=0, concat_axis=0, tiled=True)  5.45 us
    ppermute x5, waiting for transfers between devices, swap(): return lax.ppermute(value, 'core', [(0, 1), (1, 0)])  4.82 us
    ppermute x1, starting transfers between devices, shards(): far = lax.ppermute(far, 'zh', [(0, 1), (1, 0)])  3.6 us
  transfers between devices with their start and end apart: 19, of which 10 were waited for; matrix products, arithmetic and copies ran while one was open for 2% of the time, Pallas kernels for 3%

profile of v7, /device:TPU:1, one launch (start us, length us, event | category | flops | bytes accessed | tf_op | source)
XLA Modules:
  0.0 92.9 jit_solution(14558754914552959428)
XLA Ops:
  0.0 2.0 %collective-permute-start.3 = (bf16[64,1024]{1,0:T(8,128)(2,1)}, bf16[64,1024]{1,0:T(8,128)(2,1)S(1)}, u32[]{:S(2)}, u32[]{:S(2)}) collective-permute-start(bf16[64,1024]{1,0:T(8,128)(2,1)} %bitcast.21), channel_id=1, source_target_pairs={{0,4},{4,8},{8,12},{12,0},{1,5},{5,9},{9,13},{13,1},{2,6},{6,10},{... | collective-permute-start | bytes 393224 | tf_op jit(solution)/shard_map/ppermute | solution.py:21
  3.1 1.6 %copy-done = f32[128,4096]{1,0:T(8,128)S(1)} copy-done((f32[128,4096]{1,0:T(8,128)S(1)}, f32[128,4096]{1,0:T(8,128)}, u32[]{:S(2)}) %copy-start) | copy-done | bytes 2097176
  4.6 2.1 %pack.1 = (f32[128,1024]{1,0:T(8,128)S(1)}, bf16[2,128,1024]{2,1,0:T(8,128)(2,1)}, bf16[3,128,1024]{2,1,0:T(8,128)(2,1)}) custom-call(f32[128,4096]{1,0:T(8,128)S(1)} %copy-done, bf16[1024,128]{1,0:T(8,128)(2,1)S(1)} %bitcast.16), custom_call_target="tpu_custom_call" | custom-call | tf_op jit(solution)/shard_map/pack/pallas_call | solution.py:71
  7.4 3.6 %collective-permute-start.2 = (bf16[3,128,1024]{2,1,0:T(8,128)(2,1)}, bf16[3,128,1024]{2,1,0:T(8,128)(2,1)S(1)}, u32[]{:S(2)}, u32[]{:S(2)}) collective-permute-start(bf16[3,128,1024]{2,1,0:T(8,128)(2,1)} %get-tuple-element.29), channel_id=1, source_target_pairs={{0,64},{64,0},{1,65},{65,1},{2,66},{66,2},{3,67},{67,3},{4,68},{68... | collective-permute-start | bytes 2359304 | tf_op jit(solution)/shard_map/ppermute | solution.py:244
  11.0 1.5 %collective-permute-start.5 = (bf16[64,1024]{1,0:T(8,128)(2,1)S(1)}, bf16[64,1024]{1,0:T(8,128)(2,1)S(1)}, u32[]{:S(2)}, u32[]{:S(2)}) collective-permute-start(bf16[64,1024]{1,0:T(8,128)(2,1)S(1)} %bitcast.22), channel_id=1, source_target_pairs={{0,12},{4,0},{8,4},{12,8},{1,13},{5,1},{9,5},{13,9},{2,14},{6,2},{... | collective-permute-start | bytes 393224 | tf_op jit(solution)/shard_map/ppermute | solution.py:21
  12.5 1.5 %collective-permute-start.6 = (bf16[64,1024]{1,0:T(8,128)(2,1)S(1)}, bf16[64,1024]{1,0:T(8,128)(2,1)S(1)}, u32[]{:S(2)}, u32[]{:S(2)}) collective-permute-start(bf16[64,1024]{1,0:T(8,128)(2,1)S(1)} %bitcast.23), channel_id=1, source_target_pairs={{0,8},{4,12},{8,0},{12,4},{1,9},{5,13},{9,1},{13,5},{2,10},{6,14},... | collective-permute-start | bytes 393224 | tf_op jit(solution)/shard_map/ppermute | solution.py:21
  14.0 5.4 %all-to-all-start = ((bf16[16,8,1024]{2,1,0:T(8,128)(2,1)}), bf16[16,8,1024]{2,1,0:T(8,128)(2,1)S(1)}, u32[]{:S(2)}, u32[]{:S(2)}) async-start(bf16[16,8,1024]{2,1,0:T(8,128)(2,1)} %broadcast_in_dim.8), calls=%async_computation | async-start | bytes 524288 | tf_op jit(solution)/shard_map/all_to_all | solution.py:25
  19.5 2.2 %collective-permute-start.1 = (bf16[2,128,1024]{2,1,0:T(8,128)(2,1)}, bf16[2,128,1024]{2,1,0:T(8,128)(2,1)S(1)}, u32[]{:S(2)}, u32[]{:S(2)}) collective-permute-start(bf16[2,128,1024]{2,1,0:T(8,128)(2,1)} %get-tuple-element.28), channel_id=1, source_target_pairs={{0,2},{2,0},{1,3},{3,1},{4,6},{6,4},{5,7},{7,5},{8,10},{10,8},{9,1... | collective-permute-start | bytes 1572872 | tf_op jit(solution)/shard_map/ppermute | solution.py:29
  21.6 1.6 %collective-permute-start.4 = (bf16[128,1024]{1,0:T(8,128)(2,1)S(1)}, bf16[128,1024]{1,0:T(8,128)(2,1)S(1)}, u32[]{:S(2)}, u32[]{:S(2)}) collective-permute-start(bf16[128,1024]{1,0:T(8,128)(2,1)S(1)} %pad_maximum_fusion.1.refs_0_), channel_id=1, source_target_pairs={{0,16},{16,32},{32,48},{48,0},{1,17},{17,33},{33,49},{49,1},{2,18}... | collective-permute-start | bytes 786440 | tf_op jit(solution)/shard_map/ppermute | solution.py:21
  24.6 2.4 %all-to-all-done = bf16[16,8,1024]{2,1,0:T(8,128)(2,1)S(1)} async-done(((bf16[16,8,1024]{2,1,0:T(8,128)(2,1)}), bf16[16,8,1024]{2,1,0:T(8,128)(2,1)S(1)}, u32[]{:S(2)}, u32[]{:S(2)}) %all-to-all-start) | async-done | bytes 262176 | tf_op jit(solution)/shard_map/all_to_all | solution.py:25
  27.0 3.3 %collective-permute-start = (bf16[128,512]{1,0:T(8,128)(2,1)S(1)}, bf16[128,512]{1,0:T(8,128)(2,1)S(1)}, u32[]{:S(2)}, u32[]{:S(2)}) collective-permute-start(bf16[128,512]{1,0:T(8,128)(2,1)S(1)} %get-tuple-element.46), channel_id=1, source_target_pairs={{0,2},{2,0},{1,3},{3,1},{4,6},{6,4},{5,7},{7,5},{8,10},{10,8},{9,1... | collective-permute-start | bytes 393224 | tf_op jit(solution)/shard_map/ppermute | solution.py:29
  31.4 1.5 %collective-permute-done.4.refs_2_ = bf16[128,1024]{1,0:T(8,128)(2,1)S(1)} collective-permute-done((bf16[128,1024]{1,0:T(8,128)(2,1)S(1)}, bf16[128,1024]{1,0:T(8,128)(2,1)S(1)}, u32[]{:S(2)}, u32[]{:S(2)}) %collective-permute-start.4) | collective-permute-done | bytes 262176 | tf_op jit(solution)/shard_map/ppermute | solution.py:21
  34.2 3.2 %collective-permute-start.9 = (bf16[256,512]{1,0:T(8,128)(2,1)S(1)}, bf16[256,512]{1,0:T(8,128)(2,1)S(1)}, u32[]{:S(2)}, u32[]{:S(2)}) collective-permute-start(bf16[256,512]{1,0:T(8,128)(2,1)S(1)} %pad_maximum_fusion.refs_0_), channel_id=1, source_target_pairs={{0,65},{1,0},{64,1},{65,64},{2,67},{3,2},{66,3},{67,66},{4,69},{5,... | collective-permute-start | bytes 786440 | tf_op jit(solution)/shard_map/ppermute | solution.py:221
  37.4 1.6 %collective-permute-start.13 = (bf16[128,1024]{1,0:T(8,128)(2,1)S(1)}, bf16[128,1024]{1,0:T(8,128)(2,1)S(1)}, u32[]{:S(2)}, u32[]{:S(2)}) collective-permute-start(bf16[128,1024]{1,0:T(8,128)(2,1)S(1)} %pad_maximum_fusion.1.refs_0_), channel_id=1, source_target_pairs={{0,48},{16,0},{32,16},{48,32},{1,49},{17,1},{33,17},{49,33},{2,50}... | collective-permute-start | bytes 786440 | tf_op jit(solution)/shard_map/ppermute | solution.py:21
  39.0 2.5 %collective-permute-done.10.refs_3_ = bf16[256,512]{1,0:T(8,128)(2,1)S(1)} collective-permute-done((bf16[256,512]{1,0:T(8,128)(2,1)S(1)}, bf16[256,512]{1,0:T(8,128)(2,1)S(1)}, u32[]{:S(2)}, u32[]{:S(2)}) %collective-permute-start.10) | collective-permute-done | bytes 262176 | tf_op jit(solution)/shard_map/ppermute | solution.py:221
  41.8 3.6 %collective-permute-done.9.refs_2_ = bf16[256,512]{1,0:T(8,128)(2,1)S(1)} collective-permute-done((bf16[256,512]{1,0:T(8,128)(2,1)S(1)}, bf16[256,512]{1,0:T(8,128)(2,1)S(1)}, u32[]{:S(2)}, u32[]{:S(2)}) %collective-permute-start.9) | collective-permute-done | bytes 262176 | tf_op jit(solution)/shard_map/ppermute | solution.py:221
  45.8 2.4 %collective-permute-done.8.refs_1_ = bf16[256,512]{1,0:T(8,128)(2,1)S(1)} collective-permute-done((bf16[256,512]{1,0:T(8,128)(2,1)S(1)}, bf16[256,512]{1,0:T(8,128)(2,1)S(1)}, u32[]{:S(2)}, u32[]{:S(2)}) %collective-permute-start.8) | collective-permute-done | bytes 262176 | tf_op jit(solution)/shard_map/ppermute | solution.py:221
  48.2 1.8 %collective-permute-start.15 = (bf16[128,1024]{1,0:T(8,128)(2,1)S(1)}, bf16[128,1024]{1,0:T(8,128)(2,1)S(1)}, u32[]{:S(2)}, u32[]{:S(2)}) collective-permute-start(bf16[128,1024]{1,0:T(8,128)(2,1)S(1)} %collective-permute-done.7.refs_5_), channel_id=1, source_target_pairs={{0,48},{16,0},{32,16},{48,32},{1,49},{17,1},{33,17},{49,33},{2,50}... | collective-permute-start | bytes 786440 | tf_op jit(solution)/shard_map/ppermute | solution.py:21
  50.9 4.0 %collective-permute-done.14.refs_6_ = bf16[128,1024]{1,0:T(8,128)(2,1)S(1)} collective-permute-done((bf16[128,1024]{1,0:T(8,128)(2,1)S(1)}, bf16[128,1024]{1,0:T(8,128)(2,1)S(1)}, u32[]{:S(2)}, u32[]{:S(2)}) %collective-permute-start.14) | collective-permute-done | bytes 262176 | tf_op jit(solution)/shard_map/ppermute | solution.py:21
  55.3 2.4 %collective-permute-start.16 = (bf16[512,512]{1,0:T(8,128)(2,1)S(1)}, bf16[512,512]{1,0:T(8,128)(2,1)S(1)}, u32[]{:S(2)}, u32[]{:S(2)}) collective-permute-start(bf16[512,512]{1,0:T(8,128)(2,1)S(1)} %get-tuple-element.37.own_ref), channel_id=1, source_target_pairs={{0,2},{2,0},{1,3},{3,1},{4,6},{6,4},{5,7},{7,5},{8,10},{10,8},{9,1... | collective-permute-start | bytes 1572872 | tf_op jit(solution)/shard_map/ppermute | solution.py:29
  57.7 1.5 %collective-permute-done.16.other_ref = bf16[512,512]{1,0:T(8,128)(2,1)S(1)} collective-permute-done((bf16[512,512]{1,0:T(8,128)(2,1)S(1)}, bf16[512,512]{1,0:T(8,128)(2,1)S(1)}, u32[]{:S(2)}, u32[]{:S(2)}) %collective-permute-start.16) | collective-permute-done | bytes 524320 | tf_op jit(solution)/shard_map/ppermute | solution.py:29
  59.3 2.5 %direct.1 = (f32[512,512]{1,0:T(8,128)S(1)}, f32[512,512]{1,0:T(8,128)S(1)}) custom-call(bf16[512,512]{1,0:T(8,128)(2,1)S(1)} %get-tuple-element.37.own_ref, bf16[512,512]{1,0:T(8,128)(2,1)S(1)} %collective-permute-done.16.other_ref, bf16[128,1024]{1,0:T(8,128)(2,1)S(1)} %pad_maximum_fusion.1.refs_0_, ...), custom_call_target="tpu_custom_call" | custom-call | tf_op jit(solution)/shard_map/direct/pallas_call | solution.py:181
  62.3 2.3 %collective-permute-done.17.got_ref = f32[512,512]{1,0:T(8,128)S(1)} collective-permute-done((f32[512,512]{1,0:T(8,128)S(1)}, f32[512,512]{1,0:T(8,128)S(1)}, u32[]{:S(2)}, u32[]{:S(2)}) %collective-permute-start.17) | collective-permute-done | bytes 1048608 | tf_op jit(solution)/shard_map/ppermute | solution.py:29
  65.8 26.3 %all_to_all.10 = bf16[128,8,512]{2,1,0:T(8,128)(2,1)S(1)} all-to-all(bf16[128,8,512]{2,1,0:T(8,128)(2,1)S(1)} %bitcast.15), channel_id=1, replica_groups=mesh['zh'=2,'y'=4,'x'=4,'core'=2,'zl'=2] {'zh','core','zl','y','x'}, dimensions={0} | all-to-all | bytes 2097152 | tf_op jit(solution)/shard_map/all_to_all | solution.py:25
  (34 shorter events, 9.9 us)
Async XLA Ops:
  0.0 11.0 %copy-start.1 = (bf16[1024,1,64]{0,2,1:T(8,128)(2,1)S(1)}, bf16[1024,1,64]{0,2,1:T(8,128)(2,1)}, u32[]{:S(2)}) copy-start(bf16[1024,1,64]{0,2,1:T(8,128)(2,1)} %param.6) | copy-start | bytes 393220
  0.0 6.7 %copy-start.2 = (bf16[1,8,1024]{2,1,0:T(8,128)(2,1)S(1)}, bf16[1,8,1024]{2,1,0:T(8,128)(2,1)}, u32[]{:S(2)}) copy-start(bf16[1,8,1024]{2,1,0:T(8,128)(2,1)} %param.4) | copy-start | bytes 49156
  0.0 21.6 %collective-permute-start.3 = (bf16[64,1024]{1,0:T(8,128)(2,1)}, bf16[64,1024]{1,0:T(8,128)(2,1)S(1)}, u32[]{:S(2)}, u32[]{:S(2)}) collective-permute-start(bf16[64,1024]{1,0:T(8,128)(2,1)} %bitcast.21), channel_id=1, source_target_pairs={{0,4},{4,8},{8,12},{12,0},{1,5},{5,9},{9,13},{13,1},{2,6},{6,10},{... | collective-permute-start | bytes 393224 | tf_op jit(solution)/shard_map/ppermute | solution.py:21
  3.0 1.6 %copy-start = (f32[128,4096]{1,0:T(8,128)S(1)}, f32[128,4096]{1,0:T(8,128)}, u32[]{:S(2)}) copy-start(f32[128,4096]{1,0:T(8,128)} %in_ref.1) | copy-start | bytes 6291460
  7.4 25.5 %collective-permute-start.2 = (bf16[3,128,1024]{2,1,0:T(8,128)(2,1)}, bf16[3,128,1024]{2,1,0:T(8,128)(2,1)S(1)}, u32[]{:S(2)}, u32[]{:S(2)}) collective-permute-start(bf16[3,128,1024]{2,1,0:T(8,128)(2,1)} %get-tuple-element.29), channel_id=1, source_target_pairs={{0,64},{64,0},{1,65},{65,1},{2,66},{66,2},{3,67},{67,3},{4,68},{68... | collective-permute-start | bytes 2359304 | tf_op jit(solution)/shard_map/ppermute | solution.py:244
  11.0 12.3 %collective-permute-start.5 = (bf16[64,1024]{1,0:T(8,128)(2,1)S(1)}, bf16[64,1024]{1,0:T(8,128)(2,1)S(1)}, u32[]{:S(2)}, u32[]{:S(2)}) collective-permute-start(bf16[64,1024]{1,0:T(8,128)(2,1)S(1)} %bitcast.22), channel_id=1, source_target_pairs={{0,12},{4,0},{8,4},{12,8},{1,13},{5,1},{9,5},{13,9},{2,14},{6,2},{... | collective-permute-start | bytes 393224 | tf_op jit(solution)/shard_map/ppermute | solution.py:21
  12.5 10.8 %collective-permute-start.6 = (bf16[64,1024]{1,0:T(8,128)(2,1)S(1)}, bf16[64,1024]{1,0:T(8,128)(2,1)S(1)}, u32[]{:S(2)}, u32[]{:S(2)}) collective-permute-start(bf16[64,1024]{1,0:T(8,128)(2,1)S(1)} %bitcast.23), channel_id=1, source_target_pairs={{0,8},{4,12},{8,0},{12,4},{1,9},{5,13},{9,1},{13,5},{2,10},{6,14},... | collective-permute-start | bytes 393224 | tf_op jit(solution)/shard_map/ppermute | solution.py:21
  14.0 13.0 %all-to-all-start = ((bf16[16,8,1024]{2,1,0:T(8,128)(2,1)}), bf16[16,8,1024]{2,1,0:T(8,128)(2,1)S(1)}, u32[]{:S(2)}, u32[]{:S(2)}) async-start(bf16[16,8,1024]{2,1,0:T(8,128)(2,1)} %broadcast_in_dim.8), calls=%async_computation | async-start | bytes 524288 | tf_op jit(solution)/shard_map/all_to_all | solution.py:25
  19.5 13.4 %collective-permute-start.1 = (bf16[2,128,1024]{2,1,0:T(8,128)(2,1)}, bf16[2,128,1024]{2,1,0:T(8,128)(2,1)S(1)}, u32[]{:S(2)}, u32[]{:S(2)}) collective-permute-start(bf16[2,128,1024]{2,1,0:T(8,128)(2,1)} %get-tuple-element.28), channel_id=1, source_target_pairs={{0,2},{2,0},{1,3},{3,1},{4,6},{6,4},{5,7},{7,5},{8,10},{10,8},{9,1... | collective-permute-start | bytes 1572872 | tf_op jit(solution)/shard_map/ppermute | solution.py:29
  21.6 11.3 %collective-permute-start.4 = (bf16[128,1024]{1,0:T(8,128)(2,1)S(1)}, bf16[128,1024]{1,0:T(8,128)(2,1)S(1)}, u32[]{:S(2)}, u32[]{:S(2)}) collective-permute-start(bf16[128,1024]{1,0:T(8,128)(2,1)S(1)} %pad_maximum_fusion.1.refs_0_), channel_id=1, source_target_pairs={{0,16},{16,32},{32,48},{48,0},{1,17},{17,33},{33,49},{49,1},{2,18}... | collective-permute-start | bytes 786440 | tf_op jit(solution)/shard_map/ppermute | solution.py:21
  23.3 9.6 %collective-permute-start.7 = (bf16[128,1024]{1,0:T(8,128)(2,1)S(1)}, bf16[128,1024]{1,0:T(8,128)(2,1)S(1)}, u32[]{:S(2)}, u32[]{:S(2)}) collective-permute-start(bf16[128,1024]{1,0:T(8,128)(2,1)S(1)} %constant_dynamic-update-slice_fusion.refs_1_), channel_id=1, source_target_pairs={{0,48},{16,0},{32,16},{48,32},{1,49},{17,1},{33,17},{49,33},{2,50}... | collective-permute-start | bytes 786440 | tf_op jit(solution)/shard_map/ppermute | solution.py:21
  27.0 4.3 %collective-permute-start = (bf16[128,512]{1,0:T(8,128)(2,1)S(1)}, bf16[128,512]{1,0:T(8,128)(2,1)S(1)}, u32[]{:S(2)}, u32[]{:S(2)}) collective-permute-start(bf16[128,512]{1,0:T(8,128)(2,1)S(1)} %get-tuple-element.46), channel_id=1, source_target_pairs={{0,2},{2,0},{1,3},{3,1},{4,6},{6,4},{5,7},{7,5},{8,10},{10,8},{9,1... | collective-permute-start | bytes 393224 | tf_op jit(solution)/shard_map/ppermute | solution.py:29
  32.9 8.6 %collective-permute-start.10 = (bf16[256,512]{1,0:T(8,128)(2,1)S(1)}, bf16[256,512]{1,0:T(8,128)(2,1)S(1)}, u32[]{:S(2)}, u32[]{:S(2)}) collective-permute-start(bf16[256,512]{1,0:T(8,128)(2,1)S(1)} %pad_maximum_fusion.refs_0_), channel_id=1, source_target_pairs={{0,64},{1,65},{64,0},{65,1},{2,66},{3,67},{66,2},{67,3},{4,68},{5,... | collective-permute-start | bytes 786440 | tf_op jit(solution)/shard_map/ppermute | solution.py:221
  33.2 16.8 %collective-permute-start.11 = (bf16[2,128,1024]{2,1,0:T(8,128)(2,1)S(1)}, bf16[2,128,1024]{2,1,0:T(8,128)(2,1)S(1)}, u32[]{:S(2)}, u32[]{:S(2)}) collective-permute-start(bf16[2,128,1024]{2,1,0:T(8,128)(2,1)S(1)} %slice.3), channel_id=1, source_target_pairs={{0,2},{2,0},{1,3},{3,1},{4,6},{6,4},{5,7},{7,5},{8,10},{10,8},{9,1... | collective-permute-start | bytes 1572872 | tf_op jit(solution)/shard_map/ppermute | solution.py:29
  34.2 11.2 %collective-permute-start.9 = (bf16[256,512]{1,0:T(8,128)(2,1)S(1)}, bf16[256,512]{1,0:T(8,128)(2,1)S(1)}, u32[]{:S(2)}, u32[]{:S(2)}) collective-permute-start(bf16[256,512]{1,0:T(8,128)(2,1)S(1)} %pad_maximum_fusion.refs_0_), channel_id=1, source_target_pairs={{0,65},{1,0},{64,1},{65,64},{2,67},{3,2},{66,3},{67,66},{4,69},{5,... | collective-permute-start | bytes 786440 | tf_op jit(solution)/shard_map/ppermute | solution.py:221
  37.4 10.8 %collective-permute-start.8 = (bf16[256,512]{1,0:T(8,128)(2,1)S(1)}, bf16[256,512]{1,0:T(8,128)(2,1)S(1)}, u32[]{:S(2)}, u32[]{:S(2)}) collective-permute-start(bf16[256,512]{1,0:T(8,128)(2,1)S(1)} %pad_maximum_fusion.refs_0_), channel_id=1, source_target_pairs={{0,1},{1,64},{64,65},{65,0},{2,3},{3,66},{66,67},{67,2},{4,5},{5,6... | collective-permute-start | bytes 786440 | tf_op jit(solution)/shard_map/ppermute | solution.py:221
  37.4 13.5 %collective-permute-start.13 = (bf16[128,1024]{1,0:T(8,128)(2,1)S(1)}, bf16[128,1024]{1,0:T(8,128)(2,1)S(1)}, u32[]{:S(2)}, u32[]{:S(2)}) collective-permute-start(bf16[128,1024]{1,0:T(8,128)(2,1)S(1)} %pad_maximum_fusion.1.refs_0_), channel_id=1, source_target_pairs={{0,48},{16,0},{32,16},{48,32},{1,49},{17,1},{33,17},{49,33},{2,50}... | collective-permute-start | bytes 786440 | tf_op jit(solution)/shard_map/ppermute | solution.py:21
  41.5 9.4 %collective-permute-start.12 = (bf16[128,1024]{1,0:T(8,128)(2,1)S(1)}, bf16[128,1024]{1,0:T(8,128)(2,1)S(1)}, u32[]{:S(2)}, u32[]{:S(2)}) collective-permute-start(bf16[128,1024]{1,0:T(8,128)(2,1)S(1)} %constant_dynamic-update-slice_fusion.refs_1_), channel_id=1, source_target_pairs={{0,16},{16,32},{32,48},{48,0},{1,17},{17,33},{33,49},{49,1},{2,18}... | collective-permute-start | bytes 786440 | tf_op jit(solution)/shard_map/ppermute | solution.py:21
  45.4 9.5 %collective-permute-start.14 = (bf16[128,1024]{1,0:T(8,128)(2,1)S(1)}, bf16[128,1024]{1,0:T(8,128)(2,1)S(1)}, u32[]{:S(2)}, u32[]{:S(2)}) collective-permute-start(bf16[128,1024]{1,0:T(8,128)(2,1)S(1)} %collective-permute-done.4.refs_2_), channel_id=1, source_target_pairs={{0,16},{16,32},{32,48},{48,0},{1,17},{17,33},{33,49},{49,1},{2,18}... | collective-permute-start | bytes 786440 | tf_op jit(solution)/shard_map/ppermute | solution.py:21
  48.2 7.2 %collective-permute-start.15 = (bf16[128,1024]{1,0:T(8,128)(2,1)S(1)}, bf16[128,1024]{1,0:T(8,128)(2,1)S(1)}, u32[]{:S(2)}, u32[]{:S(2)}) collective-permute-start(bf16[128,1024]{1,0:T(8,128)(2,1)S(1)} %collective-permute-done.7.refs_5_), channel_id=1, source_target_pairs={{0,48},{16,0},{32,16},{48,32},{1,49},{17,1},{33,17},{49,33},{2,50}... | collective-permute-start | bytes 786440 | tf_op jit(solution)/shard_map/ppermute | solution.py:21
  55.3 3.9 %collective-permute-start.16 = (bf16[512,512]{1,0:T(8,128)(2,1)S(1)}, bf16[512,512]{1,0:T(8,128)(2,1)S(1)}, u32[]{:S(2)}, u32[]{:S(2)}) collective-permute-start(bf16[512,512]{1,0:T(8,128)(2,1)S(1)} %get-tuple-element.37.own_ref), channel_id=1, source_target_pairs={{0,2},{2,0},{1,3},{3,1},{4,6},{6,4},{5,7},{7,5},{8,10},{10,8},{9,1... | collective-permute-start | bytes 1572872 | tf_op jit(solution)/shard_map/ppermute | solution.py:29
  61.8 2.7 %collective-permute-start.17 = (f32[512,512]{1,0:T(8,128)S(1)}, f32[512,512]{1,0:T(8,128)S(1)}, u32[]{:S(2)}, u32[]{:S(2)}) collective-permute-start(f32[512,512]{1,0:T(8,128)S(1)} %get-tuple-element.44), channel_id=1, source_target_pairs={{0,2},{2,0},{1,3},{3,1},{4,6},{6,4},{5,7},{7,5},{8,10},{10,8},{9,1... | collective-permute-start | bytes 3145736 | tf_op jit(solution)/shard_map/ppermute | solution.py:29

commit v8 on v7

--- a/solution.py
+++ b/solution.py
@@ -9,7 +9,7 @@
 TILE_VEC = ("zh", "y", "x", "core", "zl")
 TILE = ("zh", "y", "x", "core")
 PLANE = ("y", "x")
-ORDER = ("zh", "core", "zl", "y", "x")
+ORDER = ("y", "x", "zh", "zl", "core")
 STEPS = (0, -1, 1, -2)
 F32 = jnp.float32
 BF16 = jnp.bfloat16
@@ -90,23 +90,12 @@
     )(screened, left)
 
 
-def project(rounds, left, near, far, passed):
+def project(trial_half, left, near, far, passed):
     states, points = left.shape
-    block = rounds[0].shape[0] // 2
-    cols = rounds[0].shape[1]
-
-    def kernel(*refs):
-        trial_refs, left_ref, boxes, (out_ref, psi_ref, trial) = refs[:4], refs[4], refs[5:8], refs[8:]
-        core = lax.axis_index("core")
-        place = 2 * lax.axis_index("zh") + lax.axis_index("zl")
-        for k in range(4):
-            source = lax.rem(place + STEPS[k] + 4, 4)
-            for m in range(2):
-                owner = core if m == 0 else 1 - core
-                group = lax.div(source, 2) * 4 + owner * 2 + lax.rem(source, 2)
-                trial[pl.ds(pl.multiple_of(group * block, block), block), :] = trial_refs[k][
-                    m * block : (m + 1) * block, :
-                ]
+    cols = trial_half.shape[1]
+
+    def kernel(trial_ref, left_ref, *refs):
+        boxes, (out_ref, psi_ref) = refs[:3], refs[3:]
         psi_ref[:, :points] = left_ref[...]
         for k in range(1, 4):
             box = boxes[k - 1]
@@ -115,7 +104,7 @@
                     box.shape[0] - 1, :, g * points : (g + 1) * points
                 ]
         out_ref[...] = lax.dot_general(
-            psi_ref[...], trial[...], (((0,), (0,)), ((), ())), preferred_element_type=F32
+            psi_ref[...], trial_ref[...], (((0,), (0,)), ((), ())), preferred_element_type=F32
         ).astype(BF16)
 
     return pl.pallas_call(
@@ -124,28 +113,28 @@
             jax.ShapeDtypeStruct((4 * points, cols), BF16),
             jax.ShapeDtypeStruct((states, 4 * points), BF16),
         ],
-        in_specs=[vmem_spec()] * 8,
+        in_specs=[vmem_spec()] * 5,
         out_specs=[vmem_spec()] * 2,
-        scratch_shapes=[pltpu.VMEM((states, cols), BF16)],
         compiler_params=params(12),
         name="project",
-    )(*rounds, left, near, far, passed)
+    )(trial_half, left, near, far, passed)
 
 
 def direct(proj_own, proj_other, lines, own, boxes):
     rows, half = proj_own.shape
     points = rows // 4
-    block = lines[0].shape[0] // 2
+    block = lines[0].shape[0] // 4
     count, states = 16 * block, lines[0].shape[1]
     chunk = 512
 
     def kernel(own_ref, other_ref, *refs):
-        line_refs, scr_refs, (keep_ref, send_ref, proj, panel_ref) = refs[:8], refs[8:12], refs[12:]
+        line_refs, scr_refs, (keep_ref, send_ref, proj, panel_ref) = refs[:5], refs[5:9], refs[9:]
         y, x = lax.axis_index("y"), lax.axis_index("x")
         for k in range(16):
             at = lax.rem(y + STEPS[k // 4] + 4, 4) * 4 + lax.rem(x + STEPS[k % 4] + 4, 4)
-            panel_ref[pl.ds(pl.multiple_of(at * block, block), block), :] = line_refs[k // 2][
-                k % 2 * block : (k % 2 + 1) * block, :
+            ref, row = (line_refs[k // 4], k % 4) if k < 12 else (line_refs[k // 2 - 3], k % 2)
+            panel_ref[pl.ds(pl.multiple_of(at * block, block), block), :] = ref[
+                row * block : (row + 1) * block, :
             ]
         core = lax.axis_index("core")
         mine = pl.ds(pl.multiple_of(core * half, half), half)
@@ -181,7 +170,7 @@
     return pl.pallas_call(
         kernel,
         out_shape=[jax.ShapeDtypeStruct((rows, half), F32)] * 2,
-        in_specs=[vmem_spec()] * 14,
+        in_specs=[vmem_spec()] * 11,
         out_specs=[vmem_spec()] * 2,
         scratch_shapes=[pltpu.VMEM((rows, half), BF16), pltpu.VMEM((count, states), BF16)],
         compiler_params=params(24),
@@ -231,40 +220,36 @@
     half = states // 2
     devices = lax.axis_size(ORDER)
     core = lax.axis_index("core")
-    left = psi_v.reshape(2, 4, 4, 2, 2, rows, -1).transpose(0, 3, 4, 1, 2, 5, 6).reshape(psi_v.shape)
+    place = 2 * lax.axis_index("zh") + lax.axis_index("zl")
+    left = psi_v.reshape(2, 4, 4, 2, 2, rows, -1).transpose(1, 2, 0, 4, 3, 5, 6).reshape(psi_v.shape)
+    mine = lax.dynamic_slice_in_dim(trial[0], core * half, half, 1)
+    got = swap(lax.dynamic_slice_in_dim(trial[0], (1 - core) * half, half, 1))
+    pair = jnp.concatenate([jnp.where(core == 0, mine, got), jnp.where(core == 0, got, mine)], 0)
+    steps = [pair, ring(pair, -1), ring(pair, 2), ring(pair, 1)]
+    column = jnp.concatenate(
+        [lax.select_n(place, *(steps[(to - at) % 4] for at in range(4))) for to in range(4)], 0
+    )
+    block = psi_c[:, 0, :].T
+    line = jnp.concatenate([block, shift(block, "x", 1), shift(block, "x", -1), shift(block, "x", 2)], 0)
     own, near, far = pack(screened, left)
-    block = psi_c[:, 0, :].T
-    line = [
-        jnp.concatenate([block, shift(block, "x", 1)], 0),
-        jnp.concatenate([shift(block, "x", -1), shift(block, "x", 2)], 0),
-    ]
-    copies, near, far = lax.optimization_barrier((to_all(trial[0]), near, far))
-    level = exchange(copies, PLANE).reshape(-1, states)
+    copies, near, far, line = lax.optimization_barrier((to_all(column), near, far, line))
+    trial_half = exchange(copies, PLANE).reshape(-1, half)
     near = swap(near)
     far = lax.ppermute(far, "zh", [(0, 1), (1, 0)])
-    behind = [shift(part, "y", 1) for part in line]
-    ahead = [shift(part, "y", -1) for part in line]
-    mine = lax.dynamic_slice_in_dim(level, core * half, half, 1)
-    sent = lax.dynamic_slice_in_dim(level, (1 - core) * half, half, 1)
-    pieces = jnp.concatenate([mine, swap(sent)], 0)
-    pieces, near, far, behind[0], ahead[1] = lax.optimization_barrier(
-        (pieces, near, far, behind[0], ahead[1])
-    )
+    behind, ahead = shift(line, "y", 1), shift(line, "y", -1)
+    far, behind, ahead = lax.optimization_barrier((far, behind, ahead))
     passed = swap(far[1:])
-    rounds = [pieces, ring(pieces, 1), ring(pieces, -1), ring(pieces, 2)]
-    beyond = [shift(behind[0], "y", 1), shift(ahead[1], "y", -1)]
-    proj_own, psi = project(rounds, left, near, far, passed)
-    proj_own, behind[1], ahead[0], beyond = lax.optimization_barrier(
-        (proj_own, behind[1], ahead[0], beyond)
-    )
+    middle = line.shape[0] // 2
+    beyond = [shift(behind[:middle], "y", 1), shift(ahead[middle:], "y", -1)]
+    proj_own, psi = project(trial_half, left, near, far, passed)
     proj_other = swap(proj_own)
-    panel = [*line, *behind, *ahead, *beyond]
+    panel = [line, behind, ahead, *beyond]
     keep, send = direct(proj_own, proj_other, panel, own, [near, far, passed])
     got = swap(send)
     term = finish(psi, keep, got)
     parts = exchange(term.reshape(devices, rows, half), ORDER)
-    parts = parts.reshape(2, 2, 2, -1, rows, half).astype(F32)
-    total = jnp.sum(parts, axis=(0, 2, 3))
+    parts = parts.reshape(-1, 2, rows, half).astype(F32)
+    total = jnp.sum(parts, axis=0)
     return total.transpose(1, 0, 2).reshape(1, rows, states)
 
 

time: 93.1 us -> 103 us (1.11)
  local copies, waits for them, and re-layouts: 3.38 us -> 8.76 us
  blocking collectives: 26.3 us -> 22.8 us
  starting transfers between devices: 33.9 us -> 36.5 us
  waiting for transfers between devices: 21.7 us -> 24.2 us
  Pallas kernels: 6.73 us -> 9.02 us
    ppermute x9 -> x7, waiting for transfers between devices: 6 us -> 19.2 us  [shift(): return lax.ppermute(value, axis, [(k, (k + by) % n) for k in range(n)])]
    ppermute x3, waiting for transfers between devices: 8.52 us -> 0.01 us  [ring(): lax.ppermute(value, ('zh', 'zl'), [(k, (k + by) % 4) for k in range(4)])]
    ppermute x5, starting transfers between devices: 9.31 us -> 17.8 us  [swap(): return lax.ppermute(value, 'core', [(0, 1), (1, 0)])]
    ppermute x9 -> x7, starting transfers between devices: 12.1 us -> 8.47 us  [shift(): return lax.ppermute(value, axis, [(k, (k + by) % n) for k in range(n)])]
    all_to_all x1, blocking collectives: 26.3 us -> 22.8 us  [exchange(): return lax.all_to_all(value, axes, split_axis=0, concat_axis=0, tiled=True)]
    ppermute x1, starting transfers between devices: 3.6 us -> 1.06 us  [shards(): far = lax.ppermute(far, 'zh', [(0, 1), (1, 0)])]
    all_to_all x1, waiting for transfers between devices: 2.39 us -> 0.01 us  [exchange(): return lax.all_to_all(value, axes, split_axis=0, concat_axis=0, tiled=True)]
    slice x0 -> x2, local copies, waits for them, and re-layouts: none -> 1.94 us  [shards(): beyond = [shift(behind[:middle], 'y', 1), shift(ahead[middle:], 'y', -1)]]
  transfers between devices with their start and end apart: 19 -> 17, of which waited for: 10 -> 8; matrix products, arithmetic and copies ran while one was open for 2% -> 4% of each run, Pallas kernels for 3% -> 2%
where the time goes in v8:
time: 103 us
  starting transfers between devices  36.5 us (35%)
  waiting for transfers between devices  24.2 us (23%)
  blocking collectives  22.8 us (22%)
  Pallas kernels  9.02 us (9%)
  local copies, waits for them, and re-layouts  8.76 us (9%)
  other arithmetic  1.56 us (2%)
    all_to_all x1, blocking collectives, exchange(): return lax.all_to_all(value, axes, split_axis=0, concat_axis=0, tiled=True)  22.8 us
    ppermute x7, waiting for transfers between devices, shift(): return lax.ppermute(value, axis, [(k, (k + by) % n) for k in range(n)])  19.2 us
    ppermute x5, starting transfers between devices, swap(): return lax.ppermute(value, 'core', [(0, 1), (1, 0)])  17.8 us
    ppermute x7, starting transfers between devices, shift(): return lax.ppermute(value, axis, [(k, (k + by) % n) for k in range(n)])  8.47 us
    ppermute x3, starting transfers between devices, ring(): lax.ppermute(value, ('zh', 'zl'), [(k, (k + by) % 4) for k in range(4)])  5.15 us
    ppermute x5, waiting for transfers between devices, swap(): return lax.ppermute(value, 'core', [(0, 1), (1, 0)])  4.99 us
    all_to_all x1, starting transfers between devices, exchange(): return lax.all_to_all(value, axes, split_axis=0, concat_axis=0, tiled=True)  4.05 us
    pallas_call x1, Pallas kernels, direct(): pl.pallas_call(kernel, out_shape=[jax.ShapeDtypeStruct((rows, half), F32)...  3.87 us
  transfers between devices with their start and end apart: 17, of which 8 were waited for; matrix products, arithmetic and copies ran while one was open for 4% of the time, Pallas kernels for 2%

profile of v8, /device:TPU:1, one launch (start us, length us, event | category | flops | bytes accessed | tf_op | source)
XLA Modules:
  0.0 102.9 jit_solution(1991066947623222222)
XLA Ops:
  0.7 1.4 %collective-permute-start = (bf16[8,512]{1,0:T(8,128)(2,1)S(1)}, bf16[8,512]{1,0:T(8,128)(2,1)S(1)}, u32[]{:S(2)}, u32[]{:S(2)}) collective-permute-start(bf16[8,512]{1,0:T(8,128)(2,1)S(1)} %dynamic-slice_bitcast_fusion), channel_id=1, source_target_pairs={{0,2},{2,0},{1,3},{3,1},{4,6},{6,4},{5,7},{7,5},{8,10},{10,8},{9,1... | collective-permute-start | bytes 24584 | tf_op jit(solution)/shard_map/ppermute | solution.py:29
  3.7 3.7 %collective-permute-start.2 = (bf16[16,512]{1,0:T(8,128)(2,1)S(1)}, bf16[16,512]{1,0:T(8,128)(2,1)S(1)}, u32[]{:S(2)}, u32[]{:S(2)}) collective-permute-start(bf16[16,512]{1,0:T(8,128)(2,1)S(1)} %pad_maximum_fusion.2), channel_id=1, source_target_pairs={{0,64},{1,65},{64,0},{65,1},{2,66},{3,67},{66,2},{67,3},{4,68},{5,... | collective-permute-start | bytes 49160 | tf_op jit(solution)/shard_map/ppermute | solution.py:210
  8.8 2.7 %collective-permute-start.6 = (bf16[64,1024]{1,0:T(8,128)(2,1)}, bf16[64,1024]{1,0:T(8,128)(2,1)S(1)}, u32[]{:S(2)}, u32[]{:S(2)}) collective-permute-start(bf16[64,1024]{1,0:T(8,128)(2,1)} %bitcast.25), channel_id=1, source_target_pairs={{0,8},{4,12},{8,0},{12,4},{1,9},{5,13},{9,1},{13,5},{2,10},{6,14},... | collective-permute-start | bytes 393224 | tf_op jit(solution)/shard_map/ppermute | solution.py:21
  13.5 1.6 %copy-done = f32[128,4096]{1,0:T(8,128)S(1)} copy-done((f32[128,4096]{1,0:T(8,128)S(1)}, f32[128,4096]{1,0:T(8,128)}, u32[]{:S(2)}) %copy-start) | copy-done | bytes 2097176
  15.1 2.0 %pack.1 = (f32[128,1024]{1,0:T(8,128)S(1)}, bf16[2,128,1024]{2,1,0:T(8,128)(2,1)S(1)}, bf16[3,128,1024]{2,1,0:T(8,128)(2,1)}) custom-call(f32[128,4096]{1,0:T(8,128)S(1)} %copy-done, bf16[1024,128]{1,0:T(8,128)(2,1)S(1)} %bitcast.21), custom_call_target="tpu_custom_call" | custom-call | tf_op jit(solution)/shard_map/pack/pallas_call | solution.py:71
  19.3 4.4 %collective-permute-done.4 = bf16[64,1024]{1,0:T(8,128)(2,1)S(1)} collective-permute-done((bf16[64,1024]{1,0:T(8,128)(2,1)S(1)}, bf16[64,1024]{1,0:T(8,128)(2,1)S(1)}, u32[]{:S(2)}, u32[]{:S(2)}) %collective-permute-start.4) | collective-permute-done | bytes 131104 | tf_op jit(solution)/shard_map/ppermute | solution.py:21
  23.7 1.1 %broadcast_in_dim.2 = bf16[16,64,512]{2,1,0:T(8,128)(2,1)} broadcast(bf16[64,512]{1,0:T(8,128)(2,1)S(1)} %pad_maximum_fusion.1), dimensions={1,2} | broadcast | bytes 1114112 | tf_op jit(solution)/shard_map/broadcast_in_dim | solution.py:214
  24.8 1.1 %collective-permute-start.8 = (bf16[3,128,1024]{2,1,0:T(8,128)(2,1)}, bf16[3,128,1024]{2,1,0:T(8,128)(2,1)S(1)}, u32[]{:S(2)}, u32[]{:S(2)}) collective-permute-start(bf16[3,128,1024]{2,1,0:T(8,128)(2,1)} %get-tuple-element.23), channel_id=1, source_target_pairs={{0,64},{64,0},{1,65},{65,1},{2,66},{66,2},{3,67},{67,3},{4,68},{68... | collective-permute-start | bytes 2359304 | tf_op jit(solution)/shard_map/ppermute | solution.py:238
  25.8 2.7 %collective-permute-start.10 = (bf16[256,1024]{1,0:T(8,128)(2,1)S(1)}, bf16[256,1024]{1,0:T(8,128)(2,1)}, u32[]{:S(2)}, u32[]{:S(2)}) collective-permute-start(bf16[256,1024]{1,0:T(8,128)(2,1)S(1)} %pad_maximum_fusion.refs_0_), channel_id=1, source_target_pairs={{0,48},{16,0},{32,16},{48,32},{1,49},{17,1},{33,17},{49,33},{2,50}... | collective-permute-start | bytes 1572872 | tf_op jit(solution)/shard_map/ppermute | solution.py:21
  28.6 4.1 %all-to-all-start = ((bf16[16,64,512]{2,1,0:T(8,128)(2,1)}), bf16[16,64,512]{2,1,0:T(8,128)(2,1)S(1)}, u32[]{:S(2)}, u32[]{:S(2)}) async-start(bf16[16,64,512]{2,1,0:T(8,128)(2,1)} %broadcast_in_dim.2), calls=%async_computation | async-start | bytes 2097152 | tf_op jit(solution)/shard_map/all_to_all | solution.py:25
  32.6 3.8 %collective-permute-start.7 = (bf16[2,128,1024]{2,1,0:T(8,128)(2,1)}, bf16[2,128,1024]{2,1,0:T(8,128)(2,1)S(1)}, u32[]{:S(2)}, u32[]{:S(2)}) collective-permute-start(bf16[2,128,1024]{2,1,0:T(8,128)(2,1)} %copy-done.3), channel_id=1, source_target_pairs={{0,2},{2,0},{1,3},{3,1},{4,6},{6,4},{5,7},{7,5},{8,10},{10,8},{9,1... | collective-permute-start | bytes 1572872 | tf_op jit(solution)/shard_map/ppermute | solution.py:29
  36.4 6.1 %collective-permute-done.10.refs_2_ = bf16[256,1024]{1,0:T(8,128)(2,1)} collective-permute-done((bf16[256,1024]{1,0:T(8,128)(2,1)S(1)}, bf16[256,1024]{1,0:T(8,128)(2,1)}, u32[]{:S(2)}, u32[]{:S(2)}) %collective-permute-start.10) | collective-permute-done | bytes 524320 | tf_op jit(solution)/shard_map/ppermute | solution.py:21
  42.6 1.3 %collective-permute-done.9.refs_1_ = bf16[256,1024]{1,0:T(8,128)(2,1)} collective-permute-done((bf16[256,1024]{1,0:T(8,128)(2,1)S(1)}, bf16[256,1024]{1,0:T(8,128)(2,1)}, u32[]{:S(2)}, u32[]{:S(2)}) %collective-permute-start.9) | collective-permute-done | bytes 524320 | tf_op jit(solution)/shard_map/ppermute | solution.py:21
  44.7 10.9 %collective-permute-start.11 = (bf16[2,128,1024]{2,1,0:T(8,128)(2,1)}, bf16[2,128,1024]{2,1,0:T(8,128)(2,1)}, u32[]{:S(2)}, u32[]{:S(2)}) collective-permute-start(bf16[2,128,1024]{2,1,0:T(8,128)(2,1)} %slice.9), channel_id=1, source_target_pairs={{0,2},{2,0},{1,3},{3,1},{4,6},{6,4},{5,7},{7,5},{8,10},{10,8},{9,1... | collective-permute-start | bytes 1572872 | tf_op jit(solution)/shard_map/ppermute | solution.py:29
  55.6 1.9 %collective-permute-done.11.refs_2_.refs_8_ = bf16[2,128,1024]{2,1,0:T(8,128)(2,1)} collective-permute-done((bf16[2,128,1024]{2,1,0:T(8,128)(2,1)}, bf16[2,128,1024]{2,1,0:T(8,128)(2,1)}, u32[]{:S(2)}, u32[]{:S(2)}) %collective-permute-start.11) | collective-permute-done | bytes 524320 | tf_op jit(solution)/shard_map/ppermute | solution.py:29
  57.4 1.9 %project.1 = (bf16[512,512]{1,0:T(8,128)(2,1)S(1)}, bf16[1024,512]{1,0:T(8,128)(2,1)S(1)}) custom-call(bf16[1024,512]{1,0:T(8,128)(2,1)S(1)} %bitcast.19, bf16[1024,128]{1,0:T(8,128)(2,1)S(1)} %bitcast.22, bf16[2,128,1024]{2,1,0:T(8,128)(2,1)S(1)} %collective-permute-done.7.refs_0_.refs_6_, bf16[3,128,1024]{2,1,0:T(8,128)(2,1)S(1)} %collective-permute-done.8.refs_1_.refs_7_, ...), custom_call_target="tpu_custom_call" | custom-call | tf_op jit(solution)/shard_map/project/pallas_call | solution.py:110
  61.8 1.5 %collective-permute-start.13 = (bf16[128,1024]{1,0:T(8,128)(2,1)S(1)}, bf16[128,1024]{1,0:T(8,128)(2,1)S(1)}, u32[]{:S(2)}, u32[]{:S(2)}) collective-permute-start(bf16[128,1024]{1,0:T(8,128)(2,1)S(1)} %slice.10), channel_id=1, source_target_pairs={{0,16},{16,32},{32,48},{48,0},{1,17},{17,33},{33,49},{49,1},{2,18}... | collective-permute-start | bytes 786440 | tf_op jit(solution)/shard_map/ppermute | solution.py:21
  63.3 6.3 %collective-permute-done.14.refs_4_ = bf16[128,1024]{1,0:T(8,128)(2,1)S(1)} collective-permute-done((bf16[128,1024]{1,0:T(8,128)(2,1)S(1)}, bf16[128,1024]{1,0:T(8,128)(2,1)S(1)}, u32[]{:S(2)}, u32[]{:S(2)}) %collective-permute-start.14) | collective-permute-done | bytes 262176 | tf_op jit(solution)/shard_map/ppermute | solution.py:21
  69.6 1.1 %collective-permute-done.13.refs_3_ = bf16[128,1024]{1,0:T(8,128)(2,1)S(1)} collective-permute-done((bf16[128,1024]{1,0:T(8,128)(2,1)S(1)}, bf16[128,1024]{1,0:T(8,128)(2,1)S(1)}, u32[]{:S(2)}, u32[]{:S(2)}) %collective-permute-start.13) | collective-permute-done | bytes 262176 | tf_op jit(solution)/shard_map/ppermute | solution.py:21
  70.7 3.9 %direct.1 = (f32[512,512]{1,0:T(8,128)S(1)}, f32[512,512]{1,0:T(8,128)S(1)}) custom-call(bf16[512,512]{1,0:T(8,128)(2,1)S(1)} %get-tuple-element.27.own_ref, bf16[512,512]{1,0:T(8,128)(2,1)S(1)} %collective-permute-done.12.other_ref, bf16[256,1024]{1,0:T(8,128)(2,1)S(1)} %pad_maximum_fusion.refs_0_, bf16[256,1024]{1,0:T(8,128)(2,1)} %collective-permute-done.9.refs_1_, ...), custom_call_target="tpu_custom_call" | custom-call | tf_op jit(solution)/shard_map/direct/pallas_call | solution.py:170
  74.6 1.3 %collective-permute-start.15 = (f32[512,512]{1,0:T(8,128)S(1)}, f32[512,512]{1,0:T(8,128)S(1)}, u32[]{:S(2)}, u32[]{:S(2)}) collective-permute-start(f32[512,512]{1,0:T(8,128)S(1)} %get-tuple-element.32), channel_id=1, source_target_pairs={{0,2},{2,0},{1,3},{3,1},{4,6},{6,4},{5,7},{7,5},{8,10},{10,8},{9,1... | collective-permute-start | bytes 3145736 | tf_op jit(solution)/shard_map/ppermute | solution.py:29
  75.8 2.3 %collective-permute-done.15.got_ref = f32[512,512]{1,0:T(8,128)S(1)} collective-permute-done((f32[512,512]{1,0:T(8,128)S(1)}, f32[512,512]{1,0:T(8,128)S(1)}, u32[]{:S(2)}, u32[]{:S(2)}) %collective-permute-start.15) | collective-permute-done | bytes 1048608 | tf_op jit(solution)/shard_map/ppermute | solution.py:29
  78.1 1.3 %finish.1 = bf16[1024,512]{1,0:T(8,128)(2,1)S(1)} custom-call(bf16[1024,512]{1,0:T(8,128)(2,1)S(1)} %get-tuple-element.26.psi_ref, f32[512,512]{1,0:T(8,128)S(1)} %get-tuple-element.31.keep_ref, f32[512,512]{1,0:T(8,128)S(1)} %collective-permute-done.15.got_ref), custom_call_target="tpu_custom_call" | custom-call | tf_op jit(solution)/shard_map/finish/pallas_call | solution.py:198
  79.4 22.8 %all_to_all.10 = bf16[128,8,512]{2,1,0:T(8,128)(2,1)S(1)} all-to-all(bf16[128,8,512]{2,1,0:T(8,128)(2,1)S(1)} %bitcast.20), channel_id=1, replica_groups=mesh['zh'=2,'y'=4,'x'=4,'core'=2,'zl'=2] {'y','x','zh','zl','core'}, dimensions={0} | all-to-all | bytes 2097152 | tf_op jit(solution)/shard_map/all_to_all | solution.py:25
  (37 shorter events, 12.0 us)
Async XLA Ops:
  0.0 18.6 %copy-start.4 = (bf16[1024,1,64]{0,2,1:T(8,128)(2,1)S(1)}, bf16[1024,1,64]{0,2,1:T(8,128)(2,1)}, u32[]{:S(2)}) copy-start(bf16[1024,1,64]{0,2,1:T(8,128)(2,1)} %param.6) | copy-start | bytes 393220
  0.7 2.3 %collective-permute-start = (bf16[8,512]{1,0:T(8,128)(2,1)S(1)}, bf16[8,512]{1,0:T(8,128)(2,1)S(1)}, u32[]{:S(2)}, u32[]{:S(2)}) collective-permute-start(bf16[8,512]{1,0:T(8,128)(2,1)S(1)} %dynamic-slice_bitcast_fusion), channel_id=1, source_target_pairs={{0,2},{2,0},{1,3},{3,1},{4,6},{6,4},{5,7},{7,5},{8,10},{10,8},{9,1... | collective-permute-start | bytes 24584 | tf_op jit(solution)/shard_map/ppermute | solution.py:29
  3.7 14.9 %collective-permute-start.2 = (bf16[16,512]{1,0:T(8,128)(2,1)S(1)}, bf16[16,512]{1,0:T(8,128)(2,1)S(1)}, u32[]{:S(2)}, u32[]{:S(2)}) collective-permute-start(bf16[16,512]{1,0:T(8,128)(2,1)S(1)} %pad_maximum_fusion.2), channel_id=1, source_target_pairs={{0,64},{1,65},{64,0},{65,1},{2,66},{3,67},{66,2},{67,3},{4,68},{5,... | collective-permute-start | bytes 49160 | tf_op jit(solution)/shard_map/ppermute | solution.py:210
  7.4 11.8 %collective-permute-start.3 = (bf16[16,512]{1,0:T(8,128)(2,1)S(1)}, bf16[16,512]{1,0:T(8,128)(2,1)S(1)}, u32[]{:S(2)}, u32[]{:S(2)}) collective-permute-start(bf16[16,512]{1,0:T(8,128)(2,1)S(1)} %pad_maximum_fusion.2), channel_id=1, source_target_pairs={{0,65},{1,0},{64,1},{65,64},{2,67},{3,2},{66,3},{67,66},{4,69},{5,... | collective-permute-start | bytes 49160 | tf_op jit(solution)/shard_map/ppermute | solution.py:210
  7.8 11.4 %collective-permute-start.1 = (bf16[16,512]{1,0:T(8,128)(2,1)S(1)}, bf16[16,512]{1,0:T(8,128)(2,1)S(1)}, u32[]{:S(2)}, u32[]{:S(2)}) collective-permute-start(bf16[16,512]{1,0:T(8,128)(2,1)S(1)} %pad_maximum_fusion.2), channel_id=1, source_target_pairs={{0,1},{1,64},{64,65},{65,0},{2,3},{3,66},{66,67},{67,2},{4,5},{5,6... | collective-permute-start | bytes 49160 | tf_op jit(solution)/shard_map/ppermute | solution.py:210
  8.8 10.4 %collective-permute-start.6 = (bf16[64,1024]{1,0:T(8,128)(2,1)}, bf16[64,1024]{1,0:T(8,128)(2,1)S(1)}, u32[]{:S(2)}, u32[]{:S(2)}) collective-permute-start(bf16[64,1024]{1,0:T(8,128)(2,1)} %bitcast.25), channel_id=1, source_target_pairs={{0,8},{4,12},{8,0},{12,4},{1,9},{5,13},{9,1},{13,5},{2,10},{6,14},... | collective-permute-start | bytes 393224 | tf_op jit(solution)/shard_map/ppermute | solution.py:21
  11.6 7.7 %collective-permute-start.5 = (bf16[64,1024]{1,0:T(8,128)(2,1)}, bf16[64,1024]{1,0:T(8,128)(2,1)S(1)}, u32[]{:S(2)}, u32[]{:S(2)}) collective-permute-start(bf16[64,1024]{1,0:T(8,128)(2,1)} %bitcast.26), channel_id=1, source_target_pairs={{0,12},{4,0},{8,4},{12,8},{1,13},{5,1},{9,5},{13,9},{2,14},{6,2},{... | collective-permute-start | bytes 393224 | tf_op jit(solution)/shard_map/ppermute | solution.py:21
  13.5 1.6 %copy-start = (f32[128,4096]{1,0:T(8,128)S(1)}, f32[128,4096]{1,0:T(8,128)}, u32[]{:S(2)}) copy-start(f32[128,4096]{1,0:T(8,128)} %in_ref.1) | copy-start | bytes 6291460
  17.0 0.8 copy-start.1
  17.8 0.8 copy-start.3
  18.6 5.0 %collective-permute-start.4 = (bf16[64,1024]{1,0:T(8,128)(2,1)S(1)}, bf16[64,1024]{1,0:T(8,128)(2,1)S(1)}, u32[]{:S(2)}, u32[]{:S(2)}) collective-permute-start(bf16[64,1024]{1,0:T(8,128)(2,1)S(1)} %bitcast.27), channel_id=1, source_target_pairs={{0,4},{4,8},{8,12},{12,0},{1,5},{5,9},{9,13},{13,1},{2,6},{6,10},{... | collective-permute-start | bytes 393224 | tf_op jit(solution)/shard_map/ppermute | solution.py:21
  24.8 19.1 %collective-permute-start.8 = (bf16[3,128,1024]{2,1,0:T(8,128)(2,1)}, bf16[3,128,1024]{2,1,0:T(8,128)(2,1)S(1)}, u32[]{:S(2)}, u32[]{:S(2)}) collective-permute-start(bf16[3,128,1024]{2,1,0:T(8,128)(2,1)} %get-tuple-element.23), channel_id=1, source_target_pairs={{0,64},{64,0},{1,65},{65,1},{2,66},{66,2},{3,67},{67,3},{4,68},{68... | collective-permute-start | bytes 2359304 | tf_op jit(solution)/shard_map/ppermute | solution.py:238
  25.8 16.7 %collective-permute-start.10 = (bf16[256,1024]{1,0:T(8,128)(2,1)S(1)}, bf16[256,1024]{1,0:T(8,128)(2,1)}, u32[]{:S(2)}, u32[]{:S(2)}) collective-permute-start(bf16[256,1024]{1,0:T(8,128)(2,1)S(1)} %pad_maximum_fusion.refs_0_), channel_id=1, source_target_pairs={{0,48},{16,0},{32,16},{48,32},{1,49},{17,1},{33,17},{49,33},{2,50}... | collective-permute-start | bytes 1572872 | tf_op jit(solution)/shard_map/ppermute | solution.py:21
  28.6 15.3 %collective-permute-start.9 = (bf16[256,1024]{1,0:T(8,128)(2,1)S(1)}, bf16[256,1024]{1,0:T(8,128)(2,1)}, u32[]{:S(2)}, u32[]{:S(2)}) collective-permute-start(bf16[256,1024]{1,0:T(8,128)(2,1)S(1)} %pad_maximum_fusion.refs_0_), channel_id=1, source_target_pairs={{0,16},{16,32},{32,48},{48,0},{1,17},{17,33},{33,49},{49,1},{2,18}... | collective-permute-start | bytes 1572872 | tf_op jit(solution)/shard_map/ppermute | solution.py:21
  28.6 27.0 %all-to-all-start = ((bf16[16,64,512]{2,1,0:T(8,128)(2,1)}), bf16[16,64,512]{2,1,0:T(8,128)(2,1)S(1)}, u32[]{:S(2)}, u32[]{:S(2)}) async-start(bf16[16,64,512]{2,1,0:T(8,128)(2,1)} %broadcast_in_dim.2), calls=%async_computation | async-start | bytes 2097152 | tf_op jit(solution)/shard_map/all_to_all | solution.py:25
  32.6 22.9 %collective-permute-start.7 = (bf16[2,128,1024]{2,1,0:T(8,128)(2,1)}, bf16[2,128,1024]{2,1,0:T(8,128)(2,1)S(1)}, u32[]{:S(2)}, u32[]{:S(2)}) collective-permute-start(bf16[2,128,1024]{2,1,0:T(8,128)(2,1)} %copy-done.3), channel_id=1, source_target_pairs={{0,2},{2,0},{1,3},{3,1},{4,6},{6,4},{5,7},{7,5},{8,10},{10,8},{9,1... | collective-permute-start | bytes 1572872 | tf_op jit(solution)/shard_map/ppermute | solution.py:29
  44.7 12.7 %collective-permute-start.11 = (bf16[2,128,1024]{2,1,0:T(8,128)(2,1)}, bf16[2,128,1024]{2,1,0:T(8,128)(2,1)}, u32[]{:S(2)}, u32[]{:S(2)}) collective-permute-start(bf16[2,128,1024]{2,1,0:T(8,128)(2,1)} %slice.9), channel_id=1, source_target_pairs={{0,2},{2,0},{1,3},{3,1},{4,6},{6,4},{5,7},{7,5},{8,10},{10,8},{9,1... | collective-permute-start | bytes 1572872 | tf_op jit(solution)/shard_map/ppermute | solution.py:29
  57.4 13.2 %copy-start.2 = (f32[128,1024]{1,0:T(8,128)S(1)}, f32[128,1024]{1,0:T(8,128)}, u32[]{:S(2)}) copy-start(f32[128,1024]{1,0:T(8,128)} %copy-done.1) | copy-start | bytes 1572868
  59.4 11.3 %collective-permute-start.12 = (bf16[512,512]{1,0:T(8,128)(2,1)S(1)}, bf16[512,512]{1,0:T(8,128)(2,1)S(1)}, u32[]{:S(2)}, u32[]{:S(2)}) collective-permute-start(bf16[512,512]{1,0:T(8,128)(2,1)S(1)} %get-tuple-element.27.own_ref), channel_id=1, source_target_pairs={{0,2},{2,0},{1,3},{3,1},{4,6},{6,4},{5,7},{7,5},{8,10},{10,8},{9,1... | collective-permute-start | bytes 1572872 | tf_op jit(solution)/shard_map/ppermute | solution.py:29
  61.8 7.8 %collective-permute-start.14 = (bf16[128,1024]{1,0:T(8,128)(2,1)S(1)}, bf16[128,1024]{1,0:T(8,128)(2,1)S(1)}, u32[]{:S(2)}, u32[]{:S(2)}) collective-permute-start(bf16[128,1024]{1,0:T(8,128)(2,1)S(1)} %slice.11), channel_id=1, source_target_pairs={{0,48},{16,0},{32,16},{48,32},{1,49},{17,1},{33,17},{49,33},{2,50}... | collective-permute-start | bytes 786440 | tf_op jit(solution)/shard_map/ppermute | solution.py:21
  61.8 8.8 %collective-permute-start.13 = (bf16[128,1024]{1,0:T(8,128)(2,1)S(1)}, bf16[128,1024]{1,0:T(8,128)(2,1)S(1)}, u32[]{:S(2)}, u32[]{:S(2)}) collective-permute-start(bf16[128,1024]{1,0:T(8,128)(2,1)S(1)} %slice.10), channel_id=1, source_target_pairs={{0,16},{16,32},{32,48},{48,0},{1,17},{17,33},{33,49},{49,1},{2,18}... | collective-permute-start | bytes 786440 | tf_op jit(solution)/shard_map/ppermute | solution.py:21
  74.6 3.5 %collective-permute-start.15 = (f32[512,512]{1,0:T(8,128)S(1)}, f32[512,512]{1,0:T(8,128)S(1)}, u32[]{:S(2)}, u32[]{:S(2)}) collective-permute-start(f32[512,512]{1,0:T(8,128)S(1)} %get-tuple-element.32), channel_id=1, source_target_pairs={{0,2},{2,0},{1,3},{3,1},{4,6},{6,4},{5,7},{7,5},{8,10},{10,8},{9,1... | collective-permute-start | bytes 3145736 | tf_op jit(solution)/shard_map/ppermute | solution.py:29

commit v9 on v7

--- a/solution.py
+++ b/solution.py
@@ -135,17 +135,18 @@
 def direct(proj_own, proj_other, lines, own, boxes):
     rows, half = proj_own.shape
     points = rows // 4
-    block = lines[0].shape[0] // 2
+    block = lines[0].shape[0] // 4
     count, states = 16 * block, lines[0].shape[1]
     chunk = 512
 
     def kernel(own_ref, other_ref, *refs):
-        line_refs, scr_refs, (keep_ref, send_ref, proj, panel_ref) = refs[:8], refs[8:12], refs[12:]
+        line_refs, scr_refs, (keep_ref, send_ref, proj, panel_ref) = refs[:5], refs[5:9], refs[9:]
         y, x = lax.axis_index("y"), lax.axis_index("x")
         for k in range(16):
             at = lax.rem(y + STEPS[k // 4] + 4, 4) * 4 + lax.rem(x + STEPS[k % 4] + 4, 4)
-            panel_ref[pl.ds(pl.multiple_of(at * block, block), block), :] = line_refs[k // 2][
-                k % 2 * block : (k % 2 + 1) * block, :
+            ref, row = (line_refs[k // 4], k % 4) if k < 12 else (line_refs[k // 2 - 3], k % 2)
+            panel_ref[pl.ds(pl.multiple_of(at * block, block), block), :] = ref[
+                row * block : (row + 1) * block, :
             ]
         core = lax.axis_index("core")
         mine = pl.ds(pl.multiple_of(core * half, half), half)
@@ -181,7 +182,7 @@
     return pl.pallas_call(
         kernel,
         out_shape=[jax.ShapeDtypeStruct((rows, half), F32)] * 2,
-        in_specs=[vmem_spec()] * 14,
+        in_specs=[vmem_spec()] * 11,
         out_specs=[vmem_spec()] * 2,
         scratch_shapes=[pltpu.VMEM((rows, half), BF16), pltpu.VMEM((count, states), BF16)],
         compiler_params=params(24),
@@ -234,31 +235,26 @@
     left = psi_v.reshape(2, 4, 4, 2, 2, rows, -1).transpose(0, 3, 4, 1, 2, 5, 6).reshape(psi_v.shape)
     own, near, far = pack(screened, left)
     block = psi_c[:, 0, :].T
-    line = [
-        jnp.concatenate([block, shift(block, "x", 1)], 0),
-        jnp.concatenate([shift(block, "x", -1), shift(block, "x", 2)], 0),
-    ]
+    line = jnp.concatenate([block, shift(block, "x", 1), shift(block, "x", -1), shift(block, "x", 2)], 0)
     copies, near, far = lax.optimization_barrier((to_all(trial[0]), near, far))
     level = exchange(copies, PLANE).reshape(-1, states)
     near = swap(near)
     far = lax.ppermute(far, "zh", [(0, 1), (1, 0)])
-    behind = [shift(part, "y", 1) for part in line]
-    ahead = [shift(part, "y", -1) for part in line]
+    behind, ahead = shift(line, "y", 1), shift(line, "y", -1)
     mine = lax.dynamic_slice_in_dim(level, core * half, half, 1)
     sent = lax.dynamic_slice_in_dim(level, (1 - core) * half, half, 1)
     pieces = jnp.concatenate([mine, swap(sent)], 0)
-    pieces, near, far, behind[0], ahead[1] = lax.optimization_barrier(
-        (pieces, near, far, behind[0], ahead[1])
-    )
+    pieces, near = lax.optimization_barrier((pieces, near))
+    rounds = [pieces, ring(pieces, 1), ring(pieces, -1), ring(pieces, 2)]
+    far, _ = lax.optimization_barrier((far, pieces))
     passed = swap(far[1:])
-    rounds = [pieces, ring(pieces, 1), ring(pieces, -1), ring(pieces, 2)]
-    beyond = [shift(behind[0], "y", 1), shift(ahead[1], "y", -1)]
+    middle = line.shape[0] // 2
+    behind, ahead, passed = lax.optimization_barrier((behind, ahead, passed))
+    beyond = [shift(behind[:middle], "y", 1), shift(ahead[middle:], "y", -1)]
+    rounds, beyond = lax.optimization_barrier((rounds, beyond))
     proj_own, psi = project(rounds, left, near, far, passed)
-    proj_own, behind[1], ahead[0], beyond = lax.optimization_barrier(
-        (proj_own, behind[1], ahead[0], beyond)
-    )
     proj_other = swap(proj_own)
-    panel = [*line, *behind, *ahead, *beyond]
+    panel = [line, behind, ahead, *beyond]
     keep, send = direct(proj_own, proj_other, panel, own, [near, far, passed])
     got = swap(send)
     term = finish(psi, keep, got)

time: 93.1 us -> 90.4 us (0.971)
  blocking collectives: 26.3 us -> 24 us
  waiting for transfers between devices: 21.7 us -> 20.1 us
  Pallas kernels: 6.73 us -> 5.56 us
  other arithmetic: 0.81 us -> 1.86 us
  local copies, waits for them, and re-layouts: 3.38 us -> 4.41 us
    ppermute x3, waiting for transfers between devices: 8.52 us -> 2.43 us  [ring(): lax.ppermute(value, ('zh', 'zl'), [(k, (k + by) % 4) for k in range(4)])]
    ppermute x9 -> x7, waiting for transfers between devices: 6 us -> 12 us  [shift(): return lax.ppermute(value, axis, [(k, (k + by) % n) for k in range(n)])]
    ppermute x9 -> x7, starting transfers between devices: 12.1 us -> 8.47 us  [shift(): return lax.ppermute(value, axis, [(k, (k + by) % n) for k in range(n)])]
    all_to_all x1, blocking collectives: 26.3 us -> 24 us  [exchange(): return lax.all_to_all(value, axes, split_axis=0, concat_axis=0, tiled=True)]
    all_to_all x1, starting transfers between devices: 5.45 us -> 6.81 us  [exchange(): return lax.all_to_all(value, axes, split_axis=0, concat_axis=0, tiled=True)]
    ppermute x5, starting transfers between devices: 9.31 us -> 10.5 us  [swap(): return lax.ppermute(value, 'core', [(0, 1), (1, 0)])]
    pallas_call x1, Pallas kernels: 2.05 us -> 0.89 us  [pack(): pl.pallas_call(kernel, grid=(steps,), out_shape=[jax.ShapeDtypeStruct((po...]
    concatenate x1, other arithmetic: 0.02 us -> 1.07 us  [shards(): jnp.concatenate([block, shift(block, 'x', 1), shift(block, 'x', -1), shif...]
  transfers between devices with their start and end apart: 19 -> 17, of which waited for: 10 -> 9; matrix products, arithmetic and copies ran while one was open for 2% -> 2% of each run, Pallas kernels for 3% -> 0%
where the time goes in v9:
time: 90.4 us; the launch traced here: 90.1 us
  starting transfers between devices  34.1 us (38%)
  blocking collectives  24 us (27%)
  waiting for transfers between devices  20.1 us (22%)
  Pallas kernels  5.56 us (6%)
  local copies, waits for them, and re-layouts  4.41 us (5%)
  other arithmetic  1.86 us (2%)
    all_to_all x1, blocking collectives, exchange(): return lax.all_to_all(value, axes, split_axis=0, concat_axis=0, tiled=True)  24 us
    ppermute x7, waiting for transfers between devices, shift(): return lax.ppermute(value, axis, [(k, (k + by) % n) for k in range(n)])  12 us
    ppermute x5, starting transfers between devices, swap(): return lax.ppermute(value, 'core', [(0, 1), (1, 0)])  10.5 us
    ppermute x7, starting transfers between devices, shift(): return lax.ppermute(value, axis, [(k, (k + by) % n) for k in range(n)])  8.47 us
    all_to_all x1, starting transfers between devices, exchange(): return lax.all_to_all(value, axes, split_axis=0, concat_axis=0, tiled=True)  6.81 us
    ppermute x1, starting transfers between devices, shards(): far = lax.ppermute(far, 'zh', [(0, 1), (1, 0)])  4.43 us
    ppermute x3, starting transfers between devices, ring(): lax.ppermute(value, ('zh', 'zl'), [(k, (k + by) % 4) for k in range(4)])  3.88 us
    ppermute x5, waiting for transfers between devices, swap(): return lax.ppermute(value, 'core', [(0, 1), (1, 0)])  3.83 us
  transfers between devices with their start and end apart: 17, of which 9 were waited for; matrix products, arithmetic and copies ran while one was open for 2% of the time, Pallas kernels for 0%

profile of v9, /device:TPU:1, one launch (start us, length us, event | category | flops | bytes accessed | tf_op | source)
XLA Modules:
  0.0 90.1 jit_solution(15679917048910608011)
XLA Ops:
  0.0 1.0 %copy.5 = bf16[2,4,4,2,2,8,128]{6,5,2,1,4,3,0:T(8,128)(2,1)S(1)} copy(bf16[2,4,4,2,2,8,128]{6,5,4,3,2,1,0:T(8,128)(2,1)} %bitcast.19) | data formatting | bytes 524288 | tf_op jit(solution)/shard_map/reshape | solution.py:235
  1.1 1.6 %copy-done = f32[128,4096]{1,0:T(8,128)S(1)} copy-done((f32[128,4096]{1,0:T(8,128)S(1)}, f32[128,4096]{1,0:T(8,128)}, u32[]{:S(2)}) %copy-start) | copy-done | bytes 2097176
  4.3 4.4 %collective-permute-start.10 = (bf16[3,128,1024]{2,1,0:T(8,128)(2,1)S(1)}, bf16[3,128,1024]{2,1,0:T(8,128)(2,1)S(1)}, u32[]{:S(2)}, u32[]{:S(2)}) collective-permute-start(bf16[3,128,1024]{2,1,0:T(8,128)(2,1)S(1)} %get-tuple-element.32), channel_id=1, source_target_pairs={{0,64},{64,0},{1,65},{65,1},{2,66},{66,2},{3,67},{67,3},{4,68},{68... | collective-permute-start | bytes 2359304 | tf_op jit(solution)/shard_map/ppermute | solution.py:242
  8.7 6.8 %all-to-all-start = ((bf16[16,8,1024]{2,1,0:T(8,128)(2,1)}), bf16[16,8,1024]{2,1,0:T(8,128)(2,1)}, u32[]{:S(2)}, u32[]{:S(2)}) async-start(bf16[16,8,1024]{2,1,0:T(8,128)(2,1)} %broadcast_in_dim.8), calls=%async_computation | async-start | bytes 524288 | tf_op jit(solution)/shard_map/all_to_all | solution.py:25
  15.5 1.3 %collective-permute-start.1 = (bf16[2,128,1024]{2,1,0:T(8,128)(2,1)S(1)}, bf16[2,128,1024]{2,1,0:T(8,128)(2,1)S(1)}, u32[]{:S(2)}, u32[]{:S(2)}) collective-permute-start(bf16[2,128,1024]{2,1,0:T(8,128)(2,1)S(1)} %get-tuple-element.30), channel_id=1, source_target_pairs={{0,2},{2,0},{1,3},{3,1},{4,6},{6,4},{5,7},{7,5},{8,10},{10,8},{9,1... | collective-permute-start | bytes 1572872 | tf_op jit(solution)/shard_map/ppermute | solution.py:29
  16.8 3.0 %collective-permute-start.7 = (bf16[64,1024]{1,0:T(8,128)(2,1)S(1)}, bf16[64,1024]{1,0:T(8,128)(2,1)}, u32[]{:S(2)}, u32[]{:S(2)}) collective-permute-start(bf16[64,1024]{1,0:T(8,128)(2,1)S(1)} %bitcast.20), channel_id=1, source_target_pairs={{0,8},{4,12},{8,0},{12,4},{1,9},{5,13},{9,1},{13,5},{2,10},{6,14},... | collective-permute-start | bytes 393224 | tf_op jit(solution)/shard_map/ppermute | solution.py:21
  21.3 1.9 %all-to-all-done = bf16[16,8,1024]{2,1,0:T(8,128)(2,1)} async-done(((bf16[16,8,1024]{2,1,0:T(8,128)(2,1)}), bf16[16,8,1024]{2,1,0:T(8,128)(2,1)}, u32[]{:S(2)}, u32[]{:S(2)}) %all-to-all-start) | async-done | bytes 262176 | tf_op jit(solution)/shard_map/all_to_all | solution.py:25
  24.2 3.7 %collective-permute-start = (bf16[128,512]{1,0:T(8,128)(2,1)S(1)}, bf16[128,512]{1,0:T(8,128)(2,1)S(1)}, u32[]{:S(2)}, u32[]{:S(2)}) collective-permute-start(bf16[128,512]{1,0:T(8,128)(2,1)S(1)} %get-tuple-element.50), channel_id=1, source_target_pairs={{0,2},{2,0},{1,3},{3,1},{4,6},{6,4},{5,7},{7,5},{8,10},{10,8},{9,1... | collective-permute-start | bytes 393224 | tf_op jit(solution)/shard_map/ppermute | solution.py:29
  28.3 1.1 %pad_maximum_fusion.refs_0_ = bf16[256,1024]{1,0:T(8,128)(2,1)S(1)} fusion(bf16[64,1024]{1,0:T(8,128)(2,1)} %collective-permute-done.7, bf16[64,1024]{1,0:T(8,128)(2,1)} %collective-permute-done.6, bf16[64,1024]{1,0:T(8,128)(2,1)} %collective-permute-done.5, bf16[64,1024]{1,0:T(8,128)(2,1)S(1)} %bitcast.23), kind=kLoop, calls=%fused_computation.1 | loop fusion | flops 2097152 | bytes 1048576 | tf_op jit(solution)/shard_map/concatenate | solution.py:238
  29.3 2.4 %collective-permute-start.9 = (bf16[256,1024]{1,0:T(8,128)(2,1)S(1)}, bf16[256,1024]{1,0:T(8,128)(2,1)S(1)}, u32[]{:S(2)}, u32[]{:S(2)}) collective-permute-start(bf16[256,1024]{1,0:T(8,128)(2,1)S(1)} %pad_maximum_fusion.refs_0_), channel_id=1, source_target_pairs={{0,48},{16,0},{32,16},{48,32},{1,49},{17,1},{33,17},{49,33},{2,50}... | collective-permute-start | bytes 1572872 | tf_op jit(solution)/shard_map/ppermute | solution.py:21
  31.9 1.3 %collective-permute-start.11 = (bf16[2,128,1024]{2,1,0:T(8,128)(2,1)S(1)}, bf16[2,128,1024]{2,1,0:T(8,128)(2,1)S(1)}, u32[]{:S(2)}, u32[]{:S(2)}) collective-permute-start(bf16[2,128,1024]{2,1,0:T(8,128)(2,1)S(1)} %slice.9), channel_id=1, source_target_pairs={{0,2},{2,0},{1,3},{3,1},{4,6},{6,4},{5,7},{7,5},{8,10},{10,8},{9,1... | collective-permute-start | bytes 1572872 | tf_op jit(solution)/shard_map/ppermute | solution.py:29
  33.2 3.1 %collective-permute-start.3 = (bf16[256,512]{1,0:T(8,128)(2,1)S(1)}, bf16[256,512]{1,0:T(8,128)(2,1)S(1)}, u32[]{:S(2)}, u32[]{:S(2)}) collective-permute-start(bf16[256,512]{1,0:T(8,128)(2,1)S(1)} %pad_maximum_fusion.1.refs_0_), channel_id=1, source_target_pairs={{0,65},{1,0},{64,1},{65,64},{2,67},{3,2},{66,3},{67,66},{4,69},{5,... | collective-permute-start | bytes 786440 | tf_op jit(solution)/shard_map/ppermute | solution.py:222
  36.3 5.7 %collective-permute-done.9.refs_2_ = bf16[256,1024]{1,0:T(8,128)(2,1)S(1)} collective-permute-done((bf16[256,1024]{1,0:T(8,128)(2,1)S(1)}, bf16[256,1024]{1,0:T(8,128)(2,1)S(1)}, u32[]{:S(2)}, u32[]{:S(2)}) %collective-permute-start.9) | collective-permute-done | bytes 524320 | tf_op jit(solution)/shard_map/ppermute | solution.py:21
  42.8 2.4 %collective-permute-done.8.refs_1_ = bf16[256,1024]{1,0:T(8,128)(2,1)S(1)} collective-permute-done((bf16[256,1024]{1,0:T(8,128)(2,1)S(1)}, bf16[256,1024]{1,0:T(8,128)(2,1)S(1)}, u32[]{:S(2)}, u32[]{:S(2)}) %collective-permute-start.8) | collective-permute-done | bytes 524320 | tf_op jit(solution)/shard_map/ppermute | solution.py:21
  45.2 1.1 %collective-permute-start.13 = (bf16[128,1024]{1,0:T(8,128)(2,1)S(1)}, bf16[128,1024]{1,0:T(8,128)(2,1)S(1)}, u32[]{:S(2)}, u32[]{:S(2)}) collective-permute-start(bf16[128,1024]{1,0:T(8,128)(2,1)S(1)} %slice.11), channel_id=1, source_target_pairs={{0,48},{16,0},{32,16},{48,32},{1,49},{17,1},{33,17},{49,33},{2,50}... | collective-permute-start | bytes 786440 | tf_op jit(solution)/shard_map/ppermute | solution.py:21
  46.8 2.4 %collective-permute-done.2.refs_1_ = bf16[256,512]{1,0:T(8,128)(2,1)S(1)} collective-permute-done((bf16[256,512]{1,0:T(8,128)(2,1)S(1)}, bf16[256,512]{1,0:T(8,128)(2,1)S(1)}, u32[]{:S(2)}, u32[]{:S(2)}) %collective-permute-start.2) | collective-permute-done | bytes 262176 | tf_op jit(solution)/shard_map/ppermute | solution.py:222
  49.2 1.7 %collective-permute-done.13.refs_4_ = bf16[128,1024]{1,0:T(8,128)(2,1)S(1)} collective-permute-done((bf16[128,1024]{1,0:T(8,128)(2,1)S(1)}, bf16[128,1024]{1,0:T(8,128)(2,1)S(1)}, u32[]{:S(2)}, u32[]{:S(2)}) %collective-permute-start.13) | collective-permute-done | bytes 262176 | tf_op jit(solution)/shard_map/ppermute | solution.py:21
  50.9 1.8 %collective-permute-done.12.refs_3_ = bf16[128,1024]{1,0:T(8,128)(2,1)S(1)} collective-permute-done((bf16[128,1024]{1,0:T(8,128)(2,1)S(1)}, bf16[128,1024]{1,0:T(8,128)(2,1)S(1)}, u32[]{:S(2)}, u32[]{:S(2)}) %collective-permute-start.12) | collective-permute-done | bytes 262176 | tf_op jit(solution)/shard_map/ppermute | solution.py:21
  53.6 3.7 %collective-permute-start.14 = (bf16[512,512]{1,0:T(8,128)(2,1)S(1)}, bf16[512,512]{1,0:T(8,128)(2,1)S(1)}, u32[]{:S(2)}, u32[]{:S(2)}) collective-permute-start(bf16[512,512]{1,0:T(8,128)(2,1)S(1)} %get-tuple-element.43.own_ref), channel_id=1, source_target_pairs={{0,2},{2,0},{1,3},{3,1},{4,6},{6,4},{5,7},{7,5},{8,10},{10,8},{9,1... | collective-permute-start | bytes 1572872 | tf_op jit(solution)/shard_map/ppermute | solution.py:29
  57.3 1.5 %collective-permute-done.14.other_ref = bf16[512,512]{1,0:T(8,128)(2,1)S(1)} collective-permute-done((bf16[512,512]{1,0:T(8,128)(2,1)S(1)}, bf16[512,512]{1,0:T(8,128)(2,1)S(1)}, u32[]{:S(2)}, u32[]{:S(2)}) %collective-permute-start.14) | collective-permute-done | bytes 524320 | tf_op jit(solution)/shard_map/ppermute | solution.py:29
  58.8 2.5 %direct.1 = (f32[512,512]{1,0:T(8,128)S(1)}, f32[512,512]{1,0:T(8,128)S(1)}) custom-call(bf16[512,512]{1,0:T(8,128)(2,1)S(1)} %get-tuple-element.43.own_ref, bf16[512,512]{1,0:T(8,128)(2,1)S(1)} %collective-permute-done.14.other_ref, bf16[256,1024]{1,0:T(8,128)(2,1)S(1)} %pad_maximum_fusion.refs_0_, bf16[256,1024]{1,0:T(8,128)(2,1)S(1)} %collective-permute-done.8.refs_1_, ...), custom_call_target="tpu_custom_call" | custom-call | tf_op jit(solution)/shard_map/direct/pallas_call | solution.py:182
  61.8 2.3 %collective-permute-done.15.got_ref = f32[512,512]{1,0:T(8,128)S(1)} collective-permute-done((f32[512,512]{1,0:T(8,128)S(1)}, f32[512,512]{1,0:T(8,128)S(1)}, u32[]{:S(2)}, u32[]{:S(2)}) %collective-permute-start.15) | collective-permute-done | bytes 1048608 | tf_op jit(solution)/shard_map/ppermute | solution.py:29
  64.1 1.3 %finish.1 = bf16[1024,512]{1,0:T(8,128)(2,1)S(1)} custom-call(bf16[1024,512]{1,0:T(8,128)(2,1)S(1)} %get-tuple-element.42.psi_ref, f32[512,512]{1,0:T(8,128)S(1)} %get-tuple-element.47.keep_ref, f32[512,512]{1,0:T(8,128)S(1)} %collective-permute-done.15.got_ref), custom_call_target="tpu_custom_call" | custom-call | tf_op jit(solution)/shard_map/finish/pallas_call | solution.py:210
  65.4 24.0 %all_to_all.10 = bf16[128,8,512]{2,1,0:T(8,128)(2,1)S(1)} all-to-all(bf16[128,8,512]{2,1,0:T(8,128)(2,1)S(1)} %bitcast.15), channel_id=1, replica_groups=mesh['zh'=2,'y'=4,'x'=4,'core'=2,'zl'=2] {'zh','core','zl','y','x'}, dimensions={0} | all-to-all | bytes 2097152 | tf_op jit(solution)/shard_map/all_to_all | solution.py:25
  (30 shorter events, 7.8 us)
Async XLA Ops:
  0.0 3.5 %copy-start.2 = (bf16[1,8,1024]{2,1,0:T(8,128)(2,1)S(1)}, bf16[1,8,1024]{2,1,0:T(8,128)(2,1)}, u32[]{:S(2)}) copy-start(bf16[1,8,1024]{2,1,0:T(8,128)(2,1)} %param.4) | copy-start | bytes 49156
  0.0 16.8 %copy-start.1 = (bf16[1024,1,64]{0,2,1:T(8,128)(2,1)S(1)}, bf16[1024,1,64]{0,2,1:T(8,128)(2,1)}, u32[]{:S(2)}) copy-start(bf16[1024,1,64]{0,2,1:T(8,128)(2,1)} %param.6) | copy-start | bytes 393220
  1.0 1.6 %copy-start = (f32[128,4096]{1,0:T(8,128)S(1)}, f32[128,4096]{1,0:T(8,128)}, u32[]{:S(2)}) copy-start(f32[128,4096]{1,0:T(8,128)} %in_ref.1) | copy-start | bytes 6291460
  4.3 27.5 %collective-permute-start.10 = (bf16[3,128,1024]{2,1,0:T(8,128)(2,1)S(1)}, bf16[3,128,1024]{2,1,0:T(8,128)(2,1)S(1)}, u32[]{:S(2)}, u32[]{:S(2)}) collective-permute-start(bf16[3,128,1024]{2,1,0:T(8,128)(2,1)S(1)} %get-tuple-element.32), channel_id=1, source_target_pairs={{0,64},{64,0},{1,65},{65,1},{2,66},{66,2},{3,67},{67,3},{4,68},{68... | collective-permute-start | bytes 2359304 | tf_op jit(solution)/shard_map/ppermute | solution.py:242
  8.7 14.5 %all-to-all-start = ((bf16[16,8,1024]{2,1,0:T(8,128)(2,1)}), bf16[16,8,1024]{2,1,0:T(8,128)(2,1)}, u32[]{:S(2)}, u32[]{:S(2)}) async-start(bf16[16,8,1024]{2,1,0:T(8,128)(2,1)} %broadcast_in_dim.8), calls=%async_computation | async-start | bytes 524288 | tf_op jit(solution)/shard_map/all_to_all | solution.py:25
  15.5 16.3 %collective-permute-start.1 = (bf16[2,128,1024]{2,1,0:T(8,128)(2,1)S(1)}, bf16[2,128,1024]{2,1,0:T(8,128)(2,1)S(1)}, u32[]{:S(2)}, u32[]{:S(2)}) collective-permute-start(bf16[2,128,1024]{2,1,0:T(8,128)(2,1)S(1)} %get-tuple-element.30), channel_id=1, source_target_pairs={{0,2},{2,0},{1,3},{3,1},{4,6},{6,4},{5,7},{7,5},{8,10},{10,8},{9,1... | collective-permute-start | bytes 1572872 | tf_op jit(solution)/shard_map/ppermute | solution.py:29
  16.8 7.4 %collective-permute-start.7 = (bf16[64,1024]{1,0:T(8,128)(2,1)S(1)}, bf16[64,1024]{1,0:T(8,128)(2,1)}, u32[]{:S(2)}, u32[]{:S(2)}) collective-permute-start(bf16[64,1024]{1,0:T(8,128)(2,1)S(1)} %bitcast.20), channel_id=1, source_target_pairs={{0,8},{4,12},{8,0},{12,4},{1,9},{5,13},{9,1},{13,5},{2,10},{6,14},... | collective-permute-start | bytes 393224 | tf_op jit(solution)/shard_map/ppermute | solution.py:21
  19.9 8.1 %collective-permute-start.6 = (bf16[64,1024]{1,0:T(8,128)(2,1)S(1)}, bf16[64,1024]{1,0:T(8,128)(2,1)}, u32[]{:S(2)}, u32[]{:S(2)}) collective-permute-start(bf16[64,1024]{1,0:T(8,128)(2,1)S(1)} %bitcast.21), channel_id=1, source_target_pairs={{0,12},{4,0},{8,4},{12,8},{1,13},{5,1},{9,5},{13,9},{2,14},{6,2},{... | collective-permute-start | bytes 393224 | tf_op jit(solution)/shard_map/ppermute | solution.py:21
  20.8 7.5 %collective-permute-start.5 = (bf16[64,1024]{1,0:T(8,128)(2,1)S(1)}, bf16[64,1024]{1,0:T(8,128)(2,1)}, u32[]{:S(2)}, u32[]{:S(2)}) collective-permute-start(bf16[64,1024]{1,0:T(8,128)(2,1)S(1)} %bitcast.22), channel_id=1, source_target_pairs={{0,4},{4,8},{8,12},{12,0},{1,5},{5,9},{9,13},{13,1},{2,6},{6,10},{... | collective-permute-start | bytes 393224 | tf_op jit(solution)/shard_map/ppermute | solution.py:21
  24.2 7.5 %collective-permute-start = (bf16[128,512]{1,0:T(8,128)(2,1)S(1)}, bf16[128,512]{1,0:T(8,128)(2,1)S(1)}, u32[]{:S(2)}, u32[]{:S(2)}) collective-permute-start(bf16[128,512]{1,0:T(8,128)(2,1)S(1)} %get-tuple-element.50), channel_id=1, source_target_pairs={{0,2},{2,0},{1,3},{3,1},{4,6},{6,4},{5,7},{7,5},{8,10},{10,8},{9,1... | collective-permute-start | bytes 393224 | tf_op jit(solution)/shard_map/ppermute | solution.py:29
  29.3 12.7 %collective-permute-start.9 = (bf16[256,1024]{1,0:T(8,128)(2,1)S(1)}, bf16[256,1024]{1,0:T(8,128)(2,1)S(1)}, u32[]{:S(2)}, u32[]{:S(2)}) collective-permute-start(bf16[256,1024]{1,0:T(8,128)(2,1)S(1)} %pad_maximum_fusion.refs_0_), channel_id=1, source_target_pairs={{0,48},{16,0},{32,16},{48,32},{1,49},{17,1},{33,17},{49,33},{2,50}... | collective-permute-start | bytes 1572872 | tf_op jit(solution)/shard_map/ppermute | solution.py:21
  31.8 13.4 %collective-permute-start.8 = (bf16[256,1024]{1,0:T(8,128)(2,1)S(1)}, bf16[256,1024]{1,0:T(8,128)(2,1)S(1)}, u32[]{:S(2)}, u32[]{:S(2)}) collective-permute-start(bf16[256,1024]{1,0:T(8,128)(2,1)S(1)} %pad_maximum_fusion.refs_0_), channel_id=1, source_target_pairs={{0,16},{16,32},{32,48},{48,0},{1,17},{17,33},{33,49},{49,1},{2,18}... | collective-permute-start | bytes 1572872 | tf_op jit(solution)/shard_map/ppermute | solution.py:21
  31.9 13.3 %collective-permute-start.11 = (bf16[2,128,1024]{2,1,0:T(8,128)(2,1)S(1)}, bf16[2,128,1024]{2,1,0:T(8,128)(2,1)S(1)}, u32[]{:S(2)}, u32[]{:S(2)}) collective-permute-start(bf16[2,128,1024]{2,1,0:T(8,128)(2,1)S(1)} %slice.9), channel_id=1, source_target_pairs={{0,2},{2,0},{1,3},{3,1},{4,6},{6,4},{5,7},{7,5},{8,10},{10,8},{9,1... | collective-permute-start | bytes 1572872 | tf_op jit(solution)/shard_map/ppermute | solution.py:29
  33.2 13.6 %collective-permute-start.4 = (bf16[256,512]{1,0:T(8,128)(2,1)S(1)}, bf16[256,512]{1,0:T(8,128)(2,1)S(1)}, u32[]{:S(2)}, u32[]{:S(2)}) collective-permute-start(bf16[256,512]{1,0:T(8,128)(2,1)S(1)} %pad_maximum_fusion.1.refs_0_), channel_id=1, source_target_pairs={{0,64},{1,65},{64,0},{65,1},{2,66},{3,67},{66,2},{67,3},{4,68},{5,... | collective-permute-start | bytes 786440 | tf_op jit(solution)/shard_map/ppermute | solution.py:222
  33.2 13.6 %collective-permute-start.3 = (bf16[256,512]{1,0:T(8,128)(2,1)S(1)}, bf16[256,512]{1,0:T(8,128)(2,1)S(1)}, u32[]{:S(2)}, u32[]{:S(2)}) collective-permute-start(bf16[256,512]{1,0:T(8,128)(2,1)S(1)} %pad_maximum_fusion.1.refs_0_), channel_id=1, source_target_pairs={{0,65},{1,0},{64,1},{65,64},{2,67},{3,2},{66,3},{67,66},{4,69},{5,... | collective-permute-start | bytes 786440 | tf_op jit(solution)/shard_map/ppermute | solution.py:222
  42.0 7.1 %collective-permute-start.2 = (bf16[256,512]{1,0:T(8,128)(2,1)S(1)}, bf16[256,512]{1,0:T(8,128)(2,1)S(1)}, u32[]{:S(2)}, u32[]{:S(2)}) collective-permute-start(bf16[256,512]{1,0:T(8,128)(2,1)S(1)} %pad_maximum_fusion.1.refs_0_), channel_id=1, source_target_pairs={{0,1},{1,64},{64,65},{65,0},{2,3},{3,66},{66,67},{67,2},{4,5},{5,6... | collective-permute-start | bytes 786440 | tf_op jit(solution)/shard_map/ppermute | solution.py:222
  45.2 5.7 %collective-permute-start.13 = (bf16[128,1024]{1,0:T(8,128)(2,1)S(1)}, bf16[128,1024]{1,0:T(8,128)(2,1)S(1)}, u32[]{:S(2)}, u32[]{:S(2)}) collective-permute-start(bf16[128,1024]{1,0:T(8,128)(2,1)S(1)} %slice.11), channel_id=1, source_target_pairs={{0,48},{16,0},{32,16},{48,32},{1,49},{17,1},{33,17},{49,33},{2,50}... | collective-permute-start | bytes 786440 | tf_op jit(solution)/shard_map/ppermute | solution.py:21
  46.3 6.4 %collective-permute-start.12 = (bf16[128,1024]{1,0:T(8,128)(2,1)S(1)}, bf16[128,1024]{1,0:T(8,128)(2,1)S(1)}, u32[]{:S(2)}, u32[]{:S(2)}) collective-permute-start(bf16[128,1024]{1,0:T(8,128)(2,1)S(1)} %slice.10), channel_id=1, source_target_pairs={{0,16},{16,32},{32,48},{48,0},{1,17},{17,33},{33,49},{49,1},{2,18}... | collective-permute-start | bytes 786440 | tf_op jit(solution)/shard_map/ppermute | solution.py:21
  53.6 5.2 %collective-permute-start.14 = (bf16[512,512]{1,0:T(8,128)(2,1)S(1)}, bf16[512,512]{1,0:T(8,128)(2,1)S(1)}, u32[]{:S(2)}, u32[]{:S(2)}) collective-permute-start(bf16[512,512]{1,0:T(8,128)(2,1)S(1)} %get-tuple-element.43.own_ref), channel_id=1, source_target_pairs={{0,2},{2,0},{1,3},{3,1},{4,6},{6,4},{5,7},{7,5},{8,10},{10,8},{9,1... | collective-permute-start | bytes 1572872 | tf_op jit(solution)/shard_map/ppermute | solution.py:29
  61.3 2.7 %collective-permute-start.15 = (f32[512,512]{1,0:T(8,128)S(1)}, f32[512,512]{1,0:T(8,128)S(1)}, u32[]{:S(2)}, u32[]{:S(2)}) collective-permute-start(f32[512,512]{1,0:T(8,128)S(1)} %get-tuple-element.48), channel_id=1, source_target_pairs={{0,2},{2,0},{1,3},{3,1},{4,6},{6,4},{5,7},{7,5},{8,10},{10,8},{9,1... | collective-permute-start | bytes 3145736 | tf_op jit(solution)/shard_map/ppermute | solution.py:29

commit v10 on v9

--- a/solution.py
+++ b/solution.py
@@ -236,7 +236,7 @@
     own, near, far = pack(screened, left)
     block = psi_c[:, 0, :].T
     line = jnp.concatenate([block, shift(block, "x", 1), shift(block, "x", -1), shift(block, "x", 2)], 0)
-    copies, near, far = lax.optimization_barrier((to_all(trial[0]), near, far))
+    copies, near, far, line = lax.optimization_barrier((to_all(trial[0]), near, far, line))
     level = exchange(copies, PLANE).reshape(-1, states)
     near = swap(near)
     far = lax.ppermute(far, "zh", [(0, 1), (1, 0)])

time: 90.4 us -> 92 us (1.018)
  waiting for transfers between devices: 20.1 us -> 26.7 us
  starting transfers between devices: 34.1 us -> 30.3 us
  other arithmetic: 1.86 us -> 0.83 us
  blocking collectives: 24 us -> 23 us
    all_to_all x1, waiting for transfers between devices: 1.91 us -> 6.41 us  [exchange(): return lax.all_to_all(value, axes, split_axis=0, concat_axis=0, tiled=True)]
    ppermute x5, starting transfers between devices: 10.5 us -> 7.27 us  [swap(): return lax.ppermute(value, 'core', [(0, 1), (1, 0)])]
    ppermute x3, waiting for transfers between devices: 2.43 us -> 5.11 us  [ring(): lax.ppermute(value, ('zh', 'zl'), [(k, (k + by) % 4) for k in range(4)])]
    concatenate x1, other arithmetic: 1.07 us -> 0.03 us  [shards(): jnp.concatenate([block, shift(block, 'x', 1), shift(block, 'x', -1), shif...]
    all_to_all x1, blocking collectives: 24 us -> 23 us  [exchange(): return lax.all_to_all(value, axes, split_axis=0, concat_axis=0, tiled=True)]
    unnamed x6 -> x8, local copies, waits for them, and re-layouts: 1.59 us -> 2.39 us
  transfers between devices with their start and end apart: 17 -> 17, of which waited for: 9 -> 8; matrix products, arithmetic and copies ran while one was open for 2% -> 2% of each run, Pallas kernels for 0% -> 1%
where the time goes in v10:
time: 92 us; the launch traced here: 91.8 us
  starting transfers between devices  30.3 us (33%)
  waiting for transfers between devices  26.7 us (29%)
  blocking collectives  23 us (25%)
  Pallas kernels  5.57 us (6%)
  local copies, waits for them, and re-layouts  5.17 us (6%)
    all_to_all x1, blocking collectives, exchange(): return lax.all_to_all(value, axes, split_axis=0, concat_axis=0, tiled=True)  23 us
    ppermute x7, waiting for transfers between devices, shift(): return lax.ppermute(value, axis, [(k, (k + by) % n) for k in range(n)])  11.3 us
    ppermute x7, starting transfers between devices, shift(): return lax.ppermute(value, axis, [(k, (k + by) % n) for k in range(n)])  8.05 us
    all_to_all x1, starting transfers between devices, exchange(): return lax.all_to_all(value, axes, split_axis=0, concat_axis=0, tiled=True)  7.47 us
    ppermute x5, starting transfers between devices, swap(): return lax.ppermute(value, 'core', [(0, 1), (1, 0)])  7.27 us
    all_to_all x1, waiting for transfers between devices, exchange(): return lax.all_to_all(value, axes, split_axis=0, concat_axis=0, tiled=True)  6.41 us
    ppermute x3, waiting for transfers between devices, ring(): lax.ppermute(value, ('zh', 'zl'), [(k, (k + by) % 4) for k in range(4)])  5.11 us
    ppermute x3, starting transfers between devices, ring(): lax.ppermute(value, ('zh', 'zl'), [(k, (k + by) % 4) for k in range(4)])  3.88 us
  transfers between devices with their start and end apart: 17, of which 8 were waited for; matrix products, arithmetic and copies ran while one was open for 2% of the time, Pallas kernels for 1%

profile of v10, /device:TPU:1, one launch (start us, length us, event | category | flops | bytes accessed | tf_op | source)
XLA Modules:
  0.0 91.8 jit_solution(1160362846556841652)
XLA Ops:
  0.0 3.6 %collective-permute-start.2 = (bf16[64,1024]{1,0:T(8,128)(2,1)}, bf16[64,1024]{1,0:T(8,128)(2,1)S(1)}, u32[]{:S(2)}, u32[]{:S(2)}) collective-permute-start(bf16[64,1024]{1,0:T(8,128)(2,1)} %bitcast.20), channel_id=1, source_target_pairs={{0,8},{4,12},{8,0},{12,4},{1,9},{5,13},{9,1},{13,5},{2,10},{6,14},... | collective-permute-start | bytes 393224 | tf_op jit(solution)/shard_map/ppermute | solution.py:21
  3.6 0.9 collective-permute-start.1
  5.0 1.0 %copy.5 = bf16[2,4,4,2,2,8,128]{6,5,2,1,4,3,0:T(8,128)(2,1)S(1)} copy(bf16[2,4,4,2,2,8,128]{6,5,4,3,2,1,0:T(8,128)(2,1)} %bitcast.19) | data formatting | bytes 524288 | tf_op jit(solution)/shard_map/reshape | solution.py:235
  6.1 1.6 %copy-done = f32[128,4096]{1,0:T(8,128)S(1)} copy-done((f32[128,4096]{1,0:T(8,128)S(1)}, f32[128,4096]{1,0:T(8,128)}, u32[]{:S(2)}) %copy-start) | copy-done | bytes 2097176
  7.6 0.9 pack.1
  10.6 3.7 %collective-permute-start.10 = (bf16[3,128,1024]{2,1,0:T(8,128)(2,1)S(1)}, bf16[3,128,1024]{2,1,0:T(8,128)(2,1)S(1)}, u32[]{:S(2)}, u32[]{:S(2)}) collective-permute-start(bf16[3,128,1024]{2,1,0:T(8,128)(2,1)S(1)} %get-tuple-element.34), channel_id=1, source_target_pairs={{0,64},{64,0},{1,65},{65,1},{2,66},{66,2},{3,67},{67,3},{4,68},{68... | collective-permute-start | bytes 2359304 | tf_op jit(solution)/shard_map/ppermute | solution.py:242
  14.3 7.5 %all-to-all-start = ((bf16[16,8,1024]{2,1,0:T(8,128)(2,1)}), bf16[16,8,1024]{2,1,0:T(8,128)(2,1)}, u32[]{:S(2)}, u32[]{:S(2)}) async-start(bf16[16,8,1024]{2,1,0:T(8,128)(2,1)} %broadcast_in_dim.8), calls=%async_computation | async-start | bytes 524288 | tf_op jit(solution)/shard_map/all_to_all | solution.py:25
  21.7 1.4 %collective-permute-start.4 = (bf16[2,128,1024]{2,1,0:T(8,128)(2,1)}, bf16[2,128,1024]{2,1,0:T(8,128)(2,1)S(1)}, u32[]{:S(2)}, u32[]{:S(2)}) collective-permute-start(bf16[2,128,1024]{2,1,0:T(8,128)(2,1)} %copy-done.1), channel_id=1, source_target_pairs={{0,2},{2,0},{1,3},{3,1},{4,6},{6,4},{5,7},{7,5},{8,10},{10,8},{9,1... | collective-permute-start | bytes 1572872 | tf_op jit(solution)/shard_map/ppermute | solution.py:29
  23.1 6.4 %all-to-all-done = bf16[16,8,1024]{2,1,0:T(8,128)(2,1)} async-done(((bf16[16,8,1024]{2,1,0:T(8,128)(2,1)}), bf16[16,8,1024]{2,1,0:T(8,128)(2,1)}, u32[]{:S(2)}, u32[]{:S(2)}) %all-to-all-start) | async-done | bytes 262176 | tf_op jit(solution)/shard_map/all_to_all | solution.py:25
  29.5 1.0 %constant_dynamic-slice_fusion.1 = (bf16[128,512]{1,0:T(8,128)(2,1)S(1)}, bf16[128,512]{1,0:T(8,128)(2,1)S(1)}) fusion(bf16[128,1024]{1,0:T(8,128)(2,1)} %bitcast.7, s32[]{:T(128)S(6)} %select_n.6, s32[]{:T(128)S(6)} %select_n.7), kind=kLoop, calls=%fused_computation.4 | loop fusion | bytes 524296 | tf_op jit(solution)/shard_map/dynamic_slice | solution.py:244
  30.5 2.3 %collective-permute-start.3 = (bf16[128,512]{1,0:T(8,128)(2,1)S(1)}, bf16[128,512]{1,0:T(8,128)(2,1)S(1)}, u32[]{:S(2)}, u32[]{:S(2)}) collective-permute-start(bf16[128,512]{1,0:T(8,128)(2,1)S(1)} %get-tuple-element.52), channel_id=1, source_target_pairs={{0,2},{2,0},{1,3},{3,1},{4,6},{6,4},{5,7},{7,5},{8,10},{10,8},{9,1... | collective-permute-start | bytes 393224 | tf_op jit(solution)/shard_map/ppermute | solution.py:29
  33.4 0.9 collective-permute-start.8
  35.9 2.4 %collective-permute-start.6 = (bf16[256,512]{1,0:T(8,128)(2,1)S(1)}, bf16[256,512]{1,0:T(8,128)(2,1)S(1)}, u32[]{:S(2)}, u32[]{:S(2)}) collective-permute-start(bf16[256,512]{1,0:T(8,128)(2,1)S(1)} %pad_maximum_fusion.1.refs_0_), channel_id=1, source_target_pairs={{0,65},{1,0},{64,1},{65,64},{2,67},{3,2},{66,3},{67,66},{4,69},{5,... | collective-permute-start | bytes 786440 | tf_op jit(solution)/shard_map/ppermute | solution.py:222
  38.3 8.1 %collective-permute-done.9.refs_2_ = bf16[256,1024]{1,0:T(8,128)(2,1)S(1)} collective-permute-done((bf16[256,1024]{1,0:T(8,128)(2,1)S(1)}, bf16[256,1024]{1,0:T(8,128)(2,1)S(1)}, u32[]{:S(2)}, u32[]{:S(2)}) %collective-permute-start.9) | collective-permute-done | bytes 524320 | tf_op jit(solution)/shard_map/ppermute | solution.py:21
  47.8 1.1 %collective-permute-start.13 = (bf16[128,1024]{1,0:T(8,128)(2,1)S(1)}, bf16[128,1024]{1,0:T(8,128)(2,1)S(1)}, u32[]{:S(2)}, u32[]{:S(2)}) collective-permute-start(bf16[128,1024]{1,0:T(8,128)(2,1)S(1)} %slice.11), channel_id=1, source_target_pairs={{0,48},{16,0},{32,16},{48,32},{1,49},{17,1},{33,17},{49,33},{2,50}... | collective-permute-start | bytes 786440 | tf_op jit(solution)/shard_map/ppermute | solution.py:21
  49.4 5.1 %collective-permute-done.5.refs_1_ = bf16[256,512]{1,0:T(8,128)(2,1)S(1)} collective-permute-done((bf16[256,512]{1,0:T(8,128)(2,1)S(1)}, bf16[256,512]{1,0:T(8,128)(2,1)S(1)}, u32[]{:S(2)}, u32[]{:S(2)}) %collective-permute-start.5) | collective-permute-done | bytes 262176 | tf_op jit(solution)/shard_map/ppermute | solution.py:222
  54.5 2.0 %collective-permute-done.12.refs_3_ = bf16[128,1024]{1,0:T(8,128)(2,1)S(1)} collective-permute-done((bf16[128,1024]{1,0:T(8,128)(2,1)S(1)}, bf16[128,1024]{1,0:T(8,128)(2,1)S(1)}, u32[]{:S(2)}, u32[]{:S(2)}) %collective-permute-start.12) | collective-permute-done | bytes 262176 | tf_op jit(solution)/shard_map/ppermute | solution.py:21
  56.6 0.9 project.1
  57.5 2.4 %collective-permute-start.14 = (bf16[512,512]{1,0:T(8,128)(2,1)S(1)}, bf16[512,512]{1,0:T(8,128)(2,1)S(1)}, u32[]{:S(2)}, u32[]{:S(2)}) collective-permute-start(bf16[512,512]{1,0:T(8,128)(2,1)S(1)} %get-tuple-element.45.own_ref), channel_id=1, source_target_pairs={{0,2},{2,0},{1,3},{3,1},{4,6},{6,4},{5,7},{7,5},{8,10},{10,8},{9,1... | collective-permute-start | bytes 1572872 | tf_op jit(solution)/shard_map/ppermute | solution.py:29
  59.9 1.5 %collective-permute-done.14.other_ref = bf16[512,512]{1,0:T(8,128)(2,1)S(1)} collective-permute-done((bf16[512,512]{1,0:T(8,128)(2,1)S(1)}, bf16[512,512]{1,0:T(8,128)(2,1)S(1)}, u32[]{:S(2)}, u32[]{:S(2)}) %collective-permute-start.14) | collective-permute-done | bytes 524320 | tf_op jit(solution)/shard_map/ppermute | solution.py:29
  61.4 2.5 %direct.1 = (f32[512,512]{1,0:T(8,128)S(1)}, f32[512,512]{1,0:T(8,128)S(1)}) custom-call(bf16[512,512]{1,0:T(8,128)(2,1)S(1)} %get-tuple-element.45.own_ref, bf16[512,512]{1,0:T(8,128)(2,1)S(1)} %collective-permute-done.14.other_ref, bf16[256,1024]{1,0:T(8,128)(2,1)S(1)} %pad_maximum_fusion.refs_0_, bf16[256,1024]{1,0:T(8,128)(2,1)S(1)} %collective-permute-done.8.refs_1_, ...), custom_call_target="tpu_custom_call" | custom-call | tf_op jit(solution)/shard_map/direct/pallas_call | solution.py:182
  64.4 2.3 %collective-permute-done.15.got_ref = f32[512,512]{1,0:T(8,128)S(1)} collective-permute-done((f32[512,512]{1,0:T(8,128)S(1)}, f32[512,512]{1,0:T(8,128)S(1)}, u32[]{:S(2)}, u32[]{:S(2)}) %collective-permute-start.15) | collective-permute-done | bytes 1048608 | tf_op jit(solution)/shard_map/ppermute | solution.py:29
  66.7 1.3 %finish.1 = bf16[1024,512]{1,0:T(8,128)(2,1)S(1)} custom-call(bf16[1024,512]{1,0:T(8,128)(2,1)S(1)} %get-tuple-element.44.psi_ref, f32[512,512]{1,0:T(8,128)S(1)} %get-tuple-element.49.keep_ref, f32[512,512]{1,0:T(8,128)S(1)} %collective-permute-done.15.got_ref), custom_call_target="tpu_custom_call" | custom-call | tf_op jit(solution)/shard_map/finish/pallas_call | solution.py:210
  68.0 23.0 %all_to_all.10 = bf16[128,8,512]{2,1,0:T(8,128)(2,1)S(1)} all-to-all(bf16[128,8,512]{2,1,0:T(8,128)(2,1)S(1)} %bitcast.15), channel_id=1, replica_groups=mesh['zh'=2,'y'=4,'x'=4,'core'=2,'zl'=2] {'zh','core','zl','y','x'}, dimensions={0} | all-to-all | bytes 2097152 | tf_op jit(solution)/shard_map/all_to_all | solution.py:25
  (32 shorter events, 7.9 us)
Async XLA Ops:
  0.0 9.8 %copy-start.2 = (bf16[1024,1,64]{0,2,1:T(8,128)(2,1)S(1)}, bf16[1024,1,64]{0,2,1:T(8,128)(2,1)}, u32[]{:S(2)}) copy-start(bf16[1024,1,64]{0,2,1:T(8,128)(2,1)} %param.6) | copy-start | bytes 393220
  0.0 9.9 %copy-start.3 = (bf16[1,8,1024]{2,1,0:T(8,128)(2,1)S(1)}, bf16[1,8,1024]{2,1,0:T(8,128)(2,1)}, u32[]{:S(2)}) copy-start(bf16[1,8,1024]{2,1,0:T(8,128)(2,1)} %param.4) | copy-start | bytes 49156
  0.0 9.3 %collective-permute-start.2 = (bf16[64,1024]{1,0:T(8,128)(2,1)}, bf16[64,1024]{1,0:T(8,128)(2,1)S(1)}, u32[]{:S(2)}, u32[]{:S(2)}) collective-permute-start(bf16[64,1024]{1,0:T(8,128)(2,1)} %bitcast.20), channel_id=1, source_target_pairs={{0,8},{4,12},{8,0},{12,4},{1,9},{5,13},{9,1},{13,5},{2,10},{6,14},... | collective-permute-start | bytes 393224 | tf_op jit(solution)/shard_map/ppermute | solution.py:21
  3.6 6.2 %collective-permute-start.1 = (bf16[64,1024]{1,0:T(8,128)(2,1)}, bf16[64,1024]{1,0:T(8,128)(2,1)S(1)}, u32[]{:S(2)}, u32[]{:S(2)}) collective-permute-start(bf16[64,1024]{1,0:T(8,128)(2,1)} %bitcast.21), channel_id=1, source_target_pairs={{0,12},{4,0},{8,4},{12,8},{1,13},{5,1},{9,5},{13,9},{2,14},{6,2},{... | collective-permute-start | bytes 393224 | tf_op jit(solution)/shard_map/ppermute | solution.py:21
  4.4 5.4 %collective-permute-start = (bf16[64,1024]{1,0:T(8,128)(2,1)}, bf16[64,1024]{1,0:T(8,128)(2,1)S(1)}, u32[]{:S(2)}, u32[]{:S(2)}) collective-permute-start(bf16[64,1024]{1,0:T(8,128)(2,1)} %bitcast.22), channel_id=1, source_target_pairs={{0,4},{4,8},{8,12},{12,0},{1,5},{5,9},{9,13},{13,1},{2,6},{6,10},{... | collective-permute-start | bytes 393224 | tf_op jit(solution)/shard_map/ppermute | solution.py:21
  6.0 1.6 %copy-start = (f32[128,4096]{1,0:T(8,128)S(1)}, f32[128,4096]{1,0:T(8,128)}, u32[]{:S(2)}) copy-start(f32[128,4096]{1,0:T(8,128)} %in_ref.1) | copy-start | bytes 6291460
  8.5 0.8 copy-start.1
  10.6 23.8 %collective-permute-start.10 = (bf16[3,128,1024]{2,1,0:T(8,128)(2,1)S(1)}, bf16[3,128,1024]{2,1,0:T(8,128)(2,1)S(1)}, u32[]{:S(2)}, u32[]{:S(2)}) collective-permute-start(bf16[3,128,1024]{2,1,0:T(8,128)(2,1)S(1)} %get-tuple-element.34), channel_id=1, source_target_pairs={{0,64},{64,0},{1,65},{65,1},{2,66},{66,2},{3,67},{67,3},{4,68},{68... | collective-permute-start | bytes 2359304 | tf_op jit(solution)/shard_map/ppermute | solution.py:242
  14.3 15.2 %all-to-all-start = ((bf16[16,8,1024]{2,1,0:T(8,128)(2,1)}), bf16[16,8,1024]{2,1,0:T(8,128)(2,1)}, u32[]{:S(2)}, u32[]{:S(2)}) async-start(bf16[16,8,1024]{2,1,0:T(8,128)(2,1)} %broadcast_in_dim.8), calls=%async_computation | async-start | bytes 524288 | tf_op jit(solution)/shard_map/all_to_all | solution.py:25
  21.7 12.6 %collective-permute-start.4 = (bf16[2,128,1024]{2,1,0:T(8,128)(2,1)}, bf16[2,128,1024]{2,1,0:T(8,128)(2,1)S(1)}, u32[]{:S(2)}, u32[]{:S(2)}) collective-permute-start(bf16[2,128,1024]{2,1,0:T(8,128)(2,1)} %copy-done.1), channel_id=1, source_target_pairs={{0,2},{2,0},{1,3},{3,1},{4,6},{6,4},{5,7},{7,5},{8,10},{10,8},{9,1... | collective-permute-start | bytes 1572872 | tf_op jit(solution)/shard_map/ppermute | solution.py:29
  30.5 3.8 %collective-permute-start.3 = (bf16[128,512]{1,0:T(8,128)(2,1)S(1)}, bf16[128,512]{1,0:T(8,128)(2,1)S(1)}, u32[]{:S(2)}, u32[]{:S(2)}) collective-permute-start(bf16[128,512]{1,0:T(8,128)(2,1)S(1)} %get-tuple-element.52), channel_id=1, source_target_pairs={{0,2},{2,0},{1,3},{3,1},{4,6},{6,4},{5,7},{7,5},{8,10},{10,8},{9,1... | collective-permute-start | bytes 393224 | tf_op jit(solution)/shard_map/ppermute | solution.py:29
  32.8 13.5 %collective-permute-start.9 = (bf16[256,1024]{1,0:T(8,128)(2,1)S(1)}, bf16[256,1024]{1,0:T(8,128)(2,1)S(1)}, u32[]{:S(2)}, u32[]{:S(2)}) collective-permute-start(bf16[256,1024]{1,0:T(8,128)(2,1)S(1)} %pad_maximum_fusion.refs_0_), channel_id=1, source_target_pairs={{0,48},{16,0},{32,16},{48,32},{1,49},{17,1},{33,17},{49,33},{2,50}... | collective-permute-start | bytes 1572872 | tf_op jit(solution)/shard_map/ppermute | solution.py:21
  33.4 14.4 %collective-permute-start.8 = (bf16[256,1024]{1,0:T(8,128)(2,1)S(1)}, bf16[256,1024]{1,0:T(8,128)(2,1)S(1)}, u32[]{:S(2)}, u32[]{:S(2)}) collective-permute-start(bf16[256,1024]{1,0:T(8,128)(2,1)S(1)} %pad_maximum_fusion.refs_0_), channel_id=1, source_target_pairs={{0,16},{16,32},{32,48},{48,0},{1,17},{17,33},{33,49},{49,1},{2,18}... | collective-permute-start | bytes 1572872 | tf_op jit(solution)/shard_map/ppermute | solution.py:21
  34.4 13.4 %collective-permute-start.11 = (bf16[2,128,1024]{2,1,0:T(8,128)(2,1)S(1)}, bf16[2,128,1024]{2,1,0:T(8,128)(2,1)S(1)}, u32[]{:S(2)}, u32[]{:S(2)}) collective-permute-start(bf16[2,128,1024]{2,1,0:T(8,128)(2,1)S(1)} %slice.9), channel_id=1, source_target_pairs={{0,2},{2,0},{1,3},{3,1},{4,6},{6,4},{5,7},{7,5},{8,10},{10,8},{9,1... | collective-permute-start | bytes 1572872 | tf_op jit(solution)/shard_map/ppermute | solution.py:29
  35.1 14.3 %collective-permute-start.7 = (bf16[256,512]{1,0:T(8,128)(2,1)S(1)}, bf16[256,512]{1,0:T(8,128)(2,1)S(1)}, u32[]{:S(2)}, u32[]{:S(2)}) collective-permute-start(bf16[256,512]{1,0:T(8,128)(2,1)S(1)} %pad_maximum_fusion.1.refs_0_), channel_id=1, source_target_pairs={{0,64},{1,65},{64,0},{65,1},{2,66},{3,67},{66,2},{67,3},{4,68},{5,... | collective-permute-start | bytes 786440 | tf_op jit(solution)/shard_map/ppermute | solution.py:222
  35.9 13.5 %collective-permute-start.6 = (bf16[256,512]{1,0:T(8,128)(2,1)S(1)}, bf16[256,512]{1,0:T(8,128)(2,1)S(1)}, u32[]{:S(2)}, u32[]{:S(2)}) collective-permute-start(bf16[256,512]{1,0:T(8,128)(2,1)S(1)} %pad_maximum_fusion.1.refs_0_), channel_id=1, source_target_pairs={{0,65},{1,0},{64,1},{65,64},{2,67},{3,2},{66,3},{67,66},{4,69},{5,... | collective-permute-start | bytes 786440 | tf_op jit(solution)/shard_map/ppermute | solution.py:222
  46.3 8.2 %collective-permute-start.5 = (bf16[256,512]{1,0:T(8,128)(2,1)S(1)}, bf16[256,512]{1,0:T(8,128)(2,1)S(1)}, u32[]{:S(2)}, u32[]{:S(2)}) collective-permute-start(bf16[256,512]{1,0:T(8,128)(2,1)S(1)} %pad_maximum_fusion.1.refs_0_), channel_id=1, source_target_pairs={{0,1},{1,64},{64,65},{65,0},{2,3},{3,66},{66,67},{67,2},{4,5},{5,6... | collective-permute-start | bytes 786440 | tf_op jit(solution)/shard_map/ppermute | solution.py:222
  47.8 6.7 %collective-permute-start.13 = (bf16[128,1024]{1,0:T(8,128)(2,1)S(1)}, bf16[128,1024]{1,0:T(8,128)(2,1)S(1)}, u32[]{:S(2)}, u32[]{:S(2)}) collective-permute-start(bf16[128,1024]{1,0:T(8,128)(2,1)S(1)} %slice.11), channel_id=1, source_target_pairs={{0,48},{16,0},{32,16},{48,32},{1,49},{17,1},{33,17},{49,33},{2,50}... | collective-permute-start | bytes 786440 | tf_op jit(solution)/shard_map/ppermute | solution.py:21
  49.0 7.6 %collective-permute-start.12 = (bf16[128,1024]{1,0:T(8,128)(2,1)S(1)}, bf16[128,1024]{1,0:T(8,128)(2,1)S(1)}, u32[]{:S(2)}, u32[]{:S(2)}) collective-permute-start(bf16[128,1024]{1,0:T(8,128)(2,1)S(1)} %slice.10), channel_id=1, source_target_pairs={{0,16},{16,32},{32,48},{48,0},{1,17},{17,33},{33,49},{49,1},{2,18}... | collective-permute-start | bytes 786440 | tf_op jit(solution)/shard_map/ppermute | solution.py:21
  57.5 4.0 %collective-permute-start.14 = (bf16[512,512]{1,0:T(8,128)(2,1)S(1)}, bf16[512,512]{1,0:T(8,128)(2,1)S(1)}, u32[]{:S(2)}, u32[]{:S(2)}) collective-permute-start(bf16[512,512]{1,0:T(8,128)(2,1)S(1)} %get-tuple-element.45.own_ref), channel_id=1, source_target_pairs={{0,2},{2,0},{1,3},{3,1},{4,6},{6,4},{5,7},{7,5},{8,10},{10,8},{9,1... | collective-permute-start | bytes 1572872 | tf_op jit(solution)/shard_map/ppermute | solution.py:29
  63.9 2.7 %collective-permute-start.15 = (f32[512,512]{1,0:T(8,128)S(1)}, f32[512,512]{1,0:T(8,128)S(1)}, u32[]{:S(2)}, u32[]{:S(2)}) collective-permute-start(f32[512,512]{1,0:T(8,128)S(1)} %get-tuple-element.50), channel_id=1, source_target_pairs={{0,2},{2,0},{1,3},{3,1},{4,6},{6,4},{5,7},{7,5},{8,10},{10,8},{9,1... | collective-permute-start | bytes 3145736 | tf_op jit(solution)/shard_map/ppermute | solution.py:29

commit v11 on v8

--- a/solution.py
+++ b/solution.py
@@ -8,8 +8,6 @@
 
 TILE_VEC = ("zh", "y", "x", "core", "zl")
 TILE = ("zh", "y", "x", "core")
-PLANE = ("y", "x")
-ORDER = ("y", "x", "zh", "zl", "core")
 STEPS = (0, -1, 1, -2)
 F32 = jnp.float32
 BF16 = jnp.bfloat16
@@ -206,34 +204,17 @@
     )(psi, keep, got)
 
 
-def ring(value, by):
-    return lax.ppermute(value, ("zh", "zl"), [(k, (k + by) % 4) for k in range(4)])
-
-
-def to_all(value):
-    copies = jnp.broadcast_to(value[None], (lax.axis_size(PLANE), *value.shape))
-    return copies
-
-
 def shards(trial, psi_v, psi_c, screened):
     rows, states = trial.shape[1:]
     half = states // 2
-    devices = lax.axis_size(ORDER)
-    core = lax.axis_index("core")
-    place = 2 * lax.axis_index("zh") + lax.axis_index("zl")
-    left = psi_v.reshape(2, 4, 4, 2, 2, rows, -1).transpose(1, 2, 0, 4, 3, 5, 6).reshape(psi_v.shape)
-    mine = lax.dynamic_slice_in_dim(trial[0], core * half, half, 1)
-    got = swap(lax.dynamic_slice_in_dim(trial[0], (1 - core) * half, half, 1))
-    pair = jnp.concatenate([jnp.where(core == 0, mine, got), jnp.where(core == 0, got, mine)], 0)
-    steps = [pair, ring(pair, -1), ring(pair, 2), ring(pair, 1)]
-    column = jnp.concatenate(
-        [lax.select_n(place, *(steps[(to - at) % 4] for at in range(4))) for to in range(4)], 0
-    )
+    devices = lax.axis_size(TILE_VEC)
+    own, near, far = pack(screened, psi_v)
     block = psi_c[:, 0, :].T
     line = jnp.concatenate([block, shift(block, "x", 1), shift(block, "x", -1), shift(block, "x", 2)], 0)
-    own, near, far = pack(screened, left)
-    copies, near, far, line = lax.optimization_barrier((to_all(column), near, far, line))
-    trial_half = exchange(copies, PLANE).reshape(-1, half)
+    halves = trial[0].reshape(rows, 2, half).transpose(1, 0, 2)
+    copies = jnp.broadcast_to(halves[None, :, None], (devices // 4, 2, 2, rows, half))
+    copies, near, far, line = lax.optimization_barrier((copies, near, far, line))
+    trial_half = exchange(copies.reshape(devices, rows, half), TILE_VEC).reshape(-1, half)
     near = swap(near)
     far = lax.ppermute(far, "zh", [(0, 1), (1, 0)])
     behind, ahead = shift(line, "y", 1), shift(line, "y", -1)
@@ -241,15 +222,16 @@
     passed = swap(far[1:])
     middle = line.shape[0] // 2
     beyond = [shift(behind[:middle], "y", 1), shift(ahead[middle:], "y", -1)]
-    proj_own, psi = project(trial_half, left, near, far, passed)
+    passed, beyond = lax.optimization_barrier((passed, beyond))
+    proj_own, psi = project(trial_half, psi_v, near, far, passed)
     proj_other = swap(proj_own)
     panel = [line, behind, ahead, *beyond]
     keep, send = direct(proj_own, proj_other, panel, own, [near, far, passed])
     got = swap(send)
     term = finish(psi, keep, got)
-    parts = exchange(term.reshape(devices, rows, half), ORDER)
-    parts = parts.reshape(-1, 2, rows, half).astype(F32)
-    total = jnp.sum(parts, axis=0)
+    parts = exchange(term.reshape(devices, rows, half), TILE_VEC)
+    parts = parts.reshape(-1, 2, 2, rows, half).astype(F32)
+    total = jnp.sum(parts, axis=(0, 2))
     return total.transpose(1, 0, 2).reshape(1, rows, states)
 
 

time: 103 us -> 97.7 us (0.949)
  starting transfers between devices: 36.5 us -> 32.5 us
  blocking collectives: 22.8 us -> 26 us
  Pallas kernels: 9.02 us -> 6.61 us
  waiting for transfers between devices: 24.2 us -> 22.4 us
    ppermute x5 -> x4, starting transfers between devices: 17.8 us -> 9.62 us  [swap(): return lax.ppermute(value, 'core', [(0, 1), (1, 0)])]
    ppermute x7, waiting for transfers between devices: 19.2 us -> 11.8 us  [shift(): return lax.ppermute(value, axis, [(k, (k + by) % n) for k in range(n)])]
    ppermute x1, waiting for transfers between devices: 0.01 us -> 6.8 us  [shards(): far = lax.ppermute(far, 'zh', [(0, 1), (1, 0)])]
    ppermute x3 -> x0, starting transfers between devices: 5.15 us -> none  [ring(): lax.ppermute(value, ('zh', 'zl'), [(k, (k + by) % 4) for k in range(4)])]
    all_to_all x1, starting transfers between devices: 4.05 us -> 8.41 us  [exchange(): return lax.all_to_all(value, axes, split_axis=0, concat_axis=0, tiled=True)]
    all_to_all x1, blocking collectives: 22.8 us -> 26 us  [exchange(): return lax.all_to_all(value, axes, split_axis=0, concat_axis=0, tiled=True)]
    unnamed x10 -> x32, local copies, waits for them, and re-layouts: 3.19 us -> 5.83 us
    ppermute x1, starting transfers between devices: 1.06 us -> 3.6 us  [shards(): far = lax.ppermute(far, 'zh', [(0, 1), (1, 0)])]
  transfers between devices with their start and end apart: 17 -> 13, of which waited for: 8 -> 7; matrix products, arithmetic and copies ran while one was open for 4% -> 2% of each run, Pallas kernels for 2% -> 2%
where the time goes in v11:
time: 97.7 us; the launch traced here: 97.4 us
  starting transfers between devices  32.5 us (33%)
  blocking collectives  26 us (27%)
  waiting for transfers between devices  22.4 us (23%)
  local copies, waits for them, and re-layouts  8.92 us (9%)
  Pallas kernels  6.61 us (7%)
    all_to_all x1, blocking collectives, exchange(): return lax.all_to_all(value, axes, split_axis=0, concat_axis=0, tiled=True)  26 us
    ppermute x7, waiting for transfers between devices, shift(): return lax.ppermute(value, axis, [(k, (k + by) % n) for k in range(n)])  11.8 us
    ppermute x7, starting transfers between devices, shift(): return lax.ppermute(value, axis, [(k, (k + by) % n) for k in range(n)])  10.8 us
    ppermute x4, starting transfers between devices, swap(): return lax.ppermute(value, 'core', [(0, 1), (1, 0)])  9.62 us
    all_to_all x1, starting transfers between devices, exchange(): return lax.all_to_all(value, axes, split_axis=0, concat_axis=0, tiled=True)  8.41 us
    ppermute x1, waiting for transfers between devices, shards(): far = lax.ppermute(far, 'zh', [(0, 1), (1, 0)])  6.8 us
    unnamed x32, local copies, waits for them, and re-layouts  5.83 us
    ppermute x4, waiting for transfers between devices, swap(): return lax.ppermute(value, 'core', [(0, 1), (1, 0)])  3.83 us
  transfers between devices with their start and end apart: 13, of which 7 were waited for; matrix products, arithmetic and copies ran while one was open for 2% of the time, Pallas kernels for 2%

profile of v11, /device:TPU:1, one launch (start us, length us, event | category | flops | bytes accessed | tf_op | source)
XLA Modules:
  0.0 97.4 jit_solution(15459935391032583678)
XLA Ops:
  0.0 3.6 %collective-permute-start.2 = (bf16[64,1024]{1,0:T(8,128)(2,1)}, bf16[64,1024]{1,0:T(8,128)(2,1)S(1)}, u32[]{:S(2)}, u32[]{:S(2)}) collective-permute-start(bf16[64,1024]{1,0:T(8,128)(2,1)} %bitcast.18), channel_id=1, source_target_pairs={{0,8},{4,12},{8,0},{12,4},{1,9},{5,13},{9,1},{13,5},{2,10},{6,14},... | collective-permute-start | bytes 393224 | tf_op jit(solution)/shard_map/ppermute | solution.py:19
  5.0 1.6 %copy-done = f32[128,4096]{1,0:T(8,128)S(1)} copy-done((f32[128,4096]{1,0:T(8,128)S(1)}, f32[128,4096]{1,0:T(8,128)}, u32[]{:S(2)}) %copy-start) | copy-done | bytes 2097176
  6.6 0.9 copy-done.5
  7.6 2.0 %pack.1 = (f32[128,1024]{1,0:T(8,128)S(1)}, bf16[2,128,1024]{2,1,0:T(8,128)(2,1)S(1)}, bf16[3,128,1024]{2,1,0:T(8,128)(2,1)}) custom-call(f32[128,4096]{1,0:T(8,128)S(1)} %copy-done, bf16[1024,128]{1,0:T(8,128)(2,1)S(1)} %copy-done.5), custom_call_target="tpu_custom_call" | custom-call | tf_op jit(solution)/shard_map/pack/pallas_call | solution.py:69
  10.5 1.1 %broadcast_in_dim.2 = bf16[32,2,2,8,512]{4,3,2,1,0:T(8,128)(2,1)} broadcast(bf16[2,8,512]{2,1,0:T(8,128)(2,1)S(1)} %bitcast.22), dimensions={1,3,4} | broadcast | bytes 1064960 | tf_op jit(solution)/shard_map/broadcast_in_dim | solution.py:215
  11.6 3.6 %collective-permute-start.4 = (bf16[3,128,1024]{2,1,0:T(8,128)(2,1)}, bf16[3,128,1024]{2,1,0:T(8,128)(2,1)S(1)}, u32[]{:S(2)}, u32[]{:S(2)}) collective-permute-start(bf16[3,128,1024]{2,1,0:T(8,128)(2,1)} %get-tuple-element.26), channel_id=1, source_target_pairs={{0,64},{64,0},{1,65},{65,1},{2,66},{66,2},{3,67},{67,3},{4,68},{68... | collective-permute-start | bytes 2359304 | tf_op jit(solution)/shard_map/ppermute | solution.py:219
  15.2 2.7 %collective-permute-start.6 = (bf16[256,1024]{1,0:T(8,128)(2,1)S(1)}, bf16[256,1024]{1,0:T(8,128)(2,1)S(1)}, u32[]{:S(2)}, u32[]{:S(2)}) collective-permute-start(bf16[256,1024]{1,0:T(8,128)(2,1)S(1)} %pad_maximum_fusion.refs_0_), channel_id=1, source_target_pairs={{0,48},{16,0},{32,16},{48,32},{1,49},{17,1},{33,17},{49,33},{2,50}... | collective-permute-start | bytes 1572872 | tf_op jit(solution)/shard_map/ppermute | solution.py:19
  17.9 8.4 %all-to-all-start = ((bf16[128,8,512]{2,1,0:T(8,128)(2,1)}), bf16[128,8,512]{2,1,0:T(8,128)(2,1)S(1)}, u32[]{:S(2)}, u32[]{:S(2)}) async-start(bf16[128,8,512]{2,1,0:T(8,128)(2,1)} %bitcast.16), calls=%async_computation | async-start | bytes 2097152 | tf_op jit(solution)/shard_map/all_to_all | solution.py:23
  26.4 0.9 collective-permute-done.6.refs_2_
  27.2 3.2 %collective-permute-done.5.refs_1_ = bf16[256,1024]{1,0:T(8,128)(2,1)S(1)} collective-permute-done((bf16[256,1024]{1,0:T(8,128)(2,1)S(1)}, bf16[256,1024]{1,0:T(8,128)(2,1)S(1)}, u32[]{:S(2)}, u32[]{:S(2)}) %collective-permute-start.5) | collective-permute-done | bytes 524320 | tf_op jit(solution)/shard_map/ppermute | solution.py:19
  30.5 6.8 %collective-permute-done.4.refs_1_.refs_7_ = bf16[3,128,1024]{2,1,0:T(8,128)(2,1)S(1)} collective-permute-done((bf16[3,128,1024]{2,1,0:T(8,128)(2,1)}, bf16[3,128,1024]{2,1,0:T(8,128)(2,1)S(1)}, u32[]{:S(2)}, u32[]{:S(2)}) %collective-permute-start.4) | collective-permute-done | bytes 786464 | tf_op jit(solution)/shard_map/ppermute | solution.py:219
  37.3 7.5 %collective-permute-start.7 = (bf16[2,128,1024]{2,1,0:T(8,128)(2,1)S(1)}, bf16[2,128,1024]{2,1,0:T(8,128)(2,1)S(1)}, u32[]{:S(2)}, u32[]{:S(2)}) collective-permute-start(bf16[2,128,1024]{2,1,0:T(8,128)(2,1)S(1)} %slice.9), channel_id=1, source_target_pairs={{0,2},{2,0},{1,3},{3,1},{4,6},{6,4},{5,7},{7,5},{8,10},{10,8},{9,1... | collective-permute-start | bytes 1572872 | tf_op jit(solution)/shard_map/ppermute | solution.py:27
  44.8 1.0 slice.10
  45.8 1.0 slice.11
  46.8 3.1 %collective-permute-start.9 = (bf16[128,1024]{1,0:T(8,128)(2,1)S(1)}, bf16[128,1024]{1,0:T(8,128)(2,1)S(1)}, u32[]{:S(2)}, u32[]{:S(2)}) collective-permute-start(bf16[128,1024]{1,0:T(8,128)(2,1)S(1)} %slice.11), channel_id=1, source_target_pairs={{0,48},{16,0},{32,16},{48,32},{1,49},{17,1},{33,17},{49,33},{2,50}... | collective-permute-start | bytes 786440 | tf_op jit(solution)/shard_map/ppermute | solution.py:19
  49.8 5.3 %collective-permute-done.9.refs_4_ = bf16[128,1024]{1,0:T(8,128)(2,1)S(1)} collective-permute-done((bf16[128,1024]{1,0:T(8,128)(2,1)S(1)}, bf16[128,1024]{1,0:T(8,128)(2,1)S(1)}, u32[]{:S(2)}, u32[]{:S(2)}) %collective-permute-start.9) | collective-permute-done | bytes 262176 | tf_op jit(solution)/shard_map/ppermute | solution.py:19
  55.8 2.4 %collective-permute-done.8.refs_3_ = bf16[128,1024]{1,0:T(8,128)(2,1)S(1)} collective-permute-done((bf16[128,1024]{1,0:T(8,128)(2,1)S(1)}, bf16[128,1024]{1,0:T(8,128)(2,1)S(1)}, u32[]{:S(2)}, u32[]{:S(2)}) %collective-permute-start.8) | collective-permute-done | bytes 262176 | tf_op jit(solution)/shard_map/ppermute | solution.py:19
  58.9 1.0 %copy-done.6 = bf16[1024,128]{1,0:T(8,128)(2,1)S(1)} copy-done((bf16[1024,128]{1,0:T(8,128)(2,1)S(1)}, bf16[1024,128]{1,0:T(8,128)(2,1)}, u32[]{:S(2)}) %copy-start.6) | copy-done | bytes 262168
  60.8 1.7 %collective-permute-start.10 = (bf16[512,512]{1,0:T(8,128)(2,1)S(1)}, bf16[512,512]{1,0:T(8,128)(2,1)S(1)}, u32[]{:S(2)}, u32[]{:S(2)}) collective-permute-start(bf16[512,512]{1,0:T(8,128)(2,1)S(1)} %get-tuple-element.33.own_ref), channel_id=1, source_target_pairs={{0,2},{2,0},{1,3},{3,1},{4,6},{6,4},{5,7},{7,5},{8,10},{10,8},{9,1... | collective-permute-start | bytes 1572872 | tf_op jit(solution)/shard_map/ppermute | solution.py:27
  62.4 1.5 %collective-permute-done.10.other_ref = bf16[512,512]{1,0:T(8,128)(2,1)S(1)} collective-permute-done((bf16[512,512]{1,0:T(8,128)(2,1)S(1)}, bf16[512,512]{1,0:T(8,128)(2,1)S(1)}, u32[]{:S(2)}, u32[]{:S(2)}) %collective-permute-start.10) | collective-permute-done | bytes 524320 | tf_op jit(solution)/shard_map/ppermute | solution.py:27
  64.0 2.5 %direct.1 = (f32[512,512]{1,0:T(8,128)S(1)}, f32[512,512]{1,0:T(8,128)S(1)}) custom-call(bf16[512,512]{1,0:T(8,128)(2,1)S(1)} %get-tuple-element.33.own_ref, bf16[512,512]{1,0:T(8,128)(2,1)S(1)} %collective-permute-done.10.other_ref, bf16[256,1024]{1,0:T(8,128)(2,1)S(1)} %pad_maximum_fusion.refs_0_, bf16[256,1024]{1,0:T(8,128)(2,1)S(1)} %copy-done.4, ...), custom_call_target="tpu_custom_call" | custom-call | tf_op jit(solution)/shard_map/direct/pallas_call | solution.py:168
  67.0 2.3 %collective-permute-done.11.got_ref = f32[512,512]{1,0:T(8,128)S(1)} collective-permute-done((f32[512,512]{1,0:T(8,128)S(1)}, f32[512,512]{1,0:T(8,128)S(1)}, u32[]{:S(2)}, u32[]{:S(2)}) %collective-permute-start.11) | collective-permute-done | bytes 1048608 | tf_op jit(solution)/shard_map/ppermute | solution.py:27
  69.3 1.3 %finish.1 = bf16[1024,512]{1,0:T(8,128)(2,1)S(1)} custom-call(bf16[1024,512]{1,0:T(8,128)(2,1)S(1)} %get-tuple-element.32.psi_ref, f32[512,512]{1,0:T(8,128)S(1)} %get-tuple-element.37.keep_ref, f32[512,512]{1,0:T(8,128)S(1)} %collective-permute-done.11.got_ref), custom_call_target="tpu_custom_call" | custom-call | tf_op jit(solution)/shard_map/finish/pallas_call | solution.py:196
  70.6 26.0 %all_to_all.10 = bf16[128,8,512]{2,1,0:T(8,128)(2,1)S(1)} all-to-all(bf16[128,8,512]{2,1,0:T(8,128)(2,1)S(1)} %bitcast.15), channel_id=1, replica_groups=mesh['zh'=2,'y'=4,'x'=4,'core'=2,'zl'=2] {'zh','y','x','core','zl'}, dimensions={0} | all-to-all | bytes 2097152 | tf_op jit(solution)/shard_map/all_to_all | solution.py:23
  (45 shorter events, 5.9 us)
Async XLA Ops:
  0.0 10.4 %collective-permute-start.2 = (bf16[64,1024]{1,0:T(8,128)(2,1)}, bf16[64,1024]{1,0:T(8,128)(2,1)S(1)}, u32[]{:S(2)}, u32[]{:S(2)}) collective-permute-start(bf16[64,1024]{1,0:T(8,128)(2,1)} %bitcast.18), channel_id=1, source_target_pairs={{0,8},{4,12},{8,0},{12,4},{1,9},{5,13},{9,1},{13,5},{2,10},{6,14},... | collective-permute-start | bytes 393224 | tf_op jit(solution)/shard_map/ppermute | solution.py:19
  3.6 6.8 %collective-permute-start.1 = (bf16[64,1024]{1,0:T(8,128)(2,1)}, bf16[64,1024]{1,0:T(8,128)(2,1)S(1)}, u32[]{:S(2)}, u32[]{:S(2)}) collective-permute-start(bf16[64,1024]{1,0:T(8,128)(2,1)} %bitcast.19), channel_id=1, source_target_pairs={{0,12},{4,0},{8,4},{12,8},{1,13},{5,1},{9,5},{13,9},{2,14},{6,2},{... | collective-permute-start | bytes 393224 | tf_op jit(solution)/shard_map/ppermute | solution.py:19
  4.4 6.0 %collective-permute-start = (bf16[64,1024]{1,0:T(8,128)(2,1)}, bf16[64,1024]{1,0:T(8,128)(2,1)S(1)}, u32[]{:S(2)}, u32[]{:S(2)}) collective-permute-start(bf16[64,1024]{1,0:T(8,128)(2,1)} %bitcast.20), channel_id=1, source_target_pairs={{0,4},{4,8},{8,12},{12,0},{1,5},{5,9},{9,13},{13,1},{2,6},{6,10},{... | collective-permute-start | bytes 393224 | tf_op jit(solution)/shard_map/ppermute | solution.py:19
  5.0 1.6 %copy-start = (f32[128,4096]{1,0:T(8,128)S(1)}, f32[128,4096]{1,0:T(8,128)}, u32[]{:S(2)}) copy-start(f32[128,4096]{1,0:T(8,128)} %in_ref.1) | copy-start | bytes 6291460
  7.6 2.8 %copy-start.14 = (bf16[1024,1,64]{0,2,1:T(8,128)(2,1)S(1)}, bf16[1024,1,64]{0,2,1:T(8,128)(2,1)}, u32[]{:S(2)}) copy-start(bf16[1024,1,64]{0,2,1:T(8,128)(2,1)} %param.6) | copy-start | bytes 393220
  7.6 2.9 %copy-start.15 = (bf16[1,8,1024]{2,1,0:T(8,128)(2,1)S(1)}, bf16[1,8,1024]{2,1,0:T(8,128)(2,1)}, u32[]{:S(2)}) copy-start(bf16[1,8,1024]{2,1,0:T(8,128)(2,1)} %param.4) | copy-start | bytes 49156
  10.4 1.2 %copy-start.7 = (f32[128,1024]{1,0:T(8,128)}, f32[128,1024]{1,0:T(8,128)S(1)}, u32[]{:S(2)}) copy-start(f32[128,1024]{1,0:T(8,128)S(1)} %get-tuple-element.36.refs_5_) | copy-start | bytes 1572868
  11.6 25.7 %collective-permute-start.4 = (bf16[3,128,1024]{2,1,0:T(8,128)(2,1)}, bf16[3,128,1024]{2,1,0:T(8,128)(2,1)S(1)}, u32[]{:S(2)}, u32[]{:S(2)}) collective-permute-start(bf16[3,128,1024]{2,1,0:T(8,128)(2,1)} %get-tuple-element.26), channel_id=1, source_target_pairs={{0,64},{64,0},{1,65},{65,1},{2,66},{66,2},{3,67},{67,3},{4,68},{68... | collective-permute-start | bytes 2359304 | tf_op jit(solution)/shard_map/ppermute | solution.py:219
  15.2 12.0 %collective-permute-start.6 = (bf16[256,1024]{1,0:T(8,128)(2,1)S(1)}, bf16[256,1024]{1,0:T(8,128)(2,1)S(1)}, u32[]{:S(2)}, u32[]{:S(2)}) collective-permute-start(bf16[256,1024]{1,0:T(8,128)(2,1)S(1)} %pad_maximum_fusion.refs_0_), channel_id=1, source_target_pairs={{0,48},{16,0},{32,16},{48,32},{1,49},{17,1},{33,17},{49,33},{2,50}... | collective-permute-start | bytes 1572872 | tf_op jit(solution)/shard_map/ppermute | solution.py:19
  17.9 12.5 %collective-permute-start.5 = (bf16[256,1024]{1,0:T(8,128)(2,1)S(1)}, bf16[256,1024]{1,0:T(8,128)(2,1)S(1)}, u32[]{:S(2)}, u32[]{:S(2)}) collective-permute-start(bf16[256,1024]{1,0:T(8,128)(2,1)S(1)} %pad_maximum_fusion.refs_0_), channel_id=1, source_target_pairs={{0,16},{16,32},{32,48},{48,0},{1,17},{17,33},{33,49},{49,1},{2,18}... | collective-permute-start | bytes 1572872 | tf_op jit(solution)/shard_map/ppermute | solution.py:19
  17.9 41.0 %all-to-all-start = ((bf16[128,8,512]{2,1,0:T(8,128)(2,1)}), bf16[128,8,512]{2,1,0:T(8,128)(2,1)S(1)}, u32[]{:S(2)}, u32[]{:S(2)}) async-start(bf16[128,8,512]{2,1,0:T(8,128)(2,1)} %bitcast.16), calls=%async_computation | async-start | bytes 2097152 | tf_op jit(solution)/shard_map/all_to_all | solution.py:23
  27.2 10.0 %copy-start.1 = (bf16[256,1024]{1,0:T(8,128)(2,1)}, bf16[256,1024]{1,0:T(8,128)(2,1)S(1)}, u32[]{:S(2)}) copy-start(bf16[256,1024]{1,0:T(8,128)(2,1)S(1)} %collective-permute-done.6.refs_2_) | copy-start | bytes 1572868
  30.5 6.8 %copy-start.3 = (bf16[256,1024]{1,0:T(8,128)(2,1)}, bf16[256,1024]{1,0:T(8,128)(2,1)S(1)}, u32[]{:S(2)}) copy-start(bf16[256,1024]{1,0:T(8,128)(2,1)S(1)} %collective-permute-done.5.refs_1_) | copy-start | bytes 1572868
  37.3 21.6 %collective-permute-start.7 = (bf16[2,128,1024]{2,1,0:T(8,128)(2,1)S(1)}, bf16[2,128,1024]{2,1,0:T(8,128)(2,1)S(1)}, u32[]{:S(2)}, u32[]{:S(2)}) collective-permute-start(bf16[2,128,1024]{2,1,0:T(8,128)(2,1)S(1)} %slice.9), channel_id=1, source_target_pairs={{0,2},{2,0},{1,3},{3,1},{4,6},{6,4},{5,7},{7,5},{8,10},{10,8},{9,1... | collective-permute-start | bytes 1572872 | tf_op jit(solution)/shard_map/ppermute | solution.py:27
  44.8 14.1 %collective-permute-start.3 = (bf16[2,128,1024]{2,1,0:T(8,128)(2,1)}, bf16[2,128,1024]{2,1,0:T(8,128)(2,1)S(1)}, u32[]{:S(2)}, u32[]{:S(2)}) collective-permute-start(bf16[2,128,1024]{2,1,0:T(8,128)(2,1)} %copy-done.13), channel_id=1, source_target_pairs={{0,2},{2,0},{1,3},{3,1},{4,6},{6,4},{5,7},{7,5},{8,10},{10,8},{9,1... | collective-permute-start | bytes 1572872 | tf_op jit(solution)/shard_map/ppermute | solution.py:27
  46.8 8.3 %collective-permute-start.9 = (bf16[128,1024]{1,0:T(8,128)(2,1)S(1)}, bf16[128,1024]{1,0:T(8,128)(2,1)S(1)}, u32[]{:S(2)}, u32[]{:S(2)}) collective-permute-start(bf16[128,1024]{1,0:T(8,128)(2,1)S(1)} %slice.11), channel_id=1, source_target_pairs={{0,48},{16,0},{32,16},{48,32},{1,49},{17,1},{33,17},{49,33},{2,50}... | collective-permute-start | bytes 786440 | tf_op jit(solution)/shard_map/ppermute | solution.py:19
  49.8 8.4 %collective-permute-start.8 = (bf16[128,1024]{1,0:T(8,128)(2,1)S(1)}, bf16[128,1024]{1,0:T(8,128)(2,1)S(1)}, u32[]{:S(2)}, u32[]{:S(2)}) collective-permute-start(bf16[128,1024]{1,0:T(8,128)(2,1)S(1)} %slice.10), channel_id=1, source_target_pairs={{0,16},{16,32},{32,48},{48,0},{1,17},{17,33},{33,49},{49,1},{2,18}... | collective-permute-start | bytes 786440 | tf_op jit(solution)/shard_map/ppermute | solution.py:19
  58.9 5.1 %copy-start.2 = (bf16[256,1024]{1,0:T(8,128)(2,1)S(1)}, bf16[256,1024]{1,0:T(8,128)(2,1)}, u32[]{:S(2)}) copy-start(bf16[256,1024]{1,0:T(8,128)(2,1)} %copy-done.1) | copy-start | bytes 1572868
  58.9 5.1 %copy-start.4 = (bf16[256,1024]{1,0:T(8,128)(2,1)S(1)}, bf16[256,1024]{1,0:T(8,128)(2,1)}, u32[]{:S(2)}) copy-start(bf16[256,1024]{1,0:T(8,128)(2,1)} %copy-done.3) | copy-start | bytes 1572868
  60.0 4.0 %copy-start.8 = (f32[128,1024]{1,0:T(8,128)S(1)}, f32[128,1024]{1,0:T(8,128)}, u32[]{:S(2)}) copy-start(f32[128,1024]{1,0:T(8,128)} %copy-done.7) | copy-start | bytes 1572868
  60.0 4.0 %copy-start.10 = (bf16[128,1024]{1,0:T(8,128)(2,1)S(1)}, bf16[128,1024]{1,0:T(8,128)(2,1)}, u32[]{:S(2)}) copy-start(bf16[128,1024]{1,0:T(8,128)(2,1)} %copy-done.9) | copy-start | bytes 786436
  60.0 4.0 %copy-start.12 = (bf16[128,1024]{1,0:T(8,128)(2,1)S(1)}, bf16[128,1024]{1,0:T(8,128)(2,1)}, u32[]{:S(2)}) copy-start(bf16[128,1024]{1,0:T(8,128)(2,1)} %copy-done.11) | copy-start | bytes 786436
  60.8 3.2 %collective-permute-start.10 = (bf16[512,512]{1,0:T(8,128)(2,1)S(1)}, bf16[512,512]{1,0:T(8,128)(2,1)S(1)}, u32[]{:S(2)}, u32[]{:S(2)}) collective-permute-start(bf16[512,512]{1,0:T(8,128)(2,1)S(1)} %get-tuple-element.33.own_ref), channel_id=1, source_target_pairs={{0,2},{2,0},{1,3},{3,1},{4,6},{6,4},{5,7},{7,5},{8,10},{10,8},{9,1... | collective-permute-start | bytes 1572872 | tf_op jit(solution)/shard_map/ppermute | solution.py:27
  66.5 2.7 %collective-permute-start.11 = (f32[512,512]{1,0:T(8,128)S(1)}, f32[512,512]{1,0:T(8,128)S(1)}, u32[]{:S(2)}, u32[]{:S(2)}) collective-permute-start(f32[512,512]{1,0:T(8,128)S(1)} %get-tuple-element.38), channel_id=1, source_target_pairs={{0,2},{2,0},{1,3},{3,1},{4,6},{6,4},{5,7},{7,5},{8,10},{10,8},{9,1... | collective-permute-start | bytes 3145736 | tf_op jit(solution)/shard_map/ppermute | solution.py:27
  (5 other events, 4.2 us)

commit v12 on v11

--- a/solution.py
+++ b/solution.py
@@ -218,11 +218,10 @@
     near = swap(near)
     far = lax.ppermute(far, "zh", [(0, 1), (1, 0)])
     behind, ahead = shift(line, "y", 1), shift(line, "y", -1)
-    far, behind, ahead = lax.optimization_barrier((far, behind, ahead))
-    passed = swap(far[1:])
     middle = line.shape[0] // 2
     beyond = [shift(behind[:middle], "y", 1), shift(ahead[middle:], "y", -1)]
-    passed, beyond = lax.optimization_barrier((passed, beyond))
+    far, beyond = lax.optimization_barrier((far, beyond))
+    passed = swap(far[1:])
     proj_own, psi = project(trial_half, psi_v, near, far, passed)
     proj_other = swap(proj_own)
     panel = [line, behind, ahead, *beyond]

time: 97.7 us -> 89.7 us (0.918)
  starting transfers between devices: 32.5 us -> 25.3 us
  waiting for transfers between devices: 22.4 us -> 20.9 us
  blocking collectives: 26 us -> 27.1 us
    ppermute x4, starting transfers between devices: 9.62 us -> 2.69 us  [swap(): return lax.ppermute(value, 'core', [(0, 1), (1, 0)])]
    ppermute x1, waiting for transfers between devices: 6.8 us -> 0.01 us  [shards(): far = lax.ppermute(far, 'zh', [(0, 1), (1, 0)])]
    ppermute x7, waiting for transfers between devices: 11.8 us -> 15.4 us  [shift(): return lax.ppermute(value, axis, [(k, (k + by) % n) for k in range(n)])]
    slice x2, local copies, waits for them, and re-layouts: 1.94 us -> 0.04 us  [shards(): beyond = [shift(behind[:middle], 'y', 1), shift(ahead[middle:], 'y', -1)]]
    ppermute x4, waiting for transfers between devices: 3.83 us -> 5.56 us  [swap(): return lax.ppermute(value, 'core', [(0, 1), (1, 0)])]
    all_to_all x1, blocking collectives: 26 us -> 27.1 us  [exchange(): return lax.all_to_all(value, axes, split_axis=0, concat_axis=0, tiled=True)]
  transfers between devices with their start and end apart: 13 -> 13, of which waited for: 7 -> 5; matrix products, arithmetic and copies ran while one was open for 2% -> 1% of each run, Pallas kernels for 2% -> 2%
where the time goes in v12:
time: 89.7 us; the launch traced here: 89.4 us
  blocking collectives  27.1 us (30%)
  starting transfers between devices  25.3 us (28%)
  waiting for transfers between devices  20.9 us (23%)
  local copies, waits for them, and re-layouts  8.53 us (10%)
  Pallas kernels  6.62 us (7%)
    all_to_all x1, blocking collectives, exchange(): return lax.all_to_all(value, axes, split_axis=0, concat_axis=0, tiled=True)  27.1 us
    ppermute x7, waiting for transfers between devices, shift(): return lax.ppermute(value, axis, [(k, (k + by) % n) for k in range(n)])  15.4 us
    ppermute x7, starting transfers between devices, shift(): return lax.ppermute(value, axis, [(k, (k + by) % n) for k in range(n)])  10.6 us
    all_to_all x1, starting transfers between devices, exchange(): return lax.all_to_all(value, axes, split_axis=0, concat_axis=0, tiled=True)  8.41 us
    unnamed x32, local copies, waits for them, and re-layouts  6.53 us
    ppermute x4, waiting for transfers between devices, swap(): return lax.ppermute(value, 'core', [(0, 1), (1, 0)])  5.56 us
    ppermute x1, starting transfers between devices, shards(): far = lax.ppermute(far, 'zh', [(0, 1), (1, 0)])  3.6 us
    ppermute x4, starting transfers between devices, swap(): return lax.ppermute(value, 'core', [(0, 1), (1, 0)])  2.69 us
  transfers between devices with their start and end apart: 13, of which 5 were waited for; matrix products, arithmetic and copies ran while one was open for 1% of the time, Pallas kernels for 2%

profile of v12, /device:TPU:1, one launch (start us, length us, event | category | flops | bytes accessed | tf_op | source)
XLA Modules:
  0.0 89.4 jit_solution(15381924584088585548)
XLA Ops:
  0.0 3.6 %collective-permute-start.2 = (bf16[64,1024]{1,0:T(8,128)(2,1)}, bf16[64,1024]{1,0:T(8,128)(2,1)S(1)}, u32[]{:S(2)}, u32[]{:S(2)}) collective-permute-start(bf16[64,1024]{1,0:T(8,128)(2,1)} %bitcast.18), channel_id=1, source_target_pairs={{0,8},{4,12},{8,0},{12,4},{1,9},{5,13},{9,1},{13,5},{2,10},{6,14},... | collective-permute-start | bytes 393224 | tf_op jit(solution)/shard_map/ppermute | solution.py:19
  3.6 0.9 collective-permute-start.1
  5.0 1.6 %copy-done = f32[128,4096]{1,0:T(8,128)S(1)} copy-done((f32[128,4096]{1,0:T(8,128)S(1)}, f32[128,4096]{1,0:T(8,128)}, u32[]{:S(2)}) %copy-start) | copy-done | bytes 2097176
  6.6 0.9 %copy-done.5 = bf16[1024,128]{1,0:T(8,128)(2,1)S(1)} copy-done((bf16[1024,128]{1,0:T(8,128)(2,1)S(1)}, bf16[1024,128]{1,0:T(8,128)(2,1)}, u32[]{:S(2)}) %copy-start.5) | copy-done | bytes 262168
  7.6 2.0 %pack.1 = (f32[128,1024]{1,0:T(8,128)S(1)}, bf16[2,128,1024]{2,1,0:T(8,128)(2,1)S(1)}, bf16[3,128,1024]{2,1,0:T(8,128)(2,1)}) custom-call(f32[128,4096]{1,0:T(8,128)S(1)} %copy-done, bf16[1024,128]{1,0:T(8,128)(2,1)S(1)} %copy-done.5), custom_call_target="tpu_custom_call" | custom-call | tf_op jit(solution)/shard_map/pack/pallas_call | solution.py:69
  9.6 0.8 copy-done.7
  11.3 1.1 %broadcast_in_dim.2 = bf16[32,2,2,8,512]{4,3,2,1,0:T(8,128)(2,1)} broadcast(bf16[2,8,512]{2,1,0:T(8,128)(2,1)S(1)} %bitcast.22), dimensions={1,3,4} | broadcast | bytes 1064960 | tf_op jit(solution)/shard_map/broadcast_in_dim | solution.py:215
  12.4 2.7 %collective-permute-start.7 = (bf16[256,1024]{1,0:T(8,128)(2,1)S(1)}, bf16[256,1024]{1,0:T(8,128)(2,1)S(1)}, u32[]{:S(2)}, u32[]{:S(2)}) collective-permute-start(bf16[256,1024]{1,0:T(8,128)(2,1)S(1)} %pad_maximum_fusion.refs_0_), channel_id=1, source_target_pairs={{0,48},{16,0},{32,16},{48,32},{1,49},{17,1},{33,17},{49,33},{2,50}... | collective-permute-start | bytes 1572872 | tf_op jit(solution)/shard_map/ppermute | solution.py:19
  15.1 3.6 %collective-permute-start.4 = (bf16[3,128,1024]{2,1,0:T(8,128)(2,1)}, bf16[3,128,1024]{2,1,0:T(8,128)(2,1)S(1)}, u32[]{:S(2)}, u32[]{:S(2)}) collective-permute-start(bf16[3,128,1024]{2,1,0:T(8,128)(2,1)} %get-tuple-element.23), channel_id=1, source_target_pairs={{0,64},{64,0},{1,65},{65,1},{2,66},{66,2},{3,67},{67,3},{4,68},{68... | collective-permute-start | bytes 2359304 | tf_op jit(solution)/shard_map/ppermute | solution.py:219
  18.7 8.4 %all-to-all-start = ((bf16[128,8,512]{2,1,0:T(8,128)(2,1)}), bf16[128,8,512]{2,1,0:T(8,128)(2,1)S(1)}, u32[]{:S(2)}, u32[]{:S(2)}) async-start(bf16[128,8,512]{2,1,0:T(8,128)(2,1)} %bitcast.16), calls=%async_computation | async-start | bytes 2097152 | tf_op jit(solution)/shard_map/all_to_all | solution.py:23
  27.2 2.7 %collective-permute-start.8 = (bf16[128,1024]{1,0:T(8,128)(2,1)S(1)}, bf16[128,1024]{1,0:T(8,128)(2,1)S(1)}, u32[]{:S(2)}, u32[]{:S(2)}) collective-permute-start(bf16[128,1024]{1,0:T(8,128)(2,1)S(1)} %slice.13), channel_id=1, source_target_pairs={{0,48},{16,0},{32,16},{48,32},{1,49},{17,1},{33,17},{49,33},{2,50}... | collective-permute-start | bytes 786440 | tf_op jit(solution)/shard_map/ppermute | solution.py:19
  30.0 1.2 %collective-permute-start.3 = (bf16[2,128,1024]{2,1,0:T(8,128)(2,1)}, bf16[2,128,1024]{2,1,0:T(8,128)(2,1)S(1)}, u32[]{:S(2)}, u32[]{:S(2)}) collective-permute-start(bf16[2,128,1024]{2,1,0:T(8,128)(2,1)} %copy-done.13), channel_id=1, source_target_pairs={{0,2},{2,0},{1,3},{3,1},{4,6},{6,4},{5,7},{7,5},{8,10},{10,8},{9,1... | collective-permute-start | bytes 1572872 | tf_op jit(solution)/shard_map/ppermute | solution.py:27
  31.2 14.2 %collective-permute-done.8.refs_4_ = bf16[128,1024]{1,0:T(8,128)(2,1)S(1)} collective-permute-done((bf16[128,1024]{1,0:T(8,128)(2,1)S(1)}, bf16[128,1024]{1,0:T(8,128)(2,1)S(1)}, u32[]{:S(2)}, u32[]{:S(2)}) %collective-permute-start.8) | collective-permute-done | bytes 262176 | tf_op jit(solution)/shard_map/ppermute | solution.py:19
  46.1 1.2 %collective-permute-done.6.refs_3_ = bf16[128,1024]{1,0:T(8,128)(2,1)S(1)} collective-permute-done((bf16[128,1024]{1,0:T(8,128)(2,1)S(1)}, bf16[128,1024]{1,0:T(8,128)(2,1)S(1)}, u32[]{:S(2)}, u32[]{:S(2)}) %collective-permute-start.6) | collective-permute-done | bytes 262176 | tf_op jit(solution)/shard_map/ppermute | solution.py:19
  48.0 0.9 slice.11
  49.4 1.7 %collective-permute-done.9.refs_2_.refs_8_ = bf16[2,128,1024]{2,1,0:T(8,128)(2,1)S(1)} collective-permute-done((bf16[2,128,1024]{2,1,0:T(8,128)(2,1)}, bf16[2,128,1024]{2,1,0:T(8,128)(2,1)S(1)}, u32[]{:S(2)}, u32[]{:S(2)}) %collective-permute-start.9) | collective-permute-done | bytes 524320 | tf_op jit(solution)/shard_map/ppermute | solution.py:27
  51.2 0.9 %copy-done.6 = bf16[1024,128]{1,0:T(8,128)(2,1)S(1)} copy-done((bf16[1024,128]{1,0:T(8,128)(2,1)S(1)}, bf16[1024,128]{1,0:T(8,128)(2,1)}, u32[]{:S(2)}) %copy-start.6) | copy-done | bytes 262168
  52.1 0.8 project.1
  53.4 1.5 %collective-permute-done.10.other_ref = bf16[512,512]{1,0:T(8,128)(2,1)S(1)} collective-permute-done((bf16[512,512]{1,0:T(8,128)(2,1)S(1)}, bf16[512,512]{1,0:T(8,128)(2,1)S(1)}, u32[]{:S(2)}, u32[]{:S(2)}) %collective-permute-start.10) | collective-permute-done | bytes 524320 | tf_op jit(solution)/shard_map/ppermute | solution.py:27
  55.0 2.5 %direct.1 = (f32[512,512]{1,0:T(8,128)S(1)}, f32[512,512]{1,0:T(8,128)S(1)}) custom-call(bf16[512,512]{1,0:T(8,128)(2,1)S(1)} %get-tuple-element.27.own_ref, bf16[512,512]{1,0:T(8,128)(2,1)S(1)} %collective-permute-done.10.other_ref, bf16[256,1024]{1,0:T(8,128)(2,1)S(1)} %pad_maximum_fusion.refs_0_, bf16[256,1024]{1,0:T(8,128)(2,1)S(1)} %copy-done.4, ...), custom_call_target="tpu_custom_call" | custom-call | tf_op jit(solution)/shard_map/direct/pallas_call | solution.py:168
  57.9 2.3 %collective-permute-done.11.got_ref = f32[512,512]{1,0:T(8,128)S(1)} collective-permute-done((f32[512,512]{1,0:T(8,128)S(1)}, f32[512,512]{1,0:T(8,128)S(1)}, u32[]{:S(2)}, u32[]{:S(2)}) %collective-permute-start.11) | collective-permute-done | bytes 1048608 | tf_op jit(solution)/shard_map/ppermute | solution.py:27
  60.2 1.3 %finish.1 = bf16[1024,512]{1,0:T(8,128)(2,1)S(1)} custom-call(bf16[1024,512]{1,0:T(8,128)(2,1)S(1)} %get-tuple-element.26.psi_ref, f32[512,512]{1,0:T(8,128)S(1)} %get-tuple-element.31.keep_ref, f32[512,512]{1,0:T(8,128)S(1)} %collective-permute-done.11.got_ref), custom_call_target="tpu_custom_call" | custom-call | tf_op jit(solution)/shard_map/finish/pallas_call | solution.py:196
  61.5 27.1 %all_to_all.10 = bf16[128,8,512]{2,1,0:T(8,128)(2,1)S(1)} all-to-all(bf16[128,8,512]{2,1,0:T(8,128)(2,1)S(1)} %bitcast.15), channel_id=1, replica_groups=mesh['zh'=2,'y'=4,'x'=4,'core'=2,'zl'=2] {'zh','y','x','core','zl'}, dimensions={0} | all-to-all | bytes 2097152 | tf_op jit(solution)/shard_map/all_to_all | solution.py:23
  88.6 0.8 convert_reduce_fusion
  (45 shorter events, 4.5 us)
Async XLA Ops:
  0.0 11.2 %collective-permute-start.2 = (bf16[64,1024]{1,0:T(8,128)(2,1)}, bf16[64,1024]{1,0:T(8,128)(2,1)S(1)}, u32[]{:S(2)}, u32[]{:S(2)}) collective-permute-start(bf16[64,1024]{1,0:T(8,128)(2,1)} %bitcast.18), channel_id=1, source_target_pairs={{0,8},{4,12},{8,0},{12,4},{1,9},{5,13},{9,1},{13,5},{2,10},{6,14},... | collective-permute-start | bytes 393224 | tf_op jit(solution)/shard_map/ppermute | solution.py:19
  3.6 7.6 %collective-permute-start.1 = (bf16[64,1024]{1,0:T(8,128)(2,1)}, bf16[64,1024]{1,0:T(8,128)(2,1)S(1)}, u32[]{:S(2)}, u32[]{:S(2)}) collective-permute-start(bf16[64,1024]{1,0:T(8,128)(2,1)} %bitcast.19), channel_id=1, source_target_pairs={{0,12},{4,0},{8,4},{12,8},{1,13},{5,1},{9,5},{13,9},{2,14},{6,2},{... | collective-permute-start | bytes 393224 | tf_op jit(solution)/shard_map/ppermute | solution.py:19
  4.4 6.7 %collective-permute-start = (bf16[64,1024]{1,0:T(8,128)(2,1)}, bf16[64,1024]{1,0:T(8,128)(2,1)S(1)}, u32[]{:S(2)}, u32[]{:S(2)}) collective-permute-start(bf16[64,1024]{1,0:T(8,128)(2,1)} %bitcast.20), channel_id=1, source_target_pairs={{0,4},{4,8},{8,12},{12,0},{1,5},{5,9},{9,13},{13,1},{2,6},{6,10},{... | collective-permute-start | bytes 393224 | tf_op jit(solution)/shard_map/ppermute | solution.py:19
  5.0 1.6 %copy-start = (f32[128,4096]{1,0:T(8,128)S(1)}, f32[128,4096]{1,0:T(8,128)}, u32[]{:S(2)}) copy-start(f32[128,4096]{1,0:T(8,128)} %in_ref.1) | copy-start | bytes 6291460
  6.6 0.9 %copy-start.5 = (bf16[1024,128]{1,0:T(8,128)(2,1)S(1)}, bf16[1024,128]{1,0:T(8,128)(2,1)}, u32[]{:S(2)}) copy-start(bf16[1024,128]{1,0:T(8,128)(2,1)} %left_ref.3) | copy-start | bytes 786436
  7.6 3.6 %copy-start.14 = (bf16[1024,1,64]{0,2,1:T(8,128)(2,1)S(1)}, bf16[1024,1,64]{0,2,1:T(8,128)(2,1)}, u32[]{:S(2)}) copy-start(bf16[1024,1,64]{0,2,1:T(8,128)(2,1)} %param.6) | copy-start | bytes 393220
  7.6 3.7 %copy-start.15 = (bf16[1,8,1024]{2,1,0:T(8,128)(2,1)S(1)}, bf16[1,8,1024]{2,1,0:T(8,128)(2,1)}, u32[]{:S(2)}) copy-start(bf16[1,8,1024]{2,1,0:T(8,128)(2,1)} %param.4) | copy-start | bytes 49156
  12.4 14.8 %collective-permute-start.7 = (bf16[256,1024]{1,0:T(8,128)(2,1)S(1)}, bf16[256,1024]{1,0:T(8,128)(2,1)S(1)}, u32[]{:S(2)}, u32[]{:S(2)}) collective-permute-start(bf16[256,1024]{1,0:T(8,128)(2,1)S(1)} %pad_maximum_fusion.refs_0_), channel_id=1, source_target_pairs={{0,48},{16,0},{32,16},{48,32},{1,49},{17,1},{33,17},{49,33},{2,50}... | collective-permute-start | bytes 1572872 | tf_op jit(solution)/shard_map/ppermute | solution.py:19
  15.1 14.8 %collective-permute-start.5 = (bf16[256,1024]{1,0:T(8,128)(2,1)S(1)}, bf16[256,1024]{1,0:T(8,128)(2,1)S(1)}, u32[]{:S(2)}, u32[]{:S(2)}) collective-permute-start(bf16[256,1024]{1,0:T(8,128)(2,1)S(1)} %pad_maximum_fusion.refs_0_), channel_id=1, source_target_pairs={{0,16},{16,32},{32,48},{48,0},{1,17},{17,33},{33,49},{49,1},{2,18}... | collective-permute-start | bytes 1572872 | tf_op jit(solution)/shard_map/ppermute | solution.py:19
  15.1 32.9 %collective-permute-start.4 = (bf16[3,128,1024]{2,1,0:T(8,128)(2,1)}, bf16[3,128,1024]{2,1,0:T(8,128)(2,1)S(1)}, u32[]{:S(2)}, u32[]{:S(2)}) collective-permute-start(bf16[3,128,1024]{2,1,0:T(8,128)(2,1)} %get-tuple-element.23), channel_id=1, source_target_pairs={{0,64},{64,0},{1,65},{65,1},{2,66},{66,2},{3,67},{67,3},{4,68},{68... | collective-permute-start | bytes 2359304 | tf_op jit(solution)/shard_map/ppermute | solution.py:219
  18.7 30.7 %all-to-all-start = ((bf16[128,8,512]{2,1,0:T(8,128)(2,1)}), bf16[128,8,512]{2,1,0:T(8,128)(2,1)S(1)}, u32[]{:S(2)}, u32[]{:S(2)}) async-start(bf16[128,8,512]{2,1,0:T(8,128)(2,1)} %bitcast.16), calls=%async_computation | async-start | bytes 2097152 | tf_op jit(solution)/shard_map/all_to_all | solution.py:23
  27.1 2.8 %copy-start.1 = (bf16[256,1024]{1,0:T(8,128)(2,1)}, bf16[256,1024]{1,0:T(8,128)(2,1)S(1)}, u32[]{:S(2)}) copy-start(bf16[256,1024]{1,0:T(8,128)(2,1)S(1)} %collective-permute-done.7.refs_2_) | copy-start | bytes 1572868
  27.2 18.2 %collective-permute-start.8 = (bf16[128,1024]{1,0:T(8,128)(2,1)S(1)}, bf16[128,1024]{1,0:T(8,128)(2,1)S(1)}, u32[]{:S(2)}, u32[]{:S(2)}) collective-permute-start(bf16[128,1024]{1,0:T(8,128)(2,1)S(1)} %slice.13), channel_id=1, source_target_pairs={{0,48},{16,0},{32,16},{48,32},{1,49},{17,1},{33,17},{49,33},{2,50}... | collective-permute-start | bytes 786440 | tf_op jit(solution)/shard_map/ppermute | solution.py:19
  29.9 18.1 %copy-start.3 = (bf16[256,1024]{1,0:T(8,128)(2,1)}, bf16[256,1024]{1,0:T(8,128)(2,1)S(1)}, u32[]{:S(2)}) copy-start(bf16[256,1024]{1,0:T(8,128)(2,1)S(1)} %collective-permute-done.5.refs_1_) | copy-start | bytes 1572868
  29.9 17.4 %collective-permute-start.6 = (bf16[128,1024]{1,0:T(8,128)(2,1)S(1)}, bf16[128,1024]{1,0:T(8,128)(2,1)S(1)}, u32[]{:S(2)}, u32[]{:S(2)}) collective-permute-start(bf16[128,1024]{1,0:T(8,128)(2,1)S(1)} %slice.12), channel_id=1, source_target_pairs={{0,16},{16,32},{32,48},{48,0},{1,17},{17,33},{33,49},{49,1},{2,18}... | collective-permute-start | bytes 786440 | tf_op jit(solution)/shard_map/ppermute | solution.py:19
  30.0 19.4 %collective-permute-start.3 = (bf16[2,128,1024]{2,1,0:T(8,128)(2,1)}, bf16[2,128,1024]{2,1,0:T(8,128)(2,1)S(1)}, u32[]{:S(2)}, u32[]{:S(2)}) collective-permute-start(bf16[2,128,1024]{2,1,0:T(8,128)(2,1)} %copy-done.13), channel_id=1, source_target_pairs={{0,2},{2,0},{1,3},{3,1},{4,6},{6,4},{5,7},{7,5},{8,10},{10,8},{9,1... | collective-permute-start | bytes 1572872 | tf_op jit(solution)/shard_map/ppermute | solution.py:27
  48.8 2.3 %collective-permute-start.9 = (bf16[2,128,1024]{2,1,0:T(8,128)(2,1)}, bf16[2,128,1024]{2,1,0:T(8,128)(2,1)S(1)}, u32[]{:S(2)}, u32[]{:S(2)}) collective-permute-start(bf16[2,128,1024]{2,1,0:T(8,128)(2,1)} %slice.11), channel_id=1, source_target_pairs={{0,2},{2,0},{1,3},{3,1},{4,6},{6,4},{5,7},{7,5},{8,10},{10,8},{9,1... | collective-permute-start | bytes 1572872 | tf_op jit(solution)/shard_map/ppermute | solution.py:27
  49.4 5.5 %copy-start.2 = (bf16[256,1024]{1,0:T(8,128)(2,1)S(1)}, bf16[256,1024]{1,0:T(8,128)(2,1)}, u32[]{:S(2)}) copy-start(bf16[256,1024]{1,0:T(8,128)(2,1)} %copy-done.1) | copy-start | bytes 1572868
  49.4 5.5 %copy-start.4 = (bf16[256,1024]{1,0:T(8,128)(2,1)S(1)}, bf16[256,1024]{1,0:T(8,128)(2,1)}, u32[]{:S(2)}) copy-start(bf16[256,1024]{1,0:T(8,128)(2,1)} %copy-done.3) | copy-start | bytes 1572868
  52.1 2.8 %copy-start.8 = (f32[128,1024]{1,0:T(8,128)S(1)}, f32[128,1024]{1,0:T(8,128)}, u32[]{:S(2)}) copy-start(f32[128,1024]{1,0:T(8,128)} %copy-done.7) | copy-start | bytes 1572868
  52.1 2.8 %copy-start.10 = (bf16[128,1024]{1,0:T(8,128)(2,1)S(1)}, bf16[128,1024]{1,0:T(8,128)(2,1)}, u32[]{:S(2)}) copy-start(bf16[128,1024]{1,0:T(8,128)(2,1)} %copy-done.9) | copy-start | bytes 786436
  52.1 2.8 %copy-start.12 = (bf16[128,1024]{1,0:T(8,128)(2,1)S(1)}, bf16[128,1024]{1,0:T(8,128)(2,1)}, u32[]{:S(2)}) copy-start(bf16[128,1024]{1,0:T(8,128)(2,1)} %copy-done.11) | copy-start | bytes 786436
  52.9 2.0 %collective-permute-start.10 = (bf16[512,512]{1,0:T(8,128)(2,1)S(1)}, bf16[512,512]{1,0:T(8,128)(2,1)S(1)}, u32[]{:S(2)}, u32[]{:S(2)}) collective-permute-start(bf16[512,512]{1,0:T(8,128)(2,1)S(1)} %get-tuple-element.27.own_ref), channel_id=1, source_target_pairs={{0,2},{2,0},{1,3},{3,1},{4,6},{6,4},{5,7},{7,5},{8,10},{10,8},{9,1... | collective-permute-start | bytes 1572872 | tf_op jit(solution)/shard_map/ppermute | solution.py:27
  57.5 2.7 %collective-permute-start.11 = (f32[512,512]{1,0:T(8,128)S(1)}, f32[512,512]{1,0:T(8,128)S(1)}, u32[]{:S(2)}, u32[]{:S(2)}) collective-permute-start(f32[512,512]{1,0:T(8,128)S(1)} %get-tuple-element.32), channel_id=1, source_target_pairs={{0,2},{2,0},{1,3},{3,1},{4,6},{6,4},{5,7},{7,5},{8,10},{10,8},{9,1... | collective-permute-start | bytes 3145736 | tf_op jit(solution)/shard_map/ppermute | solution.py:27
  (5 other events, 4.0 us)

commit v13 on v12

--- a/solution.py
+++ b/solution.py
@@ -83,7 +83,7 @@
             pl.BlockSpec((2, rows, width), lambda k: (0, k, 0)),
             pl.BlockSpec((3, rows, width), lambda k: (0, k, 0)),
         ],
-        compiler_params=params(8),
+        compiler_params=params(58),
         name="pack",
     )(screened, left)
 
@@ -149,7 +149,7 @@
             weighted = jnp.concatenate(
                 [
                     (
-                        (scr_refs[0][:, here] if j == 0 else scr_refs[j][0, :, here].astype(F32))
+                        (scr_refs[0][:, here] if j == 0 else scr_refs[j][j // 3, :, here].astype(F32))
                         * pair[j * points : (j + 1) * points]
                     ).astype(BF16)
                     for j in range(4)
@@ -220,9 +220,10 @@
     behind, ahead = shift(line, "y", 1), shift(line, "y", -1)
     middle = line.shape[0] // 2
     beyond = [shift(behind[:middle], "y", 1), shift(ahead[middle:], "y", -1)]
-    far, beyond = lax.optimization_barrier((far, beyond))
-    passed = swap(far[1:])
+    far, *_ = lax.optimization_barrier((far, behind, ahead))
+    passed = swap(far)
     proj_own, psi = project(trial_half, psi_v, near, far, passed)
+    proj_own, beyond = lax.optimization_barrier((proj_own, beyond))
     proj_other = swap(proj_own)
     panel = [line, behind, ahead, *beyond]
     keep, send = direct(proj_own, proj_other, panel, own, [near, far, passed])

time: 89.7 us -> 97.2 us (1.084)
  starting transfers between devices: 25.3 us -> 36.1 us
  waiting for transfers between devices: 20.9 us -> 17.6 us
  Pallas kernels: 6.62 us -> 9.87 us
  local copies, waits for them, and re-layouts: 8.53 us -> 6.26 us
  blocking collectives: 27.1 us -> 26.1 us
    ppermute x4, starting transfers between devices: 2.69 us -> 12.3 us  [swap(): return lax.ppermute(value, 'core', [(0, 1), (1, 0)])]
    ppermute x7, waiting for transfers between devices: 15.4 us -> 9.62 us  [shift(): return lax.ppermute(value, axis, [(k, (k + by) % n) for k in range(n)])]
    unnamed x32 -> x18, local copies, waits for them, and re-layouts: 6.53 us -> 1.84 us
    ppermute x1, waiting for transfers between devices: 0.01 us -> 4.16 us  [shards(): far = lax.ppermute(far, 'zh', [(0, 1), (1, 0)])]
    slice x2, local copies, waits for them, and re-layouts: 0.04 us -> 3.32 us  [shards(): beyond = [shift(behind[:middle], 'y', 1), shift(ahead[middle:], 'y', -1)]]
    pallas_call x1, Pallas kernels: 2 us -> 4.07 us  [pack(): pl.pallas_call(kernel, grid=(steps,), out_shape=[jax.ShapeDtypeStruct((po...]
    ppermute x4, waiting for transfers between devices: 5.56 us -> 3.83 us  [swap(): return lax.ppermute(value, 'core', [(0, 1), (1, 0)])]
    pallas_call x1, Pallas kernels: 2.53 us -> 3.7 us  [direct(): pl.pallas_call(kernel, out_shape=[jax.ShapeDtypeStruct((rows, half), F32)...]
  transfers between devices with their start and end apart: 13 -> 13, of which waited for: 5 -> 7; matrix products, arithmetic and copies ran while one was open for 1% -> 3% of each run, Pallas kernels for 2% -> 5%
where the time goes in v13:
time: 97.2 us; the launch traced here: 96.9 us
  starting transfers between devices  36.1 us (37%)
  blocking collectives  26.1 us (27%)
  waiting for transfers between devices  17.6 us (18%)
  Pallas kernels  9.87 us (10%)
  local copies, waits for them, and re-layouts  6.26 us (6%)
    all_to_all x1, blocking collectives, exchange(): return lax.all_to_all(value, axes, split_axis=0, concat_axis=0, tiled=True)  26.1 us
    ppermute x4, starting transfers between devices, swap(): return lax.ppermute(value, 'core', [(0, 1), (1, 0)])  12.3 us
    ppermute x7, starting transfers between devices, shift(): return lax.ppermute(value, axis, [(k, (k + by) % n) for k in range(n)])  11.2 us
    ppermute x7, waiting for transfers between devices, shift(): return lax.ppermute(value, axis, [(k, (k + by) % n) for k in range(n)])  9.62 us
    all_to_all x1, starting transfers between devices, exchange(): return lax.all_to_all(value, axes, split_axis=0, concat_axis=0, tiled=True)  8.95 us
    ppermute x1, waiting for transfers between devices, shards(): far = lax.ppermute(far, 'zh', [(0, 1), (1, 0)])  4.16 us
    pallas_call x1, Pallas kernels, pack(): pl.pallas_call(kernel, grid=(steps,), out_shape=[jax.ShapeDtypeStruct((po...  4.07 us
    ppermute x4, waiting for transfers between devices, swap(): return lax.ppermute(value, 'core', [(0, 1), (1, 0)])  3.83 us
  transfers between devices with their start and end apart: 13, of which 7 were waited for; matrix products, arithmetic and copies ran while one was open for 3% of the time, Pallas kernels for 5%

profile of v13, /device:TPU:1, one launch (start us, length us, event | category | flops | bytes accessed | tf_op | source)
XLA Modules:
  0.0 96.9 jit_solution(897760496474342211)
XLA Ops:
  0.0 3.6 %collective-permute-start.2 = (bf16[64,1024]{1,0:T(8,128)(2,1)}, bf16[64,1024]{1,0:T(8,128)(2,1)S(1)}, u32[]{:S(2)}, u32[]{:S(2)}) collective-permute-start(bf16[64,1024]{1,0:T(8,128)(2,1)} %bitcast.18), channel_id=1, source_target_pairs={{0,8},{4,12},{8,0},{12,4},{1,9},{5,13},{9,1},{13,5},{2,10},{6,14},... | collective-permute-start | bytes 393224 | tf_op jit(solution)/shard_map/ppermute | solution.py:19
  3.6 0.9 collective-permute-start.1
  5.0 4.1 %pack.1 = (f32[128,1024]{1,0:T(8,128)}, bf16[2,128,1024]{2,1,0:T(8,128)(2,1)}, bf16[3,128,1024]{2,1,0:T(8,128)(2,1)}) custom-call(f32[128,4096]{1,0:T(8,128)} %in_ref.1, bf16[1024,128]{1,0:T(8,128)(2,1)} %left_ref.3), custom_call_target="tpu_custom_call" | custom-call | tf_op jit(solution)/shard_map/pack/pallas_call | solution.py:69
  9.9 1.1 %broadcast_in_dim.2 = bf16[32,2,2,8,512]{4,3,2,1,0:T(8,128)(2,1)} broadcast(bf16[2,8,512]{2,1,0:T(8,128)(2,1)S(1)} %bitcast.22), dimensions={1,3,4} | broadcast | bytes 1064960 | tf_op jit(solution)/shard_map/broadcast_in_dim | solution.py:215
  11.0 3.7 %collective-permute-start.4 = (bf16[3,128,1024]{2,1,0:T(8,128)(2,1)}, bf16[3,128,1024]{2,1,0:T(8,128)(2,1)S(1)}, u32[]{:S(2)}, u32[]{:S(2)}) collective-permute-start(bf16[3,128,1024]{2,1,0:T(8,128)(2,1)} %get-tuple-element.24), channel_id=1, source_target_pairs={{0,64},{64,0},{1,65},{65,1},{2,66},{66,2},{3,67},{67,3},{4,68},{68... | collective-permute-start | bytes 2359304 | tf_op jit(solution)/shard_map/ppermute | solution.py:219
  14.7 2.7 %collective-permute-start.6 = (bf16[256,1024]{1,0:T(8,128)(2,1)S(1)}, bf16[256,1024]{1,0:T(8,128)(2,1)S(1)}, u32[]{:S(2)}, u32[]{:S(2)}) collective-permute-start(bf16[256,1024]{1,0:T(8,128)(2,1)S(1)} %pad_maximum_fusion.refs_0_), channel_id=1, source_target_pairs={{0,48},{16,0},{32,16},{48,32},{1,49},{17,1},{33,17},{49,33},{2,50}... | collective-permute-start | bytes 1572872 | tf_op jit(solution)/shard_map/ppermute | solution.py:19
  17.4 8.9 %all-to-all-start = ((bf16[128,8,512]{2,1,0:T(8,128)(2,1)}), bf16[128,8,512]{2,1,0:T(8,128)(2,1)S(1)}, u32[]{:S(2)}, u32[]{:S(2)}) async-start(bf16[128,8,512]{2,1,0:T(8,128)(2,1)} %bitcast.16), calls=%async_computation | async-start | bytes 2097152 | tf_op jit(solution)/shard_map/all_to_all | solution.py:23
  26.4 3.0 %collective-permute-done.5.refs_1_ = bf16[256,1024]{1,0:T(8,128)(2,1)} collective-permute-done((bf16[256,1024]{1,0:T(8,128)(2,1)S(1)}, bf16[256,1024]{1,0:T(8,128)(2,1)}, u32[]{:S(2)}, u32[]{:S(2)}) %collective-permute-start.5) | collective-permute-done | bytes 524320 | tf_op jit(solution)/shard_map/ppermute | solution.py:19
  29.4 4.2 %collective-permute-done.4.refs_1_.refs_7_ = bf16[3,128,1024]{2,1,0:T(8,128)(2,1)S(1)} collective-permute-done((bf16[3,128,1024]{2,1,0:T(8,128)(2,1)}, bf16[3,128,1024]{2,1,0:T(8,128)(2,1)S(1)}, u32[]{:S(2)}, u32[]{:S(2)}) %collective-permute-start.4) | collective-permute-done | bytes 786464 | tf_op jit(solution)/shard_map/ppermute | solution.py:219
  33.5 10.1 %collective-permute-start.7 = (bf16[3,128,1024]{2,1,0:T(8,128)(2,1)S(1)}, bf16[3,128,1024]{2,1,0:T(8,128)(2,1)S(1)}, u32[]{:S(2)}, u32[]{:S(2)}) collective-permute-start(bf16[3,128,1024]{2,1,0:T(8,128)(2,1)S(1)} %collective-permute-done.4.refs_1_.refs_7_), channel_id=1, source_target_pairs={{0,2},{2,0},{1,3},{3,1},{4,6},{6,4},{5,7},{7,5},{8,10},{10,8},{9,1... | collective-permute-start | bytes 2359304 | tf_op jit(solution)/shard_map/ppermute | solution.py:27
  43.7 1.6 %slice.9 = bf16[128,1024]{1,0:T(8,128)(2,1)} slice(bf16[256,1024]{1,0:T(8,128)(2,1)} %copy-done.3), slice={[128:256], [0:1024]} | slice | bytes 524288 | tf_op jit(solution)/shard_map/slice | solution.py:222
  45.3 3.4 %collective-permute-start.9 = (bf16[128,1024]{1,0:T(8,128)(2,1)}, bf16[128,1024]{1,0:T(8,128)(2,1)}, u32[]{:S(2)}, u32[]{:S(2)}) collective-permute-start(bf16[128,1024]{1,0:T(8,128)(2,1)} %slice.9), channel_id=1, source_target_pairs={{0,48},{16,0},{32,16},{48,32},{1,49},{17,1},{33,17},{49,33},{2,50}... | collective-permute-start | bytes 786440 | tf_op jit(solution)/shard_map/ppermute | solution.py:19
  48.7 1.7 %slice.8 = bf16[128,1024]{1,0:T(8,128)(2,1)} slice(bf16[256,1024]{1,0:T(8,128)(2,1)} %collective-permute-done.5.refs_1_), slice={[0:128], [0:1024]} | slice | bytes 524288 | tf_op jit(solution)/shard_map/slice | solution.py:222
  51.2 1.0 %copy-done.1 = bf16[2,128,1024]{2,1,0:T(8,128)(2,1)S(1)} copy-done((bf16[2,128,1024]{2,1,0:T(8,128)(2,1)S(1)}, bf16[2,128,1024]{2,1,0:T(8,128)(2,1)}, u32[]{:S(2)}) %copy-start.1) | copy-done | bytes 524312
  52.3 0.8 project.1
  53.1 1.1 %collective-permute-done.9.refs_4_ = bf16[128,1024]{1,0:T(8,128)(2,1)} collective-permute-done((bf16[128,1024]{1,0:T(8,128)(2,1)}, bf16[128,1024]{1,0:T(8,128)(2,1)}, u32[]{:S(2)}, u32[]{:S(2)}) %collective-permute-start.9) | collective-permute-done | bytes 262176 | tf_op jit(solution)/shard_map/ppermute | solution.py:19
  54.2 4.8 %collective-permute-done.8.refs_3_ = bf16[128,1024]{1,0:T(8,128)(2,1)} collective-permute-done((bf16[128,1024]{1,0:T(8,128)(2,1)}, bf16[128,1024]{1,0:T(8,128)(2,1)}, u32[]{:S(2)}, u32[]{:S(2)}) %collective-permute-start.8) | collective-permute-done | bytes 262176 | tf_op jit(solution)/shard_map/ppermute | solution.py:19
  59.0 1.7 %collective-permute-start.10 = (bf16[512,512]{1,0:T(8,128)(2,1)S(1)}, bf16[512,512]{1,0:T(8,128)(2,1)S(1)}, u32[]{:S(2)}, u32[]{:S(2)}) collective-permute-start(bf16[512,512]{1,0:T(8,128)(2,1)S(1)} %get-tuple-element.29.own_ref), channel_id=1, source_target_pairs={{0,2},{2,0},{1,3},{3,1},{4,6},{6,4},{5,7},{7,5},{8,10},{10,8},{9,1... | collective-permute-start | bytes 1572872 | tf_op jit(solution)/shard_map/ppermute | solution.py:27
  60.7 1.5 %collective-permute-done.10.other_ref = bf16[512,512]{1,0:T(8,128)(2,1)S(1)} collective-permute-done((bf16[512,512]{1,0:T(8,128)(2,1)S(1)}, bf16[512,512]{1,0:T(8,128)(2,1)S(1)}, u32[]{:S(2)}, u32[]{:S(2)}) %collective-permute-start.10) | collective-permute-done | bytes 524320 | tf_op jit(solution)/shard_map/ppermute | solution.py:27
  62.2 3.7 %direct.1 = (f32[512,512]{1,0:T(8,128)S(1)}, f32[512,512]{1,0:T(8,128)S(1)}) custom-call(bf16[512,512]{1,0:T(8,128)(2,1)S(1)} %get-tuple-element.29.own_ref, bf16[512,512]{1,0:T(8,128)(2,1)S(1)} %collective-permute-done.10.other_ref, bf16[256,1024]{1,0:T(8,128)(2,1)S(1)} %pad_maximum_fusion.refs_0_, bf16[256,1024]{1,0:T(8,128)(2,1)} %collective-permute-done.5.refs_1_, ...), custom_call_target="tpu_custom_call" | custom-call | tf_op jit(solution)/shard_map/direct/pallas_call | solution.py:168
  66.4 2.3 %collective-permute-done.11.got_ref = f32[512,512]{1,0:T(8,128)S(1)} collective-permute-done((f32[512,512]{1,0:T(8,128)S(1)}, f32[512,512]{1,0:T(8,128)S(1)}, u32[]{:S(2)}, u32[]{:S(2)}) %collective-permute-start.11) | collective-permute-done | bytes 1048608 | tf_op jit(solution)/shard_map/ppermute | solution.py:27
  68.7 1.3 %finish.1 = bf16[1024,512]{1,0:T(8,128)(2,1)S(1)} custom-call(bf16[1024,512]{1,0:T(8,128)(2,1)S(1)} %get-tuple-element.27.psi_ref, f32[512,512]{1,0:T(8,128)S(1)} %get-tuple-element.33.keep_ref, f32[512,512]{1,0:T(8,128)S(1)} %collective-permute-done.11.got_ref), custom_call_target="tpu_custom_call" | custom-call | tf_op jit(solution)/shard_map/finish/pallas_call | solution.py:196
  70.0 26.1 %all_to_all.10 = bf16[128,8,512]{2,1,0:T(8,128)(2,1)S(1)} all-to-all(bf16[128,8,512]{2,1,0:T(8,128)(2,1)S(1)} %bitcast.15), channel_id=1, replica_groups=mesh['zh'=2,'y'=4,'x'=4,'core'=2,'zl'=2] {'zh','y','x','core','zl'}, dimensions={0} | all-to-all | bytes 2097152 | tf_op jit(solution)/shard_map/all_to_all | solution.py:23
  96.1 0.8 convert_reduce_fusion
  (30 shorter events, 2.6 us)
Async XLA Ops:
  0.0 9.8 %copy-start.7 = (bf16[1024,1,64]{0,2,1:T(8,128)(2,1)S(1)}, bf16[1024,1,64]{0,2,1:T(8,128)(2,1)}, u32[]{:S(2)}) copy-start(bf16[1024,1,64]{0,2,1:T(8,128)(2,1)} %param.6) | copy-start | bytes 393220
  0.0 9.9 %copy-start.8 = (bf16[1,8,1024]{2,1,0:T(8,128)(2,1)S(1)}, bf16[1,8,1024]{2,1,0:T(8,128)(2,1)}, u32[]{:S(2)}) copy-start(bf16[1,8,1024]{2,1,0:T(8,128)(2,1)} %param.4) | copy-start | bytes 49156
  0.0 9.1 %collective-permute-start.2 = (bf16[64,1024]{1,0:T(8,128)(2,1)}, bf16[64,1024]{1,0:T(8,128)(2,1)S(1)}, u32[]{:S(2)}, u32[]{:S(2)}) collective-permute-start(bf16[64,1024]{1,0:T(8,128)(2,1)} %bitcast.18), channel_id=1, source_target_pairs={{0,8},{4,12},{8,0},{12,4},{1,9},{5,13},{9,1},{13,5},{2,10},{6,14},... | collective-permute-start | bytes 393224 | tf_op jit(solution)/shard_map/ppermute | solution.py:19
  3.6 6.2 %collective-permute-start.1 = (bf16[64,1024]{1,0:T(8,128)(2,1)}, bf16[64,1024]{1,0:T(8,128)(2,1)S(1)}, u32[]{:S(2)}, u32[]{:S(2)}) collective-permute-start(bf16[64,1024]{1,0:T(8,128)(2,1)} %bitcast.19), channel_id=1, source_target_pairs={{0,12},{4,0},{8,4},{12,8},{1,13},{5,1},{9,5},{13,9},{2,14},{6,2},{... | collective-permute-start | bytes 393224 | tf_op jit(solution)/shard_map/ppermute | solution.py:19
  4.4 5.4 %collective-permute-start = (bf16[64,1024]{1,0:T(8,128)(2,1)}, bf16[64,1024]{1,0:T(8,128)(2,1)S(1)}, u32[]{:S(2)}, u32[]{:S(2)}) collective-permute-start(bf16[64,1024]{1,0:T(8,128)(2,1)} %bitcast.20), channel_id=1, source_target_pairs={{0,4},{4,8},{8,12},{12,0},{1,5},{5,9},{9,13},{13,1},{2,6},{6,10},{... | collective-permute-start | bytes 393224 | tf_op jit(solution)/shard_map/ppermute | solution.py:19
  9.9 41.3 %copy-start.5 = (bf16[1024,128]{1,0:T(8,128)(2,1)S(1)}, bf16[1024,128]{1,0:T(8,128)(2,1)}, u32[]{:S(2)}) copy-start(bf16[1024,128]{1,0:T(8,128)(2,1)} %left_ref.3) | copy-start | bytes 786436
  11.0 22.6 %collective-permute-start.4 = (bf16[3,128,1024]{2,1,0:T(8,128)(2,1)}, bf16[3,128,1024]{2,1,0:T(8,128)(2,1)S(1)}, u32[]{:S(2)}, u32[]{:S(2)}) collective-permute-start(bf16[3,128,1024]{2,1,0:T(8,128)(2,1)} %get-tuple-element.24), channel_id=1, source_target_pairs={{0,64},{64,0},{1,65},{65,1},{2,66},{66,2},{3,67},{67,3},{4,68},{68... | collective-permute-start | bytes 2359304 | tf_op jit(solution)/shard_map/ppermute | solution.py:219
  14.7 11.7 %collective-permute-start.6 = (bf16[256,1024]{1,0:T(8,128)(2,1)S(1)}, bf16[256,1024]{1,0:T(8,128)(2,1)S(1)}, u32[]{:S(2)}, u32[]{:S(2)}) collective-permute-start(bf16[256,1024]{1,0:T(8,128)(2,1)S(1)} %pad_maximum_fusion.refs_0_), channel_id=1, source_target_pairs={{0,48},{16,0},{32,16},{48,32},{1,49},{17,1},{33,17},{49,33},{2,50}... | collective-permute-start | bytes 1572872 | tf_op jit(solution)/shard_map/ppermute | solution.py:19
  17.4 12.0 %collective-permute-start.5 = (bf16[256,1024]{1,0:T(8,128)(2,1)S(1)}, bf16[256,1024]{1,0:T(8,128)(2,1)}, u32[]{:S(2)}, u32[]{:S(2)}) collective-permute-start(bf16[256,1024]{1,0:T(8,128)(2,1)S(1)} %pad_maximum_fusion.refs_0_), channel_id=1, source_target_pairs={{0,16},{16,32},{32,48},{48,0},{1,17},{17,33},{33,49},{49,1},{2,18}... | collective-permute-start | bytes 1572872 | tf_op jit(solution)/shard_map/ppermute | solution.py:19
  17.4 33.8 %all-to-all-start = ((bf16[128,8,512]{2,1,0:T(8,128)(2,1)}), bf16[128,8,512]{2,1,0:T(8,128)(2,1)S(1)}, u32[]{:S(2)}, u32[]{:S(2)}) async-start(bf16[128,8,512]{2,1,0:T(8,128)(2,1)} %bitcast.16), calls=%async_computation | async-start | bytes 2097152 | tf_op jit(solution)/shard_map/all_to_all | solution.py:23
  26.4 3.0 %copy-start.3 = (bf16[256,1024]{1,0:T(8,128)(2,1)}, bf16[256,1024]{1,0:T(8,128)(2,1)S(1)}, u32[]{:S(2)}) copy-start(bf16[256,1024]{1,0:T(8,128)(2,1)S(1)} %collective-permute-done.6.refs_2_) | copy-start | bytes 1572868
  33.5 17.7 %collective-permute-start.7 = (bf16[3,128,1024]{2,1,0:T(8,128)(2,1)S(1)}, bf16[3,128,1024]{2,1,0:T(8,128)(2,1)S(1)}, u32[]{:S(2)}, u32[]{:S(2)}) collective-permute-start(bf16[3,128,1024]{2,1,0:T(8,128)(2,1)S(1)} %collective-permute-done.4.refs_1_.refs_7_), channel_id=1, source_target_pairs={{0,2},{2,0},{1,3},{3,1},{4,6},{6,4},{5,7},{7,5},{8,10},{10,8},{9,1... | collective-permute-start | bytes 2359304 | tf_op jit(solution)/shard_map/ppermute | solution.py:27
  43.7 6.7 %collective-permute-start.3 = (bf16[2,128,1024]{2,1,0:T(8,128)(2,1)}, bf16[2,128,1024]{2,1,0:T(8,128)(2,1)S(1)}, u32[]{:S(2)}, u32[]{:S(2)}) collective-permute-start(bf16[2,128,1024]{2,1,0:T(8,128)(2,1)} %get-tuple-element.23), channel_id=1, source_target_pairs={{0,2},{2,0},{1,3},{3,1},{4,6},{6,4},{5,7},{7,5},{8,10},{10,8},{9,1... | collective-permute-start | bytes 1572872 | tf_op jit(solution)/shard_map/ppermute | solution.py:27
  45.3 8.9 %collective-permute-start.9 = (bf16[128,1024]{1,0:T(8,128)(2,1)}, bf16[128,1024]{1,0:T(8,128)(2,1)}, u32[]{:S(2)}, u32[]{:S(2)}) collective-permute-start(bf16[128,1024]{1,0:T(8,128)(2,1)} %slice.9), channel_id=1, source_target_pairs={{0,48},{16,0},{32,16},{48,32},{1,49},{17,1},{33,17},{49,33},{2,50}... | collective-permute-start | bytes 786440 | tf_op jit(solution)/shard_map/ppermute | solution.py:19
  50.4 8.6 %collective-permute-start.8 = (bf16[128,1024]{1,0:T(8,128)(2,1)}, bf16[128,1024]{1,0:T(8,128)(2,1)}, u32[]{:S(2)}, u32[]{:S(2)}) collective-permute-start(bf16[128,1024]{1,0:T(8,128)(2,1)} %slice.8), channel_id=1, source_target_pairs={{0,16},{16,32},{32,48},{48,0},{1,17},{17,33},{33,49},{49,1},{2,18}... | collective-permute-start | bytes 786440 | tf_op jit(solution)/shard_map/ppermute | solution.py:19
  50.4 0.8 copy-start
  51.2 1.0 %copy-start.1 = (bf16[2,128,1024]{2,1,0:T(8,128)(2,1)S(1)}, bf16[2,128,1024]{2,1,0:T(8,128)(2,1)}, u32[]{:S(2)}) copy-start(bf16[2,128,1024]{2,1,0:T(8,128)(2,1)} %copy-done) | copy-start | bytes 1572868
  52.2 9.9 %copy-start.2 = (bf16[2,128,1024]{2,1,0:T(8,128)(2,1)S(1)}, bf16[2,128,1024]{2,1,0:T(8,128)(2,1)}, u32[]{:S(2)}) copy-start(bf16[2,128,1024]{2,1,0:T(8,128)(2,1)} %copy-done) | copy-start | bytes 1572868
  52.2 9.9 %copy-start.4 = (bf16[256,1024]{1,0:T(8,128)(2,1)S(1)}, bf16[256,1024]{1,0:T(8,128)(2,1)}, u32[]{:S(2)}) copy-start(bf16[256,1024]{1,0:T(8,128)(2,1)} %copy-done.3) | copy-start | bytes 1572868
  52.3 9.9 %copy-start.6 = (f32[128,1024]{1,0:T(8,128)S(1)}, f32[128,1024]{1,0:T(8,128)}, u32[]{:S(2)}) copy-start(f32[128,1024]{1,0:T(8,128)} %get-tuple-element.32.refs_5_) | copy-start | bytes 1572868
  59.0 3.2 %collective-permute-start.10 = (bf16[512,512]{1,0:T(8,128)(2,1)S(1)}, bf16[512,512]{1,0:T(8,128)(2,1)S(1)}, u32[]{:S(2)}, u32[]{:S(2)}) collective-permute-start(bf16[512,512]{1,0:T(8,128)(2,1)S(1)} %get-tuple-element.29.own_ref), channel_id=1, source_target_pairs={{0,2},{2,0},{1,3},{3,1},{4,6},{6,4},{5,7},{7,5},{8,10},{10,8},{9,1... | collective-permute-start | bytes 1572872 | tf_op jit(solution)/shard_map/ppermute | solution.py:27
  65.9 2.7 %collective-permute-start.11 = (f32[512,512]{1,0:T(8,128)S(1)}, f32[512,512]{1,0:T(8,128)S(1)}, u32[]{:S(2)}, u32[]{:S(2)}) collective-permute-start(f32[512,512]{1,0:T(8,128)S(1)} %get-tuple-element.34), channel_id=1, source_target_pairs={{0,2},{2,0},{1,3},{3,1},{4,6},{6,4},{5,7},{7,5},{8,10},{10,8},{9,1... | collective-permute-start | bytes 3145736 | tf_op jit(solution)/shard_map/ppermute | solution.py:27

commit v14 on v13

v14 whole, which is shorter than its diff:
```python
import jax
import jax.numpy as jnp
from jax import lax
from jax.experimental import pallas as pl
from jax.experimental.pallas import tpu as pltpu
from jax.sharding import Mesh
from jax.sharding import PartitionSpec as P

TILE_VEC = ("zh", "y", "x", "core", "zl")
TILE = ("zh", "y", "x", "core")
STEPS = (0, -1, 1, -2)
F32 = jnp.float32
BF16 = jnp.bfloat16
SIBLING = (1, 0, 3, 2)


def shift(value, axis, by):
    n = lax.axis_size(axis)
    return lax.ppermute(value, axis, [(k, (k + by) % n) for k in range(n)])


def exchange(value, axes):
    return lax.all_to_all(value, axes, split_axis=0, concat_axis=0, tiled=True)


def swap(value):
    return lax.ppermute(value, "core", [(0, 1), (1, 0)])


def across(value):
    return lax.ppermute(value, "zh", [(0, 1), (1, 0)])


def vmem_spec():
    return pl.BlockSpec(memory_space=pltpu.VMEM)


def params(mebibytes):
    return pltpu.CompilerParams(vmem_limit_bytes=mebibytes * 1024 * 1024)


def project(trial_half, lefts):
    states, points = lefts[0].shape
    cols = trial_half.shape[1]

    def kernel(trial_ref, *refs):
        left_refs, (out_ref, psi_ref) = refs[:4], refs[4:]
        for k in range(4):
            psi_ref[:, k * points : (k + 1) * points] = left_refs[k][...]
        out_ref[...] = lax.dot_general(
            psi_ref[...], trial_ref[...], (((0,), (0,)), ((), ())), preferred_element_type=F32
        ).astype(BF16)

    return pl.pallas_call(
        kernel,
        out_shape=[
            jax.ShapeDtypeStruct((4 * points, cols), BF16),
            jax.ShapeDtypeStruct((states, 4 * points), BF16),
        ],
        in_specs=[vmem_spec()] * 5,
        out_specs=[vmem_spec()] * 2,
        compiler_params=params(12),
        name="project",
    )(trial_half, *lefts)


def direct(proj_own, proj_other, lines, screened, raws):
    rows, half = proj_own.shape
    points = rows // 4
    block = lines[0].shape[0] // 4
    count, states = 16 * block, lines[0].shape[1]
    chunk = 512

    def kernel(own_ref, other_ref, *refs):
        line_refs, screened_ref, raw_refs, refs = refs[:5], refs[5], refs[6:9], refs[9:]
        keep_ref, send_ref, proj, panel_ref, weighted, mine_ref, sem = refs
        y, x, zh = lax.axis_index("y"), lax.axis_index("x"), lax.axis_index("zh")
        core = lax.axis_index("core")
        plane = pl.ds(pl.multiple_of(zh * 2 * count, 2 * count), 2 * count)
        load = pltpu.make_async_copy(screened_ref.at[:, plane], mine_ref, sem)
        load.start()
        for k in range(16):
            at = lax.rem(y + STEPS[k // 4] + 4, 4) * 4 + lax.rem(x + STEPS[k % 4] + 4, 4)
            ref, row = (line_refs[k // 4], k % 4) if k < 12 else (line_refs[k // 2 - 3], k % 2)
            panel_ref[pl.ds(pl.multiple_of(at * block, block), block), :] = ref[
                row * block : (row + 1) * block, :
            ]
        mine = pl.ds(pl.multiple_of(core * half, half), half)
        sibs = pl.ds(pl.multiple_of((1 - core) * half, half), half)
        for k in range(4):
            proj[k * points : (k + 1) * points, :] = other_ref[
                SIBLING[k] * points : (SIBLING[k] + 1) * points, :
            ]
        low = lax.broadcasted_iota(jnp.int32, (points, 128), 1) < 64
        first = core == 0
        nt = (((1,), (1,)), ((), ()))
        for k in range(count // chunk):
            here = pl.ds(k * chunk, chunk)
            pair = lax.dot_general(own_ref[...], panel_ref[here, mine], nt, preferred_element_type=F32)
            pair += lax.dot_general(proj[...], panel_ref[here, sibs], nt, preferred_element_type=F32)
            if k == 0:
                load.wait()
            for j, ref in enumerate((mine_ref, *raw_refs)):
                for m in range(chunk // 128):
                    start = 2 * (k * chunk + m * 128)
                    a = ref[:, start : start + 128].astype(F32)
                    b = ref[:, start + 128 : start + 256].astype(F32)
                    rolled = pltpu.roll(jnp.where(first, b, a), 64, 1)
                    weights = jnp.where(
                        low, jnp.where(first, a, rolled), jnp.where(first, rolled, b)
                    )
                    part = pair[j * points : (j + 1) * points, m * 128 : (m + 1) * 128]
                    weighted[j * points : (j + 1) * points, m * 128 : (m + 1) * 128] = (
                        weights * part
                    ).astype(BF16)
            send = jnp.dot(weighted[...], panel_ref[here, sibs], preferred_element_type=F32)
            keep = jnp.dot(weighted[...], panel_ref[here, mine], preferred_element_type=F32)
            if k == 0:
                send_ref[...] = send
                keep_ref[...] = keep
            else:
                send_ref[...] += send
                keep_ref[...] += keep

    return pl.pallas_call(
        kernel,
        out_shape=[jax.ShapeDtypeStruct((rows, half), F32)] * 2,
        in_specs=[vmem_spec()] * 7 + [pl.BlockSpec(memory_space=pl.ANY)] + [vmem_spec()] * 3,
        out_specs=[vmem_spec()] * 2,
        scratch_shapes=[
            pltpu.VMEM((rows, half), BF16),
            pltpu.VMEM((count, states), BF16),
            pltpu.VMEM((rows, chunk), BF16),
            pltpu.VMEM((points, 2 * count), F32),
            pltpu.SemaphoreType.DMA,
        ],
        compiler_params=params(24),
        name="direct",
    )(proj_own, proj_other, *lines, screened, *raws)


def finish(psi, keep, got):
    states, count = psi.shape
    points = count // 4
    cols = keep.shape[1]

    def kernel(psi_ref, keep_ref, got_ref, out_ref, high, low):
        for k in range(4):
            here = slice(k * points, (k + 1) * points)
            there = slice(SIBLING[k] * points, (SIBLING[k] + 1) * points)
            back = keep_ref[here, :] + got_ref[there, :]
            top = back.astype(BF16)
            high[here, :] = top
            low[here, :] = (back - top.astype(F32)).astype(BF16)
        total = jnp.dot(psi_ref[...], high[...], preferred_element_type=F32)
        total += jnp.dot(psi_ref[...], low[...], preferred_element_type=F32)
        out_ref[...] = total.astype(BF16)

    return pl.pallas_call(
        kernel,
        out_shape=jax.ShapeDtypeStruct((states, cols), BF16),
        in_specs=[vmem_spec()] * 3,
        out_specs=vmem_spec(),
        scratch_shapes=[pltpu.VMEM((count, cols), BF16)] * 2,
        compiler_params=params(16),
        name="finish",
    )(psi, keep, got)


def shards(trial, psi_v, psi_c, screened):
    rows, states = trial.shape[1:]
    half = states // 2
    devices = lax.axis_size(TILE_VEC)
    zh = lax.axis_index("zh")
    width = screened.shape[1] // 2
    partner = across(psi_v)
    far = across(lax.dynamic_slice_in_dim(screened, (1 - zh) * width, width, 1).astype(BF16))
    near = lax.dynamic_slice_in_dim(screened, zh * width, width, 1).astype(BF16)
    block = psi_c[:, 0, :].T
    line = jnp.concatenate([block, shift(block, "x", 1), shift(block, "x", -1), shift(block, "x", 2)], 0)
    halves = trial[0].reshape(rows, 2, half).transpose(1, 0, 2)
    copies = jnp.broadcast_to(halves[None, :, None], (devices // 4, 2, 2, rows, half))
    copies, line, near, partner = lax.optimization_barrier((copies, line, near, partner))
    trial_half = exchange(copies.reshape(devices, rows, half), TILE_VEC).reshape(-1, half)
    behind, ahead = shift(line, "y", 1), shift(line, "y", -1)
    middle = line.shape[0] // 2
    beyond = [shift(behind[:middle], "y", 1), shift(ahead[middle:], "y", -1)]
    far, *_ = lax.optimization_barrier((far, behind, ahead))
    raws = [swap(near), far, swap(far)]
    lefts = [psi_v, swap(psi_v), partner, swap(partner)]
    proj_own, psi = project(trial_half, lefts)
    proj_own, beyond = lax.optimization_barrier((proj_own, beyond))
    proj_other = swap(proj_own)
    panel = [line, behind, ahead, *beyond]
    keep, send = direct(proj_own, proj_other, panel, screened, raws)
    got = swap(send)
    term = finish(psi, keep, got)
    parts = exchange(term.reshape(devices, rows, half), TILE_VEC)
    parts = parts.reshape(-1, 2, 2, rows, half).astype(F32)
    total = jnp.sum(parts, axis=(0, 2))
    return total.transpose(1, 0, 2).reshape(1, rows, states)


def solution(mesh):
    split = Mesh(
        mesh.devices.reshape(2, 4, 4, 2, mesh.shape["vec"]),
        TILE_VEC,
    )
    return jax.shard_map(
        shards,
        mesh=split,
        in_specs=(P(None, TILE_VEC, None), P(None, TILE), P(None, "zl", TILE), P(TILE, "zl")),
        out_specs=P(None, TILE_VEC, None),
        check_vma=False,
    )
```

time: 97.2 us -> 101 us (1.039)
  waiting for transfers between devices: 17.6 us -> 25.2 us
  starting transfers between devices: 36.1 us -> 31.1 us
  local copies, waits for them, and re-layouts: 6.26 us -> 10.8 us
  Pallas kernels: 9.87 us -> 6.62 us
    ppermute x7, waiting for transfers between devices: 9.62 us -> 18.8 us  [shift(): return lax.ppermute(value, axis, [(k, (k + by) % n) for k in range(n)])]
    ppermute x4 -> x6, starting transfers between devices: 12.3 us -> 3.96 us  [swap(): return lax.ppermute(value, 'core', [(0, 1), (1, 0)])]
    pallas_call x1 -> x0, Pallas kernels: 4.07 us -> none  [pack(): pl.pallas_call(kernel, grid=(steps,), out_shape=[jax.ShapeDtypeStruct((po...]
    unnamed x18 -> x30, local copies, waits for them, and re-layouts: 1.84 us -> 5.43 us
    ppermute x1 -> x2, starting transfers between devices: 3.68 us -> 6.82 us  [across(): return lax.ppermute(value, 'zh', [(0, 1), (1, 0)])]
    convert_element_type x0 -> x1, local copies, waits for them, and re-layouts: none -> 2.67 us  [shards(): lax.dynamic_slice_in_dim(screened, (1 - zh) * width, width, 1).astype(BF16)]
    all_to_all x1, starting transfers between devices: 8.95 us -> 10.9 us  [exchange(): return lax.all_to_all(value, axes, split_axis=0, concat_axis=0, tiled=True)]
    slice x2, local copies, waits for them, and re-layouts: 3.32 us -> 1.54 us  [shards(): beyond = [shift(behind[:middle], 'y', 1), shift(ahead[middle:], 'y', -1)]]
  transfers between devices with their start and end apart: 13 -> 16, of which waited for: 7 -> 6; matrix products, arithmetic and copies ran while one was open for 3% -> 5% of each run, Pallas kernels for 5% -> 1%
where the time goes in v14:
time: 101 us
  starting transfers between devices  31.1 us (31%)
  blocking collectives  25.4 us (25%)
  waiting for transfers between devices  25.2 us (25%)
  local copies, waits for them, and re-layouts  10.8 us (11%)
  Pallas kernels  6.62 us (7%)
  other arithmetic  1.65 us (2%)
    all_to_all x1, blocking collectives, exchange(): return lax.all_to_all(value, axes, split_axis=0, concat_axis=0, tiled=True)  25.4 us
    ppermute x7, waiting for transfers between devices, shift(): return lax.ppermute(value, axis, [(k, (k + by) % n) for k in range(n)])  18.8 us
    all_to_all x1, starting transfers between devices, exchange(): return lax.all_to_all(value, axes, split_axis=0, concat_axis=0, tiled=True)  10.9 us
    ppermute x7, starting transfers between devices, shift(): return lax.ppermute(value, axis, [(k, (k + by) % n) for k in range(n)])  9.47 us
    ppermute x2, starting transfers between devices, across(): return lax.ppermute(value, 'zh', [(0, 1), (1, 0)])  6.82 us
    unnamed x30, local copies, waits for them, and re-layouts  5.43 us
    pallas_call x1, Pallas kernels, direct(): pl.pallas_call(kernel, out_shape=[jax.ShapeDtypeStruct((rows, half), F32)...  4.54 us
    ppermute x6, starting transfers between devices, swap(): return lax.ppermute(value, 'core', [(0, 1), (1, 0)])  3.96 us
  transfers between devices with their start and end apart: 16, of which 6 were waited for; matrix products, arithmetic and copies ran while one was open for 5% of the time, Pallas kernels for 1%

profile of v14, /device:TPU:1, one launch (start us, length us, event | category | flops | bytes accessed | tf_op | source)
XLA Modules:
  0.0 100.9 jit_solution(10155414411499766939)
XLA Ops:
  0.0 3.6 %collective-permute-start.2 = (bf16[64,1024]{1,0:T(8,128)(2,1)}, bf16[64,1024]{1,0:T(8,128)(2,1)S(1)}, u32[]{:S(2)}, u32[]{:S(2)}) collective-permute-start(bf16[64,1024]{1,0:T(8,128)(2,1)} %bitcast.17), channel_id=1, source_target_pairs={{0,8},{4,12},{8,0},{12,4},{1,9},{5,13},{9,1},{13,5},{2,10},{6,14},... | collective-permute-start | bytes 393224 | tf_op jit(solution)/shard_map/ppermute | solution.py:19
  3.6 0.9 collective-permute-start.1
  5.0 3.6 %collective-permute-start.3 = (bf16[1024,128]{1,0:T(8,128)(2,1)}, bf16[1024,128]{1,0:T(8,128)(2,1)S(1)}, u32[]{:S(2)}, u32[]{:S(2)}) collective-permute-start(bf16[1024,128]{1,0:T(8,128)(2,1)} %refs_0_.1), channel_id=1, source_target_pairs={{0,64},{64,0},{1,65},{65,1},{2,66},{66,2},{3,67},{67,3},{4,68},{68... | collective-permute-start | bytes 786440 | tf_op jit(solution)/shard_map/ppermute | solution.py:31
  8.6 2.7 %dynamic-slice_convert_fusion = (bf16[128,2048]{1,0:T(8,128)(2,1)}, bf16[128,2048]{1,0:T(8,128)(2,1)}) fusion(f32[128,4096]{1,0:T(8,128)} %refs_5_.1, s32[]{:T(128)S(6)} %select_n.7, s32[]{:T(128)S(6)} %select_n.6), kind=kLoop, calls=%fused_computation.1 | loop fusion | bytes 2097160 | tf_op jit(solution)/shard_map/convert_element_type | solution.py:177
  11.3 0.8 pad_maximum_fusion.refs_0_
  12.2 1.8 %collective-permute-done.3.refs_2_ = bf16[1024,128]{1,0:T(8,128)(2,1)S(1)} collective-permute-done((bf16[1024,128]{1,0:T(8,128)(2,1)}, bf16[1024,128]{1,0:T(8,128)(2,1)S(1)}, u32[]{:S(2)}, u32[]{:S(2)}) %collective-permute-start.3) | collective-permute-done | bytes 262176 | tf_op jit(solution)/shard_map/ppermute | solution.py:31
  14.0 1.1 %broadcast_in_dim.2 = bf16[32,2,2,8,512]{4,3,2,1,0:T(8,128)(2,1)} broadcast(bf16[2,8,512]{2,1,0:T(8,128)(2,1)S(1)} %bitcast.21), dimensions={1,3,4} | broadcast | bytes 1064960 | tf_op jit(solution)/shard_map/broadcast_in_dim | solution.py:182
  15.1 10.9 %all-to-all-start = ((bf16[128,8,512]{2,1,0:T(8,128)(2,1)}), bf16[128,8,512]{2,1,0:T(8,128)(2,1)S(1)}, u32[]{:S(2)}, u32[]{:S(2)}) async-start(bf16[128,8,512]{2,1,0:T(8,128)(2,1)} %bitcast.5), calls=%async_computation | async-start | bytes 2097152 | tf_op jit(solution)/shard_map/all_to_all | solution.py:23
  25.9 2.7 %collective-permute-start.8 = (bf16[256,1024]{1,0:T(8,128)(2,1)}, bf16[256,1024]{1,0:T(8,128)(2,1)S(1)}, u32[]{:S(2)}, u32[]{:S(2)}) collective-permute-start(bf16[256,1024]{1,0:T(8,128)(2,1)} %pad_maximum_fusion.refs_0_), channel_id=1, source_target_pairs={{0,48},{16,0},{32,16},{48,32},{1,49},{17,1},{33,17},{49,33},{2,50}... | collective-permute-start | bytes 1572872 | tf_op jit(solution)/shard_map/ppermute | solution.py:19
  28.7 3.2 %collective-permute-start.12 = (bf16[128,2048]{1,0:T(8,128)(2,1)}, bf16[128,2048]{1,0:T(8,128)(2,1)}, u32[]{:S(2)}, u32[]{:S(2)}) collective-permute-start(bf16[128,2048]{1,0:T(8,128)(2,1)} %get-tuple-element.29), channel_id=1, source_target_pairs={{0,64},{64,0},{1,65},{65,1},{2,66},{66,2},{3,67},{67,3},{4,68},{68... | collective-permute-start | bytes 1572872 | tf_op jit(solution)/shard_map/ppermute | solution.py:31
  31.9 0.9 collective-permute-start.4
  32.8 17.1 %collective-permute-done.8.refs_2_ = bf16[256,1024]{1,0:T(8,128)(2,1)S(1)} collective-permute-done((bf16[256,1024]{1,0:T(8,128)(2,1)}, bf16[256,1024]{1,0:T(8,128)(2,1)S(1)}, u32[]{:S(2)}, u32[]{:S(2)}) %collective-permute-start.8) | collective-permute-done | bytes 524320 | tf_op jit(solution)/shard_map/ppermute | solution.py:19
  50.7 1.7 %collective-permute-start.9 = (bf16[128,1024]{1,0:T(8,128)(2,1)}, bf16[128,1024]{1,0:T(8,128)(2,1)}, u32[]{:S(2)}, u32[]{:S(2)}) collective-permute-start(bf16[128,1024]{1,0:T(8,128)(2,1)} %slice.9), channel_id=1, source_target_pairs={{0,48},{16,0},{32,16},{48,32},{1,49},{17,1},{33,17},{49,33},{2,50}... | collective-permute-start | bytes 786440 | tf_op jit(solution)/shard_map/ppermute | solution.py:19
  56.0 1.0 %copy-done.8 = bf16[1024,128]{1,0:T(8,128)(2,1)S(1)} copy-done((bf16[1024,128]{1,0:T(8,128)(2,1)S(1)}, bf16[1024,128]{1,0:T(8,128)(2,1)}, u32[]{:S(2)}) %copy-start.8) | copy-done | bytes 262168
  57.0 0.9 copy-done.10
  58.0 0.9 copy-done.12
  59.8 1.6 %collective-permute-done.7.refs_3_ = bf16[128,1024]{1,0:T(8,128)(2,1)} collective-permute-done((bf16[128,1024]{1,0:T(8,128)(2,1)}, bf16[128,1024]{1,0:T(8,128)(2,1)}, u32[]{:S(2)}, u32[]{:S(2)}) %collective-permute-start.7) | collective-permute-done | bytes 262176 | tf_op jit(solution)/shard_map/ppermute | solution.py:19
  61.4 2.0 %collective-permute-start.10 = (bf16[512,512]{1,0:T(8,128)(2,1)S(1)}, bf16[512,512]{1,0:T(8,128)(2,1)S(1)}, u32[]{:S(2)}, u32[]{:S(2)}) collective-permute-start(bf16[512,512]{1,0:T(8,128)(2,1)S(1)} %get-tuple-element.22.own_ref), channel_id=1, source_target_pairs={{0,2},{2,0},{1,3},{3,1},{4,6},{6,4},{5,7},{7,5},{8,10},{10,8},{9,1... | collective-permute-start | bytes 1572872 | tf_op jit(solution)/shard_map/ppermute | solution.py:27
  63.4 1.5 %collective-permute-done.10.other_ref = bf16[512,512]{1,0:T(8,128)(2,1)S(1)} collective-permute-done((bf16[512,512]{1,0:T(8,128)(2,1)S(1)}, bf16[512,512]{1,0:T(8,128)(2,1)S(1)}, u32[]{:S(2)}, u32[]{:S(2)}) %collective-permute-start.10) | collective-permute-done | bytes 524320 | tf_op jit(solution)/shard_map/ppermute | solution.py:27
  65.0 1.0 %copy-done.5 = bf16[256,1024]{1,0:T(8,128)(2,1)S(1)} copy-done((bf16[256,1024]{1,0:T(8,128)(2,1)S(1)}, bf16[256,1024]{1,0:T(8,128)(2,1)}, u32[]{:S(2)}) %copy-start.5) | copy-done | bytes 524312
  66.0 4.5 %direct.1 = (f32[512,512]{1,0:T(8,128)S(1)}, f32[512,512]{1,0:T(8,128)S(1)}) custom-call(bf16[512,512]{1,0:T(8,128)(2,1)S(1)} %get-tuple-element.22.own_ref, bf16[512,512]{1,0:T(8,128)(2,1)S(1)} %collective-permute-done.10.other_ref, bf16[256,1024]{1,0:T(8,128)(2,1)S(1)} %copy-done.1, bf16[256,1024]{1,0:T(8,128)(2,1)S(1)} %copy-done.5, ...), custom_call_target="tpu_custom_call" | custom-call | tf_op jit(solution)/shard_map/direct/pallas_call | solution.py:125
  71.0 2.3 %collective-permute-done.14.got_ref = f32[512,512]{1,0:T(8,128)S(1)} collective-permute-done((f32[512,512]{1,0:T(8,128)S(1)}, f32[512,512]{1,0:T(8,128)S(1)}, u32[]{:S(2)}, u32[]{:S(2)}) %collective-permute-start.14) | collective-permute-done | bytes 1048608 | tf_op jit(solution)/shard_map/ppermute | solution.py:27
  73.3 1.3 %finish.1 = bf16[1024,512]{1,0:T(8,128)(2,1)S(1)} custom-call(bf16[1024,512]{1,0:T(8,128)(2,1)S(1)} %get-tuple-element.19.psi_ref, f32[512,512]{1,0:T(8,128)S(1)} %get-tuple-element.27.keep_ref, f32[512,512]{1,0:T(8,128)S(1)} %collective-permute-done.14.got_ref), custom_call_target="tpu_custom_call" | custom-call | tf_op jit(solution)/shard_map/finish/pallas_call | solution.py:159
  74.6 25.4 %all_to_all.10 = bf16[128,8,512]{2,1,0:T(8,128)(2,1)S(1)} all-to-all(bf16[128,8,512]{2,1,0:T(8,128)(2,1)S(1)} %bitcast.15), channel_id=1, replica_groups=mesh['zh'=2,'y'=4,'x'=4,'core'=2,'zl'=2] {'zh','y','x','core','zl'}, dimensions={0} | all-to-all | bytes 2097152 | tf_op jit(solution)/shard_map/all_to_all | solution.py:23
  (48 shorter events, 7.1 us)
Async XLA Ops:
  0.0 11.3 %copy-start.13 = (bf16[1024,1,64]{0,2,1:T(8,128)(2,1)S(1)}, bf16[1024,1,64]{0,2,1:T(8,128)(2,1)}, u32[]{:S(2)}) copy-start(bf16[1024,1,64]{0,2,1:T(8,128)(2,1)} %param.6) | copy-start | bytes 393220
  0.0 14.0 %copy-start.14 = (bf16[1,8,1024]{2,1,0:T(8,128)(2,1)S(1)}, bf16[1,8,1024]{2,1,0:T(8,128)(2,1)}, u32[]{:S(2)}) copy-start(bf16[1,8,1024]{2,1,0:T(8,128)(2,1)} %param.4) | copy-start | bytes 49156
  0.0 11.3 %collective-permute-start.2 = (bf16[64,1024]{1,0:T(8,128)(2,1)}, bf16[64,1024]{1,0:T(8,128)(2,1)S(1)}, u32[]{:S(2)}, u32[]{:S(2)}) collective-permute-start(bf16[64,1024]{1,0:T(8,128)(2,1)} %bitcast.17), channel_id=1, source_target_pairs={{0,8},{4,12},{8,0},{12,4},{1,9},{5,13},{9,1},{13,5},{2,10},{6,14},... | collective-permute-start | bytes 393224 | tf_op jit(solution)/shard_map/ppermute | solution.py:19
  3.6 7.7 %collective-permute-start.1 = (bf16[64,1024]{1,0:T(8,128)(2,1)}, bf16[64,1024]{1,0:T(8,128)(2,1)S(1)}, u32[]{:S(2)}, u32[]{:S(2)}) collective-permute-start(bf16[64,1024]{1,0:T(8,128)(2,1)} %bitcast.18), channel_id=1, source_target_pairs={{0,12},{4,0},{8,4},{12,8},{1,13},{5,1},{9,5},{13,9},{2,14},{6,2},{... | collective-permute-start | bytes 393224 | tf_op jit(solution)/shard_map/ppermute | solution.py:19
  4.4 6.9 %collective-permute-start = (bf16[64,1024]{1,0:T(8,128)(2,1)}, bf16[64,1024]{1,0:T(8,128)(2,1)S(1)}, u32[]{:S(2)}, u32[]{:S(2)}) collective-permute-start(bf16[64,1024]{1,0:T(8,128)(2,1)} %bitcast.19), channel_id=1, source_target_pairs={{0,4},{4,8},{8,12},{12,0},{1,5},{5,9},{9,13},{13,1},{2,6},{6,10},{... | collective-permute-start | bytes 393224 | tf_op jit(solution)/shard_map/ppermute | solution.py:19
  5.0 8.9 %collective-permute-start.3 = (bf16[1024,128]{1,0:T(8,128)(2,1)}, bf16[1024,128]{1,0:T(8,128)(2,1)S(1)}, u32[]{:S(2)}, u32[]{:S(2)}) collective-permute-start(bf16[1024,128]{1,0:T(8,128)(2,1)} %refs_0_.1), channel_id=1, source_target_pairs={{0,64},{64,0},{1,65},{65,1},{2,66},{66,2},{3,67},{67,3},{4,68},{68... | collective-permute-start | bytes 786440 | tf_op jit(solution)/shard_map/ppermute | solution.py:31
  11.3 20.6 %copy-start.6 = (bf16[1024,128]{1,0:T(8,128)(2,1)S(1)}, bf16[1024,128]{1,0:T(8,128)(2,1)}, u32[]{:S(2)}) copy-start(bf16[1024,128]{1,0:T(8,128)(2,1)} %refs_0_.1) | copy-start | bytes 786436
  15.1 40.9 %all-to-all-start = ((bf16[128,8,512]{2,1,0:T(8,128)(2,1)}), bf16[128,8,512]{2,1,0:T(8,128)(2,1)S(1)}, u32[]{:S(2)}, u32[]{:S(2)}) async-start(bf16[128,8,512]{2,1,0:T(8,128)(2,1)} %bitcast.5), calls=%async_computation | async-start | bytes 2097152 | tf_op jit(solution)/shard_map/all_to_all | solution.py:23
  25.9 39.0 %copy-start = (f32[128,4096]{1,0:T(8,128)S(1)}, f32[128,4096]{1,0:T(8,128)}, u32[]{:S(2)}) copy-start(f32[128,4096]{1,0:T(8,128)} %refs_5_.1) | copy-start | bytes 6291460
  25.9 24.0 %collective-permute-start.8 = (bf16[256,1024]{1,0:T(8,128)(2,1)}, bf16[256,1024]{1,0:T(8,128)(2,1)S(1)}, u32[]{:S(2)}, u32[]{:S(2)}) collective-permute-start(bf16[256,1024]{1,0:T(8,128)(2,1)} %pad_maximum_fusion.refs_0_), channel_id=1, source_target_pairs={{0,48},{16,0},{32,16},{48,32},{1,49},{17,1},{33,17},{49,33},{2,50}... | collective-permute-start | bytes 1572872 | tf_op jit(solution)/shard_map/ppermute | solution.py:19
  28.7 23.7 %collective-permute-start.6 = (bf16[256,1024]{1,0:T(8,128)(2,1)}, bf16[256,1024]{1,0:T(8,128)(2,1)S(1)}, u32[]{:S(2)}, u32[]{:S(2)}) collective-permute-start(bf16[256,1024]{1,0:T(8,128)(2,1)} %pad_maximum_fusion.refs_0_), channel_id=1, source_target_pairs={{0,16},{16,32},{32,48},{48,0},{1,17},{17,33},{33,49},{49,1},{2,18}... | collective-permute-start | bytes 1572872 | tf_op jit(solution)/shard_map/ppermute | solution.py:19
  28.7 25.3 %collective-permute-start.12 = (bf16[128,2048]{1,0:T(8,128)(2,1)}, bf16[128,2048]{1,0:T(8,128)(2,1)}, u32[]{:S(2)}, u32[]{:S(2)}) collective-permute-start(bf16[128,2048]{1,0:T(8,128)(2,1)} %get-tuple-element.29), channel_id=1, source_target_pairs={{0,64},{64,0},{1,65},{65,1},{2,66},{66,2},{3,67},{67,3},{4,68},{68... | collective-permute-start | bytes 1572872 | tf_op jit(solution)/shard_map/ppermute | solution.py:31
  31.9 22.6 %collective-permute-start.4 = (bf16[1024,128]{1,0:T(8,128)(2,1)S(1)}, bf16[1024,128]{1,0:T(8,128)(2,1)S(1)}, u32[]{:S(2)}, u32[]{:S(2)}) collective-permute-start(bf16[1024,128]{1,0:T(8,128)(2,1)S(1)} %copy-done.6), channel_id=1, source_target_pairs={{0,2},{2,0},{1,3},{3,1},{4,6},{6,4},{5,7},{7,5},{8,10},{10,8},{9,1... | collective-permute-start | bytes 786440 | tf_op jit(solution)/shard_map/ppermute | solution.py:27
  32.8 22.4 %collective-permute-start.5 = (bf16[1024,128]{1,0:T(8,128)(2,1)}, bf16[1024,128]{1,0:T(8,128)(2,1)S(1)}, u32[]{:S(2)}, u32[]{:S(2)}) collective-permute-start(bf16[1024,128]{1,0:T(8,128)(2,1)} %copy-done.7), channel_id=1, source_target_pairs={{0,2},{2,0},{1,3},{3,1},{4,6},{6,4},{5,7},{7,5},{8,10},{10,8},{9,1... | collective-permute-start | bytes 786440 | tf_op jit(solution)/shard_map/ppermute | solution.py:27
  49.9 5.3 %copy-start.2 = (bf16[256,1024]{1,0:T(8,128)(2,1)}, bf16[256,1024]{1,0:T(8,128)(2,1)S(1)}, u32[]{:S(2)}) copy-start(bf16[256,1024]{1,0:T(8,128)(2,1)S(1)} %collective-permute-done.8.refs_2_) | copy-start | bytes 1572868
  50.7 9.1 %collective-permute-start.9 = (bf16[128,1024]{1,0:T(8,128)(2,1)}, bf16[128,1024]{1,0:T(8,128)(2,1)}, u32[]{:S(2)}, u32[]{:S(2)}) collective-permute-start(bf16[128,1024]{1,0:T(8,128)(2,1)} %slice.9), channel_id=1, source_target_pairs={{0,48},{16,0},{32,16},{48,32},{1,49},{17,1},{33,17},{49,33},{2,50}... | collective-permute-start | bytes 786440 | tf_op jit(solution)/shard_map/ppermute | solution.py:19
  52.4 2.8 %copy-start.4 = (bf16[256,1024]{1,0:T(8,128)(2,1)}, bf16[256,1024]{1,0:T(8,128)(2,1)S(1)}, u32[]{:S(2)}) copy-start(bf16[256,1024]{1,0:T(8,128)(2,1)S(1)} %collective-permute-done.6.refs_1_) | copy-start | bytes 1572868
  53.2 8.2 %collective-permute-start.7 = (bf16[128,1024]{1,0:T(8,128)(2,1)}, bf16[128,1024]{1,0:T(8,128)(2,1)}, u32[]{:S(2)}, u32[]{:S(2)}) collective-permute-start(bf16[128,1024]{1,0:T(8,128)(2,1)} %slice.8), channel_id=1, source_target_pairs={{0,16},{16,32},{32,48},{48,0},{1,17},{17,33},{33,49},{49,1},{2,18}... | collective-permute-start | bytes 786440 | tf_op jit(solution)/shard_map/ppermute | solution.py:19
  54.0 9.4 %collective-permute-start.11 = (bf16[128,2048]{1,0:T(8,128)(2,1)}, bf16[128,2048]{1,0:T(8,128)(2,1)}, u32[]{:S(2)}, u32[]{:S(2)}) collective-permute-start(bf16[128,2048]{1,0:T(8,128)(2,1)} %get-tuple-element.25), channel_id=1, source_target_pairs={{0,2},{2,0},{1,3},{3,1},{4,6},{6,4},{5,7},{7,5},{8,10},{10,8},{9,1... | collective-permute-start | bytes 1572872 | tf_op jit(solution)/shard_map/ppermute | solution.py:27
  55.2 8.2 %collective-permute-start.13 = (bf16[128,2048]{1,0:T(8,128)(2,1)}, bf16[128,2048]{1,0:T(8,128)(2,1)}, u32[]{:S(2)}, u32[]{:S(2)}) collective-permute-start(bf16[128,2048]{1,0:T(8,128)(2,1)} %collective-permute-done.12.refs_7_), channel_id=1, source_target_pairs={{0,2},{2,0},{1,3},{3,1},{4,6},{6,4},{5,7},{7,5},{8,10},{10,8},{9,1... | collective-permute-start | bytes 1572872 | tf_op jit(solution)/shard_map/ppermute | solution.py:27
  56.0 9.0 %copy-start.1 = (bf16[256,1024]{1,0:T(8,128)(2,1)S(1)}, bf16[256,1024]{1,0:T(8,128)(2,1)}, u32[]{:S(2)}) copy-start(bf16[256,1024]{1,0:T(8,128)(2,1)} %pad_maximum_fusion.refs_0_) | copy-start | bytes 1572868
  56.0 9.0 %copy-start.3 = (bf16[256,1024]{1,0:T(8,128)(2,1)S(1)}, bf16[256,1024]{1,0:T(8,128)(2,1)}, u32[]{:S(2)}) copy-start(bf16[256,1024]{1,0:T(8,128)(2,1)} %copy-done.2) | copy-start | bytes 1572868
  61.4 3.6 %collective-permute-start.10 = (bf16[512,512]{1,0:T(8,128)(2,1)S(1)}, bf16[512,512]{1,0:T(8,128)(2,1)S(1)}, u32[]{:S(2)}, u32[]{:S(2)}) collective-permute-start(bf16[512,512]{1,0:T(8,128)(2,1)S(1)} %get-tuple-element.22.own_ref), channel_id=1, source_target_pairs={{0,2},{2,0},{1,3},{3,1},{4,6},{6,4},{5,7},{7,5},{8,10},{10,8},{9,1... | collective-permute-start | bytes 1572872 | tf_op jit(solution)/shard_map/ppermute | solution.py:27
  70.6 2.8 %collective-permute-start.14 = (f32[512,512]{1,0:T(8,128)S(1)}, f32[512,512]{1,0:T(8,128)S(1)}, u32[]{:S(2)}, u32[]{:S(2)}) collective-permute-start(f32[512,512]{1,0:T(8,128)S(1)} %get-tuple-element.28), channel_id=1, source_target_pairs={{0,2},{2,0},{1,3},{3,1},{4,6},{6,4},{5,7},{7,5},{8,10},{10,8},{9,1... | collective-permute-start | bytes 3145736 | tf_op jit(solution)/shard_map/ppermute | solution.py:27
  (7 other events, 6.5 us)

commit v15 on v13

--- a/solution.py
+++ b/solution.py
@@ -83,7 +83,7 @@
             pl.BlockSpec((2, rows, width), lambda k: (0, k, 0)),
             pl.BlockSpec((3, rows, width), lambda k: (0, k, 0)),
         ],
-        compiler_params=params(58),
+        compiler_params=params(8),
         name="pack",
     )(screened, left)
 
@@ -126,13 +126,12 @@
     chunk = 512
 
     def kernel(own_ref, other_ref, *refs):
-        line_refs, scr_refs, (keep_ref, send_ref, proj, panel_ref) = refs[:5], refs[5:9], refs[9:]
+        line_refs, scr_refs, (keep_ref, send_ref, proj, panel_ref) = refs[:4], refs[4:8], refs[8:]
         y, x = lax.axis_index("y"), lax.axis_index("x")
         for k in range(16):
             at = lax.rem(y + STEPS[k // 4] + 4, 4) * 4 + lax.rem(x + STEPS[k % 4] + 4, 4)
-            ref, row = (line_refs[k // 4], k % 4) if k < 12 else (line_refs[k // 2 - 3], k % 2)
-            panel_ref[pl.ds(pl.multiple_of(at * block, block), block), :] = ref[
-                row * block : (row + 1) * block, :
+            panel_ref[pl.ds(pl.multiple_of(at * block, block), block), :] = line_refs[k // 4][
+                k % 4 * block : (k % 4 + 1) * block, :
             ]
         core = lax.axis_index("core")
         mine = pl.ds(pl.multiple_of(core * half, half), half)
@@ -168,7 +167,7 @@
     return pl.pallas_call(
         kernel,
         out_shape=[jax.ShapeDtypeStruct((rows, half), F32)] * 2,
-        in_specs=[vmem_spec()] * 11,
+        in_specs=[vmem_spec()] * 10,
         out_specs=[vmem_spec()] * 2,
         scratch_shapes=[pltpu.VMEM((rows, half), BF16), pltpu.VMEM((count, states), BF16)],
         compiler_params=params(24),
@@ -218,14 +217,12 @@
     near = swap(near)
     far = lax.ppermute(far, "zh", [(0, 1), (1, 0)])
     behind, ahead = shift(line, "y", 1), shift(line, "y", -1)
-    middle = line.shape[0] // 2
-    beyond = [shift(behind[:middle], "y", 1), shift(ahead[middle:], "y", -1)]
-    far, *_ = lax.optimization_barrier((far, behind, ahead))
+    opposite = shift(line, "y", 2)
+    far, *_ = lax.optimization_barrier((far, behind, ahead, opposite))
     passed = swap(far)
     proj_own, psi = project(trial_half, psi_v, near, far, passed)
-    proj_own, beyond = lax.optimization_barrier((proj_own, beyond))
     proj_other = swap(proj_own)
-    panel = [line, behind, ahead, *beyond]
+    panel = [line, behind, ahead, opposite]
     keep, send = direct(proj_own, proj_other, panel, own, [near, far, passed])
     got = swap(send)
     term = finish(psi, keep, got)

time: 97.2 us -> 93.8 us (0.965)
  starting transfers between devices: 36.1 us -> 23.6 us
  waiting for transfers between devices: 17.6 us -> 29.3 us
  Pallas kernels: 9.87 us -> 7.76 us
  blocking collectives: 26.1 us -> 24 us
  local copies, waits for them, and re-layouts: 6.26 us -> 7.95 us
    ppermute x7 -> x6, waiting for transfers between devices: 9.62 us -> 22.6 us  [shift(): return lax.ppermute(value, axis, [(k, (k + by) % n) for k in range(n)])]
    ppermute x4, starting transfers between devices: 12.3 us -> 2.58 us  [swap(): return lax.ppermute(value, 'core', [(0, 1), (1, 0)])]
    unnamed x18 -> x26, local copies, waits for them, and re-layouts: 1.84 us -> 6.81 us
    ppermute x1, waiting for transfers between devices: 4.16 us -> 0.01 us  [shards(): far = lax.ppermute(far, 'zh', [(0, 1), (1, 0)])]
    slice x2 -> x0, local copies, waits for them, and re-layouts: 3.32 us -> none  [shards(): beyond = [shift(behind[:middle], 'y', 1), shift(ahead[middle:], 'y', -1)]]
    ppermute x4, waiting for transfers between devices: 3.83 us -> 6.61 us  [swap(): return lax.ppermute(value, 'core', [(0, 1), (1, 0)])]
    all_to_all x1, blocking collectives: 26.1 us -> 24 us  [exchange(): return lax.all_to_all(value, axes, split_axis=0, concat_axis=0, tiled=True)]
    pallas_call x1, Pallas kernels: 4.07 us -> 1.95 us  [pack(): pl.pallas_call(kernel, grid=(steps,), out_shape=[jax.ShapeDtypeStruct((po...]
  transfers between devices with their start and end apart: 13 -> 12, of which waited for: 7 -> 6; matrix products, arithmetic and copies ran while one was open for 3% -> 0% of each run, Pallas kernels for 5% -> 2%
where the time goes in v15:
time: 93.8 us; the launch traced here: 93.5 us
  waiting for transfers between devices  29.3 us (31%)
  blocking collectives  24 us (26%)
  starting transfers between devices  23.6 us (25%)
  local copies, waits for them, and re-layouts  7.95 us (8%)
  Pallas kernels  7.76 us (8%)
    all_to_all x1, blocking collectives, exchange(): return lax.all_to_all(value, axes, split_axis=0, concat_axis=0, tiled=True)  24 us
    ppermute x6, waiting for transfers between devices, shift(): return lax.ppermute(value, axis, [(k, (k + by) % n) for k in range(n)])  22.6 us
    ppermute x6, starting transfers between devices, shift(): return lax.ppermute(value, axis, [(k, (k + by) % n) for k in range(n)])  9.42 us
    all_to_all x1, starting transfers between devices, exchange(): return lax.all_to_all(value, axes, split_axis=0, concat_axis=0, tiled=True)  8.01 us
    unnamed x26, local copies, waits for them, and re-layouts  6.81 us
    ppermute x4, waiting for transfers between devices, swap(): return lax.ppermute(value, 'core', [(0, 1), (1, 0)])  6.61 us
    pallas_call x1, Pallas kernels, direct(): pl.pallas_call(kernel, out_shape=[jax.ShapeDtypeStruct((rows, half), F32)...  3.72 us
    ppermute x1, starting transfers between devices, shards(): far = lax.ppermute(far, 'zh', [(0, 1), (1, 0)])  3.6 us
  transfers between devices with their start and end apart: 12, of which 6 were waited for; matrix products, arithmetic and copies ran while one was open for 0% of the time, Pallas kernels for 2%

profile of v15, /device:TPU:1, one launch (start us, length us, event | category | flops | bytes accessed | tf_op | source)
XLA Modules:
  0.0 93.5 jit_solution(15339759671671994172)
XLA Ops:
  0.0 3.6 %collective-permute-start.2 = (bf16[64,1024]{1,0:T(8,128)(2,1)}, bf16[64,1024]{1,0:T(8,128)(2,1)S(1)}, u32[]{:S(2)}, u32[]{:S(2)}) collective-permute-start(bf16[64,1024]{1,0:T(8,128)(2,1)} %bitcast.18), channel_id=1, source_target_pairs={{0,8},{4,12},{8,0},{12,4},{1,9},{5,13},{9,1},{13,5},{2,10},{6,14},... | collective-permute-start | bytes 393224 | tf_op jit(solution)/shard_map/ppermute | solution.py:19
  3.6 0.9 collective-permute-start.1
  5.0 1.6 %copy-done = f32[128,4096]{1,0:T(8,128)S(1)} copy-done((f32[128,4096]{1,0:T(8,128)S(1)}, f32[128,4096]{1,0:T(8,128)}, u32[]{:S(2)}) %copy-start) | copy-done | bytes 2097176
  6.6 0.9 %copy-done.4 = bf16[1024,128]{1,0:T(8,128)(2,1)S(1)} copy-done((bf16[1024,128]{1,0:T(8,128)(2,1)S(1)}, bf16[1024,128]{1,0:T(8,128)(2,1)}, u32[]{:S(2)}) %copy-start.4) | copy-done | bytes 262168
  7.6 2.0 %pack.1 = (f32[128,1024]{1,0:T(8,128)S(1)}, bf16[2,128,1024]{2,1,0:T(8,128)(2,1)S(1)}, bf16[3,128,1024]{2,1,0:T(8,128)(2,1)}) custom-call(f32[128,4096]{1,0:T(8,128)S(1)} %copy-done, bf16[1024,128]{1,0:T(8,128)(2,1)S(1)} %copy-done.4), custom_call_target="tpu_custom_call" | custom-call | tf_op jit(solution)/shard_map/pack/pallas_call | solution.py:69
  9.5 0.8 copy-done.6
  10.3 0.8 copy-done.10
  11.2 1.1 %broadcast_in_dim.2 = bf16[32,2,2,8,512]{4,3,2,1,0:T(8,128)(2,1)} broadcast(bf16[2,8,512]{2,1,0:T(8,128)(2,1)S(1)} %bitcast.22), dimensions={1,3,4} | broadcast | bytes 1064960 | tf_op jit(solution)/shard_map/broadcast_in_dim | solution.py:214
  12.4 3.6 %collective-permute-start.4 = (bf16[3,128,1024]{2,1,0:T(8,128)(2,1)}, bf16[3,128,1024]{2,1,0:T(8,128)(2,1)S(1)}, u32[]{:S(2)}, u32[]{:S(2)}) collective-permute-start(bf16[3,128,1024]{2,1,0:T(8,128)(2,1)} %get-tuple-element.21), channel_id=1, source_target_pairs={{0,64},{64,0},{1,65},{65,1},{2,66},{66,2},{3,67},{67,3},{4,68},{68... | collective-permute-start | bytes 2359304 | tf_op jit(solution)/shard_map/ppermute | solution.py:218
  16.0 2.9 %collective-permute-start.7 = (bf16[256,1024]{1,0:T(8,128)(2,1)S(1)}, bf16[256,1024]{1,0:T(8,128)(2,1)S(1)}, u32[]{:S(2)}, u32[]{:S(2)}) collective-permute-start(bf16[256,1024]{1,0:T(8,128)(2,1)S(1)} %pad_maximum_fusion.refs_0_), channel_id=1, source_target_pairs={{0,32},{16,48},{32,0},{48,16},{1,33},{17,49},{33,1},{49,17},{2,34}... | collective-permute-start | bytes 1572872 | tf_op jit(solution)/shard_map/ppermute | solution.py:19
  20.4 8.0 %all-to-all-start = ((bf16[128,8,512]{2,1,0:T(8,128)(2,1)}), bf16[128,8,512]{2,1,0:T(8,128)(2,1)S(1)}, u32[]{:S(2)}, u32[]{:S(2)}) async-start(bf16[128,8,512]{2,1,0:T(8,128)(2,1)} %bitcast.16), calls=%async_computation | async-start | bytes 2097152 | tf_op jit(solution)/shard_map/all_to_all | solution.py:23
  29.9 20.9 %collective-permute-done.6.refs_2_ = bf16[256,1024]{1,0:T(8,128)(2,1)} collective-permute-done((bf16[256,1024]{1,0:T(8,128)(2,1)S(1)}, bf16[256,1024]{1,0:T(8,128)(2,1)}, u32[]{:S(2)}, u32[]{:S(2)}) %collective-permute-start.6) | collective-permute-done | bytes 524320 | tf_op jit(solution)/shard_map/ppermute | solution.py:19
  50.9 0.9 collective-permute-done.5.refs_1_
  51.8 1.6 %collective-permute-start.8 = (bf16[3,128,1024]{2,1,0:T(8,128)(2,1)S(1)}, bf16[3,128,1024]{2,1,0:T(8,128)(2,1)S(1)}, u32[]{:S(2)}, u32[]{:S(2)}) collective-permute-start(bf16[3,128,1024]{2,1,0:T(8,128)(2,1)S(1)} %collective-permute-done.4.refs_1_.refs_6_), channel_id=1, source_target_pairs={{0,2},{2,0},{1,3},{3,1},{4,6},{6,4},{5,7},{7,5},{8,10},{10,8},{9,1... | collective-permute-start | bytes 2359304 | tf_op jit(solution)/shard_map/ppermute | solution.py:27
  53.5 2.8 %collective-permute-done.3.refs_0_.refs_5_ = bf16[2,128,1024]{2,1,0:T(8,128)(2,1)S(1)} collective-permute-done((bf16[2,128,1024]{2,1,0:T(8,128)(2,1)}, bf16[2,128,1024]{2,1,0:T(8,128)(2,1)S(1)}, u32[]{:S(2)}, u32[]{:S(2)}) %collective-permute-start.3) | collective-permute-done | bytes 524320 | tf_op jit(solution)/shard_map/ppermute | solution.py:27
  56.3 0.8 copy-done.1
  57.1 1.0 %copy-done.2 = bf16[2,128,1024]{2,1,0:T(8,128)(2,1)S(1)} copy-done((bf16[2,128,1024]{2,1,0:T(8,128)(2,1)S(1)}, bf16[2,128,1024]{2,1,0:T(8,128)(2,1)}, u32[]{:S(2)}) %copy-start.2) | copy-done | bytes 524312
  58.1 0.8 project.1
  59.4 1.5 %collective-permute-done.9.other_ref = bf16[512,512]{1,0:T(8,128)(2,1)S(1)} collective-permute-done((bf16[512,512]{1,0:T(8,128)(2,1)S(1)}, bf16[512,512]{1,0:T(8,128)(2,1)S(1)}, u32[]{:S(2)}, u32[]{:S(2)}) %collective-permute-start.9) | collective-permute-done | bytes 524320 | tf_op jit(solution)/shard_map/ppermute | solution.py:27
  60.9 3.7 %direct.1 = (f32[512,512]{1,0:T(8,128)S(1)}, f32[512,512]{1,0:T(8,128)S(1)}) custom-call(bf16[512,512]{1,0:T(8,128)(2,1)S(1)} %get-tuple-element.25.own_ref, bf16[512,512]{1,0:T(8,128)(2,1)S(1)} %collective-permute-done.9.other_ref, bf16[256,1024]{1,0:T(8,128)(2,1)S(1)} %pad_maximum_fusion.refs_0_, bf16[256,1024]{1,0:T(8,128)(2,1)} %collective-permute-done.5.refs_1_, ...), custom_call_target="tpu_custom_call" | custom-call | tf_op jit(solution)/shard_map/direct/pallas_call | solution.py:167
  65.1 2.3 %collective-permute-done.10.got_ref = f32[512,512]{1,0:T(8,128)S(1)} collective-permute-done((f32[512,512]{1,0:T(8,128)S(1)}, f32[512,512]{1,0:T(8,128)S(1)}, u32[]{:S(2)}, u32[]{:S(2)}) %collective-permute-start.10) | collective-permute-done | bytes 1048608 | tf_op jit(solution)/shard_map/ppermute | solution.py:27
  67.4 1.3 %finish.1 = bf16[1024,512]{1,0:T(8,128)(2,1)S(1)} custom-call(bf16[1024,512]{1,0:T(8,128)(2,1)S(1)} %get-tuple-element.24.psi_ref, f32[512,512]{1,0:T(8,128)S(1)} %get-tuple-element.27.keep_ref, f32[512,512]{1,0:T(8,128)S(1)} %collective-permute-done.10.got_ref), custom_call_target="tpu_custom_call" | custom-call | tf_op jit(solution)/shard_map/finish/pallas_call | solution.py:195
  68.7 24.0 %all_to_all.10 = bf16[128,8,512]{2,1,0:T(8,128)(2,1)S(1)} all-to-all(bf16[128,8,512]{2,1,0:T(8,128)(2,1)S(1)} %bitcast.15), channel_id=1, replica_groups=mesh['zh'=2,'y'=4,'x'=4,'core'=2,'zl'=2] {'zh','y','x','core','zl'}, dimensions={0} | all-to-all | bytes 2097152 | tf_op jit(solution)/shard_map/all_to_all | solution.py:23
  92.7 0.8 convert_reduce_fusion
  (34 shorter events, 4.7 us)
Async XLA Ops:
  0.0 11.2 %collective-permute-start.2 = (bf16[64,1024]{1,0:T(8,128)(2,1)}, bf16[64,1024]{1,0:T(8,128)(2,1)S(1)}, u32[]{:S(2)}, u32[]{:S(2)}) collective-permute-start(bf16[64,1024]{1,0:T(8,128)(2,1)} %bitcast.18), channel_id=1, source_target_pairs={{0,8},{4,12},{8,0},{12,4},{1,9},{5,13},{9,1},{13,5},{2,10},{6,14},... | collective-permute-start | bytes 393224 | tf_op jit(solution)/shard_map/ppermute | solution.py:19
  3.6 7.6 %collective-permute-start.1 = (bf16[64,1024]{1,0:T(8,128)(2,1)}, bf16[64,1024]{1,0:T(8,128)(2,1)S(1)}, u32[]{:S(2)}, u32[]{:S(2)}) collective-permute-start(bf16[64,1024]{1,0:T(8,128)(2,1)} %bitcast.19), channel_id=1, source_target_pairs={{0,12},{4,0},{8,4},{12,8},{1,13},{5,1},{9,5},{13,9},{2,14},{6,2},{... | collective-permute-start | bytes 393224 | tf_op jit(solution)/shard_map/ppermute | solution.py:19
  4.4 6.7 %collective-permute-start = (bf16[64,1024]{1,0:T(8,128)(2,1)}, bf16[64,1024]{1,0:T(8,128)(2,1)S(1)}, u32[]{:S(2)}, u32[]{:S(2)}) collective-permute-start(bf16[64,1024]{1,0:T(8,128)(2,1)} %bitcast.20), channel_id=1, source_target_pairs={{0,4},{4,8},{8,12},{12,0},{1,5},{5,9},{9,13},{13,1},{2,6},{6,10},{... | collective-permute-start | bytes 393224 | tf_op jit(solution)/shard_map/ppermute | solution.py:19
  5.0 1.6 %copy-start = (f32[128,4096]{1,0:T(8,128)S(1)}, f32[128,4096]{1,0:T(8,128)}, u32[]{:S(2)}) copy-start(f32[128,4096]{1,0:T(8,128)} %in_ref.1) | copy-start | bytes 6291460
  6.6 0.9 %copy-start.4 = (bf16[1024,128]{1,0:T(8,128)(2,1)S(1)}, bf16[1024,128]{1,0:T(8,128)(2,1)}, u32[]{:S(2)}) copy-start(bf16[1024,128]{1,0:T(8,128)(2,1)} %left_ref.3) | copy-start | bytes 786436
  7.6 3.6 %copy-start.11 = (bf16[1024,1,64]{0,2,1:T(8,128)(2,1)S(1)}, bf16[1024,1,64]{0,2,1:T(8,128)(2,1)}, u32[]{:S(2)}) copy-start(bf16[1024,1,64]{0,2,1:T(8,128)(2,1)} %param.6) | copy-start | bytes 393220
  7.6 3.6 %copy-start.12 = (bf16[1,8,1024]{2,1,0:T(8,128)(2,1)S(1)}, bf16[1,8,1024]{2,1,0:T(8,128)(2,1)}, u32[]{:S(2)}) copy-start(bf16[1,8,1024]{2,1,0:T(8,128)(2,1)} %param.4) | copy-start | bytes 49156
  9.5 0.8 copy-start.6
  10.3 0.8 copy-start.10
  11.1 45.9 %copy-start.5 = (bf16[1024,128]{1,0:T(8,128)(2,1)S(1)}, bf16[1024,128]{1,0:T(8,128)(2,1)}, u32[]{:S(2)}) copy-start(bf16[1024,128]{1,0:T(8,128)(2,1)} %left_ref.3) | copy-start | bytes 786436
  12.4 39.4 %collective-permute-start.4 = (bf16[3,128,1024]{2,1,0:T(8,128)(2,1)}, bf16[3,128,1024]{2,1,0:T(8,128)(2,1)S(1)}, u32[]{:S(2)}, u32[]{:S(2)}) collective-permute-start(bf16[3,128,1024]{2,1,0:T(8,128)(2,1)} %get-tuple-element.21), channel_id=1, source_target_pairs={{0,64},{64,0},{1,65},{65,1},{2,66},{66,2},{3,67},{67,3},{4,68},{68... | collective-permute-start | bytes 2359304 | tf_op jit(solution)/shard_map/ppermute | solution.py:218
  16.0 13.2 %collective-permute-start.7 = (bf16[256,1024]{1,0:T(8,128)(2,1)S(1)}, bf16[256,1024]{1,0:T(8,128)(2,1)S(1)}, u32[]{:S(2)}, u32[]{:S(2)}) collective-permute-start(bf16[256,1024]{1,0:T(8,128)(2,1)S(1)} %pad_maximum_fusion.refs_0_), channel_id=1, source_target_pairs={{0,32},{16,48},{32,0},{48,16},{1,33},{17,49},{33,1},{49,17},{2,34}... | collective-permute-start | bytes 1572872 | tf_op jit(solution)/shard_map/ppermute | solution.py:19
  18.9 32.0 %collective-permute-start.6 = (bf16[256,1024]{1,0:T(8,128)(2,1)S(1)}, bf16[256,1024]{1,0:T(8,128)(2,1)}, u32[]{:S(2)}, u32[]{:S(2)}) collective-permute-start(bf16[256,1024]{1,0:T(8,128)(2,1)S(1)} %pad_maximum_fusion.refs_0_), channel_id=1, source_target_pairs={{0,48},{16,0},{32,16},{48,32},{1,49},{17,1},{33,17},{49,33},{2,50}... | collective-permute-start | bytes 1572872 | tf_op jit(solution)/shard_map/ppermute | solution.py:19
  19.7 32.1 %collective-permute-start.5 = (bf16[256,1024]{1,0:T(8,128)(2,1)S(1)}, bf16[256,1024]{1,0:T(8,128)(2,1)}, u32[]{:S(2)}, u32[]{:S(2)}) collective-permute-start(bf16[256,1024]{1,0:T(8,128)(2,1)S(1)} %pad_maximum_fusion.refs_0_), channel_id=1, source_target_pairs={{0,16},{16,32},{32,48},{48,0},{1,17},{17,33},{33,49},{49,1},{2,18}... | collective-permute-start | bytes 1572872 | tf_op jit(solution)/shard_map/ppermute | solution.py:19
  20.4 36.7 %all-to-all-start = ((bf16[128,8,512]{2,1,0:T(8,128)(2,1)}), bf16[128,8,512]{2,1,0:T(8,128)(2,1)S(1)}, u32[]{:S(2)}, u32[]{:S(2)}) async-start(bf16[128,8,512]{2,1,0:T(8,128)(2,1)} %bitcast.16), calls=%async_computation | async-start | bytes 2097152 | tf_op jit(solution)/shard_map/all_to_all | solution.py:23
  51.8 5.3 %collective-permute-start.8 = (bf16[3,128,1024]{2,1,0:T(8,128)(2,1)S(1)}, bf16[3,128,1024]{2,1,0:T(8,128)(2,1)S(1)}, u32[]{:S(2)}, u32[]{:S(2)}) collective-permute-start(bf16[3,128,1024]{2,1,0:T(8,128)(2,1)S(1)} %collective-permute-done.4.refs_1_.refs_6_), channel_id=1, source_target_pairs={{0,2},{2,0},{1,3},{3,1},{4,6},{6,4},{5,7},{7,5},{8,10},{10,8},{9,1... | collective-permute-start | bytes 2359304 | tf_op jit(solution)/shard_map/ppermute | solution.py:27
  53.4 2.9 %collective-permute-start.3 = (bf16[2,128,1024]{2,1,0:T(8,128)(2,1)}, bf16[2,128,1024]{2,1,0:T(8,128)(2,1)S(1)}, u32[]{:S(2)}, u32[]{:S(2)}) collective-permute-start(bf16[2,128,1024]{2,1,0:T(8,128)(2,1)} %copy-done.10), channel_id=1, source_target_pairs={{0,2},{2,0},{1,3},{3,1},{4,6},{6,4},{5,7},{7,5},{8,10},{10,8},{9,1... | collective-permute-start | bytes 1572872 | tf_op jit(solution)/shard_map/ppermute | solution.py:27
  56.3 0.8 copy-start.1
  57.1 1.0 %copy-start.2 = (bf16[2,128,1024]{2,1,0:T(8,128)(2,1)S(1)}, bf16[2,128,1024]{2,1,0:T(8,128)(2,1)}, u32[]{:S(2)}) copy-start(bf16[2,128,1024]{2,1,0:T(8,128)(2,1)} %copy-done.1) | copy-start | bytes 1572868
  58.1 2.8 %copy-start.3 = (bf16[2,128,1024]{2,1,0:T(8,128)(2,1)S(1)}, bf16[2,128,1024]{2,1,0:T(8,128)(2,1)}, u32[]{:S(2)}) copy-start(bf16[2,128,1024]{2,1,0:T(8,128)(2,1)} %copy-done.1) | copy-start | bytes 1572868
  58.1 2.8 %copy-start.7 = (f32[128,1024]{1,0:T(8,128)S(1)}, f32[128,1024]{1,0:T(8,128)}, u32[]{:S(2)}) copy-start(f32[128,1024]{1,0:T(8,128)} %copy-done.6) | copy-start | bytes 1572868
  58.1 2.8 %copy-start.9 = (bf16[256,1024]{1,0:T(8,128)(2,1)S(1)}, bf16[256,1024]{1,0:T(8,128)(2,1)}, u32[]{:S(2)}) copy-start(bf16[256,1024]{1,0:T(8,128)(2,1)} %copy-done.8) | copy-start | bytes 1572868
  58.9 2.0 %collective-permute-start.9 = (bf16[512,512]{1,0:T(8,128)(2,1)S(1)}, bf16[512,512]{1,0:T(8,128)(2,1)S(1)}, u32[]{:S(2)}, u32[]{:S(2)}) collective-permute-start(bf16[512,512]{1,0:T(8,128)(2,1)S(1)} %get-tuple-element.25.own_ref), channel_id=1, source_target_pairs={{0,2},{2,0},{1,3},{3,1},{4,6},{6,4},{5,7},{7,5},{8,10},{10,8},{9,1... | collective-permute-start | bytes 1572872 | tf_op jit(solution)/shard_map/ppermute | solution.py:27
  64.7 2.7 %collective-permute-start.10 = (f32[512,512]{1,0:T(8,128)S(1)}, f32[512,512]{1,0:T(8,128)S(1)}, u32[]{:S(2)}, u32[]{:S(2)}) collective-permute-start(f32[512,512]{1,0:T(8,128)S(1)} %get-tuple-element.28), channel_id=1, source_target_pairs={{0,2},{2,0},{1,3},{3,1},{4,6},{6,4},{5,7},{7,5},{8,10},{10,8},{9,1... | collective-permute-start | bytes 3145736 | tf_op jit(solution)/shard_map/ppermute | solution.py:27
  (1 other events, 0.8 us)

commit v16 on v10

--- a/solution.py
+++ b/solution.py
@@ -244,12 +244,11 @@
     mine = lax.dynamic_slice_in_dim(level, core * half, half, 1)
     sent = lax.dynamic_slice_in_dim(level, (1 - core) * half, half, 1)
     pieces = jnp.concatenate([mine, swap(sent)], 0)
-    pieces, near = lax.optimization_barrier((pieces, near))
+    pieces, near, behind, ahead = lax.optimization_barrier((pieces, near, behind, ahead))
     rounds = [pieces, ring(pieces, 1), ring(pieces, -1), ring(pieces, 2)]
     far, _ = lax.optimization_barrier((far, pieces))
     passed = swap(far[1:])
     middle = line.shape[0] // 2
-    behind, ahead, passed = lax.optimization_barrier((behind, ahead, passed))
     beyond = [shift(behind[:middle], "y", 1), shift(ahead[middle:], "y", -1)]
     rounds, beyond = lax.optimization_barrier((rounds, beyond))
     proj_own, psi = project(rounds, left, near, far, passed)

time: 92 us -> 93.3 us (1.014)
  waiting for transfers between devices: 26.7 us -> 25.1 us
  blocking collectives: 23 us -> 24.5 us
  starting transfers between devices: 30.3 us -> 31.6 us
  Pallas kernels: 5.57 us -> 6.73 us
  local copies, waits for them, and re-layouts: 5.17 us -> 4.2 us
    all_to_all x1, waiting for transfers between devices: 6.41 us -> 3.3 us  [exchange(): return lax.all_to_all(value, axes, split_axis=0, concat_axis=0, tiled=True)]
    all_to_all x1, blocking collectives: 23 us -> 24.5 us  [exchange(): return lax.all_to_all(value, axes, split_axis=0, concat_axis=0, tiled=True)]
    ppermute x7, starting transfers between devices: 8.05 us -> 9.46 us  [shift(): return lax.ppermute(value, axis, [(k, (k + by) % n) for k in range(n)])]
    pallas_call x1, Pallas kernels: 0.89 us -> 2.05 us  [pack(): pl.pallas_call(kernel, grid=(steps,), out_shape=[jax.ShapeDtypeStruct((po...]
    ppermute x5, waiting for transfers between devices: 3.83 us -> 4.82 us  [swap(): return lax.ppermute(value, 'core', [(0, 1), (1, 0)])]
    dynamic_slice x1, local copies, waits for them, and re-layouts: 0.99 us -> 0.02 us  [shards(): mine = lax.dynamic_slice_in_dim(level, core * half, half, 1)]
    unnamed x8 -> x10, local copies, waits for them, and re-layouts: 2.39 us -> 2.39 us
  transfers between devices with their start and end apart: 17 -> 17, of which waited for: 8 -> 11; matrix products, arithmetic and copies ran while one was open for 2% -> 1% of each run, Pallas kernels for 1% -> 2%
where the time goes in v16:
time: 93.3 us; the launch traced here: 93.1 us
  starting transfers between devices  31.6 us (34%)
  waiting for transfers between devices  25.1 us (27%)
  blocking collectives  24.5 us (26%)
  Pallas kernels  6.73 us (7%)
  local copies, waits for them, and re-layouts  4.2 us (5%)
    all_to_all x1, blocking collectives, exchange(): return lax.all_to_all(value, axes, split_axis=0, concat_axis=0, tiled=True)  24.5 us
    ppermute x7, waiting for transfers between devices, shift(): return lax.ppermute(value, axis, [(k, (k + by) % n) for k in range(n)])  12.2 us
    ppermute x7, starting transfers between devices, shift(): return lax.ppermute(value, axis, [(k, (k + by) % n) for k in range(n)])  9.46 us
    ppermute x5, starting transfers between devices, swap(): return lax.ppermute(value, 'core', [(0, 1), (1, 0)])  7.9 us
    all_to_all x1, starting transfers between devices, exchange(): return lax.all_to_all(value, axes, split_axis=0, concat_axis=0, tiled=True)  6.8 us
    ppermute x5, waiting for transfers between devices, swap(): return lax.ppermute(value, 'core', [(0, 1), (1, 0)])  4.82 us
    ppermute x3, waiting for transfers between devices, ring(): lax.ppermute(value, ('zh', 'zl'), [(k, (k + by) % 4) for k in range(4)])  4.75 us
    ppermute x3, starting transfers between devices, ring(): lax.ppermute(value, ('zh', 'zl'), [(k, (k + by) % 4) for k in range(4)])  3.88 us
  transfers between devices with their start and end apart: 17, of which 11 were waited for; matrix products, arithmetic and copies ran while one was open for 1% of the time, Pallas kernels for 2%

profile of v16, /device:TPU:1, one launch (start us, length us, event | category | flops | bytes accessed | tf_op | source)
XLA Modules:
  0.0 93.1 jit_solution(1034319664646374579)
XLA Ops:
  0.0 3.6 %collective-permute-start.2 = (bf16[64,1024]{1,0:T(8,128)(2,1)}, bf16[64,1024]{1,0:T(8,128)(2,1)S(1)}, u32[]{:S(2)}, u32[]{:S(2)}) collective-permute-start(bf16[64,1024]{1,0:T(8,128)(2,1)} %bitcast.21), channel_id=1, source_target_pairs={{0,8},{4,12},{8,0},{12,4},{1,9},{5,13},{9,1},{13,5},{2,10},{6,14},... | collective-permute-start | bytes 393224 | tf_op jit(solution)/shard_map/ppermute | solution.py:21
  5.0 1.0 %copy.5 = bf16[2,4,4,2,2,8,128]{6,5,2,1,4,3,0:T(8,128)(2,1)S(1)} copy(bf16[2,4,4,2,2,8,128]{6,5,4,3,2,1,0:T(8,128)(2,1)} %bitcast.20) | data formatting | bytes 524288 | tf_op jit(solution)/shard_map/reshape | solution.py:235
  6.1 1.6 %copy-done = f32[128,4096]{1,0:T(8,128)S(1)} copy-done((f32[128,4096]{1,0:T(8,128)S(1)}, f32[128,4096]{1,0:T(8,128)}, u32[]{:S(2)}) %copy-start) | copy-done | bytes 2097176
  7.6 2.1 %pack.1 = (f32[128,1024]{1,0:T(8,128)S(1)}, bf16[2,128,1024]{2,1,0:T(8,128)(2,1)}, bf16[3,128,1024]{2,1,0:T(8,128)(2,1)}) custom-call(f32[128,4096]{1,0:T(8,128)S(1)} %copy-done, bf16[1024,128]{1,0:T(8,128)(2,1)S(1)} %bitcast.16), custom_call_target="tpu_custom_call" | custom-call | tf_op jit(solution)/shard_map/pack/pallas_call | solution.py:71
  11.3 3.6 %collective-permute-start.12 = (bf16[3,128,1024]{2,1,0:T(8,128)(2,1)}, bf16[3,128,1024]{2,1,0:T(8,128)(2,1)S(1)}, u32[]{:S(2)}, u32[]{:S(2)}) collective-permute-start(bf16[3,128,1024]{2,1,0:T(8,128)(2,1)} %get-tuple-element.40), channel_id=1, source_target_pairs={{0,64},{64,0},{1,65},{65,1},{2,66},{66,2},{3,67},{67,3},{4,68},{68... | collective-permute-start | bytes 2359304 | tf_op jit(solution)/shard_map/ppermute | solution.py:242
  14.9 6.8 %all-to-all-start = ((bf16[16,8,1024]{2,1,0:T(8,128)(2,1)}), bf16[16,8,1024]{2,1,0:T(8,128)(2,1)S(1)}, u32[]{:S(2)}, u32[]{:S(2)}) async-start(bf16[16,8,1024]{2,1,0:T(8,128)(2,1)} %broadcast_in_dim.8), calls=%async_computation | async-start | bytes 524288 | tf_op jit(solution)/shard_map/all_to_all | solution.py:25
  21.7 1.4 %collective-permute-start.4 = (bf16[2,128,1024]{2,1,0:T(8,128)(2,1)}, bf16[2,128,1024]{2,1,0:T(8,128)(2,1)S(1)}, u32[]{:S(2)}, u32[]{:S(2)}) collective-permute-start(bf16[2,128,1024]{2,1,0:T(8,128)(2,1)} %get-tuple-element.30), channel_id=1, source_target_pairs={{0,2},{2,0},{1,3},{3,1},{4,6},{6,4},{5,7},{7,5},{8,10},{10,8},{9,1... | collective-permute-start | bytes 1572872 | tf_op jit(solution)/shard_map/ppermute | solution.py:29
  23.1 2.8 %collective-permute-start.6 = (bf16[256,1024]{1,0:T(8,128)(2,1)S(1)}, bf16[256,1024]{1,0:T(8,128)(2,1)S(1)}, u32[]{:S(2)}, u32[]{:S(2)}) collective-permute-start(bf16[256,1024]{1,0:T(8,128)(2,1)S(1)} %pad_maximum_fusion.refs_0_), channel_id=1, source_target_pairs={{0,48},{16,0},{32,16},{48,32},{1,49},{17,1},{33,17},{49,33},{2,50}... | collective-permute-start | bytes 1572872 | tf_op jit(solution)/shard_map/ppermute | solution.py:21
  25.9 3.3 %all-to-all-done = bf16[16,8,1024]{2,1,0:T(8,128)(2,1)S(1)} async-done(((bf16[16,8,1024]{2,1,0:T(8,128)(2,1)}), bf16[16,8,1024]{2,1,0:T(8,128)(2,1)S(1)}, u32[]{:S(2)}, u32[]{:S(2)}) %all-to-all-start) | async-done | bytes 262176 | tf_op jit(solution)/shard_map/all_to_all | solution.py:25
  29.3 2.6 %collective-permute-start.3 = (bf16[128,512]{1,0:T(8,128)(2,1)S(1)}, bf16[128,512]{1,0:T(8,128)(2,1)S(1)}, u32[]{:S(2)}, u32[]{:S(2)}) collective-permute-start(bf16[128,512]{1,0:T(8,128)(2,1)S(1)} %get-tuple-element.50), channel_id=1, source_target_pairs={{0,2},{2,0},{1,3},{3,1},{4,6},{6,4},{5,7},{7,5},{8,10},{10,8},{9,1... | collective-permute-start | bytes 393224 | tf_op jit(solution)/shard_map/ppermute | solution.py:29
  32.9 6.1 %collective-permute-done.6.refs_2_ = bf16[256,1024]{1,0:T(8,128)(2,1)S(1)} collective-permute-done((bf16[256,1024]{1,0:T(8,128)(2,1)S(1)}, bf16[256,1024]{1,0:T(8,128)(2,1)S(1)}, u32[]{:S(2)}, u32[]{:S(2)}) %collective-permute-start.6) | collective-permute-done | bytes 524320 | tf_op jit(solution)/shard_map/ppermute | solution.py:21
  39.0 2.2 %collective-permute-done.5.refs_1_ = bf16[256,1024]{1,0:T(8,128)(2,1)S(1)} collective-permute-done((bf16[256,1024]{1,0:T(8,128)(2,1)S(1)}, bf16[256,1024]{1,0:T(8,128)(2,1)S(1)}, u32[]{:S(2)}, u32[]{:S(2)}) %collective-permute-start.5) | collective-permute-done | bytes 524320 | tf_op jit(solution)/shard_map/ppermute | solution.py:21
  41.7 1.2 %collective-permute-start.13 = (bf16[2,128,1024]{2,1,0:T(8,128)(2,1)S(1)}, bf16[2,128,1024]{2,1,0:T(8,128)(2,1)S(1)}, u32[]{:S(2)}, u32[]{:S(2)}) collective-permute-start(bf16[2,128,1024]{2,1,0:T(8,128)(2,1)S(1)} %slice.11), channel_id=1, source_target_pairs={{0,2},{2,0},{1,3},{3,1},{4,6},{6,4},{5,7},{7,5},{8,10},{10,8},{9,1... | collective-permute-start | bytes 1572872 | tf_op jit(solution)/shard_map/ppermute | solution.py:29
  42.9 1.2 %collective-permute-start.10 = (bf16[128,1024]{1,0:T(8,128)(2,1)S(1)}, bf16[128,1024]{1,0:T(8,128)(2,1)S(1)}, u32[]{:S(2)}, u32[]{:S(2)}) collective-permute-start(bf16[128,1024]{1,0:T(8,128)(2,1)S(1)} %slice.9), channel_id=1, source_target_pairs={{0,16},{16,32},{32,48},{48,0},{1,17},{17,33},{33,49},{49,1},{2,18}... | collective-permute-start | bytes 786440 | tf_op jit(solution)/shard_map/ppermute | solution.py:21
  44.1 3.1 %collective-permute-start.8 = (bf16[256,512]{1,0:T(8,128)(2,1)S(1)}, bf16[256,512]{1,0:T(8,128)(2,1)S(1)}, u32[]{:S(2)}, u32[]{:S(2)}) collective-permute-start(bf16[256,512]{1,0:T(8,128)(2,1)S(1)} %pad_maximum_fusion.1.refs_0_), channel_id=1, source_target_pairs={{0,65},{1,0},{64,1},{65,64},{2,67},{3,2},{66,3},{67,66},{4,69},{5,... | collective-permute-start | bytes 786440 | tf_op jit(solution)/shard_map/ppermute | solution.py:222
  47.3 1.0 %collective-permute-done.11.refs_4_ = bf16[128,1024]{1,0:T(8,128)(2,1)S(1)} collective-permute-done((bf16[128,1024]{1,0:T(8,128)(2,1)S(1)}, bf16[128,1024]{1,0:T(8,128)(2,1)S(1)}, u32[]{:S(2)}, u32[]{:S(2)}) %collective-permute-start.11) | collective-permute-done | bytes 262176 | tf_op jit(solution)/shard_map/ppermute | solution.py:21
  49.0 2.8 %collective-permute-done.10.refs_3_ = bf16[128,1024]{1,0:T(8,128)(2,1)S(1)} collective-permute-done((bf16[128,1024]{1,0:T(8,128)(2,1)S(1)}, bf16[128,1024]{1,0:T(8,128)(2,1)S(1)}, u32[]{:S(2)}, u32[]{:S(2)}) %collective-permute-start.10) | collective-permute-done | bytes 262176 | tf_op jit(solution)/shard_map/ppermute | solution.py:21
  52.2 3.7 %collective-permute-done.8.refs_2_ = bf16[256,512]{1,0:T(8,128)(2,1)S(1)} collective-permute-done((bf16[256,512]{1,0:T(8,128)(2,1)S(1)}, bf16[256,512]{1,0:T(8,128)(2,1)S(1)}, u32[]{:S(2)}, u32[]{:S(2)}) %collective-permute-start.8) | collective-permute-done | bytes 262176 | tf_op jit(solution)/shard_map/ppermute | solution.py:222
  57.5 2.2 %collective-permute-start.14 = (bf16[512,512]{1,0:T(8,128)(2,1)S(1)}, bf16[512,512]{1,0:T(8,128)(2,1)S(1)}, u32[]{:S(2)}, u32[]{:S(2)}) collective-permute-start(bf16[512,512]{1,0:T(8,128)(2,1)S(1)} %get-tuple-element.43.own_ref), channel_id=1, source_target_pairs={{0,2},{2,0},{1,3},{3,1},{4,6},{6,4},{5,7},{7,5},{8,10},{10,8},{9,1... | collective-permute-start | bytes 1572872 | tf_op jit(solution)/shard_map/ppermute | solution.py:29
  59.7 1.5 %collective-permute-done.14.other_ref = bf16[512,512]{1,0:T(8,128)(2,1)S(1)} collective-permute-done((bf16[512,512]{1,0:T(8,128)(2,1)S(1)}, bf16[512,512]{1,0:T(8,128)(2,1)S(1)}, u32[]{:S(2)}, u32[]{:S(2)}) %collective-permute-start.14) | collective-permute-done | bytes 524320 | tf_op jit(solution)/shard_map/ppermute | solution.py:29
  61.2 2.5 %direct.1 = (f32[512,512]{1,0:T(8,128)S(1)}, f32[512,512]{1,0:T(8,128)S(1)}) custom-call(bf16[512,512]{1,0:T(8,128)(2,1)S(1)} %get-tuple-element.43.own_ref, bf16[512,512]{1,0:T(8,128)(2,1)S(1)} %collective-permute-done.14.other_ref, bf16[256,1024]{1,0:T(8,128)(2,1)S(1)} %pad_maximum_fusion.refs_0_, bf16[256,1024]{1,0:T(8,128)(2,1)S(1)} %collective-permute-done.5.refs_1_, ...), custom_call_target="tpu_custom_call" | custom-call | tf_op jit(solution)/shard_map/direct/pallas_call | solution.py:182
  64.2 2.3 %collective-permute-done.15.got_ref = f32[512,512]{1,0:T(8,128)S(1)} collective-permute-done((f32[512,512]{1,0:T(8,128)S(1)}, f32[512,512]{1,0:T(8,128)S(1)}, u32[]{:S(2)}, u32[]{:S(2)}) %collective-permute-start.15) | collective-permute-done | bytes 1048608 | tf_op jit(solution)/shard_map/ppermute | solution.py:29
  66.5 1.3 %finish.1 = bf16[1024,512]{1,0:T(8,128)(2,1)S(1)} custom-call(bf16[1024,512]{1,0:T(8,128)(2,1)S(1)} %get-tuple-element.42.psi_ref, f32[512,512]{1,0:T(8,128)S(1)} %get-tuple-element.47.keep_ref, f32[512,512]{1,0:T(8,128)S(1)} %collective-permute-done.15.got_ref), custom_call_target="tpu_custom_call" | custom-call | tf_op jit(solution)/shard_map/finish/pallas_call | solution.py:210
  67.8 24.5 %all_to_all.10 = bf16[128,8,512]{2,1,0:T(8,128)(2,1)S(1)} all-to-all(bf16[128,8,512]{2,1,0:T(8,128)(2,1)S(1)} %bitcast.15), channel_id=1, replica_groups=mesh['zh'=2,'y'=4,'x'=4,'core'=2,'zl'=2] {'zh','core','zl','y','x'}, dimensions={0} | all-to-all | bytes 2097152 | tf_op jit(solution)/shard_map/all_to_all | solution.py:25
  (34 shorter events, 8.5 us)
Async XLA Ops:
  0.0 10.5 %copy-start.3 = (bf16[1024,1,64]{0,2,1:T(8,128)(2,1)S(1)}, bf16[1024,1,64]{0,2,1:T(8,128)(2,1)}, u32[]{:S(2)}) copy-start(bf16[1024,1,64]{0,2,1:T(8,128)(2,1)} %param.6) | copy-start | bytes 393220
  0.0 10.6 %copy-start.4 = (bf16[1,8,1024]{2,1,0:T(8,128)(2,1)S(1)}, bf16[1,8,1024]{2,1,0:T(8,128)(2,1)}, u32[]{:S(2)}) copy-start(bf16[1,8,1024]{2,1,0:T(8,128)(2,1)} %param.4) | copy-start | bytes 49156
  0.0 10.5 %collective-permute-start.2 = (bf16[64,1024]{1,0:T(8,128)(2,1)}, bf16[64,1024]{1,0:T(8,128)(2,1)S(1)}, u32[]{:S(2)}, u32[]{:S(2)}) collective-permute-start(bf16[64,1024]{1,0:T(8,128)(2,1)} %bitcast.21), channel_id=1, source_target_pairs={{0,8},{4,12},{8,0},{12,4},{1,9},{5,13},{9,1},{13,5},{2,10},{6,14},... | collective-permute-start | bytes 393224 | tf_op jit(solution)/shard_map/ppermute | solution.py:21
  3.6 6.9 %collective-permute-start.1 = (bf16[64,1024]{1,0:T(8,128)(2,1)}, bf16[64,1024]{1,0:T(8,128)(2,1)S(1)}, u32[]{:S(2)}, u32[]{:S(2)}) collective-permute-start(bf16[64,1024]{1,0:T(8,128)(2,1)} %bitcast.22), channel_id=1, source_target_pairs={{0,12},{4,0},{8,4},{12,8},{1,13},{5,1},{9,5},{13,9},{2,14},{6,2},{... | collective-permute-start | bytes 393224 | tf_op jit(solution)/shard_map/ppermute | solution.py:21
  4.4 6.1 %collective-permute-start = (bf16[64,1024]{1,0:T(8,128)(2,1)}, bf16[64,1024]{1,0:T(8,128)(2,1)S(1)}, u32[]{:S(2)}, u32[]{:S(2)}) collective-permute-start(bf16[64,1024]{1,0:T(8,128)(2,1)} %bitcast.23), channel_id=1, source_target_pairs={{0,4},{4,8},{8,12},{12,0},{1,5},{5,9},{9,13},{13,1},{2,6},{6,10},{... | collective-permute-start | bytes 393224 | tf_op jit(solution)/shard_map/ppermute | solution.py:21
  6.0 1.6 %copy-start = (f32[128,4096]{1,0:T(8,128)S(1)}, f32[128,4096]{1,0:T(8,128)}, u32[]{:S(2)}) copy-start(f32[128,4096]{1,0:T(8,128)} %in_ref.1) | copy-start | bytes 6291460
  9.7 0.8 copy-start.1
  11.3 30.3 %collective-permute-start.12 = (bf16[3,128,1024]{2,1,0:T(8,128)(2,1)}, bf16[3,128,1024]{2,1,0:T(8,128)(2,1)S(1)}, u32[]{:S(2)}, u32[]{:S(2)}) collective-permute-start(bf16[3,128,1024]{2,1,0:T(8,128)(2,1)} %get-tuple-element.40), channel_id=1, source_target_pairs={{0,64},{64,0},{1,65},{65,1},{2,66},{66,2},{3,67},{67,3},{4,68},{68... | collective-permute-start | bytes 2359304 | tf_op jit(solution)/shard_map/ppermute | solution.py:242
  14.9 14.3 %all-to-all-start = ((bf16[16,8,1024]{2,1,0:T(8,128)(2,1)}), bf16[16,8,1024]{2,1,0:T(8,128)(2,1)S(1)}, u32[]{:S(2)}, u32[]{:S(2)}) async-start(bf16[16,8,1024]{2,1,0:T(8,128)(2,1)} %broadcast_in_dim.8), calls=%async_computation | async-start | bytes 524288 | tf_op jit(solution)/shard_map/all_to_all | solution.py:25
  21.7 11.2 %collective-permute-start.4 = (bf16[2,128,1024]{2,1,0:T(8,128)(2,1)}, bf16[2,128,1024]{2,1,0:T(8,128)(2,1)S(1)}, u32[]{:S(2)}, u32[]{:S(2)}) collective-permute-start(bf16[2,128,1024]{2,1,0:T(8,128)(2,1)} %get-tuple-element.30), channel_id=1, source_target_pairs={{0,2},{2,0},{1,3},{3,1},{4,6},{6,4},{5,7},{7,5},{8,10},{10,8},{9,1... | collective-permute-start | bytes 1572872 | tf_op jit(solution)/shard_map/ppermute | solution.py:29
  23.1 15.9 %collective-permute-start.6 = (bf16[256,1024]{1,0:T(8,128)(2,1)S(1)}, bf16[256,1024]{1,0:T(8,128)(2,1)S(1)}, u32[]{:S(2)}, u32[]{:S(2)}) collective-permute-start(bf16[256,1024]{1,0:T(8,128)(2,1)S(1)} %pad_maximum_fusion.refs_0_), channel_id=1, source_target_pairs={{0,48},{16,0},{32,16},{48,32},{1,49},{17,1},{33,17},{49,33},{2,50}... | collective-permute-start | bytes 1572872 | tf_op jit(solution)/shard_map/ppermute | solution.py:21
  25.9 15.3 %collective-permute-start.5 = (bf16[256,1024]{1,0:T(8,128)(2,1)S(1)}, bf16[256,1024]{1,0:T(8,128)(2,1)S(1)}, u32[]{:S(2)}, u32[]{:S(2)}) collective-permute-start(bf16[256,1024]{1,0:T(8,128)(2,1)S(1)} %pad_maximum_fusion.refs_0_), channel_id=1, source_target_pairs={{0,16},{16,32},{32,48},{48,0},{1,17},{17,33},{33,49},{49,1},{2,18}... | collective-permute-start | bytes 1572872 | tf_op jit(solution)/shard_map/ppermute | solution.py:21
  29.3 3.6 %collective-permute-start.3 = (bf16[128,512]{1,0:T(8,128)(2,1)S(1)}, bf16[128,512]{1,0:T(8,128)(2,1)S(1)}, u32[]{:S(2)}, u32[]{:S(2)}) collective-permute-start(bf16[128,512]{1,0:T(8,128)(2,1)S(1)} %get-tuple-element.50), channel_id=1, source_target_pairs={{0,2},{2,0},{1,3},{3,1},{4,6},{6,4},{5,7},{7,5},{8,10},{10,8},{9,1... | collective-permute-start | bytes 393224 | tf_op jit(solution)/shard_map/ppermute | solution.py:29
  41.2 7.1 %collective-permute-start.11 = (bf16[128,1024]{1,0:T(8,128)(2,1)S(1)}, bf16[128,1024]{1,0:T(8,128)(2,1)S(1)}, u32[]{:S(2)}, u32[]{:S(2)}) collective-permute-start(bf16[128,1024]{1,0:T(8,128)(2,1)S(1)} %slice.10), channel_id=1, source_target_pairs={{0,48},{16,0},{32,16},{48,32},{1,49},{17,1},{33,17},{49,33},{2,50}... | collective-permute-start | bytes 786440 | tf_op jit(solution)/shard_map/ppermute | solution.py:21
  41.7 19.6 %copy-start.2 = (f32[128,1024]{1,0:T(8,128)S(1)}, f32[128,1024]{1,0:T(8,128)}, u32[]{:S(2)}) copy-start(f32[128,1024]{1,0:T(8,128)} %copy-done.1) | copy-start | bytes 1572868
  41.7 14.9 %collective-permute-start.13 = (bf16[2,128,1024]{2,1,0:T(8,128)(2,1)S(1)}, bf16[2,128,1024]{2,1,0:T(8,128)(2,1)S(1)}, u32[]{:S(2)}, u32[]{:S(2)}) collective-permute-start(bf16[2,128,1024]{2,1,0:T(8,128)(2,1)S(1)} %slice.11), channel_id=1, source_target_pairs={{0,2},{2,0},{1,3},{3,1},{4,6},{6,4},{5,7},{7,5},{8,10},{10,8},{9,1... | collective-permute-start | bytes 1572872 | tf_op jit(solution)/shard_map/ppermute | solution.py:29
  42.9 9.4 %collective-permute-start.9 = (bf16[256,512]{1,0:T(8,128)(2,1)S(1)}, bf16[256,512]{1,0:T(8,128)(2,1)S(1)}, u32[]{:S(2)}, u32[]{:S(2)}) collective-permute-start(bf16[256,512]{1,0:T(8,128)(2,1)S(1)} %pad_maximum_fusion.1.refs_0_), channel_id=1, source_target_pairs={{0,64},{1,65},{64,0},{65,1},{2,66},{3,67},{66,2},{67,3},{4,68},{5,... | collective-permute-start | bytes 786440 | tf_op jit(solution)/shard_map/ppermute | solution.py:222
  42.9 8.9 %collective-permute-start.10 = (bf16[128,1024]{1,0:T(8,128)(2,1)S(1)}, bf16[128,1024]{1,0:T(8,128)(2,1)S(1)}, u32[]{:S(2)}, u32[]{:S(2)}) collective-permute-start(bf16[128,1024]{1,0:T(8,128)(2,1)S(1)} %slice.9), channel_id=1, source_target_pairs={{0,16},{16,32},{32,48},{48,0},{1,17},{17,33},{33,49},{49,1},{2,18}... | collective-permute-start | bytes 786440 | tf_op jit(solution)/shard_map/ppermute | solution.py:21
  44.1 11.8 %collective-permute-start.8 = (bf16[256,512]{1,0:T(8,128)(2,1)S(1)}, bf16[256,512]{1,0:T(8,128)(2,1)S(1)}, u32[]{:S(2)}, u32[]{:S(2)}) collective-permute-start(bf16[256,512]{1,0:T(8,128)(2,1)S(1)} %pad_maximum_fusion.1.refs_0_), channel_id=1, source_target_pairs={{0,65},{1,0},{64,1},{65,64},{2,67},{3,2},{66,3},{67,66},{4,69},{5,... | collective-permute-start | bytes 786440 | tf_op jit(solution)/shard_map/ppermute | solution.py:222
  48.3 8.3 %collective-permute-start.7 = (bf16[256,512]{1,0:T(8,128)(2,1)S(1)}, bf16[256,512]{1,0:T(8,128)(2,1)S(1)}, u32[]{:S(2)}, u32[]{:S(2)}) collective-permute-start(bf16[256,512]{1,0:T(8,128)(2,1)S(1)} %pad_maximum_fusion.1.refs_0_), channel_id=1, source_target_pairs={{0,1},{1,64},{64,65},{65,0},{2,3},{3,66},{66,67},{67,2},{4,5},{5,6... | collective-permute-start | bytes 786440 | tf_op jit(solution)/shard_map/ppermute | solution.py:222
  57.5 3.8 %collective-permute-start.14 = (bf16[512,512]{1,0:T(8,128)(2,1)S(1)}, bf16[512,512]{1,0:T(8,128)(2,1)S(1)}, u32[]{:S(2)}, u32[]{:S(2)}) collective-permute-start(bf16[512,512]{1,0:T(8,128)(2,1)S(1)} %get-tuple-element.43.own_ref), channel_id=1, source_target_pairs={{0,2},{2,0},{1,3},{3,1},{4,6},{6,4},{5,7},{7,5},{8,10},{10,8},{9,1... | collective-permute-start | bytes 1572872 | tf_op jit(solution)/shard_map/ppermute | solution.py:29
  63.8 2.7 %collective-permute-start.15 = (f32[512,512]{1,0:T(8,128)S(1)}, f32[512,512]{1,0:T(8,128)S(1)}, u32[]{:S(2)}, u32[]{:S(2)}) collective-permute-start(f32[512,512]{1,0:T(8,128)S(1)} %get-tuple-element.48), channel_id=1, source_target_pairs={{0,2},{2,0},{1,3},{3,1},{4,6},{6,4},{5,7},{7,5},{8,10},{10,8},{9,1... | collective-permute-start | bytes 3145736 | tf_op jit(solution)/shard_map/ppermute | solution.py:29

commit v17 on v12

--- a/solution.py
+++ b/solution.py
@@ -93,14 +93,16 @@
     cols = trial_half.shape[1]
 
     def kernel(trial_ref, left_ref, *refs):
-        boxes, (out_ref, psi_ref) = refs[:3], refs[3:]
-        psi_ref[:, :points] = left_ref[...]
+        boxes, (out_ref, psi_ref, sem) = refs[:3], refs[3:]
+        load = pltpu.make_async_copy(left_ref, psi_ref.at[:, :points], sem)
+        load.start()
         for k in range(1, 4):
             box = boxes[k - 1]
             for g in range(states // points):
                 psi_ref[g * points : (g + 1) * points, k * points : (k + 1) * points] = box[
                     box.shape[0] - 1, :, g * points : (g + 1) * points
                 ]
+        load.wait()
         out_ref[...] = lax.dot_general(
             psi_ref[...], trial_ref[...], (((0,), (0,)), ((), ())), preferred_element_type=F32
         ).astype(BF16)
@@ -111,8 +113,9 @@
             jax.ShapeDtypeStruct((4 * points, cols), BF16),
             jax.ShapeDtypeStruct((states, 4 * points), BF16),
         ],
-        in_specs=[vmem_spec()] * 5,
+        in_specs=[vmem_spec(), pl.BlockSpec(memory_space=pl.ANY)] + [vmem_spec()] * 3,
         out_specs=[vmem_spec()] * 2,
+        scratch_shapes=[pltpu.SemaphoreType.DMA],
         compiler_params=params(12),
         name="project",
     )(trial_half, left, near, far, passed)
@@ -126,7 +129,7 @@
     chunk = 512
 
     def kernel(own_ref, other_ref, *refs):
-        line_refs, scr_refs, (keep_ref, send_ref, proj, panel_ref) = refs[:5], refs[5:9], refs[9:]
+        line_refs, scr_refs, (weighted_ref, panel_ref, send_ref, proj) = refs[:5], refs[5:9], refs[9:]
         y, x = lax.axis_index("y"), lax.axis_index("x")
         for k in range(16):
             at = lax.rem(y + STEPS[k // 4] + 4, 4) * 4 + lax.rem(x + STEPS[k % 4] + 4, 4)
@@ -156,24 +159,40 @@
                 ],
                 0,
             )
-            send = jnp.dot(weighted, panel_ref[here, sibs], preferred_element_type=F32)
-            keep = jnp.dot(weighted, panel_ref[here, mine], preferred_element_type=F32)
-            if k == 0:
-                send_ref[...] = send
-                keep_ref[...] = keep
-            else:
-                send_ref[...] += send
-                keep_ref[...] += keep
-
-    return pl.pallas_call(
-        kernel,
-        out_shape=[jax.ShapeDtypeStruct((rows, half), F32)] * 2,
+            weighted_ref[:, here] = weighted
+        send_ref[...] = jnp.dot(weighted_ref[...], panel_ref[:, sibs], preferred_element_type=F32)
+
+    return pl.pallas_call(
+        kernel,
+        out_shape=[
+            jax.ShapeDtypeStruct((rows, count), BF16),
+            jax.ShapeDtypeStruct((count, states), BF16),
+            jax.ShapeDtypeStruct((rows, half), F32),
+        ],
         in_specs=[vmem_spec()] * 11,
-        out_specs=[vmem_spec()] * 2,
-        scratch_shapes=[pltpu.VMEM((rows, half), BF16), pltpu.VMEM((count, states), BF16)],
+        out_specs=[vmem_spec()] * 3,
+        scratch_shapes=[pltpu.VMEM((rows, half), BF16)],
         compiler_params=params(24),
         name="direct",
     )(proj_own, proj_other, *lines, own, *boxes)
+
+
+def own_half(weighted, panel):
+    rows, count = weighted.shape
+    half = panel.shape[1] // 2
+
+    def kernel(weighted_ref, panel_ref, keep_ref):
+        mine = pl.ds(pl.multiple_of(lax.axis_index("core") * half, half), half)
+        keep_ref[...] = jnp.dot(weighted_ref[...], panel_ref[:, mine], preferred_element_type=F32)
+
+    return pl.pallas_call(
+        kernel,
+        out_shape=jax.ShapeDtypeStruct((rows, half), F32),
+        in_specs=[vmem_spec()] * 2,
+        out_specs=vmem_spec(),
+        compiler_params=params(16),
+        name="own_half",
+    )(weighted, panel)
 
 
 def finish(psi, keep, got):
@@ -225,8 +244,9 @@
     proj_own, psi = project(trial_half, psi_v, near, far, passed)
     proj_other = swap(proj_own)
     panel = [line, behind, ahead, *beyond]
-    keep, send = direct(proj_own, proj_other, panel, own, [near, far, passed])
+    weighted, ordered, send = direct(proj_own, proj_other, panel, own, [near, far, passed])
     got = swap(send)
+    keep = own_half(weighted, ordered)
     term = finish(psi, keep, got)
     parts = exchange(term.reshape(devices, rows, half), TILE_VEC)
     parts = parts.reshape(-1, 2, 2, rows, half).astype(F32)

time: 89.7 us -> 89.3 us (level)
    pallas_call x1 -> x2, Pallas kernels: 2.53 us -> 2.69 us  [the longest x1 1.98 us: direct(): pl.pallas_call(kernel, out_shape=[jax.ShapeDtypeStruct((rows, count), BF1...]
  transfers between devices with their start and end apart: 13 -> 13, of which waited for: 5 -> 5; matrix products, arithmetic and copies ran while one was open for 1% -> 1% of each run, Pallas kernels for 2% -> 3%
where the time goes in v17:
time: 89.3 us; the launch traced here: 89 us
  blocking collectives  27.1 us (30%)
  starting transfers between devices  25.3 us (28%)
  waiting for transfers between devices  20.2 us (23%)
  local copies, waits for them, and re-layouts  8.53 us (10%)
  Pallas kernels  6.9 us (8%)
    all_to_all x1, blocking collectives, exchange(): return lax.all_to_all(value, axes, split_axis=0, concat_axis=0, tiled=True)  27.1 us
    ppermute x7, waiting for transfers between devices, shift(): return lax.ppermute(value, axis, [(k, (k + by) % n) for k in range(n)])  15.4 us
    ppermute x7, starting transfers between devices, shift(): return lax.ppermute(value, axis, [(k, (k + by) % n) for k in range(n)])  10.6 us
    all_to_all x1, starting transfers between devices, exchange(): return lax.all_to_all(value, axes, split_axis=0, concat_axis=0, tiled=True)  8.41 us
    unnamed x32, local copies, waits for them, and re-layouts  6.53 us
    ppermute x4, waiting for transfers between devices, swap(): return lax.ppermute(value, 'core', [(0, 1), (1, 0)])  4.84 us
    ppermute x1, starting transfers between devices, shards(): far = lax.ppermute(far, 'zh', [(0, 1), (1, 0)])  3.6 us
    ppermute x4, starting transfers between devices, swap(): return lax.ppermute(value, 'core', [(0, 1), (1, 0)])  2.69 us
  transfers between devices with their start and end apart: 13, of which 5 were waited for; matrix products, arithmetic and copies ran while one was open for 1% of the time, Pallas kernels for 3%

profile of v17, /device:TPU:1, one launch (start us, length us, event | category | flops | bytes accessed | tf_op | source)
XLA Modules:
  0.0 89.0 jit_solution(18019426435588818058)
XLA Ops:
  0.0 3.6 %collective-permute-start.2 = (bf16[64,1024]{1,0:T(8,128)(2,1)}, bf16[64,1024]{1,0:T(8,128)(2,1)S(1)}, u32[]{:S(2)}, u32[]{:S(2)}) collective-permute-start(bf16[64,1024]{1,0:T(8,128)(2,1)} %bitcast.18), channel_id=1, source_target_pairs={{0,8},{4,12},{8,0},{12,4},{1,9},{5,13},{9,1},{13,5},{2,10},{6,14},... | collective-permute-start | bytes 393224 | tf_op jit(solution)/shard_map/ppermute | solution.py:19
  3.6 0.9 collective-permute-start.1
  5.0 1.6 %copy-done = f32[128,4096]{1,0:T(8,128)S(1)} copy-done((f32[128,4096]{1,0:T(8,128)S(1)}, f32[128,4096]{1,0:T(8,128)}, u32[]{:S(2)}) %copy-start) | copy-done | bytes 2097176
  6.6 0.9 %copy-done.5 = bf16[1024,128]{1,0:T(8,128)(2,1)S(1)} copy-done((bf16[1024,128]{1,0:T(8,128)(2,1)S(1)}, bf16[1024,128]{1,0:T(8,128)(2,1)}, u32[]{:S(2)}) %copy-start.5) | copy-done | bytes 262168
  7.6 2.0 %pack.1 = (f32[128,1024]{1,0:T(8,128)S(1)}, bf16[2,128,1024]{2,1,0:T(8,128)(2,1)S(1)}, bf16[3,128,1024]{2,1,0:T(8,128)(2,1)}) custom-call(f32[128,4096]{1,0:T(8,128)S(1)} %copy-done, bf16[1024,128]{1,0:T(8,128)(2,1)S(1)} %copy-done.5), custom_call_target="tpu_custom_call" | custom-call | tf_op jit(solution)/shard_map/pack/pallas_call | solution.py:69
  9.6 0.8 copy-done.7
  11.3 1.1 %broadcast_in_dim.2 = bf16[32,2,2,8,512]{4,3,2,1,0:T(8,128)(2,1)} broadcast(bf16[2,8,512]{2,1,0:T(8,128)(2,1)S(1)} %bitcast.22), dimensions={1,3,4} | broadcast | bytes 1064960 | tf_op jit(solution)/shard_map/broadcast_in_dim | solution.py:234
  12.4 2.7 %collective-permute-start.7 = (bf16[256,1024]{1,0:T(8,128)(2,1)S(1)}, bf16[256,1024]{1,0:T(8,128)(2,1)S(1)}, u32[]{:S(2)}, u32[]{:S(2)}) collective-permute-start(bf16[256,1024]{1,0:T(8,128)(2,1)S(1)} %pad_maximum_fusion.refs_0_), channel_id=1, source_target_pairs={{0,48},{16,0},{32,16},{48,32},{1,49},{17,1},{33,17},{49,33},{2,50}... | collective-permute-start | bytes 1572872 | tf_op jit(solution)/shard_map/ppermute | solution.py:19
  15.1 3.6 %collective-permute-start.4 = (bf16[3,128,1024]{2,1,0:T(8,128)(2,1)}, bf16[3,128,1024]{2,1,0:T(8,128)(2,1)S(1)}, u32[]{:S(2)}, u32[]{:S(2)}) collective-permute-start(bf16[3,128,1024]{2,1,0:T(8,128)(2,1)} %get-tuple-element.24), channel_id=1, source_target_pairs={{0,64},{64,0},{1,65},{65,1},{2,66},{66,2},{3,67},{67,3},{4,68},{68... | collective-permute-start | bytes 2359304 | tf_op jit(solution)/shard_map/ppermute | solution.py:238
  18.7 8.4 %all-to-all-start = ((bf16[128,8,512]{2,1,0:T(8,128)(2,1)}), bf16[128,8,512]{2,1,0:T(8,128)(2,1)S(1)}, u32[]{:S(2)}, u32[]{:S(2)}) async-start(bf16[128,8,512]{2,1,0:T(8,128)(2,1)} %bitcast.16), calls=%async_computation | async-start | bytes 2097152 | tf_op jit(solution)/shard_map/all_to_all | solution.py:23
  27.2 2.7 %collective-permute-start.8 = (bf16[128,1024]{1,0:T(8,128)(2,1)S(1)}, bf16[128,1024]{1,0:T(8,128)(2,1)S(1)}, u32[]{:S(2)}, u32[]{:S(2)}) collective-permute-start(bf16[128,1024]{1,0:T(8,128)(2,1)S(1)} %slice.13), channel_id=1, source_target_pairs={{0,48},{16,0},{32,16},{48,32},{1,49},{17,1},{33,17},{49,33},{2,50}... | collective-permute-start | bytes 786440 | tf_op jit(solution)/shard_map/ppermute | solution.py:19
  30.0 1.2 %collective-permute-start.3 = (bf16[2,128,1024]{2,1,0:T(8,128)(2,1)}, bf16[2,128,1024]{2,1,0:T(8,128)(2,1)S(1)}, u32[]{:S(2)}, u32[]{:S(2)}) collective-permute-start(bf16[2,128,1024]{2,1,0:T(8,128)(2,1)} %copy-done.13), channel_id=1, source_target_pairs={{0,2},{2,0},{1,3},{3,1},{4,6},{6,4},{5,7},{7,5},{8,10},{10,8},{9,1... | collective-permute-start | bytes 1572872 | tf_op jit(solution)/shard_map/ppermute | solution.py:27
  31.2 14.2 %collective-permute-done.8.refs_4_ = bf16[128,1024]{1,0:T(8,128)(2,1)S(1)} collective-permute-done((bf16[128,1024]{1,0:T(8,128)(2,1)S(1)}, bf16[128,1024]{1,0:T(8,128)(2,1)S(1)}, u32[]{:S(2)}, u32[]{:S(2)}) %collective-permute-start.8) | collective-permute-done | bytes 262176 | tf_op jit(solution)/shard_map/ppermute | solution.py:19
  46.1 1.2 %collective-permute-done.6.refs_3_ = bf16[128,1024]{1,0:T(8,128)(2,1)S(1)} collective-permute-done((bf16[128,1024]{1,0:T(8,128)(2,1)S(1)}, bf16[128,1024]{1,0:T(8,128)(2,1)S(1)}, u32[]{:S(2)}, u32[]{:S(2)}) %collective-permute-start.6) | collective-permute-done | bytes 262176 | tf_op jit(solution)/shard_map/ppermute | solution.py:19
  48.0 0.9 slice.11
  49.4 1.7 %collective-permute-done.9.refs_2_.refs_8_ = bf16[2,128,1024]{2,1,0:T(8,128)(2,1)S(1)} collective-permute-done((bf16[2,128,1024]{2,1,0:T(8,128)(2,1)}, bf16[2,128,1024]{2,1,0:T(8,128)(2,1)S(1)}, u32[]{:S(2)}, u32[]{:S(2)}) %collective-permute-start.9) | collective-permute-done | bytes 524320 | tf_op jit(solution)/shard_map/ppermute | solution.py:27
  51.2 0.9 %copy-done.6 = bf16[1024,128]{1,0:T(8,128)(2,1)S(1)} copy-done((bf16[1024,128]{1,0:T(8,128)(2,1)S(1)}, bf16[1024,128]{1,0:T(8,128)(2,1)}, u32[]{:S(2)}) %copy-start.6) | copy-done | bytes 262168
  52.1 0.9 %project.1 = (bf16[512,512]{1,0:T(8,128)(2,1)S(1)}, bf16[1024,512]{1,0:T(8,128)(2,1)S(1)}) custom-call(bf16[1024,512]{1,0:T(8,128)(2,1)S(1)} %bitcast.14, bf16[1024,128]{1,0:T(8,128)(2,1)S(1)} %copy-done.6, bf16[2,128,1024]{2,1,0:T(8,128)(2,1)S(1)} %collective-permute-done.3.refs_0_.refs_6_, ...), custom_call_target="tpu_custom_call" | custom-call | tf_op jit(solution)/shard_map/project/pallas_call | solution.py:110
  53.5 1.5 %collective-permute-done.10.other_ref = bf16[512,512]{1,0:T(8,128)(2,1)S(1)} collective-permute-done((bf16[512,512]{1,0:T(8,128)(2,1)S(1)}, bf16[512,512]{1,0:T(8,128)(2,1)S(1)}, u32[]{:S(2)}, u32[]{:S(2)}) %collective-permute-start.10) | collective-permute-done | bytes 524320 | tf_op jit(solution)/shard_map/ppermute | solution.py:27
  55.1 2.0 %direct.1 = (bf16[512,1024]{1,0:T(8,128)(2,1)S(1)}, bf16[1024,1024]{1,0:T(8,128)(2,1)S(1)}, f32[512,512]{1,0:T(8,128)S(1)}) custom-call(bf16[512,512]{1,0:T(8,128)(2,1)S(1)} %get-tuple-element.28.own_ref, bf16[512,512]{1,0:T(8,128)(2,1)S(1)} %collective-permute-done.10.other_ref, bf16[256,1024]{1,0:T(8,128)(2,1)S(1)} %pad_maximum_fusion.refs_0_, ...), custom_call_target="tpu_custom_call" | custom-call | tf_op jit(solution)/shard_map/direct/pallas_call | solution.py:165
  58.2 1.6 %collective-permute-done.11.got_ref = f32[512,512]{1,0:T(8,128)S(1)} collective-permute-done((f32[512,512]{1,0:T(8,128)S(1)}, f32[512,512]{1,0:T(8,128)S(1)}, u32[]{:S(2)}, u32[]{:S(2)}) %collective-permute-start.11) | collective-permute-done | bytes 1048608 | tf_op jit(solution)/shard_map/ppermute | solution.py:27
  59.8 1.3 %finish.1 = bf16[1024,512]{1,0:T(8,128)(2,1)S(1)} custom-call(bf16[1024,512]{1,0:T(8,128)(2,1)S(1)} %get-tuple-element.27.psi_ref, f32[512,512]{1,0:T(8,128)S(1)} %own_half.1.keep_ref, f32[512,512]{1,0:T(8,128)S(1)} %collective-permute-done.11.got_ref), custom_call_target="tpu_custom_call" | custom-call | tf_op jit(solution)/shard_map/finish/pallas_call | solution.py:215
  61.1 27.1 %all_to_all.10 = bf16[128,8,512]{2,1,0:T(8,128)(2,1)S(1)} all-to-all(bf16[128,8,512]{2,1,0:T(8,128)(2,1)S(1)} %bitcast.15), channel_id=1, replica_groups=mesh['zh'=2,'y'=4,'x'=4,'core'=2,'zl'=2] {'zh','y','x','core','zl'}, dimensions={0} | all-to-all | bytes 2097152 | tf_op jit(solution)/shard_map/all_to_all | solution.py:23
  88.2 0.8 convert_reduce_fusion
  (46 shorter events, 5.2 us)
Async XLA Ops:
  0.0 11.2 %collective-permute-start.2 = (bf16[64,1024]{1,0:T(8,128)(2,1)}, bf16[64,1024]{1,0:T(8,128)(2,1)S(1)}, u32[]{:S(2)}, u32[]{:S(2)}) collective-permute-start(bf16[64,1024]{1,0:T(8,128)(2,1)} %bitcast.18), channel_id=1, source_target_pairs={{0,8},{4,12},{8,0},{12,4},{1,9},{5,13},{9,1},{13,5},{2,10},{6,14},... | collective-permute-start | bytes 393224 | tf_op jit(solution)/shard_map/ppermute | solution.py:19
  3.6 7.6 %collective-permute-start.1 = (bf16[64,1024]{1,0:T(8,128)(2,1)}, bf16[64,1024]{1,0:T(8,128)(2,1)S(1)}, u32[]{:S(2)}, u32[]{:S(2)}) collective-permute-start(bf16[64,1024]{1,0:T(8,128)(2,1)} %bitcast.19), channel_id=1, source_target_pairs={{0,12},{4,0},{8,4},{12,8},{1,13},{5,1},{9,5},{13,9},{2,14},{6,2},{... | collective-permute-start | bytes 393224 | tf_op jit(solution)/shard_map/ppermute | solution.py:19
  4.4 6.7 %collective-permute-start = (bf16[64,1024]{1,0:T(8,128)(2,1)}, bf16[64,1024]{1,0:T(8,128)(2,1)S(1)}, u32[]{:S(2)}, u32[]{:S(2)}) collective-permute-start(bf16[64,1024]{1,0:T(8,128)(2,1)} %bitcast.20), channel_id=1, source_target_pairs={{0,4},{4,8},{8,12},{12,0},{1,5},{5,9},{9,13},{13,1},{2,6},{6,10},{... | collective-permute-start | bytes 393224 | tf_op jit(solution)/shard_map/ppermute | solution.py:19
  5.0 1.6 %copy-start = (f32[128,4096]{1,0:T(8,128)S(1)}, f32[128,4096]{1,0:T(8,128)}, u32[]{:S(2)}) copy-start(f32[128,4096]{1,0:T(8,128)} %in_ref.1) | copy-start | bytes 6291460
  6.6 0.9 %copy-start.5 = (bf16[1024,128]{1,0:T(8,128)(2,1)S(1)}, bf16[1024,128]{1,0:T(8,128)(2,1)}, u32[]{:S(2)}) copy-start(bf16[1024,128]{1,0:T(8,128)(2,1)} %left_ref.3) | copy-start | bytes 786436
  7.6 3.6 %copy-start.14 = (bf16[1024,1,64]{0,2,1:T(8,128)(2,1)S(1)}, bf16[1024,1,64]{0,2,1:T(8,128)(2,1)}, u32[]{:S(2)}) copy-start(bf16[1024,1,64]{0,2,1:T(8,128)(2,1)} %param.6) | copy-start | bytes 393220
  7.6 3.7 %copy-start.15 = (bf16[1,8,1024]{2,1,0:T(8,128)(2,1)S(1)}, bf16[1,8,1024]{2,1,0:T(8,128)(2,1)}, u32[]{:S(2)}) copy-start(bf16[1,8,1024]{2,1,0:T(8,128)(2,1)} %param.4) | copy-start | bytes 49156
  12.4 14.8 %collective-permute-start.7 = (bf16[256,1024]{1,0:T(8,128)(2,1)S(1)}, bf16[256,1024]{1,0:T(8,128)(2,1)S(1)}, u32[]{:S(2)}, u32[]{:S(2)}) collective-permute-start(bf16[256,1024]{1,0:T(8,128)(2,1)S(1)} %pad_maximum_fusion.refs_0_), channel_id=1, source_target_pairs={{0,48},{16,0},{32,16},{48,32},{1,49},{17,1},{33,17},{49,33},{2,50}... | collective-permute-start | bytes 1572872 | tf_op jit(solution)/shard_map/ppermute | solution.py:19
  15.1 14.8 %collective-permute-start.5 = (bf16[256,1024]{1,0:T(8,128)(2,1)S(1)}, bf16[256,1024]{1,0:T(8,128)(2,1)S(1)}, u32[]{:S(2)}, u32[]{:S(2)}) collective-permute-start(bf16[256,1024]{1,0:T(8,128)(2,1)S(1)} %pad_maximum_fusion.refs_0_), channel_id=1, source_target_pairs={{0,16},{16,32},{32,48},{48,0},{1,17},{17,33},{33,49},{49,1},{2,18}... | collective-permute-start | bytes 1572872 | tf_op jit(solution)/shard_map/ppermute | solution.py:19
  15.1 32.9 %collective-permute-start.4 = (bf16[3,128,1024]{2,1,0:T(8,128)(2,1)}, bf16[3,128,1024]{2,1,0:T(8,128)(2,1)S(1)}, u32[]{:S(2)}, u32[]{:S(2)}) collective-permute-start(bf16[3,128,1024]{2,1,0:T(8,128)(2,1)} %get-tuple-element.24), channel_id=1, source_target_pairs={{0,64},{64,0},{1,65},{65,1},{2,66},{66,2},{3,67},{67,3},{4,68},{68... | collective-permute-start | bytes 2359304 | tf_op jit(solution)/shard_map/ppermute | solution.py:238
  18.7 30.7 %all-to-all-start = ((bf16[128,8,512]{2,1,0:T(8,128)(2,1)}), bf16[128,8,512]{2,1,0:T(8,128)(2,1)S(1)}, u32[]{:S(2)}, u32[]{:S(2)}) async-start(bf16[128,8,512]{2,1,0:T(8,128)(2,1)} %bitcast.16), calls=%async_computation | async-start | bytes 2097152 | tf_op jit(solution)/shard_map/all_to_all | solution.py:23
  27.1 2.8 %copy-start.1 = (bf16[256,1024]{1,0:T(8,128)(2,1)}, bf16[256,1024]{1,0:T(8,128)(2,1)S(1)}, u32[]{:S(2)}) copy-start(bf16[256,1024]{1,0:T(8,128)(2,1)S(1)} %collective-permute-done.7.refs_2_) | copy-start | bytes 1572868
  27.2 18.2 %collective-permute-start.8 = (bf16[128,1024]{1,0:T(8,128)(2,1)S(1)}, bf16[128,1024]{1,0:T(8,128)(2,1)S(1)}, u32[]{:S(2)}, u32[]{:S(2)}) collective-permute-start(bf16[128,1024]{1,0:T(8,128)(2,1)S(1)} %slice.13), channel_id=1, source_target_pairs={{0,48},{16,0},{32,16},{48,32},{1,49},{17,1},{33,17},{49,33},{2,50}... | collective-permute-start | bytes 786440 | tf_op jit(solution)/shard_map/ppermute | solution.py:19
  29.9 18.1 %copy-start.3 = (bf16[256,1024]{1,0:T(8,128)(2,1)}, bf16[256,1024]{1,0:T(8,128)(2,1)S(1)}, u32[]{:S(2)}) copy-start(bf16[256,1024]{1,0:T(8,128)(2,1)S(1)} %collective-permute-done.5.refs_1_) | copy-start | bytes 1572868
  29.9 17.4 %collective-permute-start.6 = (bf16[128,1024]{1,0:T(8,128)(2,1)S(1)}, bf16[128,1024]{1,0:T(8,128)(2,1)S(1)}, u32[]{:S(2)}, u32[]{:S(2)}) collective-permute-start(bf16[128,1024]{1,0:T(8,128)(2,1)S(1)} %slice.12), channel_id=1, source_target_pairs={{0,16},{16,32},{32,48},{48,0},{1,17},{17,33},{33,49},{49,1},{2,18}... | collective-permute-start | bytes 786440 | tf_op jit(solution)/shard_map/ppermute | solution.py:19
  30.0 19.4 %collective-permute-start.3 = (bf16[2,128,1024]{2,1,0:T(8,128)(2,1)}, bf16[2,128,1024]{2,1,0:T(8,128)(2,1)S(1)}, u32[]{:S(2)}, u32[]{:S(2)}) collective-permute-start(bf16[2,128,1024]{2,1,0:T(8,128)(2,1)} %copy-done.13), channel_id=1, source_target_pairs={{0,2},{2,0},{1,3},{3,1},{4,6},{6,4},{5,7},{7,5},{8,10},{10,8},{9,1... | collective-permute-start | bytes 1572872 | tf_op jit(solution)/shard_map/ppermute | solution.py:27
  48.8 2.3 %collective-permute-start.9 = (bf16[2,128,1024]{2,1,0:T(8,128)(2,1)}, bf16[2,128,1024]{2,1,0:T(8,128)(2,1)S(1)}, u32[]{:S(2)}, u32[]{:S(2)}) collective-permute-start(bf16[2,128,1024]{2,1,0:T(8,128)(2,1)} %slice.11), channel_id=1, source_target_pairs={{0,2},{2,0},{1,3},{3,1},{4,6},{6,4},{5,7},{7,5},{8,10},{10,8},{9,1... | collective-permute-start | bytes 1572872 | tf_op jit(solution)/shard_map/ppermute | solution.py:27
  49.4 5.6 %copy-start.2 = (bf16[256,1024]{1,0:T(8,128)(2,1)S(1)}, bf16[256,1024]{1,0:T(8,128)(2,1)}, u32[]{:S(2)}) copy-start(bf16[256,1024]{1,0:T(8,128)(2,1)} %copy-done.1) | copy-start | bytes 1572868
  49.4 5.6 %copy-start.4 = (bf16[256,1024]{1,0:T(8,128)(2,1)S(1)}, bf16[256,1024]{1,0:T(8,128)(2,1)}, u32[]{:S(2)}) copy-start(bf16[256,1024]{1,0:T(8,128)(2,1)} %copy-done.3) | copy-start | bytes 1572868
  52.1 2.9 %copy-start.8 = (f32[128,1024]{1,0:T(8,128)S(1)}, f32[128,1024]{1,0:T(8,128)}, u32[]{:S(2)}) copy-start(f32[128,1024]{1,0:T(8,128)} %copy-done.7) | copy-start | bytes 1572868
  52.1 2.9 %copy-start.10 = (bf16[128,1024]{1,0:T(8,128)(2,1)S(1)}, bf16[128,1024]{1,0:T(8,128)(2,1)}, u32[]{:S(2)}) copy-start(bf16[128,1024]{1,0:T(8,128)(2,1)} %copy-done.9) | copy-start | bytes 786436
  52.1 3.0 %copy-start.12 = (bf16[128,1024]{1,0:T(8,128)(2,1)S(1)}, bf16[128,1024]{1,0:T(8,128)(2,1)}, u32[]{:S(2)}) copy-start(bf16[128,1024]{1,0:T(8,128)(2,1)} %copy-done.11) | copy-start | bytes 786436
  53.1 2.0 %collective-permute-start.10 = (bf16[512,512]{1,0:T(8,128)(2,1)S(1)}, bf16[512,512]{1,0:T(8,128)(2,1)S(1)}, u32[]{:S(2)}, u32[]{:S(2)}) collective-permute-start(bf16[512,512]{1,0:T(8,128)(2,1)S(1)} %get-tuple-element.28.own_ref), channel_id=1, source_target_pairs={{0,2},{2,0},{1,3},{3,1},{4,6},{6,4},{5,7},{7,5},{8,10},{10,8},{9,1... | collective-permute-start | bytes 1572872 | tf_op jit(solution)/shard_map/ppermute | solution.py:27
  57.1 2.7 %collective-permute-start.11 = (f32[512,512]{1,0:T(8,128)S(1)}, f32[512,512]{1,0:T(8,128)S(1)}, u32[]{:S(2)}, u32[]{:S(2)}) collective-permute-start(f32[512,512]{1,0:T(8,128)S(1)} %get-tuple-element.34), channel_id=1, source_target_pairs={{0,2},{2,0},{1,3},{3,1},{4,6},{6,4},{5,7},{7,5},{8,10},{10,8},{9,1... | collective-permute-start | bytes 3145736 | tf_op jit(solution)/shard_map/ppermute | solution.py:27
  (5 other events, 4.0 us)

commit v18 on v17

--- a/solution.py
+++ b/solution.py
@@ -228,20 +228,21 @@
     half = states // 2
     devices = lax.axis_size(TILE_VEC)
     own, near, far = pack(screened, psi_v)
-    block = psi_c[:, 0, :].T
+    block, near, far = lax.optimization_barrier((psi_c[:, 0, :].T, near, far))
     line = jnp.concatenate([block, shift(block, "x", 1), shift(block, "x", -1), shift(block, "x", 2)], 0)
     halves = trial[0].reshape(rows, 2, half).transpose(1, 0, 2)
     copies = jnp.broadcast_to(halves[None, :, None], (devices // 4, 2, 2, rows, half))
-    copies, near, far, line = lax.optimization_barrier((copies, near, far, line))
+    copies, line = lax.optimization_barrier((copies, line))
     trial_half = exchange(copies.reshape(devices, rows, half), TILE_VEC).reshape(-1, half)
     near = swap(near)
     far = lax.ppermute(far, "zh", [(0, 1), (1, 0)])
     behind, ahead = shift(line, "y", 1), shift(line, "y", -1)
     middle = line.shape[0] // 2
     beyond = [shift(behind[:middle], "y", 1), shift(ahead[middle:], "y", -1)]
-    far, beyond = lax.optimization_barrier((far, beyond))
+    far, *_ = lax.optimization_barrier((far, behind, ahead))
     passed = swap(far[1:])
     proj_own, psi = project(trial_half, psi_v, near, far, passed)
+    proj_own, beyond = lax.optimization_barrier((proj_own, beyond))
     proj_other = swap(proj_own)
     panel = [line, behind, ahead, *beyond]
     weighted, ordered, send = direct(proj_own, proj_other, panel, own, [near, far, passed])

time: 89.3 us -> 97.9 us (1.096)
  starting transfers between devices: 25.3 us -> 37.6 us
  blocking collectives: 27.1 us -> 23 us
  waiting for transfers between devices: 20.2 us -> 17.4 us
  local copies, waits for them, and re-layouts: 8.53 us -> 10.5 us
  Pallas kernels: 6.9 us -> 8.04 us
    ppermute x4, starting transfers between devices: 2.69 us -> 16.5 us  [swap(): return lax.ppermute(value, 'core', [(0, 1), (1, 0)])]
    all_to_all x1, blocking collectives: 27.1 us -> 23 us  [exchange(): return lax.all_to_all(value, axes, split_axis=0, concat_axis=0, tiled=True)]
    slice x2, local copies, waits for them, and re-layouts: 0.04 us -> 3.38 us  [shards(): beyond = [shift(behind[:middle], 'y', 1), shift(ahead[middle:], 'y', -1)]]
    ppermute x7, starting transfers between devices: 10.6 us -> 8.41 us  [shift(): return lax.ppermute(value, axis, [(k, (k + by) % n) for k in range(n)])]
    ppermute x4, waiting for transfers between devices: 4.84 us -> 3.11 us  [swap(): return lax.ppermute(value, 'core', [(0, 1), (1, 0)])]
    unnamed x32 -> x20, local copies, waits for them, and re-layouts: 6.53 us -> 5.16 us
    pallas_call x1, Pallas kernels: 1.98 us -> 3.15 us  [direct(): pl.pallas_call(kernel, out_shape=[jax.ShapeDtypeStruct((rows, count), BF1...]
    ppermute x7, waiting for transfers between devices: 15.4 us -> 14.3 us  [shift(): return lax.ppermute(value, axis, [(k, (k + by) % n) for k in range(n)])]
  transfers between devices with their start and end apart: 13 -> 13, of which waited for: 5 -> 8; matrix products, arithmetic and copies ran while one was open for 1% -> 5% of each run, Pallas kernels for 3% -> 2%
where the time goes in v18:
time: 97.9 us; the launch traced here: 97.5 us
  starting transfers between devices  37.6 us (38%)
  blocking collectives  23 us (23%)
  waiting for transfers between devices  17.4 us (18%)
  local copies, waits for them, and re-layouts  10.5 us (11%)
  Pallas kernels  8.04 us (8%)
    all_to_all x1, blocking collectives, exchange(): return lax.all_to_all(value, axes, split_axis=0, concat_axis=0, tiled=True)  23 us
    ppermute x4, starting transfers between devices, swap(): return lax.ppermute(value, 'core', [(0, 1), (1, 0)])  16.5 us
    ppermute x7, waiting for transfers between devices, shift(): return lax.ppermute(value, axis, [(k, (k + by) % n) for k in range(n)])  14.3 us
    ppermute x7, starting transfers between devices, shift(): return lax.ppermute(value, axis, [(k, (k + by) % n) for k in range(n)])  8.41 us
    all_to_all x1, starting transfers between devices, exchange(): return lax.all_to_all(value, axes, split_axis=0, concat_axis=0, tiled=True)  8.33 us
    unnamed x20, local copies, waits for them, and re-layouts  5.16 us
    ppermute x1, starting transfers between devices, shards(): far = lax.ppermute(far, 'zh', [(0, 1), (1, 0)])  4.43 us
    slice x2, local copies, waits for them, and re-layouts, shards(): beyond = [shift(behind[:middle], 'y', 1), shift(ahead[middle:], 'y', -1)]  3.38 us
  transfers between devices with their start and end apart: 13, of which 8 were waited for; matrix products, arithmetic and copies ran while one was open for 5% of the time, Pallas kernels for 2%

profile of v18, /device:TPU:1, one launch (start us, length us, event | category | flops | bytes accessed | tf_op | source)
XLA Modules:
  0.0 97.5 jit_solution(11288474285804387477)
XLA Ops:
  0.0 1.6 %copy-done = f32[128,4096]{1,0:T(8,128)S(1)} copy-done((f32[128,4096]{1,0:T(8,128)S(1)}, f32[128,4096]{1,0:T(8,128)}, u32[]{:S(2)}) %copy-start) | copy-done | bytes 2097176
  1.6 0.9 copy-done.3
  2.5 2.0 %pack.1 = (f32[128,1024]{1,0:T(8,128)S(1)}, bf16[2,128,1024]{2,1,0:T(8,128)(2,1)S(1)}, bf16[3,128,1024]{2,1,0:T(8,128)(2,1)}) custom-call(f32[128,4096]{1,0:T(8,128)S(1)} %copy-done, bf16[1024,128]{1,0:T(8,128)(2,1)S(1)} %copy-done.3), custom_call_target="tpu_custom_call" | custom-call | tf_op jit(solution)/shard_map/pack/pallas_call | solution.py:69
  6.1 4.4 %collective-permute-start.4 = (bf16[3,128,1024]{2,1,0:T(8,128)(2,1)}, bf16[3,128,1024]{2,1,0:T(8,128)(2,1)S(1)}, u32[]{:S(2)}, u32[]{:S(2)}) collective-permute-start(bf16[3,128,1024]{2,1,0:T(8,128)(2,1)} %get-tuple-element.27), channel_id=1, source_target_pairs={{0,64},{64,0},{1,65},{65,1},{2,66},{66,2},{3,67},{67,3},{4,68},{68... | collective-permute-start | bytes 2359304 | tf_op jit(solution)/shard_map/ppermute | solution.py:238
  10.5 2.7 %collective-permute-start.2 = (bf16[64,1024]{1,0:T(8,128)(2,1)S(1)}, bf16[64,1024]{1,0:T(8,128)(2,1)S(1)}, u32[]{:S(2)}, u32[]{:S(2)}) collective-permute-start(bf16[64,1024]{1,0:T(8,128)(2,1)S(1)} %bitcast.18), channel_id=1, source_target_pairs={{0,8},{4,12},{8,0},{12,4},{1,9},{5,13},{9,1},{13,5},{2,10},{6,14},... | collective-permute-start | bytes 393224 | tf_op jit(solution)/shard_map/ppermute | solution.py:19
  14.8 1.4 %collective-permute-done.2 = bf16[64,1024]{1,0:T(8,128)(2,1)S(1)} collective-permute-done((bf16[64,1024]{1,0:T(8,128)(2,1)S(1)}, bf16[64,1024]{1,0:T(8,128)(2,1)S(1)}, u32[]{:S(2)}, u32[]{:S(2)}) %collective-permute-start.2) | collective-permute-done | bytes 131104 | tf_op jit(solution)/shard_map/ppermute | solution.py:19
  16.2 2.8 %collective-permute-done.1 = bf16[64,1024]{1,0:T(8,128)(2,1)S(1)} collective-permute-done((bf16[64,1024]{1,0:T(8,128)(2,1)S(1)}, bf16[64,1024]{1,0:T(8,128)(2,1)S(1)}, u32[]{:S(2)}, u32[]{:S(2)}) %collective-permute-start.1) | collective-permute-done | bytes 131104 | tf_op jit(solution)/shard_map/ppermute | solution.py:19
  19.8 1.1 %broadcast_in_dim.2 = bf16[32,2,2,8,512]{4,3,2,1,0:T(8,128)(2,1)} broadcast(bf16[2,8,512]{2,1,0:T(8,128)(2,1)S(1)} %bitcast.22), dimensions={1,3,4} | broadcast | bytes 1064960 | tf_op jit(solution)/shard_map/broadcast_in_dim | solution.py:234
  20.9 2.7 %collective-permute-start.6 = (bf16[256,1024]{1,0:T(8,128)(2,1)S(1)}, bf16[256,1024]{1,0:T(8,128)(2,1)S(1)}, u32[]{:S(2)}, u32[]{:S(2)}) collective-permute-start(bf16[256,1024]{1,0:T(8,128)(2,1)S(1)} %pad_maximum_fusion.refs_0_), channel_id=1, source_target_pairs={{0,48},{16,0},{32,16},{48,32},{1,49},{17,1},{33,17},{49,33},{2,50}... | collective-permute-start | bytes 1572872 | tf_op jit(solution)/shard_map/ppermute | solution.py:19
  23.6 8.3 %all-to-all-start = ((bf16[128,8,512]{2,1,0:T(8,128)(2,1)}), bf16[128,8,512]{2,1,0:T(8,128)(2,1)S(1)}, u32[]{:S(2)}, u32[]{:S(2)}) async-start(bf16[128,8,512]{2,1,0:T(8,128)(2,1)} %bitcast.16), calls=%async_computation | async-start | bytes 2097152 | tf_op jit(solution)/shard_map/all_to_all | solution.py:23
  32.0 1.1 %collective-permute-start.3 = (bf16[2,128,1024]{2,1,0:T(8,128)(2,1)}, bf16[2,128,1024]{2,1,0:T(8,128)(2,1)S(1)}, u32[]{:S(2)}, u32[]{:S(2)}) collective-permute-start(bf16[2,128,1024]{2,1,0:T(8,128)(2,1)} %copy-done.7), channel_id=1, source_target_pairs={{0,2},{2,0},{1,3},{3,1},{4,6},{6,4},{5,7},{7,5},{8,10},{10,8},{9,1... | collective-permute-start | bytes 1572872 | tf_op jit(solution)/shard_map/ppermute | solution.py:27
  33.1 2.9 %collective-permute-done.5.refs_1_ = bf16[256,1024]{1,0:T(8,128)(2,1)} collective-permute-done((bf16[256,1024]{1,0:T(8,128)(2,1)S(1)}, bf16[256,1024]{1,0:T(8,128)(2,1)}, u32[]{:S(2)}, u32[]{:S(2)}) %collective-permute-start.5) | collective-permute-done | bytes 524320 | tf_op jit(solution)/shard_map/ppermute | solution.py:19
  36.9 13.8 %collective-permute-start.7 = (bf16[2,128,1024]{2,1,0:T(8,128)(2,1)}, bf16[2,128,1024]{2,1,0:T(8,128)(2,1)S(1)}, u32[]{:S(2)}, u32[]{:S(2)}) collective-permute-start(bf16[2,128,1024]{2,1,0:T(8,128)(2,1)} %slice.9), channel_id=1, source_target_pairs={{0,2},{2,0},{1,3},{3,1},{4,6},{6,4},{5,7},{7,5},{8,10},{10,8},{9,1... | collective-permute-start | bytes 1572872 | tf_op jit(solution)/shard_map/ppermute | solution.py:27
  50.6 1.7 %slice.13 = bf16[128,1024]{1,0:T(8,128)(2,1)} slice(bf16[256,1024]{1,0:T(8,128)(2,1)} %copy-done.1), slice={[128:256], [0:1024]} | slice | bytes 524288 | tf_op jit(solution)/shard_map/slice | solution.py:241
  53.0 1.7 %slice.12 = bf16[128,1024]{1,0:T(8,128)(2,1)} slice(bf16[256,1024]{1,0:T(8,128)(2,1)} %collective-permute-done.5.refs_1_), slice={[0:128], [0:1024]} | slice | bytes 524288 | tf_op jit(solution)/shard_map/slice | solution.py:241
  55.5 1.0 %copy-done.4 = bf16[1024,128]{1,0:T(8,128)(2,1)S(1)} copy-done((bf16[1024,128]{1,0:T(8,128)(2,1)S(1)}, bf16[1024,128]{1,0:T(8,128)(2,1)}, u32[]{:S(2)}) %copy-start.4) | copy-done | bytes 262168
  57.5 3.1 %collective-permute-done.9.refs_4_ = bf16[128,1024]{1,0:T(8,128)(2,1)} collective-permute-done((bf16[128,1024]{1,0:T(8,128)(2,1)}, bf16[128,1024]{1,0:T(8,128)(2,1)}, u32[]{:S(2)}, u32[]{:S(2)}) %collective-permute-start.9) | collective-permute-done | bytes 262176 | tf_op jit(solution)/shard_map/ppermute | solution.py:19
  60.6 3.3 %collective-permute-done.8.refs_3_ = bf16[128,1024]{1,0:T(8,128)(2,1)} collective-permute-done((bf16[128,1024]{1,0:T(8,128)(2,1)}, bf16[128,1024]{1,0:T(8,128)(2,1)}, u32[]{:S(2)}, u32[]{:S(2)}) %collective-permute-start.8) | collective-permute-done | bytes 262176 | tf_op jit(solution)/shard_map/ppermute | solution.py:19
  63.9 1.1 %collective-permute-start.10 = (bf16[512,512]{1,0:T(8,128)(2,1)S(1)}, bf16[512,512]{1,0:T(8,128)(2,1)S(1)}, u32[]{:S(2)}, u32[]{:S(2)}) collective-permute-start(bf16[512,512]{1,0:T(8,128)(2,1)S(1)} %get-tuple-element.32.own_ref), channel_id=1, source_target_pairs={{0,2},{2,0},{1,3},{3,1},{4,6},{6,4},{5,7},{7,5},{8,10},{10,8},{9,1... | collective-permute-start | bytes 1572872 | tf_op jit(solution)/shard_map/ppermute | solution.py:27
  65.0 1.5 %collective-permute-done.10.other_ref = bf16[512,512]{1,0:T(8,128)(2,1)S(1)} collective-permute-done((bf16[512,512]{1,0:T(8,128)(2,1)S(1)}, bf16[512,512]{1,0:T(8,128)(2,1)S(1)}, u32[]{:S(2)}, u32[]{:S(2)}) %collective-permute-start.10) | collective-permute-done | bytes 524320 | tf_op jit(solution)/shard_map/ppermute | solution.py:27
  66.5 3.2 %direct.1 = (bf16[512,1024]{1,0:T(8,128)(2,1)S(1)}, bf16[1024,1024]{1,0:T(8,128)(2,1)S(1)}, f32[512,512]{1,0:T(8,128)S(1)}) custom-call(bf16[512,512]{1,0:T(8,128)(2,1)S(1)} %get-tuple-element.32.own_ref, bf16[512,512]{1,0:T(8,128)(2,1)S(1)} %collective-permute-done.10.other_ref, bf16[256,1024]{1,0:T(8,128)(2,1)S(1)} %pad_maximum_fusion.refs_0_, ...), custom_call_target="tpu_custom_call" | custom-call | tf_op jit(solution)/shard_map/direct/pallas_call | solution.py:165
  70.8 1.6 %collective-permute-done.11.got_ref = f32[512,512]{1,0:T(8,128)S(1)} collective-permute-done((f32[512,512]{1,0:T(8,128)S(1)}, f32[512,512]{1,0:T(8,128)S(1)}, u32[]{:S(2)}, u32[]{:S(2)}) %collective-permute-start.11) | collective-permute-done | bytes 1048608 | tf_op jit(solution)/shard_map/ppermute | solution.py:27
  72.4 1.3 %finish.1 = bf16[1024,512]{1,0:T(8,128)(2,1)S(1)} custom-call(bf16[1024,512]{1,0:T(8,128)(2,1)S(1)} %get-tuple-element.30.psi_ref, f32[512,512]{1,0:T(8,128)S(1)} %own_half.1.keep_ref, f32[512,512]{1,0:T(8,128)S(1)} %collective-permute-done.11.got_ref), custom_call_target="tpu_custom_call" | custom-call | tf_op jit(solution)/shard_map/finish/pallas_call | solution.py:215
  73.7 23.0 %all_to_all.10 = bf16[128,8,512]{2,1,0:T(8,128)(2,1)S(1)} all-to-all(bf16[128,8,512]{2,1,0:T(8,128)(2,1)S(1)} %bitcast.15), channel_id=1, replica_groups=mesh['zh'=2,'y'=4,'x'=4,'core'=2,'zl'=2] {'zh','y','x','core','zl'}, dimensions={0} | all-to-all | bytes 2097152 | tf_op jit(solution)/shard_map/all_to_all | solution.py:23
  (34 shorter events, 9.1 us)
Async XLA Ops:
  0.0 1.6 %copy-start = (f32[128,4096]{1,0:T(8,128)S(1)}, f32[128,4096]{1,0:T(8,128)}, u32[]{:S(2)}) copy-start(f32[128,4096]{1,0:T(8,128)} %in_ref.1) | copy-start | bytes 6291460
  1.6 0.9 copy-start.3
  2.5 8.0 %copy-start.8 = (bf16[1024,1,64]{0,2,1:T(8,128)(2,1)S(1)}, bf16[1024,1,64]{0,2,1:T(8,128)(2,1)}, u32[]{:S(2)}) copy-start(bf16[1024,1,64]{0,2,1:T(8,128)(2,1)} %param.6) | copy-start | bytes 393220
  2.5 17.2 %copy-start.9 = (bf16[1,8,1024]{2,1,0:T(8,128)(2,1)S(1)}, bf16[1,8,1024]{2,1,0:T(8,128)(2,1)}, u32[]{:S(2)}) copy-start(bf16[1,8,1024]{2,1,0:T(8,128)(2,1)} %param.4) | copy-start | bytes 49156
  4.5 0.8 copy-start.5
  5.3 0.8 copy-start.7
  6.1 30.0 %collective-permute-start.4 = (bf16[3,128,1024]{2,1,0:T(8,128)(2,1)}, bf16[3,128,1024]{2,1,0:T(8,128)(2,1)S(1)}, u32[]{:S(2)}, u32[]{:S(2)}) collective-permute-start(bf16[3,128,1024]{2,1,0:T(8,128)(2,1)} %get-tuple-element.27), channel_id=1, source_target_pairs={{0,64},{64,0},{1,65},{65,1},{2,66},{66,2},{3,67},{67,3},{4,68},{68... | collective-permute-start | bytes 2359304 | tf_op jit(solution)/shard_map/ppermute | solution.py:238
  10.5 5.6 %collective-permute-start.2 = (bf16[64,1024]{1,0:T(8,128)(2,1)S(1)}, bf16[64,1024]{1,0:T(8,128)(2,1)S(1)}, u32[]{:S(2)}, u32[]{:S(2)}) collective-permute-start(bf16[64,1024]{1,0:T(8,128)(2,1)S(1)} %bitcast.18), channel_id=1, source_target_pairs={{0,8},{4,12},{8,0},{12,4},{1,9},{5,13},{9,1},{13,5},{2,10},{6,14},... | collective-permute-start | bytes 393224 | tf_op jit(solution)/shard_map/ppermute | solution.py:19
  13.3 5.7 %collective-permute-start.1 = (bf16[64,1024]{1,0:T(8,128)(2,1)S(1)}, bf16[64,1024]{1,0:T(8,128)(2,1)S(1)}, u32[]{:S(2)}, u32[]{:S(2)}) collective-permute-start(bf16[64,1024]{1,0:T(8,128)(2,1)S(1)} %bitcast.19), channel_id=1, source_target_pairs={{0,12},{4,0},{8,4},{12,8},{1,13},{5,1},{9,5},{13,9},{2,14},{6,2},{... | collective-permute-start | bytes 393224 | tf_op jit(solution)/shard_map/ppermute | solution.py:19
  14.1 5.6 %collective-permute-start = (bf16[64,1024]{1,0:T(8,128)(2,1)S(1)}, bf16[64,1024]{1,0:T(8,128)(2,1)S(1)}, u32[]{:S(2)}, u32[]{:S(2)}) collective-permute-start(bf16[64,1024]{1,0:T(8,128)(2,1)S(1)} %bitcast.20), channel_id=1, source_target_pairs={{0,4},{4,8},{8,12},{12,0},{1,5},{5,9},{9,13},{13,1},{2,6},{6,10},{... | collective-permute-start | bytes 393224 | tf_op jit(solution)/shard_map/ppermute | solution.py:19
  20.9 12.2 %collective-permute-start.6 = (bf16[256,1024]{1,0:T(8,128)(2,1)S(1)}, bf16[256,1024]{1,0:T(8,128)(2,1)S(1)}, u32[]{:S(2)}, u32[]{:S(2)}) collective-permute-start(bf16[256,1024]{1,0:T(8,128)(2,1)S(1)} %pad_maximum_fusion.refs_0_), channel_id=1, source_target_pairs={{0,48},{16,0},{32,16},{48,32},{1,49},{17,1},{33,17},{49,33},{2,50}... | collective-permute-start | bytes 1572872 | tf_op jit(solution)/shard_map/ppermute | solution.py:19
  23.6 12.4 %collective-permute-start.5 = (bf16[256,1024]{1,0:T(8,128)(2,1)S(1)}, bf16[256,1024]{1,0:T(8,128)(2,1)}, u32[]{:S(2)}, u32[]{:S(2)}) collective-permute-start(bf16[256,1024]{1,0:T(8,128)(2,1)S(1)} %pad_maximum_fusion.refs_0_), channel_id=1, source_target_pairs={{0,16},{16,32},{32,48},{48,0},{1,17},{17,33},{33,49},{49,1},{2,18}... | collective-permute-start | bytes 1572872 | tf_op jit(solution)/shard_map/ppermute | solution.py:19
  23.6 31.9 %all-to-all-start = ((bf16[128,8,512]{2,1,0:T(8,128)(2,1)}), bf16[128,8,512]{2,1,0:T(8,128)(2,1)S(1)}, u32[]{:S(2)}, u32[]{:S(2)}) async-start(bf16[128,8,512]{2,1,0:T(8,128)(2,1)} %bitcast.16), calls=%async_computation | async-start | bytes 2097152 | tf_op jit(solution)/shard_map/all_to_all | solution.py:23
  32.0 23.5 %collective-permute-start.3 = (bf16[2,128,1024]{2,1,0:T(8,128)(2,1)}, bf16[2,128,1024]{2,1,0:T(8,128)(2,1)S(1)}, u32[]{:S(2)}, u32[]{:S(2)}) collective-permute-start(bf16[2,128,1024]{2,1,0:T(8,128)(2,1)} %copy-done.7), channel_id=1, source_target_pairs={{0,2},{2,0},{1,3},{3,1},{4,6},{6,4},{5,7},{7,5},{8,10},{10,8},{9,1... | collective-permute-start | bytes 1572872 | tf_op jit(solution)/shard_map/ppermute | solution.py:27
  33.1 3.0 %copy-start.1 = (bf16[256,1024]{1,0:T(8,128)(2,1)}, bf16[256,1024]{1,0:T(8,128)(2,1)S(1)}, u32[]{:S(2)}) copy-start(bf16[256,1024]{1,0:T(8,128)(2,1)S(1)} %collective-permute-done.6.refs_2_) | copy-start | bytes 1572868
  36.9 18.6 %collective-permute-start.7 = (bf16[2,128,1024]{2,1,0:T(8,128)(2,1)}, bf16[2,128,1024]{2,1,0:T(8,128)(2,1)S(1)}, u32[]{:S(2)}, u32[]{:S(2)}) collective-permute-start(bf16[2,128,1024]{2,1,0:T(8,128)(2,1)} %slice.9), channel_id=1, source_target_pairs={{0,2},{2,0},{1,3},{3,1},{4,6},{6,4},{5,7},{7,5},{8,10},{10,8},{9,1... | collective-permute-start | bytes 1572872 | tf_op jit(solution)/shard_map/ppermute | solution.py:27
  52.3 8.3 %collective-permute-start.9 = (bf16[128,1024]{1,0:T(8,128)(2,1)}, bf16[128,1024]{1,0:T(8,128)(2,1)}, u32[]{:S(2)}, u32[]{:S(2)}) collective-permute-start(bf16[128,1024]{1,0:T(8,128)(2,1)} %slice.13), channel_id=1, source_target_pairs={{0,48},{16,0},{32,16},{48,32},{1,49},{17,1},{33,17},{49,33},{2,50}... | collective-permute-start | bytes 786440 | tf_op jit(solution)/shard_map/ppermute | solution.py:19
  54.7 9.1 %collective-permute-start.8 = (bf16[128,1024]{1,0:T(8,128)(2,1)}, bf16[128,1024]{1,0:T(8,128)(2,1)}, u32[]{:S(2)}, u32[]{:S(2)}) collective-permute-start(bf16[128,1024]{1,0:T(8,128)(2,1)} %slice.12), channel_id=1, source_target_pairs={{0,16},{16,32},{32,48},{48,0},{1,17},{17,33},{33,49},{49,1},{2,18}... | collective-permute-start | bytes 786440 | tf_op jit(solution)/shard_map/ppermute | solution.py:19
  55.5 11.0 %copy-start.2 = (bf16[256,1024]{1,0:T(8,128)(2,1)S(1)}, bf16[256,1024]{1,0:T(8,128)(2,1)}, u32[]{:S(2)}) copy-start(bf16[256,1024]{1,0:T(8,128)(2,1)} %copy-done.1) | copy-start | bytes 1572868
  55.5 1.0 %copy-start.4 = (bf16[1024,128]{1,0:T(8,128)(2,1)S(1)}, bf16[1024,128]{1,0:T(8,128)(2,1)}, u32[]{:S(2)}) copy-start(bf16[1024,128]{1,0:T(8,128)(2,1)} %left_ref.3) | copy-start | bytes 786436
  56.5 10.0 %copy-start.6 = (f32[128,1024]{1,0:T(8,128)S(1)}, f32[128,1024]{1,0:T(8,128)}, u32[]{:S(2)}) copy-start(f32[128,1024]{1,0:T(8,128)} %copy-done.5) | copy-start | bytes 1572868
  63.9 2.6 %collective-permute-start.10 = (bf16[512,512]{1,0:T(8,128)(2,1)S(1)}, bf16[512,512]{1,0:T(8,128)(2,1)S(1)}, u32[]{:S(2)}, u32[]{:S(2)}) collective-permute-start(bf16[512,512]{1,0:T(8,128)(2,1)S(1)} %get-tuple-element.32.own_ref), channel_id=1, source_target_pairs={{0,2},{2,0},{1,3},{3,1},{4,6},{6,4},{5,7},{7,5},{8,10},{10,8},{9,1... | collective-permute-start | bytes 1572872 | tf_op jit(solution)/shard_map/ppermute | solution.py:27
  69.7 2.8 %collective-permute-start.11 = (f32[512,512]{1,0:T(8,128)S(1)}, f32[512,512]{1,0:T(8,128)S(1)}, u32[]{:S(2)}, u32[]{:S(2)}) collective-permute-start(f32[512,512]{1,0:T(8,128)S(1)} %get-tuple-element.38), channel_id=1, source_target_pairs={{0,2},{2,0},{1,3},{3,1},{4,6},{6,4},{5,7},{7,5},{8,10},{10,8},{9,1... | collective-permute-start | bytes 3145736 | tf_op jit(solution)/shard_map/ppermute | solution.py:27

commit v19 on v17

--- a/solution.py
+++ b/solution.py
@@ -35,13 +35,13 @@
     return pltpu.CompilerParams(vmem_limit_bytes=mebibytes * 1024 * 1024)
 
 
-def pack(screened, left):
+def pack(screened):
     points, count = screened.shape
     plane, steps = count // 2, 4
     width = plane // 2
     rows = points // steps
 
-    def kernel(in_ref, left_ref, own_ref, near_ref, far_ref):
+    def kernel(in_ref, own_ref, near_ref, far_ref):
         core, zh = lax.axis_index("core"), lax.axis_index("zh")
         low = lax.broadcasted_iota(jnp.int32, (rows, 128), 1) < 64
         first = core == 0
@@ -56,69 +56,46 @@
                 mine, others = jnp.where(first, zero, one), jnp.where(first, one, zero)
                 if far == 0:
                     own_ref[:, here] = mine
-                    near_ref[0, :, here] = others.astype(BF16)
+                    near_ref[:, here] = others.astype(BF16)
                 else:
                     far_ref[0, :, here] = mine.astype(BF16)
                     far_ref[1, :, here] = others.astype(BF16)
-        for g in range(left_ref.shape[0] // points):
-            start = pl.multiple_of(g * points + pl.program_id(0) * rows, rows)
-            piece = left_ref[pl.ds(start, rows), :]
-            near_ref[1, :, pl.ds(g * points, points)] = piece
-            far_ref[2, :, pl.ds(g * points, points)] = piece
 
     return pl.pallas_call(
         kernel,
         grid=(steps,),
         out_shape=[
             jax.ShapeDtypeStruct((points, width), F32),
+            jax.ShapeDtypeStruct((points, width), BF16),
             jax.ShapeDtypeStruct((2, points, width), BF16),
-            jax.ShapeDtypeStruct((3, points, width), BF16),
         ],
-        in_specs=[
-            pl.BlockSpec((rows, count), lambda k: (k, 0)),
-            pl.BlockSpec(left.shape, lambda k: (0, 0)),
-        ],
+        in_specs=[pl.BlockSpec((rows, count), lambda k: (k, 0))],
         out_specs=[
             pl.BlockSpec((rows, width), lambda k: (k, 0)),
+            pl.BlockSpec((rows, width), lambda k: (k, 0)),
             pl.BlockSpec((2, rows, width), lambda k: (0, k, 0)),
-            pl.BlockSpec((3, rows, width), lambda k: (0, k, 0)),
         ],
         compiler_params=params(8),
         name="pack",
-    )(screened, left)
-
-
-def project(trial_half, left, near, far, passed):
-    states, points = left.shape
-    cols = trial_half.shape[1]
-
-    def kernel(trial_ref, left_ref, *refs):
-        boxes, (out_ref, psi_ref, sem) = refs[:3], refs[3:]
-        load = pltpu.make_async_copy(left_ref, psi_ref.at[:, :points], sem)
-        load.start()
-        for k in range(1, 4):
-            box = boxes[k - 1]
-            for g in range(states // points):
-                psi_ref[g * points : (g + 1) * points, k * points : (k + 1) * points] = box[
-                    box.shape[0] - 1, :, g * points : (g + 1) * points
-                ]
-        load.wait()
+    )(screened)
+
+
+def project(trial_half, psi):
+    count, cols = psi.shape[1], trial_half.shape[1]
+
+    def kernel(trial_ref, psi_ref, out_ref):
         out_ref[...] = lax.dot_general(
             psi_ref[...], trial_ref[...], (((0,), (0,)), ((), ())), preferred_element_type=F32
         ).astype(BF16)
 
     return pl.pallas_call(
         kernel,
-        out_shape=[
-            jax.ShapeDtypeStruct((4 * points, cols), BF16),
-            jax.ShapeDtypeStruct((states, 4 * points), BF16),
-        ],
-        in_specs=[vmem_spec(), pl.BlockSpec(memory_space=pl.ANY)] + [vmem_spec()] * 3,
-        out_specs=[vmem_spec()] * 2,
-        scratch_shapes=[pltpu.SemaphoreType.DMA],
+        out_shape=jax.ShapeDtypeStruct((count, cols), BF16),
+        in_specs=[vmem_spec()] * 2,
+        out_specs=vmem_spec(),
         compiler_params=params(12),
         name="project",
-    )(trial_half, left, near, far, passed)
+    )(trial_half, psi)
 
 
 def direct(proj_own, proj_other, lines, own, boxes):
@@ -152,7 +129,7 @@
             weighted = jnp.concatenate(
                 [
                     (
-                        (scr_refs[0][:, here] if j == 0 else scr_refs[j][0, :, here].astype(F32))
+                        (scr_refs[j][0, :, here] if j == 2 else scr_refs[j][:, here]).astype(F32)
                         * pair[j * points : (j + 1) * points]
                     ).astype(BF16)
                     for j in range(4)
@@ -227,21 +204,25 @@
     rows, states = trial.shape[1:]
     half = states // 2
     devices = lax.axis_size(TILE_VEC)
-    own, near, far = pack(screened, psi_v)
+    partner = lax.ppermute(psi_v, "zh", [(0, 1), (1, 0)])
+    own, near, far = pack(screened)
     block = psi_c[:, 0, :].T
     line = jnp.concatenate([block, shift(block, "x", 1), shift(block, "x", -1), shift(block, "x", 2)], 0)
     halves = trial[0].reshape(rows, 2, half).transpose(1, 0, 2)
     copies = jnp.broadcast_to(halves[None, :, None], (devices // 4, 2, 2, rows, half))
-    copies, near, far, line = lax.optimization_barrier((copies, near, far, line))
+    copies, near, far, line, partner = lax.optimization_barrier((copies, near, far, line, partner))
     trial_half = exchange(copies.reshape(devices, rows, half), TILE_VEC).reshape(-1, half)
-    near = swap(near)
     far = lax.ppermute(far, "zh", [(0, 1), (1, 0)])
     behind, ahead = shift(line, "y", 1), shift(line, "y", -1)
     middle = line.shape[0] // 2
     beyond = [shift(behind[:middle], "y", 1), shift(ahead[middle:], "y", -1)]
-    far, beyond = lax.optimization_barrier((far, beyond))
-    passed = swap(far[1:])
-    proj_own, psi = project(trial_half, psi_v, near, far, passed)
+    far, partner = lax.optimization_barrier((far, partner))
+    psi = jnp.concatenate([psi_v, swap(psi_v), partner, swap(partner)], 1)
+    near, psi, beyond = lax.optimization_barrier((near, psi, beyond))
+    near = swap(near)
+    trial_half, near = lax.optimization_barrier((trial_half, near))
+    passed = swap(far[1])
+    proj_own = project(trial_half, psi)
     proj_other = swap(proj_own)
     panel = [line, behind, ahead, *beyond]
     weighted, ordered, send = direct(proj_own, proj_other, panel, own, [near, far, passed])

time: 89.3 us -> 89.4 us (level)
  starting transfers between devices: 25.3 us -> 29.4 us
  local copies, waits for them, and re-layouts: 8.53 us -> 4.98 us
  blocking collectives: 27.1 us -> 25.9 us
  other arithmetic: 0.84 us -> 1.98 us
  waiting for transfers between devices: 20.2 us -> 19.1 us
    ppermute x0 -> x1, starting transfers between devices: none -> 4.43 us  [shards(): partner = lax.ppermute(psi_v, 'zh', [(0, 1), (1, 0)])]
    ppermute x1, starting transfers between devices: 3.6 us -> 0.22 us  [shards(): far = lax.ppermute(far, 'zh', [(0, 1), (1, 0)])]
    unnamed x32 -> x22, local copies, waits for them, and re-layouts: 6.53 us -> 3.79 us
    all_to_all x1, starting transfers between devices: 8.41 us -> 11.1 us  [exchange(): return lax.all_to_all(value, axes, split_axis=0, concat_axis=0, tiled=True)]
    ppermute x4 -> x6, starting transfers between devices: 2.69 us -> 3.88 us  [swap(): return lax.ppermute(value, 'core', [(0, 1), (1, 0)])]
    all_to_all x1, blocking collectives: 27.1 us -> 25.9 us  [exchange(): return lax.all_to_all(value, axes, split_axis=0, concat_axis=0, tiled=True)]
    concatenate x0 -> x1, other arithmetic: none -> 1.14 us  [shards(): psi = jnp.concatenate([psi_v, swap(psi_v), partner, swap(partner)], 1)]
    ppermute x7, waiting for transfers between devices: 15.4 us -> 14.4 us  [shift(): return lax.ppermute(value, axis, [(k, (k + by) % n) for k in range(n)])]
  transfers between devices with their start and end apart: 13 -> 16, of which waited for: 5 -> 6; matrix products, arithmetic and copies ran while one was open for 1% -> 1% of each run, Pallas kernels for 3% -> 3%
where the time goes in v19:
time: 89.4 us; the launch traced here: 89.1 us
  starting transfers between devices  29.4 us (33%)
  blocking collectives  25.9 us (29%)
  waiting for transfers between devices  19.1 us (21%)
  Pallas kernels  7.52 us (8%)
  local copies, waits for them, and re-layouts  4.98 us (6%)
  other arithmetic  1.98 us (2%)
    all_to_all x1, blocking collectives, exchange(): return lax.all_to_all(value, axes, split_axis=0, concat_axis=0, tiled=True)  25.9 us
    ppermute x7, waiting for transfers between devices, shift(): return lax.ppermute(value, axis, [(k, (k + by) % n) for k in range(n)])  14.4 us
    all_to_all x1, starting transfers between devices, exchange(): return lax.all_to_all(value, axes, split_axis=0, concat_axis=0, tiled=True)  11.1 us
    ppermute x7, starting transfers between devices, shift(): return lax.ppermute(value, axis, [(k, (k + by) % n) for k in range(n)])  9.82 us
    ppermute x6, waiting for transfers between devices, swap(): return lax.ppermute(value, 'core', [(0, 1), (1, 0)])  4.74 us
    ppermute x1, starting transfers between devices, shards(): partner = lax.ppermute(psi_v, 'zh', [(0, 1), (1, 0)])  4.43 us
    ppermute x6, starting transfers between devices, swap(): return lax.ppermute(value, 'core', [(0, 1), (1, 0)])  3.88 us
    unnamed x22, local copies, waits for them, and re-layouts  3.79 us
  transfers between devices with their start and end apart: 16, of which 6 were waited for; matrix products, arithmetic and copies ran while one was open for 1% of the time, Pallas kernels for 3%

profile of v19, /device:TPU:1, one launch (start us, length us, event | category | flops | bytes accessed | tf_op | source)
XLA Modules:
  0.0 89.1 jit_solution(3834738737905509711)
XLA Ops:
  0.0 4.4 %collective-permute-start.3 = (bf16[1024,128]{1,0:T(8,128)(2,1)}, bf16[1024,128]{1,0:T(8,128)(2,1)}, u32[]{:S(2)}, u32[]{:S(2)}) collective-permute-start(bf16[1024,128]{1,0:T(8,128)(2,1)} %param.5), channel_id=1, source_target_pairs={{0,64},{64,0},{1,65},{65,1},{2,66},{66,2},{3,67},{67,3},{4,68},{68... | collective-permute-start | bytes 786440 | tf_op jit(solution)/shard_map/ppermute | solution.py:207
  4.4 2.7 %collective-permute-start.2 = (bf16[64,1024]{1,0:T(8,128)(2,1)}, bf16[64,1024]{1,0:T(8,128)(2,1)S(1)}, u32[]{:S(2)}, u32[]{:S(2)}) collective-permute-start(bf16[64,1024]{1,0:T(8,128)(2,1)} %bitcast.20), channel_id=1, source_target_pairs={{0,8},{4,12},{8,0},{12,4},{1,9},{5,13},{9,1},{13,5},{2,10},{6,14},... | collective-permute-start | bytes 393224 | tf_op jit(solution)/shard_map/ppermute | solution.py:19
  7.2 0.9 collective-permute-start.1
  8.6 1.6 %copy-done = f32[128,4096]{1,0:T(8,128)S(1)} copy-done((f32[128,4096]{1,0:T(8,128)S(1)}, f32[128,4096]{1,0:T(8,128)}, u32[]{:S(2)}) %copy-start) | copy-done | bytes 2097176
  10.2 1.9 %pack.1 = (f32[128,1024]{1,0:T(8,128)S(1)}, bf16[128,1024]{1,0:T(8,128)(2,1)}, bf16[2,128,1024]{2,1,0:T(8,128)(2,1)}) custom-call(f32[128,4096]{1,0:T(8,128)S(1)} %copy-done), custom_call_target="tpu_custom_call" | custom-call | tf_op jit(solution)/shard_map/pack/pallas_call | solution.py:64
  12.1 0.8 copy-done.5
  13.6 1.1 %broadcast_in_dim.2 = bf16[32,2,2,8,512]{4,3,2,1,0:T(8,128)(2,1)} broadcast(bf16[2,8,512]{2,1,0:T(8,128)(2,1)S(1)} %bitcast.24), dimensions={1,3,4} | broadcast | bytes 1064960 | tf_op jit(solution)/shard_map/broadcast_in_dim | solution.py:212
  14.9 2.7 %collective-permute-start.9 = (bf16[256,1024]{1,0:T(8,128)(2,1)S(1)}, bf16[256,1024]{1,0:T(8,128)(2,1)S(1)}, u32[]{:S(2)}, u32[]{:S(2)}) collective-permute-start(bf16[256,1024]{1,0:T(8,128)(2,1)S(1)} %pad_maximum_fusion.1.refs_0_), channel_id=1, source_target_pairs={{0,48},{16,0},{32,16},{48,32},{1,49},{17,1},{33,17},{49,33},{2,50}... | collective-permute-start | bytes 1572872 | tf_op jit(solution)/shard_map/ppermute | solution.py:19
  17.7 11.1 %all-to-all-start = ((bf16[128,8,512]{2,1,0:T(8,128)(2,1)}), bf16[128,8,512]{2,1,0:T(8,128)(2,1)S(1)}, u32[]{:S(2)}, u32[]{:S(2)}) async-start(bf16[128,8,512]{2,1,0:T(8,128)(2,1)} %bitcast.18), calls=%async_computation | async-start | bytes 2097152 | tf_op jit(solution)/shard_map/all_to_all | solution.py:23
  28.8 1.1 %collective-permute-start.4 = (bf16[1024,128]{1,0:T(8,128)(2,1)}, bf16[1024,128]{1,0:T(8,128)(2,1)S(1)}, u32[]{:S(2)}, u32[]{:S(2)}) collective-permute-start(bf16[1024,128]{1,0:T(8,128)(2,1)} %param.5), channel_id=1, source_target_pairs={{0,2},{2,0},{1,3},{3,1},{4,6},{6,4},{5,7},{7,5},{8,10},{10,8},{9,1... | collective-permute-start | bytes 786440 | tf_op jit(solution)/shard_map/ppermute | solution.py:27
  29.9 0.8 collective-permute-start.6
  30.8 2.8 %collective-permute-start.10 = (bf16[128,1024]{1,0:T(8,128)(2,1)S(1)}, bf16[128,1024]{1,0:T(8,128)(2,1)S(1)}, u32[]{:S(2)}, u32[]{:S(2)}) collective-permute-start(bf16[128,1024]{1,0:T(8,128)(2,1)S(1)} %slice.13), channel_id=1, source_target_pairs={{0,48},{16,0},{32,16},{48,32},{1,49},{17,1},{33,17},{49,33},{2,50}... | collective-permute-start | bytes 786440 | tf_op jit(solution)/shard_map/ppermute | solution.py:19
  34.4 1.1 %pad_maximum_fusion.psi_ref = bf16[1024,512]{1,0:T(8,128)(2,1)S(1)} fusion(bf16[1024,128]{1,0:T(8,128)(2,1)S(1)} %collective-permute-done.6, bf16[1024,128]{1,0:T(8,128)(2,1)} %collective-permute-done.3, bf16[1024,128]{1,0:T(8,128)(2,1)S(1)} %collective-permute-done.4, bf16[1024,128]{1,0:T(8,128)(2,1)} %param.5), kind=kLoop, calls=%fused_computation.1 | loop fusion | flops 4194304 | bytes 2097152 | tf_op jit(solution)/shard_map/concatenate | solution.py:220
  35.5 11.5 %collective-permute-done.10.refs_4_ = bf16[128,1024]{1,0:T(8,128)(2,1)S(1)} collective-permute-done((bf16[128,1024]{1,0:T(8,128)(2,1)S(1)}, bf16[128,1024]{1,0:T(8,128)(2,1)S(1)}, u32[]{:S(2)}, u32[]{:S(2)}) %collective-permute-start.10) | collective-permute-done | bytes 262176 | tf_op jit(solution)/shard_map/ppermute | solution.py:19
  47.0 2.3 %collective-permute-done.8.refs_3_ = bf16[128,1024]{1,0:T(8,128)(2,1)S(1)} collective-permute-done((bf16[128,1024]{1,0:T(8,128)(2,1)S(1)}, bf16[128,1024]{1,0:T(8,128)(2,1)S(1)}, u32[]{:S(2)}, u32[]{:S(2)}) %collective-permute-start.8) | collective-permute-done | bytes 262176 | tf_op jit(solution)/shard_map/ppermute | solution.py:19
  50.0 0.8 collective-permute-start.11
  50.8 1.5 %collective-permute-done.11.refs_6_ = bf16[128,1024]{1,0:T(8,128)(2,1)} collective-permute-done((bf16[128,1024]{1,0:T(8,128)(2,1)}, bf16[128,1024]{1,0:T(8,128)(2,1)}, u32[]{:S(2)}, u32[]{:S(2)}) %collective-permute-start.11) | collective-permute-done | bytes 262176 | tf_op jit(solution)/shard_map/ppermute | solution.py:27
  52.3 0.7 project.1.own_ref
  53.7 1.7 %collective-permute-done.13.refs_8_ = bf16[128,1024]{1,0:T(8,128)(2,1)S(1)} collective-permute-done((bf16[128,1024]{1,0:T(8,128)(2,1)S(1)}, bf16[128,1024]{1,0:T(8,128)(2,1)S(1)}, u32[]{:S(2)}, u32[]{:S(2)}) %collective-permute-start.13) | collective-permute-done | bytes 262176 | tf_op jit(solution)/shard_map/ppermute | solution.py:27
  55.4 2.9 %direct.1 = (bf16[512,1024]{1,0:T(8,128)(2,1)S(1)}, bf16[1024,1024]{1,0:T(8,128)(2,1)S(1)}, f32[512,512]{1,0:T(8,128)S(1)}) custom-call(bf16[512,512]{1,0:T(8,128)(2,1)S(1)} %project.1.own_ref, bf16[512,512]{1,0:T(8,128)(2,1)S(1)} %collective-permute-done.12.other_ref, bf16[256,1024]{1,0:T(8,128)(2,1)S(1)} %pad_maximum_fusion.1.refs_0_, ...), custom_call_target="tpu_custom_call" | custom-call | tf_op jit(solution)/shard_map/direct/pallas_call | solution.py:142
  59.5 1.6 %collective-permute-done.14.got_ref = f32[512,512]{1,0:T(8,128)S(1)} collective-permute-done((f32[512,512]{1,0:T(8,128)S(1)}, f32[512,512]{1,0:T(8,128)S(1)}, u32[]{:S(2)}, u32[]{:S(2)}) %collective-permute-start.14) | collective-permute-done | bytes 1048608 | tf_op jit(solution)/shard_map/ppermute | solution.py:27
  61.1 1.3 %finish.1 = bf16[1024,512]{1,0:T(8,128)(2,1)S(1)} custom-call(bf16[1024,512]{1,0:T(8,128)(2,1)S(1)} %pad_maximum_fusion.psi_ref, f32[512,512]{1,0:T(8,128)S(1)} %own_half.1.keep_ref, f32[512,512]{1,0:T(8,128)S(1)} %collective-permute-done.14.got_ref), custom_call_target="tpu_custom_call" | custom-call | tf_op jit(solution)/shard_map/finish/pallas_call | solution.py:192
  62.4 25.9 %all_to_all.10 = bf16[128,8,512]{2,1,0:T(8,128)(2,1)S(1)} all-to-all(bf16[128,8,512]{2,1,0:T(8,128)(2,1)S(1)} %bitcast.17), channel_id=1, replica_groups=mesh['zh'=2,'y'=4,'x'=4,'core'=2,'zl'=2] {'zh','y','x','core','zl'}, dimensions={0} | all-to-all | bytes 2097152 | tf_op jit(solution)/shard_map/all_to_all | solution.py:23
  88.3 0.8 convert_reduce_fusion
  (43 shorter events, 4.9 us)
Async XLA Ops:
  0.0 13.6 %collective-permute-start.3 = (bf16[1024,128]{1,0:T(8,128)(2,1)}, bf16[1024,128]{1,0:T(8,128)(2,1)}, u32[]{:S(2)}, u32[]{:S(2)}) collective-permute-start(bf16[1024,128]{1,0:T(8,128)(2,1)} %param.5), channel_id=1, source_target_pairs={{0,64},{64,0},{1,65},{65,1},{2,66},{66,2},{3,67},{67,3},{4,68},{68... | collective-permute-start | bytes 786440 | tf_op jit(solution)/shard_map/ppermute | solution.py:207
  4.4 8.5 %collective-permute-start.2 = (bf16[64,1024]{1,0:T(8,128)(2,1)}, bf16[64,1024]{1,0:T(8,128)(2,1)S(1)}, u32[]{:S(2)}, u32[]{:S(2)}) collective-permute-start(bf16[64,1024]{1,0:T(8,128)(2,1)} %bitcast.20), channel_id=1, source_target_pairs={{0,8},{4,12},{8,0},{12,4},{1,9},{5,13},{9,1},{13,5},{2,10},{6,14},... | collective-permute-start | bytes 393224 | tf_op jit(solution)/shard_map/ppermute | solution.py:19
  7.2 5.7 %collective-permute-start.1 = (bf16[64,1024]{1,0:T(8,128)(2,1)}, bf16[64,1024]{1,0:T(8,128)(2,1)S(1)}, u32[]{:S(2)}, u32[]{:S(2)}) collective-permute-start(bf16[64,1024]{1,0:T(8,128)(2,1)} %bitcast.21), channel_id=1, source_target_pairs={{0,12},{4,0},{8,4},{12,8},{1,13},{5,1},{9,5},{13,9},{2,14},{6,2},{... | collective-permute-start | bytes 393224 | tf_op jit(solution)/shard_map/ppermute | solution.py:19
  8.0 5.5 %collective-permute-start = (bf16[64,1024]{1,0:T(8,128)(2,1)}, bf16[64,1024]{1,0:T(8,128)(2,1)S(1)}, u32[]{:S(2)}, u32[]{:S(2)}) collective-permute-start(bf16[64,1024]{1,0:T(8,128)(2,1)} %bitcast.22), channel_id=1, source_target_pairs={{0,4},{4,8},{8,12},{12,0},{1,5},{5,9},{9,13},{13,1},{2,6},{6,10},{... | collective-permute-start | bytes 393224 | tf_op jit(solution)/shard_map/ppermute | solution.py:19
  8.6 1.6 %copy-start = (f32[128,4096]{1,0:T(8,128)S(1)}, f32[128,4096]{1,0:T(8,128)}, u32[]{:S(2)}) copy-start(f32[128,4096]{1,0:T(8,128)} %in_ref.1) | copy-start | bytes 6291460
  10.2 3.3 %copy-start.9 = (bf16[1024,1,64]{0,2,1:T(8,128)(2,1)S(1)}, bf16[1024,1,64]{0,2,1:T(8,128)(2,1)}, u32[]{:S(2)}) copy-start(bf16[1024,1,64]{0,2,1:T(8,128)(2,1)} %param.6) | copy-start | bytes 393220
  10.2 3.3 %copy-start.10 = (bf16[1,8,1024]{2,1,0:T(8,128)(2,1)S(1)}, bf16[1,8,1024]{2,1,0:T(8,128)(2,1)}, u32[]{:S(2)}) copy-start(bf16[1,8,1024]{2,1,0:T(8,128)(2,1)} %param.4) | copy-start | bytes 49156
  14.7 15.2 %collective-permute-start.5 = (bf16[2,128,1024]{2,1,0:T(8,128)(2,1)}, bf16[2,128,1024]{2,1,0:T(8,128)(2,1)S(1)}, u32[]{:S(2)}, u32[]{:S(2)}) collective-permute-start(bf16[2,128,1024]{2,1,0:T(8,128)(2,1)} %get-tuple-element.27), channel_id=1, source_target_pairs={{0,64},{64,0},{1,65},{65,1},{2,66},{66,2},{3,67},{67,3},{4,68},{68... | collective-permute-start | bytes 1572872 | tf_op jit(solution)/shard_map/ppermute | solution.py:215
  14.9 15.8 %collective-permute-start.9 = (bf16[256,1024]{1,0:T(8,128)(2,1)S(1)}, bf16[256,1024]{1,0:T(8,128)(2,1)S(1)}, u32[]{:S(2)}, u32[]{:S(2)}) collective-permute-start(bf16[256,1024]{1,0:T(8,128)(2,1)S(1)} %pad_maximum_fusion.1.refs_0_), channel_id=1, source_target_pairs={{0,48},{16,0},{32,16},{48,32},{1,49},{17,1},{33,17},{49,33},{2,50}... | collective-permute-start | bytes 1572872 | tf_op jit(solution)/shard_map/ppermute | solution.py:19
  17.7 15.9 %collective-permute-start.7 = (bf16[256,1024]{1,0:T(8,128)(2,1)S(1)}, bf16[256,1024]{1,0:T(8,128)(2,1)S(1)}, u32[]{:S(2)}, u32[]{:S(2)}) collective-permute-start(bf16[256,1024]{1,0:T(8,128)(2,1)S(1)} %pad_maximum_fusion.1.refs_0_), channel_id=1, source_target_pairs={{0,16},{16,32},{32,48},{48,0},{1,17},{17,33},{33,49},{49,1},{2,18}... | collective-permute-start | bytes 1572872 | tf_op jit(solution)/shard_map/ppermute | solution.py:19
  17.7 33.1 %all-to-all-start = ((bf16[128,8,512]{2,1,0:T(8,128)(2,1)}), bf16[128,8,512]{2,1,0:T(8,128)(2,1)S(1)}, u32[]{:S(2)}, u32[]{:S(2)}) async-start(bf16[128,8,512]{2,1,0:T(8,128)(2,1)} %bitcast.18), calls=%async_computation | async-start | bytes 2097152 | tf_op jit(solution)/shard_map/all_to_all | solution.py:23
  28.8 4.9 %collective-permute-start.4 = (bf16[1024,128]{1,0:T(8,128)(2,1)}, bf16[1024,128]{1,0:T(8,128)(2,1)S(1)}, u32[]{:S(2)}, u32[]{:S(2)}) collective-permute-start(bf16[1024,128]{1,0:T(8,128)(2,1)} %param.5), channel_id=1, source_target_pairs={{0,2},{2,0},{1,3},{3,1},{4,6},{6,4},{5,7},{7,5},{8,10},{10,8},{9,1... | collective-permute-start | bytes 786440 | tf_op jit(solution)/shard_map/ppermute | solution.py:27
  29.9 4.5 %collective-permute-start.6 = (bf16[1024,128]{1,0:T(8,128)(2,1)}, bf16[1024,128]{1,0:T(8,128)(2,1)S(1)}, u32[]{:S(2)}, u32[]{:S(2)}) collective-permute-start(bf16[1024,128]{1,0:T(8,128)(2,1)} %collective-permute-done.3), channel_id=1, source_target_pairs={{0,2},{2,0},{1,3},{3,1},{4,6},{6,4},{5,7},{7,5},{8,10},{10,8},{9,1... | collective-permute-start | bytes 786440 | tf_op jit(solution)/shard_map/ppermute | solution.py:27
  30.8 3.0 %copy-start.1 = (bf16[256,1024]{1,0:T(8,128)(2,1)}, bf16[256,1024]{1,0:T(8,128)(2,1)S(1)}, u32[]{:S(2)}) copy-start(bf16[256,1024]{1,0:T(8,128)(2,1)S(1)} %collective-permute-done.9.refs_2_) | copy-start | bytes 1572868
  30.8 16.2 %collective-permute-start.10 = (bf16[128,1024]{1,0:T(8,128)(2,1)S(1)}, bf16[128,1024]{1,0:T(8,128)(2,1)S(1)}, u32[]{:S(2)}, u32[]{:S(2)}) collective-permute-start(bf16[128,1024]{1,0:T(8,128)(2,1)S(1)} %slice.13), channel_id=1, source_target_pairs={{0,48},{16,0},{32,16},{48,32},{1,49},{17,1},{33,17},{49,33},{2,50}... | collective-permute-start | bytes 786440 | tf_op jit(solution)/shard_map/ppermute | solution.py:19
  33.6 15.7 %collective-permute-start.8 = (bf16[128,1024]{1,0:T(8,128)(2,1)S(1)}, bf16[128,1024]{1,0:T(8,128)(2,1)S(1)}, u32[]{:S(2)}, u32[]{:S(2)}) collective-permute-start(bf16[128,1024]{1,0:T(8,128)(2,1)S(1)} %slice.12), channel_id=1, source_target_pairs={{0,16},{16,32},{32,48},{48,0},{1,17},{17,33},{33,49},{49,1},{2,18}... | collective-permute-start | bytes 786440 | tf_op jit(solution)/shard_map/ppermute | solution.py:19
  50.0 2.3 %collective-permute-start.11 = (bf16[128,1024]{1,0:T(8,128)(2,1)}, bf16[128,1024]{1,0:T(8,128)(2,1)}, u32[]{:S(2)}, u32[]{:S(2)}) collective-permute-start(bf16[128,1024]{1,0:T(8,128)(2,1)} %get-tuple-element.33), channel_id=1, source_target_pairs={{0,2},{2,0},{1,3},{3,1},{4,6},{6,4},{5,7},{7,5},{8,10},{10,8},{9,1... | collective-permute-start | bytes 786440 | tf_op jit(solution)/shard_map/ppermute | solution.py:27
  50.8 4.6 %copy-start.2 = (bf16[256,1024]{1,0:T(8,128)(2,1)S(1)}, bf16[256,1024]{1,0:T(8,128)(2,1)}, u32[]{:S(2)}) copy-start(bf16[256,1024]{1,0:T(8,128)(2,1)} %copy-done.1) | copy-start | bytes 1572868
  50.8 4.6 %copy-start.4 = (bf16[256,1024]{1,0:T(8,128)(2,1)S(1)}, bf16[256,1024]{1,0:T(8,128)(2,1)}, u32[]{:S(2)}) copy-start(bf16[256,1024]{1,0:T(8,128)(2,1)} %copy-done.3) | copy-start | bytes 1572868
  50.8 4.6 %copy-start.6 = (f32[128,1024]{1,0:T(8,128)S(1)}, f32[128,1024]{1,0:T(8,128)}, u32[]{:S(2)}) copy-start(f32[128,1024]{1,0:T(8,128)} %copy-done.5) | copy-start | bytes 1572868
  50.8 4.6 %copy-start.8 = (bf16[128,1024]{1,0:T(8,128)(2,1)S(1)}, bf16[128,1024]{1,0:T(8,128)(2,1)}, u32[]{:S(2)}) copy-start(bf16[128,1024]{1,0:T(8,128)(2,1)} %copy-done.7) | copy-start | bytes 786436
  53.0 2.4 %collective-permute-start.12 = (bf16[512,512]{1,0:T(8,128)(2,1)S(1)}, bf16[512,512]{1,0:T(8,128)(2,1)S(1)}, u32[]{:S(2)}, u32[]{:S(2)}) collective-permute-start(bf16[512,512]{1,0:T(8,128)(2,1)S(1)} %project.1.own_ref), channel_id=1, source_target_pairs={{0,2},{2,0},{1,3},{3,1},{4,6},{6,4},{5,7},{7,5},{8,10},{10,8},{9,1... | collective-permute-start | bytes 1572872 | tf_op jit(solution)/shard_map/ppermute | solution.py:27
  53.5 1.9 %collective-permute-start.13 = (bf16[128,1024]{1,0:T(8,128)(2,1)S(1)}, bf16[128,1024]{1,0:T(8,128)(2,1)S(1)}, u32[]{:S(2)}, u32[]{:S(2)}) collective-permute-start(bf16[128,1024]{1,0:T(8,128)(2,1)S(1)} %slice_bitcast_fusion), channel_id=1, source_target_pairs={{0,2},{2,0},{1,3},{3,1},{4,6},{6,4},{5,7},{7,5},{8,10},{10,8},{9,1... | collective-permute-start | bytes 786440 | tf_op jit(solution)/shard_map/ppermute | solution.py:27
  58.3 2.8 %collective-permute-start.14 = (f32[512,512]{1,0:T(8,128)S(1)}, f32[512,512]{1,0:T(8,128)S(1)}, u32[]{:S(2)}, u32[]{:S(2)}) collective-permute-start(f32[512,512]{1,0:T(8,128)S(1)} %get-tuple-element.42), channel_id=1, source_target_pairs={{0,2},{2,0},{1,3},{3,1},{4,6},{6,4},{5,7},{7,5},{8,10},{10,8},{9,1... | collective-permute-start | bytes 3145736 | tf_op jit(solution)/shard_map/ppermute | solution.py:27
  (3 other events, 2.3 us)

commit v20 on v19

--- a/solution.py
+++ b/solution.py
@@ -216,11 +216,11 @@
     behind, ahead = shift(line, "y", 1), shift(line, "y", -1)
     middle = line.shape[0] // 2
     beyond = [shift(behind[:middle], "y", 1), shift(ahead[middle:], "y", -1)]
-    far, partner = lax.optimization_barrier((far, partner))
+    far, partner, *_ = lax.optimization_barrier((far, partner, behind, ahead))
     psi = jnp.concatenate([psi_v, swap(psi_v), partner, swap(partner)], 1)
-    near, psi, beyond = lax.optimization_barrier((near, psi, beyond))
+    near, psi = lax.optimization_barrier((near, psi))
     near = swap(near)
-    trial_half, near = lax.optimization_barrier((trial_half, near))
+    trial_half, near, beyond = lax.optimization_barrier((trial_half, near, beyond))
     passed = swap(far[1])
     proj_own = project(trial_half, psi)
     proj_other = swap(proj_own)

time: 89.4 us -> 90.3 us (1.010)
  waiting for transfers between devices: 19.1 us -> 13.2 us
  starting transfers between devices: 29.4 us -> 34.3 us
  blocking collectives: 25.9 us -> 28.5 us
    ppermute x6, starting transfers between devices: 3.88 us -> 10 us  [swap(): return lax.ppermute(value, 'core', [(0, 1), (1, 0)])]
    ppermute x7, waiting for transfers between devices: 14.4 us -> 9.85 us  [shift(): return lax.ppermute(value, axis, [(k, (k + by) % n) for k in range(n)])]
    all_to_all x1, blocking collectives: 25.9 us -> 28.5 us  [exchange(): return lax.all_to_all(value, axes, split_axis=0, concat_axis=0, tiled=True)]
    ppermute x6, waiting for transfers between devices: 4.74 us -> 3.36 us  [swap(): return lax.ppermute(value, 'core', [(0, 1), (1, 0)])]
    ppermute x7, starting transfers between devices: 9.82 us -> 8.55 us  [shift(): return lax.ppermute(value, axis, [(k, (k + by) % n) for k in range(n)])]
  transfers between devices with their start and end apart: 16 -> 16, of which waited for: 6 -> 5; matrix products, arithmetic and copies ran while one was open for 1% -> 1% of each run, Pallas kernels for 3% -> 3%
where the time goes in v20:
time: 90.3 us; the launch traced here: 90 us
  starting transfers between devices  34.3 us (38%)
  blocking collectives  28.5 us (32%)
  waiting for transfers between devices  13.2 us (15%)
  Pallas kernels  7.52 us (8%)
  local copies, waits for them, and re-layouts  4.33 us (5%)
  other arithmetic  1.98 us (2%)
    all_to_all x1, blocking collectives, exchange(): return lax.all_to_all(value, axes, split_axis=0, concat_axis=0, tiled=True)  28.5 us
    all_to_all x1, starting transfers between devices, exchange(): return lax.all_to_all(value, axes, split_axis=0, concat_axis=0, tiled=True)  11.1 us
    ppermute x6, starting transfers between devices, swap(): return lax.ppermute(value, 'core', [(0, 1), (1, 0)])  10 us
    ppermute x7, waiting for transfers between devices, shift(): return lax.ppermute(value, axis, [(k, (k + by) % n) for k in range(n)])  9.85 us
    ppermute x7, starting transfers between devices, shift(): return lax.ppermute(value, axis, [(k, (k + by) % n) for k in range(n)])  8.55 us
    ppermute x1, starting transfers between devices, shards(): partner = lax.ppermute(psi_v, 'zh', [(0, 1), (1, 0)])  4.43 us
    ppermute x6, waiting for transfers between devices, swap(): return lax.ppermute(value, 'core', [(0, 1), (1, 0)])  3.36 us
    unnamed x22, local copies, waits for them, and re-layouts  3.14 us
  transfers between devices with their start and end apart: 16, of which 5 were waited for; matrix products, arithmetic and copies ran while one was open for 1% of the time, Pallas kernels for 3%

profile of v20, /device:TPU:1, one launch (start us, length us, event | category | flops | bytes accessed | tf_op | source)
XLA Modules:
  0.0 90.0 jit_solution(15180033720032309050)
XLA Ops:
  0.0 4.4 %collective-permute-start.3 = (bf16[1024,128]{1,0:T(8,128)(2,1)}, bf16[1024,128]{1,0:T(8,128)(2,1)}, u32[]{:S(2)}, u32[]{:S(2)}) collective-permute-start(bf16[1024,128]{1,0:T(8,128)(2,1)} %param.5), channel_id=1, source_target_pairs={{0,64},{64,0},{1,65},{65,1},{2,66},{66,2},{3,67},{67,3},{4,68},{68... | collective-permute-start | bytes 786440 | tf_op jit(solution)/shard_map/ppermute | solution.py:207
  4.4 2.7 %collective-permute-start.2 = (bf16[64,1024]{1,0:T(8,128)(2,1)}, bf16[64,1024]{1,0:T(8,128)(2,1)S(1)}, u32[]{:S(2)}, u32[]{:S(2)}) collective-permute-start(bf16[64,1024]{1,0:T(8,128)(2,1)} %bitcast.20), channel_id=1, source_target_pairs={{0,8},{4,12},{8,0},{12,4},{1,9},{5,13},{9,1},{13,5},{2,10},{6,14},... | collective-permute-start | bytes 393224 | tf_op jit(solution)/shard_map/ppermute | solution.py:19
  7.2 0.9 collective-permute-start.1
  8.6 1.6 %copy-done = f32[128,4096]{1,0:T(8,128)S(1)} copy-done((f32[128,4096]{1,0:T(8,128)S(1)}, f32[128,4096]{1,0:T(8,128)}, u32[]{:S(2)}) %copy-start) | copy-done | bytes 2097176
  10.2 1.9 %pack.1 = (f32[128,1024]{1,0:T(8,128)S(1)}, bf16[128,1024]{1,0:T(8,128)(2,1)}, bf16[2,128,1024]{2,1,0:T(8,128)(2,1)}) custom-call(f32[128,4096]{1,0:T(8,128)S(1)} %copy-done), custom_call_target="tpu_custom_call" | custom-call | tf_op jit(solution)/shard_map/pack/pallas_call | solution.py:64
  12.1 0.8 copy-done.5
  13.6 1.1 %broadcast_in_dim.2 = bf16[32,2,2,8,512]{4,3,2,1,0:T(8,128)(2,1)} broadcast(bf16[2,8,512]{2,1,0:T(8,128)(2,1)S(1)} %bitcast.24), dimensions={1,3,4} | broadcast | bytes 1064960 | tf_op jit(solution)/shard_map/broadcast_in_dim | solution.py:212
  14.9 2.7 %collective-permute-start.7 = (bf16[256,1024]{1,0:T(8,128)(2,1)S(1)}, bf16[256,1024]{1,0:T(8,128)(2,1)S(1)}, u32[]{:S(2)}, u32[]{:S(2)}) collective-permute-start(bf16[256,1024]{1,0:T(8,128)(2,1)S(1)} %pad_maximum_fusion.1.refs_0_), channel_id=1, source_target_pairs={{0,48},{16,0},{32,16},{48,32},{1,49},{17,1},{33,17},{49,33},{2,50}... | collective-permute-start | bytes 1572872 | tf_op jit(solution)/shard_map/ppermute | solution.py:19
  17.7 11.1 %all-to-all-start = ((bf16[128,8,512]{2,1,0:T(8,128)(2,1)}), bf16[128,8,512]{2,1,0:T(8,128)(2,1)S(1)}, u32[]{:S(2)}, u32[]{:S(2)}) async-start(bf16[128,8,512]{2,1,0:T(8,128)(2,1)} %bitcast.18), calls=%async_computation | async-start | bytes 2097152 | tf_op jit(solution)/shard_map/all_to_all | solution.py:23
  28.8 1.1 %collective-permute-start.4 = (bf16[1024,128]{1,0:T(8,128)(2,1)}, bf16[1024,128]{1,0:T(8,128)(2,1)S(1)}, u32[]{:S(2)}, u32[]{:S(2)}) collective-permute-start(bf16[1024,128]{1,0:T(8,128)(2,1)} %param.5), channel_id=1, source_target_pairs={{0,2},{2,0},{1,3},{3,1},{4,6},{6,4},{5,7},{7,5},{8,10},{10,8},{9,1... | collective-permute-start | bytes 786440 | tf_op jit(solution)/shard_map/ppermute | solution.py:27
  29.9 7.1 %collective-permute-start.8 = (bf16[1024,128]{1,0:T(8,128)(2,1)}, bf16[1024,128]{1,0:T(8,128)(2,1)S(1)}, u32[]{:S(2)}, u32[]{:S(2)}) collective-permute-start(bf16[1024,128]{1,0:T(8,128)(2,1)} %collective-permute-done.3), channel_id=1, source_target_pairs={{0,2},{2,0},{1,3},{3,1},{4,6},{6,4},{5,7},{7,5},{8,10},{10,8},{9,1... | collective-permute-start | bytes 786440 | tf_op jit(solution)/shard_map/ppermute | solution.py:27
  37.5 1.2 %collective-permute-start.10 = (bf16[128,1024]{1,0:T(8,128)(2,1)S(1)}, bf16[128,1024]{1,0:T(8,128)(2,1)S(1)}, u32[]{:S(2)}, u32[]{:S(2)}) collective-permute-start(bf16[128,1024]{1,0:T(8,128)(2,1)S(1)} %slice.12), channel_id=1, source_target_pairs={{0,16},{16,32},{32,48},{48,0},{1,17},{17,33},{33,49},{49,1},{2,18}... | collective-permute-start | bytes 786440 | tf_op jit(solution)/shard_map/ppermute | solution.py:19
  38.7 1.1 %pad_maximum_fusion.psi_ref = bf16[1024,512]{1,0:T(8,128)(2,1)S(1)} fusion(bf16[1024,128]{1,0:T(8,128)(2,1)S(1)} %collective-permute-done.8, bf16[1024,128]{1,0:T(8,128)(2,1)} %collective-permute-done.3, bf16[1024,128]{1,0:T(8,128)(2,1)S(1)} %collective-permute-done.4, bf16[1024,128]{1,0:T(8,128)(2,1)} %param.5), kind=kLoop, calls=%fused_computation.1 | loop fusion | flops 4194304 | bytes 2097152 | tf_op jit(solution)/shard_map/concatenate | solution.py:220
  40.5 8.2 %collective-permute-done.11.refs_4_ = bf16[128,1024]{1,0:T(8,128)(2,1)S(1)} collective-permute-done((bf16[128,1024]{1,0:T(8,128)(2,1)S(1)}, bf16[128,1024]{1,0:T(8,128)(2,1)S(1)}, u32[]{:S(2)}, u32[]{:S(2)}) %collective-permute-start.11) | collective-permute-done | bytes 262176 | tf_op jit(solution)/shard_map/ppermute | solution.py:19
  48.7 1.0 %collective-permute-done.10.refs_3_ = bf16[128,1024]{1,0:T(8,128)(2,1)S(1)} collective-permute-done((bf16[128,1024]{1,0:T(8,128)(2,1)S(1)}, bf16[128,1024]{1,0:T(8,128)(2,1)S(1)}, u32[]{:S(2)}, u32[]{:S(2)}) %collective-permute-start.10) | collective-permute-done | bytes 262176 | tf_op jit(solution)/shard_map/ppermute | solution.py:19
  49.7 0.7 copy-done.7
  50.5 0.7 project.1.own_ref
  51.9 1.8 %collective-permute-done.13.refs_8_ = bf16[128,1024]{1,0:T(8,128)(2,1)S(1)} collective-permute-done((bf16[128,1024]{1,0:T(8,128)(2,1)S(1)}, bf16[128,1024]{1,0:T(8,128)(2,1)S(1)}, u32[]{:S(2)}, u32[]{:S(2)}) %collective-permute-start.13) | collective-permute-done | bytes 262176 | tf_op jit(solution)/shard_map/ppermute | solution.py:27
  53.7 2.9 %direct.1 = (bf16[512,1024]{1,0:T(8,128)(2,1)S(1)}, bf16[1024,1024]{1,0:T(8,128)(2,1)S(1)}, f32[512,512]{1,0:T(8,128)S(1)}) custom-call(bf16[512,512]{1,0:T(8,128)(2,1)S(1)} %project.1.own_ref, bf16[512,512]{1,0:T(8,128)(2,1)S(1)} %collective-permute-done.12.other_ref, bf16[256,1024]{1,0:T(8,128)(2,1)S(1)} %pad_maximum_fusion.1.refs_0_, ...), custom_call_target="tpu_custom_call" | custom-call | tf_op jit(solution)/shard_map/direct/pallas_call | solution.py:142
  57.1 0.7 own_half.1.keep_ref
  57.8 1.6 %collective-permute-done.14.got_ref = f32[512,512]{1,0:T(8,128)S(1)} collective-permute-done((f32[512,512]{1,0:T(8,128)S(1)}, f32[512,512]{1,0:T(8,128)S(1)}, u32[]{:S(2)}, u32[]{:S(2)}) %collective-permute-start.14) | collective-permute-done | bytes 1048608 | tf_op jit(solution)/shard_map/ppermute | solution.py:27
  59.4 1.3 %finish.1 = bf16[1024,512]{1,0:T(8,128)(2,1)S(1)} custom-call(bf16[1024,512]{1,0:T(8,128)(2,1)S(1)} %pad_maximum_fusion.psi_ref, f32[512,512]{1,0:T(8,128)S(1)} %own_half.1.keep_ref, f32[512,512]{1,0:T(8,128)S(1)} %collective-permute-done.14.got_ref), custom_call_target="tpu_custom_call" | custom-call | tf_op jit(solution)/shard_map/finish/pallas_call | solution.py:192
  60.7 28.5 %all_to_all.10 = bf16[128,8,512]{2,1,0:T(8,128)(2,1)S(1)} all-to-all(bf16[128,8,512]{2,1,0:T(8,128)(2,1)S(1)} %bitcast.17), channel_id=1, replica_groups=mesh['zh'=2,'y'=4,'x'=4,'core'=2,'zl'=2] {'zh','y','x','core','zl'}, dimensions={0} | all-to-all | bytes 2097152 | tf_op jit(solution)/shard_map/all_to_all | solution.py:23
  89.2 0.8 convert_reduce_fusion
  (43 shorter events, 3.8 us)
Async XLA Ops:
  0.0 13.6 %collective-permute-start.3 = (bf16[1024,128]{1,0:T(8,128)(2,1)}, bf16[1024,128]{1,0:T(8,128)(2,1)}, u32[]{:S(2)}, u32[]{:S(2)}) collective-permute-start(bf16[1024,128]{1,0:T(8,128)(2,1)} %param.5), channel_id=1, source_target_pairs={{0,64},{64,0},{1,65},{65,1},{2,66},{66,2},{3,67},{67,3},{4,68},{68... | collective-permute-start | bytes 786440 | tf_op jit(solution)/shard_map/ppermute | solution.py:207
  4.4 8.5 %collective-permute-start.2 = (bf16[64,1024]{1,0:T(8,128)(2,1)}, bf16[64,1024]{1,0:T(8,128)(2,1)S(1)}, u32[]{:S(2)}, u32[]{:S(2)}) collective-permute-start(bf16[64,1024]{1,0:T(8,128)(2,1)} %bitcast.20), channel_id=1, source_target_pairs={{0,8},{4,12},{8,0},{12,4},{1,9},{5,13},{9,1},{13,5},{2,10},{6,14},... | collective-permute-start | bytes 393224 | tf_op jit(solution)/shard_map/ppermute | solution.py:19
  7.2 5.7 %collective-permute-start.1 = (bf16[64,1024]{1,0:T(8,128)(2,1)}, bf16[64,1024]{1,0:T(8,128)(2,1)S(1)}, u32[]{:S(2)}, u32[]{:S(2)}) collective-permute-start(bf16[64,1024]{1,0:T(8,128)(2,1)} %bitcast.21), channel_id=1, source_target_pairs={{0,12},{4,0},{8,4},{12,8},{1,13},{5,1},{9,5},{13,9},{2,14},{6,2},{... | collective-permute-start | bytes 393224 | tf_op jit(solution)/shard_map/ppermute | solution.py:19
  8.0 5.5 %collective-permute-start = (bf16[64,1024]{1,0:T(8,128)(2,1)}, bf16[64,1024]{1,0:T(8,128)(2,1)S(1)}, u32[]{:S(2)}, u32[]{:S(2)}) collective-permute-start(bf16[64,1024]{1,0:T(8,128)(2,1)} %bitcast.22), channel_id=1, source_target_pairs={{0,4},{4,8},{8,12},{12,0},{1,5},{5,9},{9,13},{13,1},{2,6},{6,10},{... | collective-permute-start | bytes 393224 | tf_op jit(solution)/shard_map/ppermute | solution.py:19
  10.2 3.3 %copy-start.9 = (bf16[1024,1,64]{0,2,1:T(8,128)(2,1)S(1)}, bf16[1024,1,64]{0,2,1:T(8,128)(2,1)}, u32[]{:S(2)}) copy-start(bf16[1024,1,64]{0,2,1:T(8,128)(2,1)} %param.6) | copy-start | bytes 393220
  10.2 3.3 %copy-start.10 = (bf16[1,8,1024]{2,1,0:T(8,128)(2,1)S(1)}, bf16[1,8,1024]{2,1,0:T(8,128)(2,1)}, u32[]{:S(2)}) copy-start(bf16[1,8,1024]{2,1,0:T(8,128)(2,1)} %param.4) | copy-start | bytes 49156
  14.7 15.2 %collective-permute-start.5 = (bf16[2,128,1024]{2,1,0:T(8,128)(2,1)}, bf16[2,128,1024]{2,1,0:T(8,128)(2,1)S(1)}, u32[]{:S(2)}, u32[]{:S(2)}) collective-permute-start(bf16[2,128,1024]{2,1,0:T(8,128)(2,1)} %get-tuple-element.27), channel_id=1, source_target_pairs={{0,64},{64,0},{1,65},{65,1},{2,66},{66,2},{3,67},{67,3},{4,68},{68... | collective-permute-start | bytes 1572872 | tf_op jit(solution)/shard_map/ppermute | solution.py:215
  14.9 15.0 %collective-permute-start.7 = (bf16[256,1024]{1,0:T(8,128)(2,1)S(1)}, bf16[256,1024]{1,0:T(8,128)(2,1)S(1)}, u32[]{:S(2)}, u32[]{:S(2)}) collective-permute-start(bf16[256,1024]{1,0:T(8,128)(2,1)S(1)} %pad_maximum_fusion.1.refs_0_), channel_id=1, source_target_pairs={{0,48},{16,0},{32,16},{48,32},{1,49},{17,1},{33,17},{49,33},{2,50}... | collective-permute-start | bytes 1572872 | tf_op jit(solution)/shard_map/ppermute | solution.py:19
  17.7 12.3 %collective-permute-start.6 = (bf16[256,1024]{1,0:T(8,128)(2,1)S(1)}, bf16[256,1024]{1,0:T(8,128)(2,1)S(1)}, u32[]{:S(2)}, u32[]{:S(2)}) collective-permute-start(bf16[256,1024]{1,0:T(8,128)(2,1)S(1)} %pad_maximum_fusion.1.refs_0_), channel_id=1, source_target_pairs={{0,16},{16,32},{32,48},{48,0},{1,17},{17,33},{33,49},{49,1},{2,18}... | collective-permute-start | bytes 1572872 | tf_op jit(solution)/shard_map/ppermute | solution.py:19
  17.7 32.8 %all-to-all-start = ((bf16[128,8,512]{2,1,0:T(8,128)(2,1)}), bf16[128,8,512]{2,1,0:T(8,128)(2,1)S(1)}, u32[]{:S(2)}, u32[]{:S(2)}) async-start(bf16[128,8,512]{2,1,0:T(8,128)(2,1)} %bitcast.18), calls=%async_computation | async-start | bytes 2097152 | tf_op jit(solution)/shard_map/all_to_all | solution.py:23
  28.8 9.9 %collective-permute-start.4 = (bf16[1024,128]{1,0:T(8,128)(2,1)}, bf16[1024,128]{1,0:T(8,128)(2,1)S(1)}, u32[]{:S(2)}, u32[]{:S(2)}) collective-permute-start(bf16[1024,128]{1,0:T(8,128)(2,1)} %param.5), channel_id=1, source_target_pairs={{0,2},{2,0},{1,3},{3,1},{4,6},{6,4},{5,7},{7,5},{8,10},{10,8},{9,1... | collective-permute-start | bytes 786440 | tf_op jit(solution)/shard_map/ppermute | solution.py:27
  29.9 8.8 %copy-start.1 = (bf16[256,1024]{1,0:T(8,128)(2,1)}, bf16[256,1024]{1,0:T(8,128)(2,1)S(1)}, u32[]{:S(2)}) copy-start(bf16[256,1024]{1,0:T(8,128)(2,1)S(1)} %collective-permute-done.7.refs_2_) | copy-start | bytes 1572868
  29.9 8.8 %copy-start.3 = (bf16[256,1024]{1,0:T(8,128)(2,1)}, bf16[256,1024]{1,0:T(8,128)(2,1)S(1)}, u32[]{:S(2)}) copy-start(bf16[256,1024]{1,0:T(8,128)(2,1)S(1)} %collective-permute-done.6.refs_1_) | copy-start | bytes 1572868
  29.9 8.8 %collective-permute-start.8 = (bf16[1024,128]{1,0:T(8,128)(2,1)}, bf16[1024,128]{1,0:T(8,128)(2,1)S(1)}, u32[]{:S(2)}, u32[]{:S(2)}) collective-permute-start(bf16[1024,128]{1,0:T(8,128)(2,1)} %collective-permute-done.3), channel_id=1, source_target_pairs={{0,2},{2,0},{1,3},{3,1},{4,6},{6,4},{5,7},{7,5},{8,10},{10,8},{9,1... | collective-permute-start | bytes 786440 | tf_op jit(solution)/shard_map/ppermute | solution.py:27
  37.1 11.7 %collective-permute-start.11 = (bf16[128,1024]{1,0:T(8,128)(2,1)S(1)}, bf16[128,1024]{1,0:T(8,128)(2,1)S(1)}, u32[]{:S(2)}, u32[]{:S(2)}) collective-permute-start(bf16[128,1024]{1,0:T(8,128)(2,1)S(1)} %slice.13), channel_id=1, source_target_pairs={{0,48},{16,0},{32,16},{48,32},{1,49},{17,1},{33,17},{49,33},{2,50}... | collective-permute-start | bytes 786440 | tf_op jit(solution)/shard_map/ppermute | solution.py:19
  37.5 12.2 %collective-permute-start.10 = (bf16[128,1024]{1,0:T(8,128)(2,1)S(1)}, bf16[128,1024]{1,0:T(8,128)(2,1)S(1)}, u32[]{:S(2)}, u32[]{:S(2)}) collective-permute-start(bf16[128,1024]{1,0:T(8,128)(2,1)S(1)} %slice.12), channel_id=1, source_target_pairs={{0,16},{16,32},{32,48},{48,0},{1,17},{17,33},{33,49},{49,1},{2,18}... | collective-permute-start | bytes 786440 | tf_op jit(solution)/shard_map/ppermute | solution.py:19
  39.9 10.6 %collective-permute-start.9 = (bf16[128,1024]{1,0:T(8,128)(2,1)}, bf16[128,1024]{1,0:T(8,128)(2,1)}, u32[]{:S(2)}, u32[]{:S(2)}) collective-permute-start(bf16[128,1024]{1,0:T(8,128)(2,1)} %get-tuple-element.33), channel_id=1, source_target_pairs={{0,2},{2,0},{1,3},{3,1},{4,6},{6,4},{5,7},{7,5},{8,10},{10,8},{9,1... | collective-permute-start | bytes 786440 | tf_op jit(solution)/shard_map/ppermute | solution.py:27
  50.5 3.2 %copy-start.2 = (bf16[256,1024]{1,0:T(8,128)(2,1)S(1)}, bf16[256,1024]{1,0:T(8,128)(2,1)}, u32[]{:S(2)}) copy-start(bf16[256,1024]{1,0:T(8,128)(2,1)} %copy-done.1) | copy-start | bytes 1572868
  50.5 3.2 %copy-start.4 = (bf16[256,1024]{1,0:T(8,128)(2,1)S(1)}, bf16[256,1024]{1,0:T(8,128)(2,1)}, u32[]{:S(2)}) copy-start(bf16[256,1024]{1,0:T(8,128)(2,1)} %copy-done.3) | copy-start | bytes 1572868
  50.5 3.2 %copy-start.6 = (f32[128,1024]{1,0:T(8,128)S(1)}, f32[128,1024]{1,0:T(8,128)}, u32[]{:S(2)}) copy-start(f32[128,1024]{1,0:T(8,128)} %copy-done.5) | copy-start | bytes 1572868
  50.5 3.2 %copy-start.8 = (bf16[128,1024]{1,0:T(8,128)(2,1)S(1)}, bf16[128,1024]{1,0:T(8,128)(2,1)}, u32[]{:S(2)}) copy-start(bf16[128,1024]{1,0:T(8,128)(2,1)} %copy-done.7) | copy-start | bytes 786436
  51.2 2.5 %collective-permute-start.12 = (bf16[512,512]{1,0:T(8,128)(2,1)S(1)}, bf16[512,512]{1,0:T(8,128)(2,1)S(1)}, u32[]{:S(2)}, u32[]{:S(2)}) collective-permute-start(bf16[512,512]{1,0:T(8,128)(2,1)S(1)} %project.1.own_ref), channel_id=1, source_target_pairs={{0,2},{2,0},{1,3},{3,1},{4,6},{6,4},{5,7},{7,5},{8,10},{10,8},{9,1... | collective-permute-start | bytes 1572872 | tf_op jit(solution)/shard_map/ppermute | solution.py:27
  51.8 1.9 %collective-permute-start.13 = (bf16[128,1024]{1,0:T(8,128)(2,1)S(1)}, bf16[128,1024]{1,0:T(8,128)(2,1)S(1)}, u32[]{:S(2)}, u32[]{:S(2)}) collective-permute-start(bf16[128,1024]{1,0:T(8,128)(2,1)S(1)} %slice_bitcast_fusion), channel_id=1, source_target_pairs={{0,2},{2,0},{1,3},{3,1},{4,6},{6,4},{5,7},{7,5},{8,10},{10,8},{9,1... | collective-permute-start | bytes 786440 | tf_op jit(solution)/shard_map/ppermute | solution.py:27
  56.7 2.8 %collective-permute-start.14 = (f32[512,512]{1,0:T(8,128)S(1)}, f32[512,512]{1,0:T(8,128)S(1)}, u32[]{:S(2)}, u32[]{:S(2)}) collective-permute-start(f32[512,512]{1,0:T(8,128)S(1)} %get-tuple-element.42), channel_id=1, source_target_pairs={{0,2},{2,0},{1,3},{3,1},{4,6},{6,4},{5,7},{7,5},{8,10},{10,8},{9,1... | collective-permute-start | bytes 3145736 | tf_op jit(solution)/shard_map/ppermute | solution.py:27
  (3 other events, 3.1 us)

commit v21 on v20

--- a/solution.py
+++ b/solution.py
@@ -220,9 +220,10 @@
     psi = jnp.concatenate([psi_v, swap(psi_v), partner, swap(partner)], 1)
     near, psi = lax.optimization_barrier((near, psi))
     near = swap(near)
-    trial_half, near, beyond = lax.optimization_barrier((trial_half, near, beyond))
+    trial_half, near = lax.optimization_barrier((trial_half, near))
     passed = swap(far[1])
     proj_own = project(trial_half, psi)
+    proj_own, beyond = lax.optimization_barrier((proj_own, beyond))
     proj_other = swap(proj_own)
     panel = [line, behind, ahead, *beyond]
     weighted, ordered, send = direct(proj_own, proj_other, panel, own, [near, far, passed])

time: 90.3 us -> 93.3 us (1.033)
  blocking collectives: 28.5 us -> 31.2 us
  local copies, waits for them, and re-layouts: 4.33 us -> 5.75 us
  waiting for transfers between devices: 13.2 us -> 12 us
    ppermute x7, waiting for transfers between devices: 9.85 us -> 2.78 us  [shift(): return lax.ppermute(value, axis, [(k, (k + by) % n) for k in range(n)])]
    all_to_all x1, waiting for transfers between devices: 0.01 us -> 4.47 us  [exchange(): return lax.all_to_all(value, axes, split_axis=0, concat_axis=0, tiled=True)]
    all_to_all x1, blocking collectives: 28.5 us -> 31.2 us  [exchange(): return lax.all_to_all(value, axes, split_axis=0, concat_axis=0, tiled=True)]
    slice x2, local copies, waits for them, and re-layouts: 0.04 us -> 1.46 us  [shards(): beyond = [shift(behind[:middle], 'y', 1), shift(ahead[middle:], 'y', -1)]]
    ppermute x6, waiting for transfers between devices: 3.36 us -> 4.74 us  [swap(): return lax.ppermute(value, 'core', [(0, 1), (1, 0)])]
    unnamed x22 -> x28, local copies, waits for them, and re-layouts: 3.14 us -> 3.17 us
  transfers between devices with their start and end apart: 16 -> 16, of which waited for: 5 -> 6; matrix products, arithmetic and copies ran while one was open for 1% -> 3% of each run, Pallas kernels for 3% -> 4%
where the time goes in v21:
time: 93.3 us; the launch traced here: 93.1 us
  starting transfers between devices  34.3 us (37%)
  blocking collectives  31.2 us (33%)
  waiting for transfers between devices  12 us (13%)
  Pallas kernels  7.65 us (8%)
  local copies, waits for them, and re-layouts  5.75 us (6%)
  other arithmetic  1.99 us (2%)
    all_to_all x1, blocking collectives, exchange(): return lax.all_to_all(value, axes, split_axis=0, concat_axis=0, tiled=True)  31.2 us
    all_to_all x1, starting transfers between devices, exchange(): return lax.all_to_all(value, axes, split_axis=0, concat_axis=0, tiled=True)  11.1 us
    ppermute x6, starting transfers between devices, swap(): return lax.ppermute(value, 'core', [(0, 1), (1, 0)])  10.3 us
    ppermute x7, starting transfers between devices, shift(): return lax.ppermute(value, axis, [(k, (k + by) % n) for k in range(n)])  8.41 us
    ppermute x6, waiting for transfers between devices, swap(): return lax.ppermute(value, 'core', [(0, 1), (1, 0)])  4.74 us
    all_to_all x1, waiting for transfers between devices, exchange(): return lax.all_to_all(value, axes, split_axis=0, concat_axis=0, tiled=True)  4.47 us
    ppermute x1, starting transfers between devices, shards(): partner = lax.ppermute(psi_v, 'zh', [(0, 1), (1, 0)])  4.43 us
    unnamed x28, local copies, waits for them, and re-layouts  3.17 us
  transfers between devices with their start and end apart: 16, of which 6 were waited for; matrix products, arithmetic and copies ran while one was open for 3% of the time, Pallas kernels for 4%

profile of v21, /device:TPU:1, one launch (start us, length us, event | category | flops | bytes accessed | tf_op | source)
XLA Modules:
  0.0 93.1 jit_solution(1526977181443764325)
XLA Ops:
  0.0 4.4 %collective-permute-start.3 = (bf16[1024,128]{1,0:T(8,128)(2,1)}, bf16[1024,128]{1,0:T(8,128)(2,1)S(1)}, u32[]{:S(2)}, u32[]{:S(2)}) collective-permute-start(bf16[1024,128]{1,0:T(8,128)(2,1)} %param.5), channel_id=1, source_target_pairs={{0,64},{64,0},{1,65},{65,1},{2,66},{66,2},{3,67},{67,3},{4,68},{68... | collective-permute-start | bytes 786440 | tf_op jit(solution)/shard_map/ppermute | solution.py:207
  4.4 2.7 %collective-permute-start.2 = (bf16[64,1024]{1,0:T(8,128)(2,1)}, bf16[64,1024]{1,0:T(8,128)(2,1)S(1)}, u32[]{:S(2)}, u32[]{:S(2)}) collective-permute-start(bf16[64,1024]{1,0:T(8,128)(2,1)} %bitcast.20), channel_id=1, source_target_pairs={{0,8},{4,12},{8,0},{12,4},{1,9},{5,13},{9,1},{13,5},{2,10},{6,14},... | collective-permute-start | bytes 393224 | tf_op jit(solution)/shard_map/ppermute | solution.py:19
  7.2 0.9 collective-permute-start.1
  8.6 1.6 %copy-done = f32[128,4096]{1,0:T(8,128)S(1)} copy-done((f32[128,4096]{1,0:T(8,128)S(1)}, f32[128,4096]{1,0:T(8,128)}, u32[]{:S(2)}) %copy-start) | copy-done | bytes 2097176
  10.2 1.9 %pack.1 = (f32[128,1024]{1,0:T(8,128)S(1)}, bf16[128,1024]{1,0:T(8,128)(2,1)S(1)}, bf16[2,128,1024]{2,1,0:T(8,128)(2,1)}) custom-call(f32[128,4096]{1,0:T(8,128)S(1)} %copy-done), custom_call_target="tpu_custom_call" | custom-call | tf_op jit(solution)/shard_map/pack/pallas_call | solution.py:64
  12.1 0.8 copy-done.7
  13.8 1.1 %broadcast_in_dim.2 = bf16[32,2,2,8,512]{4,3,2,1,0:T(8,128)(2,1)} broadcast(bf16[2,8,512]{2,1,0:T(8,128)(2,1)S(1)} %bitcast.24), dimensions={1,3,4} | broadcast | bytes 1064960 | tf_op jit(solution)/shard_map/broadcast_in_dim | solution.py:212
  14.9 2.7 %collective-permute-start.7 = (bf16[256,1024]{1,0:T(8,128)(2,1)S(1)}, bf16[256,1024]{1,0:T(8,128)(2,1)S(1)}, u32[]{:S(2)}, u32[]{:S(2)}) collective-permute-start(bf16[256,1024]{1,0:T(8,128)(2,1)S(1)} %pad_maximum_fusion.1.refs_0_), channel_id=1, source_target_pairs={{0,48},{16,0},{32,16},{48,32},{1,49},{17,1},{33,17},{49,33},{2,50}... | collective-permute-start | bytes 1572872 | tf_op jit(solution)/shard_map/ppermute | solution.py:19
  17.6 11.1 %all-to-all-start = ((bf16[128,8,512]{2,1,0:T(8,128)(2,1)}), bf16[128,8,512]{2,1,0:T(8,128)(2,1)S(1)}, u32[]{:S(2)}, u32[]{:S(2)}) async-start(bf16[128,8,512]{2,1,0:T(8,128)(2,1)} %bitcast.18), calls=%async_computation | async-start | bytes 2097152 | tf_op jit(solution)/shard_map/all_to_all | solution.py:23
  28.8 1.1 %collective-permute-start.4 = (bf16[1024,128]{1,0:T(8,128)(2,1)S(1)}, bf16[1024,128]{1,0:T(8,128)(2,1)S(1)}, u32[]{:S(2)}, u32[]{:S(2)}) collective-permute-start(bf16[1024,128]{1,0:T(8,128)(2,1)S(1)} %copy-done.10), channel_id=1, source_target_pairs={{0,2},{2,0},{1,3},{3,1},{4,6},{6,4},{5,7},{7,5},{8,10},{10,8},{9,1... | collective-permute-start | bytes 786440 | tf_op jit(solution)/shard_map/ppermute | solution.py:27
  29.9 6.9 %collective-permute-start.8 = (bf16[1024,128]{1,0:T(8,128)(2,1)}, bf16[1024,128]{1,0:T(8,128)(2,1)S(1)}, u32[]{:S(2)}, u32[]{:S(2)}) collective-permute-start(bf16[1024,128]{1,0:T(8,128)(2,1)} %copy-done.11), channel_id=1, source_target_pairs={{0,2},{2,0},{1,3},{3,1},{4,6},{6,4},{5,7},{7,5},{8,10},{10,8},{9,1... | collective-permute-start | bytes 786440 | tf_op jit(solution)/shard_map/ppermute | solution.py:27
  36.9 1.4 %collective-permute-done.8 = bf16[1024,128]{1,0:T(8,128)(2,1)S(1)} collective-permute-done((bf16[1024,128]{1,0:T(8,128)(2,1)}, bf16[1024,128]{1,0:T(8,128)(2,1)S(1)}, u32[]{:S(2)}, u32[]{:S(2)}) %collective-permute-start.8) | collective-permute-done | bytes 262176 | tf_op jit(solution)/shard_map/ppermute | solution.py:27
  38.2 1.2 %pad_maximum_fusion.psi_ref = bf16[1024,512]{1,0:T(8,128)(2,1)S(1)} fusion(bf16[1024,128]{1,0:T(8,128)(2,1)S(1)} %collective-permute-done.8, bf16[1024,128]{1,0:T(8,128)(2,1)} %copy-done.11, bf16[1024,128]{1,0:T(8,128)(2,1)S(1)} %collective-permute-done.4, bf16[1024,128]{1,0:T(8,128)(2,1)S(1)} %copy-done.10), kind=kLoop, calls=%fused_computation.1 | loop fusion | flops 4194304 | bytes 2097152 | tf_op jit(solution)/shard_map/concatenate | solution.py:220
  41.8 1.0 %collective-permute-start.10 = (bf16[128,1024]{1,0:T(8,128)(2,1)}, bf16[128,1024]{1,0:T(8,128)(2,1)}, u32[]{:S(2)}, u32[]{:S(2)}) collective-permute-start(bf16[128,1024]{1,0:T(8,128)(2,1)} %slice.12), channel_id=1, source_target_pairs={{0,16},{16,32},{32,48},{48,0},{1,17},{17,33},{33,49},{49,1},{2,18}... | collective-permute-start | bytes 786440 | tf_op jit(solution)/shard_map/ppermute | solution.py:19
  42.8 4.5 %all-to-all-done = bf16[128,8,512]{2,1,0:T(8,128)(2,1)S(1)} async-done(((bf16[128,8,512]{2,1,0:T(8,128)(2,1)}), bf16[128,8,512]{2,1,0:T(8,128)(2,1)S(1)}, u32[]{:S(2)}, u32[]{:S(2)}) %all-to-all-start) | async-done | bytes 1048608 | tf_op jit(solution)/shard_map/all_to_all | solution.py:23
  48.0 1.2 %collective-permute-done.11.refs_4_ = bf16[128,1024]{1,0:T(8,128)(2,1)} collective-permute-done((bf16[128,1024]{1,0:T(8,128)(2,1)}, bf16[128,1024]{1,0:T(8,128)(2,1)}, u32[]{:S(2)}, u32[]{:S(2)}) %collective-permute-start.11) | collective-permute-done | bytes 262176 | tf_op jit(solution)/shard_map/ppermute | solution.py:19
  49.2 1.5 %collective-permute-done.10.refs_3_ = bf16[128,1024]{1,0:T(8,128)(2,1)} collective-permute-done((bf16[128,1024]{1,0:T(8,128)(2,1)}, bf16[128,1024]{1,0:T(8,128)(2,1)}, u32[]{:S(2)}, u32[]{:S(2)}) %collective-permute-start.10) | collective-permute-done | bytes 262176 | tf_op jit(solution)/shard_map/ppermute | solution.py:19
  50.8 1.3 %collective-permute-start.12 = (bf16[512,512]{1,0:T(8,128)(2,1)S(1)}, bf16[512,512]{1,0:T(8,128)(2,1)S(1)}, u32[]{:S(2)}, u32[]{:S(2)}) collective-permute-start(bf16[512,512]{1,0:T(8,128)(2,1)S(1)} %project.1.own_ref), channel_id=1, source_target_pairs={{0,2},{2,0},{1,3},{3,1},{4,6},{6,4},{5,7},{7,5},{8,10},{10,8},{9,1... | collective-permute-start | bytes 1572872 | tf_op jit(solution)/shard_map/ppermute | solution.py:27
  52.2 1.8 %collective-permute-done.13.refs_8_ = bf16[128,1024]{1,0:T(8,128)(2,1)S(1)} collective-permute-done((bf16[128,1024]{1,0:T(8,128)(2,1)S(1)}, bf16[128,1024]{1,0:T(8,128)(2,1)S(1)}, u32[]{:S(2)}, u32[]{:S(2)}) %collective-permute-start.13) | collective-permute-done | bytes 262176 | tf_op jit(solution)/shard_map/ppermute | solution.py:27
  54.0 3.0 %direct.1 = (bf16[512,1024]{1,0:T(8,128)(2,1)S(1)}, bf16[1024,1024]{1,0:T(8,128)(2,1)S(1)}, f32[512,512]{1,0:T(8,128)S(1)}) custom-call(bf16[512,512]{1,0:T(8,128)(2,1)S(1)} %project.1.own_ref, bf16[512,512]{1,0:T(8,128)(2,1)S(1)} %collective-permute-done.12.other_ref, bf16[256,1024]{1,0:T(8,128)(2,1)S(1)} %pad_maximum_fusion.1.refs_0_, ...), custom_call_target="tpu_custom_call" | custom-call | tf_op jit(solution)/shard_map/direct/pallas_call | solution.py:142
  58.2 1.6 %collective-permute-done.14.got_ref = f32[512,512]{1,0:T(8,128)S(1)} collective-permute-done((f32[512,512]{1,0:T(8,128)S(1)}, f32[512,512]{1,0:T(8,128)S(1)}, u32[]{:S(2)}, u32[]{:S(2)}) %collective-permute-start.14) | collective-permute-done | bytes 1048608 | tf_op jit(solution)/shard_map/ppermute | solution.py:27
  59.7 1.3 %finish.1 = bf16[1024,512]{1,0:T(8,128)(2,1)S(1)} custom-call(bf16[1024,512]{1,0:T(8,128)(2,1)S(1)} %pad_maximum_fusion.psi_ref, f32[512,512]{1,0:T(8,128)S(1)} %own_half.1.keep_ref, f32[512,512]{1,0:T(8,128)S(1)} %collective-permute-done.14.got_ref), custom_call_target="tpu_custom_call" | custom-call | tf_op jit(solution)/shard_map/finish/pallas_call | solution.py:192
  61.0 31.2 %all_to_all.10 = bf16[128,8,512]{2,1,0:T(8,128)(2,1)S(1)} all-to-all(bf16[128,8,512]{2,1,0:T(8,128)(2,1)S(1)} %bitcast.17), channel_id=1, replica_groups=mesh['zh'=2,'y'=4,'x'=4,'core'=2,'zl'=2] {'zh','y','x','core','zl'}, dimensions={0} | all-to-all | bytes 2097152 | tf_op jit(solution)/shard_map/all_to_all | solution.py:23
  92.3 0.8 convert_reduce_fusion
  (49 shorter events, 5.9 us)
Async XLA Ops:
  0.0 13.8 %collective-permute-start.3 = (bf16[1024,128]{1,0:T(8,128)(2,1)}, bf16[1024,128]{1,0:T(8,128)(2,1)S(1)}, u32[]{:S(2)}, u32[]{:S(2)}) collective-permute-start(bf16[1024,128]{1,0:T(8,128)(2,1)} %param.5), channel_id=1, source_target_pairs={{0,64},{64,0},{1,65},{65,1},{2,66},{66,2},{3,67},{67,3},{4,68},{68... | collective-permute-start | bytes 786440 | tf_op jit(solution)/shard_map/ppermute | solution.py:207
  4.4 9.3 %collective-permute-start.2 = (bf16[64,1024]{1,0:T(8,128)(2,1)}, bf16[64,1024]{1,0:T(8,128)(2,1)S(1)}, u32[]{:S(2)}, u32[]{:S(2)}) collective-permute-start(bf16[64,1024]{1,0:T(8,128)(2,1)} %bitcast.20), channel_id=1, source_target_pairs={{0,8},{4,12},{8,0},{12,4},{1,9},{5,13},{9,1},{13,5},{2,10},{6,14},... | collective-permute-start | bytes 393224 | tf_op jit(solution)/shard_map/ppermute | solution.py:19
  7.2 6.5 %collective-permute-start.1 = (bf16[64,1024]{1,0:T(8,128)(2,1)}, bf16[64,1024]{1,0:T(8,128)(2,1)S(1)}, u32[]{:S(2)}, u32[]{:S(2)}) collective-permute-start(bf16[64,1024]{1,0:T(8,128)(2,1)} %bitcast.21), channel_id=1, source_target_pairs={{0,12},{4,0},{8,4},{12,8},{1,13},{5,1},{9,5},{13,9},{2,14},{6,2},{... | collective-permute-start | bytes 393224 | tf_op jit(solution)/shard_map/ppermute | solution.py:19
  8.0 5.7 %collective-permute-start = (bf16[64,1024]{1,0:T(8,128)(2,1)}, bf16[64,1024]{1,0:T(8,128)(2,1)S(1)}, u32[]{:S(2)}, u32[]{:S(2)}) collective-permute-start(bf16[64,1024]{1,0:T(8,128)(2,1)} %bitcast.22), channel_id=1, source_target_pairs={{0,4},{4,8},{8,12},{12,0},{1,5},{5,9},{9,13},{13,1},{2,6},{6,10},{... | collective-permute-start | bytes 393224 | tf_op jit(solution)/shard_map/ppermute | solution.py:19
  10.2 3.5 %copy-start.12 = (bf16[1024,1,64]{0,2,1:T(8,128)(2,1)S(1)}, bf16[1024,1,64]{0,2,1:T(8,128)(2,1)}, u32[]{:S(2)}) copy-start(bf16[1024,1,64]{0,2,1:T(8,128)(2,1)} %param.6) | copy-start | bytes 393220
  10.2 3.6 %copy-start.13 = (bf16[1,8,1024]{2,1,0:T(8,128)(2,1)S(1)}, bf16[1,8,1024]{2,1,0:T(8,128)(2,1)}, u32[]{:S(2)}) copy-start(bf16[1,8,1024]{2,1,0:T(8,128)(2,1)} %param.4) | copy-start | bytes 49156
  13.7 15.1 %copy-start.10 = (bf16[1024,128]{1,0:T(8,128)(2,1)S(1)}, bf16[1024,128]{1,0:T(8,128)(2,1)}, u32[]{:S(2)}) copy-start(bf16[1024,128]{1,0:T(8,128)(2,1)} %param.5) | copy-start | bytes 786436
  14.9 15.0 %collective-permute-start.5 = (bf16[2,128,1024]{2,1,0:T(8,128)(2,1)}, bf16[2,128,1024]{2,1,0:T(8,128)(2,1)S(1)}, u32[]{:S(2)}, u32[]{:S(2)}) collective-permute-start(bf16[2,128,1024]{2,1,0:T(8,128)(2,1)} %get-tuple-element.28), channel_id=1, source_target_pairs={{0,64},{64,0},{1,65},{65,1},{2,66},{66,2},{3,67},{67,3},{4,68},{68... | collective-permute-start | bytes 1572872 | tf_op jit(solution)/shard_map/ppermute | solution.py:215
  14.9 15.0 %collective-permute-start.7 = (bf16[256,1024]{1,0:T(8,128)(2,1)S(1)}, bf16[256,1024]{1,0:T(8,128)(2,1)S(1)}, u32[]{:S(2)}, u32[]{:S(2)}) collective-permute-start(bf16[256,1024]{1,0:T(8,128)(2,1)S(1)} %pad_maximum_fusion.1.refs_0_), channel_id=1, source_target_pairs={{0,48},{16,0},{32,16},{48,32},{1,49},{17,1},{33,17},{49,33},{2,50}... | collective-permute-start | bytes 1572872 | tf_op jit(solution)/shard_map/ppermute | solution.py:19
  17.6 12.3 %collective-permute-start.6 = (bf16[256,1024]{1,0:T(8,128)(2,1)S(1)}, bf16[256,1024]{1,0:T(8,128)(2,1)S(1)}, u32[]{:S(2)}, u32[]{:S(2)}) collective-permute-start(bf16[256,1024]{1,0:T(8,128)(2,1)S(1)} %pad_maximum_fusion.1.refs_0_), channel_id=1, source_target_pairs={{0,16},{16,32},{32,48},{48,0},{1,17},{17,33},{33,49},{49,1},{2,18}... | collective-permute-start | bytes 1572872 | tf_op jit(solution)/shard_map/ppermute | solution.py:19
  17.6 29.6 %all-to-all-start = ((bf16[128,8,512]{2,1,0:T(8,128)(2,1)}), bf16[128,8,512]{2,1,0:T(8,128)(2,1)S(1)}, u32[]{:S(2)}, u32[]{:S(2)}) async-start(bf16[128,8,512]{2,1,0:T(8,128)(2,1)} %bitcast.18), calls=%async_computation | async-start | bytes 2097152 | tf_op jit(solution)/shard_map/all_to_all | solution.py:23
  28.8 8.1 %collective-permute-start.4 = (bf16[1024,128]{1,0:T(8,128)(2,1)S(1)}, bf16[1024,128]{1,0:T(8,128)(2,1)S(1)}, u32[]{:S(2)}, u32[]{:S(2)}) collective-permute-start(bf16[1024,128]{1,0:T(8,128)(2,1)S(1)} %copy-done.10), channel_id=1, source_target_pairs={{0,2},{2,0},{1,3},{3,1},{4,6},{6,4},{5,7},{7,5},{8,10},{10,8},{9,1... | collective-permute-start | bytes 786440 | tf_op jit(solution)/shard_map/ppermute | solution.py:27
  29.9 6.9 %copy-start.1 = (bf16[256,1024]{1,0:T(8,128)(2,1)}, bf16[256,1024]{1,0:T(8,128)(2,1)S(1)}, u32[]{:S(2)}) copy-start(bf16[256,1024]{1,0:T(8,128)(2,1)S(1)} %collective-permute-done.7.refs_2_) | copy-start | bytes 1572868
  29.9 6.9 %copy-start.4 = (bf16[256,1024]{1,0:T(8,128)(2,1)}, bf16[256,1024]{1,0:T(8,128)(2,1)S(1)}, u32[]{:S(2)}) copy-start(bf16[256,1024]{1,0:T(8,128)(2,1)S(1)} %collective-permute-done.6.refs_1_) | copy-start | bytes 1572868
  29.9 8.3 %collective-permute-start.8 = (bf16[1024,128]{1,0:T(8,128)(2,1)}, bf16[1024,128]{1,0:T(8,128)(2,1)S(1)}, u32[]{:S(2)}, u32[]{:S(2)}) collective-permute-start(bf16[1024,128]{1,0:T(8,128)(2,1)} %copy-done.11), channel_id=1, source_target_pairs={{0,2},{2,0},{1,3},{3,1},{4,6},{6,4},{5,7},{7,5},{8,10},{10,8},{9,1... | collective-permute-start | bytes 786440 | tf_op jit(solution)/shard_map/ppermute | solution.py:27
  39.4 7.9 %collective-permute-start.9 = (bf16[128,1024]{1,0:T(8,128)(2,1)}, bf16[128,1024]{1,0:T(8,128)(2,1)S(1)}, u32[]{:S(2)}, u32[]{:S(2)}) collective-permute-start(bf16[128,1024]{1,0:T(8,128)(2,1)} %copy-done.9), channel_id=1, source_target_pairs={{0,2},{2,0},{1,3},{3,1},{4,6},{6,4},{5,7},{7,5},{8,10},{10,8},{9,1... | collective-permute-start | bytes 786440 | tf_op jit(solution)/shard_map/ppermute | solution.py:27
  40.6 8.6 %collective-permute-start.11 = (bf16[128,1024]{1,0:T(8,128)(2,1)}, bf16[128,1024]{1,0:T(8,128)(2,1)}, u32[]{:S(2)}, u32[]{:S(2)}) collective-permute-start(bf16[128,1024]{1,0:T(8,128)(2,1)} %slice.13), channel_id=1, source_target_pairs={{0,48},{16,0},{32,16},{48,32},{1,49},{17,1},{33,17},{49,33},{2,50}... | collective-permute-start | bytes 786440 | tf_op jit(solution)/shard_map/ppermute | solution.py:19
  41.8 9.0 %collective-permute-start.10 = (bf16[128,1024]{1,0:T(8,128)(2,1)}, bf16[128,1024]{1,0:T(8,128)(2,1)}, u32[]{:S(2)}, u32[]{:S(2)}) collective-permute-start(bf16[128,1024]{1,0:T(8,128)(2,1)} %slice.12), channel_id=1, source_target_pairs={{0,16},{16,32},{32,48},{48,0},{1,17},{17,33},{33,49},{49,1},{2,18}... | collective-permute-start | bytes 786440 | tf_op jit(solution)/shard_map/ppermute | solution.py:19
  47.3 6.7 %copy-start.3 = (bf16[256,1024]{1,0:T(8,128)(2,1)S(1)}, bf16[256,1024]{1,0:T(8,128)(2,1)}, u32[]{:S(2)}) copy-start(bf16[256,1024]{1,0:T(8,128)(2,1)} %copy-done.1) | copy-start | bytes 1572868
  47.3 6.7 %copy-start.6 = (bf16[256,1024]{1,0:T(8,128)(2,1)S(1)}, bf16[256,1024]{1,0:T(8,128)(2,1)}, u32[]{:S(2)}) copy-start(bf16[256,1024]{1,0:T(8,128)(2,1)} %copy-done.4) | copy-start | bytes 1572868
  47.3 6.7 %copy-start.8 = (f32[128,1024]{1,0:T(8,128)S(1)}, f32[128,1024]{1,0:T(8,128)}, u32[]{:S(2)}) copy-start(f32[128,1024]{1,0:T(8,128)} %copy-done.7) | copy-start | bytes 1572868
  50.8 3.2 %collective-permute-start.12 = (bf16[512,512]{1,0:T(8,128)(2,1)S(1)}, bf16[512,512]{1,0:T(8,128)(2,1)S(1)}, u32[]{:S(2)}, u32[]{:S(2)}) collective-permute-start(bf16[512,512]{1,0:T(8,128)(2,1)S(1)} %project.1.own_ref), channel_id=1, source_target_pairs={{0,2},{2,0},{1,3},{3,1},{4,6},{6,4},{5,7},{7,5},{8,10},{10,8},{9,1... | collective-permute-start | bytes 1572872 | tf_op jit(solution)/shard_map/ppermute | solution.py:27
  52.1 1.9 %collective-permute-start.13 = (bf16[128,1024]{1,0:T(8,128)(2,1)S(1)}, bf16[128,1024]{1,0:T(8,128)(2,1)S(1)}, u32[]{:S(2)}, u32[]{:S(2)}) collective-permute-start(bf16[128,1024]{1,0:T(8,128)(2,1)S(1)} %slice_bitcast_fusion), channel_id=1, source_target_pairs={{0,2},{2,0},{1,3},{3,1},{4,6},{6,4},{5,7},{7,5},{8,10},{10,8},{9,1... | collective-permute-start | bytes 786440 | tf_op jit(solution)/shard_map/ppermute | solution.py:27
  57.0 2.8 %collective-permute-start.14 = (f32[512,512]{1,0:T(8,128)S(1)}, f32[512,512]{1,0:T(8,128)S(1)}, u32[]{:S(2)}, u32[]{:S(2)}) collective-permute-start(f32[512,512]{1,0:T(8,128)S(1)} %get-tuple-element.44), channel_id=1, source_target_pairs={{0,2},{2,0},{1,3},{3,1},{4,6},{6,4},{5,7},{7,5},{8,10},{10,8},{9,1... | collective-permute-start | bytes 3145736 | tf_op jit(solution)/shard_map/ppermute | solution.py:27
  (6 other events, 8.7 us)

commit v22 on v17

--- a/solution.py
+++ b/solution.py
@@ -8,6 +8,7 @@
 
 TILE_VEC = ("zh", "y", "x", "core", "zl")
 TILE = ("zh", "y", "x", "core")
+ORDER = ("y", "x", "zh", "zl", "core")
 STEPS = (0, -1, 1, -2)
 F32 = jnp.float32
 BF16 = jnp.bfloat16
@@ -227,13 +228,14 @@
     rows, states = trial.shape[1:]
     half = states // 2
     devices = lax.axis_size(TILE_VEC)
-    own, near, far = pack(screened, psi_v)
+    left = psi_v.reshape(2, 4, 4, 2, 2, rows, -1).transpose(1, 2, 0, 4, 3, 5, 6).reshape(psi_v.shape)
+    own, near, far = pack(screened, left)
     block = psi_c[:, 0, :].T
     line = jnp.concatenate([block, shift(block, "x", 1), shift(block, "x", -1), shift(block, "x", 2)], 0)
     halves = trial[0].reshape(rows, 2, half).transpose(1, 0, 2)
-    copies = jnp.broadcast_to(halves[None, :, None], (devices // 4, 2, 2, rows, half))
+    copies = jnp.broadcast_to(halves[None], (devices // 2, 2, rows, half))
     copies, near, far, line = lax.optimization_barrier((copies, near, far, line))
-    trial_half = exchange(copies.reshape(devices, rows, half), TILE_VEC).reshape(-1, half)
+    trial_half = exchange(copies.reshape(devices, rows, half), ORDER).reshape(-1, half)
     near = swap(near)
     far = lax.ppermute(far, "zh", [(0, 1), (1, 0)])
     behind, ahead = shift(line, "y", 1), shift(line, "y", -1)
@@ -241,16 +243,16 @@
     beyond = [shift(behind[:middle], "y", 1), shift(ahead[middle:], "y", -1)]
     far, beyond = lax.optimization_barrier((far, beyond))
     passed = swap(far[1:])
-    proj_own, psi = project(trial_half, psi_v, near, far, passed)
+    proj_own, psi = project(trial_half, left, near, far, passed)
     proj_other = swap(proj_own)
     panel = [line, behind, ahead, *beyond]
     weighted, ordered, send = direct(proj_own, proj_other, panel, own, [near, far, passed])
     got = swap(send)
     keep = own_half(weighted, ordered)
     term = finish(psi, keep, got)
-    parts = exchange(term.reshape(devices, rows, half), TILE_VEC)
-    parts = parts.reshape(-1, 2, 2, rows, half).astype(F32)
-    total = jnp.sum(parts, axis=(0, 2))
+    parts = exchange(term.reshape(devices, rows, half), ORDER)
+    parts = parts.reshape(-1, 2, rows, half).astype(F32)
+    total = jnp.sum(parts, axis=0)
     return total.transpose(1, 0, 2).reshape(1, rows, states)
 
 

time: 89.3 us -> 91.4 us (1.024)
  Pallas kernels: 6.9 us -> 9.1 us
    unnamed x32 -> x20, local copies, waits for them, and re-layouts: 6.53 us -> 3.94 us
    pallas_call x1, Pallas kernels: 1.98 us -> 3.17 us  [direct(): pl.pallas_call(kernel, out_shape=[jax.ShapeDtypeStruct((rows, count), BF1...]
    pallas_call x1, Pallas kernels: 0.93 us -> 1.97 us  [project(): pl.pallas_call(kernel, out_shape=[jax.ShapeDtypeStruct((4 * points, cols)...]
    reshape x0 -> x1, local copies, waits for them, and re-layouts: none -> 1 us  [shards(): psi_v.reshape(2, 4, 4, 2, 2, rows, -1).transpose(1, 2, 0, 4, 3, 5, 6)]
    slice x2, local copies, waits for them, and re-layouts: 0.04 us -> 0.99 us  [shards(): beyond = [shift(behind[:middle], 'y', 1), shift(ahead[middle:], 'y', -1)]]
  transfers between devices with their start and end apart: 13 -> 13, of which waited for: 5 -> 5; matrix products, arithmetic and copies ran while one was open for 1% -> 3% of each run, Pallas kernels for 3% -> 3%
where the time goes in v22:
time: 91.4 us; the launch traced here: 91 us
  blocking collectives  27.7 us (30%)
  starting transfers between devices  25.6 us (28%)
  waiting for transfers between devices  19.7 us (22%)
  Pallas kernels  9.1 us (10%)
  local copies, waits for them, and re-layouts  7.9 us (9%)
    all_to_all x1, blocking collectives, exchange(): return lax.all_to_all(value, axes, split_axis=0, concat_axis=0, tiled=True)  27.7 us
    ppermute x7, waiting for transfers between devices, shift(): return lax.ppermute(value, axis, [(k, (k + by) % n) for k in range(n)])  14.8 us
    ppermute x7, starting transfers between devices, shift(): return lax.ppermute(value, axis, [(k, (k + by) % n) for k in range(n)])  10.6 us
    all_to_all x1, starting transfers between devices, exchange(): return lax.all_to_all(value, axes, split_axis=0, concat_axis=0, tiled=True)  8.41 us
    ppermute x4, waiting for transfers between devices, swap(): return lax.ppermute(value, 'core', [(0, 1), (1, 0)])  4.96 us
    unnamed x20, local copies, waits for them, and re-layouts  3.94 us
    ppermute x1, starting transfers between devices, shards(): far = lax.ppermute(far, 'zh', [(0, 1), (1, 0)])  3.6 us
    pallas_call x1, Pallas kernels, direct(): pl.pallas_call(kernel, out_shape=[jax.ShapeDtypeStruct((rows, count), BF1...  3.17 us
  transfers between devices with their start and end apart: 13, of which 5 were waited for; matrix products, arithmetic and copies ran while one was open for 3% of the time, Pallas kernels for 3%

profile of v22, /device:TPU:1, one launch (start us, length us, event | category | flops | bytes accessed | tf_op | source)
XLA Modules:
  0.0 91.0 jit_solution(1984207274205793740)
XLA Ops:
  0.0 3.6 %collective-permute-start.2 = (bf16[64,1024]{1,0:T(8,128)(2,1)}, bf16[64,1024]{1,0:T(8,128)(2,1)S(1)}, u32[]{:S(2)}, u32[]{:S(2)}) collective-permute-start(bf16[64,1024]{1,0:T(8,128)(2,1)} %bitcast.25), channel_id=1, source_target_pairs={{0,8},{4,12},{8,0},{12,4},{1,9},{5,13},{9,1},{13,5},{2,10},{6,14},... | collective-permute-start | bytes 393224 | tf_op jit(solution)/shard_map/ppermute | solution.py:20
  3.6 0.9 collective-permute-start.1
  5.0 1.0 %copy.5 = bf16[2,4,4,2,2,8,128]{6,5,3,4,0,2,1:T(8,128)(2,1)S(1)} copy(bf16[2,4,4,2,2,8,128]{6,5,4,3,2,1,0:T(8,128)(2,1)} %bitcast.24) | data formatting | bytes 524288 | tf_op jit(solution)/shard_map/reshape | solution.py:231
  6.1 1.6 %copy-done = f32[128,4096]{1,0:T(8,128)S(1)} copy-done((f32[128,4096]{1,0:T(8,128)S(1)}, f32[128,4096]{1,0:T(8,128)}, u32[]{:S(2)}) %copy-start) | copy-done | bytes 2097176
  7.7 2.0 %pack.1 = (f32[128,1024]{1,0:T(8,128)S(1)}, bf16[2,128,1024]{2,1,0:T(8,128)(2,1)S(1)}, bf16[3,128,1024]{2,1,0:T(8,128)(2,1)}) custom-call(f32[128,4096]{1,0:T(8,128)S(1)} %copy-done, bf16[1024,128]{1,0:T(8,128)(2,1)S(1)} %bitcast.20), custom_call_target="tpu_custom_call" | custom-call | tf_op jit(solution)/shard_map/pack/pallas_call | solution.py:70
  9.6 0.8 copy-done.3
  11.3 1.1 %broadcast_in_dim.2 = bf16[64,2,8,512]{3,2,1,0:T(8,128)(2,1)} broadcast(bf16[2,8,512]{2,1,0:T(8,128)(2,1)S(1)} %bitcast.29), dimensions={1,2,3} | broadcast | bytes 1064960 | tf_op jit(solution)/shard_map/broadcast_in_dim | solution.py:236
  12.4 2.7 %collective-permute-start.7 = (bf16[256,1024]{1,0:T(8,128)(2,1)S(1)}, bf16[256,1024]{1,0:T(8,128)(2,1)S(1)}, u32[]{:S(2)}, u32[]{:S(2)}) collective-permute-start(bf16[256,1024]{1,0:T(8,128)(2,1)S(1)} %pad_maximum_fusion.refs_0_), channel_id=1, source_target_pairs={{0,48},{16,0},{32,16},{48,32},{1,49},{17,1},{33,17},{49,33},{2,50}... | collective-permute-start | bytes 1572872 | tf_op jit(solution)/shard_map/ppermute | solution.py:20
  15.2 3.6 %collective-permute-start.4 = (bf16[3,128,1024]{2,1,0:T(8,128)(2,1)}, bf16[3,128,1024]{2,1,0:T(8,128)(2,1)S(1)}, u32[]{:S(2)}, u32[]{:S(2)}) collective-permute-start(bf16[3,128,1024]{2,1,0:T(8,128)(2,1)} %get-tuple-element.24), channel_id=1, source_target_pairs={{0,64},{64,0},{1,65},{65,1},{2,66},{66,2},{3,67},{67,3},{4,68},{68... | collective-permute-start | bytes 2359304 | tf_op jit(solution)/shard_map/ppermute | solution.py:240
  18.8 8.4 %all-to-all-start = ((bf16[128,8,512]{2,1,0:T(8,128)(2,1)}), bf16[128,8,512]{2,1,0:T(8,128)(2,1)S(1)}, u32[]{:S(2)}, u32[]{:S(2)}) async-start(bf16[128,8,512]{2,1,0:T(8,128)(2,1)} %bitcast.22), calls=%async_computation | async-start | bytes 2097152 | tf_op jit(solution)/shard_map/all_to_all | solution.py:24
  27.2 2.7 %collective-permute-start.8 = (bf16[128,1024]{1,0:T(8,128)(2,1)S(1)}, bf16[128,1024]{1,0:T(8,128)(2,1)S(1)}, u32[]{:S(2)}, u32[]{:S(2)}) collective-permute-start(bf16[128,1024]{1,0:T(8,128)(2,1)S(1)} %slice.13), channel_id=1, source_target_pairs={{0,48},{16,0},{32,16},{48,32},{1,49},{17,1},{33,17},{49,33},{2,50}... | collective-permute-start | bytes 786440 | tf_op jit(solution)/shard_map/ppermute | solution.py:20
  29.9 1.0 %slice.12 = bf16[128,1024]{1,0:T(8,128)(2,1)S(1)} slice(bf16[256,1024]{1,0:T(8,128)(2,1)} %collective-permute-done.5.refs_1_), slice={[0:128], [0:1024]} | slice | bytes 524288 | tf_op jit(solution)/shard_map/slice | solution.py:243
  31.0 1.2 %collective-permute-start.3 = (bf16[2,128,1024]{2,1,0:T(8,128)(2,1)}, bf16[2,128,1024]{2,1,0:T(8,128)(2,1)S(1)}, u32[]{:S(2)}, u32[]{:S(2)}) collective-permute-start(bf16[2,128,1024]{2,1,0:T(8,128)(2,1)} %copy-done.7), channel_id=1, source_target_pairs={{0,2},{2,0},{1,3},{3,1},{4,6},{6,4},{5,7},{7,5},{8,10},{10,8},{9,1... | collective-permute-start | bytes 1572872 | tf_op jit(solution)/shard_map/ppermute | solution.py:28
  32.2 13.3 %collective-permute-done.8.refs_4_ = bf16[128,1024]{1,0:T(8,128)(2,1)S(1)} collective-permute-done((bf16[128,1024]{1,0:T(8,128)(2,1)S(1)}, bf16[128,1024]{1,0:T(8,128)(2,1)S(1)}, u32[]{:S(2)}, u32[]{:S(2)}) %collective-permute-start.8) | collective-permute-done | bytes 262176 | tf_op jit(solution)/shard_map/ppermute | solution.py:20
  45.5 1.5 %collective-permute-done.6.refs_3_ = bf16[128,1024]{1,0:T(8,128)(2,1)S(1)} collective-permute-done((bf16[128,1024]{1,0:T(8,128)(2,1)S(1)}, bf16[128,1024]{1,0:T(8,128)(2,1)S(1)}, u32[]{:S(2)}, u32[]{:S(2)}) %collective-permute-start.6) | collective-permute-done | bytes 262176 | tf_op jit(solution)/shard_map/ppermute | solution.py:20
  47.7 0.8 slice.11
  48.6 0.9 collective-permute-start.9
  49.5 1.8 %collective-permute-done.9.refs_2_.refs_8_ = bf16[2,128,1024]{2,1,0:T(8,128)(2,1)} collective-permute-done((bf16[2,128,1024]{2,1,0:T(8,128)(2,1)}, bf16[2,128,1024]{2,1,0:T(8,128)(2,1)}, u32[]{:S(2)}, u32[]{:S(2)}) %collective-permute-start.9) | collective-permute-done | bytes 524320 | tf_op jit(solution)/shard_map/ppermute | solution.py:28
  51.3 2.0 %project.1 = (bf16[512,512]{1,0:T(8,128)(2,1)S(1)}, bf16[1024,512]{1,0:T(8,128)(2,1)S(1)}) custom-call(bf16[1024,512]{1,0:T(8,128)(2,1)S(1)} %bitcast.18, bf16[1024,128]{1,0:T(8,128)(2,1)S(1)} %bitcast.21, bf16[2,128,1024]{2,1,0:T(8,128)(2,1)S(1)} %collective-permute-done.3.refs_0_.refs_6_, bf16[3,128,1024]{2,1,0:T(8,128)(2,1)S(1)} %collective-permute-done.4.refs_1_.refs_7_, ...), custom_call_target="tpu_custom_call" | custom-call | tf_op jit(solution)/shard_map/project/pallas_call | solution.py:111
  53.7 1.5 %collective-permute-done.10.other_ref = bf16[512,512]{1,0:T(8,128)(2,1)S(1)} collective-permute-done((bf16[512,512]{1,0:T(8,128)(2,1)S(1)}, bf16[512,512]{1,0:T(8,128)(2,1)S(1)}, u32[]{:S(2)}, u32[]{:S(2)}) %collective-permute-start.10) | collective-permute-done | bytes 524320 | tf_op jit(solution)/shard_map/ppermute | solution.py:28
  55.3 3.2 %direct.1 = (bf16[512,1024]{1,0:T(8,128)(2,1)S(1)}, bf16[1024,1024]{1,0:T(8,128)(2,1)S(1)}, f32[512,512]{1,0:T(8,128)S(1)}) custom-call(bf16[512,512]{1,0:T(8,128)(2,1)S(1)} %get-tuple-element.28.own_ref, bf16[512,512]{1,0:T(8,128)(2,1)S(1)} %collective-permute-done.10.other_ref, bf16[256,1024]{1,0:T(8,128)(2,1)S(1)} %pad_maximum_fusion.refs_0_, ...), custom_call_target="tpu_custom_call" | custom-call | tf_op jit(solution)/shard_map/direct/pallas_call | solution.py:166
  59.6 1.6 %collective-permute-done.11.got_ref = f32[512,512]{1,0:T(8,128)S(1)} collective-permute-done((f32[512,512]{1,0:T(8,128)S(1)}, f32[512,512]{1,0:T(8,128)S(1)}, u32[]{:S(2)}, u32[]{:S(2)}) %collective-permute-start.11) | collective-permute-done | bytes 1048608 | tf_op jit(solution)/shard_map/ppermute | solution.py:28
  61.2 1.3 %finish.1 = bf16[1024,512]{1,0:T(8,128)(2,1)S(1)} custom-call(bf16[1024,512]{1,0:T(8,128)(2,1)S(1)} %get-tuple-element.27.psi_ref, f32[512,512]{1,0:T(8,128)S(1)} %own_half.1.keep_ref, f32[512,512]{1,0:T(8,128)S(1)} %collective-permute-done.11.got_ref), custom_call_target="tpu_custom_call" | custom-call | tf_op jit(solution)/shard_map/finish/pallas_call | solution.py:216
  62.5 27.7 %all_to_all.10 = bf16[128,8,512]{2,1,0:T(8,128)(2,1)S(1)} all-to-all(bf16[128,8,512]{2,1,0:T(8,128)(2,1)S(1)} %bitcast.19), channel_id=1, replica_groups=mesh['zh'=2,'y'=4,'x'=4,'core'=2,'zl'=2] {'y','x','zh','zl','core'}, dimensions={0} | all-to-all | bytes 2097152 | tf_op jit(solution)/shard_map/all_to_all | solution.py:24
  (35 shorter events, 4.7 us)
Async XLA Ops:
  0.0 11.2 %copy-start.8 = (bf16[1024,1,64]{0,2,1:T(8,128)(2,1)S(1)}, bf16[1024,1,64]{0,2,1:T(8,128)(2,1)}, u32[]{:S(2)}) copy-start(bf16[1024,1,64]{0,2,1:T(8,128)(2,1)} %param.6) | copy-start | bytes 393220
  0.0 11.3 %copy-start.9 = (bf16[1,8,1024]{2,1,0:T(8,128)(2,1)S(1)}, bf16[1,8,1024]{2,1,0:T(8,128)(2,1)}, u32[]{:S(2)}) copy-start(bf16[1,8,1024]{2,1,0:T(8,128)(2,1)} %param.4) | copy-start | bytes 49156
  0.0 11.2 %collective-permute-start.2 = (bf16[64,1024]{1,0:T(8,128)(2,1)}, bf16[64,1024]{1,0:T(8,128)(2,1)S(1)}, u32[]{:S(2)}, u32[]{:S(2)}) collective-permute-start(bf16[64,1024]{1,0:T(8,128)(2,1)} %bitcast.25), channel_id=1, source_target_pairs={{0,8},{4,12},{8,0},{12,4},{1,9},{5,13},{9,1},{13,5},{2,10},{6,14},... | collective-permute-start | bytes 393224 | tf_op jit(solution)/shard_map/ppermute | solution.py:20
  3.6 7.7 %collective-permute-start.1 = (bf16[64,1024]{1,0:T(8,128)(2,1)}, bf16[64,1024]{1,0:T(8,128)(2,1)S(1)}, u32[]{:S(2)}, u32[]{:S(2)}) collective-permute-start(bf16[64,1024]{1,0:T(8,128)(2,1)} %bitcast.26), channel_id=1, source_target_pairs={{0,12},{4,0},{8,4},{12,8},{1,13},{5,1},{9,5},{13,9},{2,14},{6,2},{... | collective-permute-start | bytes 393224 | tf_op jit(solution)/shard_map/ppermute | solution.py:20
  4.4 6.8 %collective-permute-start = (bf16[64,1024]{1,0:T(8,128)(2,1)}, bf16[64,1024]{1,0:T(8,128)(2,1)S(1)}, u32[]{:S(2)}, u32[]{:S(2)}) collective-permute-start(bf16[64,1024]{1,0:T(8,128)(2,1)} %bitcast.27), channel_id=1, source_target_pairs={{0,4},{4,8},{8,12},{12,0},{1,5},{5,9},{9,13},{13,1},{2,6},{6,10},{... | collective-permute-start | bytes 393224 | tf_op jit(solution)/shard_map/ppermute | solution.py:20
  6.1 1.6 %copy-start = (f32[128,4096]{1,0:T(8,128)S(1)}, f32[128,4096]{1,0:T(8,128)}, u32[]{:S(2)}) copy-start(f32[128,4096]{1,0:T(8,128)} %in_ref.1) | copy-start | bytes 6291460
  9.6 0.8 copy-start.3
  10.4 0.8 copy-start.7
  12.4 14.8 %collective-permute-start.7 = (bf16[256,1024]{1,0:T(8,128)(2,1)S(1)}, bf16[256,1024]{1,0:T(8,128)(2,1)S(1)}, u32[]{:S(2)}, u32[]{:S(2)}) collective-permute-start(bf16[256,1024]{1,0:T(8,128)(2,1)S(1)} %pad_maximum_fusion.refs_0_), channel_id=1, source_target_pairs={{0,48},{16,0},{32,16},{48,32},{1,49},{17,1},{33,17},{49,33},{2,50}... | collective-permute-start | bytes 1572872 | tf_op jit(solution)/shard_map/ppermute | solution.py:20
  15.2 14.8 %collective-permute-start.5 = (bf16[256,1024]{1,0:T(8,128)(2,1)S(1)}, bf16[256,1024]{1,0:T(8,128)(2,1)}, u32[]{:S(2)}, u32[]{:S(2)}) collective-permute-start(bf16[256,1024]{1,0:T(8,128)(2,1)S(1)} %pad_maximum_fusion.refs_0_), channel_id=1, source_target_pairs={{0,16},{16,32},{32,48},{48,0},{1,17},{17,33},{33,49},{49,1},{2,18}... | collective-permute-start | bytes 1572872 | tf_op jit(solution)/shard_map/ppermute | solution.py:20
  15.2 32.6 %collective-permute-start.4 = (bf16[3,128,1024]{2,1,0:T(8,128)(2,1)}, bf16[3,128,1024]{2,1,0:T(8,128)(2,1)S(1)}, u32[]{:S(2)}, u32[]{:S(2)}) collective-permute-start(bf16[3,128,1024]{2,1,0:T(8,128)(2,1)} %get-tuple-element.24), channel_id=1, source_target_pairs={{0,64},{64,0},{1,65},{65,1},{2,66},{66,2},{3,67},{67,3},{4,68},{68... | collective-permute-start | bytes 2359304 | tf_op jit(solution)/shard_map/ppermute | solution.py:240
  18.8 30.7 %all-to-all-start = ((bf16[128,8,512]{2,1,0:T(8,128)(2,1)}), bf16[128,8,512]{2,1,0:T(8,128)(2,1)S(1)}, u32[]{:S(2)}, u32[]{:S(2)}) async-start(bf16[128,8,512]{2,1,0:T(8,128)(2,1)} %bitcast.22), calls=%async_computation | async-start | bytes 2097152 | tf_op jit(solution)/shard_map/all_to_all | solution.py:24
  27.2 3.7 %copy-start.1 = (bf16[256,1024]{1,0:T(8,128)(2,1)}, bf16[256,1024]{1,0:T(8,128)(2,1)S(1)}, u32[]{:S(2)}) copy-start(bf16[256,1024]{1,0:T(8,128)(2,1)S(1)} %collective-permute-done.7.refs_2_) | copy-start | bytes 1572868
  27.2 18.3 %collective-permute-start.8 = (bf16[128,1024]{1,0:T(8,128)(2,1)S(1)}, bf16[128,1024]{1,0:T(8,128)(2,1)S(1)}, u32[]{:S(2)}, u32[]{:S(2)}) collective-permute-start(bf16[128,1024]{1,0:T(8,128)(2,1)S(1)} %slice.13), channel_id=1, source_target_pairs={{0,48},{16,0},{32,16},{48,32},{1,49},{17,1},{33,17},{49,33},{2,50}... | collective-permute-start | bytes 786440 | tf_op jit(solution)/shard_map/ppermute | solution.py:20
  30.9 16.1 %collective-permute-start.6 = (bf16[128,1024]{1,0:T(8,128)(2,1)S(1)}, bf16[128,1024]{1,0:T(8,128)(2,1)S(1)}, u32[]{:S(2)}, u32[]{:S(2)}) collective-permute-start(bf16[128,1024]{1,0:T(8,128)(2,1)S(1)} %slice.12), channel_id=1, source_target_pairs={{0,16},{16,32},{32,48},{48,0},{1,17},{17,33},{33,49},{49,1},{2,18}... | collective-permute-start | bytes 786440 | tf_op jit(solution)/shard_map/ppermute | solution.py:20
  31.0 18.4 %collective-permute-start.3 = (bf16[2,128,1024]{2,1,0:T(8,128)(2,1)}, bf16[2,128,1024]{2,1,0:T(8,128)(2,1)S(1)}, u32[]{:S(2)}, u32[]{:S(2)}) collective-permute-start(bf16[2,128,1024]{2,1,0:T(8,128)(2,1)} %copy-done.7), channel_id=1, source_target_pairs={{0,2},{2,0},{1,3},{3,1},{4,6},{6,4},{5,7},{7,5},{8,10},{10,8},{9,1... | collective-permute-start | bytes 1572872 | tf_op jit(solution)/shard_map/ppermute | solution.py:28
  47.0 0.7 copy-start.5
  48.6 2.7 %collective-permute-start.9 = (bf16[2,128,1024]{2,1,0:T(8,128)(2,1)}, bf16[2,128,1024]{2,1,0:T(8,128)(2,1)}, u32[]{:S(2)}, u32[]{:S(2)}) collective-permute-start(bf16[2,128,1024]{2,1,0:T(8,128)(2,1)} %slice.11), channel_id=1, source_target_pairs={{0,2},{2,0},{1,3},{3,1},{4,6},{6,4},{5,7},{7,5},{8,10},{10,8},{9,1... | collective-permute-start | bytes 1572872 | tf_op jit(solution)/shard_map/ppermute | solution.py:28
  49.4 5.8 %copy-start.2 = (bf16[256,1024]{1,0:T(8,128)(2,1)S(1)}, bf16[256,1024]{1,0:T(8,128)(2,1)}, u32[]{:S(2)}) copy-start(bf16[256,1024]{1,0:T(8,128)(2,1)} %copy-done.1) | copy-start | bytes 1572868
  49.4 5.8 %copy-start.4 = (f32[128,1024]{1,0:T(8,128)S(1)}, f32[128,1024]{1,0:T(8,128)}, u32[]{:S(2)}) copy-start(f32[128,1024]{1,0:T(8,128)} %copy-done.3) | copy-start | bytes 1572868
  49.5 5.8 %copy-start.6 = (bf16[128,1024]{1,0:T(8,128)(2,1)S(1)}, bf16[128,1024]{1,0:T(8,128)(2,1)}, u32[]{:S(2)}) copy-start(bf16[128,1024]{1,0:T(8,128)(2,1)} %copy-done.5) | copy-start | bytes 786436
  53.3 2.0 %collective-permute-start.10 = (bf16[512,512]{1,0:T(8,128)(2,1)S(1)}, bf16[512,512]{1,0:T(8,128)(2,1)S(1)}, u32[]{:S(2)}, u32[]{:S(2)}) collective-permute-start(bf16[512,512]{1,0:T(8,128)(2,1)S(1)} %get-tuple-element.28.own_ref), channel_id=1, source_target_pairs={{0,2},{2,0},{1,3},{3,1},{4,6},{6,4},{5,7},{7,5},{8,10},{10,8},{9,1... | collective-permute-start | bytes 1572872 | tf_op jit(solution)/shard_map/ppermute | solution.py:28
  58.5 2.8 %collective-permute-start.11 = (f32[512,512]{1,0:T(8,128)S(1)}, f32[512,512]{1,0:T(8,128)S(1)}, u32[]{:S(2)}, u32[]{:S(2)}) collective-permute-start(f32[512,512]{1,0:T(8,128)S(1)} %get-tuple-element.34), channel_id=1, source_target_pairs={{0,2},{2,0},{1,3},{3,1},{4,6},{6,4},{5,7},{7,5},{8,10},{10,8},{9,1... | collective-permute-start | bytes 3145736 | tf_op jit(solution)/shard_map/ppermute | solution.py:28

commit v23 on v17

--- a/solution.py
+++ b/solution.py
@@ -160,14 +160,15 @@
                 0,
             )
             weighted_ref[:, here] = weighted
-        send_ref[...] = jnp.dot(weighted_ref[...], panel_ref[:, sibs], preferred_element_type=F32)
+        send = jnp.dot(weighted_ref[...], panel_ref[:, sibs], preferred_element_type=F32)
+        send_ref[...] = send.astype(BF16)
 
     return pl.pallas_call(
         kernel,
         out_shape=[
             jax.ShapeDtypeStruct((rows, count), BF16),
             jax.ShapeDtypeStruct((count, states), BF16),
-            jax.ShapeDtypeStruct((rows, half), F32),
+            jax.ShapeDtypeStruct((rows, half), BF16),
         ],
         in_specs=[vmem_spec()] * 11,
         out_specs=[vmem_spec()] * 3,
@@ -204,7 +205,7 @@
         for k in range(4):
             here = slice(k * points, (k + 1) * points)
             there = slice(SIBLING[k] * points, (SIBLING[k] + 1) * points)
-            back = keep_ref[here, :] + got_ref[there, :]
+            back = keep_ref[here, :] + got_ref[there, :].astype(F32)
             top = back.astype(BF16)
             high[here, :] = top
             low[here, :] = (back - top.astype(F32)).astype(BF16)

time: 89.3 us -> 88.5 us (level)
  no operation moved by 1% of the time
where the time goes in v23:
time: 88.5 us; the launch traced here: 88.3 us
  blocking collectives  27.1 us (31%)
  starting transfers between devices  25.3 us (29%)
  waiting for transfers between devices  19.4 us (22%)
  local copies, waits for them, and re-layouts  8.53 us (10%)
  Pallas kernels  6.92 us (8%)
    all_to_all x1, blocking collectives, exchange(): return lax.all_to_all(value, axes, split_axis=0, concat_axis=0, tiled=True)  27.1 us
    ppermute x7, waiting for transfers between devices, shift(): return lax.ppermute(value, axis, [(k, (k + by) % n) for k in range(n)])  15.4 us
    ppermute x7, starting transfers between devices, shift(): return lax.ppermute(value, axis, [(k, (k + by) % n) for k in range(n)])  10.6 us
    all_to_all x1, starting transfers between devices, exchange(): return lax.all_to_all(value, axes, split_axis=0, concat_axis=0, tiled=True)  8.41 us
    unnamed x32, local copies, waits for them, and re-layouts  6.53 us
    ppermute x4, waiting for transfers between devices, swap(): return lax.ppermute(value, 'core', [(0, 1), (1, 0)])  4.09 us
    ppermute x1, starting transfers between devices, shards(): far = lax.ppermute(far, 'zh', [(0, 1), (1, 0)])  3.6 us
    ppermute x4, starting transfers between devices, swap(): return lax.ppermute(value, 'core', [(0, 1), (1, 0)])  2.69 us
  transfers between devices with their start and end apart: 13, of which 5 were waited for; matrix products, arithmetic and copies ran while one was open for 1% of the time, Pallas kernels for 3%

profile of v23, /device:TPU:1, one launch (start us, length us, event | category | flops | bytes accessed | tf_op | source)
XLA Modules:
  0.0 88.3 jit_solution(4035560094006556226)
XLA Ops:
  0.0 3.6 %collective-permute-start.2 = (bf16[64,1024]{1,0:T(8,128)(2,1)}, bf16[64,1024]{1,0:T(8,128)(2,1)S(1)}, u32[]{:S(2)}, u32[]{:S(2)}) collective-permute-start(bf16[64,1024]{1,0:T(8,128)(2,1)} %bitcast.18), channel_id=1, source_target_pairs={{0,8},{4,12},{8,0},{12,4},{1,9},{5,13},{9,1},{13,5},{2,10},{6,14},... | collective-permute-start | bytes 393224 | tf_op jit(solution)/shard_map/ppermute | solution.py:19
  3.6 0.9 collective-permute-start.1
  5.0 1.6 %copy-done = f32[128,4096]{1,0:T(8,128)S(1)} copy-done((f32[128,4096]{1,0:T(8,128)S(1)}, f32[128,4096]{1,0:T(8,128)}, u32[]{:S(2)}) %copy-start) | copy-done | bytes 2097176
  6.6 0.9 %copy-done.5 = bf16[1024,128]{1,0:T(8,128)(2,1)S(1)} copy-done((bf16[1024,128]{1,0:T(8,128)(2,1)S(1)}, bf16[1024,128]{1,0:T(8,128)(2,1)}, u32[]{:S(2)}) %copy-start.5) | copy-done | bytes 262168
  7.6 2.0 %pack.1 = (f32[128,1024]{1,0:T(8,128)S(1)}, bf16[2,128,1024]{2,1,0:T(8,128)(2,1)S(1)}, bf16[3,128,1024]{2,1,0:T(8,128)(2,1)}) custom-call(f32[128,4096]{1,0:T(8,128)S(1)} %copy-done, bf16[1024,128]{1,0:T(8,128)(2,1)S(1)} %copy-done.5), custom_call_target="tpu_custom_call" | custom-call | tf_op jit(solution)/shard_map/pack/pallas_call | solution.py:69
  9.6 0.8 copy-done.7
  11.3 1.1 %broadcast_in_dim.2 = bf16[32,2,2,8,512]{4,3,2,1,0:T(8,128)(2,1)} broadcast(bf16[2,8,512]{2,1,0:T(8,128)(2,1)S(1)} %bitcast.22), dimensions={1,3,4} | broadcast | bytes 1064960 | tf_op jit(solution)/shard_map/broadcast_in_dim | solution.py:235
  12.4 2.7 %collective-permute-start.7 = (bf16[256,1024]{1,0:T(8,128)(2,1)S(1)}, bf16[256,1024]{1,0:T(8,128)(2,1)S(1)}, u32[]{:S(2)}, u32[]{:S(2)}) collective-permute-start(bf16[256,1024]{1,0:T(8,128)(2,1)S(1)} %pad_maximum_fusion.refs_0_), channel_id=1, source_target_pairs={{0,48},{16,0},{32,16},{48,32},{1,49},{17,1},{33,17},{49,33},{2,50}... | collective-permute-start | bytes 1572872 | tf_op jit(solution)/shard_map/ppermute | solution.py:19
  15.1 3.6 %collective-permute-start.4 = (bf16[3,128,1024]{2,1,0:T(8,128)(2,1)}, bf16[3,128,1024]{2,1,0:T(8,128)(2,1)S(1)}, u32[]{:S(2)}, u32[]{:S(2)}) collective-permute-start(bf16[3,128,1024]{2,1,0:T(8,128)(2,1)} %get-tuple-element.24), channel_id=1, source_target_pairs={{0,64},{64,0},{1,65},{65,1},{2,66},{66,2},{3,67},{67,3},{4,68},{68... | collective-permute-start | bytes 2359304 | tf_op jit(solution)/shard_map/ppermute | solution.py:239
  18.7 8.4 %all-to-all-start = ((bf16[128,8,512]{2,1,0:T(8,128)(2,1)}), bf16[128,8,512]{2,1,0:T(8,128)(2,1)S(1)}, u32[]{:S(2)}, u32[]{:S(2)}) async-start(bf16[128,8,512]{2,1,0:T(8,128)(2,1)} %bitcast.16), calls=%async_computation | async-start | bytes 2097152 | tf_op jit(solution)/shard_map/all_to_all | solution.py:23
  27.2 2.7 %collective-permute-start.8 = (bf16[128,1024]{1,0:T(8,128)(2,1)S(1)}, bf16[128,1024]{1,0:T(8,128)(2,1)S(1)}, u32[]{:S(2)}, u32[]{:S(2)}) collective-permute-start(bf16[128,1024]{1,0:T(8,128)(2,1)S(1)} %slice.13), channel_id=1, source_target_pairs={{0,48},{16,0},{32,16},{48,32},{1,49},{17,1},{33,17},{49,33},{2,50}... | collective-permute-start | bytes 786440 | tf_op jit(solution)/shard_map/ppermute | solution.py:19
  30.0 1.2 %collective-permute-start.3 = (bf16[2,128,1024]{2,1,0:T(8,128)(2,1)}, bf16[2,128,1024]{2,1,0:T(8,128)(2,1)S(1)}, u32[]{:S(2)}, u32[]{:S(2)}) collective-permute-start(bf16[2,128,1024]{2,1,0:T(8,128)(2,1)} %copy-done.13), channel_id=1, source_target_pairs={{0,2},{2,0},{1,3},{3,1},{4,6},{6,4},{5,7},{7,5},{8,10},{10,8},{9,1... | collective-permute-start | bytes 1572872 | tf_op jit(solution)/shard_map/ppermute | solution.py:27
  31.2 14.2 %collective-permute-done.8.refs_4_ = bf16[128,1024]{1,0:T(8,128)(2,1)S(1)} collective-permute-done((bf16[128,1024]{1,0:T(8,128)(2,1)S(1)}, bf16[128,1024]{1,0:T(8,128)(2,1)S(1)}, u32[]{:S(2)}, u32[]{:S(2)}) %collective-permute-start.8) | collective-permute-done | bytes 262176 | tf_op jit(solution)/shard_map/ppermute | solution.py:19
  46.1 1.2 %collective-permute-done.6.refs_3_ = bf16[128,1024]{1,0:T(8,128)(2,1)S(1)} collective-permute-done((bf16[128,1024]{1,0:T(8,128)(2,1)S(1)}, bf16[128,1024]{1,0:T(8,128)(2,1)S(1)}, u32[]{:S(2)}, u32[]{:S(2)}) %collective-permute-start.6) | collective-permute-done | bytes 262176 | tf_op jit(solution)/shard_map/ppermute | solution.py:19
  48.0 0.9 slice.11
  49.4 1.7 %collective-permute-done.9.refs_2_.refs_8_ = bf16[2,128,1024]{2,1,0:T(8,128)(2,1)S(1)} collective-permute-done((bf16[2,128,1024]{2,1,0:T(8,128)(2,1)}, bf16[2,128,1024]{2,1,0:T(8,128)(2,1)S(1)}, u32[]{:S(2)}, u32[]{:S(2)}) %collective-permute-start.9) | collective-permute-done | bytes 524320 | tf_op jit(solution)/shard_map/ppermute | solution.py:27
  51.2 0.9 %copy-done.6 = bf16[1024,128]{1,0:T(8,128)(2,1)S(1)} copy-done((bf16[1024,128]{1,0:T(8,128)(2,1)S(1)}, bf16[1024,128]{1,0:T(8,128)(2,1)}, u32[]{:S(2)}) %copy-start.6) | copy-done | bytes 262168
  52.1 0.9 %project.1 = (bf16[512,512]{1,0:T(8,128)(2,1)S(1)}, bf16[1024,512]{1,0:T(8,128)(2,1)S(1)}) custom-call(bf16[1024,512]{1,0:T(8,128)(2,1)S(1)} %bitcast.14, bf16[1024,128]{1,0:T(8,128)(2,1)S(1)} %copy-done.6, bf16[2,128,1024]{2,1,0:T(8,128)(2,1)S(1)} %collective-permute-done.3.refs_0_.refs_6_, ...), custom_call_target="tpu_custom_call" | custom-call | tf_op jit(solution)/shard_map/project/pallas_call | solution.py:110
  53.5 1.5 %collective-permute-done.10.other_ref = bf16[512,512]{1,0:T(8,128)(2,1)S(1)} collective-permute-done((bf16[512,512]{1,0:T(8,128)(2,1)S(1)}, bf16[512,512]{1,0:T(8,128)(2,1)S(1)}, u32[]{:S(2)}, u32[]{:S(2)}) %collective-permute-start.10) | collective-permute-done | bytes 524320 | tf_op jit(solution)/shard_map/ppermute | solution.py:27
  55.1 2.0 %direct.1 = (bf16[512,1024]{1,0:T(8,128)(2,1)S(1)}, bf16[1024,1024]{1,0:T(8,128)(2,1)S(1)}, bf16[512,512]{1,0:T(8,128)(2,1)S(1)}) custom-call(bf16[512,512]{1,0:T(8,128)(2,1)S(1)} %get-tuple-element.28.own_ref, bf16[512,512]{1,0:T(8,128)(2,1)S(1)} %collective-permute-done.10.other_ref, bf16[256,1024]{1,0:T(8,128)(2,1)S(1)} %pad_maximum_fusion.refs_0_, ...), custom_call_target="tpu_custom_call" | custom-call | tf_op jit(solution)/shard_map/direct/pallas_call | solution.py:166
  58.2 0.8 collective-permute-done.11.got_ref
  59.1 1.3 %finish.1 = bf16[1024,512]{1,0:T(8,128)(2,1)S(1)} custom-call(bf16[1024,512]{1,0:T(8,128)(2,1)S(1)} %get-tuple-element.27.psi_ref, f32[512,512]{1,0:T(8,128)S(1)} %own_half.1.keep_ref, bf16[512,512]{1,0:T(8,128)(2,1)S(1)} %collective-permute-done.11.got_ref), custom_call_target="tpu_custom_call" | custom-call | tf_op jit(solution)/shard_map/finish/pallas_call | solution.py:216
  60.4 27.1 %all_to_all.10 = bf16[128,8,512]{2,1,0:T(8,128)(2,1)S(1)} all-to-all(bf16[128,8,512]{2,1,0:T(8,128)(2,1)S(1)} %bitcast.15), channel_id=1, replica_groups=mesh['zh'=2,'y'=4,'x'=4,'core'=2,'zl'=2] {'zh','y','x','core','zl'}, dimensions={0} | all-to-all | bytes 2097152 | tf_op jit(solution)/shard_map/all_to_all | solution.py:23
  87.5 0.8 convert_reduce_fusion
  (46 shorter events, 5.2 us)
Async XLA Ops:
  0.0 11.2 %collective-permute-start.2 = (bf16[64,1024]{1,0:T(8,128)(2,1)}, bf16[64,1024]{1,0:T(8,128)(2,1)S(1)}, u32[]{:S(2)}, u32[]{:S(2)}) collective-permute-start(bf16[64,1024]{1,0:T(8,128)(2,1)} %bitcast.18), channel_id=1, source_target_pairs={{0,8},{4,12},{8,0},{12,4},{1,9},{5,13},{9,1},{13,5},{2,10},{6,14},... | collective-permute-start | bytes 393224 | tf_op jit(solution)/shard_map/ppermute | solution.py:19
  3.6 7.6 %collective-permute-start.1 = (bf16[64,1024]{1,0:T(8,128)(2,1)}, bf16[64,1024]{1,0:T(8,128)(2,1)S(1)}, u32[]{:S(2)}, u32[]{:S(2)}) collective-permute-start(bf16[64,1024]{1,0:T(8,128)(2,1)} %bitcast.19), channel_id=1, source_target_pairs={{0,12},{4,0},{8,4},{12,8},{1,13},{5,1},{9,5},{13,9},{2,14},{6,2},{... | collective-permute-start | bytes 393224 | tf_op jit(solution)/shard_map/ppermute | solution.py:19
  4.4 6.7 %collective-permute-start = (bf16[64,1024]{1,0:T(8,128)(2,1)}, bf16[64,1024]{1,0:T(8,128)(2,1)S(1)}, u32[]{:S(2)}, u32[]{:S(2)}) collective-permute-start(bf16[64,1024]{1,0:T(8,128)(2,1)} %bitcast.20), channel_id=1, source_target_pairs={{0,4},{4,8},{8,12},{12,0},{1,5},{5,9},{9,13},{13,1},{2,6},{6,10},{... | collective-permute-start | bytes 393224 | tf_op jit(solution)/shard_map/ppermute | solution.py:19
  5.0 1.6 %copy-start = (f32[128,4096]{1,0:T(8,128)S(1)}, f32[128,4096]{1,0:T(8,128)}, u32[]{:S(2)}) copy-start(f32[128,4096]{1,0:T(8,128)} %in_ref.1) | copy-start | bytes 6291460
  6.6 0.9 %copy-start.5 = (bf16[1024,128]{1,0:T(8,128)(2,1)S(1)}, bf16[1024,128]{1,0:T(8,128)(2,1)}, u32[]{:S(2)}) copy-start(bf16[1024,128]{1,0:T(8,128)(2,1)} %left_ref.3) | copy-start | bytes 786436
  7.6 3.6 %copy-start.14 = (bf16[1024,1,64]{0,2,1:T(8,128)(2,1)S(1)}, bf16[1024,1,64]{0,2,1:T(8,128)(2,1)}, u32[]{:S(2)}) copy-start(bf16[1024,1,64]{0,2,1:T(8,128)(2,1)} %param.6) | copy-start | bytes 393220
  7.6 3.7 %copy-start.15 = (bf16[1,8,1024]{2,1,0:T(8,128)(2,1)S(1)}, bf16[1,8,1024]{2,1,0:T(8,128)(2,1)}, u32[]{:S(2)}) copy-start(bf16[1,8,1024]{2,1,0:T(8,128)(2,1)} %param.4) | copy-start | bytes 49156
  12.4 14.8 %collective-permute-start.7 = (bf16[256,1024]{1,0:T(8,128)(2,1)S(1)}, bf16[256,1024]{1,0:T(8,128)(2,1)S(1)}, u32[]{:S(2)}, u32[]{:S(2)}) collective-permute-start(bf16[256,1024]{1,0:T(8,128)(2,1)S(1)} %pad_maximum_fusion.refs_0_), channel_id=1, source_target_pairs={{0,48},{16,0},{32,16},{48,32},{1,49},{17,1},{33,17},{49,33},{2,50}... | collective-permute-start | bytes 1572872 | tf_op jit(solution)/shard_map/ppermute | solution.py:19
  15.1 14.8 %collective-permute-start.5 = (bf16[256,1024]{1,0:T(8,128)(2,1)S(1)}, bf16[256,1024]{1,0:T(8,128)(2,1)S(1)}, u32[]{:S(2)}, u32[]{:S(2)}) collective-permute-start(bf16[256,1024]{1,0:T(8,128)(2,1)S(1)} %pad_maximum_fusion.refs_0_), channel_id=1, source_target_pairs={{0,16},{16,32},{32,48},{48,0},{1,17},{17,33},{33,49},{49,1},{2,18}... | collective-permute-start | bytes 1572872 | tf_op jit(solution)/shard_map/ppermute | solution.py:19
  15.1 32.9 %collective-permute-start.4 = (bf16[3,128,1024]{2,1,0:T(8,128)(2,1)}, bf16[3,128,1024]{2,1,0:T(8,128)(2,1)S(1)}, u32[]{:S(2)}, u32[]{:S(2)}) collective-permute-start(bf16[3,128,1024]{2,1,0:T(8,128)(2,1)} %get-tuple-element.24), channel_id=1, source_target_pairs={{0,64},{64,0},{1,65},{65,1},{2,66},{66,2},{3,67},{67,3},{4,68},{68... | collective-permute-start | bytes 2359304 | tf_op jit(solution)/shard_map/ppermute | solution.py:239
  18.7 30.7 %all-to-all-start = ((bf16[128,8,512]{2,1,0:T(8,128)(2,1)}), bf16[128,8,512]{2,1,0:T(8,128)(2,1)S(1)}, u32[]{:S(2)}, u32[]{:S(2)}) async-start(bf16[128,8,512]{2,1,0:T(8,128)(2,1)} %bitcast.16), calls=%async_computation | async-start | bytes 2097152 | tf_op jit(solution)/shard_map/all_to_all | solution.py:23
  27.1 2.8 %copy-start.1 = (bf16[256,1024]{1,0:T(8,128)(2,1)}, bf16[256,1024]{1,0:T(8,128)(2,1)S(1)}, u32[]{:S(2)}) copy-start(bf16[256,1024]{1,0:T(8,128)(2,1)S(1)} %collective-permute-done.7.refs_2_) | copy-start | bytes 1572868
  27.2 18.2 %collective-permute-start.8 = (bf16[128,1024]{1,0:T(8,128)(2,1)S(1)}, bf16[128,1024]{1,0:T(8,128)(2,1)S(1)}, u32[]{:S(2)}, u32[]{:S(2)}) collective-permute-start(bf16[128,1024]{1,0:T(8,128)(2,1)S(1)} %slice.13), channel_id=1, source_target_pairs={{0,48},{16,0},{32,16},{48,32},{1,49},{17,1},{33,17},{49,33},{2,50}... | collective-permute-start | bytes 786440 | tf_op jit(solution)/shard_map/ppermute | solution.py:19
  29.9 18.1 %copy-start.3 = (bf16[256,1024]{1,0:T(8,128)(2,1)}, bf16[256,1024]{1,0:T(8,128)(2,1)S(1)}, u32[]{:S(2)}) copy-start(bf16[256,1024]{1,0:T(8,128)(2,1)S(1)} %collective-permute-done.5.refs_1_) | copy-start | bytes 1572868
  29.9 17.4 %collective-permute-start.6 = (bf16[128,1024]{1,0:T(8,128)(2,1)S(1)}, bf16[128,1024]{1,0:T(8,128)(2,1)S(1)}, u32[]{:S(2)}, u32[]{:S(2)}) collective-permute-start(bf16[128,1024]{1,0:T(8,128)(2,1)S(1)} %slice.12), channel_id=1, source_target_pairs={{0,16},{16,32},{32,48},{48,0},{1,17},{17,33},{33,49},{49,1},{2,18}... | collective-permute-start | bytes 786440 | tf_op jit(solution)/shard_map/ppermute | solution.py:19
  30.0 19.4 %collective-permute-start.3 = (bf16[2,128,1024]{2,1,0:T(8,128)(2,1)}, bf16[2,128,1024]{2,1,0:T(8,128)(2,1)S(1)}, u32[]{:S(2)}, u32[]{:S(2)}) collective-permute-start(bf16[2,128,1024]{2,1,0:T(8,128)(2,1)} %copy-done.13), channel_id=1, source_target_pairs={{0,2},{2,0},{1,3},{3,1},{4,6},{6,4},{5,7},{7,5},{8,10},{10,8},{9,1... | collective-permute-start | bytes 1572872 | tf_op jit(solution)/shard_map/ppermute | solution.py:27
  48.8 2.3 %collective-permute-start.9 = (bf16[2,128,1024]{2,1,0:T(8,128)(2,1)}, bf16[2,128,1024]{2,1,0:T(8,128)(2,1)S(1)}, u32[]{:S(2)}, u32[]{:S(2)}) collective-permute-start(bf16[2,128,1024]{2,1,0:T(8,128)(2,1)} %slice.11), channel_id=1, source_target_pairs={{0,2},{2,0},{1,3},{3,1},{4,6},{6,4},{5,7},{7,5},{8,10},{10,8},{9,1... | collective-permute-start | bytes 1572872 | tf_op jit(solution)/shard_map/ppermute | solution.py:27
  49.4 5.6 %copy-start.2 = (bf16[256,1024]{1,0:T(8,128)(2,1)S(1)}, bf16[256,1024]{1,0:T(8,128)(2,1)}, u32[]{:S(2)}) copy-start(bf16[256,1024]{1,0:T(8,128)(2,1)} %copy-done.1) | copy-start | bytes 1572868
  49.4 5.6 %copy-start.4 = (bf16[256,1024]{1,0:T(8,128)(2,1)S(1)}, bf16[256,1024]{1,0:T(8,128)(2,1)}, u32[]{:S(2)}) copy-start(bf16[256,1024]{1,0:T(8,128)(2,1)} %copy-done.3) | copy-start | bytes 1572868
  52.1 2.9 %copy-start.8 = (f32[128,1024]{1,0:T(8,128)S(1)}, f32[128,1024]{1,0:T(8,128)}, u32[]{:S(2)}) copy-start(f32[128,1024]{1,0:T(8,128)} %copy-done.7) | copy-start | bytes 1572868
  52.1 2.9 %copy-start.10 = (bf16[128,1024]{1,0:T(8,128)(2,1)S(1)}, bf16[128,1024]{1,0:T(8,128)(2,1)}, u32[]{:S(2)}) copy-start(bf16[128,1024]{1,0:T(8,128)(2,1)} %copy-done.9) | copy-start | bytes 786436
  52.1 3.0 %copy-start.12 = (bf16[128,1024]{1,0:T(8,128)(2,1)S(1)}, bf16[128,1024]{1,0:T(8,128)(2,1)}, u32[]{:S(2)}) copy-start(bf16[128,1024]{1,0:T(8,128)(2,1)} %copy-done.11) | copy-start | bytes 786436
  53.1 2.0 %collective-permute-start.10 = (bf16[512,512]{1,0:T(8,128)(2,1)S(1)}, bf16[512,512]{1,0:T(8,128)(2,1)S(1)}, u32[]{:S(2)}, u32[]{:S(2)}) collective-permute-start(bf16[512,512]{1,0:T(8,128)(2,1)S(1)} %get-tuple-element.28.own_ref), channel_id=1, source_target_pairs={{0,2},{2,0},{1,3},{3,1},{4,6},{6,4},{5,7},{7,5},{8,10},{10,8},{9,1... | collective-permute-start | bytes 1572872 | tf_op jit(solution)/shard_map/ppermute | solution.py:27
  57.1 2.0 %collective-permute-start.11 = (bf16[512,512]{1,0:T(8,128)(2,1)S(1)}, bf16[512,512]{1,0:T(8,128)(2,1)S(1)}, u32[]{:S(2)}, u32[]{:S(2)}) collective-permute-start(bf16[512,512]{1,0:T(8,128)(2,1)S(1)} %get-tuple-element.34), channel_id=1, source_target_pairs={{0,2},{2,0},{1,3},{3,1},{4,6},{6,4},{5,7},{7,5},{8,10},{10,8},{9,1... | collective-permute-start | bytes 1572872 | tf_op jit(solution)/shard_map/ppermute | solution.py:27
  (5 other events, 4.0 us)

commit v24 on v23

--- a/solution.py
+++ b/solution.py
@@ -121,15 +121,16 @@
     )(trial_half, left, near, far, passed)
 
 
-def direct(proj_own, proj_other, lines, own, boxes):
+NT = (((1,), (1,)), ((), ()))
+
+
+def own_pairs(proj_own, lines):
     rows, half = proj_own.shape
-    points = rows // 4
     block = lines[0].shape[0] // 4
     count, states = 16 * block, lines[0].shape[1]
-    chunk = 512
-
-    def kernel(own_ref, other_ref, *refs):
-        line_refs, scr_refs, (weighted_ref, panel_ref, send_ref, proj) = refs[:5], refs[5:9], refs[9:]
+
+    def kernel(own_ref, *refs):
+        line_refs, (panel_ref, pair_ref) = refs[:5], refs[5:]
         y, x = lax.axis_index("y"), lax.axis_index("x")
         for k in range(16):
             at = lax.rem(y + STEPS[k // 4] + 4, 4) * 4 + lax.rem(x + STEPS[k % 4] + 4, 4)
@@ -137,29 +138,45 @@
             panel_ref[pl.ds(pl.multiple_of(at * block, block), block), :] = ref[
                 row * block : (row + 1) * block, :
             ]
+        mine = pl.ds(pl.multiple_of(lax.axis_index("core") * half, half), half)
+        pair_ref[...] = lax.dot_general(own_ref[...], panel_ref[:, mine], NT, preferred_element_type=F32)
+
+    return pl.pallas_call(
+        kernel,
+        out_shape=[
+            jax.ShapeDtypeStruct((count, states), BF16),
+            jax.ShapeDtypeStruct((rows, count), F32),
+        ],
+        in_specs=[vmem_spec()] * 6,
+        out_specs=[vmem_spec()] * 2,
+        compiler_params=params(16),
+        name="own_pairs",
+    )(proj_own, *lines)
+
+
+def direct(proj_other, panel, pairs, own, boxes):
+    rows, half = proj_other.shape
+    points = rows // 4
+    count = panel.shape[0]
+    chunk = 512
+
+    def kernel(other_ref, panel_ref, pair_ref, *refs):
+        scr_refs, (weighted_ref, send_ref, proj) = refs[:4], refs[4:]
         core = lax.axis_index("core")
-        mine = pl.ds(pl.multiple_of(core * half, half), half)
         sibs = pl.ds(pl.multiple_of((1 - core) * half, half), half)
         for k in range(4):
             proj[k * points : (k + 1) * points, :] = other_ref[
                 SIBLING[k] * points : (SIBLING[k] + 1) * points, :
             ]
-        nt = (((1,), (1,)), ((), ()))
         for k in range(count // chunk):
             here = pl.ds(k * chunk, chunk)
-            pair = lax.dot_general(own_ref[...], panel_ref[here, mine], nt, preferred_element_type=F32)
-            pair += lax.dot_general(proj[...], panel_ref[here, sibs], nt, preferred_element_type=F32)
-            weighted = jnp.concatenate(
-                [
-                    (
-                        (scr_refs[0][:, here] if j == 0 else scr_refs[j][0, :, here].astype(F32))
-                        * pair[j * points : (j + 1) * points]
-                    ).astype(BF16)
-                    for j in range(4)
-                ],
-                0,
+            pair = pair_ref[:, here] + lax.dot_general(
+                proj[...], panel_ref[here, sibs], NT, preferred_element_type=F32
             )
-            weighted_ref[:, here] = weighted
+            for j in range(4):
+                mine = slice(j * points, (j + 1) * points)
+                weights = scr_refs[j][:, here] if j == 0 else scr_refs[j][0, :, here].astype(F32)
+                weighted_ref[mine, here] = (weights * pair[mine]).astype(BF16)
         send = jnp.dot(weighted_ref[...], panel_ref[:, sibs], preferred_element_type=F32)
         send_ref[...] = send.astype(BF16)
 
@@ -167,15 +184,14 @@
         kernel,
         out_shape=[
             jax.ShapeDtypeStruct((rows, count), BF16),
-            jax.ShapeDtypeStruct((count, states), BF16),
             jax.ShapeDtypeStruct((rows, half), BF16),
         ],
-        in_specs=[vmem_spec()] * 11,
-        out_specs=[vmem_spec()] * 3,
+        in_specs=[vmem_spec()] * 7,
+        out_specs=[vmem_spec()] * 2,
         scratch_shapes=[pltpu.VMEM((rows, half), BF16)],
         compiler_params=params(24),
         name="direct",
-    )(proj_own, proj_other, *lines, own, *boxes)
+    )(proj_other, panel, pairs, own, *boxes)
 
 
 def own_half(weighted, panel):
@@ -245,7 +261,8 @@
     proj_own, psi = project(trial_half, psi_v, near, far, passed)
     proj_other = swap(proj_own)
     panel = [line, behind, ahead, *beyond]
-    weighted, ordered, send = direct(proj_own, proj_other, panel, own, [near, far, passed])
+    ordered, pairs = own_pairs(proj_own, panel)
+    weighted, send = direct(proj_other, ordered, pairs, own, [near, far, passed])
     got = swap(send)
     keep = own_half(weighted, ordered)
     term = finish(psi, keep, got)

time: 88.5 us -> 86.1 us (0.973)
  waiting for transfers between devices: 19.4 us -> 11.4 us
  starting transfers between devices: 25.3 us -> 32.4 us
  blocking collectives: 27.1 us -> 25.5 us
    ppermute x4, starting transfers between devices: 2.69 us -> 11 us  [swap(): return lax.ppermute(value, 'core', [(0, 1), (1, 0)])]
    ppermute x7, waiting for transfers between devices: 15.4 us -> 8.18 us  [shift(): return lax.ppermute(value, axis, [(k, (k + by) % n) for k in range(n)])]
    all_to_all x1, starting transfers between devices: 8.41 us -> 6.75 us  [exchange(): return lax.all_to_all(value, axes, split_axis=0, concat_axis=0, tiled=True)]
    all_to_all x1, blocking collectives: 27.1 us -> 25.5 us  [exchange(): return lax.all_to_all(value, axes, split_axis=0, concat_axis=0, tiled=True)]
    ppermute x4, waiting for transfers between devices: 4.09 us -> 3.18 us  [swap(): return lax.ppermute(value, 'core', [(0, 1), (1, 0)])]
    pallas_call x0 -> x1, Pallas kernels: none -> 0.9 us  [own_pairs(): pl.pallas_call(kernel, out_shape=[jax.ShapeDtypeStruct((count, states), B...]
  transfers between devices with their start and end apart: 13 -> 13, of which waited for: 5 -> 5; matrix products, arithmetic and copies ran while one was open for 1% -> 1% of each run, Pallas kernels for 3% -> 4%
where the time goes in v24:
time: 86.1 us; the launch traced here: 85.8 us
  starting transfers between devices  32.4 us (38%)
  blocking collectives  25.5 us (30%)
  waiting for transfers between devices  11.4 us (13%)
  local copies, waits for them, and re-layouts  8.52 us (10%)
  Pallas kernels  7.09 us (8%)
    all_to_all x1, blocking collectives, exchange(): return lax.all_to_all(value, axes, split_axis=0, concat_axis=0, tiled=True)  25.5 us
    ppermute x7, starting transfers between devices, shift(): return lax.ppermute(value, axis, [(k, (k + by) % n) for k in range(n)])  11.1 us
    ppermute x4, starting transfers between devices, swap(): return lax.ppermute(value, 'core', [(0, 1), (1, 0)])  11 us
    ppermute x7, waiting for transfers between devices, shift(): return lax.ppermute(value, axis, [(k, (k + by) % n) for k in range(n)])  8.18 us
    all_to_all x1, starting transfers between devices, exchange(): return lax.all_to_all(value, axes, split_axis=0, concat_axis=0, tiled=True)  6.75 us
    unnamed x32, local copies, waits for them, and re-layouts  6.53 us
    ppermute x1, starting transfers between devices, shards(): far = lax.ppermute(far, 'zh', [(0, 1), (1, 0)])  3.6 us
    ppermute x4, waiting for transfers between devices, swap(): return lax.ppermute(value, 'core', [(0, 1), (1, 0)])  3.18 us
  transfers between devices with their start and end apart: 13, of which 5 were waited for; matrix products, arithmetic and copies ran while one was open for 1% of the time, Pallas kernels for 4%

profile of v24, /device:TPU:1, one launch (start us, length us, event | category | flops | bytes accessed | tf_op | source)
XLA Modules:
  0.0 85.8 jit_solution(688647494920579480)
XLA Ops:
  0.0 2.0 %collective-permute-start = (bf16[64,1024]{1,0:T(8,128)(2,1)}, bf16[64,1024]{1,0:T(8,128)(2,1)S(1)}, u32[]{:S(2)}, u32[]{:S(2)}) collective-permute-start(bf16[64,1024]{1,0:T(8,128)(2,1)} %bitcast.18), channel_id=1, source_target_pairs={{0,4},{4,8},{8,12},{12,0},{1,5},{5,9},{9,13},{13,1},{2,6},{6,10},{... | collective-permute-start | bytes 393224 | tf_op jit(solution)/shard_map/ppermute | solution.py:19
  2.0 1.3 %collective-permute-start.1 = (bf16[64,1024]{1,0:T(8,128)(2,1)}, bf16[64,1024]{1,0:T(8,128)(2,1)S(1)}, u32[]{:S(2)}, u32[]{:S(2)}) collective-permute-start(bf16[64,1024]{1,0:T(8,128)(2,1)} %bitcast.19), channel_id=1, source_target_pairs={{0,12},{4,0},{8,4},{12,8},{1,13},{5,1},{9,5},{13,9},{2,14},{6,2},{... | collective-permute-start | bytes 393224 | tf_op jit(solution)/shard_map/ppermute | solution.py:19
  3.3 1.7 %collective-permute-start.2 = (bf16[64,1024]{1,0:T(8,128)(2,1)}, bf16[64,1024]{1,0:T(8,128)(2,1)S(1)}, u32[]{:S(2)}, u32[]{:S(2)}) collective-permute-start(bf16[64,1024]{1,0:T(8,128)(2,1)} %bitcast.20), channel_id=1, source_target_pairs={{0,8},{4,12},{8,0},{12,4},{1,9},{5,13},{9,1},{13,5},{2,10},{6,14},... | collective-permute-start | bytes 393224 | tf_op jit(solution)/shard_map/ppermute | solution.py:19
  5.0 1.6 %copy-done = f32[128,4096]{1,0:T(8,128)S(1)} copy-done((f32[128,4096]{1,0:T(8,128)S(1)}, f32[128,4096]{1,0:T(8,128)}, u32[]{:S(2)}) %copy-start) | copy-done | bytes 2097176
  6.6 0.9 %copy-done.5 = bf16[1024,128]{1,0:T(8,128)(2,1)S(1)} copy-done((bf16[1024,128]{1,0:T(8,128)(2,1)S(1)}, bf16[1024,128]{1,0:T(8,128)(2,1)}, u32[]{:S(2)}) %copy-start.5) | copy-done | bytes 262168
  7.6 2.0 %pack.1 = (f32[128,1024]{1,0:T(8,128)S(1)}, bf16[2,128,1024]{2,1,0:T(8,128)(2,1)S(1)}, bf16[3,128,1024]{2,1,0:T(8,128)(2,1)}) custom-call(f32[128,4096]{1,0:T(8,128)S(1)} %copy-done, bf16[1024,128]{1,0:T(8,128)(2,1)S(1)} %copy-done.5), custom_call_target="tpu_custom_call" | custom-call | tf_op jit(solution)/shard_map/pack/pallas_call | solution.py:69
  11.2 1.1 %broadcast_in_dim.2 = bf16[32,2,2,8,512]{4,3,2,1,0:T(8,128)(2,1)} broadcast(bf16[2,8,512]{2,1,0:T(8,128)(2,1)S(1)} %bitcast.22), dimensions={1,3,4} | broadcast | bytes 1064960 | tf_op jit(solution)/shard_map/broadcast_in_dim | solution.py:251
  12.3 1.3 %collective-permute-start.5 = (bf16[256,1024]{1,0:T(8,128)(2,1)S(1)}, bf16[256,1024]{1,0:T(8,128)(2,1)S(1)}, u32[]{:S(2)}, u32[]{:S(2)}) collective-permute-start(bf16[256,1024]{1,0:T(8,128)(2,1)S(1)} %pad_maximum_fusion.refs_0_), channel_id=1, source_target_pairs={{0,16},{16,32},{32,48},{48,0},{1,17},{17,33},{33,49},{49,1},{2,18}... | collective-permute-start | bytes 1572872 | tf_op jit(solution)/shard_map/ppermute | solution.py:19
  13.6 1.4 %collective-permute-start.7 = (bf16[256,1024]{1,0:T(8,128)(2,1)S(1)}, bf16[256,1024]{1,0:T(8,128)(2,1)S(1)}, u32[]{:S(2)}, u32[]{:S(2)}) collective-permute-start(bf16[256,1024]{1,0:T(8,128)(2,1)S(1)} %pad_maximum_fusion.refs_0_), channel_id=1, source_target_pairs={{0,48},{16,0},{32,16},{48,32},{1,49},{17,1},{33,17},{49,33},{2,50}... | collective-permute-start | bytes 1572872 | tf_op jit(solution)/shard_map/ppermute | solution.py:19
  15.1 3.6 %collective-permute-start.4 = (bf16[3,128,1024]{2,1,0:T(8,128)(2,1)}, bf16[3,128,1024]{2,1,0:T(8,128)(2,1)S(1)}, u32[]{:S(2)}, u32[]{:S(2)}) collective-permute-start(bf16[3,128,1024]{2,1,0:T(8,128)(2,1)} %get-tuple-element.25), channel_id=1, source_target_pairs={{0,64},{64,0},{1,65},{65,1},{2,66},{66,2},{3,67},{67,3},{4,68},{68... | collective-permute-start | bytes 2359304 | tf_op jit(solution)/shard_map/ppermute | solution.py:255
  18.7 6.8 %all-to-all-start = ((bf16[128,8,512]{2,1,0:T(8,128)(2,1)}), bf16[128,8,512]{2,1,0:T(8,128)(2,1)S(1)}, u32[]{:S(2)}, u32[]{:S(2)}) async-start(bf16[128,8,512]{2,1,0:T(8,128)(2,1)} %bitcast.16), calls=%async_computation | async-start | bytes 2097152 | tf_op jit(solution)/shard_map/all_to_all | solution.py:23
  25.6 1.3 %collective-permute-start.6 = (bf16[128,1024]{1,0:T(8,128)(2,1)S(1)}, bf16[128,1024]{1,0:T(8,128)(2,1)S(1)}, u32[]{:S(2)}, u32[]{:S(2)}) collective-permute-start(bf16[128,1024]{1,0:T(8,128)(2,1)S(1)} %slice.12), channel_id=1, source_target_pairs={{0,16},{16,32},{32,48},{48,0},{1,17},{17,33},{33,49},{49,1},{2,18}... | collective-permute-start | bytes 786440 | tf_op jit(solution)/shard_map/ppermute | solution.py:19
  27.0 1.9 %collective-permute-start.8 = (bf16[128,1024]{1,0:T(8,128)(2,1)S(1)}, bf16[128,1024]{1,0:T(8,128)(2,1)S(1)}, u32[]{:S(2)}, u32[]{:S(2)}) collective-permute-start(bf16[128,1024]{1,0:T(8,128)(2,1)S(1)} %slice.13), channel_id=1, source_target_pairs={{0,48},{16,0},{32,16},{48,32},{1,49},{17,1},{33,17},{49,33},{2,50}... | collective-permute-start | bytes 786440 | tf_op jit(solution)/shard_map/ppermute | solution.py:19
  28.9 8.6 %collective-permute-start.3 = (bf16[2,128,1024]{2,1,0:T(8,128)(2,1)}, bf16[2,128,1024]{2,1,0:T(8,128)(2,1)S(1)}, u32[]{:S(2)}, u32[]{:S(2)}) collective-permute-start(bf16[2,128,1024]{2,1,0:T(8,128)(2,1)} %copy-done.13), channel_id=1, source_target_pairs={{0,2},{2,0},{1,3},{3,1},{4,6},{6,4},{5,7},{7,5},{8,10},{10,8},{9,1... | collective-permute-start | bytes 1572872 | tf_op jit(solution)/shard_map/ppermute | solution.py:27
  37.6 8.0 %collective-permute-done.6.refs_3_ = bf16[128,1024]{1,0:T(8,128)(2,1)S(1)} collective-permute-done((bf16[128,1024]{1,0:T(8,128)(2,1)S(1)}, bf16[128,1024]{1,0:T(8,128)(2,1)S(1)}, u32[]{:S(2)}, u32[]{:S(2)}) %collective-permute-start.6) | collective-permute-done | bytes 262176 | tf_op jit(solution)/shard_map/ppermute | solution.py:19
  47.0 0.8 slice.11
  47.9 1.4 %collective-permute-start.9 = (bf16[2,128,1024]{2,1,0:T(8,128)(2,1)}, bf16[2,128,1024]{2,1,0:T(8,128)(2,1)S(1)}, u32[]{:S(2)}, u32[]{:S(2)}) collective-permute-start(bf16[2,128,1024]{2,1,0:T(8,128)(2,1)} %slice.11), channel_id=1, source_target_pairs={{0,2},{2,0},{1,3},{3,1},{4,6},{6,4},{5,7},{7,5},{8,10},{10,8},{9,1... | collective-permute-start | bytes 1572872 | tf_op jit(solution)/shard_map/ppermute | solution.py:27
  49.3 1.7 %collective-permute-done.9.refs_2_.refs_3_ = bf16[2,128,1024]{2,1,0:T(8,128)(2,1)S(1)} collective-permute-done((bf16[2,128,1024]{2,1,0:T(8,128)(2,1)}, bf16[2,128,1024]{2,1,0:T(8,128)(2,1)S(1)}, u32[]{:S(2)}, u32[]{:S(2)}) %collective-permute-start.9) | collective-permute-done | bytes 524320 | tf_op jit(solution)/shard_map/ppermute | solution.py:27
  51.0 0.9 %copy-done.6 = bf16[1024,128]{1,0:T(8,128)(2,1)S(1)} copy-done((bf16[1024,128]{1,0:T(8,128)(2,1)S(1)}, bf16[1024,128]{1,0:T(8,128)(2,1)}, u32[]{:S(2)}) %copy-start.6) | copy-done | bytes 262168
  52.0 0.9 %project.1 = (bf16[512,512]{1,0:T(8,128)(2,1)S(1)}, bf16[1024,512]{1,0:T(8,128)(2,1)S(1)}) custom-call(bf16[1024,512]{1,0:T(8,128)(2,1)S(1)} %bitcast.14, bf16[1024,128]{1,0:T(8,128)(2,1)S(1)} %copy-done.6, bf16[2,128,1024]{2,1,0:T(8,128)(2,1)S(1)} %collective-permute-done.3.refs_0_.refs_1_, ...), custom_call_target="tpu_custom_call" | custom-call | tf_op jit(solution)/shard_map/project/pallas_call | solution.py:110
  53.4 0.9 %own_pairs.1 = (bf16[1024,1024]{1,0:T(8,128)(2,1)S(1)}, f32[512,1024]{1,0:T(8,128)S(1)}) custom-call(bf16[512,512]{1,0:T(8,128)(2,1)S(1)} %get-tuple-element.29.own_ref, bf16[256,1024]{1,0:T(8,128)(2,1)S(1)} %pad_maximum_fusion.refs_0_, bf16[256,1024]{1,0:T(8,128)(2,1)S(1)} %copy-done.2, bf16[256,1024]{1,0:T(8,128)(2,1)S(1)} %copy-done.4, ...), custom_call_target="tpu_custom_call" | custom-call | tf_op jit(solution)/shard_map/own_pairs/pallas_call | solution.py:144
  54.9 1.3 %direct.1 = (bf16[512,1024]{1,0:T(8,128)(2,1)S(1)}, bf16[512,512]{1,0:T(8,128)(2,1)S(1)}) custom-call(bf16[512,512]{1,0:T(8,128)(2,1)S(1)} %collective-permute-done.10.other_ref, bf16[1024,1024]{1,0:T(8,128)(2,1)S(1)} %get-tuple-element.32.panel_ref, f32[512,1024]{1,0:T(8,128)S(1)} %get-tuple-element.33.pair_ref, f32[128,1024]{1,0:T(8,128)S(1)} %copy-done.8, ...), custom_call_target="tpu_custom_call" | custom-call | tf_op jit(solution)/shard_map/direct/pallas_call | solution.py:183
  58.2 1.3 %finish.1 = bf16[1024,512]{1,0:T(8,128)(2,1)S(1)} custom-call(bf16[1024,512]{1,0:T(8,128)(2,1)S(1)} %get-tuple-element.28.psi_ref, f32[512,512]{1,0:T(8,128)S(1)} %own_half.1.keep_ref, bf16[512,512]{1,0:T(8,128)(2,1)S(1)} %collective-permute-done.11.got_ref), custom_call_target="tpu_custom_call" | custom-call | tf_op jit(solution)/shard_map/finish/pallas_call | solution.py:232
  59.5 25.5 %all_to_all.10 = bf16[128,8,512]{2,1,0:T(8,128)(2,1)S(1)} all-to-all(bf16[128,8,512]{2,1,0:T(8,128)(2,1)S(1)} %bitcast.15), channel_id=1, replica_groups=mesh['zh'=2,'y'=4,'x'=4,'core'=2,'zl'=2] {'zh','y','x','core','zl'}, dimensions={0} | all-to-all | bytes 2097152 | tf_op jit(solution)/shard_map/all_to_all | solution.py:23
  (47 shorter events, 7.2 us)
Async XLA Ops:
  0.0 11.2 %collective-permute-start = (bf16[64,1024]{1,0:T(8,128)(2,1)}, bf16[64,1024]{1,0:T(8,128)(2,1)S(1)}, u32[]{:S(2)}, u32[]{:S(2)}) collective-permute-start(bf16[64,1024]{1,0:T(8,128)(2,1)} %bitcast.18), channel_id=1, source_target_pairs={{0,4},{4,8},{8,12},{12,0},{1,5},{5,9},{9,13},{13,1},{2,6},{6,10},{... | collective-permute-start | bytes 393224 | tf_op jit(solution)/shard_map/ppermute | solution.py:19
  2.0 9.1 %collective-permute-start.1 = (bf16[64,1024]{1,0:T(8,128)(2,1)}, bf16[64,1024]{1,0:T(8,128)(2,1)S(1)}, u32[]{:S(2)}, u32[]{:S(2)}) collective-permute-start(bf16[64,1024]{1,0:T(8,128)(2,1)} %bitcast.19), channel_id=1, source_target_pairs={{0,12},{4,0},{8,4},{12,8},{1,13},{5,1},{9,5},{13,9},{2,14},{6,2},{... | collective-permute-start | bytes 393224 | tf_op jit(solution)/shard_map/ppermute | solution.py:19
  3.3 7.9 %collective-permute-start.2 = (bf16[64,1024]{1,0:T(8,128)(2,1)}, bf16[64,1024]{1,0:T(8,128)(2,1)S(1)}, u32[]{:S(2)}, u32[]{:S(2)}) collective-permute-start(bf16[64,1024]{1,0:T(8,128)(2,1)} %bitcast.20), channel_id=1, source_target_pairs={{0,8},{4,12},{8,0},{12,4},{1,9},{5,13},{9,1},{13,5},{2,10},{6,14},... | collective-permute-start | bytes 393224 | tf_op jit(solution)/shard_map/ppermute | solution.py:19
  5.0 1.6 %copy-start = (f32[128,4096]{1,0:T(8,128)S(1)}, f32[128,4096]{1,0:T(8,128)}, u32[]{:S(2)}) copy-start(f32[128,4096]{1,0:T(8,128)} %in_ref.1) | copy-start | bytes 6291460
  6.6 0.9 %copy-start.5 = (bf16[1024,128]{1,0:T(8,128)(2,1)S(1)}, bf16[1024,128]{1,0:T(8,128)(2,1)}, u32[]{:S(2)}) copy-start(bf16[1024,128]{1,0:T(8,128)(2,1)} %left_ref.3) | copy-start | bytes 786436
  7.6 3.6 %copy-start.14 = (bf16[1024,1,64]{0,2,1:T(8,128)(2,1)S(1)}, bf16[1024,1,64]{0,2,1:T(8,128)(2,1)}, u32[]{:S(2)}) copy-start(bf16[1024,1,64]{0,2,1:T(8,128)(2,1)} %param.6) | copy-start | bytes 393220
  7.6 3.6 %copy-start.15 = (bf16[1,8,1024]{2,1,0:T(8,128)(2,1)S(1)}, bf16[1,8,1024]{2,1,0:T(8,128)(2,1)}, u32[]{:S(2)}) copy-start(bf16[1,8,1024]{2,1,0:T(8,128)(2,1)} %param.4) | copy-start | bytes 49156
  12.3 13.2 %collective-permute-start.5 = (bf16[256,1024]{1,0:T(8,128)(2,1)S(1)}, bf16[256,1024]{1,0:T(8,128)(2,1)S(1)}, u32[]{:S(2)}, u32[]{:S(2)}) collective-permute-start(bf16[256,1024]{1,0:T(8,128)(2,1)S(1)} %pad_maximum_fusion.refs_0_), channel_id=1, source_target_pairs={{0,16},{16,32},{32,48},{48,0},{1,17},{17,33},{33,49},{49,1},{2,18}... | collective-permute-start | bytes 1572872 | tf_op jit(solution)/shard_map/ppermute | solution.py:19
  13.6 13.3 %collective-permute-start.7 = (bf16[256,1024]{1,0:T(8,128)(2,1)S(1)}, bf16[256,1024]{1,0:T(8,128)(2,1)S(1)}, u32[]{:S(2)}, u32[]{:S(2)}) collective-permute-start(bf16[256,1024]{1,0:T(8,128)(2,1)S(1)} %pad_maximum_fusion.refs_0_), channel_id=1, source_target_pairs={{0,48},{16,0},{32,16},{48,32},{1,49},{17,1},{33,17},{49,33},{2,50}... | collective-permute-start | bytes 1572872 | tf_op jit(solution)/shard_map/ppermute | solution.py:19
  15.1 31.9 %collective-permute-start.4 = (bf16[3,128,1024]{2,1,0:T(8,128)(2,1)}, bf16[3,128,1024]{2,1,0:T(8,128)(2,1)S(1)}, u32[]{:S(2)}, u32[]{:S(2)}) collective-permute-start(bf16[3,128,1024]{2,1,0:T(8,128)(2,1)} %get-tuple-element.25), channel_id=1, source_target_pairs={{0,64},{64,0},{1,65},{65,1},{2,66},{66,2},{3,67},{67,3},{4,68},{68... | collective-permute-start | bytes 2359304 | tf_op jit(solution)/shard_map/ppermute | solution.py:255
  18.7 30.6 %all-to-all-start = ((bf16[128,8,512]{2,1,0:T(8,128)(2,1)}), bf16[128,8,512]{2,1,0:T(8,128)(2,1)S(1)}, u32[]{:S(2)}, u32[]{:S(2)}) async-start(bf16[128,8,512]{2,1,0:T(8,128)(2,1)} %bitcast.16), calls=%async_computation | async-start | bytes 2097152 | tf_op jit(solution)/shard_map/all_to_all | solution.py:23
  25.6 1.4 %copy-start.1 = (bf16[256,1024]{1,0:T(8,128)(2,1)}, bf16[256,1024]{1,0:T(8,128)(2,1)S(1)}, u32[]{:S(2)}) copy-start(bf16[256,1024]{1,0:T(8,128)(2,1)S(1)} %collective-permute-done.5.refs_1_) | copy-start | bytes 1572868
  25.6 20.0 %collective-permute-start.6 = (bf16[128,1024]{1,0:T(8,128)(2,1)S(1)}, bf16[128,1024]{1,0:T(8,128)(2,1)S(1)}, u32[]{:S(2)}, u32[]{:S(2)}) collective-permute-start(bf16[128,1024]{1,0:T(8,128)(2,1)S(1)} %slice.12), channel_id=1, source_target_pairs={{0,16},{16,32},{32,48},{48,0},{1,17},{17,33},{33,49},{49,1},{2,18}... | collective-permute-start | bytes 786440 | tf_op jit(solution)/shard_map/ppermute | solution.py:19
  26.9 20.1 %copy-start.3 = (bf16[256,1024]{1,0:T(8,128)(2,1)}, bf16[256,1024]{1,0:T(8,128)(2,1)S(1)}, u32[]{:S(2)}) copy-start(bf16[256,1024]{1,0:T(8,128)(2,1)S(1)} %collective-permute-done.7.refs_2_) | copy-start | bytes 1572868
  27.0 19.3 %collective-permute-start.8 = (bf16[128,1024]{1,0:T(8,128)(2,1)S(1)}, bf16[128,1024]{1,0:T(8,128)(2,1)S(1)}, u32[]{:S(2)}, u32[]{:S(2)}) collective-permute-start(bf16[128,1024]{1,0:T(8,128)(2,1)S(1)} %slice.13), channel_id=1, source_target_pairs={{0,48},{16,0},{32,16},{48,32},{1,49},{17,1},{33,17},{49,33},{2,50}... | collective-permute-start | bytes 786440 | tf_op jit(solution)/shard_map/ppermute | solution.py:19
  28.9 20.4 %collective-permute-start.3 = (bf16[2,128,1024]{2,1,0:T(8,128)(2,1)}, bf16[2,128,1024]{2,1,0:T(8,128)(2,1)S(1)}, u32[]{:S(2)}, u32[]{:S(2)}) collective-permute-start(bf16[2,128,1024]{2,1,0:T(8,128)(2,1)} %copy-done.13), channel_id=1, source_target_pairs={{0,2},{2,0},{1,3},{3,1},{4,6},{6,4},{5,7},{7,5},{8,10},{10,8},{9,1... | collective-permute-start | bytes 1572872 | tf_op jit(solution)/shard_map/ppermute | solution.py:27
  47.9 3.2 %collective-permute-start.9 = (bf16[2,128,1024]{2,1,0:T(8,128)(2,1)}, bf16[2,128,1024]{2,1,0:T(8,128)(2,1)S(1)}, u32[]{:S(2)}, u32[]{:S(2)}) collective-permute-start(bf16[2,128,1024]{2,1,0:T(8,128)(2,1)} %slice.11), channel_id=1, source_target_pairs={{0,2},{2,0},{1,3},{3,1},{4,6},{6,4},{5,7},{7,5},{8,10},{10,8},{9,1... | collective-permute-start | bytes 1572872 | tf_op jit(solution)/shard_map/ppermute | solution.py:27
  49.3 4.1 %copy-start.2 = (bf16[256,1024]{1,0:T(8,128)(2,1)S(1)}, bf16[256,1024]{1,0:T(8,128)(2,1)}, u32[]{:S(2)}) copy-start(bf16[256,1024]{1,0:T(8,128)(2,1)} %copy-done.1) | copy-start | bytes 1572868
  49.3 4.1 %copy-start.4 = (bf16[256,1024]{1,0:T(8,128)(2,1)S(1)}, bf16[256,1024]{1,0:T(8,128)(2,1)}, u32[]{:S(2)}) copy-start(bf16[256,1024]{1,0:T(8,128)(2,1)} %copy-done.3) | copy-start | bytes 1572868
  52.0 1.4 %copy-start.10 = (bf16[128,1024]{1,0:T(8,128)(2,1)S(1)}, bf16[128,1024]{1,0:T(8,128)(2,1)}, u32[]{:S(2)}) copy-start(bf16[128,1024]{1,0:T(8,128)(2,1)} %copy-done.9) | copy-start | bytes 786436
  52.0 1.4 %copy-start.12 = (bf16[128,1024]{1,0:T(8,128)(2,1)S(1)}, bf16[128,1024]{1,0:T(8,128)(2,1)}, u32[]{:S(2)}) copy-start(bf16[128,1024]{1,0:T(8,128)(2,1)} %copy-done.11) | copy-start | bytes 786436
  52.9 2.0 %copy-start.8 = (f32[128,1024]{1,0:T(8,128)S(1)}, f32[128,1024]{1,0:T(8,128)}, u32[]{:S(2)}) copy-start(f32[128,1024]{1,0:T(8,128)} %copy-done.7) | copy-start | bytes 1572868
  52.9 2.0 %collective-permute-start.10 = (bf16[512,512]{1,0:T(8,128)(2,1)S(1)}, bf16[512,512]{1,0:T(8,128)(2,1)S(1)}, u32[]{:S(2)}, u32[]{:S(2)}) collective-permute-start(bf16[512,512]{1,0:T(8,128)(2,1)S(1)} %get-tuple-element.29.own_ref), channel_id=1, source_target_pairs={{0,2},{2,0},{1,3},{3,1},{4,6},{6,4},{5,7},{7,5},{8,10},{10,8},{9,1... | collective-permute-start | bytes 1572872 | tf_op jit(solution)/shard_map/ppermute | solution.py:27
  56.2 2.0 %collective-permute-start.11 = (bf16[512,512]{1,0:T(8,128)(2,1)S(1)}, bf16[512,512]{1,0:T(8,128)(2,1)S(1)}, u32[]{:S(2)}, u32[]{:S(2)}) collective-permute-start(bf16[512,512]{1,0:T(8,128)(2,1)S(1)} %get-tuple-element.36), channel_id=1, source_target_pairs={{0,2},{2,0},{1,3},{3,1},{4,6},{6,4},{5,7},{7,5},{8,10},{10,8},{9,1... | collective-permute-start | bytes 1572872 | tf_op jit(solution)/shard_map/ppermute | solution.py:27
  (5 other events, 4.0 us)

commit v25 on v24

--- a/solution.py
+++ b/solution.py
@@ -88,20 +88,22 @@
     )(screened, left)
 
 
-def project(trial_half, left, near, far, passed):
+def joined(box, slot, psi_ref, column, points):
+    for g in range(psi_ref.shape[0] // points):
+        psi_ref[g * points : (g + 1) * points, column * points : (column + 1) * points] = box[
+            slot, :, g * points : (g + 1) * points
+        ]
+
+
+def project(trial_half, left, near, far):
     states, points = left.shape
     cols = trial_half.shape[1]
 
-    def kernel(trial_ref, left_ref, *refs):
-        boxes, (out_ref, psi_ref, sem) = refs[:3], refs[3:]
+    def kernel(trial_ref, left_ref, near_ref, far_ref, out_ref, psi_ref, sem):
         load = pltpu.make_async_copy(left_ref, psi_ref.at[:, :points], sem)
         load.start()
-        for k in range(1, 4):
-            box = boxes[k - 1]
-            for g in range(states // points):
-                psi_ref[g * points : (g + 1) * points, k * points : (k + 1) * points] = box[
-                    box.shape[0] - 1, :, g * points : (g + 1) * points
-                ]
+        joined(near_ref, 1, psi_ref, 1, points)
+        joined(far_ref, 2, psi_ref, 2, points)
         load.wait()
         out_ref[...] = lax.dot_general(
             psi_ref[...], trial_ref[...], (((0,), (0,)), ((), ())), preferred_element_type=F32
@@ -110,15 +112,40 @@
     return pl.pallas_call(
         kernel,
         out_shape=[
-            jax.ShapeDtypeStruct((4 * points, cols), BF16),
-            jax.ShapeDtypeStruct((states, 4 * points), BF16),
-        ],
-        in_specs=[vmem_spec(), pl.BlockSpec(memory_space=pl.ANY)] + [vmem_spec()] * 3,
+            jax.ShapeDtypeStruct((3 * points, cols), BF16),
+            jax.ShapeDtypeStruct((states, 3 * points), BF16),
+        ],
+        in_specs=[vmem_spec(), pl.BlockSpec(memory_space=pl.ANY)] + [vmem_spec()] * 2,
         out_specs=[vmem_spec()] * 2,
         scratch_shapes=[pltpu.SemaphoreType.DMA],
         compiler_params=params(12),
         name="project",
-    )(trial_half, left, near, far, passed)
+    )(trial_half, left, near, far)
+
+
+def project_last(trial_half, passed, three):
+    states = trial_half.shape[0]
+    cols = trial_half.shape[1]
+    points = three.shape[0] // 3
+
+    def kernel(trial_ref, passed_ref, three_ref, out_ref, psi_ref):
+        joined(passed_ref, 1, psi_ref, 0, points)
+        out_ref[: 3 * points, :] = three_ref[...]
+        out_ref[3 * points :, :] = lax.dot_general(
+            psi_ref[...], trial_ref[...], (((0,), (0,)), ((), ())), preferred_element_type=F32
+        ).astype(BF16)
+
+    return pl.pallas_call(
+        kernel,
+        out_shape=[
+            jax.ShapeDtypeStruct((4 * points, cols), BF16),
+            jax.ShapeDtypeStruct((states, points), BF16),
+        ],
+        in_specs=[vmem_spec()] * 3,
+        out_specs=[vmem_spec()] * 2,
+        compiler_params=params(12),
+        name="project_last",
+    )(trial_half, passed, three)
 
 
 NT = (((1,), (1,)), ((), ()))
@@ -212,12 +239,12 @@
     )(weighted, panel)
 
 
-def finish(psi, keep, got):
-    states, count = psi.shape
-    points = count // 4
+def finish(psi, psi_last, keep, got):
+    states, points = psi_last.shape
+    count = 4 * points
     cols = keep.shape[1]
 
-    def kernel(psi_ref, keep_ref, got_ref, out_ref, high, low):
+    def kernel(psi_ref, last_ref, keep_ref, got_ref, out_ref, high, low):
         for k in range(4):
             here = slice(k * points, (k + 1) * points)
             there = slice(SIBLING[k] * points, (SIBLING[k] + 1) * points)
@@ -225,19 +252,22 @@
             top = back.astype(BF16)
             high[here, :] = top
             low[here, :] = (back - top.astype(F32)).astype(BF16)
-        total = jnp.dot(psi_ref[...], high[...], preferred_element_type=F32)
-        total += jnp.dot(psi_ref[...], low[...], preferred_element_type=F32)
+        total = None
+        for piece in (high, low):
+            for ref, here in ((psi_ref, slice(0, 3 * points)), (last_ref, slice(3 * points, count))):
+                part = jnp.dot(ref[...], piece[here, :], preferred_element_type=F32)
+                total = part if total is None else total + part
         out_ref[...] = total.astype(BF16)
 
     return pl.pallas_call(
         kernel,
         out_shape=jax.ShapeDtypeStruct((states, cols), BF16),
-        in_specs=[vmem_spec()] * 3,
+        in_specs=[vmem_spec()] * 4,
         out_specs=vmem_spec(),
         scratch_shapes=[pltpu.VMEM((count, cols), BF16)] * 2,
         compiler_params=params(16),
         name="finish",
-    )(psi, keep, got)
+    )(psi, psi_last, keep, got)
 
 
 def shards(trial, psi_v, psi_c, screened):
@@ -258,14 +288,15 @@
     beyond = [shift(behind[:middle], "y", 1), shift(ahead[middle:], "y", -1)]
     far, beyond = lax.optimization_barrier((far, beyond))
     passed = swap(far[1:])
-    proj_own, psi = project(trial_half, psi_v, near, far, passed)
+    three, psi = project(trial_half, psi_v, near, far)
+    proj_own, psi_last = project_last(trial_half, passed, three)
     proj_other = swap(proj_own)
     panel = [line, behind, ahead, *beyond]
     ordered, pairs = own_pairs(proj_own, panel)
     weighted, send = direct(proj_other, ordered, pairs, own, [near, far, passed])
     got = swap(send)
     keep = own_half(weighted, ordered)
-    term = finish(psi, keep, got)
+    term = finish(psi, psi_last, keep, got)
     parts = exchange(term.reshape(devices, rows, half), TILE_VEC)
     parts = parts.reshape(-1, 2, 2, rows, half).astype(F32)
     total = jnp.sum(parts, axis=(0, 2))

time: 86.1 us -> 85 us (0.987)
  waiting for transfers between devices: 11.4 us -> 9.66 us
    ppermute x4, waiting for transfers between devices: 3.18 us -> 1.47 us  [swap(): return lax.ppermute(value, 'core', [(0, 1), (1, 0)])]
  transfers between devices with their start and end apart: 13 -> 13, of which waited for: 5 -> 4; matrix products, arithmetic and copies ran while one was open for 1% -> 1% of each run, Pallas kernels for 4% -> 5%
where the time goes in v25:
time: 85 us; the launch traced here: 84.8 us
  starting transfers between devices  32.4 us (38%)
  blocking collectives  25.5 us (30%)
  waiting for transfers between devices  9.66 us (11%)
  local copies, waits for them, and re-layouts  8.53 us (10%)
  Pallas kernels  7.74 us (9%)
    all_to_all x1, blocking collectives, exchange(): return lax.all_to_all(value, axes, split_axis=0, concat_axis=0, tiled=True)  25.5 us
    ppermute x7, starting transfers between devices, shift(): return lax.ppermute(value, axis, [(k, (k + by) % n) for k in range(n)])  11 us
    ppermute x4, starting transfers between devices, swap(): return lax.ppermute(value, 'core', [(0, 1), (1, 0)])  11 us
    ppermute x7, waiting for transfers between devices, shift(): return lax.ppermute(value, axis, [(k, (k + by) % n) for k in range(n)])  8.18 us
    all_to_all x1, starting transfers between devices, exchange(): return lax.all_to_all(value, axes, split_axis=0, concat_axis=0, tiled=True)  6.75 us
    unnamed x32, local copies, waits for them, and re-layouts  6.55 us
    ppermute x1, starting transfers between devices, shards(): far = lax.ppermute(far, 'zh', [(0, 1), (1, 0)])  3.6 us
    pallas_call x1, Pallas kernels, pack(): pl.pallas_call(kernel, grid=(steps,), out_shape=[jax.ShapeDtypeStruct((po...  1.97 us
  transfers between devices with their start and end apart: 13, of which 4 were waited for; matrix products, arithmetic and copies ran while one was open for 1% of the time, Pallas kernels for 5%

profile of v25, /device:TPU:1, one launch (start us, length us, event | category | flops | bytes accessed | tf_op | source)
XLA Modules:
  0.0 84.8 jit_solution(11913378848559568676)
XLA Ops:
  0.0 2.0 %collective-permute-start = (bf16[64,1024]{1,0:T(8,128)(2,1)}, bf16[64,1024]{1,0:T(8,128)(2,1)S(1)}, u32[]{:S(2)}, u32[]{:S(2)}) collective-permute-start(bf16[64,1024]{1,0:T(8,128)(2,1)} %bitcast.19), channel_id=1, source_target_pairs={{0,4},{4,8},{8,12},{12,0},{1,5},{5,9},{9,13},{13,1},{2,6},{6,10},{... | collective-permute-start | bytes 393224 | tf_op jit(solution)/shard_map/ppermute | solution.py:19
  2.0 1.3 %collective-permute-start.1 = (bf16[64,1024]{1,0:T(8,128)(2,1)}, bf16[64,1024]{1,0:T(8,128)(2,1)S(1)}, u32[]{:S(2)}, u32[]{:S(2)}) collective-permute-start(bf16[64,1024]{1,0:T(8,128)(2,1)} %bitcast.20), channel_id=1, source_target_pairs={{0,12},{4,0},{8,4},{12,8},{1,13},{5,1},{9,5},{13,9},{2,14},{6,2},{... | collective-permute-start | bytes 393224 | tf_op jit(solution)/shard_map/ppermute | solution.py:19
  3.3 1.7 %collective-permute-start.2 = (bf16[64,1024]{1,0:T(8,128)(2,1)}, bf16[64,1024]{1,0:T(8,128)(2,1)S(1)}, u32[]{:S(2)}, u32[]{:S(2)}) collective-permute-start(bf16[64,1024]{1,0:T(8,128)(2,1)} %bitcast.21), channel_id=1, source_target_pairs={{0,8},{4,12},{8,0},{12,4},{1,9},{5,13},{9,1},{13,5},{2,10},{6,14},... | collective-permute-start | bytes 393224 | tf_op jit(solution)/shard_map/ppermute | solution.py:19
  5.0 1.6 %copy-done = f32[128,4096]{1,0:T(8,128)S(1)} copy-done((f32[128,4096]{1,0:T(8,128)S(1)}, f32[128,4096]{1,0:T(8,128)}, u32[]{:S(2)}) %copy-start) | copy-done | bytes 2097176
  6.6 0.9 %copy-done.5 = bf16[1024,128]{1,0:T(8,128)(2,1)S(1)} copy-done((bf16[1024,128]{1,0:T(8,128)(2,1)S(1)}, bf16[1024,128]{1,0:T(8,128)(2,1)}, u32[]{:S(2)}) %copy-start.5) | copy-done | bytes 262168
  7.6 2.0 %pack.1 = (f32[128,1024]{1,0:T(8,128)S(1)}, bf16[2,128,1024]{2,1,0:T(8,128)(2,1)S(1)}, bf16[3,128,1024]{2,1,0:T(8,128)(2,1)}) custom-call(f32[128,4096]{1,0:T(8,128)S(1)} %copy-done, bf16[1024,128]{1,0:T(8,128)(2,1)S(1)} %copy-done.5), custom_call_target="tpu_custom_call" | custom-call | tf_op jit(solution)/shard_map/pack/pallas_call | solution.py:69
  9.6 0.8 copy-done.7
  11.3 1.1 %broadcast_in_dim.2 = bf16[32,2,2,8,512]{4,3,2,1,0:T(8,128)(2,1)} broadcast(bf16[2,8,512]{2,1,0:T(8,128)(2,1)S(1)} %bitcast.23), dimensions={1,3,4} | broadcast | bytes 1064960 | tf_op jit(solution)/shard_map/broadcast_in_dim | solution.py:281
  12.4 1.3 %collective-permute-start.5 = (bf16[256,1024]{1,0:T(8,128)(2,1)S(1)}, bf16[256,1024]{1,0:T(8,128)(2,1)S(1)}, u32[]{:S(2)}, u32[]{:S(2)}) collective-permute-start(bf16[256,1024]{1,0:T(8,128)(2,1)S(1)} %pad_maximum_fusion.refs_0_), channel_id=1, source_target_pairs={{0,16},{16,32},{32,48},{48,0},{1,17},{17,33},{33,49},{49,1},{2,18}... | collective-permute-start | bytes 1572872 | tf_op jit(solution)/shard_map/ppermute | solution.py:19
  13.7 1.4 %collective-permute-start.7 = (bf16[256,1024]{1,0:T(8,128)(2,1)S(1)}, bf16[256,1024]{1,0:T(8,128)(2,1)S(1)}, u32[]{:S(2)}, u32[]{:S(2)}) collective-permute-start(bf16[256,1024]{1,0:T(8,128)(2,1)S(1)} %pad_maximum_fusion.refs_0_), channel_id=1, source_target_pairs={{0,48},{16,0},{32,16},{48,32},{1,49},{17,1},{33,17},{49,33},{2,50}... | collective-permute-start | bytes 1572872 | tf_op jit(solution)/shard_map/ppermute | solution.py:19
  15.1 3.6 %collective-permute-start.4 = (bf16[3,128,1024]{2,1,0:T(8,128)(2,1)}, bf16[3,128,1024]{2,1,0:T(8,128)(2,1)S(1)}, u32[]{:S(2)}, u32[]{:S(2)}) collective-permute-start(bf16[3,128,1024]{2,1,0:T(8,128)(2,1)} %get-tuple-element.27), channel_id=1, source_target_pairs={{0,64},{64,0},{1,65},{65,1},{2,66},{66,2},{3,67},{67,3},{4,68},{68... | collective-permute-start | bytes 2359304 | tf_op jit(solution)/shard_map/ppermute | solution.py:285
  18.7 6.8 %all-to-all-start = ((bf16[128,8,512]{2,1,0:T(8,128)(2,1)}), bf16[128,8,512]{2,1,0:T(8,128)(2,1)S(1)}, u32[]{:S(2)}, u32[]{:S(2)}) async-start(bf16[128,8,512]{2,1,0:T(8,128)(2,1)} %bitcast.17), calls=%async_computation | async-start | bytes 2097152 | tf_op jit(solution)/shard_map/all_to_all | solution.py:23
  25.6 1.3 %collective-permute-start.6 = (bf16[128,1024]{1,0:T(8,128)(2,1)S(1)}, bf16[128,1024]{1,0:T(8,128)(2,1)S(1)}, u32[]{:S(2)}, u32[]{:S(2)}) collective-permute-start(bf16[128,1024]{1,0:T(8,128)(2,1)S(1)} %slice.12), channel_id=1, source_target_pairs={{0,16},{16,32},{32,48},{48,0},{1,17},{17,33},{33,49},{49,1},{2,18}... | collective-permute-start | bytes 786440 | tf_op jit(solution)/shard_map/ppermute | solution.py:19
  27.0 1.9 %collective-permute-start.8 = (bf16[128,1024]{1,0:T(8,128)(2,1)S(1)}, bf16[128,1024]{1,0:T(8,128)(2,1)S(1)}, u32[]{:S(2)}, u32[]{:S(2)}) collective-permute-start(bf16[128,1024]{1,0:T(8,128)(2,1)S(1)} %slice.13), channel_id=1, source_target_pairs={{0,48},{16,0},{32,16},{48,32},{1,49},{17,1},{33,17},{49,33},{2,50}... | collective-permute-start | bytes 786440 | tf_op jit(solution)/shard_map/ppermute | solution.py:19
  28.9 8.7 %collective-permute-start.3 = (bf16[2,128,1024]{2,1,0:T(8,128)(2,1)}, bf16[2,128,1024]{2,1,0:T(8,128)(2,1)S(1)}, u32[]{:S(2)}, u32[]{:S(2)}) collective-permute-start(bf16[2,128,1024]{2,1,0:T(8,128)(2,1)} %copy-done.13), channel_id=1, source_target_pairs={{0,2},{2,0},{1,3},{3,1},{4,6},{6,4},{5,7},{7,5},{8,10},{10,8},{9,1... | collective-permute-start | bytes 1572872 | tf_op jit(solution)/shard_map/ppermute | solution.py:27
  37.6 8.0 %collective-permute-done.6.refs_3_ = bf16[128,1024]{1,0:T(8,128)(2,1)S(1)} collective-permute-done((bf16[128,1024]{1,0:T(8,128)(2,1)S(1)}, bf16[128,1024]{1,0:T(8,128)(2,1)S(1)}, u32[]{:S(2)}, u32[]{:S(2)}) %collective-permute-start.6) | collective-permute-done | bytes 262176 | tf_op jit(solution)/shard_map/ppermute | solution.py:19
  47.0 0.8 slice.11
  47.9 1.4 %collective-permute-start.9 = (bf16[2,128,1024]{2,1,0:T(8,128)(2,1)}, bf16[2,128,1024]{2,1,0:T(8,128)(2,1)S(1)}, u32[]{:S(2)}, u32[]{:S(2)}) collective-permute-start(bf16[2,128,1024]{2,1,0:T(8,128)(2,1)} %slice.11), channel_id=1, source_target_pairs={{0,2},{2,0},{1,3},{3,1},{4,6},{6,4},{5,7},{7,5},{8,10},{10,8},{9,1... | collective-permute-start | bytes 1572872 | tf_op jit(solution)/shard_map/ppermute | solution.py:27
  49.3 0.9 %copy-done.6 = bf16[1024,128]{1,0:T(8,128)(2,1)S(1)} copy-done((bf16[1024,128]{1,0:T(8,128)(2,1)S(1)}, bf16[1024,128]{1,0:T(8,128)(2,1)}, u32[]{:S(2)}) %copy-start.6) | copy-done | bytes 262168
  51.9 0.9 %own_pairs.1 = (bf16[1024,1024]{1,0:T(8,128)(2,1)S(1)}, f32[512,1024]{1,0:T(8,128)S(1)}) custom-call(bf16[512,512]{1,0:T(8,128)(2,1)S(1)} %get-tuple-element.33.own_ref, bf16[256,1024]{1,0:T(8,128)(2,1)S(1)} %pad_maximum_fusion.refs_0_, bf16[256,1024]{1,0:T(8,128)(2,1)S(1)} %copy-done.2, bf16[256,1024]{1,0:T(8,128)(2,1)S(1)} %copy-done.4, ...), custom_call_target="tpu_custom_call" | custom-call | tf_op jit(solution)/shard_map/own_pairs/pallas_call | solution.py:171
  53.4 1.3 %direct.1 = (bf16[512,1024]{1,0:T(8,128)(2,1)S(1)}, bf16[512,512]{1,0:T(8,128)(2,1)S(1)}) custom-call(bf16[512,512]{1,0:T(8,128)(2,1)S(1)} %collective-permute-done.10.other_ref, bf16[1024,1024]{1,0:T(8,128)(2,1)S(1)} %get-tuple-element.36.panel_ref, f32[512,1024]{1,0:T(8,128)S(1)} %get-tuple-element.37.pair_ref, f32[128,1024]{1,0:T(8,128)S(1)} %copy-done.8, ...), custom_call_target="tpu_custom_call" | custom-call | tf_op jit(solution)/shard_map/direct/pallas_call | solution.py:210
  55.9 0.8 collective-permute-done.11.got_ref
  56.7 1.8 %finish.1 = bf16[1024,512]{1,0:T(8,128)(2,1)S(1)} custom-call(bf16[1024,384]{1,0:T(8,128)(2,1)S(1)} %get-tuple-element.30.psi_ref, bf16[1024,128]{1,0:T(8,128)(2,1)S(1)} %get-tuple-element.32.last_ref, f32[512,512]{1,0:T(8,128)S(1)} %own_half.1.keep_ref, bf16[512,512]{1,0:T(8,128)(2,1)S(1)} %collective-permute-done.11.got_ref), custom_call_target="tpu_custom_call" | custom-call | tf_op jit(solution)/shard_map/finish/pallas_call | solution.py:262
  58.5 25.5 %all_to_all.10 = bf16[128,8,512]{2,1,0:T(8,128)(2,1)S(1)} all-to-all(bf16[128,8,512]{2,1,0:T(8,128)(2,1)S(1)} %bitcast.16), channel_id=1, replica_groups=mesh['zh'=2,'y'=4,'x'=4,'core'=2,'zl'=2] {'zh','y','x','core','zl'}, dimensions={0} | all-to-all | bytes 2097152 | tf_op jit(solution)/shard_map/all_to_all | solution.py:23
  (48 shorter events, 6.7 us)
Async XLA Ops:
  0.0 11.2 %collective-permute-start = (bf16[64,1024]{1,0:T(8,128)(2,1)}, bf16[64,1024]{1,0:T(8,128)(2,1)S(1)}, u32[]{:S(2)}, u32[]{:S(2)}) collective-permute-start(bf16[64,1024]{1,0:T(8,128)(2,1)} %bitcast.19), channel_id=1, source_target_pairs={{0,4},{4,8},{8,12},{12,0},{1,5},{5,9},{9,13},{13,1},{2,6},{6,10},{... | collective-permute-start | bytes 393224 | tf_op jit(solution)/shard_map/ppermute | solution.py:19
  2.0 9.1 %collective-permute-start.1 = (bf16[64,1024]{1,0:T(8,128)(2,1)}, bf16[64,1024]{1,0:T(8,128)(2,1)S(1)}, u32[]{:S(2)}, u32[]{:S(2)}) collective-permute-start(bf16[64,1024]{1,0:T(8,128)(2,1)} %bitcast.20), channel_id=1, source_target_pairs={{0,12},{4,0},{8,4},{12,8},{1,13},{5,1},{9,5},{13,9},{2,14},{6,2},{... | collective-permute-start | bytes 393224 | tf_op jit(solution)/shard_map/ppermute | solution.py:19
  3.3 7.9 %collective-permute-start.2 = (bf16[64,1024]{1,0:T(8,128)(2,1)}, bf16[64,1024]{1,0:T(8,128)(2,1)S(1)}, u32[]{:S(2)}, u32[]{:S(2)}) collective-permute-start(bf16[64,1024]{1,0:T(8,128)(2,1)} %bitcast.21), channel_id=1, source_target_pairs={{0,8},{4,12},{8,0},{12,4},{1,9},{5,13},{9,1},{13,5},{2,10},{6,14},... | collective-permute-start | bytes 393224 | tf_op jit(solution)/shard_map/ppermute | solution.py:19
  5.0 1.6 %copy-start = (f32[128,4096]{1,0:T(8,128)S(1)}, f32[128,4096]{1,0:T(8,128)}, u32[]{:S(2)}) copy-start(f32[128,4096]{1,0:T(8,128)} %in_ref.1) | copy-start | bytes 6291460
  7.6 3.6 %copy-start.14 = (bf16[1024,1,64]{0,2,1:T(8,128)(2,1)S(1)}, bf16[1024,1,64]{0,2,1:T(8,128)(2,1)}, u32[]{:S(2)}) copy-start(bf16[1024,1,64]{0,2,1:T(8,128)(2,1)} %param.6) | copy-start | bytes 393220
  7.6 3.7 %copy-start.15 = (bf16[1,8,1024]{2,1,0:T(8,128)(2,1)S(1)}, bf16[1,8,1024]{2,1,0:T(8,128)(2,1)}, u32[]{:S(2)}) copy-start(bf16[1,8,1024]{2,1,0:T(8,128)(2,1)} %param.4) | copy-start | bytes 49156
  12.4 13.2 %collective-permute-start.5 = (bf16[256,1024]{1,0:T(8,128)(2,1)S(1)}, bf16[256,1024]{1,0:T(8,128)(2,1)S(1)}, u32[]{:S(2)}, u32[]{:S(2)}) collective-permute-start(bf16[256,1024]{1,0:T(8,128)(2,1)S(1)} %pad_maximum_fusion.refs_0_), channel_id=1, source_target_pairs={{0,16},{16,32},{32,48},{48,0},{1,17},{17,33},{33,49},{49,1},{2,18}... | collective-permute-start | bytes 1572872 | tf_op jit(solution)/shard_map/ppermute | solution.py:19
  13.7 13.3 %collective-permute-start.7 = (bf16[256,1024]{1,0:T(8,128)(2,1)S(1)}, bf16[256,1024]{1,0:T(8,128)(2,1)S(1)}, u32[]{:S(2)}, u32[]{:S(2)}) collective-permute-start(bf16[256,1024]{1,0:T(8,128)(2,1)S(1)} %pad_maximum_fusion.refs_0_), channel_id=1, source_target_pairs={{0,48},{16,0},{32,16},{48,32},{1,49},{17,1},{33,17},{49,33},{2,50}... | collective-permute-start | bytes 1572872 | tf_op jit(solution)/shard_map/ppermute | solution.py:19
  15.1 31.9 %collective-permute-start.4 = (bf16[3,128,1024]{2,1,0:T(8,128)(2,1)}, bf16[3,128,1024]{2,1,0:T(8,128)(2,1)S(1)}, u32[]{:S(2)}, u32[]{:S(2)}) collective-permute-start(bf16[3,128,1024]{2,1,0:T(8,128)(2,1)} %get-tuple-element.27), channel_id=1, source_target_pairs={{0,64},{64,0},{1,65},{65,1},{2,66},{66,2},{3,67},{67,3},{4,68},{68... | collective-permute-start | bytes 2359304 | tf_op jit(solution)/shard_map/ppermute | solution.py:285
  18.7 30.6 %all-to-all-start = ((bf16[128,8,512]{2,1,0:T(8,128)(2,1)}), bf16[128,8,512]{2,1,0:T(8,128)(2,1)S(1)}, u32[]{:S(2)}, u32[]{:S(2)}) async-start(bf16[128,8,512]{2,1,0:T(8,128)(2,1)} %bitcast.17), calls=%async_computation | async-start | bytes 2097152 | tf_op jit(solution)/shard_map/all_to_all | solution.py:23
  25.6 1.4 %copy-start.1 = (bf16[256,1024]{1,0:T(8,128)(2,1)}, bf16[256,1024]{1,0:T(8,128)(2,1)S(1)}, u32[]{:S(2)}) copy-start(bf16[256,1024]{1,0:T(8,128)(2,1)S(1)} %collective-permute-done.5.refs_1_) | copy-start | bytes 1572868
  25.6 20.0 %collective-permute-start.6 = (bf16[128,1024]{1,0:T(8,128)(2,1)S(1)}, bf16[128,1024]{1,0:T(8,128)(2,1)S(1)}, u32[]{:S(2)}, u32[]{:S(2)}) collective-permute-start(bf16[128,1024]{1,0:T(8,128)(2,1)S(1)} %slice.12), channel_id=1, source_target_pairs={{0,16},{16,32},{32,48},{48,0},{1,17},{17,33},{33,49},{49,1},{2,18}... | collective-permute-start | bytes 786440 | tf_op jit(solution)/shard_map/ppermute | solution.py:19
  27.0 20.1 %copy-start.3 = (bf16[256,1024]{1,0:T(8,128)(2,1)}, bf16[256,1024]{1,0:T(8,128)(2,1)S(1)}, u32[]{:S(2)}) copy-start(bf16[256,1024]{1,0:T(8,128)(2,1)S(1)} %collective-permute-done.7.refs_2_) | copy-start | bytes 1572868
  27.0 19.3 %collective-permute-start.8 = (bf16[128,1024]{1,0:T(8,128)(2,1)S(1)}, bf16[128,1024]{1,0:T(8,128)(2,1)S(1)}, u32[]{:S(2)}, u32[]{:S(2)}) collective-permute-start(bf16[128,1024]{1,0:T(8,128)(2,1)S(1)} %slice.13), channel_id=1, source_target_pairs={{0,48},{16,0},{32,16},{48,32},{1,49},{17,1},{33,17},{49,33},{2,50}... | collective-permute-start | bytes 786440 | tf_op jit(solution)/shard_map/ppermute | solution.py:19
  28.9 20.4 %collective-permute-start.3 = (bf16[2,128,1024]{2,1,0:T(8,128)(2,1)}, bf16[2,128,1024]{2,1,0:T(8,128)(2,1)S(1)}, u32[]{:S(2)}, u32[]{:S(2)}) collective-permute-start(bf16[2,128,1024]{2,1,0:T(8,128)(2,1)} %copy-done.13), channel_id=1, source_target_pairs={{0,2},{2,0},{1,3},{3,1},{4,6},{6,4},{5,7},{7,5},{8,10},{10,8},{9,1... | collective-permute-start | bytes 1572872 | tf_op jit(solution)/shard_map/ppermute | solution.py:27
  47.9 3.2 %collective-permute-start.9 = (bf16[2,128,1024]{2,1,0:T(8,128)(2,1)}, bf16[2,128,1024]{2,1,0:T(8,128)(2,1)S(1)}, u32[]{:S(2)}, u32[]{:S(2)}) collective-permute-start(bf16[2,128,1024]{2,1,0:T(8,128)(2,1)} %slice.11), channel_id=1, source_target_pairs={{0,2},{2,0},{1,3},{3,1},{4,6},{6,4},{5,7},{7,5},{8,10},{10,8},{9,1... | collective-permute-start | bytes 1572872 | tf_op jit(solution)/shard_map/ppermute | solution.py:27
  49.3 1.0 %copy-start.6 = (bf16[1024,128]{1,0:T(8,128)(2,1)S(1)}, bf16[1024,128]{1,0:T(8,128)(2,1)}, u32[]{:S(2)}) copy-start(bf16[1024,128]{1,0:T(8,128)(2,1)} %left_ref.3) | copy-start | bytes 786436
  50.2 1.6 %copy-start.2 = (bf16[256,1024]{1,0:T(8,128)(2,1)S(1)}, bf16[256,1024]{1,0:T(8,128)(2,1)}, u32[]{:S(2)}) copy-start(bf16[256,1024]{1,0:T(8,128)(2,1)} %copy-done.1) | copy-start | bytes 1572868
  50.2 1.6 %copy-start.4 = (bf16[256,1024]{1,0:T(8,128)(2,1)S(1)}, bf16[256,1024]{1,0:T(8,128)(2,1)}, u32[]{:S(2)}) copy-start(bf16[256,1024]{1,0:T(8,128)(2,1)} %copy-done.3) | copy-start | bytes 1572868
  50.2 1.6 %copy-start.10 = (bf16[128,1024]{1,0:T(8,128)(2,1)S(1)}, bf16[128,1024]{1,0:T(8,128)(2,1)}, u32[]{:S(2)}) copy-start(bf16[128,1024]{1,0:T(8,128)(2,1)} %copy-done.9) | copy-start | bytes 786436
  50.3 1.6 %copy-start.12 = (bf16[128,1024]{1,0:T(8,128)(2,1)S(1)}, bf16[128,1024]{1,0:T(8,128)(2,1)}, u32[]{:S(2)}) copy-start(bf16[128,1024]{1,0:T(8,128)(2,1)} %copy-done.11) | copy-start | bytes 786436
  51.0 2.4 %copy-start.8 = (f32[128,1024]{1,0:T(8,128)S(1)}, f32[128,1024]{1,0:T(8,128)}, u32[]{:S(2)}) copy-start(f32[128,1024]{1,0:T(8,128)} %copy-done.7) | copy-start | bytes 1572868
  51.4 2.0 %collective-permute-start.10 = (bf16[512,512]{1,0:T(8,128)(2,1)S(1)}, bf16[512,512]{1,0:T(8,128)(2,1)S(1)}, u32[]{:S(2)}, u32[]{:S(2)}) collective-permute-start(bf16[512,512]{1,0:T(8,128)(2,1)S(1)} %get-tuple-element.33.own_ref), channel_id=1, source_target_pairs={{0,2},{2,0},{1,3},{3,1},{4,6},{6,4},{5,7},{7,5},{8,10},{10,8},{9,1... | collective-permute-start | bytes 1572872 | tf_op jit(solution)/shard_map/ppermute | solution.py:27
  54.7 2.0 %collective-permute-start.11 = (bf16[512,512]{1,0:T(8,128)(2,1)S(1)}, bf16[512,512]{1,0:T(8,128)(2,1)S(1)}, u32[]{:S(2)}, u32[]{:S(2)}) collective-permute-start(bf16[512,512]{1,0:T(8,128)(2,1)S(1)} %get-tuple-element.40), channel_id=1, source_target_pairs={{0,2},{2,0},{1,3},{3,1},{4,6},{6,4},{5,7},{7,5},{8,10},{10,8},{9,1... | collective-permute-start | bytes 1572872 | tf_op jit(solution)/shard_map/ppermute | solution.py:27
  (5 other events, 4.0 us)

commit v26 on v25

--- a/solution.py
+++ b/solution.py
@@ -221,30 +221,36 @@
     )(proj_other, panel, pairs, own, *boxes)
 
 
-def own_half(weighted, panel):
+def own_half(weighted, panel, psi, psi_last):
     rows, count = weighted.shape
     half = panel.shape[1] // 2
-
-    def kernel(weighted_ref, panel_ref, keep_ref):
+    states, three = psi.shape
+
+    def kernel(weighted_ref, panel_ref, psi_ref, last_ref, keep_ref, all_ref):
         mine = pl.ds(pl.multiple_of(lax.axis_index("core") * half, half), half)
         keep_ref[...] = jnp.dot(weighted_ref[...], panel_ref[:, mine], preferred_element_type=F32)
-
-    return pl.pallas_call(
-        kernel,
-        out_shape=jax.ShapeDtypeStruct((rows, half), F32),
-        in_specs=[vmem_spec()] * 2,
-        out_specs=vmem_spec(),
+        all_ref[:, :three] = psi_ref[...]
+        all_ref[:, three:] = last_ref[...]
+
+    return pl.pallas_call(
+        kernel,
+        out_shape=[
+            jax.ShapeDtypeStruct((rows, half), F32),
+            jax.ShapeDtypeStruct((states, three + psi_last.shape[1]), BF16),
+        ],
+        in_specs=[vmem_spec()] * 4,
+        out_specs=[vmem_spec()] * 2,
         compiler_params=params(16),
         name="own_half",
-    )(weighted, panel)
-
-
-def finish(psi, psi_last, keep, got):
-    states, points = psi_last.shape
-    count = 4 * points
+    )(weighted, panel, psi, psi_last)
+
+
+def finish(psi, keep, got):
+    states, count = psi.shape
+    points = count // 4
     cols = keep.shape[1]
 
-    def kernel(psi_ref, last_ref, keep_ref, got_ref, out_ref, high, low):
+    def kernel(psi_ref, keep_ref, got_ref, out_ref, high, low):
         for k in range(4):
             here = slice(k * points, (k + 1) * points)
             there = slice(SIBLING[k] * points, (SIBLING[k] + 1) * points)
@@ -252,22 +258,19 @@
             top = back.astype(BF16)
             high[here, :] = top
             low[here, :] = (back - top.astype(F32)).astype(BF16)
-        total = None
-        for piece in (high, low):
-            for ref, here in ((psi_ref, slice(0, 3 * points)), (last_ref, slice(3 * points, count))):
-                part = jnp.dot(ref[...], piece[here, :], preferred_element_type=F32)
-                total = part if total is None else total + part
+        total = jnp.dot(psi_ref[...], high[...], preferred_element_type=F32)
+        total += jnp.dot(psi_ref[...], low[...], preferred_element_type=F32)
         out_ref[...] = total.astype(BF16)
 
     return pl.pallas_call(
         kernel,
         out_shape=jax.ShapeDtypeStruct((states, cols), BF16),
-        in_specs=[vmem_spec()] * 4,
+        in_specs=[vmem_spec()] * 3,
         out_specs=vmem_spec(),
         scratch_shapes=[pltpu.VMEM((count, cols), BF16)] * 2,
         compiler_params=params(16),
         name="finish",
-    )(psi, psi_last, keep, got)
+    )(psi, keep, got)
 
 
 def shards(trial, psi_v, psi_c, screened):
@@ -295,8 +298,8 @@
     ordered, pairs = own_pairs(proj_own, panel)
     weighted, send = direct(proj_other, ordered, pairs, own, [near, far, passed])
     got = swap(send)
-    keep = own_half(weighted, ordered)
-    term = finish(psi, psi_last, keep, got)
+    keep, psi = own_half(weighted, ordered, psi, psi_last)
+    term = finish(psi, keep, got)
     parts = exchange(term.reshape(devices, rows, half), TILE_VEC)
     parts = parts.reshape(-1, 2, 2, rows, half).astype(F32)
     total = jnp.sum(parts, axis=(0, 2))

time: 85 us -> 84.5 us (level)
  no operation moved by 1% of the time
where the time goes in v26:
time: 84.5 us; the launch traced here: 84.2 us
  starting transfers between devices  32.4 us (38%)
  blocking collectives  25.5 us (30%)
  waiting for transfers between devices  9.6 us (11%)
  local copies, waits for them, and re-layouts  8.51 us (10%)
  Pallas kernels  7.27 us (9%)
    all_to_all x1, blocking collectives, exchange(): return lax.all_to_all(value, axes, split_axis=0, concat_axis=0, tiled=True)  25.5 us
    ppermute x7, starting transfers between devices, shift(): return lax.ppermute(value, axis, [(k, (k + by) % n) for k in range(n)])  11 us
    ppermute x4, starting transfers between devices, swap(): return lax.ppermute(value, 'core', [(0, 1), (1, 0)])  11 us
    ppermute x7, waiting for transfers between devices, shift(): return lax.ppermute(value, axis, [(k, (k + by) % n) for k in range(n)])  8.18 us
    all_to_all x1, starting transfers between devices, exchange(): return lax.all_to_all(value, axes, split_axis=0, concat_axis=0, tiled=True)  6.75 us
    unnamed x32, local copies, waits for them, and re-layouts  6.54 us
    ppermute x1, starting transfers between devices, shards(): far = lax.ppermute(far, 'zh', [(0, 1), (1, 0)])  3.6 us
    pallas_call x1, Pallas kernels, pack(): pl.pallas_call(kernel, grid=(steps,), out_shape=[jax.ShapeDtypeStruct((po...  1.92 us
  transfers between devices with their start and end apart: 13, of which 4 were waited for; matrix products, arithmetic and copies ran while one was open for 1% of the time, Pallas kernels for 5%

profile of v26, /device:TPU:1, one launch (start us, length us, event | category | flops | bytes accessed | tf_op | source)
XLA Modules:
  0.0 84.2 jit_solution(5474600983882137832)
XLA Ops:
  0.0 2.0 %collective-permute-start = (bf16[64,1024]{1,0:T(8,128)(2,1)}, bf16[64,1024]{1,0:T(8,128)(2,1)S(1)}, u32[]{:S(2)}, u32[]{:S(2)}) collective-permute-start(bf16[64,1024]{1,0:T(8,128)(2,1)} %bitcast.19), channel_id=1, source_target_pairs={{0,4},{4,8},{8,12},{12,0},{1,5},{5,9},{9,13},{13,1},{2,6},{6,10},{... | collective-permute-start | bytes 393224 | tf_op jit(solution)/shard_map/ppermute | solution.py:19
  2.0 1.3 %collective-permute-start.1 = (bf16[64,1024]{1,0:T(8,128)(2,1)}, bf16[64,1024]{1,0:T(8,128)(2,1)S(1)}, u32[]{:S(2)}, u32[]{:S(2)}) collective-permute-start(bf16[64,1024]{1,0:T(8,128)(2,1)} %bitcast.20), channel_id=1, source_target_pairs={{0,12},{4,0},{8,4},{12,8},{1,13},{5,1},{9,5},{13,9},{2,14},{6,2},{... | collective-permute-start | bytes 393224 | tf_op jit(solution)/shard_map/ppermute | solution.py:19
  3.3 1.7 %collective-permute-start.2 = (bf16[64,1024]{1,0:T(8,128)(2,1)}, bf16[64,1024]{1,0:T(8,128)(2,1)S(1)}, u32[]{:S(2)}, u32[]{:S(2)}) collective-permute-start(bf16[64,1024]{1,0:T(8,128)(2,1)} %bitcast.21), channel_id=1, source_target_pairs={{0,8},{4,12},{8,0},{12,4},{1,9},{5,13},{9,1},{13,5},{2,10},{6,14},... | collective-permute-start | bytes 393224 | tf_op jit(solution)/shard_map/ppermute | solution.py:19
  5.0 1.6 %copy-done = f32[128,4096]{1,0:T(8,128)S(1)} copy-done((f32[128,4096]{1,0:T(8,128)S(1)}, f32[128,4096]{1,0:T(8,128)}, u32[]{:S(2)}) %copy-start) | copy-done | bytes 2097176
  6.6 0.9 %copy-done.5 = bf16[1024,128]{1,0:T(8,128)(2,1)S(1)} copy-done((bf16[1024,128]{1,0:T(8,128)(2,1)S(1)}, bf16[1024,128]{1,0:T(8,128)(2,1)}, u32[]{:S(2)}) %copy-start.5) | copy-done | bytes 262168
  7.6 1.9 %pack.1 = (f32[128,1024]{1,0:T(8,128)S(1)}, bf16[2,128,1024]{2,1,0:T(8,128)(2,1)S(1)}, bf16[3,128,1024]{2,1,0:T(8,128)(2,1)}) custom-call(f32[128,4096]{1,0:T(8,128)S(1)} %copy-done, bf16[1024,128]{1,0:T(8,128)(2,1)S(1)} %copy-done.5), custom_call_target="tpu_custom_call" | custom-call | tf_op jit(solution)/shard_map/pack/pallas_call | solution.py:69
  9.5 0.8 copy-done.7
  10.3 0.8 copy-done.13
  11.2 1.1 %broadcast_in_dim.2 = bf16[32,2,2,8,512]{4,3,2,1,0:T(8,128)(2,1)} broadcast(bf16[2,8,512]{2,1,0:T(8,128)(2,1)S(1)} %bitcast.23), dimensions={1,3,4} | broadcast | bytes 1064960 | tf_op jit(solution)/shard_map/broadcast_in_dim | solution.py:284
  12.3 1.3 %collective-permute-start.4 = (bf16[256,1024]{1,0:T(8,128)(2,1)S(1)}, bf16[256,1024]{1,0:T(8,128)(2,1)S(1)}, u32[]{:S(2)}, u32[]{:S(2)}) collective-permute-start(bf16[256,1024]{1,0:T(8,128)(2,1)S(1)} %pad_maximum_fusion.refs_0_), channel_id=1, source_target_pairs={{0,16},{16,32},{32,48},{48,0},{1,17},{17,33},{33,49},{49,1},{2,18}... | collective-permute-start | bytes 1572872 | tf_op jit(solution)/shard_map/ppermute | solution.py:19
  13.6 1.4 %collective-permute-start.6 = (bf16[256,1024]{1,0:T(8,128)(2,1)S(1)}, bf16[256,1024]{1,0:T(8,128)(2,1)S(1)}, u32[]{:S(2)}, u32[]{:S(2)}) collective-permute-start(bf16[256,1024]{1,0:T(8,128)(2,1)S(1)} %pad_maximum_fusion.refs_0_), channel_id=1, source_target_pairs={{0,48},{16,0},{32,16},{48,32},{1,49},{17,1},{33,17},{49,33},{2,50}... | collective-permute-start | bytes 1572872 | tf_op jit(solution)/shard_map/ppermute | solution.py:19
  15.0 3.6 %collective-permute-start.3 = (bf16[3,128,1024]{2,1,0:T(8,128)(2,1)}, bf16[3,128,1024]{2,1,0:T(8,128)(2,1)S(1)}, u32[]{:S(2)}, u32[]{:S(2)}) collective-permute-start(bf16[3,128,1024]{2,1,0:T(8,128)(2,1)} %get-tuple-element.28), channel_id=1, source_target_pairs={{0,64},{64,0},{1,65},{65,1},{2,66},{66,2},{3,67},{67,3},{4,68},{68... | collective-permute-start | bytes 2359304 | tf_op jit(solution)/shard_map/ppermute | solution.py:288
  18.6 6.8 %all-to-all-start = ((bf16[128,8,512]{2,1,0:T(8,128)(2,1)}), bf16[128,8,512]{2,1,0:T(8,128)(2,1)S(1)}, u32[]{:S(2)}, u32[]{:S(2)}) async-start(bf16[128,8,512]{2,1,0:T(8,128)(2,1)} %bitcast.17), calls=%async_computation | async-start | bytes 2097152 | tf_op jit(solution)/shard_map/all_to_all | solution.py:23
  25.6 1.3 %collective-permute-start.5 = (bf16[128,1024]{1,0:T(8,128)(2,1)S(1)}, bf16[128,1024]{1,0:T(8,128)(2,1)S(1)}, u32[]{:S(2)}, u32[]{:S(2)}) collective-permute-start(bf16[128,1024]{1,0:T(8,128)(2,1)S(1)} %slice.12), channel_id=1, source_target_pairs={{0,16},{16,32},{32,48},{48,0},{1,17},{17,33},{33,49},{49,1},{2,18}... | collective-permute-start | bytes 786440 | tf_op jit(solution)/shard_map/ppermute | solution.py:19
  26.9 1.9 %collective-permute-start.7 = (bf16[128,1024]{1,0:T(8,128)(2,1)S(1)}, bf16[128,1024]{1,0:T(8,128)(2,1)S(1)}, u32[]{:S(2)}, u32[]{:S(2)}) collective-permute-start(bf16[128,1024]{1,0:T(8,128)(2,1)S(1)} %slice.13), channel_id=1, source_target_pairs={{0,48},{16,0},{32,16},{48,32},{1,49},{17,1},{33,17},{49,33},{2,50}... | collective-permute-start | bytes 786440 | tf_op jit(solution)/shard_map/ppermute | solution.py:19
  28.9 8.7 %collective-permute-start.9 = (bf16[2,128,1024]{2,1,0:T(8,128)(2,1)}, bf16[2,128,1024]{2,1,0:T(8,128)(2,1)S(1)}, u32[]{:S(2)}, u32[]{:S(2)}) collective-permute-start(bf16[2,128,1024]{2,1,0:T(8,128)(2,1)} %copy-done.13), channel_id=1, source_target_pairs={{0,2},{2,0},{1,3},{3,1},{4,6},{6,4},{5,7},{7,5},{8,10},{10,8},{9,1... | collective-permute-start | bytes 1572872 | tf_op jit(solution)/shard_map/ppermute | solution.py:27
  37.5 8.0 %collective-permute-done.5.refs_3_ = bf16[128,1024]{1,0:T(8,128)(2,1)S(1)} collective-permute-done((bf16[128,1024]{1,0:T(8,128)(2,1)S(1)}, bf16[128,1024]{1,0:T(8,128)(2,1)S(1)}, u32[]{:S(2)}, u32[]{:S(2)}) %collective-permute-start.5) | collective-permute-done | bytes 262176 | tf_op jit(solution)/shard_map/ppermute | solution.py:19
  47.0 0.8 slice.11
  47.8 1.4 %collective-permute-start.8 = (bf16[2,128,1024]{2,1,0:T(8,128)(2,1)}, bf16[2,128,1024]{2,1,0:T(8,128)(2,1)S(1)}, u32[]{:S(2)}, u32[]{:S(2)}) collective-permute-start(bf16[2,128,1024]{2,1,0:T(8,128)(2,1)} %slice.11), channel_id=1, source_target_pairs={{0,2},{2,0},{1,3},{3,1},{4,6},{6,4},{5,7},{7,5},{8,10},{10,8},{9,1... | collective-permute-start | bytes 1572872 | tf_op jit(solution)/shard_map/ppermute | solution.py:27
  49.2 0.9 %copy-done.6 = bf16[1024,128]{1,0:T(8,128)(2,1)S(1)} copy-done((bf16[1024,128]{1,0:T(8,128)(2,1)S(1)}, bf16[1024,128]{1,0:T(8,128)(2,1)}, u32[]{:S(2)}) %copy-start.6) | copy-done | bytes 262168
  51.8 0.9 %own_pairs.1 = (bf16[1024,1024]{1,0:T(8,128)(2,1)S(1)}, f32[512,1024]{1,0:T(8,128)S(1)}) custom-call(bf16[512,512]{1,0:T(8,128)(2,1)S(1)} %get-tuple-element.33.own_ref, bf16[256,1024]{1,0:T(8,128)(2,1)S(1)} %pad_maximum_fusion.refs_0_, bf16[256,1024]{1,0:T(8,128)(2,1)S(1)} %copy-done.2, bf16[256,1024]{1,0:T(8,128)(2,1)S(1)} %copy-done.4, ...), custom_call_target="tpu_custom_call" | custom-call | tf_op jit(solution)/shard_map/own_pairs/pallas_call | solution.py:171
  53.3 1.3 %direct.1 = (bf16[512,1024]{1,0:T(8,128)(2,1)S(1)}, bf16[512,512]{1,0:T(8,128)(2,1)S(1)}) custom-call(bf16[512,512]{1,0:T(8,128)(2,1)S(1)} %collective-permute-done.10.other_ref, bf16[1024,1024]{1,0:T(8,128)(2,1)S(1)} %get-tuple-element.36.panel_ref, f32[512,1024]{1,0:T(8,128)S(1)} %get-tuple-element.37.pair_ref, f32[128,1024]{1,0:T(8,128)S(1)} %copy-done.8, ...), custom_call_target="tpu_custom_call" | custom-call | tf_op jit(solution)/shard_map/direct/pallas_call | solution.py:210
  56.6 1.3 %finish.1 = bf16[1024,512]{1,0:T(8,128)(2,1)S(1)} custom-call(bf16[1024,512]{1,0:T(8,128)(2,1)S(1)} %get-tuple-element.42.psi_ref, f32[512,512]{1,0:T(8,128)S(1)} %get-tuple-element.43.keep_ref, bf16[512,512]{1,0:T(8,128)(2,1)S(1)} %collective-permute-done.11.got_ref), custom_call_target="tpu_custom_call" | custom-call | tf_op jit(solution)/shard_map/finish/pallas_call | solution.py:265
  57.9 25.5 %all_to_all.10 = bf16[128,8,512]{2,1,0:T(8,128)(2,1)S(1)} all-to-all(bf16[128,8,512]{2,1,0:T(8,128)(2,1)S(1)} %bitcast.16), channel_id=1, replica_groups=mesh['zh'=2,'y'=4,'x'=4,'core'=2,'zl'=2] {'zh','y','x','core','zl'}, dimensions={0} | all-to-all | bytes 2097152 | tf_op jit(solution)/shard_map/all_to_all | solution.py:23
  (48 shorter events, 6.7 us)
Async XLA Ops:
  0.0 11.1 %collective-permute-start = (bf16[64,1024]{1,0:T(8,128)(2,1)}, bf16[64,1024]{1,0:T(8,128)(2,1)S(1)}, u32[]{:S(2)}, u32[]{:S(2)}) collective-permute-start(bf16[64,1024]{1,0:T(8,128)(2,1)} %bitcast.19), channel_id=1, source_target_pairs={{0,4},{4,8},{8,12},{12,0},{1,5},{5,9},{9,13},{13,1},{2,6},{6,10},{... | collective-permute-start | bytes 393224 | tf_op jit(solution)/shard_map/ppermute | solution.py:19
  2.0 9.1 %collective-permute-start.1 = (bf16[64,1024]{1,0:T(8,128)(2,1)}, bf16[64,1024]{1,0:T(8,128)(2,1)S(1)}, u32[]{:S(2)}, u32[]{:S(2)}) collective-permute-start(bf16[64,1024]{1,0:T(8,128)(2,1)} %bitcast.20), channel_id=1, source_target_pairs={{0,12},{4,0},{8,4},{12,8},{1,13},{5,1},{9,5},{13,9},{2,14},{6,2},{... | collective-permute-start | bytes 393224 | tf_op jit(solution)/shard_map/ppermute | solution.py:19
  3.3 7.8 %collective-permute-start.2 = (bf16[64,1024]{1,0:T(8,128)(2,1)}, bf16[64,1024]{1,0:T(8,128)(2,1)S(1)}, u32[]{:S(2)}, u32[]{:S(2)}) collective-permute-start(bf16[64,1024]{1,0:T(8,128)(2,1)} %bitcast.21), channel_id=1, source_target_pairs={{0,8},{4,12},{8,0},{12,4},{1,9},{5,13},{9,1},{13,5},{2,10},{6,14},... | collective-permute-start | bytes 393224 | tf_op jit(solution)/shard_map/ppermute | solution.py:19
  5.0 1.6 %copy-start = (f32[128,4096]{1,0:T(8,128)S(1)}, f32[128,4096]{1,0:T(8,128)}, u32[]{:S(2)}) copy-start(f32[128,4096]{1,0:T(8,128)} %in_ref.1) | copy-start | bytes 6291460
  7.6 3.6 %copy-start.14 = (bf16[1024,1,64]{0,2,1:T(8,128)(2,1)S(1)}, bf16[1024,1,64]{0,2,1:T(8,128)(2,1)}, u32[]{:S(2)}) copy-start(bf16[1024,1,64]{0,2,1:T(8,128)(2,1)} %param.6) | copy-start | bytes 393220
  7.6 3.6 %copy-start.15 = (bf16[1,8,1024]{2,1,0:T(8,128)(2,1)S(1)}, bf16[1,8,1024]{2,1,0:T(8,128)(2,1)}, u32[]{:S(2)}) copy-start(bf16[1,8,1024]{2,1,0:T(8,128)(2,1)} %param.4) | copy-start | bytes 49156
  12.3 13.2 %collective-permute-start.4 = (bf16[256,1024]{1,0:T(8,128)(2,1)S(1)}, bf16[256,1024]{1,0:T(8,128)(2,1)S(1)}, u32[]{:S(2)}, u32[]{:S(2)}) collective-permute-start(bf16[256,1024]{1,0:T(8,128)(2,1)S(1)} %pad_maximum_fusion.refs_0_), channel_id=1, source_target_pairs={{0,16},{16,32},{32,48},{48,0},{1,17},{17,33},{33,49},{49,1},{2,18}... | collective-permute-start | bytes 1572872 | tf_op jit(solution)/shard_map/ppermute | solution.py:19
  13.6 13.3 %collective-permute-start.6 = (bf16[256,1024]{1,0:T(8,128)(2,1)S(1)}, bf16[256,1024]{1,0:T(8,128)(2,1)S(1)}, u32[]{:S(2)}, u32[]{:S(2)}) collective-permute-start(bf16[256,1024]{1,0:T(8,128)(2,1)S(1)} %pad_maximum_fusion.refs_0_), channel_id=1, source_target_pairs={{0,48},{16,0},{32,16},{48,32},{1,49},{17,1},{33,17},{49,33},{2,50}... | collective-permute-start | bytes 1572872 | tf_op jit(solution)/shard_map/ppermute | solution.py:19
  15.0 31.9 %collective-permute-start.3 = (bf16[3,128,1024]{2,1,0:T(8,128)(2,1)}, bf16[3,128,1024]{2,1,0:T(8,128)(2,1)S(1)}, u32[]{:S(2)}, u32[]{:S(2)}) collective-permute-start(bf16[3,128,1024]{2,1,0:T(8,128)(2,1)} %get-tuple-element.28), channel_id=1, source_target_pairs={{0,64},{64,0},{1,65},{65,1},{2,66},{66,2},{3,67},{67,3},{4,68},{68... | collective-permute-start | bytes 2359304 | tf_op jit(solution)/shard_map/ppermute | solution.py:288
  18.6 30.6 %all-to-all-start = ((bf16[128,8,512]{2,1,0:T(8,128)(2,1)}), bf16[128,8,512]{2,1,0:T(8,128)(2,1)S(1)}, u32[]{:S(2)}, u32[]{:S(2)}) async-start(bf16[128,8,512]{2,1,0:T(8,128)(2,1)} %bitcast.17), calls=%async_computation | async-start | bytes 2097152 | tf_op jit(solution)/shard_map/all_to_all | solution.py:23
  25.5 1.4 %copy-start.1 = (bf16[256,1024]{1,0:T(8,128)(2,1)}, bf16[256,1024]{1,0:T(8,128)(2,1)S(1)}, u32[]{:S(2)}) copy-start(bf16[256,1024]{1,0:T(8,128)(2,1)S(1)} %collective-permute-done.4.refs_1_) | copy-start | bytes 1572868
  25.6 20.0 %collective-permute-start.5 = (bf16[128,1024]{1,0:T(8,128)(2,1)S(1)}, bf16[128,1024]{1,0:T(8,128)(2,1)S(1)}, u32[]{:S(2)}, u32[]{:S(2)}) collective-permute-start(bf16[128,1024]{1,0:T(8,128)(2,1)S(1)} %slice.12), channel_id=1, source_target_pairs={{0,16},{16,32},{32,48},{48,0},{1,17},{17,33},{33,49},{49,1},{2,18}... | collective-permute-start | bytes 786440 | tf_op jit(solution)/shard_map/ppermute | solution.py:19
  26.9 20.1 %copy-start.3 = (bf16[256,1024]{1,0:T(8,128)(2,1)}, bf16[256,1024]{1,0:T(8,128)(2,1)S(1)}, u32[]{:S(2)}) copy-start(bf16[256,1024]{1,0:T(8,128)(2,1)S(1)} %collective-permute-done.6.refs_2_) | copy-start | bytes 1572868
  26.9 19.3 %collective-permute-start.7 = (bf16[128,1024]{1,0:T(8,128)(2,1)S(1)}, bf16[128,1024]{1,0:T(8,128)(2,1)S(1)}, u32[]{:S(2)}, u32[]{:S(2)}) collective-permute-start(bf16[128,1024]{1,0:T(8,128)(2,1)S(1)} %slice.13), channel_id=1, source_target_pairs={{0,48},{16,0},{32,16},{48,32},{1,49},{17,1},{33,17},{49,33},{2,50}... | collective-permute-start | bytes 786440 | tf_op jit(solution)/shard_map/ppermute | solution.py:19
  28.9 20.4 %collective-permute-start.9 = (bf16[2,128,1024]{2,1,0:T(8,128)(2,1)}, bf16[2,128,1024]{2,1,0:T(8,128)(2,1)S(1)}, u32[]{:S(2)}, u32[]{:S(2)}) collective-permute-start(bf16[2,128,1024]{2,1,0:T(8,128)(2,1)} %copy-done.13), channel_id=1, source_target_pairs={{0,2},{2,0},{1,3},{3,1},{4,6},{6,4},{5,7},{7,5},{8,10},{10,8},{9,1... | collective-permute-start | bytes 1572872 | tf_op jit(solution)/shard_map/ppermute | solution.py:27
  47.8 3.2 %collective-permute-start.8 = (bf16[2,128,1024]{2,1,0:T(8,128)(2,1)}, bf16[2,128,1024]{2,1,0:T(8,128)(2,1)S(1)}, u32[]{:S(2)}, u32[]{:S(2)}) collective-permute-start(bf16[2,128,1024]{2,1,0:T(8,128)(2,1)} %slice.11), channel_id=1, source_target_pairs={{0,2},{2,0},{1,3},{3,1},{4,6},{6,4},{5,7},{7,5},{8,10},{10,8},{9,1... | collective-permute-start | bytes 1572872 | tf_op jit(solution)/shard_map/ppermute | solution.py:27
  49.2 1.0 %copy-start.6 = (bf16[1024,128]{1,0:T(8,128)(2,1)S(1)}, bf16[1024,128]{1,0:T(8,128)(2,1)}, u32[]{:S(2)}) copy-start(bf16[1024,128]{1,0:T(8,128)(2,1)} %left_ref.3) | copy-start | bytes 786436
  50.2 1.6 %copy-start.2 = (bf16[256,1024]{1,0:T(8,128)(2,1)S(1)}, bf16[256,1024]{1,0:T(8,128)(2,1)}, u32[]{:S(2)}) copy-start(bf16[256,1024]{1,0:T(8,128)(2,1)} %copy-done.1) | copy-start | bytes 1572868
  50.2 1.6 %copy-start.4 = (bf16[256,1024]{1,0:T(8,128)(2,1)S(1)}, bf16[256,1024]{1,0:T(8,128)(2,1)}, u32[]{:S(2)}) copy-start(bf16[256,1024]{1,0:T(8,128)(2,1)} %copy-done.3) | copy-start | bytes 1572868
  50.2 1.6 %copy-start.10 = (bf16[128,1024]{1,0:T(8,128)(2,1)S(1)}, bf16[128,1024]{1,0:T(8,128)(2,1)}, u32[]{:S(2)}) copy-start(bf16[128,1024]{1,0:T(8,128)(2,1)} %copy-done.9) | copy-start | bytes 786436
  50.2 1.6 %copy-start.12 = (bf16[128,1024]{1,0:T(8,128)(2,1)S(1)}, bf16[128,1024]{1,0:T(8,128)(2,1)}, u32[]{:S(2)}) copy-start(bf16[128,1024]{1,0:T(8,128)(2,1)} %copy-done.11) | copy-start | bytes 786436
  51.0 2.4 %copy-start.8 = (f32[128,1024]{1,0:T(8,128)S(1)}, f32[128,1024]{1,0:T(8,128)}, u32[]{:S(2)}) copy-start(f32[128,1024]{1,0:T(8,128)} %copy-done.7) | copy-start | bytes 1572868
  51.3 2.0 %collective-permute-start.10 = (bf16[512,512]{1,0:T(8,128)(2,1)S(1)}, bf16[512,512]{1,0:T(8,128)(2,1)S(1)}, u32[]{:S(2)}, u32[]{:S(2)}) collective-permute-start(bf16[512,512]{1,0:T(8,128)(2,1)S(1)} %get-tuple-element.33.own_ref), channel_id=1, source_target_pairs={{0,2},{2,0},{1,3},{3,1},{4,6},{6,4},{5,7},{7,5},{8,10},{10,8},{9,1... | collective-permute-start | bytes 1572872 | tf_op jit(solution)/shard_map/ppermute | solution.py:27
  54.6 2.0 %collective-permute-start.11 = (bf16[512,512]{1,0:T(8,128)(2,1)S(1)}, bf16[512,512]{1,0:T(8,128)(2,1)S(1)}, u32[]{:S(2)}, u32[]{:S(2)}) collective-permute-start(bf16[512,512]{1,0:T(8,128)(2,1)S(1)} %get-tuple-element.44), channel_id=1, source_target_pairs={{0,2},{2,0},{1,3},{3,1},{4,6},{6,4},{5,7},{7,5},{8,10},{10,8},{9,1... | collective-permute-start | bytes 1572872 | tf_op jit(solution)/shard_map/ppermute | solution.py:27
  (5 other events, 4.0 us)

commit v27 on v26

--- a/solution.py
+++ b/solution.py
@@ -289,8 +289,8 @@
     behind, ahead = shift(line, "y", 1), shift(line, "y", -1)
     middle = line.shape[0] // 2
     beyond = [shift(behind[:middle], "y", 1), shift(ahead[middle:], "y", -1)]
-    far, beyond = lax.optimization_barrier((far, beyond))
-    passed = swap(far[1:])
+    tail, far, beyond = lax.optimization_barrier((far[1:], far, beyond))
+    passed = swap(tail)
     three, psi = project(trial_half, psi_v, near, far)
     proj_own, psi_last = project_last(trial_half, passed, three)
     proj_other = swap(proj_own)

time: 84.5 us -> 86.2 us (1.020)
  starting transfers between devices: 32.4 us -> 40.5 us
  waiting for transfers between devices: 9.6 us -> 3.51 us
    ppermute x7, waiting for transfers between devices: 8.18 us -> 2.1 us  [shift(): return lax.ppermute(value, axis, [(k, (k + by) % n) for k in range(n)])]
    ppermute x4, starting transfers between devices: 11 us -> 15.4 us  [swap(): return lax.ppermute(value, 'core', [(0, 1), (1, 0)])]
    ppermute x7, starting transfers between devices: 11 us -> 14.8 us  [shift(): return lax.ppermute(value, axis, [(k, (k + by) % n) for k in range(n)])]
where the time goes in v27:
time: 86.2 us; the launch traced here: 85.9 us
  starting transfers between devices  40.5 us (47%)
  blocking collectives  25.1 us (29%)
  local copies, waits for them, and re-layouts  8.54 us (10%)
  Pallas kernels  7.27 us (8%)
  waiting for transfers between devices  3.51 us (4%)
    all_to_all x1, blocking collectives, exchange(): return lax.all_to_all(value, axes, split_axis=0, concat_axis=0, tiled=True)  25.1 us
    ppermute x4, starting transfers between devices, swap(): return lax.ppermute(value, 'core', [(0, 1), (1, 0)])  15.4 us
    ppermute x7, starting transfers between devices, shift(): return lax.ppermute(value, axis, [(k, (k + by) % n) for k in range(n)])  14.8 us
    all_to_all x1, starting transfers between devices, exchange(): return lax.all_to_all(value, axes, split_axis=0, concat_axis=0, tiled=True)  6.75 us
    unnamed x32, local copies, waits for them, and re-layouts  6.58 us
    ppermute x1, starting transfers between devices, shards(): far = lax.ppermute(far, 'zh', [(0, 1), (1, 0)])  3.6 us
    ppermute x7, waiting for transfers between devices, shift(): return lax.ppermute(value, axis, [(k, (k + by) % n) for k in range(n)])  2.1 us
    pallas_call x1, Pallas kernels, pack(): pl.pallas_call(kernel, grid=(steps,), out_shape=[jax.ShapeDtypeStruct((po...  1.92 us
  transfers between devices with their start and end apart: 13, of which 4 were waited for; matrix products, arithmetic and copies ran while one was open for 1% of the time, Pallas kernels for 5%

profile of v27, /device:TPU:1, one launch (start us, length us, event | category | flops | bytes accessed | tf_op | source)
XLA Modules:
  0.0 85.9 jit_solution(12699800409960783708)
XLA Ops:
  0.0 2.0 %collective-permute-start = (bf16[64,1024]{1,0:T(8,128)(2,1)}, bf16[64,1024]{1,0:T(8,128)(2,1)S(1)}, u32[]{:S(2)}, u32[]{:S(2)}) collective-permute-start(bf16[64,1024]{1,0:T(8,128)(2,1)} %bitcast.19), channel_id=1, source_target_pairs={{0,4},{4,8},{8,12},{12,0},{1,5},{5,9},{9,13},{13,1},{2,6},{6,10},{... | collective-permute-start | bytes 393224 | tf_op jit(solution)/shard_map/ppermute | solution.py:19
  2.0 1.3 %collective-permute-start.1 = (bf16[64,1024]{1,0:T(8,128)(2,1)}, bf16[64,1024]{1,0:T(8,128)(2,1)S(1)}, u32[]{:S(2)}, u32[]{:S(2)}) collective-permute-start(bf16[64,1024]{1,0:T(8,128)(2,1)} %bitcast.20), channel_id=1, source_target_pairs={{0,12},{4,0},{8,4},{12,8},{1,13},{5,1},{9,5},{13,9},{2,14},{6,2},{... | collective-permute-start | bytes 393224 | tf_op jit(solution)/shard_map/ppermute | solution.py:19
  3.3 1.7 %collective-permute-start.2 = (bf16[64,1024]{1,0:T(8,128)(2,1)}, bf16[64,1024]{1,0:T(8,128)(2,1)S(1)}, u32[]{:S(2)}, u32[]{:S(2)}) collective-permute-start(bf16[64,1024]{1,0:T(8,128)(2,1)} %bitcast.21), channel_id=1, source_target_pairs={{0,8},{4,12},{8,0},{12,4},{1,9},{5,13},{9,1},{13,5},{2,10},{6,14},... | collective-permute-start | bytes 393224 | tf_op jit(solution)/shard_map/ppermute | solution.py:19
  5.0 1.6 %copy-done = f32[128,4096]{1,0:T(8,128)S(1)} copy-done((f32[128,4096]{1,0:T(8,128)S(1)}, f32[128,4096]{1,0:T(8,128)}, u32[]{:S(2)}) %copy-start) | copy-done | bytes 2097176
  6.6 0.9 %copy-done.5 = bf16[1024,128]{1,0:T(8,128)(2,1)S(1)} copy-done((bf16[1024,128]{1,0:T(8,128)(2,1)S(1)}, bf16[1024,128]{1,0:T(8,128)(2,1)}, u32[]{:S(2)}) %copy-start.5) | copy-done | bytes 262168
  7.6 1.9 %pack.1 = (f32[128,1024]{1,0:T(8,128)S(1)}, bf16[2,128,1024]{2,1,0:T(8,128)(2,1)S(1)}, bf16[3,128,1024]{2,1,0:T(8,128)(2,1)}) custom-call(f32[128,4096]{1,0:T(8,128)S(1)} %copy-done, bf16[1024,128]{1,0:T(8,128)(2,1)S(1)} %copy-done.5), custom_call_target="tpu_custom_call" | custom-call | tf_op jit(solution)/shard_map/pack/pallas_call | solution.py:69
  9.5 0.8 copy-done.7
  10.3 0.8 copy-done.13
  11.2 1.1 %broadcast_in_dim.2 = bf16[32,2,2,8,512]{4,3,2,1,0:T(8,128)(2,1)} broadcast(bf16[2,8,512]{2,1,0:T(8,128)(2,1)S(1)} %bitcast.23), dimensions={1,3,4} | broadcast | bytes 1064960 | tf_op jit(solution)/shard_map/broadcast_in_dim | solution.py:284
  12.3 1.3 %collective-permute-start.4 = (bf16[256,1024]{1,0:T(8,128)(2,1)S(1)}, bf16[256,1024]{1,0:T(8,128)(2,1)S(1)}, u32[]{:S(2)}, u32[]{:S(2)}) collective-permute-start(bf16[256,1024]{1,0:T(8,128)(2,1)S(1)} %pad_maximum_fusion.refs_0_), channel_id=1, source_target_pairs={{0,16},{16,32},{32,48},{48,0},{1,17},{17,33},{33,49},{49,1},{2,18}... | collective-permute-start | bytes 1572872 | tf_op jit(solution)/shard_map/ppermute | solution.py:19
  13.6 3.6 %collective-permute-start.3 = (bf16[3,128,1024]{2,1,0:T(8,128)(2,1)}, bf16[3,128,1024]{2,1,0:T(8,128)(2,1)S(1)}, u32[]{:S(2)}, u32[]{:S(2)}) collective-permute-start(bf16[3,128,1024]{2,1,0:T(8,128)(2,1)} %get-tuple-element.29), channel_id=1, source_target_pairs={{0,64},{64,0},{1,65},{65,1},{2,66},{66,2},{3,67},{67,3},{4,68},{68... | collective-permute-start | bytes 2359304 | tf_op jit(solution)/shard_map/ppermute | solution.py:288
  17.2 1.4 %collective-permute-start.6 = (bf16[256,1024]{1,0:T(8,128)(2,1)S(1)}, bf16[256,1024]{1,0:T(8,128)(2,1)S(1)}, u32[]{:S(2)}, u32[]{:S(2)}) collective-permute-start(bf16[256,1024]{1,0:T(8,128)(2,1)S(1)} %pad_maximum_fusion.refs_0_), channel_id=1, source_target_pairs={{0,48},{16,0},{32,16},{48,32},{1,49},{17,1},{33,17},{49,33},{2,50}... | collective-permute-start | bytes 1572872 | tf_op jit(solution)/shard_map/ppermute | solution.py:19
  18.6 6.8 %all-to-all-start = ((bf16[128,8,512]{2,1,0:T(8,128)(2,1)}), bf16[128,8,512]{2,1,0:T(8,128)(2,1)S(1)}, u32[]{:S(2)}, u32[]{:S(2)}) async-start(bf16[128,8,512]{2,1,0:T(8,128)(2,1)} %bitcast.17), calls=%async_computation | async-start | bytes 2097152 | tf_op jit(solution)/shard_map/all_to_all | solution.py:23
  25.6 1.3 %collective-permute-start.5 = (bf16[128,1024]{1,0:T(8,128)(2,1)S(1)}, bf16[128,1024]{1,0:T(8,128)(2,1)S(1)}, u32[]{:S(2)}, u32[]{:S(2)}) collective-permute-start(bf16[128,1024]{1,0:T(8,128)(2,1)S(1)} %slice.13), channel_id=1, source_target_pairs={{0,16},{16,32},{32,48},{48,0},{1,17},{17,33},{33,49},{49,1},{2,18}... | collective-permute-start | bytes 786440 | tf_op jit(solution)/shard_map/ppermute | solution.py:19
  26.9 1.9 %collective-permute-done.6.refs_2_ = bf16[256,1024]{1,0:T(8,128)(2,1)S(1)} collective-permute-done((bf16[256,1024]{1,0:T(8,128)(2,1)S(1)}, bf16[256,1024]{1,0:T(8,128)(2,1)S(1)}, u32[]{:S(2)}, u32[]{:S(2)}) %collective-permute-start.6) | collective-permute-done | bytes 524320 | tf_op jit(solution)/shard_map/ppermute | solution.py:19
  28.9 5.6 %collective-permute-start.7 = (bf16[128,1024]{1,0:T(8,128)(2,1)S(1)}, bf16[128,1024]{1,0:T(8,128)(2,1)S(1)}, u32[]{:S(2)}, u32[]{:S(2)}) collective-permute-start(bf16[128,1024]{1,0:T(8,128)(2,1)S(1)} %slice.14), channel_id=1, source_target_pairs={{0,48},{16,0},{32,16},{48,32},{1,49},{17,1},{33,17},{49,33},{2,50}... | collective-permute-start | bytes 786440 | tf_op jit(solution)/shard_map/ppermute | solution.py:19
  34.5 12.2 %collective-permute-start.9 = (bf16[2,128,1024]{2,1,0:T(8,128)(2,1)}, bf16[2,128,1024]{2,1,0:T(8,128)(2,1)S(1)}, u32[]{:S(2)}, u32[]{:S(2)}) collective-permute-start(bf16[2,128,1024]{2,1,0:T(8,128)(2,1)} %copy-done.13), channel_id=1, source_target_pairs={{0,2},{2,0},{1,3},{3,1},{4,6},{6,4},{5,7},{7,5},{8,10},{10,8},{9,1... | collective-permute-start | bytes 1572872 | tf_op jit(solution)/shard_map/ppermute | solution.py:27
  46.7 0.8 slice.12
  49.0 2.3 %collective-permute-start.8 = (bf16[2,128,1024]{2,1,0:T(8,128)(2,1)}, bf16[2,128,1024]{2,1,0:T(8,128)(2,1)S(1)}, u32[]{:S(2)}, u32[]{:S(2)}) collective-permute-start(bf16[2,128,1024]{2,1,0:T(8,128)(2,1)} %slice.12), channel_id=1, source_target_pairs={{0,2},{2,0},{1,3},{3,1},{4,6},{6,4},{5,7},{7,5},{8,10},{10,8},{9,1... | collective-permute-start | bytes 1572872 | tf_op jit(solution)/shard_map/ppermute | solution.py:27
  51.3 0.9 %copy-done.6 = bf16[1024,128]{1,0:T(8,128)(2,1)S(1)} copy-done((bf16[1024,128]{1,0:T(8,128)(2,1)S(1)}, bf16[1024,128]{1,0:T(8,128)(2,1)}, u32[]{:S(2)}) %copy-start.6) | copy-done | bytes 262168
  53.9 0.9 %own_pairs.1 = (bf16[1024,1024]{1,0:T(8,128)(2,1)S(1)}, f32[512,1024]{1,0:T(8,128)S(1)}) custom-call(bf16[512,512]{1,0:T(8,128)(2,1)S(1)} %get-tuple-element.35.own_ref, bf16[256,1024]{1,0:T(8,128)(2,1)S(1)} %pad_maximum_fusion.refs_0_, bf16[256,1024]{1,0:T(8,128)(2,1)S(1)} %copy-done.2, bf16[256,1024]{1,0:T(8,128)(2,1)S(1)} %copy-done.4, ...), custom_call_target="tpu_custom_call" | custom-call | tf_op jit(solution)/shard_map/own_pairs/pallas_call | solution.py:171
  55.4 1.3 %direct.1 = (bf16[512,1024]{1,0:T(8,128)(2,1)S(1)}, bf16[512,512]{1,0:T(8,128)(2,1)S(1)}) custom-call(bf16[512,512]{1,0:T(8,128)(2,1)S(1)} %collective-permute-done.10.other_ref, bf16[1024,1024]{1,0:T(8,128)(2,1)S(1)} %get-tuple-element.38.panel_ref, f32[512,1024]{1,0:T(8,128)S(1)} %get-tuple-element.39.pair_ref, f32[128,1024]{1,0:T(8,128)S(1)} %copy-done.8, ...), custom_call_target="tpu_custom_call" | custom-call | tf_op jit(solution)/shard_map/direct/pallas_call | solution.py:210
  58.7 1.3 %finish.1 = bf16[1024,512]{1,0:T(8,128)(2,1)S(1)} custom-call(bf16[1024,512]{1,0:T(8,128)(2,1)S(1)} %get-tuple-element.44.psi_ref, f32[512,512]{1,0:T(8,128)S(1)} %get-tuple-element.45.keep_ref, bf16[512,512]{1,0:T(8,128)(2,1)S(1)} %collective-permute-done.11.got_ref), custom_call_target="tpu_custom_call" | custom-call | tf_op jit(solution)/shard_map/finish/pallas_call | solution.py:265
  60.0 25.1 %all_to_all.10 = bf16[128,8,512]{2,1,0:T(8,128)(2,1)S(1)} all-to-all(bf16[128,8,512]{2,1,0:T(8,128)(2,1)S(1)} %bitcast.16), channel_id=1, replica_groups=mesh['zh'=2,'y'=4,'x'=4,'core'=2,'zl'=2] {'zh','y','x','core','zl'}, dimensions={0} | all-to-all | bytes 2097152 | tf_op jit(solution)/shard_map/all_to_all | solution.py:23
  (48 shorter events, 6.7 us)
Async XLA Ops:
  0.0 11.1 %collective-permute-start = (bf16[64,1024]{1,0:T(8,128)(2,1)}, bf16[64,1024]{1,0:T(8,128)(2,1)S(1)}, u32[]{:S(2)}, u32[]{:S(2)}) collective-permute-start(bf16[64,1024]{1,0:T(8,128)(2,1)} %bitcast.19), channel_id=1, source_target_pairs={{0,4},{4,8},{8,12},{12,0},{1,5},{5,9},{9,13},{13,1},{2,6},{6,10},{... | collective-permute-start | bytes 393224 | tf_op jit(solution)/shard_map/ppermute | solution.py:19
  2.0 9.1 %collective-permute-start.1 = (bf16[64,1024]{1,0:T(8,128)(2,1)}, bf16[64,1024]{1,0:T(8,128)(2,1)S(1)}, u32[]{:S(2)}, u32[]{:S(2)}) collective-permute-start(bf16[64,1024]{1,0:T(8,128)(2,1)} %bitcast.20), channel_id=1, source_target_pairs={{0,12},{4,0},{8,4},{12,8},{1,13},{5,1},{9,5},{13,9},{2,14},{6,2},{... | collective-permute-start | bytes 393224 | tf_op jit(solution)/shard_map/ppermute | solution.py:19
  3.3 7.8 %collective-permute-start.2 = (bf16[64,1024]{1,0:T(8,128)(2,1)}, bf16[64,1024]{1,0:T(8,128)(2,1)S(1)}, u32[]{:S(2)}, u32[]{:S(2)}) collective-permute-start(bf16[64,1024]{1,0:T(8,128)(2,1)} %bitcast.21), channel_id=1, source_target_pairs={{0,8},{4,12},{8,0},{12,4},{1,9},{5,13},{9,1},{13,5},{2,10},{6,14},... | collective-permute-start | bytes 393224 | tf_op jit(solution)/shard_map/ppermute | solution.py:19
  5.0 1.6 %copy-start = (f32[128,4096]{1,0:T(8,128)S(1)}, f32[128,4096]{1,0:T(8,128)}, u32[]{:S(2)}) copy-start(f32[128,4096]{1,0:T(8,128)} %in_ref.1) | copy-start | bytes 6291460
  7.6 3.6 %copy-start.14 = (bf16[1024,1,64]{0,2,1:T(8,128)(2,1)S(1)}, bf16[1024,1,64]{0,2,1:T(8,128)(2,1)}, u32[]{:S(2)}) copy-start(bf16[1024,1,64]{0,2,1:T(8,128)(2,1)} %param.6) | copy-start | bytes 393220
  7.6 3.6 %copy-start.15 = (bf16[1,8,1024]{2,1,0:T(8,128)(2,1)S(1)}, bf16[1,8,1024]{2,1,0:T(8,128)(2,1)}, u32[]{:S(2)}) copy-start(bf16[1,8,1024]{2,1,0:T(8,128)(2,1)} %param.4) | copy-start | bytes 49156
  12.3 13.2 %collective-permute-start.4 = (bf16[256,1024]{1,0:T(8,128)(2,1)S(1)}, bf16[256,1024]{1,0:T(8,128)(2,1)S(1)}, u32[]{:S(2)}, u32[]{:S(2)}) collective-permute-start(bf16[256,1024]{1,0:T(8,128)(2,1)S(1)} %pad_maximum_fusion.refs_0_), channel_id=1, source_target_pairs={{0,16},{16,32},{32,48},{48,0},{1,17},{17,33},{33,49},{49,1},{2,18}... | collective-permute-start | bytes 1572872 | tf_op jit(solution)/shard_map/ppermute | solution.py:19
  13.6 33.1 %collective-permute-start.3 = (bf16[3,128,1024]{2,1,0:T(8,128)(2,1)}, bf16[3,128,1024]{2,1,0:T(8,128)(2,1)S(1)}, u32[]{:S(2)}, u32[]{:S(2)}) collective-permute-start(bf16[3,128,1024]{2,1,0:T(8,128)(2,1)} %get-tuple-element.29), channel_id=1, source_target_pairs={{0,64},{64,0},{1,65},{65,1},{2,66},{66,2},{3,67},{67,3},{4,68},{68... | collective-permute-start | bytes 2359304 | tf_op jit(solution)/shard_map/ppermute | solution.py:288
  17.2 11.7 %collective-permute-start.6 = (bf16[256,1024]{1,0:T(8,128)(2,1)S(1)}, bf16[256,1024]{1,0:T(8,128)(2,1)S(1)}, u32[]{:S(2)}, u32[]{:S(2)}) collective-permute-start(bf16[256,1024]{1,0:T(8,128)(2,1)S(1)} %pad_maximum_fusion.refs_0_), channel_id=1, source_target_pairs={{0,48},{16,0},{32,16},{48,32},{1,49},{17,1},{33,17},{49,33},{2,50}... | collective-permute-start | bytes 1572872 | tf_op jit(solution)/shard_map/ppermute | solution.py:19
  18.6 32.7 %all-to-all-start = ((bf16[128,8,512]{2,1,0:T(8,128)(2,1)}), bf16[128,8,512]{2,1,0:T(8,128)(2,1)S(1)}, u32[]{:S(2)}, u32[]{:S(2)}) async-start(bf16[128,8,512]{2,1,0:T(8,128)(2,1)} %bitcast.17), calls=%async_computation | async-start | bytes 2097152 | tf_op jit(solution)/shard_map/all_to_all | solution.py:23
  25.5 3.3 %copy-start.1 = (bf16[256,1024]{1,0:T(8,128)(2,1)}, bf16[256,1024]{1,0:T(8,128)(2,1)S(1)}, u32[]{:S(2)}) copy-start(bf16[256,1024]{1,0:T(8,128)(2,1)S(1)} %collective-permute-done.4.refs_1_) | copy-start | bytes 1572868
  25.6 22.0 %collective-permute-start.5 = (bf16[128,1024]{1,0:T(8,128)(2,1)S(1)}, bf16[128,1024]{1,0:T(8,128)(2,1)S(1)}, u32[]{:S(2)}, u32[]{:S(2)}) collective-permute-start(bf16[128,1024]{1,0:T(8,128)(2,1)S(1)} %slice.13), channel_id=1, source_target_pairs={{0,16},{16,32},{32,48},{48,0},{1,17},{17,33},{33,49},{49,1},{2,18}... | collective-permute-start | bytes 786440 | tf_op jit(solution)/shard_map/ppermute | solution.py:19
  28.8 18.7 %copy-start.3 = (bf16[256,1024]{1,0:T(8,128)(2,1)}, bf16[256,1024]{1,0:T(8,128)(2,1)S(1)}, u32[]{:S(2)}) copy-start(bf16[256,1024]{1,0:T(8,128)(2,1)S(1)} %collective-permute-done.6.refs_2_) | copy-start | bytes 1572868
  28.9 19.4 %collective-permute-start.7 = (bf16[128,1024]{1,0:T(8,128)(2,1)S(1)}, bf16[128,1024]{1,0:T(8,128)(2,1)S(1)}, u32[]{:S(2)}, u32[]{:S(2)}) collective-permute-start(bf16[128,1024]{1,0:T(8,128)(2,1)S(1)} %slice.14), channel_id=1, source_target_pairs={{0,48},{16,0},{32,16},{48,32},{1,49},{17,1},{33,17},{49,33},{2,50}... | collective-permute-start | bytes 786440 | tf_op jit(solution)/shard_map/ppermute | solution.py:19
  34.5 16.8 %collective-permute-start.9 = (bf16[2,128,1024]{2,1,0:T(8,128)(2,1)}, bf16[2,128,1024]{2,1,0:T(8,128)(2,1)S(1)}, u32[]{:S(2)}, u32[]{:S(2)}) collective-permute-start(bf16[2,128,1024]{2,1,0:T(8,128)(2,1)} %copy-done.13), channel_id=1, source_target_pairs={{0,2},{2,0},{1,3},{3,1},{4,6},{6,4},{5,7},{7,5},{8,10},{10,8},{9,1... | collective-permute-start | bytes 1572872 | tf_op jit(solution)/shard_map/ppermute | solution.py:27
  49.0 4.1 %collective-permute-start.8 = (bf16[2,128,1024]{2,1,0:T(8,128)(2,1)}, bf16[2,128,1024]{2,1,0:T(8,128)(2,1)S(1)}, u32[]{:S(2)}, u32[]{:S(2)}) collective-permute-start(bf16[2,128,1024]{2,1,0:T(8,128)(2,1)} %slice.12), channel_id=1, source_target_pairs={{0,2},{2,0},{1,3},{3,1},{4,6},{6,4},{5,7},{7,5},{8,10},{10,8},{9,1... | collective-permute-start | bytes 1572872 | tf_op jit(solution)/shard_map/ppermute | solution.py:27
  51.3 1.0 %copy-start.6 = (bf16[1024,128]{1,0:T(8,128)(2,1)S(1)}, bf16[1024,128]{1,0:T(8,128)(2,1)}, u32[]{:S(2)}) copy-start(bf16[1024,128]{1,0:T(8,128)(2,1)} %left_ref.3) | copy-start | bytes 786436
  52.2 1.6 %copy-start.2 = (bf16[256,1024]{1,0:T(8,128)(2,1)S(1)}, bf16[256,1024]{1,0:T(8,128)(2,1)}, u32[]{:S(2)}) copy-start(bf16[256,1024]{1,0:T(8,128)(2,1)} %copy-done.1) | copy-start | bytes 1572868
  52.3 1.6 %copy-start.4 = (bf16[256,1024]{1,0:T(8,128)(2,1)S(1)}, bf16[256,1024]{1,0:T(8,128)(2,1)}, u32[]{:S(2)}) copy-start(bf16[256,1024]{1,0:T(8,128)(2,1)} %copy-done.3) | copy-start | bytes 1572868
  52.3 1.6 %copy-start.10 = (bf16[128,1024]{1,0:T(8,128)(2,1)S(1)}, bf16[128,1024]{1,0:T(8,128)(2,1)}, u32[]{:S(2)}) copy-start(bf16[128,1024]{1,0:T(8,128)(2,1)} %copy-done.9) | copy-start | bytes 786436
  52.3 1.6 %copy-start.12 = (bf16[128,1024]{1,0:T(8,128)(2,1)S(1)}, bf16[128,1024]{1,0:T(8,128)(2,1)}, u32[]{:S(2)}) copy-start(bf16[128,1024]{1,0:T(8,128)(2,1)} %copy-done.11) | copy-start | bytes 786436
  53.0 2.4 %copy-start.8 = (f32[128,1024]{1,0:T(8,128)S(1)}, f32[128,1024]{1,0:T(8,128)}, u32[]{:S(2)}) copy-start(f32[128,1024]{1,0:T(8,128)} %copy-done.7) | copy-start | bytes 1572868
  53.4 2.0 %collective-permute-start.10 = (bf16[512,512]{1,0:T(8,128)(2,1)S(1)}, bf16[512,512]{1,0:T(8,128)(2,1)S(1)}, u32[]{:S(2)}, u32[]{:S(2)}) collective-permute-start(bf16[512,512]{1,0:T(8,128)(2,1)S(1)} %get-tuple-element.35.own_ref), channel_id=1, source_target_pairs={{0,2},{2,0},{1,3},{3,1},{4,6},{6,4},{5,7},{7,5},{8,10},{10,8},{9,1... | collective-permute-start | bytes 1572872 | tf_op jit(solution)/shard_map/ppermute | solution.py:27
  56.7 2.0 %collective-permute-start.11 = (bf16[512,512]{1,0:T(8,128)(2,1)S(1)}, bf16[512,512]{1,0:T(8,128)(2,1)S(1)}, u32[]{:S(2)}, u32[]{:S(2)}) collective-permute-start(bf16[512,512]{1,0:T(8,128)(2,1)S(1)} %get-tuple-element.46), channel_id=1, source_target_pairs={{0,2},{2,0},{1,3},{3,1},{4,6},{6,4},{5,7},{7,5},{8,10},{10,8},{9,1... | collective-permute-start | bytes 1572872 | tf_op jit(solution)/shard_map/ppermute | solution.py:27
  (5 other events, 4.0 us)

commit v28 on v26

--- a/solution.py
+++ b/solution.py
@@ -129,7 +129,7 @@
     points = three.shape[0] // 3
 
     def kernel(trial_ref, passed_ref, three_ref, out_ref, psi_ref):
-        joined(passed_ref, 1, psi_ref, 0, points)
+        joined(passed_ref, 2, psi_ref, 0, points)
         out_ref[: 3 * points, :] = three_ref[...]
         out_ref[3 * points :, :] = lax.dot_general(
             psi_ref[...], trial_ref[...], (((0,), (0,)), ((), ())), preferred_element_type=F32
@@ -202,7 +202,7 @@
             )
             for j in range(4):
                 mine = slice(j * points, (j + 1) * points)
-                weights = scr_refs[j][:, here] if j == 0 else scr_refs[j][0, :, here].astype(F32)
+                weights = scr_refs[j][:, here] if j == 0 else scr_refs[j][j // 3, :, here].astype(F32)
                 weighted_ref[mine, here] = (weights * pair[mine]).astype(BF16)
         send = jnp.dot(weighted_ref[...], panel_ref[:, sibs], preferred_element_type=F32)
         send_ref[...] = send.astype(BF16)
@@ -290,7 +290,7 @@
     middle = line.shape[0] // 2
     beyond = [shift(behind[:middle], "y", 1), shift(ahead[middle:], "y", -1)]
     far, beyond = lax.optimization_barrier((far, beyond))
-    passed = swap(far[1:])
+    passed = swap(far)
     three, psi = project(trial_half, psi_v, near, far)
     proj_own, psi_last = project_last(trial_half, passed, three)
     proj_other = swap(proj_own)

time: 84.5 us -> 88.9 us (1.052)
  waiting for transfers between devices: 9.6 us -> 24.9 us
  starting transfers between devices: 32.4 us -> 25.8 us
  blocking collectives: 25.5 us -> 22.3 us
  Pallas kernels: 7.27 us -> 6.24 us
    all_to_all x1, waiting for transfers between devices: 0.01 us -> 13.3 us  [exchange(): return lax.all_to_all(value, axes, split_axis=0, concat_axis=0, tiled=True)]
    ppermute x4, starting transfers between devices: 11 us -> 2.87 us  [swap(): return lax.ppermute(value, 'core', [(0, 1), (1, 0)])]
    all_to_all x1, blocking collectives: 25.5 us -> 22.3 us  [exchange(): return lax.all_to_all(value, axes, split_axis=0, concat_axis=0, tiled=True)]
    ppermute x4, waiting for transfers between devices: 1.41 us -> 4.12 us  [swap(): return lax.ppermute(value, 'core', [(0, 1), (1, 0)])]
    all_to_all x1, starting transfers between devices: 6.75 us -> 8.83 us  [exchange(): return lax.all_to_all(value, axes, split_axis=0, concat_axis=0, tiled=True)]
    slice x2, local copies, waits for them, and re-layouts: 0.04 us -> 1.51 us  [shards(): beyond = [shift(behind[:middle], 'y', 1), shift(ahead[middle:], 'y', -1)]]
    pallas_call x1, Pallas kernels: 1.92 us -> 0.89 us  [pack(): pl.pallas_call(kernel, grid=(steps,), out_shape=[jax.ShapeDtypeStruct((po...]
    unnamed x32 -> x36, local copies, waits for them, and re-layouts: 6.54 us -> 5.81 us
  transfers between devices with their start and end apart: 13 -> 13, of which waited for: 4 -> 6; matrix products, arithmetic and copies ran while one was open for 1% -> 2% of each run, Pallas kernels for 5% -> 4%
where the time goes in v28:
time: 88.9 us; the launch traced here: 88.6 us
  starting transfers between devices  25.8 us (29%)
  waiting for transfers between devices  24.9 us (28%)
  blocking collectives  22.3 us (25%)
  local copies, waits for them, and re-layouts  8.42 us (9%)
  Pallas kernels  6.24 us (7%)
    all_to_all x1, blocking collectives, exchange(): return lax.all_to_all(value, axes, split_axis=0, concat_axis=0, tiled=True)  22.3 us
    all_to_all x1, waiting for transfers between devices, exchange(): return lax.all_to_all(value, axes, split_axis=0, concat_axis=0, tiled=True)  13.3 us
    ppermute x7, starting transfers between devices, shift(): return lax.ppermute(value, axis, [(k, (k + by) % n) for k in range(n)])  10.5 us
    all_to_all x1, starting transfers between devices, exchange(): return lax.all_to_all(value, axes, split_axis=0, concat_axis=0, tiled=True)  8.83 us
    ppermute x7, waiting for transfers between devices, shift(): return lax.ppermute(value, axis, [(k, (k + by) % n) for k in range(n)])  7.49 us
    unnamed x36, local copies, waits for them, and re-layouts  5.81 us
    ppermute x4, waiting for transfers between devices, swap(): return lax.ppermute(value, 'core', [(0, 1), (1, 0)])  4.12 us
    ppermute x1, starting transfers between devices, shards(): far = lax.ppermute(far, 'zh', [(0, 1), (1, 0)])  3.6 us
  transfers between devices with their start and end apart: 13, of which 6 were waited for; matrix products, arithmetic and copies ran while one was open for 2% of the time, Pallas kernels for 4%

profile of v28, /device:TPU:1, one launch (start us, length us, event | category | flops | bytes accessed | tf_op | source)
XLA Modules:
  0.0 88.6 jit_solution(13657167320280319756)
XLA Ops:
  0.0 2.0 %collective-permute-start = (bf16[64,1024]{1,0:T(8,128)(2,1)}, bf16[64,1024]{1,0:T(8,128)(2,1)S(1)}, u32[]{:S(2)}, u32[]{:S(2)}) collective-permute-start(bf16[64,1024]{1,0:T(8,128)(2,1)} %bitcast.19), channel_id=1, source_target_pairs={{0,4},{4,8},{8,12},{12,0},{1,5},{5,9},{9,13},{13,1},{2,6},{6,10},{... | collective-permute-start | bytes 393224 | tf_op jit(solution)/shard_map/ppermute | solution.py:19
  2.0 1.3 %collective-permute-start.1 = (bf16[64,1024]{1,0:T(8,128)(2,1)}, bf16[64,1024]{1,0:T(8,128)(2,1)S(1)}, u32[]{:S(2)}, u32[]{:S(2)}) collective-permute-start(bf16[64,1024]{1,0:T(8,128)(2,1)} %bitcast.20), channel_id=1, source_target_pairs={{0,12},{4,0},{8,4},{12,8},{1,13},{5,1},{9,5},{13,9},{2,14},{6,2},{... | collective-permute-start | bytes 393224 | tf_op jit(solution)/shard_map/ppermute | solution.py:19
  3.3 1.7 %collective-permute-start.2 = (bf16[64,1024]{1,0:T(8,128)(2,1)}, bf16[64,1024]{1,0:T(8,128)(2,1)S(1)}, u32[]{:S(2)}, u32[]{:S(2)}) collective-permute-start(bf16[64,1024]{1,0:T(8,128)(2,1)} %bitcast.21), channel_id=1, source_target_pairs={{0,8},{4,12},{8,0},{12,4},{1,9},{5,13},{9,1},{13,5},{2,10},{6,14},... | collective-permute-start | bytes 393224 | tf_op jit(solution)/shard_map/ppermute | solution.py:19
  5.0 1.6 %copy-done.2 = f32[128,4096]{1,0:T(8,128)S(1)} copy-done((f32[128,4096]{1,0:T(8,128)S(1)}, f32[128,4096]{1,0:T(8,128)}, u32[]{:S(2)}) %copy-start.2) | copy-done | bytes 2097176
  6.6 0.9 %copy-done.7 = bf16[1024,128]{1,0:T(8,128)(2,1)S(1)} copy-done((bf16[1024,128]{1,0:T(8,128)(2,1)S(1)}, bf16[1024,128]{1,0:T(8,128)(2,1)}, u32[]{:S(2)}) %copy-start.7) | copy-done | bytes 262168
  7.6 0.9 %pack.1 = (f32[128,1024]{1,0:T(8,128)S(1)}, bf16[2,128,1024]{2,1,0:T(8,128)(2,1)S(1)}, bf16[3,128,1024]{2,1,0:T(8,128)(2,1)S(1)}) custom-call(f32[128,4096]{1,0:T(8,128)S(1)} %copy-done.2, bf16[1024,128]{1,0:T(8,128)(2,1)S(1)} %copy-done.7), custom_call_target="tpu_custom_call" | custom-call | tf_op jit(solution)/shard_map/pack/pallas_call | solution.py:69
  8.5 0.8 copy-done.9
  9.3 0.8 copy-done.15
  10.6 1.1 %broadcast_in_dim.2 = bf16[32,2,2,8,512]{4,3,2,1,0:T(8,128)(2,1)} broadcast(bf16[2,8,512]{2,1,0:T(8,128)(2,1)S(1)} %bitcast.23), dimensions={1,3,4} | broadcast | bytes 1064960 | tf_op jit(solution)/shard_map/broadcast_in_dim | solution.py:284
  11.7 1.4 %collective-permute-start.4 = (bf16[256,1024]{1,0:T(8,128)(2,1)S(1)}, bf16[256,1024]{1,0:T(8,128)(2,1)S(1)}, u32[]{:S(2)}, u32[]{:S(2)}) collective-permute-start(bf16[256,1024]{1,0:T(8,128)(2,1)S(1)} %pad_maximum_fusion.refs_0_), channel_id=1, source_target_pairs={{0,16},{16,32},{32,48},{48,0},{1,17},{17,33},{33,49},{49,1},{2,18}... | collective-permute-start | bytes 1572872 | tf_op jit(solution)/shard_map/ppermute | solution.py:19
  13.1 1.4 %collective-permute-start.6 = (bf16[256,1024]{1,0:T(8,128)(2,1)S(1)}, bf16[256,1024]{1,0:T(8,128)(2,1)S(1)}, u32[]{:S(2)}, u32[]{:S(2)}) collective-permute-start(bf16[256,1024]{1,0:T(8,128)(2,1)S(1)} %pad_maximum_fusion.refs_0_), channel_id=1, source_target_pairs={{0,48},{16,0},{32,16},{48,32},{1,49},{17,1},{33,17},{49,33},{2,50}... | collective-permute-start | bytes 1572872 | tf_op jit(solution)/shard_map/ppermute | solution.py:19
  14.5 3.6 %collective-permute-start.3 = (bf16[3,128,1024]{2,1,0:T(8,128)(2,1)S(1)}, bf16[3,128,1024]{2,1,0:T(8,128)(2,1)S(1)}, u32[]{:S(2)}, u32[]{:S(2)}) collective-permute-start(bf16[3,128,1024]{2,1,0:T(8,128)(2,1)S(1)} %get-tuple-element.28), channel_id=1, source_target_pairs={{0,64},{64,0},{1,65},{65,1},{2,66},{66,2},{3,67},{67,3},{4,68},{68... | collective-permute-start | bytes 2359304 | tf_op jit(solution)/shard_map/ppermute | solution.py:288
  18.1 7.1 %collective-permute-done.4.refs_1_ = bf16[256,1024]{1,0:T(8,128)(2,1)S(1)} collective-permute-done((bf16[256,1024]{1,0:T(8,128)(2,1)S(1)}, bf16[256,1024]{1,0:T(8,128)(2,1)S(1)}, u32[]{:S(2)}, u32[]{:S(2)}) %collective-permute-start.4) | collective-permute-done | bytes 524320 | tf_op jit(solution)/shard_map/ppermute | solution.py:19
  27.0 2.6 %collective-permute-start.7 = (bf16[128,1024]{1,0:T(8,128)(2,1)}, bf16[128,1024]{1,0:T(8,128)(2,1)S(1)}, u32[]{:S(2)}, u32[]{:S(2)}) collective-permute-start(bf16[128,1024]{1,0:T(8,128)(2,1)} %slice.9), channel_id=1, source_target_pairs={{0,48},{16,0},{32,16},{48,32},{1,49},{17,1},{33,17},{49,33},{2,50}... | collective-permute-start | bytes 786440 | tf_op jit(solution)/shard_map/ppermute | solution.py:19
  29.5 8.8 %all-to-all-start = ((bf16[128,8,512]{2,1,0:T(8,128)(2,1)}), bf16[128,8,512]{2,1,0:T(8,128)(2,1)S(1)}, u32[]{:S(2)}, u32[]{:S(2)}) async-start(bf16[128,8,512]{2,1,0:T(8,128)(2,1)} %bitcast.17), calls=%async_computation | async-start | bytes 2097152 | tf_op jit(solution)/shard_map/all_to_all | solution.py:23
  39.8 1.1 %collective-permute-start.8 = (bf16[3,128,1024]{2,1,0:T(8,128)(2,1)S(1)}, bf16[3,128,1024]{2,1,0:T(8,128)(2,1)S(1)}, u32[]{:S(2)}, u32[]{:S(2)}) collective-permute-start(bf16[3,128,1024]{2,1,0:T(8,128)(2,1)S(1)} %collective-permute-done.3.far_ref.refs_2_), channel_id=1, source_target_pairs={{0,2},{2,0},{1,3},{3,1},{4,6},{6,4},{5,7},{7,5},{8,10},{10,8},{9,1... | collective-permute-start | bytes 2359304 | tf_op jit(solution)/shard_map/ppermute | solution.py:27
  40.9 2.7 %collective-permute-done.9.near_ref.refs_1_ = bf16[2,128,1024]{2,1,0:T(8,128)(2,1)S(1)} collective-permute-done((bf16[2,128,1024]{2,1,0:T(8,128)(2,1)}, bf16[2,128,1024]{2,1,0:T(8,128)(2,1)S(1)}, u32[]{:S(2)}, u32[]{:S(2)}) %collective-permute-start.9) | collective-permute-done | bytes 524320 | tf_op jit(solution)/shard_map/ppermute | solution.py:27
  43.6 13.3 %all-to-all-done = bf16[128,8,512]{2,1,0:T(8,128)(2,1)S(1)} async-done(((bf16[128,8,512]{2,1,0:T(8,128)(2,1)}), bf16[128,8,512]{2,1,0:T(8,128)(2,1)S(1)}, u32[]{:S(2)}, u32[]{:S(2)}) %all-to-all-start) | async-done | bytes 1048608 | tf_op jit(solution)/shard_map/all_to_all | solution.py:23
  58.0 1.3 %collective-permute-start.10 = (bf16[512,512]{1,0:T(8,128)(2,1)S(1)}, bf16[512,512]{1,0:T(8,128)(2,1)S(1)}, u32[]{:S(2)}, u32[]{:S(2)}) collective-permute-start(bf16[512,512]{1,0:T(8,128)(2,1)S(1)} %get-tuple-element.33.own_ref), channel_id=1, source_target_pairs={{0,2},{2,0},{1,3},{3,1},{4,6},{6,4},{5,7},{7,5},{8,10},{10,8},{9,1... | collective-permute-start | bytes 1572872 | tf_op jit(solution)/shard_map/ppermute | solution.py:27
  59.4 0.9 %own_pairs.1 = (bf16[1024,1024]{1,0:T(8,128)(2,1)S(1)}, f32[512,1024]{1,0:T(8,128)S(1)}) custom-call(bf16[512,512]{1,0:T(8,128)(2,1)S(1)} %get-tuple-element.33.own_ref, bf16[256,1024]{1,0:T(8,128)(2,1)S(1)} %copy-done.1, bf16[256,1024]{1,0:T(8,128)(2,1)S(1)} %copy-done.4, bf16[256,1024]{1,0:T(8,128)(2,1)S(1)} %copy-done.6, ...), custom_call_target="tpu_custom_call" | custom-call | tf_op jit(solution)/shard_map/own_pairs/pallas_call | solution.py:171
  60.9 1.3 %direct.1 = (bf16[512,1024]{1,0:T(8,128)(2,1)S(1)}, bf16[512,512]{1,0:T(8,128)(2,1)S(1)}) custom-call(bf16[512,512]{1,0:T(8,128)(2,1)S(1)} %collective-permute-done.10.other_ref, bf16[1024,1024]{1,0:T(8,128)(2,1)S(1)} %get-tuple-element.36.panel_ref, f32[512,1024]{1,0:T(8,128)S(1)} %get-tuple-element.37.pair_ref, f32[128,1024]{1,0:T(8,128)S(1)} %copy-done.10, ...), custom_call_target="tpu_custom_call" | custom-call | tf_op jit(solution)/shard_map/direct/pallas_call | solution.py:210
  64.2 1.3 %finish.1 = bf16[1024,512]{1,0:T(8,128)(2,1)S(1)} custom-call(bf16[1024,512]{1,0:T(8,128)(2,1)S(1)} %get-tuple-element.42.psi_ref, f32[512,512]{1,0:T(8,128)S(1)} %get-tuple-element.43.keep_ref, bf16[512,512]{1,0:T(8,128)(2,1)S(1)} %collective-permute-done.11.got_ref), custom_call_target="tpu_custom_call" | custom-call | tf_op jit(solution)/shard_map/finish/pallas_call | solution.py:265
  65.5 22.3 %all_to_all.10 = bf16[128,8,512]{2,1,0:T(8,128)(2,1)S(1)} all-to-all(bf16[128,8,512]{2,1,0:T(8,128)(2,1)S(1)} %bitcast.16), channel_id=1, replica_groups=mesh['zh'=2,'y'=4,'x'=4,'core'=2,'zl'=2] {'zh','y','x','core','zl'}, dimensions={0} | all-to-all | bytes 2097152 | tf_op jit(solution)/shard_map/all_to_all | solution.py:23
  87.8 0.8 convert_reduce_fusion
  (51 shorter events, 7.4 us)
Async XLA Ops:
  0.0 9.3 %collective-permute-start = (bf16[64,1024]{1,0:T(8,128)(2,1)}, bf16[64,1024]{1,0:T(8,128)(2,1)S(1)}, u32[]{:S(2)}, u32[]{:S(2)}) collective-permute-start(bf16[64,1024]{1,0:T(8,128)(2,1)} %bitcast.19), channel_id=1, source_target_pairs={{0,4},{4,8},{8,12},{12,0},{1,5},{5,9},{9,13},{13,1},{2,6},{6,10},{... | collective-permute-start | bytes 393224 | tf_op jit(solution)/shard_map/ppermute | solution.py:19
  2.0 7.2 %collective-permute-start.1 = (bf16[64,1024]{1,0:T(8,128)(2,1)}, bf16[64,1024]{1,0:T(8,128)(2,1)S(1)}, u32[]{:S(2)}, u32[]{:S(2)}) collective-permute-start(bf16[64,1024]{1,0:T(8,128)(2,1)} %bitcast.20), channel_id=1, source_target_pairs={{0,12},{4,0},{8,4},{12,8},{1,13},{5,1},{9,5},{13,9},{2,14},{6,2},{... | collective-permute-start | bytes 393224 | tf_op jit(solution)/shard_map/ppermute | solution.py:19
  3.3 7.2 %collective-permute-start.2 = (bf16[64,1024]{1,0:T(8,128)(2,1)}, bf16[64,1024]{1,0:T(8,128)(2,1)S(1)}, u32[]{:S(2)}, u32[]{:S(2)}) collective-permute-start(bf16[64,1024]{1,0:T(8,128)(2,1)} %bitcast.21), channel_id=1, source_target_pairs={{0,8},{4,12},{8,0},{12,4},{1,9},{5,13},{9,1},{13,5},{2,10},{6,14},... | collective-permute-start | bytes 393224 | tf_op jit(solution)/shard_map/ppermute | solution.py:19
  5.0 1.6 %copy-start.2 = (f32[128,4096]{1,0:T(8,128)S(1)}, f32[128,4096]{1,0:T(8,128)}, u32[]{:S(2)}) copy-start(f32[128,4096]{1,0:T(8,128)} %in_ref.1) | copy-start | bytes 6291460
  7.6 2.9 %copy-start.16 = (bf16[1024,1,64]{0,2,1:T(8,128)(2,1)S(1)}, bf16[1024,1,64]{0,2,1:T(8,128)(2,1)}, u32[]{:S(2)}) copy-start(bf16[1024,1,64]{0,2,1:T(8,128)(2,1)} %param.6) | copy-start | bytes 393220
  7.6 3.0 %copy-start.17 = (bf16[1,8,1024]{2,1,0:T(8,128)(2,1)S(1)}, bf16[1,8,1024]{2,1,0:T(8,128)(2,1)}, u32[]{:S(2)}) copy-start(bf16[1,8,1024]{2,1,0:T(8,128)(2,1)} %param.4) | copy-start | bytes 49156
  10.5 2.6 %copy-start = (bf16[256,1024]{1,0:T(8,128)(2,1)}, bf16[256,1024]{1,0:T(8,128)(2,1)S(1)}, u32[]{:S(2)}) copy-start(bf16[256,1024]{1,0:T(8,128)(2,1)S(1)} %pad_maximum_fusion.refs_0_) | copy-start | bytes 1572868
  10.6 46.3 %copy-start.8 = (bf16[1024,128]{1,0:T(8,128)(2,1)S(1)}, bf16[1024,128]{1,0:T(8,128)(2,1)}, u32[]{:S(2)}) copy-start(bf16[1024,128]{1,0:T(8,128)(2,1)} %left_ref.3) | copy-start | bytes 786436
  11.7 13.5 %collective-permute-start.4 = (bf16[256,1024]{1,0:T(8,128)(2,1)S(1)}, bf16[256,1024]{1,0:T(8,128)(2,1)S(1)}, u32[]{:S(2)}, u32[]{:S(2)}) collective-permute-start(bf16[256,1024]{1,0:T(8,128)(2,1)S(1)} %pad_maximum_fusion.refs_0_), channel_id=1, source_target_pairs={{0,16},{16,32},{32,48},{48,0},{1,17},{17,33},{33,49},{49,1},{2,18}... | collective-permute-start | bytes 1572872 | tf_op jit(solution)/shard_map/ppermute | solution.py:19
  13.1 12.9 %collective-permute-start.6 = (bf16[256,1024]{1,0:T(8,128)(2,1)S(1)}, bf16[256,1024]{1,0:T(8,128)(2,1)S(1)}, u32[]{:S(2)}, u32[]{:S(2)}) collective-permute-start(bf16[256,1024]{1,0:T(8,128)(2,1)S(1)} %pad_maximum_fusion.refs_0_), channel_id=1, source_target_pairs={{0,48},{16,0},{32,16},{48,32},{1,49},{17,1},{33,17},{49,33},{2,50}... | collective-permute-start | bytes 1572872 | tf_op jit(solution)/shard_map/ppermute | solution.py:19
  14.5 25.3 %collective-permute-start.3 = (bf16[3,128,1024]{2,1,0:T(8,128)(2,1)S(1)}, bf16[3,128,1024]{2,1,0:T(8,128)(2,1)S(1)}, u32[]{:S(2)}, u32[]{:S(2)}) collective-permute-start(bf16[3,128,1024]{2,1,0:T(8,128)(2,1)S(1)} %get-tuple-element.28), channel_id=1, source_target_pairs={{0,64},{64,0},{1,65},{65,1},{2,66},{66,2},{3,67},{67,3},{4,68},{68... | collective-permute-start | bytes 2359304 | tf_op jit(solution)/shard_map/ppermute | solution.py:288
  26.0 12.4 %collective-permute-start.5 = (bf16[128,1024]{1,0:T(8,128)(2,1)}, bf16[128,1024]{1,0:T(8,128)(2,1)S(1)}, u32[]{:S(2)}, u32[]{:S(2)}) collective-permute-start(bf16[128,1024]{1,0:T(8,128)(2,1)} %slice.8), channel_id=1, source_target_pairs={{0,16},{16,32},{32,48},{48,0},{1,17},{17,33},{33,49},{49,1},{2,18}... | collective-permute-start | bytes 786440 | tf_op jit(solution)/shard_map/ppermute | solution.py:19
  27.0 12.1 %collective-permute-start.7 = (bf16[128,1024]{1,0:T(8,128)(2,1)}, bf16[128,1024]{1,0:T(8,128)(2,1)S(1)}, u32[]{:S(2)}, u32[]{:S(2)}) collective-permute-start(bf16[128,1024]{1,0:T(8,128)(2,1)} %slice.9), channel_id=1, source_target_pairs={{0,48},{16,0},{32,16},{48,32},{1,49},{17,1},{33,17},{49,33},{2,50}... | collective-permute-start | bytes 786440 | tf_op jit(solution)/shard_map/ppermute | solution.py:19
  29.5 27.3 %all-to-all-start = ((bf16[128,8,512]{2,1,0:T(8,128)(2,1)}), bf16[128,8,512]{2,1,0:T(8,128)(2,1)S(1)}, u32[]{:S(2)}, u32[]{:S(2)}) async-start(bf16[128,8,512]{2,1,0:T(8,128)(2,1)} %bitcast.17), calls=%async_computation | async-start | bytes 2097152 | tf_op jit(solution)/shard_map/all_to_all | solution.py:23
  39.8 17.9 %collective-permute-start.8 = (bf16[3,128,1024]{2,1,0:T(8,128)(2,1)S(1)}, bf16[3,128,1024]{2,1,0:T(8,128)(2,1)S(1)}, u32[]{:S(2)}, u32[]{:S(2)}) collective-permute-start(bf16[3,128,1024]{2,1,0:T(8,128)(2,1)S(1)} %collective-permute-done.3.far_ref.refs_2_), channel_id=1, source_target_pairs={{0,2},{2,0},{1,3},{3,1},{4,6},{6,4},{5,7},{7,5},{8,10},{10,8},{9,1... | collective-permute-start | bytes 2359304 | tf_op jit(solution)/shard_map/ppermute | solution.py:27
  40.9 2.7 %collective-permute-start.9 = (bf16[2,128,1024]{2,1,0:T(8,128)(2,1)}, bf16[2,128,1024]{2,1,0:T(8,128)(2,1)S(1)}, u32[]{:S(2)}, u32[]{:S(2)}) collective-permute-start(bf16[2,128,1024]{2,1,0:T(8,128)(2,1)} %copy-done.15), channel_id=1, source_target_pairs={{0,2},{2,0},{1,3},{3,1},{4,6},{6,4},{5,7},{7,5},{8,10},{10,8},{9,1... | collective-permute-start | bytes 1572872 | tf_op jit(solution)/shard_map/ppermute | solution.py:27
  56.9 2.5 %copy-start.1 = (bf16[256,1024]{1,0:T(8,128)(2,1)S(1)}, bf16[256,1024]{1,0:T(8,128)(2,1)}, u32[]{:S(2)}) copy-start(bf16[256,1024]{1,0:T(8,128)(2,1)} %copy-done) | copy-start | bytes 1572868
  56.9 2.5 %copy-start.4 = (bf16[256,1024]{1,0:T(8,128)(2,1)S(1)}, bf16[256,1024]{1,0:T(8,128)(2,1)}, u32[]{:S(2)}) copy-start(bf16[256,1024]{1,0:T(8,128)(2,1)} %copy-done.3) | copy-start | bytes 1572868
  56.9 2.5 %copy-start.6 = (bf16[256,1024]{1,0:T(8,128)(2,1)S(1)}, bf16[256,1024]{1,0:T(8,128)(2,1)}, u32[]{:S(2)}) copy-start(bf16[256,1024]{1,0:T(8,128)(2,1)} %copy-done.5) | copy-start | bytes 1572868
  56.9 2.5 %copy-start.12 = (bf16[128,1024]{1,0:T(8,128)(2,1)S(1)}, bf16[128,1024]{1,0:T(8,128)(2,1)}, u32[]{:S(2)}) copy-start(bf16[128,1024]{1,0:T(8,128)(2,1)} %copy-done.11) | copy-start | bytes 786436
  56.9 2.5 %copy-start.14 = (bf16[128,1024]{1,0:T(8,128)(2,1)S(1)}, bf16[128,1024]{1,0:T(8,128)(2,1)}, u32[]{:S(2)}) copy-start(bf16[128,1024]{1,0:T(8,128)(2,1)} %copy-done.13) | copy-start | bytes 786436
  57.7 3.2 %copy-start.10 = (f32[128,1024]{1,0:T(8,128)S(1)}, f32[128,1024]{1,0:T(8,128)}, u32[]{:S(2)}) copy-start(f32[128,1024]{1,0:T(8,128)} %copy-done.9) | copy-start | bytes 1572868
  58.0 2.9 %collective-permute-start.10 = (bf16[512,512]{1,0:T(8,128)(2,1)S(1)}, bf16[512,512]{1,0:T(8,128)(2,1)S(1)}, u32[]{:S(2)}, u32[]{:S(2)}) collective-permute-start(bf16[512,512]{1,0:T(8,128)(2,1)S(1)} %get-tuple-element.33.own_ref), channel_id=1, source_target_pairs={{0,2},{2,0},{1,3},{3,1},{4,6},{6,4},{5,7},{7,5},{8,10},{10,8},{9,1... | collective-permute-start | bytes 1572872 | tf_op jit(solution)/shard_map/ppermute | solution.py:27
  62.2 2.0 %collective-permute-start.11 = (bf16[512,512]{1,0:T(8,128)(2,1)S(1)}, bf16[512,512]{1,0:T(8,128)(2,1)S(1)}, u32[]{:S(2)}, u32[]{:S(2)}) collective-permute-start(bf16[512,512]{1,0:T(8,128)(2,1)S(1)} %get-tuple-element.44), channel_id=1, source_target_pairs={{0,2},{2,0},{1,3},{3,1},{4,6},{6,4},{5,7},{7,5},{8,10},{10,8},{9,1... | collective-permute-start | bytes 1572872 | tf_op jit(solution)/shard_map/ppermute | solution.py:27
  (7 other events, 5.7 us)
